TPU v7x, 32 devices: a whole 2x2x4 slice. The times are simulated.
32 devices in a mesh: rep: 4 (over y, core), ep: 8 (over z, x).
Axes of the slice: x: 2, y: 2, z: 4, core: 2. Of those that a mesh axis runs over, the one named last changes fastest.
Arguments:
- tokens: bfloat16 [5120, 2048], P(('rep', 'ep')), may hold values from -6 to 6
- cotangent: bfloat16 [5120, 2048], P(('rep', 'ep')), may hold values from -6 to 6
- seq_lengths: int32 [4, 4], P('rep'), may hold values from 1 to 1024, 1120 in all within a row
- token_order: int32 [4, 1280], P('rep'), may hold values from 0 to 1279, each once within a row
- routes: int32 [5120, 8], P(('rep', 'ep')), may hold values from 0 to 15, as said below
- slot_index: int32 [5120, 8], P(('rep', 'ep')), may hold values from 0 to 100, as said below
- query_weight: bfloat16 [2048, 2048], P('ep'), may hold values from -0.125 to 0.125
- key_weight: bfloat16 [2048, 2048], P('ep'), may hold values from -0.125 to 0.125
- value_weight: bfloat16 [2048, 2048], P('ep'), may hold values from -0.125 to 0.125
- output_weight: bfloat16 [2048, 2048], P('ep'), may hold values from -1 to 1
- router_weight: bfloat16 [2048, 16], P('ep'), may hold values from -0.0625 to 0.0625
- prenorm_gain: float32 [2048], replicated, may hold values from 0.5 to 1.5
- querynorm_gain: float32 [128], replicated, may hold values from 0.6 to 1.4
- keynorm_gain: float32 [128], replicated, may hold values from 0.6 to 1.4
- postnorm_gain: float32 [2048], replicated, may hold values from 0.5 to 1.5
- gate_weight: bfloat16 [16, 2048, 1024], P('ep'), may hold values from -0.125 to 0.125
- up_weight: bfloat16 [16, 2048, 1024], P('ep'), may hold values from -0.125 to 0.125
- down_weight: bfloat16 [16, 1024, 2048], P('ep'), may hold values from -0.75 to 0.75
Outputs:
- layer_out: bfloat16 [5120, 2048], P(('rep', 'ep'))
- token_grad: float32 [5120, 2048], P(('rep', 'ep'))
- query_grad: float32 [2048, 2048], P('ep')
- key_grad: float32 [2048, 2048], P('ep')
- value_grad: float32 [2048, 2048], P('ep')
- output_grad: float32 [2048, 2048], P('ep')
- router_grad: float32 [2048, 16], P('ep')
- prenorm_grad: float32 [2048], P('ep')
- querynorm_grad: float32 [128], P('ep')
- keynorm_grad: float32 [128], P('ep')
- postnorm_grad: float32 [2048], P('ep')
- gate_grad: float32 [16, 2048, 1024], P('ep', 'rep')
- up_grad: float32 [16, 2048, 1024], P('ep', 'rep')
- down_grad: float32 [16, 1024, 2048], P('ep', 'rep')
Inputs may be any that keep to these rules, and one draw needn't show every extreme that they name: `seq_lengths`: each group's 4 lengths sum to 1120, the largest is exactly 1024; group positions 1120 to 1279 are padding. `token_order`: each row is a permutation of the group positions 0 to 1279. `routes`: the 8 experts of a row are distinct; among the rows of each device some expert is named by more than 100 rows. `slot_index`: within the rows of one device, the pairs that name one expert carry 0, 1, 2, ... in row order; counts from 100 on are stored as 100, and those pairs are dropped.
All inputs are finite; a program needn't handle non-finite values.
Results may differ from a plain program's by a relative error of at most 0.025.
Values may be sent and summed in bfloat16 or wider, within the bound.
No kernel may reach another device: no remote copies, remote signals or barrier semaphores. Data moves between devices by JAX's collectives and lax.ppermute only.
A program may use at most 448 MiB of HBM per device.

v0:
```python
import jax
import jax.numpy as jnp
from jax import lax
from jax.sharding import PartitionSpec as P

epsilon = 1e-05
rope_base = 10000.0
masked_value = -1e30


def norm_forward(values, gain_vector):
    inverse = lax.rsqrt(jnp.mean(values * values, axis=-1, keepdims=True) + epsilon)
    return (values * inverse * gain_vector, inverse)


def norm_backward(values, inverse, gain_vector, upstream):
    scaled = upstream * gain_vector
    inner_mean = jnp.mean(scaled * values, axis=-1, keepdims=True)
    result = inverse * scaled - values * (inverse * inverse * inverse) * inner_mean
    return (result, upstream * values * inverse)


def rope_tables(position, dimension):
    halfway = dimension // 2
    indices = jnp.arange(halfway, dtype=jnp.float32)
    frequency = rope_base ** (-2.0 * indices / dimension)
    angles = position.astype(jnp.float32)[:, None] * frequency[None, :]
    cosine = jnp.cos(angles)
    sine_part = jnp.sin(angles)
    return (
        jnp.concatenate([cosine, cosine], axis=-1)[:, None, :],
        jnp.concatenate([sine_part, sine_part], axis=-1)[:, None, :],
    )


def turn_half(values):
    halfway = values.shape[-1] // 2
    return jnp.concatenate([-values[..., halfway:], values[..., :halfway]], axis=-1)


def turn_back(values):
    halfway = values.shape[-1] // 2
    return jnp.concatenate([values[..., halfway:], -values[..., :halfway]], axis=-1)


def rotate(values, cosine, sine_part):
    return values * cosine + turn_half(values) * sine_part


def row_meta(lengths, group_order):
    boundary = jnp.cumsum(lengths)
    passed = (group_order[:, None] >= boundary[None, :]).astype(jnp.int32)
    segment = jnp.sum(passed, axis=1)
    offset = jnp.sum(passed * lengths[None, :], axis=1)
    return (segment, group_order - offset)


def pair_slice(values, pair_index, pair_width):
    head_dim = pair_width // 2
    picked = lax.dynamic_slice_in_dim(values, pair_index * pair_width, pair_width, 1)
    return picked.reshape(values.shape[0], 2, head_dim)


def pair_scores(query_heads, key_heads, allowed, score_scale):
    scores = (
        jnp.einsum("qhd,khd->hqk", query_heads, key_heads, preferred_element_type=jnp.float32)
        * score_scale
    )
    return jnp.where(allowed[None], scores, masked_value)


def body(
    tokens,
    cotangent,
    seq_lengths,
    token_order,
    routes,
    slot_index,
    query_weight,
    key_weight,
    value_weight,
    output_weight,
    router_weight,
    prenorm_gain,
    querynorm_gain,
    keynorm_gain,
    postnorm_gain,
    gate_weight,
    up_weight,
    down_weight,
):
    group_count = lax.axis_size("ep")
    device = lax.axis_index("ep")
    row_count, model_width = tokens.shape
    head_dim = querynorm_gain.shape[0]
    head_count = model_width // head_dim
    pair_width = 2 * head_dim
    pair_count = head_count // 2
    experts_here = gate_weight.shape[0]
    expert_total = experts_here * group_count
    top_count = routes.shape[1]
    capacity = row_count * top_count * 5 // (4 * expert_total)
    slot_total = expert_total * capacity
    group_rows = row_count * group_count
    sequence_count = seq_lengths.shape[1]
    score_scale = head_dim ** (-0.5)
    segment_all, position_all = row_meta(seq_lengths[0], token_order[0])
    segment_own = lax.dynamic_slice_in_dim(segment_all, device * row_count, row_count)
    position_own = lax.dynamic_slice_in_dim(position_all, device * row_count, row_count)
    valid_rows = (segment_own < sequence_count).astype(jnp.float32)[:, None]
    allowed = segment_own[:, None] == segment_all[None, :]
    full_query, full_key, full_value, full_output, full_router = (
        lax.all_gather(query_weight, "ep", axis=0, tiled=True),
        lax.all_gather(key_weight, "ep", axis=0, tiled=True),
        lax.all_gather(value_weight, "ep", axis=0, tiled=True),
        lax.all_gather(output_weight, "ep", axis=0, tiled=True),
        lax.all_gather(router_weight, "ep", axis=0, tiled=True),
    )
    token_values = tokens.astype(jnp.float32)
    normed_one, inverse_one = norm_forward(token_values, prenorm_gain)
    first_input = normed_one.astype(jnp.bfloat16)
    query_raw = jnp.dot(first_input, full_query, preferred_element_type=jnp.float32).reshape(
        row_count, head_count, head_dim
    )
    key_raw = jnp.dot(first_input, full_key, preferred_element_type=jnp.float32).reshape(
        row_count, head_count, head_dim
    )
    value_flat = jnp.dot(first_input, full_value, preferred_element_type=jnp.float32).astype(
        jnp.bfloat16
    )
    cosine, sine_part = rope_tables(position_own, head_dim)
    query_normed, query_inverse = norm_forward(query_raw, querynorm_gain)
    key_normed, key_inverse = norm_forward(key_raw, keynorm_gain)
    query_flat = (
        rotate(query_normed, cosine, sine_part).astype(jnp.bfloat16).reshape(row_count, model_width)
    )
    key_flat = (
        rotate(key_normed, cosine, sine_part).astype(jnp.bfloat16).reshape(row_count, model_width)
    )
    all_keys, all_values = (
        lax.all_gather(key_flat, "ep", axis=0, tiled=True),
        lax.all_gather(value_flat, "ep", axis=0, tiled=True),
    )

    def forward_pair(pair_index, running):
        mixed_heads, log_totals = running
        query_heads = pair_slice(query_flat, pair_index, pair_width)
        key_heads = pair_slice(all_keys, pair_index, pair_width)
        value_heads = pair_slice(all_values, pair_index, pair_width)
        scores = pair_scores(query_heads, key_heads, allowed, score_scale)
        top_score = jnp.max(scores, axis=-1, keepdims=True)
        log_total = top_score + jnp.log(
            jnp.sum(jnp.exp(scores - top_score), axis=-1, keepdims=True)
        )
        weights_low = jnp.exp(scores - log_total).astype(jnp.bfloat16)
        outcome = jnp.einsum(
            "hqk,khd->qhd", weights_low, value_heads, preferred_element_type=jnp.float32
        ).reshape(row_count, pair_width)
        mixed_heads = lax.dynamic_update_slice_in_dim(
            mixed_heads, outcome, pair_index * pair_width, 1
        )
        log_totals = lax.dynamic_update_slice_in_dim(
            log_totals, log_total[..., 0], pair_index * 2, 0
        )
        return (mixed_heads, log_totals)

    mixed_heads, log_totals = lax.fori_loop(
        0,
        pair_count,
        forward_pair,
        (
            jnp.zeros((row_count, model_width), jnp.float32),
            jnp.zeros((head_count, row_count), jnp.float32),
        ),
    )
    mixed_low = mixed_heads.astype(jnp.bfloat16)
    attention = jnp.dot(mixed_low, full_output, preferred_element_type=jnp.float32)
    residual = token_values + attention
    normed_two, inverse_two = norm_forward(residual, postnorm_gain)
    second_input = normed_two.astype(jnp.bfloat16)
    logits = jnp.dot(second_input, full_router, preferred_element_type=jnp.float32)
    gate_values = jax.nn.softmax(jnp.take_along_axis(logits, routes, axis=1), axis=-1)
    gates_low = gate_values.astype(jnp.bfloat16)
    kept_pair = slot_index < capacity
    flat_slot = routes * capacity + jnp.minimum(slot_index, capacity - 1)
    slot_ids = jnp.arange(slot_total, dtype=jnp.int32)
    dispatch_table = jnp.zeros((row_count, slot_total), jnp.bfloat16)
    combine_table = jnp.zeros((row_count, slot_total), jnp.bfloat16)
    for column in range(top_count):
        matching = (flat_slot[:, column, None] == slot_ids[None, :]) & kept_pair[:, column, None]
        dispatch_table = dispatch_table + matching.astype(jnp.bfloat16)
        combine_table = combine_table + jnp.where(
            matching, gates_low[:, column, None], jnp.zeros((), jnp.bfloat16)
        )
    outgoing = (
        jnp.einsum("tf,td->fd", dispatch_table, second_input, preferred_element_type=jnp.float32)
        .astype(jnp.bfloat16)
        .reshape(group_count, experts_here, capacity, model_width)
    )
    received = lax.all_to_all(outgoing, "ep", split_axis=0, concat_axis=0, tiled=True)
    gate_linear = jnp.einsum(
        "secd,edf->secf", received, gate_weight, preferred_element_type=jnp.float32
    )
    up_linear = jnp.einsum(
        "secd,edf->secf", received, up_weight, preferred_element_type=jnp.float32
    )
    inner_low = (jax.nn.silu(gate_linear) * up_linear).astype(jnp.bfloat16)
    expert_out = jnp.einsum(
        "secf,efd->secd", inner_low, down_weight, preferred_element_type=jnp.float32
    ).astype(jnp.bfloat16)
    returned = lax.all_to_all(expert_out, "ep", split_axis=0, concat_axis=0, tiled=True).reshape(
        slot_total, model_width
    )
    mixture = jnp.dot(combine_table, returned, preferred_element_type=jnp.float32)
    layer_out = (valid_rows * (residual + mixture)).astype(jnp.bfloat16)
    upstream = valid_rows * cotangent.astype(jnp.float32)
    upstream_low = upstream.astype(jnp.bfloat16)
    returned_grad = (
        jnp.einsum("tf,td->fd", combine_table, upstream_low, preferred_element_type=jnp.float32)
        .astype(jnp.bfloat16)
        .reshape(group_count, experts_here, capacity, model_width)
    )
    expert_grad = lax.all_to_all(returned_grad, "ep", split_axis=0, concat_axis=0, tiled=True)
    picked = jnp.take(returned, flat_slot, axis=0)
    pair_grad = jnp.where(
        kept_pair,
        jnp.einsum("tkd,td->tk", picked, upstream_low, preferred_element_type=jnp.float32),
        0.0,
    )
    chosen_grad = gate_values * (
        pair_grad - jnp.sum(gate_values * pair_grad, axis=1, keepdims=True)
    )
    expert_ids = jnp.arange(expert_total, dtype=jnp.int32)
    logits_grad = jnp.sum(
        jnp.where(routes[:, :, None] == expert_ids[None, None, :], chosen_grad[:, :, None], 0.0),
        axis=1,
    ).astype(jnp.bfloat16)
    router_part = jnp.einsum(
        "td,te->de", second_input, logits_grad, preferred_element_type=jnp.float32
    )
    second_grad = jnp.einsum(
        "te,de->td", logits_grad, full_router, preferred_element_type=jnp.float32
    )
    hidden_grad = jnp.einsum(
        "secd,efd->secf", expert_grad, down_weight, preferred_element_type=jnp.float32
    )
    down_part = jnp.einsum(
        "secf,secd->efd", inner_low, expert_grad, preferred_element_type=jnp.float32
    )
    sigmoid_gate = jax.nn.sigmoid(gate_linear)
    gate_back = (
        hidden_grad * up_linear * sigmoid_gate * (1.0 + gate_linear * (1.0 - sigmoid_gate))
    ).astype(jnp.bfloat16)
    up_back = (hidden_grad * gate_linear * sigmoid_gate).astype(jnp.bfloat16)
    gate_part = jnp.einsum(
        "secd,secf->edf", received, gate_back, preferred_element_type=jnp.float32
    )
    up_part = jnp.einsum("secd,secf->edf", received, up_back, preferred_element_type=jnp.float32)
    buffer_grad = (
        jnp.einsum("secf,edf->secd", gate_back, gate_weight, preferred_element_type=jnp.float32)
        + jnp.einsum("secf,edf->secd", up_back, up_weight, preferred_element_type=jnp.float32)
    ).astype(jnp.bfloat16)
    gate_total, up_total, down_total = (
        lax.psum_scatter(
            gate_part.astype(jnp.bfloat16), "rep", scatter_dimension=1, tiled=True
        ).astype(jnp.float32),
        lax.psum_scatter(
            up_part.astype(jnp.bfloat16), "rep", scatter_dimension=1, tiled=True
        ).astype(jnp.float32),
        lax.psum_scatter(
            down_part.astype(jnp.bfloat16), "rep", scatter_dimension=1, tiled=True
        ).astype(jnp.float32),
    )
    home_grad = lax.all_to_all(buffer_grad, "ep", split_axis=0, concat_axis=0, tiled=True).reshape(
        slot_total, model_width
    )
    second_grad = second_grad + jnp.dot(
        dispatch_table, home_grad, preferred_element_type=jnp.float32
    )
    post_back, postnorm_part = norm_backward(residual, inverse_two, postnorm_gain, second_grad)
    residual_grad = upstream + post_back
    attention_low = residual_grad.astype(jnp.bfloat16)
    output_part = jnp.einsum(
        "tc,td->cd", mixed_low, attention_low, preferred_element_type=jnp.float32
    )
    mixed_grad = jnp.einsum(
        "td,cd->tc", attention_low, full_output, preferred_element_type=jnp.float32
    ).astype(jnp.bfloat16)

    def backward_pair(pair_index, running):
        query_total, key_total, value_total = running
        query_heads = pair_slice(query_flat, pair_index, pair_width)
        key_heads = pair_slice(all_keys, pair_index, pair_width)
        value_heads = pair_slice(all_values, pair_index, pair_width)
        grad_heads = pair_slice(mixed_grad, pair_index, pair_width)
        scores = pair_scores(query_heads, key_heads, allowed, score_scale)
        log_total = lax.dynamic_slice_in_dim(log_totals, pair_index * 2, 2, 0)[:, :, None]
        attention_weights = jnp.exp(scores - log_total)
        weight_grad = jnp.einsum(
            "qhd,khd->hqk", grad_heads, value_heads, preferred_element_type=jnp.float32
        )
        row_dot = jnp.sum(attention_weights * weight_grad, axis=-1, keepdims=True)
        score_grad = (attention_weights * (weight_grad - row_dot)).astype(jnp.bfloat16)
        query_piece = (
            jnp.einsum("hqk,khd->qhd", score_grad, key_heads, preferred_element_type=jnp.float32)
            * score_scale
        )
        key_piece = (
            jnp.einsum("hqk,qhd->khd", score_grad, query_heads, preferred_element_type=jnp.float32)
            * score_scale
        )
        value_piece = jnp.einsum(
            "hqk,qhd->khd",
            attention_weights.astype(jnp.bfloat16),
            grad_heads,
            preferred_element_type=jnp.float32,
        )
        query_total = lax.dynamic_update_slice_in_dim(
            query_total, query_piece.reshape(row_count, pair_width), pair_index * pair_width, 1
        )
        key_total = lax.dynamic_update_slice_in_dim(
            key_total, key_piece.reshape(group_rows, pair_width), pair_index * pair_width, 1
        )
        value_total = lax.dynamic_update_slice_in_dim(
            value_total, value_piece.reshape(group_rows, pair_width), pair_index * pair_width, 1
        )
        return (query_total, key_total, value_total)

    query_total, key_total, value_total = lax.fori_loop(
        0,
        pair_count,
        backward_pair,
        (
            jnp.zeros((row_count, model_width), jnp.float32),
            jnp.zeros((group_rows, model_width), jnp.float32),
            jnp.zeros((group_rows, model_width), jnp.float32),
        ),
    )
    key_back, value_back = (
        lax.psum_scatter(
            key_total.astype(jnp.bfloat16), "ep", scatter_dimension=0, tiled=True
        ).astype(jnp.float32),
        lax.psum_scatter(
            value_total.astype(jnp.bfloat16), "ep", scatter_dimension=0, tiled=True
        ).astype(jnp.float32),
    )
    query_turned = query_total.reshape(row_count, head_count, head_dim)
    query_unturned = query_turned * cosine + turn_back(query_turned * sine_part)
    query_before, querynorm_part = norm_backward(
        query_raw, query_inverse, querynorm_gain, query_unturned
    )
    key_turned = key_back.reshape(row_count, head_count, head_dim)
    key_unturned = key_turned * cosine + turn_back(key_turned * sine_part)
    key_before, keynorm_part = norm_backward(key_raw, key_inverse, keynorm_gain, key_unturned)
    query_sent = query_before.reshape(row_count, model_width).astype(jnp.bfloat16)
    key_sent = key_before.reshape(row_count, model_width).astype(jnp.bfloat16)
    value_sent = value_back.astype(jnp.bfloat16)
    query_part = jnp.einsum(
        "td,tc->dc", first_input, query_sent, preferred_element_type=jnp.float32
    )
    key_part = jnp.einsum("td,tc->dc", first_input, key_sent, preferred_element_type=jnp.float32)
    value_part = jnp.einsum(
        "td,tc->dc", first_input, value_sent, preferred_element_type=jnp.float32
    )
    first_grad = jnp.einsum("tc,dc->td", query_sent, full_query, preferred_element_type=jnp.float32)
    first_grad = first_grad + jnp.einsum(
        "tc,dc->td", key_sent, full_key, preferred_element_type=jnp.float32
    )
    first_grad = first_grad + jnp.einsum(
        "tc,dc->td", value_sent, full_value, preferred_element_type=jnp.float32
    )
    pre_back, prenorm_part = norm_backward(token_values, inverse_one, prenorm_gain, first_grad)
    token_grad = residual_grad + pre_back
    shards = (
        lax.psum_scatter(
            query_part.astype(jnp.bfloat16), "ep", scatter_dimension=0, tiled=True
        ).astype(jnp.float32),
        lax.psum_scatter(
            key_part.astype(jnp.bfloat16), "ep", scatter_dimension=0, tiled=True
        ).astype(jnp.float32),
        lax.psum_scatter(
            value_part.astype(jnp.bfloat16), "ep", scatter_dimension=0, tiled=True
        ).astype(jnp.float32),
        lax.psum_scatter(
            output_part.astype(jnp.bfloat16), "ep", scatter_dimension=0, tiled=True
        ).astype(jnp.float32),
        lax.psum_scatter(
            router_part.astype(jnp.bfloat16), "ep", scatter_dimension=0, tiled=True
        ).astype(jnp.float32),
        lax.psum_scatter(
            jnp.sum(prenorm_part, axis=0).astype(jnp.bfloat16),
            "ep",
            scatter_dimension=0,
            tiled=True,
        ).astype(jnp.float32),
        lax.psum_scatter(
            jnp.sum(querynorm_part, axis=(0, 1)).astype(jnp.bfloat16),
            "ep",
            scatter_dimension=0,
            tiled=True,
        ).astype(jnp.float32),
        lax.psum_scatter(
            jnp.sum(keynorm_part, axis=(0, 1)).astype(jnp.bfloat16),
            "ep",
            scatter_dimension=0,
            tiled=True,
        ).astype(jnp.float32),
        lax.psum_scatter(
            jnp.sum(postnorm_part, axis=0).astype(jnp.bfloat16),
            "ep",
            scatter_dimension=0,
            tiled=True,
        ).astype(jnp.float32),
    )
    (
        query_grad,
        key_grad,
        value_grad,
        output_grad,
        router_grad,
        prenorm_grad,
        querynorm_grad,
        keynorm_grad,
        postnorm_grad,
    ) = (
        lax.psum(shards[0].astype(jnp.bfloat16), "rep").astype(jnp.float32),
        lax.psum(shards[1].astype(jnp.bfloat16), "rep").astype(jnp.float32),
        lax.psum(shards[2].astype(jnp.bfloat16), "rep").astype(jnp.float32),
        lax.psum(shards[3].astype(jnp.bfloat16), "rep").astype(jnp.float32),
        lax.psum(shards[4].astype(jnp.bfloat16), "rep").astype(jnp.float32),
        lax.psum(shards[5].astype(jnp.bfloat16), "rep").astype(jnp.float32),
        lax.psum(shards[6].astype(jnp.bfloat16), "rep").astype(jnp.float32),
        lax.psum(shards[7].astype(jnp.bfloat16), "rep").astype(jnp.float32),
        lax.psum(shards[8].astype(jnp.bfloat16), "rep").astype(jnp.float32),
    )
    return (
        layer_out,
        token_grad,
        query_grad,
        key_grad,
        value_grad,
        output_grad,
        router_grad,
        prenorm_grad,
        querynorm_grad,
        keynorm_grad,
        postnorm_grad,
        gate_total,
        up_total,
        down_total,
    )


def solution(mesh):
    in_specs = (
        P(("rep", "ep"), None),
        P(("rep", "ep"), None),
        P("rep", None),
        P("rep", None),
        P(("rep", "ep"), None),
        P(("rep", "ep"), None),
        P("ep", None),
        P("ep", None),
        P("ep", None),
        P("ep", None),
        P("ep", None),
        P(),
        P(),
        P(),
        P(),
        P("ep", None, None),
        P("ep", None, None),
        P("ep", None, None),
    )
    out_specs = (
        P(("rep", "ep"), None),
        P(("rep", "ep"), None),
        P("ep", None),
        P("ep", None),
        P("ep", None),
        P("ep", None),
        P("ep", None),
        P("ep"),
        P("ep"),
        P("ep"),
        P("ep"),
        P("ep", "rep", None),
        P("ep", "rep", None),
        P("ep", "rep", None),
    )
    return jax.shard_map(body, mesh=mesh, in_specs=in_specs, out_specs=out_specs, check_vma=False)
```

profile of v0, /device:TPU:0, one launch (start us, length us, event | category | flops | bytes accessed | tf_op | source)
XLA Modules:
  0.0 2747.1 jit_solution(6591452379442833246)
XLA Ops:
  11.3 126.5 %all-gather.13.cloned.1.call-done = bf16[2048,2048]{1,0:T(8,128)(2,1)} async-done(((bf16[256,2048]{1,0:T(8,128)(2,1)}), bf16[2048,2048]{1,0:T(8,128)(2,1)}) %all-gather.13.cloned.1.call-update) | async-done | bytes 8388624 | tf_op jit(solution)/shard_map/all_gather | solution.py:114
  143.0 120.1 %all-gather.11.cloned.1.call-done = bf16[2048,2048]{1,0:T(8,128)(2,1)} async-done(((bf16[256,2048]{1,0:T(8,128)(2,1)}), bf16[2048,2048]{1,0:T(8,128)(2,1)}) %all-gather.11.cloned.1.call-update) | async-done | bytes 8388624 | tf_op jit(solution)/shard_map/all_gather | solution.py:113
  277.5 110.8 %all-gather.7.cloned.1.call-done = bf16[2048,2048]{1,0:T(8,128)(2,1)} async-done(((bf16[256,2048]{1,0:T(8,128)(2,1)}), bf16[2048,2048]{1,0:T(8,128)(2,1)}) %all-gather.7.cloned.1.call-update) | async-done | bytes 8388624 | tf_op jit(solution)/shard_map/all_gather | solution.py:115
  388.4 5.8 convolution_convert_fusion.7
  396.5 78.9 %all-gather.15.cloned.1.call-done = bf16[1280,2048]{1,0:T(8,128)(2,1)} async-done(((bf16[160,2048]{1,0:T(8,128)(2,1)}), bf16[1280,2048]{1,0:T(8,128)(2,1)}) %all-gather.15.cloned.1.call-update) | async-done | bytes 5242896 | tf_op jit(solution)/shard_map/all_gather | solution.py:141
  475.4 7.9 copy.191
  483.3 79.2 %all-gather.9.cloned.1.call-done = bf16[1280,2048]{1,0:T(8,128)(2,1)} async-done(((bf16[160,2048]{1,0:T(8,128)(2,1)}), bf16[1280,2048]{1,0:T(8,128)(2,1)}) %all-gather.9.cloned.1.call-update) | async-done | bytes 5242896 | tf_op jit(solution)/shard_map/all_gather | solution.py:142
  562.5 7.9 copy.190
  570.4 36.3 %while.34 = (s32[]{:T(128)}, bf16[160,2048]{1,0:T(8,128)(2,1)}, f32[16,160]{1,0:T(8,128)S(1)}, bf16[1280,2048]{0,1:T(8,128)(2,1)}, bf16[160,2048]{1,0:T(8,128)(2...) while((s32[]{:T(128)}, bf16[160,2048]{1,0:T(8,128)(2,1)}, ...), condition=%wide.region_9.10_spmd.clone, body=%wide.region_6.9_spmd.clone.sunk | while | flops 212786880 | bytes 9603953 | solution.py:167
  606.7 81.0 %all-gather.17.cloned.1.call-done = bf16[2048,2048]{1,0:T(8,128)(2,1)} async-done(((bf16[256,2048]{1,0:T(8,128)(2,1)}), bf16[2048,2048]{1,0:T(8,128)(2,1)}) %all-gather.17.cloned.1.call-update) | async-done | bytes 8388624 | tf_op jit(solution)/shard_map/all_gather | solution.py:116
  687.7 5.3 multiply_reduce_fusion.5
  694.2 6.2 convolution_convert_fusion.5
  700.4 8.5 reshape.318
  708.9 13.6 copy.194
  727.7 163.3 %all_gather.27 = bf16[2048,16]{0,1:T(8,128)(2,1)S(1)} all-gather(bf16[256,16]{0,1:T(8,128)(2,1)S(1)} %copy-done.82), channel_id=1, replica_groups=mesh['rep'=4,'ep'=8] {'ep'}, dimensions={0}, use_global_device_ids=true | all-gather | bytes 73728 | tf_op jit(solution)/shard_map/all_gather | solution.py:117
  891.9 10.2 gather_fusion.1
  903.3 6.7 convolution_convert_fusion.4
  910.0 8.4 reshape.320
  918.4 13.6 copy.201
  937.1 16.5 fusion.25
  953.6 16.4 fusion.29
  970.0 105.8 %all-to-all-done.2 = bf16[8,2,100,2048]{3,1,2,0:T(2,128)(2,1)} async-done(((bf16[8,2,100,2048]{3,1,2,0:T(2,128)(2,1)}), bf16[8,2,100,2048]{3,1,2,0:T(2,128)(2,1)}, u32[]{:S(2)}, u32[]{:S(2)}) %all-to-all-start.2) | async-done | bytes 6553632 | tf_op jit(solution)/shard_map/all_to_all | solution.py:223
  1075.8 21.9 fusion.38
  1097.7 11.3 convert_bitcast_fusion
  1109.0 14.4 copy.197
  1128.4 13.6 fusion.23
  1142.0 14.4 fusion.35
  1156.4 13.6 copy.203
  1170.1 101.2 %all-to-all-done.1 = bf16[8,2,100,2048]{3,1,2,0:T(2,128)(2,1)} async-done(((bf16[8,2,100,2048]{3,1,2,0:T(2,128)(2,1)}), bf16[8,2,100,2048]{3,1,2,0:T(2,128)(2,1)}, u32[]{:S(2)}, u32[]{:S(2)}) %all-to-all-start.1) | async-done | bytes 6553632 | tf_op jit(solution)/shard_map/all_to_all | solution.py:211
  1276.6 8.8 copy.198
  1285.4 8.6 reshape.319
  1294.0 14.6 gather_fusion
  1308.6 6.6 fusion.48
  1315.4 103.4 %all-to-all-done.3 = bf16[8,2,100,2048]{3,1,2,0:T(2,128)(2,1)} async-done(((bf16[8,2,100,2048]{3,1,2,0:T(2,128)(2,1)}), bf16[8,2,100,2048]{3,1,2,0:T(2,128)(2,1)}, u32[]{:S(2)}, u32[]{:S(2)}) %all-to-all-start.3) | async-done | bytes 6553632 | tf_op jit(solution)/shard_map/all_to_all | solution.py:274
  1418.9 8.8 copy.204
  1427.8 8.9 reshape.321
  1436.9 5.8 fusion.141
  1444.4 6.8 convolution_convert_fusion.6
  1458.1 91.7 %while.35 = (s32[]{:T(128)}, f32[160,2048]{1,0:T(8,128)}, bf16[1280,2048]{1,0:T(8,128)(2,1)}, bf16[1280,2048]{0,1:T(8,128)(2,1)}, bf16[1280,2048]{0,1:T(8,128)(2...) while((s32[]{:T(128)}, f32[160,2048]{1,0:T(8,128)}, ...), condition=%wide.region_18.19_spmd.clone, body=%wide.region_16.18_spmd.clone.sunk | while | flops 528875200 | bytes 38105372 | solution.py:329
  1549.9 8.2 copy.224
  1560.0 16.9 bitcast_convert_fusion
  1579.1 33.7 %bitcast_convert_fusion.2 = bf16[2,2048,1024]{2,1,0:T(8,128)(2,1)} fusion(bf16[8,2,100,1024]{3,2,0,1:T(8,128)(2,1)S(1)} %copy-done.157, bf16[8,2,100,2048]{3,1,2,0:T(2,128)(2,1)} %all-to-all-done), kind=kOutput, calls=%fused_computation.50 | convolution fusion | flops 6715080704 | bytes 18219008 | tf_op jit(solution)/shard_map/secd,secf->edf/dot_general | solution.py:255
  1614.7 33.6 %bitcast_convert_fusion.1 = bf16[2,2048,1024]{2,1,0:T(8,128)(2,1)} fusion(bf16[8,2,100,1024]{3,2,0,1:T(8,128)(2,1)S(1)} %copy-done.159, bf16[8,2,100,2048]{3,1,2,0:T(2,128)(2,1)} %all-to-all-done), kind=kOutput, calls=%fused_computation.49 | convolution fusion | flops 6715080704 | bytes 18219008 | tf_op jit(solution)/shard_map/secd,secf->edf/dot_general | solution.py:258
  1649.6 6.8 convolution_convert_fusion
  1669.4 7.6 fusion.82
  1677.8 5.8 convolution_convert_fusion.3
  1684.8 5.8 convolution_convert_fusion.2
  1690.6 66.9 %reduce-scatter.31.cloned.1.call-done = bf16[160,2048]{1,0:T(8,128)(2,1)} async-done(((bf16[1280,2048]{1,0:T(8,128)(2,1)}), bf16[160,2048]{1,0:T(8,128)(2,1)}) %reduce-scatter.31.cloned.1.call-update) | async-done | bytes 655376
  1757.5 6.9 convolution_convert_fusion.1
  1769.4 8.4 fusion.60
  1778.1 53.5 %reduce-scatter.29.cloned.1.call-done = bf16[2,256,2048]{2,1,0:T(8,128)(2,1)} async-done(((bf16[2,1024,2048]{2,1,0:T(8,128)(2,1)}), bf16[2,256,2048]{2,1,0:T(8,128)(2,1)}) %reduce-scatter.29.cloned.1.call-update) | async-done | bytes 2097168 | tf_op jit(solution)/shard_map/reduce_scatter | solution.py:270
  1835.8 70.2 %reduce-scatter.25.cloned.1.call-done = bf16[2,512,1024]{2,1,0:T(8,128)(2,1)} async-done(((bf16[2,2048,1024]{2,1,0:T(8,128)(2,1)}), bf16[2,512,1024]{2,1,0:T(8,128)(2,1)}) %reduce-scatter.25.cloned.1.call-update) | async-done | bytes 2097168 | tf_op jit(solution)/shard_map/reduce_scatter | solution.py:264
  1910.1 70.3 %reduce-scatter.27.cloned.1.call-done = bf16[2,512,1024]{2,1,0:T(8,128)(2,1)} async-done(((bf16[2,2048,1024]{2,1,0:T(8,128)(2,1)}), bf16[2,512,1024]{2,1,0:T(8,128)(2,1)}) %reduce-scatter.27.cloned.1.call-update) | async-done | bytes 2097168 | tf_op jit(solution)/shard_map/reduce_scatter | solution.py:267
  1984.4 7.4 fusion.160
  1991.8 141.5 %reduce-scatter.21.cloned.1.call-done = bf16[256,2048]{1,0:T(8,128)(2,1)} async-done(((bf16[2048,2048]{1,0:T(8,128)(2,1)}), bf16[256,2048]{1,0:T(8,128)(2,1)}) %reduce-scatter.21.cloned.1.call-update) | async-done | bytes 1048592 | tf_op jit(solution)/shard_map/reduce_scatter | solution.py:384
  2133.2 151.7 %reduce-scatter.15.cloned.1.call-done = bf16[256,2048]{1,0:T(8,128)(2,1)} async-done(((bf16[2048,2048]{1,0:T(8,128)(2,1)}), bf16[256,2048]{1,0:T(8,128)(2,1)}) %reduce-scatter.15.cloned.1.call-update) | async-done | bytes 1048592 | tf_op jit(solution)/shard_map/reduce_scatter | solution.py:375
  2284.9 152.0 %reduce-scatter.17.cloned.1.call-done = bf16[256,2048]{1,0:T(8,128)(2,1)} async-done(((bf16[2048,2048]{1,0:T(8,128)(2,1)}), bf16[256,2048]{1,0:T(8,128)(2,1)}) %reduce-scatter.17.cloned.1.call-update) | async-done | bytes 1048592 | tf_op jit(solution)/shard_map/reduce_scatter | solution.py:378
  2436.9 151.5 %reduce-scatter.19.cloned.1.call-done = bf16[256,2048]{1,0:T(8,128)(2,1)} async-done(((bf16[2048,2048]{1,0:T(8,128)(2,1)}), bf16[256,2048]{1,0:T(8,128)(2,1)}) %reduce-scatter.19.cloned.1.call-update) | async-done | bytes 1048592 | tf_op jit(solution)/shard_map/reduce_scatter | solution.py:381
  2589.6 6.7 convolution_add_fusion.3
  2596.3 6.6 fusion.70
  2602.9 20.0 all-reduce.4
  2623.2 21.8 reduce-scatter.23.cloned.1.call-done
  2645.0 10.2 all-reduce.5
  2659.4 73.4 %all-reduce.9.cloned.1.call-done = (bf16[256,2048]{1,0:T(8,128)(2,1)}, bf16[256,2048]{1,0:T(8,128)(2,1)}, bf16[256,2048]{1,0:T(8,128)(2,1)}, bf16[256,2048]{1,0:T(8,128)(2,1)}) async-done(((bf16[256,2048]{1,0:T(8,128)(2,1)}, bf16[256,2048]{1,0:T(8,128)(2,1)}, bf16[256,2048]{1,0:T(8,128)(2,1)}, bf16[256,2048]{1,0:T(8,128)(2,1)}), (bf16[256,2048]{1,0:T(8,128)(2,1)}, bf16[256,2048]{1,0:T(8,128)(2,1)}, ...) | async-done | bytes 4194320 | tf_op jit(solution)/shard_map/psum | solution.py:426
  (695 shorter events, 236.2 us)
Async XLA Ops:
  7.2 130.6 %all-gather.13.cloned.1.call-start = ((), (), s32[]{:S(2)}) async-start(), calls=%async_computation.17 | async-start | bytes 9437184 | tf_op jit(solution)/shard_map/all_gather | solution.py:114
  7.9 255.1 %all-gather.11.cloned.1.call-start = ((), (), s32[]{:S(2)}) async-start(), calls=%async_computation.16 | async-start | bytes 9437184 | tf_op jit(solution)/shard_map/all_gather | solution.py:113
  8.7 129.1 %copy-start.41 = (f32[2048]{0:T(1024)S(1)}, f32[2048]{0:T(1024)}, u32[]{:S(2)}) copy-start(f32[2048]{0:T(1024)} %param.33) | copy-start | bytes 24580
  8.7 379.6 %all-gather.7.cloned.1.call-start = ((), (), s32[]{:S(2)}) async-start(), calls=%async_computation.14 | async-start | bytes 9437184 | tf_op jit(solution)/shard_map/all_gather | solution.py:115
  9.5 466.0 %all-gather.15.cloned.1.call-start = ((), (), s32[]{:S(2)}) async-start(), calls=%async_computation.18 | async-start | bytes 5898240 | tf_op jit(solution)/shard_map/all_gather | solution.py:141
  10.4 261.7 %copy-start.45 = (f32[160,128]{1,0:T(8,128)}, f32[160,128]{1,0:T(8,128)S(1)}, u32[]{:S(2)}) copy-start(f32[160,128]{1,0:T(8,128)S(1)} %get-tuple-element.598) | copy-start | bytes 245764
  10.5 262.5 %copy-start.43 = (f32[160,128]{1,0:T(8,128)}, f32[160,128]{1,0:T(8,128)S(1)}, u32[]{:S(2)}) copy-start(f32[160,128]{1,0:T(8,128)S(1)} %get-tuple-element.597) | copy-start | bytes 245764
  11.3 377.1 %copy-start.59 = (f32[160]{0:T(256)}, f32[160]{0:T(256)S(1)}, u32[]{:S(2)}) copy-start(f32[160]{0:T(256)S(1)} %get-tuple-element.590) | copy-start | bytes 1924
  11.3 262.6 %copy-start.65 = (f32[2048]{0:T(1024)}, f32[2048]{0:T(1024)S(1)}, u32[]{:S(2)}) copy-start(f32[2048]{0:T(1024)S(1)} %get-tuple-element.601) | copy-start | bytes 24580
  11.3 262.6 %copy-start.67 = (f32[2048]{0:T(1024)}, f32[2048]{0:T(1024)S(1)}, u32[]{:S(2)}) copy-start(f32[2048]{0:T(1024)S(1)} %get-tuple-element.602) | copy-start | bytes 24580
  142.7 131.2 %copy-start.14 = (f32[160,2048]{1,0:T(8,128)}, f32[160,2048]{1,0:T(8,128)S(1)}, u32[]{:S(2)}) copy-start(f32[160,2048]{1,0:T(8,128)S(1)} %fusion.149) | copy-start | bytes 3932164
  143.0 127.4 %copy-start.7 = (f32[20,8,16,128]{3,2,1,0:T(8,128)}, f32[20,8,16,128]{3,2,1,0:T(8,128)S(1)}, u32[]{:S(2)}) copy-start(f32[20,8,16,128]{3,2,1,0:T(8,128)S(1)} %copy.254) | copy-start | bytes 3932164
  277.5 285.0 %all-gather.9.cloned.1.call-start = ((), (), s32[]{:S(2)}) async-start(), calls=%async_computation.15 | async-start | bytes 5898240 | tf_op jit(solution)/shard_map/all_gather | solution.py:142
  394.2 293.5 %all-gather.17.cloned.1.call-start = ((), (), s32[]{:S(2)}) async-start(), calls=%async_computation.19 | async-start | bytes 9437184 | tf_op jit(solution)/shard_map/all_gather | solution.py:116
  395.7 1048.2 %copy-start.79 = (f32[160]{0:T(256)}, f32[160]{0:T(256)S(1)}, u32[]{:S(2)}) copy-start(f32[160]{0:T(256)S(1)} %get-tuple-element.541) | copy-start | bytes 1924
  396.3 87.0 %copy-start.57 = (pred[160,8]{0,1:T(8,128)(4,1)}, pred[160,8]{0,1:T(8,128)(4,1)S(1)}, u32[]{:S(2)}) copy-start(pred[160,8]{0,1:T(8,128)(4,1)S(1)} %get-tuple-element.578) | copy-start | bytes 3844
  396.3 87.0 %copy-start.69 = (s32[160,8]{0,1:T(8,128)}, s32[160,8]{0,1:T(8,128)S(1)}, u32[]{:S(2)}) copy-start(s32[160,8]{0,1:T(8,128)S(1)} %get-tuple-element.538) | copy-start | bytes 15364
  396.3 506.8 %copy-start.116 = (pred[160]{0:T(512)(128)(4,1)}, pred[160]{0:T(512)(128)(4,1)S(1)}, u32[]{:S(2)}) copy-start(pred[160]{0:T(512)(128)(4,1)S(1)} %get-tuple-element.472) | copy-start | bytes 484
  396.3 506.8 %copy-start.119 = (pred[160]{0:T(512)(128)(4,1)}, pred[160]{0:T(512)(128)(4,1)S(1)}, u32[]{:S(2)}) copy-start(pred[160]{0:T(512)(128)(4,1)S(1)} %get-tuple-element.473) | copy-start | bytes 484
  396.4 506.8 %copy-start.122 = (pred[160]{0:T(512)(128)(4,1)}, pred[160]{0:T(512)(128)(4,1)S(1)}, u32[]{:S(2)}) copy-start(pred[160]{0:T(512)(128)(4,1)S(1)} %get-tuple-element.474) | copy-start | bytes 484
  396.4 506.8 %copy-start.125 = (pred[160]{0:T(512)(128)(4,1)}, pred[160]{0:T(512)(128)(4,1)S(1)}, u32[]{:S(2)}) copy-start(pred[160]{0:T(512)(128)(4,1)S(1)} %get-tuple-element.475) | copy-start | bytes 484
  396.4 506.8 %copy-start.128 = (pred[160]{0:T(512)(128)(4,1)}, pred[160]{0:T(512)(128)(4,1)S(1)}, u32[]{:S(2)}) copy-start(pred[160]{0:T(512)(128)(4,1)S(1)} %get-tuple-element.476) | copy-start | bytes 484
  396.4 506.8 %copy-start.131 = (pred[160]{0:T(512)(128)(4,1)}, pred[160]{0:T(512)(128)(4,1)S(1)}, u32[]{:S(2)}) copy-start(pred[160]{0:T(512)(128)(4,1)S(1)} %get-tuple-element.477) | copy-start | bytes 484
  396.4 506.8 %copy-start.134 = (pred[160]{0:T(512)(128)(4,1)}, pred[160]{0:T(512)(128)(4,1)S(1)}, u32[]{:S(2)}) copy-start(pred[160]{0:T(512)(128)(4,1)S(1)} %get-tuple-element.478) | copy-start | bytes 484
  396.4 506.8 %copy-start.137 = (pred[160]{0:T(512)(128)(4,1)}, pred[160]{0:T(512)(128)(4,1)S(1)}, u32[]{:S(2)}) copy-start(pred[160]{0:T(512)(128)(4,1)S(1)} %get-tuple-element.479) | copy-start | bytes 484
  396.4 506.8 %copy-start.91 = (s32[160,1]{0,1:T(1,128)}, s32[160,1]{0,1:T(1,128)S(1)}, u32[]{:S(2)}) copy-start(s32[160,1]{0,1:T(1,128)S(1)} %get-tuple-element.579) | copy-start | bytes 1924
  396.4 506.8 %copy-start.94 = (s32[160,1]{0,1:T(1,128)}, s32[160,1]{0,1:T(1,128)S(1)}, u32[]{:S(2)}) copy-start(s32[160,1]{0,1:T(1,128)S(1)} %get-tuple-element.580) | copy-start | bytes 1924
  396.4 506.8 %copy-start.97 = (s32[160,1]{0,1:T(1,128)}, s32[160,1]{0,1:T(1,128)S(1)}, u32[]{:S(2)}) copy-start(s32[160,1]{0,1:T(1,128)S(1)} %get-tuple-element.581) | copy-start | bytes 1924
  396.5 506.8 %copy-start.100 = (s32[160,1]{0,1:T(1,128)}, s32[160,1]{0,1:T(1,128)S(1)}, u32[]{:S(2)}) copy-start(s32[160,1]{0,1:T(1,128)S(1)} %get-tuple-element.582) | copy-start | bytes 1924
  396.5 506.8 %copy-start.103 = (s32[160,1]{0,1:T(1,128)}, s32[160,1]{0,1:T(1,128)S(1)}, u32[]{:S(2)}) copy-start(s32[160,1]{0,1:T(1,128)S(1)} %get-tuple-element.583) | copy-start | bytes 1924
  396.5 506.8 %copy-start.106 = (s32[160,1]{0,1:T(1,128)}, s32[160,1]{0,1:T(1,128)S(1)}, u32[]{:S(2)}) copy-start(s32[160,1]{0,1:T(1,128)S(1)} %get-tuple-element.584) | copy-start | bytes 1924
  396.5 506.8 %copy-start.109 = (s32[160,1]{0,1:T(1,128)}, s32[160,1]{0,1:T(1,128)S(1)}, u32[]{:S(2)}) copy-start(s32[160,1]{0,1:T(1,128)S(1)} %get-tuple-element.585) | copy-start | bytes 1924
  396.5 506.8 %copy-start.112 = (s32[160,1]{0,1:T(1,128)}, s32[160,1]{0,1:T(1,128)S(1)}, u32[]{:S(2)}) copy-start(s32[160,1]{0,1:T(1,128)S(1)} %get-tuple-element.586) | copy-start | bytes 1924
  606.7 81.0 %copy-start.71 = (f32[16,160]{1,0:T(8,128)}, f32[16,160]{1,0:T(8,128)S(1)}, u32[]{:S(2)}) copy-start(f32[16,160]{1,0:T(8,128)S(1)} %get-tuple-element.791) | copy-start | bytes 30724
  606.7 86.3 %copy-start.39 = (s32[1280]{0:T(1024)}, s32[1280]{0:T(1024)S(1)}, u32[]{:S(2)}) copy-start(s32[1280]{0:T(1024)S(1)} %get-tuple-element.924) | copy-start | bytes 15364
  606.7 86.3 %copy-start.55 = (s32[160]{0:T(256)}, s32[160]{0:T(256)S(1)}, u32[]{:S(2)}) copy-start(s32[160]{0:T(256)S(1)} %get-tuple-element.929) | copy-start | bytes 1924
  694.2 196.8 %copy-start.30 = (bf16[160,2048]{1,0:T(8,128)(2,1)}, bf16[160,2048]{1,0:T(8,128)(2,1)S(1)}, u32[]{:S(2)}) copy-start(bf16[160,2048]{1,0:T(8,128)(2,1)S(1)} %multiply_convert_fusion.1) | copy-start | bytes 1966084
  722.5 209.5 %all-to-all-start = ((bf16[8,2,100,2048]{3,1,2,0:T(2,128)(2,1)}), bf16[8,2,100,2048]{3,1,2,0:T(2,128)(2,1)}, u32[]{:S(2)}, u32[]{:S(2)}) async-start(bf16[8,2,100,2048]{3,1,2,0:T(2,128)(2,1)} %copy.194), calls=%async_computation | async-start | bytes 13107200 | tf_op jit(solution)/shard_map/all_to_all | solution.py:200
  891.9 11.3 copy-start.32
  932.1 143.7 %all-to-all-start.2 = ((bf16[8,2,100,2048]{3,1,2,0:T(2,128)(2,1)}), bf16[8,2,100,2048]{3,1,2,0:T(2,128)(2,1)}, u32[]{:S(2)}, u32[]{:S(2)}) async-start(bf16[8,2,100,2048]{3,1,2,0:T(2,128)(2,1)} %copy.201), calls=%async_computation.2 | async-start | bytes 13107200 | tf_op jit(solution)/shard_map/all_to_all | solution.py:223
  1123.4 147.8 %all-to-all-start.1 = ((bf16[8,2,100,2048]{3,1,2,0:T(2,128)(2,1)}), bf16[8,2,100,2048]{3,1,2,0:T(2,128)(2,1)}, u32[]{:S(2)}, u32[]{:S(2)}) async-start(bf16[8,2,100,2048]{3,1,2,0:T(2,128)(2,1)} %copy.197), calls=%async_computation.1 | async-start | bytes 13107200 | tf_op jit(solution)/shard_map/all_to_all | solution.py:211
  1170.0 106.0 %copy-start.70 = (s32[160,8]{0,1:T(8,128)S(1)}, s32[160,8]{0,1:T(8,128)}, u32[]{:S(2)}) copy-start(s32[160,8]{0,1:T(8,128)} %copy-done.69) | copy-start | bytes 15364
  1170.0 106.2 %copy-start.83 = (pred[160,8]{0,1:T(8,128)(4,1)S(1)}, pred[160,8]{0,1:T(8,128)(4,1)}, u32[]{:S(2)}) copy-start(pred[160,8]{0,1:T(8,128)(4,1)} %get-tuple-element.537) | copy-start | bytes 3844
  1271.2 147.6 %all-to-all-start.3 = ((bf16[8,2,100,2048]{3,1,2,0:T(2,128)(2,1)}), bf16[8,2,100,2048]{3,1,2,0:T(2,128)(2,1)}, u32[]{:S(2)}, u32[]{:S(2)}) async-start(bf16[8,2,100,2048]{3,1,2,0:T(2,128)(2,1)} %copy.203), calls=%async_computation.3 | async-start | bytes 13107200 | tf_op jit(solution)/shard_map/all_to_all | solution.py:274
  1276.0 383.1 %reduce-scatter.13.cloned.1.call-start = ((), (), s32[]{:S(2)}) async-start(), calls=%async_computation.20 | async-start | bytes 5898240 | tf_op jit(solution)/shard_map/reduce_scatter | solution.py:340
  1315.4 127.3 %copy-start.63 = (bf16[160,16]{0,1:T(8,128)(2,1)}, bf16[160,16]{0,1:T(8,128)(2,1)S(1)}, u32[]{:S(2)}) copy-start(bf16[160,16]{0,1:T(8,128)(2,1)S(1)} %select_reduce_fusion) | copy-start | bytes 15364
  1427.7 9.0 copy-start.104
  1427.7 9.0 copy-start.107
  1427.7 9.0 copy-start.110
  1427.7 9.0 copy-start.113
  1427.7 9.0 copy-start.117
  1427.7 9.0 copy-start.120
  1549.8 207.7 %reduce-scatter.31.cloned.1.call-start = ((), (), s32[]{:S(2)}) async-start(), calls=%async_computation.29 | async-start | bytes 5898240
  1558.1 273.5 %reduce-scatter.29.cloned.1.call-start = ((), (), s32[]{:S(2)}) async-start(), calls=%async_computation.28 | async-start | bytes 10485760 | tf_op jit(solution)/shard_map/reduce_scatter | solution.py:270
  1577.0 329.0 %reduce-scatter.25.cloned.1.call-start = ((), (), s32[]{:S(2)}) async-start(), calls=%async_computation.26 | async-start | bytes 10485760 | tf_op jit(solution)/shard_map/reduce_scatter | solution.py:264
  1612.8 367.5 %reduce-scatter.27.cloned.1.call-start = ((), (), s32[]{:S(2)}) async-start(), calls=%async_computation.27 | async-start | bytes 10485760 | tf_op jit(solution)/shard_map/reduce_scatter | solution.py:267
  1648.3 484.9 %reduce-scatter.21.cloned.1.call-start = ((), (), s32[]{:S(2)}) async-start(), calls=%async_computation.24 | async-start | bytes 9437184 | tf_op jit(solution)/shard_map/reduce_scatter | solution.py:384
  1656.5 628.5 %reduce-scatter.15.cloned.1.call-start = ((), (), s32[]{:S(2)}) async-start(), calls=%async_computation.21 | async-start | bytes 9437184 | tf_op jit(solution)/shard_map/reduce_scatter | solution.py:375
  1683.6 753.3 %reduce-scatter.17.cloned.1.call-start = ((), (), s32[]{:S(2)}) async-start(), calls=%async_computation.22 | async-start | bytes 9437184 | tf_op jit(solution)/shard_map/reduce_scatter | solution.py:378
  1690.5 897.9 %reduce-scatter.19.cloned.1.call-start = ((), (), s32[]{:S(2)}) async-start(), calls=%async_computation.23 | async-start | bytes 9437184 | tf_op jit(solution)/shard_map/reduce_scatter | solution.py:381
  1764.8 880.3 %reduce-scatter.23.cloned.1.call-start = ((), (), s32[]{:S(2)}) async-start(), calls=%async_computation.25 | async-start | bytes 73728 | tf_op jit(solution)/shard_map/reduce_scatter | solution.py:387
  1777.8 954.9 %all-reduce.9.cloned.1.call-start = ((), (), s32[]{:S(2)}) async-start(), calls=%async_computation.30 | async-start | bytes 8388608 | tf_op jit(solution)/shard_map/psum | solution.py:426
  1910.0 74.3 %copy-start.29 = (bf16[160,2048]{1,0:T(8,128)(2,1)S(1)}, bf16[160,2048]{1,0:T(8,128)(2,1)}, u32[]{:S(2)}) copy-start(bf16[160,2048]{1,0:T(8,128)(2,1)} %copy-done.28) | copy-start | bytes 1966084
  2596.3 61.7 %copy-start.89 = (f32[160]{0:T(256)S(1)}, f32[160]{0:T(256)}, u32[]{:S(2)}) copy-start(f32[160]{0:T(256)} %get-tuple-element.589) | copy-start | bytes 1924
  (152 other events, 550.5 us)
Sparse Core Ops, SparseCore 0:
  10.1 127.6 all-gather.12
  139.9 123.1 all-gather.10
  265.2 123.1 all-gather.6
  391.0 84.4 all-gather.14
  478.0 84.4 all-gather.8
  564.5 123.1 all-gather.16
  1549.9 101.6 reduce-scatter.12
  1655.2 102.3 reduce-scatter.30
  1760.1 71.4 reduce-scatter.28
  1834.2 71.6 reduce-scatter.24
  1908.6 71.7 reduce-scatter.26
  1984.2 148.9 reduce-scatter.20
  2136.9 148.0 reduce-scatter.14
  2288.9 148.0 reduce-scatter.16
  2440.4 148.0 reduce-scatter.18
  2592.3 52.6 reduce-scatter.22
  2647.6 85.1 all-reduce.8
where the time goes:
time: 2760 us; the launch traced here: 2750 us
  waiting for transfers between devices  1860 us (67%)
  matrix products  331 us (12%)
  local copies, waits for them, and re-layouts  264 us (10%)
  blocking collectives  193 us (7%)
  other arithmetic  56.2 us (2%)
    all_gather x1, blocking collectives, body(): lax.all_gather(router_weight, 'ep', axis=0, tiled=True)  163 us
    reduce_scatter x1, waiting for transfers between devices, body(): lax.psum_scatter(key_part.astype(jnp.bfloat16), 'ep', scatter_dimension=0...  152 us
    reduce_scatter x1, waiting for transfers between devices, body(): lax.psum_scatter(query_part.astype(jnp.bfloat16), 'ep', scatter_dimension...  152 us
    reduce_scatter x1, waiting for transfers between devices, body(): lax.psum_scatter(value_part.astype(jnp.bfloat16), 'ep', scatter_dimension...  152 us
    reduce_scatter x1, waiting for transfers between devices, body(): lax.psum_scatter(output_part.astype(jnp.bfloat16), 'ep', scatter_dimensio...  141 us
    all_gather x1, waiting for transfers between devices, body(): lax.all_gather(key_weight, 'ep', axis=0, tiled=True)  126 us
    all_gather x1, waiting for transfers between devices, body(): lax.all_gather(query_weight, 'ep', axis=0, tiled=True)  120 us
    all_gather x1, waiting for transfers between devices, body(): lax.all_gather(value_weight, 'ep', axis=0, tiled=True)  111 us
  transfers between devices with their start and end apart: 21, of which 19 were waited for; matrix products, arithmetic and copies ran while one was open for 15% of the time, Pallas kernels for 0%

commit v1 on v0

v1 whole, which is shorter than its diff:
```python
import jax
import jax.numpy as jnp
from jax import lax
from jax.sharding import PartitionSpec as P

epsilon = 1e-05
rope_base = 10000.0
masked_value = -1e30
low_type = jnp.bfloat16
wide_type = jnp.float32


def inverse_rms(values):
    return lax.rsqrt(jnp.mean(values * values, axis=-1, keepdims=True) + epsilon)


def norm_backward(values, inverse, gain_vector, upstream):
    scaled = upstream * gain_vector
    inner_mean = jnp.mean(scaled * values, axis=-1, keepdims=True)
    result = inverse * scaled - values * (inverse * inverse * inverse) * inner_mean
    return (result, upstream * values * inverse)


def rope_tables(position, dimension):
    halfway = dimension // 2
    indices = jnp.arange(halfway, dtype=wide_type)
    frequency = rope_base ** (-2.0 * indices / dimension)
    angles = position.astype(wide_type)[:, None] * frequency[None, :]
    cosine = jnp.cos(angles)
    sine_part = jnp.sin(angles)
    return (
        jnp.concatenate([cosine, cosine], axis=-1),
        jnp.concatenate([sine_part, sine_part], axis=-1),
    )


def turn_half(values):
    halfway = values.shape[-1] // 2
    return jnp.concatenate([-values[..., halfway:], values[..., :halfway]], axis=-1)


def turn_back(values):
    halfway = values.shape[-1] // 2
    return jnp.concatenate([values[..., halfway:], -values[..., :halfway]], axis=-1)


def row_meta(lengths, group_order):
    boundary = jnp.cumsum(lengths)
    passed = (group_order[:, None] >= boundary[None, :]).astype(jnp.int32)
    segment = jnp.sum(passed, axis=1)
    offset = jnp.sum(passed * lengths[None, :], axis=1)
    return (segment, group_order - offset)


def mm(left, right, left_dim, right_dim):
    return lax.dot_general(
        left,
        right,
        (((left_dim,), (right_dim,)), ((), ())),
        preferred_element_type=wide_type,
    )


def gather_rows(values):
    return lax.all_gather(values, "ep", axis=0, tiled=True)


def scatter_rows(values):
    return lax.psum_scatter(
        values.astype(low_type), "ep", scatter_dimension=0, tiled=True
    ).astype(wide_type)


def body(
    tokens,
    cotangent,
    seq_lengths,
    token_order,
    routes,
    slot_index,
    query_weight,
    key_weight,
    value_weight,
    output_weight,
    router_weight,
    prenorm_gain,
    querynorm_gain,
    keynorm_gain,
    postnorm_gain,
    gate_weight,
    up_weight,
    down_weight,
):
    group_count = lax.axis_size("ep")
    device = lax.axis_index("ep")
    row_count, model_width = tokens.shape
    head_dim = querynorm_gain.shape[0]
    width_here = model_width // group_count
    heads_here = width_here // head_dim
    experts_here = gate_weight.shape[0]
    expert_total = experts_here * group_count
    top_count = routes.shape[1]
    capacity = row_count * top_count * 5 // (4 * expert_total)
    group_rows = row_count * group_count
    sequence_count = seq_lengths.shape[1]
    score_scale = head_dim ** (-0.5)

    segment, position = row_meta(seq_lengths[0], token_order[0])
    segment_own = lax.dynamic_slice_in_dim(segment, device * row_count, row_count)
    valid_own = (segment_own < sequence_count).astype(wide_type)[:, None]
    valid_all = (segment < sequence_count).astype(wide_type)[:, None]

    expert_ids = jnp.arange(expert_total, dtype=jnp.int32)
    route_code = jnp.zeros((row_count, expert_total), jnp.int32)
    for column in range(top_count):
        hit = routes[:, column, None] == expert_ids[None, :]
        kept = (slot_index[:, column, None] < capacity).astype(jnp.int32)
        route_code = route_code + jnp.where(hit, 1 + kept, 0)
    small_sent = jnp.concatenate([route_code.astype(low_type), router_weight], axis=0)

    token_all = gather_rows(tokens)
    projections = jnp.concatenate(
        [
            piece.reshape(width_here, group_count, width_here)
            for piece in (query_weight, key_weight, value_weight)
        ],
        axis=2,
    ).transpose(1, 0, 2)
    head_weight = lax.all_to_all(
        projections, "ep", split_axis=0, concat_axis=0, tiled=True
    ).reshape(model_width, 3 * width_here)
    small_all = gather_rows(small_sent).reshape(
        group_count, row_count + width_here, expert_total
    )
    code_all = small_all[:, :row_count].reshape(group_rows, expert_total)
    full_router = small_all[:, row_count:].reshape(model_width, expert_total)
    cot_all = gather_rows(cotangent)

    token_wide = token_all.astype(wide_type)
    inverse_all = inverse_rms(token_wide)
    first_all = (token_wide * inverse_all * prenorm_gain).astype(low_type)
    raw = mm(first_all, head_weight, 1, 0)
    cosine, sine_part = rope_tables(position, head_dim)

    up_stream = [mm(cot_all, down_weight[e], 1, 1) for e in range(experts_here)]

    allowed = segment[:, None] == segment[None, :]

    def head_columns(values, block, head):
        start = block * width_here + head * head_dim
        return values[:, start : start + head_dim]

    kept_heads = []
    mixed_parts = []
    for head in range(heads_here):
        query_raw = head_columns(raw, 0, head)
        key_raw = head_columns(raw, 1, head)
        query_inverse = inverse_rms(query_raw)
        key_inverse = inverse_rms(key_raw)
        query_normed = query_raw * query_inverse * querynorm_gain
        key_normed = key_raw * key_inverse * keynorm_gain
        query_low = (query_normed * cosine + turn_half(query_normed) * sine_part).astype(
            low_type
        )
        key_low = (key_normed * cosine + turn_half(key_normed) * sine_part).astype(low_type)
        value_low = head_columns(raw, 2, head).astype(low_type)
        scores = jnp.where(allowed, mm(query_low, key_low, 1, 1) * score_scale, masked_value)
        top_score = jnp.max(scores, axis=-1, keepdims=True)
        powers = jnp.exp(scores - top_score)
        log_total = top_score + jnp.log(jnp.sum(powers, axis=-1, keepdims=True))
        weights_low = jnp.exp(scores - log_total).astype(low_type)
        mixed_parts.append(mm(weights_low, value_low, 1, 0).astype(low_type))
        kept_heads.append(
            (query_raw, key_raw, query_inverse, key_inverse, query_low, key_low, value_low, log_total)
        )
    mixed_low = jnp.concatenate(mixed_parts, axis=1)

    attention = scatter_rows(mm(mixed_low, output_weight, 1, 0))
    residual = tokens.astype(wide_type) + attention
    inverse_two = inverse_rms(residual)
    second_input = (residual * inverse_two * postnorm_gain).astype(low_type)
    second_all = gather_rows(second_input)

    def gate_table(rows, code):
        logits = mm(rows, full_router, 1, 0)
        shifted = jnp.where(code > 0, logits, masked_value)
        powers = jnp.exp(shifted - jnp.max(shifted, axis=1, keepdims=True))
        return powers / jnp.sum(powers, axis=1, keepdims=True)

    gates_all = gate_table(second_all, code_all)
    masked_gates = jnp.where(code_all > 1, gates_all, 0.0) * valid_all
    gates_here = lax.dynamic_slice_in_dim(masked_gates, device * experts_here, experts_here, 1)
    kept_here = lax.dynamic_slice_in_dim(
        jnp.where(code_all > 1, valid_all, 0.0), device * experts_here, experts_here, 1
    )

    mixture_part = jnp.zeros((group_rows, model_width), wide_type)
    second_part = jnp.zeros((group_rows, model_width), wide_type)
    pair_parts = []
    gate_parts, up_parts, down_parts = [], [], []
    for e in range(experts_here):
        gate_linear = mm(second_all, gate_weight[e], 1, 0)
        up_linear = mm(second_all, up_weight[e], 1, 0)
        sigmoid_gate = jax.nn.sigmoid(gate_linear)
        silu_gate = gate_linear * sigmoid_gate
        inner = silu_gate * up_linear
        gate_column = gates_here[:, e : e + 1]
        inner_scaled = (gate_column * inner).astype(low_type)
        pair_parts.append(
            kept_here[:, e : e + 1] * jnp.sum(inner * up_stream[e], axis=1, keepdims=True)
        )
        hidden_grad = gate_column * up_stream[e]
        gate_back = (
            hidden_grad * up_linear * sigmoid_gate * (1.0 + gate_linear * (1.0 - sigmoid_gate))
        ).astype(low_type)
        up_back = (hidden_grad * silu_gate).astype(low_type)
        mixture_part = mixture_part + mm(inner_scaled, down_weight[e], 1, 0)
        second_part = (
            second_part + mm(gate_back, gate_weight[e], 1, 1) + mm(up_back, up_weight[e], 1, 1)
        )
        down_parts.append(mm(inner_scaled, cot_all, 0, 0).astype(low_type))
        gate_parts.append(mm(second_all, gate_back, 0, 0).astype(low_type))
        up_parts.append(mm(second_all, up_back, 0, 0).astype(low_type))

    pair_sent = jnp.concatenate(pair_parts, axis=1).reshape(
        group_count, row_count, experts_here
    )
    pair_grad = (
        lax.all_to_all(pair_sent, "ep", split_axis=0, concat_axis=0, tiled=True)
        .transpose(1, 0, 2)
        .reshape(row_count, expert_total)
    )
    second_scattered = scatter_rows(second_part)
    mixture = scatter_rows(mixture_part)
    layer_out = (valid_own * (residual + mixture)).astype(low_type)

    code_own = route_code
    gates_own = gate_table(second_input, code_own)
    chosen_grad = gates_own * (
        pair_grad - jnp.sum(gates_own * pair_grad, axis=1, keepdims=True)
    )
    logits_grad = jnp.where(code_own > 0, chosen_grad, 0.0).astype(low_type)
    router_part = mm(second_input, logits_grad, 0, 0)
    second_grad = mm(logits_grad, full_router, 1, 1) + second_scattered
    upstream = valid_own * cotangent.astype(wide_type)
    post_back, postnorm_part = norm_backward(residual, inverse_two, postnorm_gain, second_grad)
    residual_grad = upstream + post_back
    attention_low = residual_grad.astype(low_type)
    attention_all = gather_rows(attention_low)
    mixed_grad = mm(attention_all, output_weight, 1, 1).astype(low_type)
    output_part = mm(mixed_low, attention_all, 0, 0).astype(low_type)

    query_parts, key_parts, value_parts = [], [], []
    querynorm_part = jnp.zeros((head_dim,), wide_type)
    keynorm_part = jnp.zeros((head_dim,), wide_type)
    for head in range(heads_here):
        (query_raw, key_raw, query_inverse, key_inverse, query_low, key_low, value_low, log_total) = (
            kept_heads[head]
        )
        grad_head = mixed_grad[:, head * head_dim : (head + 1) * head_dim]
        scores = jnp.where(allowed, mm(query_low, key_low, 1, 1) * score_scale, masked_value)
        weights = jnp.exp(scores - log_total)
        weight_grad = mm(grad_head, value_low, 1, 1)
        row_dot = jnp.sum(weights * weight_grad, axis=-1, keepdims=True)
        score_grad = (weights * (weight_grad - row_dot)).astype(low_type)
        query_back = mm(score_grad, key_low, 1, 0) * score_scale
        key_back = mm(score_grad, query_low, 0, 0) * score_scale
        value_back = mm(weights.astype(low_type), grad_head, 0, 0)
        query_unturned = query_back * cosine + turn_back(query_back * sine_part)
        key_unturned = key_back * cosine + turn_back(key_back * sine_part)
        query_before, query_gain_part = norm_backward(
            query_raw, query_inverse, querynorm_gain, query_unturned
        )
        key_before, key_gain_part = norm_backward(
            key_raw, key_inverse, keynorm_gain, key_unturned
        )
        querynorm_part = querynorm_part + jnp.sum(query_gain_part, axis=0)
        keynorm_part = keynorm_part + jnp.sum(key_gain_part, axis=0)
        query_parts.append(query_before.astype(low_type))
        key_parts.append(key_before.astype(low_type))
        value_parts.append(value_back.astype(low_type))
    sent = jnp.concatenate(query_parts + key_parts + value_parts, axis=1)
    first_grad = scatter_rows(mm(sent, head_weight, 1, 1))
    head_part = mm(first_all, sent, 0, 0).astype(low_type)
    head_rows = lax.all_to_all(
        head_part.reshape(group_count, width_here, 3 * width_here),
        "ep",
        split_axis=0,
        concat_axis=0,
        tiled=True,
    )
    weight_sums = lax.psum(
        tuple(
            head_rows[:, :, block * width_here : (block + 1) * width_here]
            .transpose(1, 0, 2)
            .reshape(width_here, model_width)
            for block in range(3)
        )
        + (output_part,),
        "rep",
    )
    query_grad, key_grad, value_grad, output_grad = (
        piece.astype(wide_type) for piece in weight_sums
    )

    token_own = tokens.astype(wide_type)
    inverse_one = inverse_rms(token_own)
    pre_back, prenorm_part = norm_backward(token_own, inverse_one, prenorm_gain, first_grad)
    token_grad = residual_grad + pre_back

    small_parts = jnp.concatenate(
        [
            router_part.reshape(group_count, -1),
            jnp.sum(prenorm_part, axis=0).reshape(group_count, -1),
            jnp.sum(postnorm_part, axis=0).reshape(group_count, -1),
            querynorm_part.reshape(group_count, -1),
            keynorm_part.reshape(group_count, -1),
        ],
        axis=1,
    )
    small_sum = lax.psum(
        lax.psum_scatter(small_parts, "ep", scatter_dimension=0, tiled=True), "rep"
    ).reshape(-1)
    sizes = (width_here * expert_total, width_here, width_here) + 2 * (head_dim // group_count,)
    pieces = []
    start = 0
    for size in sizes:
        pieces.append(small_sum[start : start + size])
        start += size
    router_grad = pieces[0].reshape(width_here, expert_total)
    prenorm_grad, postnorm_grad, querynorm_grad, keynorm_grad = pieces[1:]

    gate_total, up_total, down_total = (
        lax.psum_scatter(
            jnp.stack(parts), "rep", scatter_dimension=1, tiled=True
        ).astype(wide_type)
        for parts in (gate_parts, up_parts, down_parts)
    )
    return (
        layer_out,
        token_grad,
        query_grad,
        key_grad,
        value_grad,
        output_grad,
        router_grad,
        prenorm_grad,
        querynorm_grad,
        keynorm_grad,
        postnorm_grad,
        gate_total,
        up_total,
        down_total,
    )


def solution(mesh):
    in_specs = (
        P(("rep", "ep"), None),
        P(("rep", "ep"), None),
        P("rep", None),
        P("rep", None),
        P(("rep", "ep"), None),
        P(("rep", "ep"), None),
        P("ep", None),
        P("ep", None),
        P("ep", None),
        P("ep", None),
        P("ep", None),
        P(),
        P(),
        P(),
        P(),
        P("ep", None, None),
        P("ep", None, None),
        P("ep", None, None),
    )
    out_specs = (
        P(("rep", "ep"), None),
        P(("rep", "ep"), None),
        P("ep", None),
        P("ep", None),
        P("ep", None),
        P("ep", None),
        P("ep", None),
        P("ep"),
        P("ep"),
        P("ep"),
        P("ep"),
        P("ep", "rep", None),
        P("ep", "rep", None),
        P("ep", "rep", None),
    )
    return jax.shard_map(body, mesh=mesh, in_specs=in_specs, out_specs=out_specs, check_vma=False)
```

time: 2760 us -> 1370 us (0.50)
  waiting for transfers between devices: 1860 us -> 928 us
  local copies, waits for them, and re-layouts: 264 us -> 27.1 us
  blocking collectives: 193 us -> 41.5 us
  matrix products: 331 us -> 264 us
    all_gather x6 -> x4, waiting for transfers between devices: 596 us -> 131 us  [gather_rows(): return lax.all_gather(values, 'ep', axis=0, tiled=True)]
    reduce_scatter x9 -> x7, waiting for transfers between devices: 813 us -> 445 us  [the longest x4 369 us: scatter_rows(): lax.psum_scatter(values.astype(low_type), 'ep', scatter_dimension=0, tile...]
    all_gather x1, blocking collectives: 163 us -> 31.2 us  [gather_rows(): return lax.all_gather(values, 'ep', axis=0, tiled=True)]
    all_to_all x4 -> x3, waiting for transfers between devices: 310 us -> 199 us  [the longest x1 126 us: body(): lax.all_to_all(projections, 'ep', split_axis=0, concat_axis=0, tiled=True)]
    dot_general x85 -> x40, matrix products: 331 us -> 264 us  [mm(): lax.dot_general(left, right, (((left_dim,), (right_dim,)), ((), ())), pre...]
    reshape x6 -> x11, local copies, waits for them, and re-layouts: 61.6 us -> 4.74 us  [the longest x3 3.3 us: body(): weight_sums = lax.psum(tuple((head_rows[:, :, block * width_here:(block +...]
    dynamic_slice x24 -> x0, local copies, waits for them, and re-layouts: 34.6 us -> none  [the longest x16 29 us: pair_slice(): lax.dynamic_slice_in_dim(values, pair_index * pair_width, pair_width, 1)]
    unnamed x322 -> x292, local copies, waits for them, and re-layouts: 44.5 us -> 15.1 us
  transfers between devices with their start and end apart: 21 -> 16, of which waited for: 19 -> 15; matrix products, arithmetic and copies ran while one was open for 15% -> 17% of each run, Pallas kernels for 0% -> 0%
where the time goes in v1:
time: 1370 us
  waiting for transfers between devices  928 us (68%)
  matrix products  264 us (19%)
  other arithmetic  78 us (6%)
  blocking collectives  41.5 us (3%)
  local copies, waits for them, and re-layouts  27.1 us (2%)
  between operations  16.2 us (1%)
  starting transfers between devices  15.9 us (1%)
    reduce_scatter x4, waiting for transfers between devices, scatter_rows(): lax.psum_scatter(values.astype(low_type), 'ep', scatter_dimension=0, tile...  369 us
    dot_general x40, matrix products, mm(): lax.dot_general(left, right, (((left_dim,), (right_dim,)), ((), ())), pre...  264 us
    all_gather x4, waiting for transfers between devices, gather_rows(): return lax.all_gather(values, 'ep', axis=0, tiled=True)  131 us
    all_to_all x1, waiting for transfers between devices, body(): lax.all_to_all(projections, 'ep', split_axis=0, concat_axis=0, tiled=True)  126 us
    psum x1, waiting for transfers between devices, body(): lax.psum(tuple((head_rows[:, :, block * width_here:(block + 1) * width_he...  85.1 us
    reduce_scatter x3, waiting for transfers between devices, body(): lax.psum_scatter(jnp.stack(parts), 'rep', scatter_dimension=1, tiled=True)  75.7 us
    unnamed x14, waiting for transfers between devices  69.1 us
    all_to_all x1, waiting for transfers between devices, body(): lax.all_to_all(head_part.reshape(group_count, width_here, 3 * width_here)...  65.2 us
  transfers between devices with their start and end apart: 16, of which 15 were waited for; matrix products, arithmetic and copies ran while one was open for 17% of the time, Pallas kernels for 0%

profile of v1, /device:TPU:0, one launch (start us, length us, event | category | flops | bytes accessed | tf_op | source)
XLA Modules:
  0.0 1370.7 jit_solution(4074824148785817118)
XLA Ops:
  10.9 2.3 copy.75
  13.2 2.8 maximum_bitcast_fusion
  16.0 7.3 all-to-all-start
  24.9 126.5 %all-to-all-done = bf16[8,256,768]{1,2,0:T(8,128)(2,1)} async-done(((bf16[8,256,768]{1,2,0:T(8,128)(2,1)}), bf16[8,256,768]{1,2,0:T(8,128)(2,1)}, u32[]{:S(2)}, u32[]{:S(2)}) %all-to-all-start) | async-done | bytes 3145760 | tf_op jit(solution)/shard_map/all_to_all | solution.py:129
  151.4 4.8 copy.76
  158.2 3.7 fusion
  162.2 7.1 fusion.130
  180.7 3.8 convolution_convert_fusion.1
  185.4 99.1 %reduce-scatter.8.cloned.1.call-done = bf16[160,2048]{1,0:T(8,128)(2,1)} async-done(((bf16[1280,2048]{1,0:T(8,128)(2,1)}), bf16[160,2048]{1,0:T(8,128)(2,1)}) %reduce-scatter.8.cloned.1.call-update) | async-done | bytes 655376 | tf_op jit(solution)/shard_map/reduce_scatter | solution.py:69
  287.0 2.2 multiply_convert_fusion.9
  290.1 31.2 %all-gather = bf16[8,416,16]{1,2,0:T(8,128)(2,1)S(1)} all-gather(bf16[1,416,16]{1,2,0:T(8,128)(2,1)S(1)} %maximum_bitcast_fusion.1), channel_id=1, replica_groups=mesh['rep'=4,'ep'=8] {'ep'}, dimensions={0}, use_global_device_ids=true | all-gather | bytes 119808 | tf_op jit(solution)/shard_map/all_gather | solution.py:65
  321.9 51.8 %all-gather.10.cloned.1.call-done = bf16[1280,2048]{1,0:T(8,128)(2,1)} async-done(((bf16[160,2048]{1,0:T(8,128)(2,1)}), bf16[1280,2048]{1,0:T(8,128)(2,1)}) %all-gather.10.cloned.1.call-update) | async-done | bytes 5242896 | tf_op jit(solution)/shard_map/all_gather | solution.py:65
  373.7 10.9 fusion.9
  384.6 9.1 fusion.19
  393.7 66.5 %all-gather.8.cloned.1.call-done = bf16[1280,2048]{1,0:T(8,128)(2,1)} async-done(((bf16[160,2048]{1,0:T(8,128)(2,1)}), bf16[1280,2048]{1,0:T(8,128)(2,1)}) %all-gather.8.cloned.1.call-update) | async-done | bytes 5242896 | tf_op jit(solution)/shard_map/all_gather | solution.py:65
  460.2 4.1 fusion.132
  464.5 9.4 fusion.25
  473.8 15.3 %multiply_convert_fusion.5 = (bf16[1280,1024]{0,1:T(8,128)(2,1)S(1)}, f32[1280]{0:T(1024)S(1)}, bf16[1280,1024]{0,1:T(8,128)(2,1)}, bf16[1280,1024]{0,1:T(8,128)(2,1)}) fusion(f32[1280,1024]{0,1:T(8,128)} %fusion.25, f32[1280,1024]{0,1:T(8,128)} %fusion.19, f32[1280]{0:T(1024)S(1)} %get-tuple-element.96, bf16[1280,2048]{1,0:T(8,128)(2,1)S(1)} %copy-done.11, ...), kind=kOutput, calls=%fused_computation.27 | convolution fusion | flops 5393611776 | bytes 27797504 | tf_op jit(solution)/shard_map/dot_general | solution.py:56
  489.2 11.8 fusion.23
  501.0 10.7 fusion.27
  511.7 8.1 fusion.13
  519.8 15.2 %multiply_convert_fusion.3 = (bf16[1280,1024]{0,1:T(8,128)(2,1)S(1)}, f32[1280]{0:T(1024)S(1)}, bf16[1280,1024]{0,1:T(8,128)(2,1)}, bf16[1280,1024]{0,1:T(8,128)(2,1)}) fusion(f32[1280,1024]{0,1:T(8,128)} %fusion.13, f32[1280,1024]{0,1:T(8,128)} %fusion.9, f32[1280]{0:T(1024)S(1)} %get-tuple-element.95, bf16[1280,2048]{1,0:T(8,128)(2,1)S(1)} %copy-done.11, ...), kind=kOutput, calls=%fused_computation.25 | convolution fusion | flops 5393611776 | bytes 27797504 | tf_op jit(solution)/shard_map/dot_general | solution.py:56
  534.9 11.4 fusion.15
  546.4 17.0 %add_convert_fusion = bf16[1280,2048]{1,0:T(8,128)(2,1)} fusion(f32[1280,2048]{1,0:T(8,128)} %fusion.15, f32[1280,2048]{1,0:T(8,128)} %fusion.27, f32[1280,2048]{1,0:T(8,128)} %fusion.23, bf16[1280,1024]{0,1:T(8,128)(2,1)} %get-tuple-element.115, bf16[2,2048,1024]{2,1,0:T(8,128)(2,1)} %param.34), kind=kOutput, calls=%fused_computation.5 | convolution fusion | flops 5379194880 | bytes 43515904 | tf_op jit(solution)/shard_map/dot_general | solution.py:56
  563.4 8.5 fusion.21
  571.9 10.0 add_convert_fusion.1
  584.3 3.3 all-to-all-start.1
  587.8 6.9 all-to-all-done.1
  594.7 70.4 %reduce-scatter.12.cloned.1.call-done = bf16[160,2048]{1,0:T(8,128)(2,1)} async-done(((bf16[1280,2048]{1,0:T(8,128)(2,1)}), bf16[160,2048]{1,0:T(8,128)(2,1)}) %reduce-scatter.12.cloned.1.call-update) | async-done | bytes 655376 | tf_op jit(solution)/shard_map/reduce_scatter | solution.py:69
  665.1 3.5 multiply_reduce_fusion.4
  668.6 102.3 %reduce-scatter.10.cloned.1.call-done = bf16[160,2048]{1,0:T(8,128)(2,1)} async-done(((bf16[1280,2048]{1,0:T(8,128)(2,1)}), bf16[160,2048]{1,0:T(8,128)(2,1)}) %reduce-scatter.10.cloned.1.call-update) | async-done | bytes 655376 | tf_op jit(solution)/shard_map/reduce_scatter | solution.py:69
  770.9 4.0 fusion.121
  774.9 9.0 convert_bitcast_fusion
  783.9 9.6 convert_bitcast_fusion.1
  793.5 6.3 pad_maximum_fusion.2
  799.9 9.0 convert_bitcast_fusion.2
  808.9 9.7 convert_bitcast_fusion.3
  818.7 6.3 pad_maximum_fusion.1
  825.1 9.0 convert_bitcast_fusion.4
  834.1 10.1 convert_bitcast_fusion.5
  844.2 6.4 pad_maximum_fusion
  850.6 10.4 all-gather.12.cloned.1.call-done
  861.0 4.2 convolution_convert_fusion.4
  865.3 8.9 multiply_reduce_fusion
  874.2 5.1 multiply_convert_fusion
  882.9 5.0 multiply_reduce_fusion.1
  887.9 4.1 multiply_convert_fusion.1
  900.9 6.4 convolution_convert_fusion.2
  907.3 4.6 all-to-all-start.2
  912.0 5.0 convolution_convert_fusion.3
  917.0 65.2 %all-to-all-done.2 = bf16[8,256,768]{2,1,0:T(8,128)(2,1)} async-done(((bf16[8,256,768]{2,1,0:T(8,128)(2,1)}), bf16[8,256,768]{2,1,0:T(8,128)(2,1)}, u32[]{:S(2)}, u32[]{:S(2)}) %all-to-all-start.2) | async-done | bytes 3145760 | tf_op jit(solution)/shard_map/all_to_all | solution.py:285
  987.8 8.0 convolution_convert_fusion
  998.4 4.1 convert_element_type.280
  1002.5 5.6 reduce-scatter.18.cloned.1.call-done
  1008.0 4.1 convert_element_type.277
  1012.1 70.1 %reduce-scatter.16.cloned.1.call-done = bf16[2,512,1024]{2,1,0:T(8,128)(2,1)} async-done(((bf16[2,2048,1024]{2,1,0:T(8,128)(2,1)}), bf16[2,512,1024]{2,1,0:T(8,128)(2,1)}) %reduce-scatter.16.cloned.1.call-update) | async-done | bytes 2097168 | tf_op jit(solution)/shard_map/reduce_scatter | solution.py:334
  1082.2 4.1 convert_element_type.274
  1086.5 85.1 %all-reduce.7.cloned.1.call-done = (bf16[256,2048]{1,0:T(8,128)(2,1)}, bf16[256,2048]{1,0:T(8,128)(2,1)}, bf16[256,2048]{1,0:T(8,128)(2,1)}, bf16[256,2048]{1,0:T(8,128)(2,1)}) async-done(((bf16[256,2048]{1,0:T(8,128)(2,1)}, bf16[256,2048]{1,0:T(8,128)(2,1)}, bf16[256,2048]{1,0:T(8,128)(2,1)}, bf16[256,2048]{1,0:T(8,128)(2,1)}), (bf16[256,2048]{1,0:T(8,128)(2,1)}, bf16[256,2048]{1,0:T(8,128)(2,1)}, ...) | async-done | bytes 4194320 | tf_op jit(solution)/shard_map/psum | solution.py:292
  1171.6 2.9 convert_element_type.267
  1174.6 2.9 convert_element_type.268
  1180.6 97.1 %reduce-scatter.14.cloned.1.call-done = bf16[160,2048]{1,0:T(8,128)(2,1)} async-done(((bf16[1280,2048]{1,0:T(8,128)(2,1)}), bf16[160,2048]{1,0:T(8,128)(2,1)}) %reduce-scatter.14.cloned.1.call-update) | async-done | bytes 655376 | tf_op jit(solution)/shard_map/reduce_scatter | solution.py:69
  1280.0 2.5 fusion.50
  1282.6 67.5 %all-reduce.5.cloned.1.call-done = f32[8,4640]{1,0:T(8,128)} async-done(((f32[8,4640]{1,0:T(8,128)}), f32[8,4640]{1,0:T(8,128)}) %all-reduce.5.cloned.1.call-update) | async-done | bytes 148496
  1351.7 10.3 psum.39
  (414 shorter events, 54.9 us)
Async XLA Ops:
  7.2 173.6 %copy-start = (bf16[256,2048]{1,0:T(8,128)(2,1)S(1)}, bf16[256,2048]{1,0:T(8,128)(2,1)}, u32[]{:S(2)}) copy-start(bf16[256,2048]{1,0:T(8,128)(2,1)} %param.27) | copy-start | bytes 3145732
  7.2 151.0 %all-gather.6.cloned.1.call-start = ((), (), s32[]{:S(2)}) async-start(), calls=%async_computation.10 | async-start | bytes 5898240 | tf_op jit(solution)/shard_map/all_gather | solution.py:65
  13.2 10.1 copy-start.125
  13.2 10.3 copy-start.120
  16.0 135.4 %all-to-all-start = ((bf16[8,256,768]{1,2,0:T(8,128)(2,1)}), bf16[8,256,768]{1,2,0:T(8,128)(2,1)}, u32[]{:S(2)}, u32[]{:S(2)}) async-start(bf16[8,256,768]{1,2,0:T(8,128)(2,1)} %maximum_bitcast_fusion), calls=%async_computation | async-start | bytes 6291456 | tf_op jit(solution)/shard_map/all_to_all | solution.py:129
  23.3 261.3 %reduce-scatter.8.cloned.1.call-start = ((), (), s32[]{:S(2)}) async-start(), calls=%async_computation.11 | async-start | bytes 5898240 | tf_op jit(solution)/shard_map/reduce_scatter | solution.py:69
  23.6 298.2 %copy-start.52 = (s32[1280]{0:T(1024)}, s32[1280]{0:T(1024)S(1)}, u32[]{:S(2)}) copy-start(s32[1280]{0:T(1024)S(1)} %get-tuple-element.97) | copy-start | bytes 15364
  24.9 147.5 %copy-start.15 = (f32[1280,64]{0,1:T(8,128)}, f32[1280,64]{0,1:T(8,128)S(1)}, u32[]{:S(2)}) copy-start(f32[1280,64]{0,1:T(8,128)S(1)} %get-tuple-element.164) | copy-start | bytes 983044
  24.9 147.5 %copy-start.17 = (f32[1280,64]{0,1:T(8,128)}, f32[1280,64]{0,1:T(8,128)S(1)}, u32[]{:S(2)}) copy-start(f32[1280,64]{0,1:T(8,128)S(1)} %get-tuple-element.163) | copy-start | bytes 983044
  24.9 137.0 %copy-start.59 = (f32[2048]{0:T(1024)S(1)}, f32[2048]{0:T(1024)}, u32[]{:S(2)}) copy-start(f32[2048]{0:T(1024)} %param.29) | copy-start | bytes 24580
  162.2 9.3 copy-start.110
  162.2 9.3 copy-start.112
  169.3 9.4 copy-start.37
  180.7 103.8 %copy-start.5 = (bf16[160,2048]{1,0:T(8,128)(2,1)S(1)}, bf16[160,2048]{1,0:T(8,128)(2,1)}, u32[]{:S(2)}) copy-start(bf16[160,2048]{1,0:T(8,128)(2,1)} %param.18) | copy-start | bytes 1966084
  184.6 102.5 %copy-start.53 = (f32[2048]{0:T(1024)S(1)}, f32[2048]{0:T(1024)}, u32[]{:S(2)}) copy-start(f32[2048]{0:T(1024)} %param.32) | copy-start | bytes 24580
  184.6 104.7 %copy-start.114 = (s32[160,8]{0,1:T(8,128)S(1)}, s32[160,8]{0,1:T(8,128)}, u32[]{:S(2)}) copy-start(s32[160,8]{0,1:T(8,128)} %param.22) | copy-start | bytes 15364
  184.6 104.8 %copy-start.115 = (s32[160,8]{0,1:T(8,128)S(1)}, s32[160,8]{0,1:T(8,128)}, u32[]{:S(2)}) copy-start(s32[160,8]{0,1:T(8,128)} %param.23) | copy-start | bytes 15364
  184.6 105.4 %copy-start.119 = (bf16[256,16]{0,1:T(8,128)(2,1)S(1)}, bf16[256,16]{0,1:T(8,128)(2,1)}, u32[]{:S(2)}) copy-start(bf16[256,16]{0,1:T(8,128)(2,1)} %param.28) | copy-start | bytes 24580
  184.6 189.1 %all-gather.10.cloned.1.call-start = ((), (), s32[]{:S(2)}) async-start(), calls=%async_computation.14 | async-start | bytes 5898240 | tf_op jit(solution)/shard_map/all_gather | solution.py:65
  185.3 274.9 %all-gather.8.cloned.1.call-start = ((), (), s32[]{:S(2)}) async-start(), calls=%async_computation.12 | async-start | bytes 5898240 | tf_op jit(solution)/shard_map/all_gather | solution.py:65
  289.3 375.8 %reduce-scatter.12.cloned.1.call-start = ((), (), s32[]{:S(2)}) async-start(), calls=%async_computation.15 | async-start | bytes 5898240 | tf_op jit(solution)/shard_map/reduce_scatter | solution.py:69
  289.4 31.9 %copy-start.69 = (s32[160,1]{0,1:T(1,128)}, s32[160,1]{0,1:T(1,128)S(1)}, u32[]{:S(2)}) copy-start(s32[160,1]{0,1:T(1,128)S(1)} %get-tuple-element.177) | copy-start | bytes 1924
  289.4 31.9 %copy-start.71 = (s32[160,1]{0,1:T(1,128)}, s32[160,1]{0,1:T(1,128)S(1)}, u32[]{:S(2)}) copy-start(s32[160,1]{0,1:T(1,128)S(1)} %get-tuple-element.178) | copy-start | bytes 1924
  289.4 31.9 %copy-start.74 = (s32[160,1]{0,1:T(1,128)}, s32[160,1]{0,1:T(1,128)S(1)}, u32[]{:S(2)}) copy-start(s32[160,1]{0,1:T(1,128)S(1)} %get-tuple-element.179) | copy-start | bytes 1924
  289.4 31.9 %copy-start.77 = (s32[160,1]{0,1:T(1,128)}, s32[160,1]{0,1:T(1,128)S(1)}, u32[]{:S(2)}) copy-start(s32[160,1]{0,1:T(1,128)S(1)} %get-tuple-element.180) | copy-start | bytes 1924
  289.5 31.9 %copy-start.80 = (s32[160,1]{0,1:T(1,128)}, s32[160,1]{0,1:T(1,128)S(1)}, u32[]{:S(2)}) copy-start(s32[160,1]{0,1:T(1,128)S(1)} %get-tuple-element.181) | copy-start | bytes 1924
  289.5 31.9 %copy-start.83 = (s32[160,1]{0,1:T(1,128)}, s32[160,1]{0,1:T(1,128)S(1)}, u32[]{:S(2)}) copy-start(s32[160,1]{0,1:T(1,128)S(1)} %get-tuple-element.182) | copy-start | bytes 1924
  289.5 31.9 %copy-start.86 = (s32[160,1]{0,1:T(1,128)}, s32[160,1]{0,1:T(1,128)S(1)}, u32[]{:S(2)}) copy-start(s32[160,1]{0,1:T(1,128)S(1)} %get-tuple-element.183) | copy-start | bytes 1924
  289.5 31.9 %copy-start.89 = (s32[160,1]{0,1:T(1,128)}, s32[160,1]{0,1:T(1,128)S(1)}, u32[]{:S(2)}) copy-start(s32[160,1]{0,1:T(1,128)S(1)} %get-tuple-element.184) | copy-start | bytes 1924
  289.5 31.9 %copy-start.92 = (s32[160,1]{0,1:T(1,128)}, s32[160,1]{0,1:T(1,128)S(1)}, u32[]{:S(2)}) copy-start(s32[160,1]{0,1:T(1,128)S(1)} %get-tuple-element.185) | copy-start | bytes 1924
  289.5 31.9 %copy-start.95 = (s32[160,1]{0,1:T(1,128)}, s32[160,1]{0,1:T(1,128)S(1)}, u32[]{:S(2)}) copy-start(s32[160,1]{0,1:T(1,128)S(1)} %get-tuple-element.186) | copy-start | bytes 1924
  289.5 31.9 %copy-start.98 = (s32[160,1]{0,1:T(1,128)}, s32[160,1]{0,1:T(1,128)S(1)}, u32[]{:S(2)}) copy-start(s32[160,1]{0,1:T(1,128)S(1)} %get-tuple-element.187) | copy-start | bytes 1924
  289.5 31.9 %copy-start.101 = (s32[160,1]{0,1:T(1,128)}, s32[160,1]{0,1:T(1,128)S(1)}, u32[]{:S(2)}) copy-start(s32[160,1]{0,1:T(1,128)S(1)} %get-tuple-element.188) | copy-start | bytes 1924
  373.7 10.9 copy-start.126
  489.2 11.8 copy-start.130
  489.2 22.5 %slice-start.6 = ((s8[8388608]{0:T(1024)(128)(4,1)}), s8[4194304]{0:T(1024)(128)(4,1)S(1)}, s32[]{:S(2)}) async-start(s8[8388608]{0:T(1024)(128)(4,1)} %bitcast.243), calls=%async_computation.29 | async-start | bytes 8388608
  501.0 10.7 slice-start.7
  534.9 11.4 copy-start.132
  563.3 207.5 %reduce-scatter.10.cloned.1.call-start = ((), (), s32[]{:S(2)}) async-start(), calls=%async_computation.13 | async-start | bytes 5898240 | tf_op jit(solution)/shard_map/reduce_scatter | solution.py:69
  582.1 83.0 %copy-start.6 = (bf16[160,2048]{1,0:T(8,128)(2,1)S(1)}, bf16[160,2048]{1,0:T(8,128)(2,1)}, u32[]{:S(2)}) copy-start(bf16[160,2048]{1,0:T(8,128)(2,1)} %param.18) | copy-start | bytes 1966084
  582.1 83.0 %copy-start.13 = (bf16[160,2048]{1,0:T(8,128)(2,1)S(1)}, bf16[160,2048]{1,0:T(8,128)(2,1)}, u32[]{:S(2)}) copy-start(bf16[160,2048]{1,0:T(8,128)(2,1)} %reduce-scatter.8.cloned.1.call-done) | copy-start | bytes 1966084
  582.1 83.0 %copy-start.54 = (f32[2048]{0:T(1024)S(1)}, f32[2048]{0:T(1024)}, u32[]{:S(2)}) copy-start(f32[2048]{0:T(1024)} %param.32) | copy-start | bytes 24580
  582.1 83.0 %copy-start.109 = (f32[160]{0:T(256)S(1)}, f32[160]{0:T(256)}, u32[]{:S(2)}) copy-start(f32[160]{0:T(256)} %copy-done.108) | copy-start | bytes 1924
  582.1 188.8 %copy-start.123 = (f32[160]{0:T(256)S(1)}, f32[160]{0:T(256)}, u32[]{:S(2)}) copy-start(f32[160]{0:T(256)} %get-tuple-element.191) | copy-start | bytes 1924
  583.6 191.2 %copy-start.104 = (f32[160]{0:T(256)}, f32[160]{0:T(256)S(1)}, u32[]{:S(2)}) copy-start(f32[160]{0:T(256)S(1)} %get-tuple-element.201) | copy-start | bytes 1924
  584.3 10.3 all-to-all-start.1
  587.7 273.3 %all-gather.12.cloned.1.call-start = ((), (), s32[]{:S(2)}) async-start(), calls=%async_computation.16 | async-start | bytes 5898240 | tf_op jit(solution)/shard_map/all_gather | solution.py:65
  587.8 187.1 %copy-start.106 = (f32[160]{0:T(256)}, f32[160]{0:T(256)S(1)}, u32[]{:S(2)}) copy-start(f32[160]{0:T(256)S(1)} %fusion.104) | copy-start | bytes 1924
  594.7 180.1 %copy-start.121 = (f32[160]{0:T(256)}, f32[160]{0:T(256)S(1)}, u32[]{:S(2)}) copy-start(f32[160]{0:T(256)S(1)} %multiply_reduce_fusion.19) | copy-start | bytes 1924
  774.8 223.5 %reduce-scatter.20.cloned.1.call-start = ((), (), s32[]{:S(2)}) async-start(), calls=%async_computation.20 | async-start | bytes 10485760 | tf_op jit(solution)/shard_map/reduce_scatter | solution.py:334
  774.9 9.0 copy-start.128
  799.8 208.2 %reduce-scatter.18.cloned.1.call-start = ((), (), s32[]{:S(2)}) async-start(), calls=%async_computation.19 | async-start | bytes 10485760 | tf_op jit(solution)/shard_map/reduce_scatter | solution.py:334
  799.9 9.0 copy-start.133
  825.0 257.2 %reduce-scatter.16.cloned.1.call-start = ((), (), s32[]{:S(2)}) async-start(), calls=%async_computation.18 | async-start | bytes 10485760 | tf_op jit(solution)/shard_map/reduce_scatter | solution.py:334
  825.1 9.0 copy-start.131
  850.6 14.6 %copy-start.41 = (f32[1280]{0:T(1024)S(1)}, f32[1280]{0:T(1024)}, u32[]{:S(2)}) copy-start(f32[1280]{0:T(1024)} %copy-done.40) | copy-start | bytes 15364
  861.0 13.2 slice-start.2
  865.2 17.6 %slice-start = ((s8[6553600]{0:T(1024)(128)(4,1)}), s8[4194304]{0:T(1024)(128)(4,1)S(1)}, s32[]{:S(2)}) async-start(s8[6553600]{0:T(1024)(128)(4,1)} %bitcast.155), calls=%async_computation.23 | async-start | bytes 8388608
  907.3 74.9 %all-to-all-start.2 = ((bf16[8,256,768]{2,1,0:T(8,128)(2,1)}), bf16[8,256,768]{2,1,0:T(8,128)(2,1)}, u32[]{:S(2)}, u32[]{:S(2)}) async-start(bf16[8,256,768]{2,1,0:T(8,128)(2,1)} %bitcast.169), calls=%async_computation.6 | async-start | bytes 6291456 | tf_op jit(solution)/shard_map/all_to_all | solution.py:285
  911.9 259.7 %all-reduce.7.cloned.1.call-start = ((), (), s32[]{:S(2)}) async-start(), calls=%async_computation.22 | async-start | bytes 8388608 | tf_op jit(solution)/shard_map/psum | solution.py:292
  987.8 289.9 %reduce-scatter.14.cloned.1.call-start = ((), (), s32[]{:S(2)}) async-start(), calls=%async_computation.17 | async-start | bytes 5898240 | tf_op jit(solution)/shard_map/reduce_scatter | solution.py:69
  996.0 354.1 %all-reduce.5.cloned.1.call-start = ((), (), s32[]{:S(2)}) async-start(), calls=%async_computation.21 | async-start | bytes 303104
  1174.6 103.2 %copy-start.7 = (bf16[160,2048]{1,0:T(8,128)(2,1)S(1)}, bf16[160,2048]{1,0:T(8,128)(2,1)}, u32[]{:S(2)}) copy-start(bf16[160,2048]{1,0:T(8,128)(2,1)} %param.18) | copy-start | bytes 1966084
  1174.6 105.5 %copy-start.19 = (f32[160,2048]{1,0:T(8,128)S(1)}, f32[160,2048]{1,0:T(8,128)}, u32[]{:S(2)}) copy-start(f32[160,2048]{1,0:T(8,128)} %get-tuple-element.108) | copy-start | bytes 3932164
  (94 other events, 216.8 us)
Sparse Core Ops, SparseCore 0:
  10.2 147.9 all-gather.5
  184.7 99.7 reduce-scatter.7
  286.7 86.9 all-gather.9
  375.7 84.4 all-gather.7
  563.5 101.5 reduce-scatter.11
  668.5 102.2 reduce-scatter.9
  775.0 85.9 all-gather.11
  863.6 69.9 reduce-scatter.19
  936.3 71.6 reduce-scatter.17
  1010.5 71.7 reduce-scatter.15
  1085.5 86.0 all-reduce.6
  1175.0 102.6 reduce-scatter.13
  1281.0 69.0 all-reduce.4

commit v2 on v1

--- a/solution.py
+++ b/solution.py
@@ -61,14 +61,104 @@
     )
 
 
-def gather_rows(values):
-    return lax.all_gather(values, "ep", axis=0, tiled=True)
-
-
-def scatter_rows(values):
-    return lax.psum_scatter(
-        values.astype(low_type), "ep", scatter_dimension=0, tiled=True
-    ).astype(wide_type)
+def ring_order(count):
+    return [i for i in range(count) if i % 2 == 0] + [i for i in reversed(range(count)) if i % 2]
+
+
+def ring_slots(count):
+    half = count // 2
+    offsets = [0]
+    for step in range(1, half):
+        offsets += [step, -step]
+    return offsets + [half]
+
+
+def ring_shift(values, direction):
+    order = ring_order(lax.axis_size("ep"))
+    count = len(order)
+    pairs = [(order[i], order[(i + direction) % count]) for i in range(count)]
+    return lax.ppermute(values, "ep", pairs)
+
+
+def ring_gather(values):
+    half = lax.axis_size("ep") // 2
+    middle = values.shape[0] // 2
+    onward, backward = values, values
+    blocks = [values]
+    for _ in range(1, half):
+        onward, backward = ring_shift(onward, 1), ring_shift(backward, -1)
+        blocks += [backward, onward]
+    far = [ring_shift(onward[:middle], 1), ring_shift(backward[middle:], -1)]
+    return blocks + [jnp.concatenate(far, axis=0)]
+
+
+def ring_scatter(partial):
+    count = lax.axis_size("ep")
+    half = count // 2
+    rows = partial.shape[0] // count
+    middle = rows // 2
+    slot = {offset: j for j, offset in enumerate(ring_slots(count))}
+
+    def block(offset):
+        return partial[slot[offset] * rows : (slot[offset] + 1) * rows]
+
+    onward = ring_shift(block(half)[:middle], 1)
+    backward = ring_shift(block(half)[middle:], -1)
+    up, down = block(half - 1), block(1 - half)
+    onward = jnp.concatenate([add_low(onward, up[:middle]), up[middle:]], axis=0)
+    backward = jnp.concatenate([down[:middle], add_low(backward, down[middle:])], axis=0)
+    for step in range(half - 2, -1, -1):
+        onward, backward = ring_shift(onward, 1), ring_shift(backward, -1)
+        if step:
+            onward = add_low(onward, block(step))
+            backward = add_low(backward, block(-step))
+    return (
+        block(0).astype(wide_type) + onward.astype(wide_type) + backward.astype(wide_type)
+    )
+
+
+def add_low(left, right):
+    return (left.astype(wide_type) + right.astype(wide_type)).astype(low_type)
+
+
+def rep_exchange(values, distance):
+    count = lax.axis_size("rep")
+    return lax.ppermute(values, "rep", [(i, i ^ distance) for i in range(count)])
+
+
+def rep_bit(distance):
+    return (lax.axis_index("rep") // distance) % 2
+
+
+def rep_gather(values):
+    gathered = values[None]
+    distance = lax.axis_size("rep") // 2
+    while distance:
+        other = rep_exchange(gathered, distance)
+        mine_first = jnp.stack([gathered, other], axis=1)
+        other_first = jnp.stack([other, gathered], axis=1)
+        gathered = jnp.where(rep_bit(distance) == 0, mine_first, other_first)
+        gathered = gathered.reshape((-1,) + values.shape)
+        distance //= 2
+    return gathered
+
+
+def rep_scatter(values, axis):
+    distance = 1
+    count = lax.axis_size("rep")
+    while distance < count:
+        shape = values.shape
+        pairs = values.reshape(shape[:axis] + (shape[axis] // 2, 2) + shape[axis + 1 :])
+        bit = rep_bit(distance)
+        keep = lax.dynamic_index_in_dim(pairs, bit, axis + 1, keepdims=False)
+        send = lax.dynamic_index_in_dim(pairs, 1 - bit, axis + 1, keepdims=False)
+        values = add_low(keep, rep_exchange(send, distance))
+        distance *= 2
+    return lax.index_in_dim(values, 0, axis, keepdims=False)
+
+
+def swap_all(values):
+    return lax.all_to_all(values, "ep", split_axis=0, concat_axis=0, tiled=True)
 
 
 def body(
@@ -105,8 +195,29 @@
     sequence_count = seq_lengths.shape[1]
     score_scale = head_dim ** (-0.5)
 
-    segment, position = row_meta(seq_lengths[0], token_order[0])
-    segment_own = lax.dynamic_slice_in_dim(segment, device * row_count, row_count)
+    replica_count = lax.axis_size("rep")
+    replica = lax.axis_index("rep")
+    share = width_here // replica_count
+
+    order = ring_order(group_count)
+    offsets = ring_slots(group_count)
+    place_of = jnp.array([order.index(i) for i in range(group_count)], jnp.int32)
+    place = place_of[device]
+    device_of_slot = jnp.array(order, jnp.int32)[(place + jnp.array(offsets)) % group_count]
+    slot_of_offset = jnp.array(
+        [[j for j, o in enumerate(offsets) if o % group_count == i][0] for i in range(group_count)],
+        jnp.int32,
+    )
+    slot_of_device = slot_of_offset[(place_of - place) % group_count]
+
+    def reorder(blocks, index):
+        return jnp.concatenate(
+            [lax.dynamic_slice_in_dim(blocks, index[i], 1, 0) for i in range(group_count)], axis=0
+        )
+
+    group_order = reorder(token_order[0].reshape(group_count, row_count), device_of_slot)
+    segment, position = row_meta(seq_lengths[0], group_order.reshape(group_rows))
+    segment_own = segment[:row_count]
     valid_own = (segment_own < sequence_count).astype(wide_type)[:, None]
     valid_all = (segment < sequence_count).astype(wide_type)[:, None]
 
@@ -118,23 +229,46 @@
         route_code = route_code + jnp.where(hit, 1 + kept, 0)
     small_sent = jnp.concatenate([route_code.astype(low_type), router_weight], axis=0)
 
-    token_all = gather_rows(tokens)
+    small_flat = small_sent.reshape(-1, head_dim)
+    small_all = swap_all(
+        jnp.broadcast_to(small_flat[None], (group_count,) + small_flat.shape)
+    ).reshape(group_count, row_count + width_here, expert_total)
+    code_all = reorder(small_all[:, :row_count], device_of_slot).reshape(
+        group_rows, expert_total
+    )
+    full_router = small_all[:, row_count:].reshape(model_width, expert_total)
+
     projections = jnp.concatenate(
         [
-            piece.reshape(width_here, group_count, width_here)
+            lax.dynamic_slice_in_dim(piece, replica * share, share, 0).reshape(
+                share, group_count, width_here
+            )
             for piece in (query_weight, key_weight, value_weight)
         ],
         axis=2,
     ).transpose(1, 0, 2)
-    head_weight = lax.all_to_all(
-        projections, "ep", split_axis=0, concat_axis=0, tiled=True
-    ).reshape(model_width, 3 * width_here)
-    small_all = gather_rows(small_sent).reshape(
-        group_count, row_count + width_here, expert_total
-    )
-    code_all = small_all[:, :row_count].reshape(group_rows, expert_total)
-    full_router = small_all[:, row_count:].reshape(model_width, expert_total)
-    cot_all = gather_rows(cotangent)
+    head_weight = (
+        rep_gather(swap_all(projections))
+        .transpose(1, 0, 2, 3)
+        .reshape(model_width, 3 * width_here)
+    )
+    token_blocks = ring_gather(tokens)
+    token_last, cot_own, output_weight_own = lax.optimization_barrier(
+        (token_blocks[-1], cotangent, output_weight)
+    )
+    token_all = jnp.concatenate(token_blocks[:-1] + [token_last], axis=0)
+    cot_all = jnp.concatenate(ring_gather(cot_own), axis=0)
+    column_share = model_width // replica_count
+    full_output = rep_gather(
+        lax.all_gather(
+            lax.dynamic_slice_in_dim(
+                output_weight_own, replica * column_share, column_share, 1
+            ),
+            "ep",
+            axis=0,
+            tiled=True,
+        )
+    )
 
     token_wide = token_all.astype(wide_type)
     inverse_all = inverse_rms(token_wide)
@@ -175,11 +309,18 @@
         )
     mixed_low = jnp.concatenate(mixed_parts, axis=1)
 
-    attention = scatter_rows(mm(mixed_low, output_weight, 1, 0))
+    mixed_own = (
+        swap_all(reorder(mixed_low.reshape(group_count, row_count, width_here), slot_of_device))
+        .transpose(1, 0, 2)
+        .reshape(row_count, model_width)
+    )
+    attention = lax.dot_general(
+        mixed_own, full_output, (((1,), (1,)), ((), ())), preferred_element_type=wide_type
+    ).reshape(row_count, model_width)
     residual = tokens.astype(wide_type) + attention
     inverse_two = inverse_rms(residual)
     second_input = (residual * inverse_two * postnorm_gain).astype(low_type)
-    second_all = gather_rows(second_input)
+    second_all = jnp.concatenate(ring_gather(second_input), axis=0)
 
     def gate_table(rows, code):
         logits = mm(rows, full_router, 1, 0)
@@ -226,14 +367,11 @@
         group_count, row_count, experts_here
     )
     pair_grad = (
-        lax.all_to_all(pair_sent, "ep", split_axis=0, concat_axis=0, tiled=True)
+        swap_all(reorder(pair_sent, slot_of_device))
         .transpose(1, 0, 2)
         .reshape(row_count, expert_total)
     )
-    second_scattered = scatter_rows(second_part)
-    mixture = scatter_rows(mixture_part)
-    layer_out = (valid_own * (residual + mixture)).astype(low_type)
-
+    second_scattered = ring_scatter(second_part.astype(low_type))
     code_own = route_code
     gates_own = gate_table(second_input, code_own)
     chosen_grad = gates_own * (
@@ -246,8 +384,22 @@
     post_back, postnorm_part = norm_backward(residual, inverse_two, postnorm_gain, second_grad)
     residual_grad = upstream + post_back
     attention_low = residual_grad.astype(low_type)
-    attention_all = gather_rows(attention_low)
-    mixed_grad = mm(attention_all, output_weight, 1, 1).astype(low_type)
+    mixed_grad_own = lax.dot_general(
+        attention_low.reshape(row_count, replica_count, column_share),
+        full_output,
+        (((1, 2), (0, 2)), ((), ())),
+        preferred_element_type=wide_type,
+    ).astype(low_type)
+    mixed_grad = reorder(
+        swap_all(mixed_grad_own.reshape(row_count, group_count, width_here).transpose(1, 0, 2)),
+        device_of_slot,
+    ).reshape(group_rows, width_here)
+    mixed_grad, attention_sent, mixture_low = lax.optimization_barrier(
+        (mixed_grad, attention_low, mixture_part.astype(low_type))
+    )
+    attention_all = jnp.concatenate(ring_gather(attention_sent), axis=0)
+    mixture = ring_scatter(mixture_low)
+    layer_out = (valid_own * (residual + mixture)).astype(low_type)
     output_part = mm(mixed_low, attention_all, 0, 0).astype(low_type)
 
     query_parts, key_parts, value_parts = [], [], []
@@ -280,55 +432,52 @@
         key_parts.append(key_before.astype(low_type))
         value_parts.append(value_back.astype(low_type))
     sent = jnp.concatenate(query_parts + key_parts + value_parts, axis=1)
-    first_grad = scatter_rows(mm(sent, head_weight, 1, 1))
+    first_part = mm(sent, head_weight, 1, 1)
+    prenorm_part = jnp.sum(first_part * token_wide * inverse_all, axis=0)
+    first_grad = ring_scatter(first_part.astype(low_type))
     head_part = mm(first_all, sent, 0, 0).astype(low_type)
-    head_rows = lax.all_to_all(
-        head_part.reshape(group_count, width_here, 3 * width_here),
-        "ep",
-        split_axis=0,
-        concat_axis=0,
-        tiled=True,
-    )
-    weight_sums = lax.psum(
-        tuple(
-            head_rows[:, :, block * width_here : (block + 1) * width_here]
-            .transpose(1, 0, 2)
-            .reshape(width_here, model_width)
-            for block in range(3)
-        )
-        + (output_part,),
-        "rep",
-    )
-    query_grad, key_grad, value_grad, output_grad = (
-        piece.astype(wide_type) for piece in weight_sums
+    head_rows = rep_gather(
+        swap_all(
+            rep_scatter(
+                head_part.reshape(group_count, replica_count, share, 3 * width_here), 1
+            )
+        )
+    )
+    query_grad, key_grad, value_grad = (
+        head_rows[..., block * width_here : (block + 1) * width_here]
+        .transpose(0, 2, 1, 3)
+        .reshape(width_here, model_width)
+        .astype(wide_type)
+        for block in range(3)
+    )
+    output_grad = (
+        rep_gather(rep_scatter(output_part.reshape(replica_count, share, model_width), 0))
+        .reshape(width_here, model_width)
+        .astype(wide_type)
     )
 
     token_own = tokens.astype(wide_type)
     inverse_one = inverse_rms(token_own)
-    pre_back, prenorm_part = norm_backward(token_own, inverse_one, prenorm_gain, first_grad)
+    pre_back, _ = norm_backward(token_own, inverse_one, prenorm_gain, first_grad)
     token_grad = residual_grad + pre_back
 
-    small_parts = jnp.concatenate(
-        [
-            router_part.reshape(group_count, -1),
-            jnp.sum(prenorm_part, axis=0).reshape(group_count, -1),
-            jnp.sum(postnorm_part, axis=0).reshape(group_count, -1),
-            querynorm_part.reshape(group_count, -1),
-            keynorm_part.reshape(group_count, -1),
-        ],
-        axis=1,
-    )
-    small_sum = lax.psum(
-        lax.psum_scatter(small_parts, "ep", scatter_dimension=0, tiled=True), "rep"
-    ).reshape(-1)
-    sizes = (width_here * expert_total, width_here, width_here) + 2 * (head_dim // group_count,)
-    pieces = []
-    start = 0
-    for size in sizes:
-        pieces.append(small_sum[start : start + size])
-        start += size
-    router_grad = pieces[0].reshape(width_here, expert_total)
-    prenorm_grad, postnorm_grad, querynorm_grad, keynorm_grad = pieces[1:]
+    def small_sum(parts):
+        flat = jnp.concatenate([part.reshape(group_count, -1) for part in parts], axis=1)
+        total = lax.psum(
+            lax.psum_scatter(flat, "ep", scatter_dimension=0, tiled=True), "rep"
+        ).reshape(-1)
+        pieces, start = [], 0
+        for part in parts:
+            size = part.size // group_count
+            pieces.append(total[start : start + size])
+            start += size
+        return pieces
+
+    router_grad, postnorm_grad = small_sum([router_part, jnp.sum(postnorm_part, axis=0)])
+    router_grad = router_grad.reshape(width_here, expert_total)
+    prenorm_grad, querynorm_grad, keynorm_grad = small_sum(
+        [prenorm_part, querynorm_part, keynorm_part]
+    )
 
     gate_total, up_total, down_total = (
         lax.psum_scatter(

time: 1370 us -> 982 us (0.72)
  waiting for transfers between devices: 928 us -> 262 us
  starting transfers between devices: 15.9 us -> 111 us
  local copies, waits for them, and re-layouts: 27.1 us -> 110 us
  other arithmetic: 78 us -> 118 us
  between operations: 16.2 us -> 47.2 us
    reduce_scatter x4 -> x0, waiting for transfers between devices: 369 us -> none  [scatter_rows(): lax.psum_scatter(values.astype(low_type), 'ep', scatter_dimension=0, tile...]
    ppermute x0 -> x68, waiting for transfers between devices: none -> 244 us  [the longest x56 186 us: ring_shift(): return lax.ppermute(values, 'ep', pairs)]
    all_to_all x3 -> x6, waiting for transfers between devices: 199 us -> 11.1 us  [swap_all(): return lax.all_to_all(values, 'ep', split_axis=0, concat_axis=0, tiled=True)]
    all_gather x4 -> x1, waiting for transfers between devices: 131 us -> 7.12 us  [body(): lax.all_gather(lax.dynamic_slice_in_dim(output_weight_own, replica * colu...]
    psum x1 -> x0, waiting for transfers between devices: 85.1 us -> none  [body(): lax.psum(tuple((head_rows[:, :, block * width_here:(block + 1) * width_he...]
    ppermute x0 -> x68, starting transfers between devices: none -> 78.4 us  [the longest x56 69.5 us: ring_shift(): return lax.ppermute(values, 'ep', pairs)]
    reduce_scatter x3, waiting for transfers between devices: 75.7 us -> 0.01 us  [body(): lax.psum_scatter(jnp.stack(parts), 'rep', scatter_dimension=1, tiled=True)]
    unnamed x14 -> x6, waiting for transfers between devices: 69.1 us -> 0.1 us
  transfers between devices with their start and end apart: 16 -> 79, of which waited for: 15 -> 36; matrix products, arithmetic and copies ran while one was open for 17% -> 37% of each run, Pallas kernels for 0% -> 0%
where the time goes in v2:
time: 982 us; the launch traced here: 973 us
  matrix products  275 us (28%)
  waiting for transfers between devices  262 us (27%)
  other arithmetic  118 us (12%)
  starting transfers between devices  111 us (11%)
  local copies, waits for them, and re-layouts  110 us (11%)
  blocking collectives  49.1 us (5%)
  between operations  47.2 us (5%)
    dot_general x38, matrix products, mm(): lax.dot_general(left, right, (((left_dim,), (right_dim,)), ((), ())), pre...  265 us
    ppermute x56, waiting for transfers between devices, ring_shift(): return lax.ppermute(values, 'ep', pairs)  186 us
    ppermute x56, starting transfers between devices, ring_shift(): return lax.ppermute(values, 'ep', pairs)  69.5 us
    unnamed x259, local copies, waits for them, and re-layouts  61.3 us
    ppermute x12, waiting for transfers between devices, rep_exchange(): lax.ppermute(values, 'rep', [(i, i ^ distance) for i in range(count)])  58.2 us
    unnamed x1, blocking collectives  37.5 us
    all_to_all x6, starting transfers between devices, swap_all(): return lax.all_to_all(values, 'ep', split_axis=0, concat_axis=0, tiled=True)  32.2 us
    another operation x3, other arithmetic, body(): jnp.stack(parts)  21.9 us
  transfers between devices with their start and end apart: 79, of which 36 were waited for; matrix products, arithmetic and copies ran while one was open for 37% of the time, Pallas kernels for 0%

profile of v2, /device:TPU:0, one launch (start us, length us, event | category | flops | bytes accessed | tf_op | source)
XLA Modules:
  0.0 972.6 jit_solution(16152592559587628271)
XLA Ops:
  14.1 6.2 all-to-all-start.2
  64.2 6.0 all-to-all-start
  76.9 21.5 %collective-permute-done.2 = bf16[160,2048]{1,0:T(8,128)(2,1)} collective-permute-done((bf16[160,2048]{1,0:T(8,128)(2,1)}, bf16[160,2048]{1,0:T(8,128)(2,1)}, u32[]{:S(2)}, u32[]{:S(2)}) %collective-permute-start.2) | collective-permute-done | bytes 655392 | tf_op jit(solution)/shard_map/ppermute | solution.py:80
  98.4 5.6 collective-permute-start.5
  111.6 6.4 collective-permute-done.5
  136.7 7.7 collective-permute-done.20
  150.2 15.0 %collective-permute-done.22 = bf16[160,2048]{1,0:T(8,128)(2,1)} collective-permute-done((bf16[160,2048]{1,0:T(8,128)(2,1)}, bf16[160,2048]{1,0:T(8,128)(2,1)}, u32[]{:S(2)}, u32[]{:S(2)}) %collective-permute-start.22) | collective-permute-done | bytes 655392 | tf_op jit(solution)/shard_map/ppermute | solution.py:80
  176.0 6.5 fusion.141
  187.7 7.1 all-gather.2.cloned.1.call-done
  201.3 40.8 %collective-permute-done.10 = bf16[1,2048,512]{2,1,0:T(8,128)(2,1)S(1)} collective-permute-done((bf16[1,2048,512]{2,1,0:T(8,128)(2,1)}, bf16[1,2048,512]{2,1,0:T(8,128)(2,1)S(1)}, u32[]{:S(2)}, u32[]{:S(2)}) %collective-permute-start.10) | collective-permute-done | bytes 2097184 | tf_op jit(solution)/shard_map/ppermute | solution.py:126
  258.8 6.9 all-to-all-start.1
  275.8 8.8 collective-permute-done.26
  291.1 7.9 maximum_select_fusion
  299.0 11.5 %copy.146 = bf16[4,512,2048]{2,1,0:T(8,128)(2,1)} copy(bf16[4,512,2048]{1,2,0:T(8,128)(2,1)} %bitcast.240) | data formatting | bytes 16777216 | tf_op jit(solution)/shard_map/dot_general | solution.py:317
  310.5 6.4 multiply_reduce_fusion.6
  322.6 10.6 %fusion.12 = f32[1280,1024]{0,1:T(8,128)} fusion(bf16[1280,2048]{1,0:T(8,128)(2,1)} %constant_dynamic-update-slice_fusion.33, bf16[2,1024,2048]{2,1,0:T(8,128)(2,1)} %param.39), kind=kOutput, calls=%fused_computation.45 | convolution fusion | flops 5368709120 | bytes 14680064 | tf_op jit(solution)/shard_map/dot_general | solution.py:56
  338.9 9.4 fusion.23
  348.8 3.8 collective-permute-done.14
  354.9 13.7 %collective-permute-done.17 = bf16[160,2048]{1,0:T(8,128)(2,1)S(1)} collective-permute-done((bf16[160,2048]{1,0:T(8,128)(2,1)S(1)}, bf16[160,2048]{1,0:T(8,128)(2,1)S(1)}, u32[]{:S(2)}, u32[]{:S(2)}) %collective-permute-start.17) | collective-permute-done | bytes 655392 | tf_op jit(solution)/shard_map/ppermute | solution.py:80
  371.0 4.8 collective-permute-done.18
  376.9 7.9 fusion.15
  384.9 7.9 fusion.27
  394.4 15.5 %multiply_convert_fusion.5 = (bf16[1280,1024]{0,1:T(8,128)(2,1)S(1)}, f32[1280]{0:T(1024)S(1)}, bf16[1280,1024]{0,1:T(8,128)(2,1)}, bf16[1280,1024]{0,1:T(8,128)(2,1)}) fusion(f32[1280,1024]{0,1:T(8,128)} %fusion.15, f32[1280,1024]{0,1:T(8,128)} %fusion.12, f32[1280]{0:T(1024)S(1)} %get-tuple-element.107, ...), kind=kOutput, calls=%fused_computation.31 | convolution fusion | flops 5393611776 | bytes 27797504 | tf_op jit(solution)/shard_map/dot_general | solution.py:56
  409.8 11.4 %fusion.17 = f32[1280,2048]{1,0:T(8,128)} fusion(bf16[1280,1024]{0,1:T(8,128)(2,1)S(1)} %get-tuple-element.125, bf16[2,2048,1024]{2,1,0:T(8,128)(2,1)} %param.37), kind=kOutput, calls=%fused_computation.50 | convolution fusion | flops 5368709120 | bytes 17301504 | tf_op jit(solution)/shard_map/dot_general | solution.py:56
  421.2 15.5 %multiply_convert_fusion.7 = (bf16[1280,1024]{0,1:T(8,128)(2,1)S(1)}, f32[1280]{0:T(1024)S(1)}, bf16[1280,1024]{0,1:T(8,128)(2,1)}, bf16[1280,1024]{0,1:T(8,128)(2,1)}) fusion(f32[1280,1024]{0,1:T(8,128)} %fusion.27, f32[1280,1024]{0,1:T(8,128)} %fusion.23, f32[1280]{0:T(1024)S(1)} %get-tuple-element.106, ...), kind=kOutput, calls=%fused_computation.33 | convolution fusion | flops 5393611776 | bytes 27797504 | tf_op jit(solution)/shard_map/dot_general | solution.py:56
  436.6 11.7 %fusion.25 = f32[1280,2048]{1,0:T(8,128)} fusion(bf16[1280,1024]{0,1:T(8,128)(2,1)} %get-tuple-element.130, bf16[2,2048,1024]{2,1,0:T(8,128)(2,1)} %param.38), kind=kOutput, calls=%fused_computation.58 | convolution fusion | flops 5368709120 | bytes 17301504 | tf_op jit(solution)/shard_map/dot_general | solution.py:56
  448.3 10.5 %fusion.29 = f32[1280,2048]{1,0:T(8,128)} fusion(bf16[1280,1024]{0,1:T(8,128)(2,1)S(1)} %get-tuple-element.123, bf16[2,2048,1024]{2,1,0:T(8,128)(2,1)} %param.37), kind=kOutput, calls=%fused_computation.62 | convolution fusion | flops 5368709120 | bytes 17301504 | tf_op jit(solution)/shard_map/dot_general | solution.py:56
  458.8 16.9 %add_convert_fusion.1 = bf16[1280,2048]{1,0:T(8,128)(2,1)} fusion(f32[1280,2048]{1,0:T(8,128)} %fusion.17, f32[1280,2048]{1,0:T(8,128)} %fusion.29, f32[1280,2048]{1,0:T(8,128)} %fusion.25, bf16[1280,1024]{0,1:T(8,128)(2,1)} %get-tuple-element.128, bf16[2,2048,1024]{2,1,0:T(8,128)(2,1)} %param.38), kind=kOutput, calls=%fused_computation.11 | convolution fusion | flops 5379194880 | bytes 43515904 | tf_op jit(solution)/shard_map/dot_general | solution.py:56
  492.8 4.1 all-to-all-start.3
  505.9 10.1 %convert_bitcast_fusion = bf16[1,1024,2048]{2,1,0:T(8,128)(2,1)} fusion(bf16[1280,1024]{0,1:T(8,128)(2,1)} %get-tuple-element.127, bf16[1280,2048]{1,0:T(8,128)(2,1)} %constant_dynamic-update-slice_fusion.33), kind=kOutput, calls=%fused_computation.66 | convolution fusion | flops 5370806272 | bytes 12058624 | tf_op jit(solution)/shard_map/dot_general | solution.py:56
  524.3 9.6 convert_bitcast_fusion.1
  541.7 7.4 pad_maximum_fusion.2
  549.2 10.3 %convert_bitcast_fusion.2 = bf16[1,2048,1024]{2,1,0:T(8,128)(2,1)} fusion(bf16[1280,2048]{1,0:T(8,128)(2,1)} %copy-done.9, bf16[1280,1024]{0,1:T(8,128)(2,1)} %get-tuple-element.128), kind=kOutput, calls=%fused_computation.68 | convolution fusion | flops 5370806272 | bytes 12058624 | tf_op jit(solution)/shard_map/dot_general | solution.py:56
  559.5 9.7 convert_bitcast_fusion.3
  569.2 7.5 pad_maximum_fusion.1
  578.6 10.9 %fusion.21 = f32[1280,2048]{1,0:T(8,128)} fusion(bf16[1280,1024]{0,1:T(8,128)(2,1)} %get-tuple-element.129, bf16[2,1024,2048]{2,1,0:T(8,128)(2,1)} %param.39), kind=kOutput, calls=%fused_computation.54 | convolution fusion | flops 5368709120 | bytes 17301504 | tf_op jit(solution)/shard_map/dot_general | solution.py:56
  589.6 10.1 %convert_bitcast_fusion.4 = bf16[1,2048,1024]{2,1,0:T(8,128)(2,1)} fusion(bf16[1280,2048]{1,0:T(8,128)(2,1)} %copy-done.9, bf16[1280,1024]{0,1:T(8,128)(2,1)S(1)} %copy-done.78), kind=kOutput, calls=%fused_computation.70 | convolution fusion | flops 5370806272 | bytes 12058624 | tf_op jit(solution)/shard_map/dot_general | solution.py:56
  599.7 10.9 %add_convert_fusion = bf16[1280,2048]{1,0:T(8,128)(2,1)} fusion(f32[1280,2048]{1,0:T(8,128)} %fusion.21, bf16[1280,1024]{0,1:T(8,128)(2,1)} %get-tuple-element.127, bf16[2,1024,2048]{2,1,0:T(8,128)(2,1)S(1)} %bitcast.379), kind=kOutput, calls=%fused_computation.10 | convolution fusion | flops 5373952000 | bytes 22544384 | tf_op jit(solution)/shard_map/dot_general | solution.py:56
  613.5 3.9 fusion.46
  618.4 5.3 all-to-all-start.4
  623.8 12.6 %convert_bitcast_fusion.5 = bf16[1,2048,1024]{2,1,0:T(8,128)(2,1)} fusion(bf16[1280,2048]{1,0:T(8,128)(2,1)} %copy-done.9, bf16[1280,1024]{0,1:T(8,128)(2,1)} %copy-done.76), kind=kOutput, calls=%fused_computation.71 | convolution fusion | flops 5370806272 | bytes 12058624 | tf_op jit(solution)/shard_map/dot_general | solution.py:56
  636.4 7.0 pad_maximum_fusion
  652.4 7.2 multiply_reduce_fusion
  659.6 5.0 multiply_reduce_fusion.1
  664.7 4.1 multiply_convert_fusion
  673.9 4.2 multiply_convert_fusion.1
  687.2 4.9 fusion.47
  692.1 13.7 %fusion.4 = (f32[2048]{0:T(1024)S(1)}, bf16[1280,2048]{1,0:T(8,128)(2,1)}) fusion(bf16[1280,2048]{1,0:T(8,128)(2,1)} %get-tuple-element.296, f32[1280]{0:T(1024)S(1)} %copy-done.70, bf16[1280,768]{0,1:T(8,128)(2,1)} %fusion.47, bf16[2048,768]{1,0:T(8,128)(2,1)} %bitcast.268), kind=kOutput, calls=%fused_computation.9 | convolution fusion | flops 4039636992 | bytes 15610880 | tf_op jit(solution)/shard_map/dot_general | solution.py:56
  705.8 37.5 %all-reduce.1 = f32[8,288]{1,0:T(8,128)S(1)} all-reduce(f32[8,288]{1,0:T(8,128)S(1)} %pad_maximum_fusion.15), channel_id=3, replica_groups=mesh['rep'=4,'ep'=8] {'ep'}, use_global_device_ids=true, to_apply=%region_37.38.clone | all-reduce | flops 2304 | bytes 18432
  744.0 11.5 %all-reduce.2 = (f32[1,4352]{1,0:T(1,128)S(1)}, f32[1,288]{1,0:T(1,128)S(1)}) all-reduce(f32[1,4352]{1,0:T(1,128)S(1)} %constant_dynamic-slice_fusion.35, f32[1,288]{1,0:T(1,128)S(1)} %constant_dynamic-slice_fusion.34), channel_id=1, replica_groups=mesh['rep'=4,'ep'=8] {'rep'}, use_global_device_ids=true, to_apply=%region_31.32 | all-reduce | flops 4640 | bytes 37120 | tf_op jit(solution)/shard_map/psum | solution.py:466
  757.5 8.0 convolution_convert_fusion
  771.5 4.9 collective-permute-done.44
  778.7 6.9 collective-permute-done.36
  793.5 9.8 %collective-permute-done.49 = bf16[160,2048]{1,0:T(8,128)(2,1)S(1)} collective-permute-done((bf16[160,2048]{1,0:T(8,128)(2,1)S(1)}, bf16[160,2048]{1,0:T(8,128)(2,1)S(1)}, u32[]{:S(2)}, u32[]{:S(2)}) %collective-permute-start.49) | collective-permute-done | bytes 655392 | tf_op jit(solution)/shard_map/ppermute | solution.py:80
  805.8 11.6 %collective-permute-done.41 = bf16[160,2048]{1,0:T(8,128)(2,1)S(1)} collective-permute-done((bf16[160,2048]{1,0:T(8,128)(2,1)S(1)}, bf16[160,2048]{1,0:T(8,128)(2,1)S(1)}, u32[]{:S(2)}, u32[]{:S(2)}) %collective-permute-start.41) | collective-permute-done | bytes 655392 | tf_op jit(solution)/shard_map/ppermute | solution.py:80
  821.2 10.3 %collective-permute-done.58 = bf16[160,2048]{1,0:T(8,128)(2,1)S(1)} collective-permute-done((bf16[160,2048]{1,0:T(8,128)(2,1)}, bf16[160,2048]{1,0:T(8,128)(2,1)S(1)}, u32[]{:S(2)}, u32[]{:S(2)}) %collective-permute-start.58) | collective-permute-done | bytes 655392 | tf_op jit(solution)/shard_map/ppermute | solution.py:80
  834.8 10.9 %collective-permute-done.46 = bf16[160,2048]{1,0:T(8,128)(2,1)S(1)} collective-permute-done((bf16[160,2048]{1,0:T(8,128)(2,1)S(1)}, bf16[160,2048]{1,0:T(8,128)(2,1)S(1)}, u32[]{:S(2)}, u32[]{:S(2)}) %collective-permute-start.46) | collective-permute-done | bytes 655392 | tf_op jit(solution)/shard_map/ppermute | solution.py:80
  850.3 21.2 %collective-permute-done.61 = bf16[160,2048]{1,0:T(8,128)(2,1)S(1)} collective-permute-done((bf16[160,2048]{1,0:T(8,128)(2,1)S(1)}, bf16[160,2048]{1,0:T(8,128)(2,1)S(1)}, u32[]{:S(2)}, u32[]{:S(2)}) %collective-permute-start.61) | collective-permute-done | bytes 655392 | tf_op jit(solution)/shard_map/ppermute | solution.py:80
  873.8 5.4 collective-permute-done.62
  901.7 11.1 %all-to-all-done.5 = bf16[8,64,768]{2,1,0:T(8,128)(2,1)S(1)} async-done(((bf16[8,64,768]{2,1,0:T(8,128)(2,1)}), bf16[8,64,768]{2,1,0:T(8,128)(2,1)S(1)}, u32[]{:S(2)}, u32[]{:S(2)}) %all-to-all-start.5) | async-done | bytes 786464 | tf_op jit(solution)/shard_map/all_to_all | solution.py:161
  915.9 16.7 %collective-permute-done.54 = bf16[1,8,64,768]{3,2,1,0:T(8,128)(2,1)S(1)} collective-permute-done((bf16[1,8,64,768]{3,2,1,0:T(8,128)(2,1)S(1)}, bf16[1,8,64,768]{3,2,1,0:T(8,128)(2,1)S(1)}, u32[]{:S(2)}, u32[]{:S(2)}) %collective-permute-start.54) | collective-permute-done | bytes 786464 | tf_op jit(solution)/shard_map/ppermute | solution.py:126
  953.5 4.1 convert_element_type.600
  957.6 4.2 convert_element_type.597
  961.8 4.1 convert_element_type.594
  (598 shorter events, 284.6 us)
Async XLA Ops:
  7.2 65.2 %collective-permute-start = (bf16[160,2048]{1,0:T(8,128)(2,1)}, bf16[160,2048]{1,0:T(8,128)(2,1)}, u32[]{:S(2)}, u32[]{:S(2)}) collective-permute-start(bf16[160,2048]{1,0:T(8,128)(2,1)} %param.22), channel_id=1, source_target_pairs={{0,1},{2,0},{4,2},{6,4},{7,6},{5,7},{3,5},{1,3},{8,9},{10,8},{12,1... | collective-permute-start | bytes 1966088 | tf_op jit(solution)/shard_map/ppermute | solution.py:80
  10.2 64.3 %collective-permute-start.1 = (bf16[160,2048]{1,0:T(8,128)(2,1)}, bf16[160,2048]{1,0:T(8,128)(2,1)}, u32[]{:S(2)}, u32[]{:S(2)}) collective-permute-start(bf16[160,2048]{1,0:T(8,128)(2,1)} %param.22), channel_id=1, source_target_pairs={{0,2},{2,4},{4,6},{6,7},{7,5},{5,3},{3,1},{1,0},{8,10},{10,12},{12... | collective-permute-start | bytes 1966088 | tf_op jit(solution)/shard_map/ppermute | solution.py:80
  14.1 50.1 %all-to-all-start.2 = ((bf16[8,52,128]{2,1,0:T(8,128)(2,1)}), bf16[8,52,128]{2,1,0:T(8,128)(2,1)S(1)}, u32[]{:S(2)}, u32[]{:S(2)}) async-start(bf16[8,52,128]{2,1,0:T(8,128)(2,1)} %broadcast_in_dim.203), calls=%async_computation.2 | async-start | bytes 229376 | tf_op jit(solution)/shard_map/all_to_all | solution.py:161
  64.2 41.9 %all-to-all-start = ((bf16[8,64,768]{2,1,0:T(8,128)(2,1)}), bf16[8,64,768]{2,1,0:T(8,128)(2,1)S(1)}, u32[]{:S(2)}, u32[]{:S(2)}) async-start(bf16[8,64,768]{2,1,0:T(8,128)(2,1)} %copy.140), calls=%async_computation | async-start | bytes 1572864 | tf_op jit(solution)/shard_map/all_to_all | solution.py:161
  70.2 124.6 %all-gather.2.cloned.1.call-start = ((), (), s32[]{:S(2)}) async-start(), calls=%async_computation.9 | async-start | bytes 2359296 | tf_op jit(solution)/shard_map/all_gather | solution.py:263
  72.4 26.0 %collective-permute-start.2 = (bf16[160,2048]{1,0:T(8,128)(2,1)}, bf16[160,2048]{1,0:T(8,128)(2,1)}, u32[]{:S(2)}, u32[]{:S(2)}) collective-permute-start(bf16[160,2048]{1,0:T(8,128)(2,1)} %collective-permute-done), channel_id=1, source_target_pairs={{0,1},{2,0},{4,2},{6,4},{7,6},{5,7},{3,5},{1,3},{8,9},{10,8},{12,1... | collective-permute-start | bytes 1966088 | tf_op jit(solution)/shard_map/ppermute | solution.py:80
  74.5 23.9 %collective-permute-start.3 = (bf16[160,2048]{1,0:T(8,128)(2,1)}, bf16[160,2048]{1,0:T(8,128)(2,1)}, u32[]{:S(2)}, u32[]{:S(2)}) collective-permute-start(bf16[160,2048]{1,0:T(8,128)(2,1)} %collective-permute-done.1), channel_id=1, source_target_pairs={{0,2},{2,4},{4,6},{6,7},{7,5},{5,3},{3,1},{1,0},{8,10},{10,12},{12... | collective-permute-start | bytes 1966088 | tf_op jit(solution)/shard_map/ppermute | solution.py:80
  98.4 20.6 %collective-permute-start.4 = (bf16[160,2048]{1,0:T(8,128)(2,1)}, bf16[160,2048]{1,0:T(8,128)(2,1)S(1)}, u32[]{:S(2)}, u32[]{:S(2)}) collective-permute-start(bf16[160,2048]{1,0:T(8,128)(2,1)} %collective-permute-done.2), channel_id=1, source_target_pairs={{0,1},{2,0},{4,2},{6,4},{7,6},{5,7},{3,5},{1,3},{8,9},{10,8},{12,1... | collective-permute-start | bytes 1966088 | tf_op jit(solution)/shard_map/ppermute | solution.py:80
  98.4 19.6 %collective-permute-start.5 = (bf16[160,2048]{1,0:T(8,128)(2,1)}, bf16[160,2048]{1,0:T(8,128)(2,1)S(1)}, u32[]{:S(2)}, u32[]{:S(2)}) collective-permute-start(bf16[160,2048]{1,0:T(8,128)(2,1)} %collective-permute-done.3), channel_id=1, source_target_pairs={{0,2},{2,4},{4,6},{6,7},{7,5},{5,3},{3,1},{1,0},{8,10},{10,12},{12... | collective-permute-start | bytes 1966088 | tf_op jit(solution)/shard_map/ppermute | solution.py:80
  106.1 17.2 %collective-permute-start.8 = (bf16[1,8,64,768]{3,2,1,0:T(8,128)(2,1)S(1)}, bf16[1,8,64,768]{3,2,1,0:T(8,128)(2,1)S(1)}, u32[]{:S(2)}, u32[]{:S(2)}) collective-permute-start(bf16[1,8,64,768]{3,2,1,0:T(8,128)(2,1)S(1)} %bitcast.257), channel_id=1, source_target_pairs={{0,16},{8,24},{16,0},{24,8},{1,17},{9,25},{17,1},{25,9},{2,18},{10... | collective-permute-start | bytes 2359304 | tf_op jit(solution)/shard_map/ppermute | solution.py:126
  124.6 46.1 %collective-permute-start.9 = (bf16[2,8,64,768]{3,2,1,0:T(8,128)(2,1)}, bf16[2,8,64,768]{3,2,1,0:T(8,128)(2,1)}, u32[]{:S(2)}, u32[]{:S(2)}) collective-permute-start(bf16[2,8,64,768]{3,2,1,0:T(8,128)(2,1)} %maximum_select_fusion.5), channel_id=1, source_target_pairs={{0,8},{8,0},{16,24},{24,16},{1,9},{9,1},{17,25},{25,17},{2,10},{10... | collective-permute-start | bytes 4718600 | tf_op jit(solution)/shard_map/ppermute | solution.py:126
  127.3 17.1 %collective-permute-start.20 = (bf16[160,2048]{1,0:T(8,128)(2,1)}, bf16[160,2048]{1,0:T(8,128)(2,1)}, u32[]{:S(2)}, u32[]{:S(2)}) collective-permute-start(bf16[160,2048]{1,0:T(8,128)(2,1)} %param.23), channel_id=1, source_target_pairs={{0,1},{2,0},{4,2},{6,4},{7,6},{5,7},{3,5},{1,3},{8,9},{10,8},{12,1... | collective-permute-start | bytes 1966088 | tf_op jit(solution)/shard_map/ppermute | solution.py:80
  129.2 18.7 %collective-permute-start.21 = (bf16[160,2048]{1,0:T(8,128)(2,1)}, bf16[160,2048]{1,0:T(8,128)(2,1)}, u32[]{:S(2)}, u32[]{:S(2)}) collective-permute-start(bf16[160,2048]{1,0:T(8,128)(2,1)} %param.23), channel_id=1, source_target_pairs={{0,2},{2,4},{4,6},{6,7},{7,5},{5,3},{3,1},{1,0},{8,10},{10,12},{12... | collective-permute-start | bytes 1966088 | tf_op jit(solution)/shard_map/ppermute | solution.py:80
  144.4 20.8 %collective-permute-start.22 = (bf16[160,2048]{1,0:T(8,128)(2,1)}, bf16[160,2048]{1,0:T(8,128)(2,1)}, u32[]{:S(2)}, u32[]{:S(2)}) collective-permute-start(bf16[160,2048]{1,0:T(8,128)(2,1)} %collective-permute-done.20), channel_id=1, source_target_pairs={{0,1},{2,0},{4,2},{6,4},{7,6},{5,7},{3,5},{1,3},{8,9},{10,8},{12,1... | collective-permute-start | bytes 1966088 | tf_op jit(solution)/shard_map/ppermute | solution.py:80
  147.9 20.3 %collective-permute-start.23 = (bf16[160,2048]{1,0:T(8,128)(2,1)}, bf16[160,2048]{1,0:T(8,128)(2,1)}, u32[]{:S(2)}, u32[]{:S(2)}) collective-permute-start(bf16[160,2048]{1,0:T(8,128)(2,1)} %collective-permute-done.21), channel_id=1, source_target_pairs={{0,2},{2,4},{4,6},{6,7},{7,5},{5,3},{3,1},{1,0},{8,10},{10,12},{12... | collective-permute-start | bytes 1966088 | tf_op jit(solution)/shard_map/ppermute | solution.py:80
  165.2 105.5 %collective-permute-start.24 = (bf16[160,2048]{1,0:T(8,128)(2,1)}, bf16[160,2048]{1,0:T(8,128)(2,1)}, u32[]{:S(2)}, u32[]{:S(2)}) collective-permute-start(bf16[160,2048]{1,0:T(8,128)(2,1)} %collective-permute-done.22), channel_id=1, source_target_pairs={{0,1},{2,0},{4,2},{6,4},{7,6},{5,7},{3,5},{1,3},{8,9},{10,8},{12,1... | collective-permute-start | bytes 1966088 | tf_op jit(solution)/shard_map/ppermute | solution.py:80
  168.3 99.4 %collective-permute-start.25 = (bf16[160,2048]{1,0:T(8,128)(2,1)}, bf16[160,2048]{1,0:T(8,128)(2,1)}, u32[]{:S(2)}, u32[]{:S(2)}) collective-permute-start(bf16[160,2048]{1,0:T(8,128)(2,1)} %collective-permute-done.23), channel_id=1, source_target_pairs={{0,2},{2,4},{4,6},{6,7},{7,5},{5,3},{3,1},{1,0},{8,10},{10,12},{12... | collective-permute-start | bytes 1966088 | tf_op jit(solution)/shard_map/ppermute | solution.py:80
  194.9 47.2 %collective-permute-start.10 = (bf16[1,2048,512]{2,1,0:T(8,128)(2,1)}, bf16[1,2048,512]{2,1,0:T(8,128)(2,1)S(1)}, u32[]{:S(2)}, u32[]{:S(2)}) collective-permute-start(bf16[1,2048,512]{2,1,0:T(8,128)(2,1)} %bitcast.250), channel_id=1, source_target_pairs={{0,16},{8,24},{16,0},{24,8},{1,17},{9,25},{17,1},{25,9},{2,18},{10... | collective-permute-start | bytes 6291464 | tf_op jit(solution)/shard_map/ppermute | solution.py:126
  244.9 46.2 %collective-permute-start.11 = (bf16[2,2048,512]{2,1,0:T(8,128)(2,1)}, bf16[2,2048,512]{2,1,0:T(8,128)(2,1)}, u32[]{:S(2)}, u32[]{:S(2)}) collective-permute-start(bf16[2,2048,512]{2,1,0:T(8,128)(2,1)} %maximum_select_fusion.2), channel_id=1, source_target_pairs={{0,8},{8,0},{16,24},{24,16},{1,9},{9,1},{17,25},{25,17},{2,10},{10... | collective-permute-start | bytes 12582920 | tf_op jit(solution)/shard_map/ppermute | solution.py:126
  258.8 28.6 %all-to-all-start.1 = ((bf16[8,160,256]{2,1,0:T(8,128)(2,1)}), bf16[8,160,256]{2,1,0:T(8,128)(2,1)S(1)}, u32[]{:S(2)}, u32[]{:S(2)}) async-start(bf16[8,160,256]{2,1,0:T(8,128)(2,1)} %constant_dynamic-update-slice_fusion.8), calls=%async_computation.1 | async-start | bytes 1310720 | tf_op jit(solution)/shard_map/all_to_all | solution.py:161
  268.7 15.9 %collective-permute-start.26 = (bf16[80,2048]{1,0:T(8,128)(2,1)S(1)}, bf16[80,2048]{1,0:T(8,128)(2,1)S(1)}, u32[]{:S(2)}, u32[]{:S(2)}) collective-permute-start(bf16[80,2048]{1,0:T(8,128)(2,1)S(1)} %slice.577), channel_id=1, source_target_pairs={{0,2},{2,4},{4,6},{6,7},{7,5},{5,3},{3,1},{1,0},{8,10},{10,12},{12... | collective-permute-start | bytes 983048 | tf_op jit(solution)/shard_map/ppermute | solution.py:80
  271.8 14.8 %collective-permute-start.27 = (bf16[80,2048]{1,0:T(8,128)(2,1)S(1)}, bf16[80,2048]{1,0:T(8,128)(2,1)S(1)}, u32[]{:S(2)}, u32[]{:S(2)}) collective-permute-start(bf16[80,2048]{1,0:T(8,128)(2,1)S(1)} %slice.578), channel_id=1, source_target_pairs={{0,1},{2,0},{4,2},{6,4},{7,6},{5,7},{3,5},{1,3},{8,9},{10,8},{12,1... | collective-permute-start | bytes 983048 | tf_op jit(solution)/shard_map/ppermute | solution.py:80
  317.8 19.1 %collective-permute-start.12 = (bf16[160,2048]{1,0:T(8,128)(2,1)S(1)}, bf16[160,2048]{1,0:T(8,128)(2,1)S(1)}, u32[]{:S(2)}, u32[]{:S(2)}) collective-permute-start(bf16[160,2048]{1,0:T(8,128)(2,1)S(1)} %get-tuple-element.122), channel_id=1, source_target_pairs={{0,1},{2,0},{4,2},{6,4},{7,6},{5,7},{3,5},{1,3},{8,9},{10,8},{12,1... | collective-permute-start | bytes 1966088 | tf_op jit(solution)/shard_map/ppermute | solution.py:80
  319.7 19.0 %collective-permute-start.13 = (bf16[160,2048]{1,0:T(8,128)(2,1)S(1)}, bf16[160,2048]{1,0:T(8,128)(2,1)S(1)}, u32[]{:S(2)}, u32[]{:S(2)}) collective-permute-start(bf16[160,2048]{1,0:T(8,128)(2,1)S(1)} %get-tuple-element.122), channel_id=1, source_target_pairs={{0,2},{2,4},{4,6},{6,7},{7,5},{5,3},{3,1},{1,0},{8,10},{10,12},{12... | collective-permute-start | bytes 1966088 | tf_op jit(solution)/shard_map/ppermute | solution.py:80
  336.9 15.7 %collective-permute-start.14 = (bf16[160,2048]{1,0:T(8,128)(2,1)S(1)}, bf16[160,2048]{1,0:T(8,128)(2,1)S(1)}, u32[]{:S(2)}, u32[]{:S(2)}) collective-permute-start(bf16[160,2048]{1,0:T(8,128)(2,1)S(1)} %collective-permute-done.12), channel_id=1, source_target_pairs={{0,1},{2,0},{4,2},{6,4},{7,6},{5,7},{3,5},{1,3},{8,9},{10,8},{12,1... | collective-permute-start | bytes 1966088 | tf_op jit(solution)/shard_map/ppermute | solution.py:80
  338.7 15.1 %collective-permute-start.15 = (bf16[160,2048]{1,0:T(8,128)(2,1)S(1)}, bf16[160,2048]{1,0:T(8,128)(2,1)S(1)}, u32[]{:S(2)}, u32[]{:S(2)}) collective-permute-start(bf16[160,2048]{1,0:T(8,128)(2,1)S(1)} %collective-permute-done.13), channel_id=1, source_target_pairs={{0,2},{2,4},{4,6},{6,7},{7,5},{5,3},{3,1},{1,0},{8,10},{10,12},{12... | collective-permute-start | bytes 1966088 | tf_op jit(solution)/shard_map/ppermute | solution.py:80
  352.6 17.1 %collective-permute-start.16 = (bf16[160,2048]{1,0:T(8,128)(2,1)S(1)}, bf16[160,2048]{1,0:T(8,128)(2,1)S(1)}, u32[]{:S(2)}, u32[]{:S(2)}) collective-permute-start(bf16[160,2048]{1,0:T(8,128)(2,1)S(1)} %collective-permute-done.14), channel_id=1, source_target_pairs={{0,1},{2,0},{4,2},{6,4},{7,6},{5,7},{3,5},{1,3},{8,9},{10,8},{12,1... | collective-permute-start | bytes 1966088 | tf_op jit(solution)/shard_map/ppermute | solution.py:80
  353.8 14.8 %collective-permute-start.17 = (bf16[160,2048]{1,0:T(8,128)(2,1)S(1)}, bf16[160,2048]{1,0:T(8,128)(2,1)S(1)}, u32[]{:S(2)}, u32[]{:S(2)}) collective-permute-start(bf16[160,2048]{1,0:T(8,128)(2,1)S(1)} %collective-permute-done.15), channel_id=1, source_target_pairs={{0,2},{2,4},{4,6},{6,7},{7,5},{5,3},{3,1},{1,0},{8,10},{10,12},{12... | collective-permute-start | bytes 1966088 | tf_op jit(solution)/shard_map/ppermute | solution.py:80
  489.0 12.0 %collective-permute-start.29 = (bf16[160,2048]{1,0:T(8,128)(2,1)S(1)}, bf16[160,2048]{1,0:T(8,128)(2,1)S(1)}, u32[]{:S(2)}, u32[]{:S(2)}) collective-permute-start(bf16[160,2048]{1,0:T(8,128)(2,1)S(1)} %pad_maximum_fusion.7), channel_id=1, source_target_pairs={{0,2},{2,4},{4,6},{6,7},{7,5},{5,3},{3,1},{1,0},{8,10},{10,12},{12... | collective-permute-start | bytes 1966088 | tf_op jit(solution)/shard_map/ppermute | solution.py:80
  492.8 41.1 %all-to-all-start.3 = ((f32[8,160,2]{1,2,0:T(2,128)}), f32[8,160,2]{1,2,0:T(2,128)S(1)}, u32[]{:S(2)}, u32[]{:S(2)}) async-start(f32[8,160,2]{1,2,0:T(2,128)} %constant_dynamic-update-slice_fusion.42), calls=%async_computation.3 | async-start | bytes 32768 | tf_op jit(solution)/shard_map/all_to_all | solution.py:161
  497.0 146.5 %all-reduce.5.cloned.1.call-start = ((), (), s32[]{:S(2)}) async-start(), calls=%async_computation.13 | async-start | bytes 278528
  503.0 13.1 %collective-permute-start.30 = (bf16[160,2048]{1,0:T(8,128)(2,1)S(1)}, bf16[160,2048]{1,0:T(8,128)(2,1)S(1)}, u32[]{:S(2)}, u32[]{:S(2)}) collective-permute-start(bf16[160,2048]{1,0:T(8,128)(2,1)S(1)} %get-tuple-element.155), channel_id=1, source_target_pairs={{0,2},{2,4},{4,6},{6,7},{7,5},{5,3},{3,1},{1,0},{8,10},{10,12},{12... | collective-permute-start | bytes 1966088 | tf_op jit(solution)/shard_map/ppermute | solution.py:80
  505.9 12.7 %collective-permute-start.34 = (bf16[160,2048]{1,0:T(8,128)(2,1)S(1)}, bf16[160,2048]{1,0:T(8,128)(2,1)S(1)}, u32[]{:S(2)}, u32[]{:S(2)}) collective-permute-start(bf16[160,2048]{1,0:T(8,128)(2,1)S(1)} %get-tuple-element.156), channel_id=1, source_target_pairs={{0,1},{2,0},{4,2},{6,4},{7,6},{5,7},{3,5},{1,3},{8,9},{10,8},{12,1... | collective-permute-start | bytes 1966088 | tf_op jit(solution)/shard_map/ppermute | solution.py:80
  521.5 16.2 %collective-permute-start.31 = (bf16[160,2048]{1,0:T(8,128)(2,1)}, bf16[160,2048]{1,0:T(8,128)(2,1)}, u32[]{:S(2)}, u32[]{:S(2)}) collective-permute-start(bf16[160,2048]{1,0:T(8,128)(2,1)} %get-tuple-element.153), channel_id=1, source_target_pairs={{0,2},{2,4},{4,6},{6,7},{7,5},{5,3},{3,1},{1,0},{8,10},{10,12},{12... | collective-permute-start | bytes 1966088 | tf_op jit(solution)/shard_map/ppermute | solution.py:80
  524.3 13.4 %collective-permute-start.35 = (bf16[160,2048]{1,0:T(8,128)(2,1)}, bf16[160,2048]{1,0:T(8,128)(2,1)}, u32[]{:S(2)}, u32[]{:S(2)}) collective-permute-start(bf16[160,2048]{1,0:T(8,128)(2,1)} %get-tuple-element.154), channel_id=1, source_target_pairs={{0,1},{2,0},{4,2},{6,4},{7,6},{5,7},{3,5},{1,3},{8,9},{10,8},{12,1... | collective-permute-start | bytes 1966088 | tf_op jit(solution)/shard_map/ppermute | solution.py:80
  541.5 412.1 %reduce-scatter.8.cloned.1.call-start = ((), (), s32[]{:S(2)}) async-start(), calls=%async_computation.12 | async-start | bytes 10485760 | tf_op jit(solution)/shard_map/reduce_scatter | solution.py:483
  549.1 408.5 %reduce-scatter.6.cloned.1.call-start = ((), (), s32[]{:S(2)}) async-start(), calls=%async_computation.11 | async-start | bytes 10485760 | tf_op jit(solution)/shard_map/reduce_scatter | solution.py:483
  618.4 26.8 %all-to-all-start.4 = ((bf16[8,160,256]{2,1,0:T(8,128)(2,1)}), bf16[8,160,256]{2,1,0:T(8,128)(2,1)}, u32[]{:S(2)}, u32[]{:S(2)}) async-start(bf16[8,160,256]{2,1,0:T(8,128)(2,1)} %bitcast.235), calls=%async_computation.4 | async-start | bytes 1310720 | tf_op jit(solution)/shard_map/all_to_all | solution.py:161
  623.7 338.1 %reduce-scatter.4.cloned.1.call-start = ((), (), s32[]{:S(2)}) async-start(), calls=%async_computation.10 | async-start | bytes 10485760 | tf_op jit(solution)/shard_map/reduce_scatter | solution.py:483
  671.6 117.5 %collective-permute-start.56 = (bf16[160,2048]{1,0:T(8,128)(2,1)}, bf16[160,2048]{1,0:T(8,128)(2,1)}, u32[]{:S(2)}, u32[]{:S(2)}) collective-permute-start(bf16[160,2048]{1,0:T(8,128)(2,1)} %get-tuple-element.25), channel_id=1, source_target_pairs={{0,1},{2,0},{4,2},{6,4},{7,6},{5,7},{3,5},{1,3},{8,9},{10,8},{12,1... | collective-permute-start | bytes 1966088 | tf_op jit(solution)/shard_map/ppermute | solution.py:80
  673.6 117.2 %collective-permute-start.57 = (bf16[160,2048]{1,0:T(8,128)(2,1)}, bf16[160,2048]{1,0:T(8,128)(2,1)}, u32[]{:S(2)}, u32[]{:S(2)}) collective-permute-start(bf16[160,2048]{1,0:T(8,128)(2,1)} %get-tuple-element.25), channel_id=1, source_target_pairs={{0,2},{2,4},{4,6},{6,7},{7,5},{5,3},{3,1},{1,0},{8,10},{10,12},{12... | collective-permute-start | bytes 1966088 | tf_op jit(solution)/shard_map/ppermute | solution.py:80
  766.0 67.6 %collective-permute-start.52 = (bf16[8,2,64,768]{3,2,0,1:T(8,128)(2,1)S(1)}, bf16[8,2,64,768]{3,2,0,1:T(8,128)(2,1)S(1)}, u32[]{:S(2)}, u32[]{:S(2)}) collective-permute-start(bf16[8,2,64,768]{3,2,0,1:T(8,128)(2,1)S(1)} %bitcast.292), channel_id=1, source_target_pairs={{0,8},{8,0},{16,24},{24,16},{1,9},{9,1},{17,25},{25,17},{2,10},{10... | collective-permute-start | bytes 4718600 | tf_op jit(solution)/shard_map/ppermute | solution.py:126
  785.7 17.7 %collective-permute-start.49 = (bf16[160,2048]{1,0:T(8,128)(2,1)S(1)}, bf16[160,2048]{1,0:T(8,128)(2,1)S(1)}, u32[]{:S(2)}, u32[]{:S(2)}) collective-permute-start(bf16[160,2048]{1,0:T(8,128)(2,1)S(1)} %pad_maximum_fusion.12), channel_id=1, source_target_pairs={{0,1},{2,0},{4,2},{6,4},{7,6},{5,7},{3,5},{1,3},{8,9},{10,8},{12,1... | collective-permute-start | bytes 1966088 | tf_op jit(solution)/shard_map/ppermute | solution.py:80
  785.9 17.7 %collective-permute-start.45 = (bf16[160,2048]{1,0:T(8,128)(2,1)S(1)}, bf16[160,2048]{1,0:T(8,128)(2,1)S(1)}, u32[]{:S(2)}, u32[]{:S(2)}) collective-permute-start(bf16[160,2048]{1,0:T(8,128)(2,1)S(1)} %pad_maximum_fusion.11), channel_id=1, source_target_pairs={{0,2},{2,4},{4,6},{6,7},{7,5},{5,3},{3,1},{1,0},{8,10},{10,12},{12... | collective-permute-start | bytes 1966088 | tf_op jit(solution)/shard_map/ppermute | solution.py:80
  789.1 28.3 %collective-permute-start.41 = (bf16[160,2048]{1,0:T(8,128)(2,1)S(1)}, bf16[160,2048]{1,0:T(8,128)(2,1)S(1)}, u32[]{:S(2)}, u32[]{:S(2)}) collective-permute-start(bf16[160,2048]{1,0:T(8,128)(2,1)S(1)} %pad_maximum_fusion.10), channel_id=1, source_target_pairs={{0,1},{2,0},{4,2},{6,4},{7,6},{5,7},{3,5},{1,3},{8,9},{10,8},{12,1... | collective-permute-start | bytes 1966088 | tf_op jit(solution)/shard_map/ppermute | solution.py:80
  790.7 27.2 %collective-permute-start.37 = (bf16[160,2048]{1,0:T(8,128)(2,1)S(1)}, bf16[160,2048]{1,0:T(8,128)(2,1)S(1)}, u32[]{:S(2)}, u32[]{:S(2)}) collective-permute-start(bf16[160,2048]{1,0:T(8,128)(2,1)S(1)} %pad_maximum_fusion.9), channel_id=1, source_target_pairs={{0,2},{2,4},{4,6},{6,7},{7,5},{5,3},{3,1},{1,0},{8,10},{10,12},{12... | collective-permute-start | bytes 1966088 | tf_op jit(solution)/shard_map/ppermute | solution.py:80
  803.4 28.1 %collective-permute-start.58 = (bf16[160,2048]{1,0:T(8,128)(2,1)}, bf16[160,2048]{1,0:T(8,128)(2,1)S(1)}, u32[]{:S(2)}, u32[]{:S(2)}) collective-permute-start(bf16[160,2048]{1,0:T(8,128)(2,1)} %collective-permute-done.56), channel_id=1, source_target_pairs={{0,1},{2,0},{4,2},{6,4},{7,6},{5,7},{3,5},{1,3},{8,9},{10,8},{12,1... | collective-permute-start | bytes 1966088 | tf_op jit(solution)/shard_map/ppermute | solution.py:80
  803.6 28.4 %collective-permute-start.59 = (bf16[160,2048]{1,0:T(8,128)(2,1)}, bf16[160,2048]{1,0:T(8,128)(2,1)S(1)}, u32[]{:S(2)}, u32[]{:S(2)}) collective-permute-start(bf16[160,2048]{1,0:T(8,128)(2,1)} %collective-permute-done.57), channel_id=1, source_target_pairs={{0,2},{2,4},{4,6},{6,7},{7,5},{5,3},{3,1},{1,0},{8,10},{10,12},{12... | collective-permute-start | bytes 1966088 | tf_op jit(solution)/shard_map/ppermute | solution.py:80
  817.4 28.3 %collective-permute-start.46 = (bf16[160,2048]{1,0:T(8,128)(2,1)S(1)}, bf16[160,2048]{1,0:T(8,128)(2,1)S(1)}, u32[]{:S(2)}, u32[]{:S(2)}) collective-permute-start(bf16[160,2048]{1,0:T(8,128)(2,1)S(1)} %get-tuple-element.135), channel_id=1, source_target_pairs={{0,2},{2,4},{4,6},{6,7},{7,5},{5,3},{3,1},{1,0},{8,10},{10,12},{12... | collective-permute-start | bytes 1966088 | tf_op jit(solution)/shard_map/ppermute | solution.py:80
  817.9 29.4 %collective-permute-start.50 = (bf16[160,2048]{1,0:T(8,128)(2,1)S(1)}, bf16[160,2048]{1,0:T(8,128)(2,1)S(1)}, u32[]{:S(2)}, u32[]{:S(2)}) collective-permute-start(bf16[160,2048]{1,0:T(8,128)(2,1)S(1)} %get-tuple-element.136), channel_id=1, source_target_pairs={{0,1},{2,0},{4,2},{6,4},{7,6},{5,7},{3,5},{1,3},{8,9},{10,8},{12,1... | collective-permute-start | bytes 1966088 | tf_op jit(solution)/shard_map/ppermute | solution.py:80
  831.5 58.0 %collective-permute-start.38 = (bf16[160,2048]{1,0:T(8,128)(2,1)S(1)}, bf16[160,2048]{1,0:T(8,128)(2,1)}, u32[]{:S(2)}, u32[]{:S(2)}) collective-permute-start(bf16[160,2048]{1,0:T(8,128)(2,1)S(1)} %get-tuple-element.145), channel_id=1, source_target_pairs={{0,2},{2,4},{4,6},{6,7},{7,5},{5,3},{3,1},{1,0},{8,10},{10,12},{12... | collective-permute-start | bytes 1966088 | tf_op jit(solution)/shard_map/ppermute | solution.py:80
  832.0 41.2 %collective-permute-start.60 = (bf16[160,2048]{1,0:T(8,128)(2,1)S(1)}, bf16[160,2048]{1,0:T(8,128)(2,1)S(1)}, u32[]{:S(2)}, u32[]{:S(2)}) collective-permute-start(bf16[160,2048]{1,0:T(8,128)(2,1)S(1)} %collective-permute-done.58), channel_id=1, source_target_pairs={{0,1},{2,0},{4,2},{6,4},{7,6},{5,7},{3,5},{1,3},{8,9},{10,8},{12,1... | collective-permute-start | bytes 1966088 | tf_op jit(solution)/shard_map/ppermute | solution.py:80
  833.7 37.8 %collective-permute-start.61 = (bf16[160,2048]{1,0:T(8,128)(2,1)S(1)}, bf16[160,2048]{1,0:T(8,128)(2,1)S(1)}, u32[]{:S(2)}, u32[]{:S(2)}) collective-permute-start(bf16[160,2048]{1,0:T(8,128)(2,1)S(1)} %collective-permute-done.59), channel_id=1, source_target_pairs={{0,2},{2,4},{4,6},{6,7},{7,5},{5,3},{3,1},{1,0},{8,10},{10,12},{12... | collective-permute-start | bytes 1966088 | tf_op jit(solution)/shard_map/ppermute | solution.py:80
  845.7 43.7 %collective-permute-start.42 = (bf16[160,2048]{1,0:T(8,128)(2,1)S(1)}, bf16[160,2048]{1,0:T(8,128)(2,1)}, u32[]{:S(2)}, u32[]{:S(2)}) collective-permute-start(bf16[160,2048]{1,0:T(8,128)(2,1)S(1)} %get-tuple-element.146), channel_id=1, source_target_pairs={{0,1},{2,0},{4,2},{6,4},{7,6},{5,7},{3,5},{1,3},{8,9},{10,8},{12,1... | collective-permute-start | bytes 1966088 | tf_op jit(solution)/shard_map/ppermute | solution.py:80
  847.3 37.5 %collective-permute-start.53 = (bf16[8,1,64,768]{3,2,0,1:T(8,128)(2,1)S(1)}, bf16[8,1,64,768]{3,2,0,1:T(8,128)(2,1)S(1)}, u32[]{:S(2)}, u32[]{:S(2)}) collective-permute-start(bf16[8,1,64,768]{3,2,0,1:T(8,128)(2,1)S(1)} %constant_dynamic-slice_fusion.1), channel_id=1, source_target_pairs={{0,16},{8,24},{16,0},{24,8},{1,17},{9,25},{17,1},{25,9},{2,18},{10... | collective-permute-start | bytes 2359304 | tf_op jit(solution)/shard_map/ppermute | solution.py:126
  879.2 15.8 %collective-permute-start.47 = (bf16[160,2048]{1,0:T(8,128)(2,1)}, bf16[160,2048]{1,0:T(8,128)(2,1)}, u32[]{:S(2)}, u32[]{:S(2)}) collective-permute-start(bf16[160,2048]{1,0:T(8,128)(2,1)} %get-tuple-element.133), channel_id=1, source_target_pairs={{0,2},{2,4},{4,6},{6,7},{7,5},{5,3},{3,1},{1,0},{8,10},{10,12},{12... | collective-permute-start | bytes 1966088 | tf_op jit(solution)/shard_map/ppermute | solution.py:80
  880.9 15.3 %collective-permute-start.51 = (bf16[160,2048]{1,0:T(8,128)(2,1)}, bf16[160,2048]{1,0:T(8,128)(2,1)}, u32[]{:S(2)}, u32[]{:S(2)}) collective-permute-start(bf16[160,2048]{1,0:T(8,128)(2,1)} %get-tuple-element.134), channel_id=1, source_target_pairs={{0,1},{2,0},{4,2},{6,4},{7,6},{5,7},{3,5},{1,3},{8,9},{10,8},{12,1... | collective-permute-start | bytes 1966088 | tf_op jit(solution)/shard_map/ppermute | solution.py:80
  884.8 13.5 %collective-permute-start.64 = (bf16[2,64,2048]{2,1,0:T(8,128)(2,1)}, bf16[2,64,2048]{2,1,0:T(8,128)(2,1)}, u32[]{:S(2)}, u32[]{:S(2)}) collective-permute-start(bf16[2,64,2048]{2,1,0:T(8,128)(2,1)} %dynamic-slice_bitcast_fusion), channel_id=1, source_target_pairs={{0,8},{8,0},{16,24},{24,16},{1,9},{9,1},{17,25},{25,17},{2,10},{10... | collective-permute-start | bytes 1572872 | tf_op jit(solution)/shard_map/ppermute | solution.py:126
  885.9 26.9 %all-to-all-start.5 = ((bf16[8,64,768]{2,1,0:T(8,128)(2,1)}), bf16[8,64,768]{2,1,0:T(8,128)(2,1)S(1)}, u32[]{:S(2)}, u32[]{:S(2)}) async-start(bf16[8,64,768]{2,1,0:T(8,128)(2,1)} %fusion.63), calls=%async_computation.5 | async-start | bytes 1572864 | tf_op jit(solution)/shard_map/all_to_all | solution.py:161
  892.8 43.9 %collective-permute-start.39 = (bf16[160,2048]{1,0:T(8,128)(2,1)}, bf16[160,2048]{1,0:T(8,128)(2,1)}, u32[]{:S(2)}, u32[]{:S(2)}) collective-permute-start(bf16[160,2048]{1,0:T(8,128)(2,1)} %get-tuple-element.143), channel_id=1, source_target_pairs={{0,2},{2,4},{4,6},{6,7},{7,5},{5,3},{3,1},{1,0},{8,10},{10,12},{12... | collective-permute-start | bytes 1966088 | tf_op jit(solution)/shard_map/ppermute | solution.py:80
  894.7 42.0 %collective-permute-start.43 = (bf16[160,2048]{1,0:T(8,128)(2,1)}, bf16[160,2048]{1,0:T(8,128)(2,1)}, u32[]{:S(2)}, u32[]{:S(2)}) collective-permute-start(bf16[160,2048]{1,0:T(8,128)(2,1)} %get-tuple-element.144), channel_id=1, source_target_pairs={{0,1},{2,0},{4,2},{6,4},{7,6},{5,7},{3,5},{1,3},{8,9},{10,8},{12,1... | collective-permute-start | bytes 1966088 | tf_op jit(solution)/shard_map/ppermute | solution.py:80
  900.2 14.1 %collective-permute-start.65 = (bf16[1,64,2048]{2,1,0:T(8,128)(2,1)S(1)}, bf16[1,64,2048]{2,1,0:T(8,128)(2,1)S(1)}, u32[]{:S(2)}, u32[]{:S(2)}) collective-permute-start(bf16[1,64,2048]{2,1,0:T(8,128)(2,1)S(1)} %constant_dynamic-slice_fusion), channel_id=1, source_target_pairs={{0,16},{8,24},{16,0},{24,8},{1,17},{9,25},{17,1},{25,9},{2,18},{10... | collective-permute-start | bytes 786440 | tf_op jit(solution)/shard_map/ppermute | solution.py:126
  912.8 19.8 %collective-permute-start.54 = (bf16[1,8,64,768]{3,2,1,0:T(8,128)(2,1)S(1)}, bf16[1,8,64,768]{3,2,1,0:T(8,128)(2,1)S(1)}, u32[]{:S(2)}, u32[]{:S(2)}) collective-permute-start(bf16[1,8,64,768]{3,2,1,0:T(8,128)(2,1)S(1)} %bitcast.260), channel_id=1, source_target_pairs={{0,16},{8,24},{16,0},{24,8},{1,17},{9,25},{17,1},{25,9},{2,18},{10... | collective-permute-start | bytes 2359304 | tf_op jit(solution)/shard_map/ppermute | solution.py:126
  915.4 20.7 %collective-permute-start.66 = (bf16[1,64,2048]{2,1,0:T(8,128)(2,1)S(1)}, bf16[1,64,2048]{2,1,0:T(8,128)(2,1)S(1)}, u32[]{:S(2)}, u32[]{:S(2)}) collective-permute-start(bf16[1,64,2048]{2,1,0:T(8,128)(2,1)S(1)} %add_convert_fusion.21), channel_id=1, source_target_pairs={{0,16},{8,24},{16,0},{24,8},{1,17},{9,25},{17,1},{25,9},{2,18},{10... | collective-permute-start | bytes 786440 | tf_op jit(solution)/shard_map/ppermute | solution.py:126
  (111 other events, 1784.5 us)
Sparse Core Ops, SparseCore 0:
  131.2 63.6 all-gather.1
  541.6 70.5 all-reduce.4
  614.9 70.8 reduce-scatter.7
  688.2 72.2 reduce-scatter.5
  763.2 71.6 reduce-scatter.3

commit v3 on v2

--- a/solution.py
+++ b/solution.py
@@ -1,6 +1,8 @@
 import jax
 import jax.numpy as jnp
 from jax import lax
+from jax.experimental import pallas as pl
+from jax.experimental.pallas import tpu as pltpu
 from jax.sharding import PartitionSpec as P
 
 epsilon = 1e-05
@@ -59,6 +61,10 @@
         (((left_dim,), (right_dim,)), ((), ())),
         preferred_element_type=wide_type,
     )
+
+
+def gather_rows(values):
+    return lax.all_gather(values, "ep", axis=0, tiled=True)
 
 
 def ring_order(count):
@@ -121,6 +127,26 @@
     return (left.astype(wide_type) + right.astype(wide_type)).astype(low_type)
 
 
+def ring_place(member, count):
+    return jnp.where(member % 2 == 0, member // 2, count - 1 - member // 2)
+
+
+def ring_member(place, count):
+    return jnp.where(place < count // 2, 2 * place, 2 * (count - 1 - place) + 1)
+
+
+def ring_indices(device, count):
+    place = ring_place(device, count)
+    half = count // 2
+    members = [ring_member((place + offset) % count, count) for offset in ring_slots(count)]
+    slots = []
+    for other in range(count):
+        ahead = (ring_place(jnp.int32(other), count) - place) % count
+        slot = jnp.where(ahead < half, 2 * ahead - 1, 2 * (count - ahead))
+        slots.append(jnp.where(ahead == 0, 0, jnp.where(ahead == half, count - 1, slot)))
+    return members, slots
+
+
 def rep_exchange(values, distance):
     count = lax.axis_size("rep")
     return lax.ppermute(values, "rep", [(i, i ^ distance) for i in range(count)])
@@ -157,8 +183,121 @@
     return lax.index_in_dim(values, 0, axis, keepdims=False)
 
 
+def rep_pieces(values):
+    pieces = {0: values}
+    distance = lax.axis_size("rep") // 2
+    while distance:
+        for j in list(pieces):
+            pieces[j ^ distance] = rep_exchange(pieces[j], distance)
+        distance //= 2
+    return pieces
+
+
+def rep_sum(values):
+    distance = 1
+    while distance < lax.axis_size("rep"):
+        values = values + rep_exchange(values, distance)
+        distance *= 2
+    return values
+
+
 def swap_all(values):
     return lax.all_to_all(values, "ep", split_axis=0, concat_axis=0, tiled=True)
+
+
+def expert_kernel(
+    rows_ref, gate_ref, up_ref, stream_ref, gates_ref, inner_ref, gback_ref, uback_ref, pair_ref
+):
+    expert, step = pl.program_id(0), pl.program_id(1)
+    rows = rows_ref[...]
+    gate_linear = jnp.dot(rows, gate_ref[0], preferred_element_type=wide_type)
+    up_linear = jnp.dot(rows, up_ref[0], preferred_element_type=wide_type)
+    stream = stream_ref[...]
+    column = gates_ref[:, 0:1]
+    for other in range(1, gates_ref.shape[1]):
+        column = jnp.where(expert == other, gates_ref[:, other : other + 1], column)
+    sigmoid_gate = jax.nn.sigmoid(gate_linear)
+    silu_gate = gate_linear * sigmoid_gate
+    inner = silu_gate * up_linear
+    inner_ref[...] = (column * inner).astype(low_type)
+    hidden_grad = column * stream
+    gback_ref[...] = (
+        hidden_grad * up_linear * sigmoid_gate * (1.0 + gate_linear * (1.0 - sigmoid_gate))
+    ).astype(low_type)
+    uback_ref[...] = (hidden_grad * silu_gate).astype(low_type)
+    product = inner * stream
+    lanes = pair_ref.shape[2]
+    folded = product[:, :lanes]
+    for start in range(lanes, product.shape[1], lanes):
+        folded = folded + product[:, start : start + lanes]
+
+    @pl.when(step == 0)
+    def _():
+        pair_ref[0] = folded
+
+    @pl.when(step > 0)
+    def _():
+        pair_ref[0] += folded
+
+
+def expert_pass(rows, gate_weight, up_weight, stream, gates):
+    count, depth = rows.shape
+    experts, _, hidden = gate_weight.shape
+    width = 256
+    steps = hidden // width
+    wide = pl.BlockSpec((count, width), lambda e, j: (0, e * steps + j))
+    weight = pl.BlockSpec((1, depth, width), lambda e, j: (e, 0, j))
+    return pl.pallas_call(
+        expert_kernel,
+        grid=(experts, steps),
+        in_specs=[
+            pl.BlockSpec((count, depth), lambda e, j: (0, 0)),
+            weight,
+            weight,
+            wide,
+            pl.BlockSpec(gates.shape, lambda e, j: (0, 0)),
+        ],
+        out_specs=[wide, wide, wide, pl.BlockSpec((1, count, 128), lambda e, j: (e, 0, 0))],
+        out_shape=[jax.ShapeDtypeStruct((count, experts * hidden), low_type)] * 3
+        + [jax.ShapeDtypeStruct((experts, count, 128), wide_type)],
+        compiler_params=pltpu.CompilerParams(vmem_limit_bytes=56 << 20),
+        cost_estimate=pl.CostEstimate(
+            flops=4 * count * depth * experts * hidden,
+            bytes_accessed=4 * depth * experts * hidden + 20 * count * depth,
+            transcendentals=count * experts * hidden,
+        ),
+    )(rows, gate_weight, up_weight, stream, gates)
+
+
+def expert_back_kernel(gback_ref, uback_ref, gate_ref, up_ref, out_ref):
+    experts, _, hidden = gate_ref.shape
+    total = None
+    for e in range(experts):
+        for grad_ref, weight_ref in ((gback_ref, gate_ref), (uback_ref, up_ref)):
+            term = mm(grad_ref[:, e * hidden : (e + 1) * hidden], weight_ref[e], 1, 1)
+            total = term if total is None else total + term
+    out_ref[...] = total.astype(low_type)
+
+
+def expert_back(gback, uback, gate_weight, up_weight):
+    count = gback.shape[0]
+    experts, depth, hidden = gate_weight.shape
+    width = 256
+    whole = pl.BlockSpec((count, experts * hidden), lambda j: (0, 0))
+    weight = pl.BlockSpec((experts, width, hidden), lambda j: (0, j, 0))
+    return pl.pallas_call(
+        expert_back_kernel,
+        grid=(depth // width,),
+        in_specs=[whole, whole, weight, weight],
+        out_specs=pl.BlockSpec((count, width), lambda j: (0, j)),
+        out_shape=jax.ShapeDtypeStruct((count, depth), low_type),
+        compiler_params=pltpu.CompilerParams(vmem_limit_bytes=56 << 20),
+        cost_estimate=pl.CostEstimate(
+            flops=4 * count * depth * experts * hidden,
+            bytes_accessed=4 * depth * experts * hidden + 6 * count * depth,
+            transcendentals=0,
+        ),
+    )(gback, uback, gate_weight, up_weight)
 
 
 def body(
@@ -199,16 +338,7 @@
     replica = lax.axis_index("rep")
     share = width_here // replica_count
 
-    order = ring_order(group_count)
-    offsets = ring_slots(group_count)
-    place_of = jnp.array([order.index(i) for i in range(group_count)], jnp.int32)
-    place = place_of[device]
-    device_of_slot = jnp.array(order, jnp.int32)[(place + jnp.array(offsets)) % group_count]
-    slot_of_offset = jnp.array(
-        [[j for j, o in enumerate(offsets) if o % group_count == i][0] for i in range(group_count)],
-        jnp.int32,
-    )
-    slot_of_device = slot_of_offset[(place_of - place) % group_count]
+    device_of_slot, slot_of_device = ring_indices(device, group_count)
 
     def reorder(blocks, index):
         return jnp.concatenate(
@@ -252,23 +382,23 @@
         .transpose(1, 0, 2, 3)
         .reshape(model_width, 3 * width_here)
     )
-    token_blocks = ring_gather(tokens)
-    token_last, cot_own, output_weight_own = lax.optimization_barrier(
-        (token_blocks[-1], cotangent, output_weight)
-    )
-    token_all = jnp.concatenate(token_blocks[:-1] + [token_last], axis=0)
-    cot_all = jnp.concatenate(ring_gather(cot_own), axis=0)
+    token_all = jnp.concatenate(ring_gather(tokens), axis=0)
     column_share = model_width // replica_count
-    full_output = rep_gather(
-        lax.all_gather(
-            lax.dynamic_slice_in_dim(
-                output_weight_own, replica * column_share, column_share, 1
-            ),
-            "ep",
-            axis=0,
-            tiled=True,
-        )
-    )
+    output_pieces = rep_pieces(
+        gather_rows(
+            lax.dynamic_slice_in_dim(output_weight, replica * column_share, column_share, 1)
+        )
+    )
+
+    def reorder_rows(rows, index):
+        return reorder(
+            rows.reshape(group_count, row_count, rows.shape[1]), index
+        ).reshape(rows.shape)
+
+    token_late, cot_own = lax.optimization_barrier((token_all, cotangent))
+    token_all = token_late
+    cot_ordered = gather_rows(cot_own)
+    cot_all = reorder_rows(cot_ordered, device_of_slot)
 
     token_wide = token_all.astype(wide_type)
     inverse_all = inverse_rms(token_wide)
@@ -276,7 +406,9 @@
     raw = mm(first_all, head_weight, 1, 0)
     cosine, sine_part = rope_tables(position, head_dim)
 
-    up_stream = [mm(cot_all, down_weight[e], 1, 1) for e in range(experts_here)]
+    hidden_here = down_weight.shape[1]
+    flat_down = down_weight.reshape(experts_here * hidden_here, model_width)
+    up_stream = mm(cot_all, flat_down, 1, 1)
 
     allowed = segment[:, None] == segment[None, :]
 
@@ -309,14 +441,17 @@
         )
     mixed_low = jnp.concatenate(mixed_parts, axis=1)
 
+    mixed_ordered = reorder_rows(mixed_low, slot_of_device)
     mixed_own = (
-        swap_all(reorder(mixed_low.reshape(group_count, row_count, width_here), slot_of_device))
+        swap_all(mixed_ordered.reshape(group_count, row_count, width_here))
         .transpose(1, 0, 2)
         .reshape(row_count, model_width)
     )
-    attention = lax.dot_general(
-        mixed_own, full_output, (((1,), (1,)), ((), ())), preferred_element_type=wide_type
-    ).reshape(row_count, model_width)
+    attention = jnp.zeros((row_count, model_width), wide_type)
+    for j, piece in output_pieces.items():
+        attention = lax.dynamic_update_slice_in_dim(
+            attention, mm(mixed_own, piece, 1, 0), (replica ^ j) * column_share, 1
+        )
     residual = tokens.astype(wide_type) + attention
     inverse_two = inverse_rms(residual)
     second_input = (residual * inverse_two * postnorm_gain).astype(low_type)
@@ -335,43 +470,25 @@
         jnp.where(code_all > 1, valid_all, 0.0), device * experts_here, experts_here, 1
     )
 
-    mixture_part = jnp.zeros((group_rows, model_width), wide_type)
-    second_part = jnp.zeros((group_rows, model_width), wide_type)
-    pair_parts = []
-    gate_parts, up_parts, down_parts = [], [], []
-    for e in range(experts_here):
-        gate_linear = mm(second_all, gate_weight[e], 1, 0)
-        up_linear = mm(second_all, up_weight[e], 1, 0)
-        sigmoid_gate = jax.nn.sigmoid(gate_linear)
-        silu_gate = gate_linear * sigmoid_gate
-        inner = silu_gate * up_linear
-        gate_column = gates_here[:, e : e + 1]
-        inner_scaled = (gate_column * inner).astype(low_type)
-        pair_parts.append(
-            kept_here[:, e : e + 1] * jnp.sum(inner * up_stream[e], axis=1, keepdims=True)
-        )
-        hidden_grad = gate_column * up_stream[e]
-        gate_back = (
-            hidden_grad * up_linear * sigmoid_gate * (1.0 + gate_linear * (1.0 - sigmoid_gate))
-        ).astype(low_type)
-        up_back = (hidden_grad * silu_gate).astype(low_type)
-        mixture_part = mixture_part + mm(inner_scaled, down_weight[e], 1, 0)
-        second_part = (
-            second_part + mm(gate_back, gate_weight[e], 1, 1) + mm(up_back, up_weight[e], 1, 1)
-        )
-        down_parts.append(mm(inner_scaled, cot_all, 0, 0).astype(low_type))
-        gate_parts.append(mm(second_all, gate_back, 0, 0).astype(low_type))
-        up_parts.append(mm(second_all, up_back, 0, 0).astype(low_type))
-
-    pair_sent = jnp.concatenate(pair_parts, axis=1).reshape(
-        group_count, row_count, experts_here
-    )
+    inner_all, gback_all, uback_all, pair_lanes = expert_pass(
+        second_all, gate_weight, up_weight, up_stream, gates_here
+    )
+    second_part = expert_back(gback_all, uback_all, gate_weight, up_weight)
+    pair_sent = (
+        (kept_here * jnp.sum(pair_lanes, axis=2).transpose(1, 0))
+    ).reshape(group_count, row_count, experts_here)
+    down_part = mm(inner_all, cot_all, 0, 0).astype(low_type)
+    gate_part = mm(second_all, gback_all, 0, 0).astype(low_type)
     pair_grad = (
         swap_all(reorder(pair_sent, slot_of_device))
         .transpose(1, 0, 2)
         .reshape(row_count, expert_total)
     )
-    second_scattered = ring_scatter(second_part.astype(low_type))
+    second_scattered, uback_late, inner_late = lax.optimization_barrier(
+        (ring_scatter(second_part), uback_all, inner_all)
+    )
+    up_part = mm(second_all, uback_late, 0, 0).astype(low_type)
+    mixture_part = mm(inner_late, flat_down, 1, 0).astype(low_type)
     code_own = route_code
     gates_own = gate_table(second_input, code_own)
     chosen_grad = gates_own * (
@@ -384,23 +501,29 @@
     post_back, postnorm_part = norm_backward(residual, inverse_two, postnorm_gain, second_grad)
     residual_grad = upstream + post_back
     attention_low = residual_grad.astype(low_type)
-    mixed_grad_own = lax.dot_general(
-        attention_low.reshape(row_count, replica_count, column_share),
-        full_output,
-        (((1, 2), (0, 2)), ((), ())),
-        preferred_element_type=wide_type,
-    ).astype(low_type)
-    mixed_grad = reorder(
-        swap_all(mixed_grad_own.reshape(row_count, group_count, width_here).transpose(1, 0, 2)),
+    attention_all = gather_rows(attention_low)
+    mixed_grad_own = jnp.zeros((row_count, model_width), wide_type)
+    for j, piece in output_pieces.items():
+        mixed_grad_own = mixed_grad_own + mm(
+            lax.dynamic_slice_in_dim(
+                attention_low, (replica ^ j) * column_share, column_share, 1
+            ),
+            piece,
+            1,
+            1,
+        )
+    mixed_grad = reorder_rows(
+        swap_all(
+            mixed_grad_own.astype(low_type)
+            .reshape(row_count, group_count, width_here)
+            .transpose(1, 0, 2)
+        ).reshape(group_rows, width_here),
         device_of_slot,
-    ).reshape(group_rows, width_here)
-    mixed_grad, attention_sent, mixture_low = lax.optimization_barrier(
-        (mixed_grad, attention_low, mixture_part.astype(low_type))
-    )
-    attention_all = jnp.concatenate(ring_gather(attention_sent), axis=0)
+    )
+    mixed_grad, mixture_low = lax.optimization_barrier((mixed_grad, mixture_part))
     mixture = ring_scatter(mixture_low)
     layer_out = (valid_own * (residual + mixture)).astype(low_type)
-    output_part = mm(mixed_low, attention_all, 0, 0).astype(low_type)
+    output_part = mm(mixed_ordered, attention_all, 0, 0).astype(low_type)
 
     query_parts, key_parts, value_parts = [], [], []
     querynorm_part = jnp.zeros((head_dim,), wide_type)
@@ -436,18 +559,16 @@
     prenorm_part = jnp.sum(first_part * token_wide * inverse_all, axis=0)
     first_grad = ring_scatter(first_part.astype(low_type))
     head_part = mm(first_all, sent, 0, 0).astype(low_type)
+    head_rows = swap_all(
+        rep_scatter(head_part.reshape(group_count, replica_count, share, 3 * width_here), 1)
+    )
     head_rows = rep_gather(
-        swap_all(
-            rep_scatter(
-                head_part.reshape(group_count, replica_count, share, 3 * width_here), 1
-            )
-        )
+        head_rows.reshape(group_count, share, 3, width_here)
+        .transpose(2, 1, 0, 3)
+        .reshape(3, share, model_width)
     )
     query_grad, key_grad, value_grad = (
-        head_rows[..., block * width_here : (block + 1) * width_here]
-        .transpose(0, 2, 1, 3)
-        .reshape(width_here, model_width)
-        .astype(wide_type)
+        head_rows[:, block].reshape(width_here, model_width).astype(wide_type)
         for block in range(3)
     )
     output_grad = (
@@ -463,9 +584,7 @@
 
     def small_sum(parts):
         flat = jnp.concatenate([part.reshape(group_count, -1) for part in parts], axis=1)
-        total = lax.psum(
-            lax.psum_scatter(flat, "ep", scatter_dimension=0, tiled=True), "rep"
-        ).reshape(-1)
+        total = rep_sum(jnp.sum(swap_all(flat), axis=0))
         pieces, start = [], 0
         for part in parts:
             size = part.size // group_count
@@ -479,11 +598,18 @@
         [prenorm_part, querynorm_part, keynorm_part]
     )
 
-    gate_total, up_total, down_total = (
-        lax.psum_scatter(
-            jnp.stack(parts), "rep", scatter_dimension=1, tiled=True
-        ).astype(wide_type)
-        for parts in (gate_parts, up_parts, down_parts)
+    down_total = lax.psum_scatter(
+        down_part.reshape(experts_here, hidden_here, model_width),
+        "rep",
+        scatter_dimension=1,
+        tiled=True,
+    ).astype(wide_type)
+    gate_total, up_total = (
+        lax.psum_scatter(part, "rep", scatter_dimension=0, tiled=True)
+        .reshape(column_share, experts_here, hidden_here)
+        .transpose(1, 0, 2)
+        .astype(wide_type)
+        for part in (gate_part, up_part)
     )
     return (
         layer_out,

time: 982 us -> 787 us (0.80)
  matrix products: 275 us -> 156 us
  Pallas kernels: 0 us -> 64.1 us
  blocking collectives: 49.1 us -> 0 us
  between operations: 47.2 us -> 17.6 us
  other arithmetic: 118 us -> 95 us
  local copies, waits for them, and re-layouts: 110 us -> 87.1 us
  waiting for transfers between devices: 262 us -> 241 us
    dot_general x38 -> x33, matrix products: 265 us -> 156 us  [mm(): lax.dot_general(left, right, (((left_dim,), (right_dim,)), ((), ())), pre...]
    ppermute x56 -> x40, waiting for transfers between devices: 186 us -> 118 us  [ring_shift(): return lax.ppermute(values, 'ep', pairs)]
    pallas_call x0 -> x2, Pallas kernels: none -> 64.1 us  [the longest x1 34.9 us: expert_pass(): pl.pallas_call(expert_kernel, grid=(experts, steps), in_specs=[pl.BlockSp...]
    all_to_all x6 -> x8, waiting for transfers between devices: 11.1 us -> 74 us  [swap_all(): return lax.all_to_all(values, 'ep', split_axis=0, concat_axis=0, tiled=True)]
    unnamed x1 -> x0, blocking collectives: 37.5 us -> none
    another operation x4 -> x1, other arithmetic: 22.1 us -> 0.18 us  [the longest x3 21.9 us: body(): jnp.stack(parts)]
    unnamed x259 -> x315, local copies, waits for them, and re-layouts: 61.3 us -> 49.2 us
    psum x1 -> x0, blocking collectives: 11.5 us -> none  [small_sum(): lax.psum(lax.psum_scatter(flat, 'ep', scatter_dimension=0, tiled=True), '...]
  transfers between devices with their start and end apart: 79 -> 71, of which waited for: 36 -> 38; matrix products, arithmetic and copies ran while one was open for 37% -> 37% of each run, Pallas kernels for 0% -> 0%
where the time goes in v3:
time: 787 us; the launch traced here: 779 us
  waiting for transfers between devices  241 us (31%)
  matrix products  156 us (20%)
  starting transfers between devices  118 us (15%)
  other arithmetic  95 us (12%)
  local copies, waits for them, and re-layouts  87.1 us (11%)
  Pallas kernels  64.1 us (8%)
  between operations  17.6 us (2%)
    dot_general x33, matrix products, mm(): lax.dot_general(left, right, (((left_dim,), (right_dim,)), ((), ())), pre...  156 us
    ppermute x40, waiting for transfers between devices, ring_shift(): return lax.ppermute(values, 'ep', pairs)  118 us
    all_to_all x8, waiting for transfers between devices, swap_all(): return lax.all_to_all(values, 'ep', split_axis=0, concat_axis=0, tiled=True)  74 us
    ppermute x40, starting transfers between devices, ring_shift(): return lax.ppermute(values, 'ep', pairs)  66.2 us
    unnamed x315, local copies, waits for them, and re-layouts  49.2 us
    ppermute x17, waiting for transfers between devices, rep_exchange(): lax.ppermute(values, 'rep', [(i, i ^ distance) for i in range(count)])  48.5 us
    all_to_all x8, starting transfers between devices, swap_all(): return lax.all_to_all(values, 'ep', split_axis=0, concat_axis=0, tiled=True)  39.4 us
    pallas_call x1, Pallas kernels, expert_pass(): pl.pallas_call(expert_kernel, grid=(experts, steps), in_specs=[pl.BlockSp...  34.9 us
  transfers between devices with their start and end apart: 71, of which 38 were waited for; matrix products, arithmetic and copies ran while one was open for 37% of the time, Pallas kernels for 0%

profile of v3, /device:TPU:0, one launch (start us, length us, event | category | flops | bytes accessed | tf_op | source)
XLA Modules:
  0.0 779.2 jit_solution(12572171319305536215)
XLA Ops:
  7.2 3.0 collective-permute-start
  12.8 6.2 all-to-all-start
  23.5 4.1 collective-permute-done
  27.6 2.9 collective-permute-start.2
  31.8 20.7 %all-to-all-done = bf16[8,64,768]{2,1,0:T(8,128)(2,1)S(1)} async-done(((bf16[8,64,768]{2,1,0:T(8,128)(2,1)}), bf16[8,64,768]{2,1,0:T(8,128)(2,1)S(1)}, u32[]{:S(2)}, u32[]{:S(2)}) %all-to-all-start) | async-done | bytes 786464 | tf_op jit(solution)/shard_map/all_to_all | solution.py:205
  53.1 5.1 all-to-all-start.2
  64.9 19.3 %collective-permute-start.5 = (bf16[160,2048]{1,0:T(8,128)(2,1)}, bf16[160,2048]{1,0:T(8,128)(2,1)S(1)}, u32[]{:S(2)}, u32[]{:S(2)}) collective-permute-start(bf16[160,2048]{1,0:T(8,128)(2,1)} %collective-permute-done.3), channel_id=1, source_target_pairs={{0,2},{2,4},{4,6},{6,7},{7,5},{5,3},{3,1},{1,0},{8,10},{10,12},{12... | collective-permute-start | bytes 1966088 | tf_op jit(solution)/shard_map/ppermute | solution.py:86
  89.1 4.9 collective-permute-done.5
  94.0 5.5 collective-permute-start.6
  107.8 3.7 fusion
  113.1 3.5 maximum_select_fusion
  117.6 5.1 fusion.110
  139.8 18.0 %collective-permute-done.10 = bf16[2048,512]{1,0:T(8,128)(2,1)} collective-permute-done((bf16[2048,512]{1,0:T(8,128)(2,1)}, bf16[2048,512]{1,0:T(8,128)(2,1)}, u32[]{:S(2)}, u32[]{:S(2)}) %collective-permute-start.10) | collective-permute-done | bytes 2097184 | tf_op jit(solution)/shard_map/ppermute | solution.py:152
  158.5 6.2 all-to-all-start.1
  169.7 30.6 %all-to-all-done.1 = bf16[8,160,256]{2,1,0:T(8,128)(2,1)} async-done(((bf16[8,160,256]{2,1,0:T(8,128)(2,1)}), bf16[8,160,256]{2,1,0:T(8,128)(2,1)}, u32[]{:S(2)}, u32[]{:S(2)}) %all-to-all-start.1) | async-done | bytes 655392 | tf_op jit(solution)/shard_map/all_to_all | solution.py:205
  212.5 14.6 %collective-permute-done.13 = bf16[160,2048]{1,0:T(8,128)(2,1)} collective-permute-done((bf16[160,2048]{1,0:T(8,128)(2,1)S(1)}, bf16[160,2048]{1,0:T(8,128)(2,1)}, u32[]{:S(2)}, u32[]{:S(2)}) %collective-permute-start.13) | collective-permute-done | bytes 655392 | tf_op jit(solution)/shard_map/ppermute | solution.py:86
  231.8 11.3 %collective-permute-done.15 = bf16[160,2048]{1,0:T(8,128)(2,1)} collective-permute-done((bf16[160,2048]{1,0:T(8,128)(2,1)}, bf16[160,2048]{1,0:T(8,128)(2,1)}, u32[]{:S(2)}, u32[]{:S(2)}) %collective-permute-start.15) | collective-permute-done | bytes 655392 | tf_op jit(solution)/shard_map/ppermute | solution.py:86
  250.1 9.4 %collective-permute-done.18 = bf16[160,2048]{1,0:T(8,128)(2,1)S(1)} collective-permute-done((bf16[160,2048]{1,0:T(8,128)(2,1)}, bf16[160,2048]{1,0:T(8,128)(2,1)S(1)}, u32[]{:S(2)}, u32[]{:S(2)}) %collective-permute-start.18) | collective-permute-done | bytes 655392 | tf_op jit(solution)/shard_map/ppermute | solution.py:86
  263.5 3.1 collective-permute-done.19
  268.2 4.1 fusion.112
  281.8 16.2 %fusion.115.stream_ref = f32[1280,2048]{1,0:T(8,128)} fusion(bf16[1280,2048]{1,0:T(8,128)(2,1)S(1)} %bitcast.232, bf16[2048,2048]{1,0:T(8,128)(2,1)} %bitcast.304), kind=kOutput, calls=%fused_computation.372 | convolution fusion | flops 10737418240 | bytes 24117248 | tf_op jit(solution)/shard_map/dot_general | solution.py:58
  298.1 34.9 %shard_map.281 = (bf16[1280,2048]{1,0:T(8,128)(2,1)}, bf16[1280,2048]{1,0:T(8,128)(2,1)}, bf16[1280,2048]{1,0:T(8,128)(2,1)}, f32[2,1280,128]{2,1,0:T(8,128)}) custom-call(bf16[1280,2048]{1,0:T(8,128)(2,1)} %constant_dynamic-update-slice_fusion.25.rows_ref, bf16[2,2048,1024]{2,1,0:T(8,128)(2,1)} %gate_ref.3, bf16[2,2048,1024]{2,1,0:T(8,128)(2,1)} %up_ref.3, ...), custom_call_target="tpu_custom_call" | custom-call | flops 21474836480 | bytes 69206016 | tf_op jit(solution)/shard_map/pallas_call | solution.py:250
  333.0 29.1 %shard_map.282 = bf16[1280,2048]{1,0:T(8,128)(2,1)} custom-call(bf16[1280,2048]{1,0:T(8,128)(2,1)} %get-tuple-element.28.gback_ref, bf16[1280,2048]{1,0:T(8,128)(2,1)} %get-tuple-element.35.uback_ref, bf16[2,2048,1024]{2,1,0:T(8,128)(2,1)} %gate_ref.3, bf16[2,2048,1024]{2,1,0:T(8,128)(2,1)} %up_ref.3), custom_call_target="tpu_custom_call" | custom-call | flops 21474836480 | bytes 32505856 | tf_op jit(solution)/shard_map/pallas_call | solution.py:288
  365.6 5.0 collective-permute-done.21
  376.3 9.5 %collective-permute-done.26 = bf16[160,2048]{1,0:T(8,128)(2,1)S(1)} collective-permute-done((bf16[160,2048]{1,0:T(8,128)(2,1)S(1)}, bf16[160,2048]{1,0:T(8,128)(2,1)S(1)}, u32[]{:S(2)}, u32[]{:S(2)}) %collective-permute-start.26) | collective-permute-done | bytes 655392 | tf_op jit(solution)/shard_map/ppermute | solution.py:86
  388.0 2.8 add_convert_fusion.12
  397.4 6.9 collective-permute-done.23
  406.1 3.0 add_convert_fusion.11
  412.9 4.0 all-to-all-start.3
  417.7 5.8 all-to-all-done.3
  429.4 16.7 %convolution_convert_fusion.2 = bf16[2048,2048]{1,0:T(8,128)(2,1)} fusion(bf16[1280,2048]{1,0:T(8,128)(2,1)} %constant_dynamic-update-slice_fusion.25.rows_ref, bf16[1280,2048]{1,0:T(8,128)(2,1)} %get-tuple-element.28.gback_ref), kind=kOutput, calls=%fused_computation.14 | convolution fusion | flops 10741612544 | bytes 18874368 | tf_op jit(solution)/shard_map/dot_general | solution.py:58
  446.4 16.7 %convolution_convert_fusion = bf16[2048,2048]{1,0:T(8,128)(2,1)} fusion(bf16[1280,2048]{1,0:T(8,128)(2,1)} %get-tuple-element.32, bf16[1280,2048]{1,0:T(8,128)(2,1)} %bitcast.233), kind=kOutput, calls=%fused_computation.12 | convolution fusion | flops 10741612544 | bytes 18874368 | tf_op jit(solution)/shard_map/dot_general | solution.py:58
  463.8 2.7 fusion.114
  469.2 2.4 convolution_add_fusion.2
  474.1 2.5 fusion.10
  477.5 3.5 all-to-all-start.4
  482.4 16.7 %convolution_convert_fusion.3 = bf16[1280,2048]{1,0:T(8,128)(2,1)} fusion(bf16[1280,2048]{1,0:T(8,128)(2,1)} %get-tuple-element.32, bf16[2048,2048]{1,0:T(8,128)(2,1)} %bitcast.305), kind=kOutput, calls=%fused_computation.15 | convolution fusion | flops 10740039680 | bytes 18874368 | tf_op jit(solution)/shard_map/dot_general | solution.py:58
  499.1 15.7 %convolution_convert_fusion.1 = bf16[2048,2048]{1,0:T(8,128)(2,1)} fusion(bf16[1280,2048]{1,0:T(8,128)(2,1)S(1)} %bitcast.235, bf16[1280,2048]{1,0:T(8,128)(2,1)} %get-tuple-element.35.uback_ref), kind=kOutput, calls=%fused_computation.13 | convolution fusion | flops 10741612544 | bytes 18874368 | tf_op jit(solution)/shard_map/dot_general | solution.py:58
  515.7 6.2 all-to-all-start.6
  529.1 8.0 %multiply_reduce_fusion = (f32[1280]{0:T(1024)S(1)}, f32[1280,1280]{0,1:T(8,128)}) fusion(f32[1280,1280]{0,1:T(8,128)} %copy-done.3, f32[1280]{0:T(1024)S(1)} %copy-done.41, bf16[1280,768]{0,1:T(8,128)(2,1)} %copy-done.37, bf16[1280,256]{1,0:T(8,128)(2,1)S(1)} %bitcast.202), kind=kOutput, calls=%fused_computation.17 | convolution fusion | flops 424344320 | bytes 13775872 | tf_op jit(solution)/shard_map/dot_general | solution.py:58
  537.2 5.8 multiply_reduce_fusion.1
  543.0 4.2 multiply_convert_fusion
  551.0 4.4 multiply_convert_fusion.1
  566.1 5.5 convolution_convert_fusion.4
  575.1 6.2 fusion.4
  591.5 3.9 collective-permute-done.37
  613.7 4.7 collective-permute-done.42
  618.4 2.8 add_convert_fusion.4
  623.2 4.6 all-to-all-start.7
  628.9 16.9 %all-to-all-done.7 = f32[8,1,288]{2,1,0:T(1,128)S(1)} async-done(((f32[8,1,288]{2,1,0:T(1,128)}), f32[8,1,288]{2,1,0:T(1,128)S(1)}, u32[]{:S(2)}, u32[]{:S(2)}) %all-to-all-start.7) | async-done | bytes 9248 | tf_op jit(solution)/shard_map/all_to_all | solution.py:205
  645.9 3.5 all-to-all-start.5
  653.4 2.8 collective-permute-done.54
  660.3 3.3 add_convert_fusion.8
  665.6 3.1 add_convert_fusion.3
  674.4 7.2 collective-permute-done.31
  683.5 2.6 add_convert_fusion.7
  688.2 7.4 collective-permute-done.40
  701.0 6.4 collective-permute-done.32
  711.8 3.1 fusion.19
  715.5 3.8 maximum_select_fusion.1
  719.3 4.6 convolution_convert_fusion.5
  729.0 11.7 %collective-permute-done.50 = bf16[1,64,2048]{2,1,0:T(8,128)(2,1)S(1)} collective-permute-done((bf16[1,64,2048]{2,1,0:T(8,128)(2,1)S(1)}, bf16[1,64,2048]{2,1,0:T(8,128)(2,1)S(1)}, u32[]{:S(2)}, u32[]{:S(2)}) %collective-permute-start.50) | collective-permute-done | bytes 262176 | tf_op jit(solution)/shard_map/ppermute | solution.py:152
  743.6 11.4 %collective-permute-done.51 = bf16[1,64,2048]{2,1,0:T(8,128)(2,1)S(1)} collective-permute-done((bf16[1,64,2048]{2,1,0:T(8,128)(2,1)S(1)}, bf16[1,64,2048]{2,1,0:T(8,128)(2,1)S(1)}, u32[]{:S(2)}, u32[]{:S(2)}) %collective-permute-start.51) | collective-permute-done | bytes 262176 | tf_op jit(solution)/shard_map/ppermute | solution.py:152
  763.3 4.1 convert_element_type.564
  (622 shorter events, 237.4 us)
Async XLA Ops:
  7.2 20.4 %collective-permute-start = (bf16[160,2048]{1,0:T(8,128)(2,1)}, bf16[160,2048]{1,0:T(8,128)(2,1)}, u32[]{:S(2)}, u32[]{:S(2)}) collective-permute-start(bf16[160,2048]{1,0:T(8,128)(2,1)} %param.18), channel_id=1, source_target_pairs={{0,1},{2,0},{4,2},{6,4},{7,6},{5,7},{3,5},{1,3},{8,9},{10,8},{12,1... | collective-permute-start | bytes 1966088 | tf_op jit(solution)/shard_map/ppermute | solution.py:86
  10.2 20.3 %collective-permute-start.1 = (bf16[160,2048]{1,0:T(8,128)(2,1)}, bf16[160,2048]{1,0:T(8,128)(2,1)S(1)}, u32[]{:S(2)}, u32[]{:S(2)}) collective-permute-start(bf16[160,2048]{1,0:T(8,128)(2,1)} %param.18), channel_id=1, source_target_pairs={{0,2},{2,4},{4,6},{6,7},{7,5},{5,3},{3,1},{1,0},{8,10},{10,12},{12... | collective-permute-start | bytes 1966088 | tf_op jit(solution)/shard_map/ppermute | solution.py:86
  12.8 39.6 %all-to-all-start = ((bf16[8,64,768]{2,1,0:T(8,128)(2,1)}), bf16[8,64,768]{2,1,0:T(8,128)(2,1)S(1)}, u32[]{:S(2)}, u32[]{:S(2)}) async-start(bf16[8,64,768]{2,1,0:T(8,128)(2,1)} %copy.109), calls=%async_computation | async-start | bytes 1572864 | tf_op jit(solution)/shard_map/all_to_all | solution.py:205
  19.0 92.5 %all-gather.4.cloned.1.call-start = ((), (), s32[]{:S(2)}) async-start(), calls=%async_computation.11 | async-start | bytes 2359296 | tf_op jit(solution)/shard_map/all_gather | solution.py:67
  27.6 35.0 %collective-permute-start.2 = (bf16[160,2048]{1,0:T(8,128)(2,1)}, bf16[160,2048]{1,0:T(8,128)(2,1)}, u32[]{:S(2)}, u32[]{:S(2)}) collective-permute-start(bf16[160,2048]{1,0:T(8,128)(2,1)} %collective-permute-done), channel_id=1, source_target_pairs={{0,1},{2,0},{4,2},{6,4},{7,6},{5,7},{3,5},{1,3},{8,9},{10,8},{12,1... | collective-permute-start | bytes 1966088 | tf_op jit(solution)/shard_map/ppermute | solution.py:86
  30.5 34.4 %collective-permute-start.3 = (bf16[160,2048]{1,0:T(8,128)(2,1)S(1)}, bf16[160,2048]{1,0:T(8,128)(2,1)}, u32[]{:S(2)}, u32[]{:S(2)}) collective-permute-start(bf16[160,2048]{1,0:T(8,128)(2,1)S(1)} %collective-permute-done.1), channel_id=1, source_target_pairs={{0,2},{2,4},{4,6},{6,7},{7,5},{5,3},{3,1},{1,0},{8,10},{10,12},{12... | collective-permute-start | bytes 1966088 | tf_op jit(solution)/shard_map/ppermute | solution.py:86
  53.1 105.4 %all-to-all-start.2 = ((bf16[8,52,128]{2,1,0:T(8,128)(2,1)}), bf16[8,52,128]{2,1,0:T(8,128)(2,1)S(1)}, u32[]{:S(2)}, u32[]{:S(2)}) async-start(bf16[8,52,128]{2,1,0:T(8,128)(2,1)} %broadcast_in_dim.186), calls=%async_computation.2 | async-start | bytes 229376 | tf_op jit(solution)/shard_map/all_to_all | solution.py:205
  58.2 216.1 %all-gather.6.cloned.1.call-start = ((), (), s32[]{:S(2)}) async-start(), calls=%async_computation.12 | async-start | bytes 5898240 | tf_op jit(solution)/shard_map/all_gather | solution.py:67
  58.2 41.4 %collective-permute-start.8 = (bf16[1,8,64,768]{3,2,1,0:T(8,128)(2,1)S(1)}, bf16[1,8,64,768]{3,2,1,0:T(8,128)(2,1)S(1)}, u32[]{:S(2)}, u32[]{:S(2)}) collective-permute-start(bf16[1,8,64,768]{3,2,1,0:T(8,128)(2,1)S(1)} %bitcast.174), channel_id=1, source_target_pairs={{0,16},{8,24},{16,0},{24,8},{1,17},{9,25},{17,1},{25,9},{2,18},{10... | collective-permute-start | bytes 2359304 | tf_op jit(solution)/shard_map/ppermute | solution.py:152
  62.6 36.9 %collective-permute-start.4 = (bf16[160,2048]{1,0:T(8,128)(2,1)}, bf16[160,2048]{1,0:T(8,128)(2,1)S(1)}, u32[]{:S(2)}, u32[]{:S(2)}) collective-permute-start(bf16[160,2048]{1,0:T(8,128)(2,1)} %collective-permute-done.2), channel_id=1, source_target_pairs={{0,1},{2,0},{4,2},{6,4},{7,6},{5,7},{3,5},{1,3},{8,9},{10,8},{12,1... | collective-permute-start | bytes 1966088 | tf_op jit(solution)/shard_map/ppermute | solution.py:86
  64.9 29.1 %collective-permute-start.5 = (bf16[160,2048]{1,0:T(8,128)(2,1)}, bf16[160,2048]{1,0:T(8,128)(2,1)S(1)}, u32[]{:S(2)}, u32[]{:S(2)}) collective-permute-start(bf16[160,2048]{1,0:T(8,128)(2,1)} %collective-permute-done.3), channel_id=1, source_target_pairs={{0,2},{2,4},{4,6},{6,7},{7,5},{5,3},{3,1},{1,0},{8,10},{10,12},{12... | collective-permute-start | bytes 1966088 | tf_op jit(solution)/shard_map/ppermute | solution.py:86
  94.0 10.2 %collective-permute-start.6 = (bf16[80,2048]{1,0:T(8,128)(2,1)S(1)}, bf16[80,2048]{1,0:T(8,128)(2,1)S(1)}, u32[]{:S(2)}, u32[]{:S(2)}) collective-permute-start(bf16[80,2048]{1,0:T(8,128)(2,1)S(1)} %slice.396), channel_id=1, source_target_pairs={{0,2},{2,4},{4,6},{6,7},{7,5},{5,3},{3,1},{1,0},{8,10},{10,12},{12... | collective-permute-start | bytes 983048 | tf_op jit(solution)/shard_map/ppermute | solution.py:86
  99.5 7.5 collective-permute-start.7
  101.0 12.1 %collective-permute-start.9 = (bf16[2,8,64,768]{3,2,1,0:T(8,128)(2,1)}, bf16[2,8,64,768]{3,2,1,0:T(8,128)(2,1)}, u32[]{:S(2)}, u32[]{:S(2)}) collective-permute-start(bf16[2,8,64,768]{3,2,1,0:T(8,128)(2,1)} %maximum_select_fusion.3), channel_id=1, source_target_pairs={{0,8},{8,0},{16,24},{24,16},{1,9},{9,1},{17,25},{25,17},{2,10},{10... | collective-permute-start | bytes 4718600 | tf_op jit(solution)/shard_map/ppermute | solution.py:152
  111.5 46.3 %collective-permute-start.10 = (bf16[2048,512]{1,0:T(8,128)(2,1)}, bf16[2048,512]{1,0:T(8,128)(2,1)}, u32[]{:S(2)}, u32[]{:S(2)}) collective-permute-start(bf16[2048,512]{1,0:T(8,128)(2,1)} %all-gather.4.cloned.1.call-done), channel_id=1, source_target_pairs={{0,16},{8,24},{16,0},{24,8},{1,17},{9,25},{17,1},{25,9},{2,18},{10... | collective-permute-start | bytes 6291464 | tf_op jit(solution)/shard_map/ppermute | solution.py:152
  113.1 91.1 %collective-permute-start.11 = (bf16[2048,512]{1,0:T(8,128)(2,1)}, bf16[2048,512]{1,0:T(8,128)(2,1)}, u32[]{:S(2)}, u32[]{:S(2)}) collective-permute-start(bf16[2048,512]{1,0:T(8,128)(2,1)} %all-gather.4.cloned.1.call-done), channel_id=1, source_target_pairs={{0,8},{8,0},{16,24},{24,16},{1,9},{9,1},{17,25},{25,17},{2,10},{10... | collective-permute-start | bytes 6291464 | tf_op jit(solution)/shard_map/ppermute | solution.py:152
  157.9 48.5 %collective-permute-start.12 = (bf16[2048,512]{1,0:T(8,128)(2,1)}, bf16[2048,512]{1,0:T(8,128)(2,1)}, u32[]{:S(2)}, u32[]{:S(2)}) collective-permute-start(bf16[2048,512]{1,0:T(8,128)(2,1)} %collective-permute-done.10), channel_id=1, source_target_pairs={{0,8},{8,0},{16,24},{24,16},{1,9},{9,1},{17,25},{25,17},{2,10},{10... | collective-permute-start | bytes 6291464 | tf_op jit(solution)/shard_map/ppermute | solution.py:152
  158.5 41.8 %all-to-all-start.1 = ((bf16[8,160,256]{2,1,0:T(8,128)(2,1)}), bf16[8,160,256]{2,1,0:T(8,128)(2,1)}, u32[]{:S(2)}, u32[]{:S(2)}) async-start(bf16[8,160,256]{2,1,0:T(8,128)(2,1)} %constant_dynamic-update-slice_fusion.9), calls=%async_computation.1 | async-start | bytes 1310720 | tf_op jit(solution)/shard_map/all_to_all | solution.py:205
  210.4 16.7 %collective-permute-start.13 = (bf16[160,2048]{1,0:T(8,128)(2,1)S(1)}, bf16[160,2048]{1,0:T(8,128)(2,1)}, u32[]{:S(2)}, u32[]{:S(2)}) collective-permute-start(bf16[160,2048]{1,0:T(8,128)(2,1)S(1)} %get-tuple-element.127), channel_id=1, source_target_pairs={{0,1},{2,0},{4,2},{6,4},{7,6},{5,7},{3,5},{1,3},{8,9},{10,8},{12,1... | collective-permute-start | bytes 1966088 | tf_op jit(solution)/shard_map/ppermute | solution.py:86
  211.8 16.7 %collective-permute-start.14 = (bf16[160,2048]{1,0:T(8,128)(2,1)S(1)}, bf16[160,2048]{1,0:T(8,128)(2,1)S(1)}, u32[]{:S(2)}, u32[]{:S(2)}) collective-permute-start(bf16[160,2048]{1,0:T(8,128)(2,1)S(1)} %get-tuple-element.127), channel_id=1, source_target_pairs={{0,2},{2,4},{4,6},{6,7},{7,5},{5,3},{3,1},{1,0},{8,10},{10,12},{12... | collective-permute-start | bytes 1966088 | tf_op jit(solution)/shard_map/ppermute | solution.py:86
  227.1 16.0 %collective-permute-start.15 = (bf16[160,2048]{1,0:T(8,128)(2,1)}, bf16[160,2048]{1,0:T(8,128)(2,1)}, u32[]{:S(2)}, u32[]{:S(2)}) collective-permute-start(bf16[160,2048]{1,0:T(8,128)(2,1)} %collective-permute-done.13), channel_id=1, source_target_pairs={{0,1},{2,0},{4,2},{6,4},{7,6},{5,7},{3,5},{1,3},{8,9},{10,8},{12,1... | collective-permute-start | bytes 1966088 | tf_op jit(solution)/shard_map/ppermute | solution.py:86
  228.5 16.0 %collective-permute-start.16 = (bf16[160,2048]{1,0:T(8,128)(2,1)S(1)}, bf16[160,2048]{1,0:T(8,128)(2,1)}, u32[]{:S(2)}, u32[]{:S(2)}) collective-permute-start(bf16[160,2048]{1,0:T(8,128)(2,1)S(1)} %collective-permute-done.14), channel_id=1, source_target_pairs={{0,2},{2,4},{4,6},{6,7},{7,5},{5,3},{3,1},{1,0},{8,10},{10,12},{12... | collective-permute-start | bytes 1966088 | tf_op jit(solution)/shard_map/ppermute | solution.py:86
  243.1 17.1 %collective-permute-start.17 = (bf16[160,2048]{1,0:T(8,128)(2,1)}, bf16[160,2048]{1,0:T(8,128)(2,1)S(1)}, u32[]{:S(2)}, u32[]{:S(2)}) collective-permute-start(bf16[160,2048]{1,0:T(8,128)(2,1)} %collective-permute-done.15), channel_id=1, source_target_pairs={{0,1},{2,0},{4,2},{6,4},{7,6},{5,7},{3,5},{1,3},{8,9},{10,8},{12,1... | collective-permute-start | bytes 1966088 | tf_op jit(solution)/shard_map/ppermute | solution.py:86
  244.5 15.0 %collective-permute-start.18 = (bf16[160,2048]{1,0:T(8,128)(2,1)}, bf16[160,2048]{1,0:T(8,128)(2,1)S(1)}, u32[]{:S(2)}, u32[]{:S(2)}) collective-permute-start(bf16[160,2048]{1,0:T(8,128)(2,1)} %collective-permute-done.16), channel_id=1, source_target_pairs={{0,2},{2,4},{4,6},{6,7},{7,5},{5,3},{3,1},{1,0},{8,10},{10,12},{12... | collective-permute-start | bytes 1966088 | tf_op jit(solution)/shard_map/ppermute | solution.py:86
  259.5 7.1 collective-permute-start.19
  260.2 7.2 collective-permute-start.20
  364.2 8.4 %collective-permute-start.25 = (bf16[80,2048]{1,0:T(8,128)(2,1)S(1)}, bf16[80,2048]{1,0:T(8,128)(2,1)S(1)}, u32[]{:S(2)}, u32[]{:S(2)}) collective-permute-start(bf16[80,2048]{1,0:T(8,128)(2,1)S(1)} %get-tuple-element.159), channel_id=1, source_target_pairs={{0,1},{2,0},{4,2},{6,4},{7,6},{5,7},{3,5},{1,3},{8,9},{10,8},{12,1... | collective-permute-start | bytes 983048 | tf_op jit(solution)/shard_map/ppermute | solution.py:86
  374.1 11.7 %collective-permute-start.26 = (bf16[160,2048]{1,0:T(8,128)(2,1)S(1)}, bf16[160,2048]{1,0:T(8,128)(2,1)S(1)}, u32[]{:S(2)}, u32[]{:S(2)}) collective-permute-start(bf16[160,2048]{1,0:T(8,128)(2,1)S(1)} %pad_maximum_fusion.4), channel_id=1, source_target_pairs={{0,1},{2,0},{4,2},{6,4},{7,6},{5,7},{3,5},{1,3},{8,9},{10,8},{12,1... | collective-permute-start | bytes 1966088 | tf_op jit(solution)/shard_map/ppermute | solution.py:86
  375.6 12.4 %collective-permute-start.22 = (bf16[160,2048]{1,0:T(8,128)(2,1)S(1)}, bf16[160,2048]{1,0:T(8,128)(2,1)S(1)}, u32[]{:S(2)}, u32[]{:S(2)}) collective-permute-start(bf16[160,2048]{1,0:T(8,128)(2,1)S(1)} %pad_maximum_fusion.3), channel_id=1, source_target_pairs={{0,2},{2,4},{4,6},{6,7},{7,5},{5,3},{3,1},{1,0},{8,10},{10,12},{12... | collective-permute-start | bytes 1966088 | tf_op jit(solution)/shard_map/ppermute | solution.py:86
  390.8 13.5 %collective-permute-start.23 = (bf16[160,2048]{1,0:T(8,128)(2,1)}, bf16[160,2048]{1,0:T(8,128)(2,1)S(1)}, u32[]{:S(2)}, u32[]{:S(2)}) collective-permute-start(bf16[160,2048]{1,0:T(8,128)(2,1)} %get-tuple-element.154), channel_id=1, source_target_pairs={{0,2},{2,4},{4,6},{6,7},{7,5},{5,3},{3,1},{1,0},{8,10},{10,12},{12... | collective-permute-start | bytes 1966088 | tf_op jit(solution)/shard_map/ppermute | solution.py:86
  391.7 14.3 %collective-permute-start.27 = (bf16[160,2048]{1,0:T(8,128)(2,1)}, bf16[160,2048]{1,0:T(8,128)(2,1)}, u32[]{:S(2)}, u32[]{:S(2)}) collective-permute-start(bf16[160,2048]{1,0:T(8,128)(2,1)} %get-tuple-element.155), channel_id=1, source_target_pairs={{0,1},{2,0},{4,2},{6,4},{7,6},{5,7},{3,5},{1,3},{8,9},{10,8},{12,1... | collective-permute-start | bytes 1966088 | tf_op jit(solution)/shard_map/ppermute | solution.py:86
  409.1 15.2 %collective-permute-start.24 = (bf16[160,2048]{1,0:T(8,128)(2,1)}, bf16[160,2048]{1,0:T(8,128)(2,1)S(1)}, u32[]{:S(2)}, u32[]{:S(2)}) collective-permute-start(bf16[160,2048]{1,0:T(8,128)(2,1)} %get-tuple-element.152), channel_id=1, source_target_pairs={{0,2},{2,4},{4,6},{6,7},{7,5},{5,3},{3,1},{1,0},{8,10},{10,12},{12... | collective-permute-start | bytes 1966088 | tf_op jit(solution)/shard_map/ppermute | solution.py:86
  409.1 15.2 %collective-permute-start.28 = (bf16[160,2048]{1,0:T(8,128)(2,1)}, bf16[160,2048]{1,0:T(8,128)(2,1)}, u32[]{:S(2)}, u32[]{:S(2)}) collective-permute-start(bf16[160,2048]{1,0:T(8,128)(2,1)} %get-tuple-element.153), channel_id=1, source_target_pairs={{0,1},{2,0},{4,2},{6,4},{7,6},{5,7},{3,5},{1,3},{8,9},{10,8},{12,1... | collective-permute-start | bytes 1966088 | tf_op jit(solution)/shard_map/ppermute | solution.py:86
  412.9 10.6 %all-to-all-start.3 = ((f32[8,160,2]{1,2,0:T(2,128)}), f32[8,160,2]{1,2,0:T(2,128)S(1)}, u32[]{:S(2)}, u32[]{:S(2)}) async-start(f32[8,160,2]{1,2,0:T(2,128)} %copy.134), calls=%async_computation.3 | async-start | bytes 32768 | tf_op jit(solution)/shard_map/all_to_all | solution.py:205
  417.0 302.3 %all-gather.8.cloned.1.call-start = ((), (), s32[]{:S(2)}) async-start(), calls=%async_computation.13 | async-start | bytes 5898240 | tf_op jit(solution)/shard_map/all_gather | solution.py:67
  429.3 329.5 %reduce-scatter.4.cloned.1.call-start = ((), (), s32[]{:S(2)}) async-start(), calls=%async_computation.14 | async-start | bytes 10485760 | tf_op jit(solution)/shard_map/reduce_scatter | solution.py:608
  446.2 317.2 %reduce-scatter.8.cloned.1.call-start = ((), (), s32[]{:S(2)}) async-start(), calls=%async_computation.16 | async-start | bytes 10485760 | tf_op jit(solution)/shard_map/reduce_scatter | solution.py:601
  477.5 37.3 %all-to-all-start.4 = ((bf16[8,160,256]{2,1,0:T(8,128)(2,1)}), bf16[8,160,256]{2,1,0:T(8,128)(2,1)S(1)}, u32[]{:S(2)}, u32[]{:S(2)}) async-start(bf16[8,160,256]{2,1,0:T(8,128)(2,1)} %bitcast.160), calls=%async_computation.4 | async-start | bytes 1310720 | tf_op jit(solution)/shard_map/all_to_all | solution.py:205
  481.1 286.4 %reduce-scatter.6.cloned.1.call-start = ((), (), s32[]{:S(2)}) async-start(), calls=%async_computation.15 | async-start | bytes 10485760 | tf_op jit(solution)/shard_map/reduce_scatter | solution.py:608
  515.7 107.5 %all-to-all-start.6 = ((f32[8,1,4352]{2,1,0:T(1,128)}), f32[8,1,4352]{2,1,0:T(1,128)S(1)}, u32[]{:S(2)}, u32[]{:S(2)}) async-start(f32[8,1,4352]{2,1,0:T(1,128)} %copy.142), calls=%async_computation.6 | async-start | bytes 278528 | tf_op jit(solution)/shard_map/all_to_all | solution.py:205
  573.2 32.4 %collective-permute-start.45 = (bf16[8,2,64,768]{3,2,0,1:T(8,128)(2,1)S(1)}, bf16[8,2,64,768]{3,2,0,1:T(8,128)(2,1)}, u32[]{:S(2)}, u32[]{:S(2)}) collective-permute-start(bf16[8,2,64,768]{3,2,0,1:T(8,128)(2,1)S(1)} %bitcast.218), channel_id=1, source_target_pairs={{0,8},{8,0},{16,24},{24,16},{1,9},{9,1},{17,25},{25,17},{2,10},{10... | collective-permute-start | bytes 4718600 | tf_op jit(solution)/shard_map/ppermute | solution.py:152
  584.5 11.0 %collective-permute-start.37 = (bf16[80,2048]{1,0:T(8,128)(2,1)}, bf16[80,2048]{1,0:T(8,128)(2,1)}, u32[]{:S(2)}, u32[]{:S(2)}) collective-permute-start(bf16[80,2048]{1,0:T(8,128)(2,1)} %get-tuple-element.138), channel_id=1, source_target_pairs={{0,2},{2,4},{4,6},{6,7},{7,5},{5,3},{3,1},{1,0},{8,10},{10,12},{12... | collective-permute-start | bytes 983048 | tf_op jit(solution)/shard_map/ppermute | solution.py:86
  586.4 11.0 %collective-permute-start.41 = (bf16[80,2048]{1,0:T(8,128)(2,1)}, bf16[80,2048]{1,0:T(8,128)(2,1)}, u32[]{:S(2)}, u32[]{:S(2)}) collective-permute-start(bf16[80,2048]{1,0:T(8,128)(2,1)} %get-tuple-element.139), channel_id=1, source_target_pairs={{0,1},{2,0},{4,2},{6,4},{7,6},{5,7},{3,5},{1,3},{8,9},{10,8},{12,1... | collective-permute-start | bytes 983048 | tf_op jit(solution)/shard_map/ppermute | solution.py:86
  589.5 12.8 %collective-permute-start.29 = (bf16[80,2048]{1,0:T(8,128)(2,1)}, bf16[80,2048]{1,0:T(8,128)(2,1)S(1)}, u32[]{:S(2)}, u32[]{:S(2)}) collective-permute-start(bf16[80,2048]{1,0:T(8,128)(2,1)} %get-tuple-element.148), channel_id=1, source_target_pairs={{0,2},{2,4},{4,6},{6,7},{7,5},{5,3},{3,1},{1,0},{8,10},{10,12},{12... | collective-permute-start | bytes 983048 | tf_op jit(solution)/shard_map/ppermute | solution.py:86
  591.5 12.8 %collective-permute-start.33 = (bf16[80,2048]{1,0:T(8,128)(2,1)S(1)}, bf16[80,2048]{1,0:T(8,128)(2,1)S(1)}, u32[]{:S(2)}, u32[]{:S(2)}) collective-permute-start(bf16[80,2048]{1,0:T(8,128)(2,1)S(1)} %get-tuple-element.149), channel_id=1, source_target_pairs={{0,1},{2,0},{4,2},{6,4},{7,6},{5,7},{3,5},{1,3},{8,9},{10,8},{12,1... | collective-permute-start | bytes 983048 | tf_op jit(solution)/shard_map/ppermute | solution.py:86
  598.9 19.4 %collective-permute-start.42 = (bf16[160,2048]{1,0:T(8,128)(2,1)S(1)}, bf16[160,2048]{1,0:T(8,128)(2,1)S(1)}, u32[]{:S(2)}, u32[]{:S(2)}) collective-permute-start(bf16[160,2048]{1,0:T(8,128)(2,1)S(1)} %pad_maximum_fusion.8), channel_id=1, source_target_pairs={{0,1},{2,0},{4,2},{6,4},{7,6},{5,7},{3,5},{1,3},{8,9},{10,8},{12,1... | collective-permute-start | bytes 1966088 | tf_op jit(solution)/shard_map/ppermute | solution.py:86
  599.1 19.3 %collective-permute-start.38 = (bf16[160,2048]{1,0:T(8,128)(2,1)S(1)}, bf16[160,2048]{1,0:T(8,128)(2,1)S(1)}, u32[]{:S(2)}, u32[]{:S(2)}) collective-permute-start(bf16[160,2048]{1,0:T(8,128)(2,1)S(1)} %pad_maximum_fusion.7), channel_id=1, source_target_pairs={{0,2},{2,4},{4,6},{6,7},{7,5},{5,3},{3,1},{1,0},{8,10},{10,12},{12... | collective-permute-start | bytes 1966088 | tf_op jit(solution)/shard_map/ppermute | solution.py:86
  608.4 19.4 %collective-permute-start.46 = (bf16[8,1,64,768]{3,2,0,1:T(8,128)(2,1)}, bf16[8,1,64,768]{3,2,0,1:T(8,128)(2,1)S(1)}, u32[]{:S(2)}, u32[]{:S(2)}) collective-permute-start(bf16[8,1,64,768]{3,2,0,1:T(8,128)(2,1)} %constant_dynamic-slice_fusion.1), channel_id=1, source_target_pairs={{0,16},{8,24},{16,0},{24,8},{1,17},{9,25},{17,1},{25,9},{2,18},{10... | collective-permute-start | bytes 2359304 | tf_op jit(solution)/shard_map/ppermute | solution.py:152
  610.7 49.6 %collective-permute-start.34 = (bf16[160,2048]{1,0:T(8,128)(2,1)}, bf16[160,2048]{1,0:T(8,128)(2,1)}, u32[]{:S(2)}, u32[]{:S(2)}) collective-permute-start(bf16[160,2048]{1,0:T(8,128)(2,1)} %pad_maximum_fusion.6), channel_id=1, source_target_pairs={{0,1},{2,0},{4,2},{6,4},{7,6},{5,7},{3,5},{1,3},{8,9},{10,8},{12,1... | collective-permute-start | bytes 1966088 | tf_op jit(solution)/shard_map/ppermute | solution.py:86
  611.9 48.4 %collective-permute-start.30 = (bf16[160,2048]{1,0:T(8,128)(2,1)}, bf16[160,2048]{1,0:T(8,128)(2,1)}, u32[]{:S(2)}, u32[]{:S(2)}) collective-permute-start(bf16[160,2048]{1,0:T(8,128)(2,1)} %pad_maximum_fusion.5), channel_id=1, source_target_pairs={{0,2},{2,4},{4,6},{6,7},{7,5},{5,3},{3,1},{1,0},{8,10},{10,12},{12... | collective-permute-start | bytes 1966088 | tf_op jit(solution)/shard_map/ppermute | solution.py:86
  621.2 44.4 %collective-permute-start.39 = (bf16[160,2048]{1,0:T(8,128)(2,1)}, bf16[160,2048]{1,0:T(8,128)(2,1)S(1)}, u32[]{:S(2)}, u32[]{:S(2)}) collective-permute-start(bf16[160,2048]{1,0:T(8,128)(2,1)} %get-tuple-element.134), channel_id=1, source_target_pairs={{0,2},{2,4},{4,6},{6,7},{7,5},{5,3},{3,1},{1,0},{8,10},{10,12},{12... | collective-permute-start | bytes 1966088 | tf_op jit(solution)/shard_map/ppermute | solution.py:86
  622.7 42.9 %collective-permute-start.43 = (bf16[160,2048]{1,0:T(8,128)(2,1)}, bf16[160,2048]{1,0:T(8,128)(2,1)}, u32[]{:S(2)}, u32[]{:S(2)}) collective-permute-start(bf16[160,2048]{1,0:T(8,128)(2,1)} %get-tuple-element.135), channel_id=1, source_target_pairs={{0,1},{2,0},{4,2},{6,4},{7,6},{5,7},{3,5},{1,3},{8,9},{10,8},{12,1... | collective-permute-start | bytes 1966088 | tf_op jit(solution)/shard_map/ppermute | solution.py:86
  623.2 22.7 %all-to-all-start.7 = ((f32[8,1,288]{2,1,0:T(1,128)}), f32[8,1,288]{2,1,0:T(1,128)S(1)}, u32[]{:S(2)}, u32[]{:S(2)}) async-start(f32[8,1,288]{2,1,0:T(1,128)} %all_to_all.38), calls=%async_computation.7 | async-start | bytes 24576 | tf_op jit(solution)/shard_map/all_to_all | solution.py:205
  645.9 25.4 %all-to-all-start.5 = ((bf16[8,64,768]{2,1,0:T(8,128)(2,1)}), bf16[8,64,768]{2,1,0:T(8,128)(2,1)S(1)}, u32[]{:S(2)}, u32[]{:S(2)}) async-start(bf16[8,64,768]{2,1,0:T(8,128)(2,1)} %fusion.27), calls=%async_computation.5 | async-start | bytes 1572864 | tf_op jit(solution)/shard_map/all_to_all | solution.py:205
  663.6 18.0 %collective-permute-start.31 = (bf16[160,2048]{1,0:T(8,128)(2,1)}, bf16[160,2048]{1,0:T(8,128)(2,1)}, u32[]{:S(2)}, u32[]{:S(2)}) collective-permute-start(bf16[160,2048]{1,0:T(8,128)(2,1)} %get-tuple-element.144), channel_id=1, source_target_pairs={{0,2},{2,4},{4,6},{6,7},{7,5},{5,3},{3,1},{1,0},{8,10},{10,12},{12... | collective-permute-start | bytes 1966088 | tf_op jit(solution)/shard_map/ppermute | solution.py:86
  665.5 18.0 %collective-permute-start.35 = (bf16[160,2048]{1,0:T(8,128)(2,1)}, bf16[160,2048]{1,0:T(8,128)(2,1)}, u32[]{:S(2)}, u32[]{:S(2)}) collective-permute-start(bf16[160,2048]{1,0:T(8,128)(2,1)} %get-tuple-element.145), channel_id=1, source_target_pairs={{0,1},{2,0},{4,2},{6,4},{7,6},{5,7},{3,5},{1,3},{8,9},{10,8},{12,1... | collective-permute-start | bytes 1966088 | tf_op jit(solution)/shard_map/ppermute | solution.py:86
  668.7 26.9 %collective-permute-start.40 = (bf16[160,2048]{1,0:T(8,128)(2,1)}, bf16[160,2048]{1,0:T(8,128)(2,1)}, u32[]{:S(2)}, u32[]{:S(2)}) collective-permute-start(bf16[160,2048]{1,0:T(8,128)(2,1)} %get-tuple-element.132), channel_id=1, source_target_pairs={{0,2},{2,4},{4,6},{6,7},{7,5},{5,3},{3,1},{1,0},{8,10},{10,12},{12... | collective-permute-start | bytes 1966088 | tf_op jit(solution)/shard_map/ppermute | solution.py:86
  670.6 26.9 %collective-permute-start.44 = (bf16[160,2048]{1,0:T(8,128)(2,1)}, bf16[160,2048]{1,0:T(8,128)(2,1)}, u32[]{:S(2)}, u32[]{:S(2)}) collective-permute-start(bf16[160,2048]{1,0:T(8,128)(2,1)} %get-tuple-element.133), channel_id=1, source_target_pairs={{0,1},{2,0},{4,2},{6,4},{7,6},{5,7},{3,5},{1,3},{8,9},{10,8},{12,1... | collective-permute-start | bytes 1966088 | tf_op jit(solution)/shard_map/ppermute | solution.py:86
  672.9 26.7 %collective-permute-start.47 = (bf16[1,3,64,2048]{3,2,1,0:T(8,128)(2,1)S(1)}, bf16[1,3,64,2048]{3,2,1,0:T(8,128)(2,1)S(1)}, u32[]{:S(2)}, u32[]{:S(2)}) collective-permute-start(bf16[1,3,64,2048]{3,2,1,0:T(8,128)(2,1)S(1)} %broadcast_in_dim_reshape.2), channel_id=1, source_target_pairs={{0,16},{8,24},{16,0},{24,8},{1,17},{9,25},{17,1},{25,9},{2,18},{10... | collective-permute-start | bytes 2359304 | tf_op jit(solution)/shard_map/ppermute | solution.py:152
  686.1 21.2 %collective-permute-start.32 = (bf16[160,2048]{1,0:T(8,128)(2,1)S(1)}, bf16[160,2048]{1,0:T(8,128)(2,1)S(1)}, u32[]{:S(2)}, u32[]{:S(2)}) collective-permute-start(bf16[160,2048]{1,0:T(8,128)(2,1)S(1)} %get-tuple-element.142), channel_id=1, source_target_pairs={{0,2},{2,4},{4,6},{6,7},{7,5},{5,3},{3,1},{1,0},{8,10},{10,12},{12... | collective-permute-start | bytes 1966088 | tf_op jit(solution)/shard_map/ppermute | solution.py:86
  687.5 21.9 %collective-permute-start.36 = (bf16[160,2048]{1,0:T(8,128)(2,1)S(1)}, bf16[160,2048]{1,0:T(8,128)(2,1)S(1)}, u32[]{:S(2)}, u32[]{:S(2)}) collective-permute-start(bf16[160,2048]{1,0:T(8,128)(2,1)S(1)} %get-tuple-element.143), channel_id=1, source_target_pairs={{0,1},{2,0},{4,2},{6,4},{7,6},{5,7},{3,5},{1,3},{8,9},{10,8},{12,1... | collective-permute-start | bytes 1966088 | tf_op jit(solution)/shard_map/ppermute | solution.py:86
  701.0 14.5 %collective-permute-start.48 = (bf16[2,3,64,2048]{3,2,1,0:T(8,128)(2,1)}, bf16[2,3,64,2048]{3,2,1,0:T(8,128)(2,1)}, u32[]{:S(2)}, u32[]{:S(2)}) collective-permute-start(bf16[2,3,64,2048]{3,2,1,0:T(8,128)(2,1)} %maximum_select_fusion.5), channel_id=1, source_target_pairs={{0,8},{8,0},{16,24},{24,16},{1,9},{9,1},{17,25},{25,17},{2,10},{10... | collective-permute-start | bytes 4718600 | tf_op jit(solution)/shard_map/ppermute | solution.py:152
  726.1 14.5 %collective-permute-start.50 = (bf16[1,64,2048]{2,1,0:T(8,128)(2,1)S(1)}, bf16[1,64,2048]{2,1,0:T(8,128)(2,1)S(1)}, u32[]{:S(2)}, u32[]{:S(2)}) collective-permute-start(bf16[1,64,2048]{2,1,0:T(8,128)(2,1)S(1)} %constant_dynamic-slice_fusion), channel_id=1, source_target_pairs={{0,16},{8,24},{16,0},{24,8},{1,17},{9,25},{17,1},{25,9},{2,18},{10... | collective-permute-start | bytes 786440 | tf_op jit(solution)/shard_map/ppermute | solution.py:152
  740.7 14.3 %collective-permute-start.51 = (bf16[1,64,2048]{2,1,0:T(8,128)(2,1)S(1)}, bf16[1,64,2048]{2,1,0:T(8,128)(2,1)S(1)}, u32[]{:S(2)}, u32[]{:S(2)}) collective-permute-start(bf16[1,64,2048]{2,1,0:T(8,128)(2,1)S(1)} %add_convert_fusion.19), channel_id=1, source_target_pairs={{0,16},{8,24},{16,0},{24,8},{1,17},{9,25},{17,1},{25,9},{2,18},{10... | collective-permute-start | bytes 786440 | tf_op jit(solution)/shard_map/ppermute | solution.py:152
  (137 other events, 1699.0 us)
Sparse Core Ops, SparseCore 0:
  22.5 62.8 all-gather.3
  107.9 98.7 all-gather.5
  429.5 96.8 all-gather.7
  528.8 70.7 reduce-scatter.3
  602.2 72.1 reduce-scatter.7
  676.9 82.9 reduce-scatter.5

commit v4 on v3

--- a/solution.py
+++ b/solution.py
@@ -1,3 +1,5 @@
+import functools
+
 import jax
 import jax.numpy as jnp
 from jax import lax
@@ -86,41 +88,67 @@
     return lax.ppermute(values, "ep", pairs)
 
 
-def ring_gather(values):
+def tie(*arrays):
+    return lax.optimization_barrier(arrays)
+
+
+def fill_window(fill, sent, received):
+    if fill is None:
+        return received, None
+    work, inputs = fill
+    inputs, _ = lax.optimization_barrier((inputs, sent))
+    return lax.optimization_barrier((received, work(*inputs)))
+
+
+def ring_gather(values, fills=()):
     half = lax.axis_size("ep") // 2
     middle = values.shape[0] // 2
+    fills = dict(fills)
     onward, backward = values, values
-    blocks = [values]
-    for _ in range(1, half):
-        onward, backward = ring_shift(onward, 1), ring_shift(backward, -1)
-        blocks += [backward, onward]
-    far = [ring_shift(onward[:middle], 1), ring_shift(backward[middle:], -1)]
-    return blocks + [jnp.concatenate(far, axis=0)]
-
-
-def ring_scatter(partial):
+    blocks, results = [values], {}
+    for step in range(1, half + 1):
+        if step == half:
+            sent = (onward[:middle], backward[middle:])
+        else:
+            sent = (onward, backward)
+        received = (ring_shift(sent[0], 1), ring_shift(sent[1], -1))
+        fill = fills[step](blocks, results) if step in fills else None
+        (onward, backward), results[step] = fill_window(fill, sent, received)
+        if step < half:
+            blocks = blocks + [backward, onward]
+    return blocks + [jnp.concatenate([onward, backward], axis=0)], results
+
+
+def ring_scatter(block, rows, fills=()):
     count = lax.axis_size("ep")
     half = count // 2
-    rows = partial.shape[0] // count
     middle = rows // 2
+    fills = dict(fills)
     slot = {offset: j for j, offset in enumerate(ring_slots(count))}
-
-    def block(offset):
-        return partial[slot[offset] * rows : (slot[offset] + 1) * rows]
-
-    onward = ring_shift(block(half)[:middle], 1)
-    backward = ring_shift(block(half)[middle:], -1)
-    up, down = block(half - 1), block(1 - half)
-    onward = jnp.concatenate([add_low(onward, up[:middle]), up[middle:]], axis=0)
-    backward = jnp.concatenate([down[:middle], add_low(backward, down[middle:])], axis=0)
-    for step in range(half - 2, -1, -1):
-        onward, backward = ring_shift(onward, 1), ring_shift(backward, -1)
-        if step:
-            onward = add_low(onward, block(step))
-            backward = add_low(backward, block(-step))
-    return (
-        block(0).astype(wide_type) + onward.astype(wide_type) + backward.astype(wide_type)
-    )
+    results = {}
+    far = block(slot[half], results)
+    onward, backward = far[:middle], far[middle:]
+    for step in range(1, half + 1):
+        sent = (onward, backward)
+        received = (ring_shift(onward, 1), ring_shift(backward, -1))
+        fill = fills[step](results) if step in fills else None
+        (onward, backward), results[step] = fill_window(fill, sent, received)
+        left = half - step
+        if left:
+            up, down = block(slot[left], results), block(slot[-left], results)
+            if step == 1:
+                onward = jnp.concatenate([add_low(onward, up[:middle]), up[middle:]], axis=0)
+                backward = jnp.concatenate(
+                    [down[:middle], add_low(backward, down[middle:])], axis=0
+                )
+            else:
+                onward, backward = add_low(onward, up), add_low(backward, down)
+    total = (
+        block(slot[0], results).astype(wide_type)
+        + onward.astype(wide_type)
+        + backward.astype(wide_type)
+    )
+    return total, results
 
 
 def add_low(left, right):
@@ -183,16 +211,6 @@
     return lax.index_in_dim(values, 0, axis, keepdims=False)
 
 
-def rep_pieces(values):
-    pieces = {0: values}
-    distance = lax.axis_size("rep") // 2
-    while distance:
-        for j in list(pieces):
-            pieces[j ^ distance] = rep_exchange(pieces[j], distance)
-        distance //= 2
-    return pieces
-
-
 def rep_sum(values):
     distance = 1
     while distance < lax.axis_size("rep"):
@@ -205,9 +223,8 @@
     return lax.all_to_all(values, "ep", split_axis=0, concat_axis=0, tiled=True)
 
 
-def expert_kernel(
-    rows_ref, gate_ref, up_ref, stream_ref, gates_ref, inner_ref, gback_ref, uback_ref, pair_ref
-):
+def expert_kernel(rows_ref, gate_ref, up_ref, stream_ref, gates_ref, *refs):
+    inner_ref, gback_ref, uback_ref, pair_ref = refs[-4:]
     expert, step = pl.program_id(0), pl.program_id(1)
     rows = rows_ref[...]
     gate_linear = jnp.dot(rows, gate_ref[0], preferred_element_type=wide_type)
@@ -240,13 +257,13 @@
         pair_ref[0] += folded
 
 
-def expert_pass(rows, gate_weight, up_weight, stream, gates):
+def expert_pass(rows, gate_weight, up_weight, stream, gates, chunk, chunks, earlier=()):
     count, depth = rows.shape
     experts, _, hidden = gate_weight.shape
     width = 256
     steps = hidden // width
-    wide = pl.BlockSpec((count, width), lambda e, j: (0, e * steps + j))
     weight = pl.BlockSpec((1, depth, width), lambda e, j: (e, 0, j))
+    out = pl.BlockSpec((count, width), lambda e, j: (chunk, e * steps + j))
     return pl.pallas_call(
         expert_kernel,
         grid=(experts, steps),
@@ -254,19 +271,21 @@
             pl.BlockSpec((count, depth), lambda e, j: (0, 0)),
             weight,
             weight,
-            wide,
+            pl.BlockSpec((count, width), lambda e, j: (0, e * steps + j)),
             pl.BlockSpec(gates.shape, lambda e, j: (0, 0)),
-        ],
-        out_specs=[wide, wide, wide, pl.BlockSpec((1, count, 128), lambda e, j: (e, 0, 0))],
-        out_shape=[jax.ShapeDtypeStruct((count, experts * hidden), low_type)] * 3
+        ]
+        + [pl.BlockSpec(memory_space=pl.ANY)] * len(earlier),
+        out_specs=[out, out, out, pl.BlockSpec((1, count, 128), lambda e, j: (e, 0, 0))],
+        out_shape=[jax.ShapeDtypeStruct((count * chunks, experts * hidden), low_type)] * 3
         + [jax.ShapeDtypeStruct((experts, count, 128), wide_type)],
+        input_output_aliases={5 + i: i for i in range(len(earlier))},
         compiler_params=pltpu.CompilerParams(vmem_limit_bytes=56 << 20),
         cost_estimate=pl.CostEstimate(
             flops=4 * count * depth * experts * hidden,
             bytes_accessed=4 * depth * experts * hidden + 20 * count * depth,
             transcendentals=count * experts * hidden,
         ),
-    )(rows, gate_weight, up_weight, stream, gates)
+    )(rows, gate_weight, up_weight, stream, gates, *earlier)
 
 
 def expert_back_kernel(gback_ref, uback_ref, gate_ref, up_ref, out_ref):
@@ -279,11 +298,11 @@
     out_ref[...] = total.astype(low_type)
 
 
-def expert_back(gback, uback, gate_weight, up_weight):
-    count = gback.shape[0]
+def expert_back(gback, uback, gate_weight, up_weight, chunk, chunks):
+    count = gback.shape[0] // chunks
     experts, depth, hidden = gate_weight.shape
     width = 256
-    whole = pl.BlockSpec((count, experts * hidden), lambda j: (0, 0))
+    whole = pl.BlockSpec((count, experts * hidden), lambda j: (chunk, 0))
     weight = pl.BlockSpec((experts, width, hidden), lambda j: (0, j, 0))
     return pl.pallas_call(
         expert_back_kernel,
@@ -382,12 +401,10 @@
         .transpose(1, 0, 2, 3)
         .reshape(model_width, 3 * width_here)
     )
-    token_all = jnp.concatenate(ring_gather(tokens), axis=0)
+    token_all = jnp.concatenate(ring_gather(tokens)[0], axis=0)
     column_share = model_width // replica_count
-    output_pieces = rep_pieces(
-        gather_rows(
-            lax.dynamic_slice_in_dim(output_weight, replica * column_share, column_share, 1)
-        )
+    output_share = gather_rows(
+        lax.dynamic_slice_in_dim(output_weight, replica * column_share, column_share, 1)
     )
 
     def reorder_rows(rows, index):
@@ -408,7 +425,6 @@
 
     hidden_here = down_weight.shape[1]
     flat_down = down_weight.reshape(experts_here * hidden_here, model_width)
-    up_stream = mm(cot_all, flat_down, 1, 1)
 
     allowed = segment[:, None] == segment[None, :]
 
@@ -442,6 +458,14 @@
     mixed_low = jnp.concatenate(mixed_parts, axis=1)
 
     mixed_ordered = reorder_rows(mixed_low, slot_of_device)
+    output_pieces = {0: output_share}
+    distance = replica_count // 2
+    while distance:
+        for j in list(output_pieces):
+            output_pieces[j ^ distance] = rep_exchange(output_pieces[j], distance)
+        if distance == replica_count // 2:
+            output_pieces[distance], mixed_ordered = tie(output_pieces[distance], mixed_ordered)
+        distance //= 2
     mixed_own = (
         swap_all(mixed_ordered.reshape(group_count, row_count, width_here))
         .transpose(1, 0, 2)
@@ -455,7 +479,6 @@
     residual = tokens.astype(wide_type) + attention
     inverse_two = inverse_rms(residual)
     second_input = (residual * inverse_two * postnorm_gain).astype(low_type)
-    second_all = jnp.concatenate(ring_gather(second_input), axis=0)
 
     def gate_table(rows, code):
         logits = mm(rows, full_router, 1, 0)
@@ -463,40 +486,98 @@
         powers = jnp.exp(shifted - jnp.max(shifted, axis=1, keepdims=True))
         return powers / jnp.sum(powers, axis=1, keepdims=True)
 
-    gates_all = gate_table(second_all, code_all)
-    masked_gates = jnp.where(code_all > 1, gates_all, 0.0) * valid_all
-    gates_here = lax.dynamic_slice_in_dim(masked_gates, device * experts_here, experts_here, 1)
-    kept_here = lax.dynamic_slice_in_dim(
-        jnp.where(code_all > 1, valid_all, 0.0), device * experts_here, experts_here, 1
-    )
-
-    inner_all, gback_all, uback_all, pair_lanes = expert_pass(
-        second_all, gate_weight, up_weight, up_stream, gates_here
-    )
-    second_part = expert_back(gback_all, uback_all, gate_weight, up_weight)
-    pair_sent = (
-        (kept_here * jnp.sum(pair_lanes, axis=2).transpose(1, 0))
-    ).reshape(group_count, row_count, experts_here)
-    down_part = mm(inner_all, cot_all, 0, 0).astype(low_type)
-    gate_part = mm(second_all, gback_all, 0, 0).astype(low_type)
-    pair_grad = (
-        swap_all(reorder(pair_sent, slot_of_device))
-        .transpose(1, 0, 2)
-        .reshape(row_count, expert_total)
-    )
-    second_scattered, uback_late, inner_late = lax.optimization_barrier(
-        (ring_scatter(second_part), uback_all, inner_all)
-    )
-    up_part = mm(second_all, uback_late, 0, 0).astype(low_type)
-    mixture_part = mm(inner_late, flat_down, 1, 0).astype(low_type)
+    chunks = 2
+    chunk_rows = group_rows // chunks
+    kept_all = jnp.where(code_all > 1, valid_all, 0.0)
+    kept_here = lax.dynamic_slice_in_dim(kept_all, device * experts_here, experts_here, 1)
+
+    def chunk_of(array, chunk):
+        return array[chunk * chunk_rows : (chunk + 1) * chunk_rows]
+
+    def stream_of(chunk):
+        return (lambda cot_part: (mm(cot_part, flat_down, 1, 1),)), (chunk_of(cot_all, chunk),)
+
+    def expert_chunk(chunk, rows, stream, *earlier):
+        gates = gate_table(rows, chunk_of(code_all, chunk)) * chunk_of(kept_all, chunk)
+        gates_here = lax.dynamic_slice_in_dim(gates, device * experts_here, experts_here, 1)
+        return expert_pass(
+            rows, gate_weight, up_weight, stream, gates_here, chunk, chunks, earlier
+        )
+
+    blocks_here = group_count // chunks
+
+    def first_chunk(blocks, results):
+        rows = jnp.concatenate(blocks[:blocks_here], axis=0)
+        return (
+            lambda stream, rows: (rows,) + tuple(expert_chunk(0, rows, stream))
+        ), (results[1][0], rows)
+
+    blocks, results = ring_gather(
+        second_input,
+        {
+            1: lambda blocks, results: stream_of(0),
+            2: lambda blocks, results: stream_of(1),
+            3: first_chunk,
+        },
+    )
+    rows_first, *earlier, pair_first = results[3]
+    rows_last = jnp.concatenate(blocks[blocks_here:], axis=0)
+    inner_all, gback_all, uback_all, pair_last = expert_chunk(
+        1, rows_last, results[2][0], *earlier
+    )
+    second_all = jnp.concatenate([rows_first, rows_last], axis=0)
+    back_last = expert_back(gback_all, uback_all, gate_weight, up_weight, 1, chunks)
+
+    def back_first(results):
+        return (
+            lambda gback, uback: (
+                expert_back(gback, uback, gate_weight, up_weight, 0, chunks),
+            )
+        ), (gback_all, uback_all)
+
+    def back_block(slot, results):
+        part = back_last if slot >= blocks_here else results[1][0]
+        start = (slot % blocks_here) * row_count
+        return part[start : start + row_count]
+
+    pair_lanes = jnp.concatenate([pair_first, pair_last], axis=1)
+    pair_sent = (kept_here * jnp.sum(pair_lanes, axis=2).transpose(1, 0)).reshape(
+        group_count, row_count, experts_here
+    )
     code_own = route_code
     gates_own = gate_table(second_input, code_own)
-    chosen_grad = gates_own * (
-        pair_grad - jnp.sum(gates_own * pair_grad, axis=1, keepdims=True)
-    )
-    logits_grad = jnp.where(code_own > 0, chosen_grad, 0.0).astype(low_type)
+
+    def grad_of(left, right):
+        return mm(left, right, 0, 0).astype(low_type)
+
+    def down_fill(results):
+        return (
+            lambda inner, pair: (grad_of(inner, cot_all), swap_all(reorder(pair, slot_of_device)))
+        ), (inner_all, pair_sent)
+
+    def gate_fill(results):
+        def work(gback, pair):
+            pair_grad = pair.transpose(1, 0, 2).reshape(row_count, expert_total)
+            chosen_grad = gates_own * (
+                pair_grad - jnp.sum(gates_own * pair_grad, axis=1, keepdims=True)
+            )
+            logits_grad = jnp.where(code_own > 0, chosen_grad, 0.0).astype(low_type)
+            router_back = mm(logits_grad, full_router, 1, 1)
+            return grad_of(second_all, gback), logits_grad, router_back
+
+        return work, (gback_all, results[2][1])
+
+    def up_fill(results):
+        return (lambda uback: (grad_of(second_all, uback),)), (uback_all,)
+
+    second_scattered, results = ring_scatter(
+        back_block, row_count, {1: back_first, 2: down_fill, 3: gate_fill, 4: up_fill}
+    )
+    down_part = results[2][0]
+    gate_part, logits_grad, router_back = results[3]
+    up_part = results[4][0]
     router_part = mm(second_input, logits_grad, 0, 0)
-    second_grad = mm(logits_grad, full_router, 1, 1) + second_scattered
+    second_grad = router_back + second_scattered
     upstream = valid_own * cotangent.astype(wide_type)
     post_back, postnorm_part = norm_backward(residual, inverse_two, postnorm_gain, second_grad)
     residual_grad = upstream + post_back
@@ -512,27 +593,25 @@
             1,
             1,
         )
-    mixed_grad = reorder_rows(
-        swap_all(
-            mixed_grad_own.astype(low_type)
-            .reshape(row_count, group_count, width_here)
-            .transpose(1, 0, 2)
-        ).reshape(group_rows, width_here),
-        device_of_slot,
-    )
-    mixed_grad, mixture_low = lax.optimization_barrier((mixed_grad, mixture_part))
-    mixture = ring_scatter(mixture_low)
-    layer_out = (valid_own * (residual + mixture)).astype(low_type)
-    output_part = mm(mixed_ordered, attention_all, 0, 0).astype(low_type)
-
-    query_parts, key_parts, value_parts = [], [], []
-    querynorm_part = jnp.zeros((head_dim,), wide_type)
-    keynorm_part = jnp.zeros((head_dim,), wide_type)
-    for head in range(heads_here):
+    swap_sent = (
+        mixed_grad_own.astype(low_type)
+        .reshape(row_count, group_count, width_here)
+        .transpose(1, 0, 2)
+    )
+    mixed_swapped, (mixture_part,) = fill_window(
+        ((lambda inner: (mm(inner, flat_down, 1, 0).astype(low_type),)), (inner_all,)),
+        swap_sent,
+        swap_all(swap_sent),
+    )
+    mixed_grad = reorder_rows(mixed_swapped.reshape(group_rows, width_here), device_of_slot)
+
+    def mixture_block(slot, results):
+        return mixture_part[slot * row_count : (slot + 1) * row_count]
+
+    def head_backward(head, grad_head):
         (query_raw, key_raw, query_inverse, key_inverse, query_low, key_low, value_low, log_total) = (
             kept_heads[head]
         )
-        grad_head = mixed_grad[:, head * head_dim : (head + 1) * head_dim]
         scores = jnp.where(allowed, mm(query_low, key_low, 1, 1) * score_scale, masked_value)
         weights = jnp.exp(scores - log_total)
         weight_grad = mm(grad_head, value_low, 1, 1)
@@ -549,16 +628,48 @@
         key_before, key_gain_part = norm_backward(
             key_raw, key_inverse, keynorm_gain, key_unturned
         )
-        querynorm_part = querynorm_part + jnp.sum(query_gain_part, axis=0)
-        keynorm_part = keynorm_part + jnp.sum(key_gain_part, axis=0)
-        query_parts.append(query_before.astype(low_type))
-        key_parts.append(key_before.astype(low_type))
-        value_parts.append(value_back.astype(low_type))
-    sent = jnp.concatenate(query_parts + key_parts + value_parts, axis=1)
+        return (
+            query_before.astype(low_type),
+            key_before.astype(low_type),
+            value_back.astype(low_type),
+            jnp.sum(query_gain_part, axis=0),
+            jnp.sum(key_gain_part, axis=0),
+        )
+
+    def head_fill(head):
+        def fill(results):
+            start = head * head_dim
+            return functools.partial(head_backward, head), (
+                mixed_grad[:, start : start + head_dim],
+            )
+
+        return fill
+
+    mixture, results = ring_scatter(
+        mixture_block, row_count, {2 + head: head_fill(head) for head in range(heads_here)}
+    )
+    layer_out = (valid_own * (residual + mixture)).astype(low_type)
+    head_results = [results[2 + head] for head in range(heads_here)]
+    sent = jnp.concatenate(
+        [head_results[head][part] for part in range(3) for head in range(heads_here)], axis=1
+    )
+    querynorm_part = sum(result[3] for result in head_results)
+    keynorm_part = sum(result[4] for result in head_results)
     first_part = mm(sent, head_weight, 1, 1)
     prenorm_part = jnp.sum(first_part * token_wide * inverse_all, axis=0)
-    first_grad = ring_scatter(first_part.astype(low_type))
-    head_part = mm(first_all, sent, 0, 0).astype(low_type)
+    first_low = first_part.astype(low_type)
+
+    def product_fill(results):
+        return (
+            lambda first, sent, mixed, attention: (grad_of(first, sent), grad_of(mixed, attention))
+        ), (first_all, sent, mixed_ordered, attention_all)
+
+    first_grad, results = ring_scatter(
+        lambda slot, results: first_low[slot * row_count : (slot + 1) * row_count],
+        row_count,
+        {1: product_fill},
+    )
+    head_part, output_part = results[1]
     head_rows = swap_all(
         rep_scatter(head_part.reshape(group_count, replica_count, share, 3 * width_here), 1)
     )
@@ -577,6 +688,9 @@
         .astype(wide_type)
     )
 
+    first_grad, query_grad, key_grad, value_grad, output_grad = tie(
+        first_grad, query_grad, key_grad, value_grad, output_grad
+    )
     token_own = tokens.astype(wide_type)
     inverse_one = inverse_rms(token_own)
     pre_back, _ = norm_backward(token_own, inverse_one, prenorm_gain, first_grad)
@@ -605,11 +719,16 @@
         tiled=True,
     ).astype(wide_type)
     gate_total, up_total = (
-        lax.psum_scatter(part, "rep", scatter_dimension=0, tiled=True)
-        .reshape(column_share, experts_here, hidden_here)
-        .transpose(1, 0, 2)
-        .astype(wide_type)
-        for part in (gate_part, up_part)
+        jnp.stack(
+            [
+                total[:, e * hidden_here : (e + 1) * hidden_here].astype(wide_type)
+                for e in range(experts_here)
+            ]
+        )
+        for total in (
+            lax.psum_scatter(part, "rep", scatter_dimension=0, tiled=True)
+            for part in (gate_part, up_part)
+        )
     )
     return (
         layer_out,

time: 787 us -> 825 us (1.048)
  waiting for transfers between devices: 241 us -> 269 us
  blocking collectives: 0 us -> 20.2 us
  starting transfers between devices: 118 us -> 102 us
  other arithmetic: 95 us -> 110 us
  local copies, waits for them, and re-layouts: 87.1 us -> 75.6 us
  matrix products: 156 us -> 147 us
  Pallas kernels: 64.1 us -> 72.7 us
    reduce_scatter x2, waiting for transfers between devices: 0.01 us -> 50 us  [body(): lax.psum_scatter(part, 'rep', scatter_dimension=0, tiled=True)]
    all_to_all x8 -> x6, waiting for transfers between devices: 74 us -> 51.4 us  [swap_all(): return lax.all_to_all(values, 'ep', split_axis=0, concat_axis=0, tiled=True)]
    all_to_all x0 -> x2, blocking collectives: none -> 20.2 us  [swap_all(): return lax.all_to_all(values, 'ep', split_axis=0, concat_axis=0, tiled=True)]
    ppermute x40, waiting for transfers between devices: 118 us -> 106 us  [ring_shift(): return lax.ppermute(values, 'ep', pairs)]
    ppermute x17, waiting for transfers between devices: 48.5 us -> 60.5 us  [rep_exchange(): lax.ppermute(values, 'rep', [(i, i ^ distance) for i in range(count)])]
    unnamed x315 -> x330, local copies, waits for them, and re-layouts: 49.2 us -> 37.5 us
    all_to_all x8 -> x6, starting transfers between devices: 39.4 us -> 29.3 us  [swap_all(): return lax.all_to_all(values, 'ep', split_axis=0, concat_axis=0, tiled=True)]
    dot_general x33 -> x35, matrix products: 156 us -> 147 us  [mm(): lax.dot_general(left, right, (((left_dim,), (right_dim,)), ((), ())), pre...]
  transfers between devices with their start and end apart: 71 -> 69, of which waited for: 38 -> 23; matrix products, arithmetic and copies ran while one was open for 37% -> 36% of each run, Pallas kernels for 0% -> 4%
where the time goes in v4:
time: 825 us; the launch traced here: 815 us
  waiting for transfers between devices  269 us (33%)
  matrix products  147 us (18%)
  other arithmetic  110 us (13%)
  starting transfers between devices  102 us (12%)
  local copies, waits for them, and re-layouts  75.6 us (9%)
  Pallas kernels  72.7 us (9%)
  blocking collectives  20.2 us (2%)
  between operations  17.7 us (2%)
    dot_general x35, matrix products, mm(): lax.dot_general(left, right, (((left_dim,), (right_dim,)), ((), ())), pre...  147 us
    ppermute x40, waiting for transfers between devices, ring_shift(): return lax.ppermute(values, 'ep', pairs)  106 us
    ppermute x17, waiting for transfers between devices, rep_exchange(): lax.ppermute(values, 'rep', [(i, i ^ distance) for i in range(count)])  60.5 us
    ppermute x40, starting transfers between devices, ring_shift(): return lax.ppermute(values, 'ep', pairs)  59.4 us
    all_to_all x6, waiting for transfers between devices, swap_all(): return lax.all_to_all(values, 'ep', split_axis=0, concat_axis=0, tiled=True)  51.4 us
    reduce_scatter x2, waiting for transfers between devices, body(): lax.psum_scatter(part, 'rep', scatter_dimension=0, tiled=True)  50 us
    pallas_call x2, Pallas kernels, expert_pass(): pl.pallas_call(expert_kernel, grid=(experts, steps), in_specs=[pl.BlockSp...  39 us
    unnamed x330, local copies, waits for them, and re-layouts  37.5 us
  transfers between devices with their start and end apart: 69, of which 23 were waited for; matrix products, arithmetic and copies ran while one was open for 36% of the time, Pallas kernels for 4%

profile of v4, /device:TPU:0, one launch (start us, length us, event | category | flops | bytes accessed | tf_op | source)
XLA Modules:
  0.0 814.7 jit_solution(13726415859547417878)
XLA Ops:
  7.2 3.0 collective-permute-start.1
  14.8 6.2 all-to-all-start.2
  31.3 5.1 all-to-all-start
  44.4 42.4 %collective-permute-done.3 = bf16[160,2048]{1,0:T(8,128)(2,1)} collective-permute-done((bf16[160,2048]{1,0:T(8,128)(2,1)S(1)}, bf16[160,2048]{1,0:T(8,128)(2,1)}, u32[]{:S(2)}, u32[]{:S(2)}) %collective-permute-start.3) | collective-permute-done | bytes 655392 | tf_op jit(solution)/shard_map/ppermute | solution.py:88
  86.8 7.9 collective-permute-start.6
  102.1 6.5 collective-permute-done.6
  120.5 3.6 fusion
  124.2 6.0 fusion.2
  131.7 3.6 maximum_select_fusion
  135.5 3.4 copy-done.22
  138.9 4.3 fusion.100
  156.0 21.4 %collective-permute-done = bf16[2048,512]{1,0:T(8,128)(2,1)S(1)} collective-permute-done((bf16[2048,512]{1,0:T(8,128)(2,1)}, bf16[2048,512]{1,0:T(8,128)(2,1)S(1)}, u32[]{:S(2)}, u32[]{:S(2)}) %collective-permute-start) | collective-permute-done | bytes 2097184 | tf_op jit(solution)/shard_map/ppermute | solution.py:180
  181.4 4.5 all-to-all-start.1
  188.1 29.7 %all-to-all-done.1 = bf16[8,160,256]{2,1,0:T(8,128)(2,1)} async-done(((bf16[8,160,256]{2,1,0:T(8,128)(2,1)}), bf16[8,160,256]{2,1,0:T(8,128)(2,1)}, u32[]{:S(2)}, u32[]{:S(2)}) %all-to-all-start.1) | async-done | bytes 655392 | tf_op jit(solution)/shard_map/all_to_all | solution.py:223
  226.7 2.3 collective-permute-start.14
  235.1 9.5 %fusion.105.stream_ref = f32[640,2048]{1,0:T(8,128)} fusion(bf16[640,2048]{1,0:T(8,128)(2,1)S(1)} %bitcast.212, bf16[2048,2048]{1,0:T(8,128)(2,1)} %bitcast.286), kind=kOutput, calls=%fused_computation.394 | convolution fusion | flops 5368709120 | bytes 16252928 | tf_op jit(solution)/shard_map/dot_general | solution.py:60
  247.5 9.5 %fusion.106.stream_ref = f32[640,2048]{1,0:T(8,128)} fusion(bf16[640,2048]{1,0:T(8,128)(2,1)S(1)} %bitcast.213, bf16[2048,2048]{1,0:T(8,128)(2,1)} %bitcast.287), kind=kOutput, calls=%fused_computation.395 | convolution fusion | flops 5368709120 | bytes 16252928 | tf_op jit(solution)/shard_map/dot_general | solution.py:60
  257.1 3.6 collective-permute-done.15
  267.3 19.6 %shard_map.281 = (bf16[1280,2048]{1,0:T(8,128)(2,1)}, bf16[1280,2048]{1,0:T(8,128)(2,1)}, bf16[1280,2048]{1,0:T(8,128)(2,1)}, f32[2,640,128]{2,1,0:T(8,128)}) custom-call(bf16[640,2048]{1,0:T(8,128)(2,1)} %copy-done.9, bf16[2,2048,1024]{2,1,0:T(8,128)(2,1)} %gate_ref.7, bf16[2,2048,1024]{2,1,0:T(8,128)(2,1)} %up_ref.7, f32[640,2048]{1,0:T(8,128)} %fusion.105.stream_ref, ...), custom_call_target="tpu_custom_call" | custom-call | flops 10737418240 | bytes 42991616 | tf_op jit(solution)/shard_map/pallas_call | solution.py:267
  290.8 5.3 collective-permute-done.19
  302.2 19.4 %shard_map.282 = (bf16[1280,2048]{1,0:T(8,128)(2,1)}, bf16[1280,2048]{1,0:T(8,128)(2,1)}, bf16[1280,2048]{1,0:T(8,128)(2,1)}, f32[2,640,128]{2,1,0:T(8,128)}) custom-call(bf16[640,2048]{1,0:T(8,128)(2,1)} %copy-done.27, bf16[2,2048,1024]{2,1,0:T(8,128)(2,1)} %gate_ref.7, ...), custom_call_target="tpu_custom_call", output_to_operand_aliasing={{0}: (5, {}), {1}: (6, {}), {2}: (7, {})} | custom-call | flops 10737418240 | bytes 42991616 | tf_op jit(solution)/shard_map/pallas_call | solution.py:267
  321.6 16.8 %shard_map.283 = bf16[640,2048]{1,0:T(8,128)(2,1)} custom-call(bf16[1280,2048]{1,0:T(8,128)(2,1)} %get-tuple-element.136.gback_ref, bf16[1280,2048]{1,0:T(8,128)(2,1)} %get-tuple-element.141.uback_ref, bf16[2,2048,1024]{2,1,0:T(8,128)(2,1)} %gate_ref.7, bf16[2,2048,1024]{2,1,0:T(8,128)(2,1)} %up_ref.7), custom_call_target="tpu_custom_call" | custom-call | flops 10737418240 | bytes 24641536 | tf_op jit(solution)/shard_map/pallas_call | solution.py:307
  338.4 2.3 fusion.90
  343.5 16.8 %shard_map.284 = bf16[640,2048]{1,0:T(8,128)(2,1)} custom-call(bf16[1280,2048]{1,0:T(8,128)(2,1)} %get-tuple-element.136.gback_ref, bf16[1280,2048]{1,0:T(8,128)(2,1)} %get-tuple-element.141.uback_ref, bf16[2,2048,1024]{2,1,0:T(8,128)(2,1)} %gate_ref.7, bf16[2,2048,1024]{2,1,0:T(8,128)(2,1)} %up_ref.7), custom_call_target="tpu_custom_call" | custom-call | flops 10737418240 | bytes 24641536 | tf_op jit(solution)/shard_map/pallas_call | solution.py:307
  366.1 4.1 all-to-all-start.3
  370.4 16.7 %convolution_convert_fusion.3 = bf16[2048,2048]{1,0:T(8,128)(2,1)} fusion(bf16[1280,2048]{1,0:T(8,128)(2,1)} %get-tuple-element.144, bf16[1280,2048]{1,0:T(8,128)(2,1)} %bitcast.231), kind=kOutput, calls=%fused_computation.15 | convolution fusion | flops 10741612544 | bytes 18874368 | tf_op jit(solution)/shard_map/dot_general | solution.py:60
  387.2 2.3 add_convert_fusion.11
  393.7 16.7 %convolution_convert_fusion.2 = bf16[2048,2048]{1,0:T(8,128)(2,1)} fusion(bf16[1280,2048]{1,0:T(8,128)(2,1)} %copy-done.44, bf16[1280,2048]{1,0:T(8,128)(2,1)} %get-tuple-element.136.gback_ref), kind=kOutput, calls=%fused_computation.14 | convolution fusion | flops 10741612544 | bytes 18874368 | tf_op jit(solution)/shard_map/dot_general | solution.py:60
  411.0 3.0 add_convert_fusion.9
  416.3 16.8 %convolution_convert_fusion.1 = bf16[2048,2048]{1,0:T(8,128)(2,1)} fusion(bf16[1280,2048]{1,0:T(8,128)(2,1)} %copy-done.44, bf16[1280,2048]{1,0:T(8,128)(2,1)} %get-tuple-element.141.uback_ref), kind=kOutput, calls=%fused_computation.13 | convolution fusion | flops 10741612544 | bytes 18874368 | tf_op jit(solution)/shard_map/dot_general | solution.py:60
  440.2 2.4 fusion.61
  442.7 2.6 fusion.57
  446.1 2.6 fusion.11
  449.6 5.9 all-to-all-start.4
  455.9 16.5 %convolution_convert_fusion = bf16[1280,2048]{1,0:T(8,128)(2,1)} fusion(bf16[1280,2048]{1,0:T(8,128)(2,1)} %get-tuple-element.144, bf16[2048,2048]{1,0:T(8,128)(2,1)} %bitcast.288), kind=kOutput, calls=%fused_computation.12 | convolution fusion | flops 10740039680 | bytes 18874368 | tf_op jit(solution)/shard_map/dot_general | solution.py:60
  472.5 13.5 %all-to-all-done.4 = bf16[8,160,256]{2,1,0:T(8,128)(2,1)S(1)} async-done(((bf16[8,160,256]{2,1,0:T(8,128)(2,1)}), bf16[8,160,256]{2,1,0:T(8,128)(2,1)S(1)}, u32[]{:S(2)}, u32[]{:S(2)}) %all-to-all-start.4) | async-done | bytes 655392 | tf_op jit(solution)/shard_map/all_to_all | solution.py:223
  489.9 8.2 %collective-permute-done.29 = bf16[80,2048]{1,0:T(8,128)(2,1)S(1)} collective-permute-done((bf16[80,2048]{1,0:T(8,128)(2,1)S(1)}, bf16[80,2048]{1,0:T(8,128)(2,1)S(1)}, u32[]{:S(2)}, u32[]{:S(2)}) %collective-permute-start.29) | collective-permute-done | bytes 327712 | tf_op jit(solution)/shard_map/ppermute | solution.py:88
  498.1 4.4 collective-permute-done.31
  506.0 4.9 multiply_reduce_fusion.1
  510.8 5.8 collective-permute-start.32
  516.8 4.1 multiply_convert_fusion.1
  525.7 25.4 %collective-permute-done.32 = bf16[160,2048]{1,0:T(8,128)(2,1)} collective-permute-done((bf16[160,2048]{1,0:T(8,128)(2,1)S(1)}, bf16[160,2048]{1,0:T(8,128)(2,1)}, u32[]{:S(2)}, u32[]{:S(2)}) %collective-permute-start.32) | collective-permute-done | bytes 655392 | tf_op jit(solution)/shard_map/ppermute | solution.py:88
  551.1 3.3 add_convert_fusion.7
  555.7 5.3 multiply_reduce_fusion
  563.2 5.5 multiply_convert_fusion
  574.7 8.4 %fusion.4 = (f32[2048]{0:T(1024)S(1)}, bf16[1280,2048]{1,0:T(8,128)(2,1)S(1)}) fusion(bf16[1280,2048]{1,0:T(8,128)(2,1)} %constant_dynamic-update-slice_fusion, f32[1280]{0:T(1024)S(1)} %copy-done.84, bf16[1280,768]{0,1:T(8,128)(2,1)S(1)} %constant_dynamic-update-slice_fusion.52, bf16[2048,768]{1,0:T(8,128)(2,1)S(1)} %bitcast.200), kind=kOutput, calls=%fused_computation.7 | convolution fusion | flops 4039636992 | bytes 15610880 | tf_op jit(solution)/shard_map/dot_general | solution.py:60
  588.4 7.6 convolution_convert_fusion.4
  596.1 2.5 convolution_convert_fusion.5
  601.1 11.3 %all_to_all.48 = f32[8,1,4352]{2,1,0:T(1,128)} all-to-all(f32[8,1,4352]{2,1,0:T(1,128)S(1)} %copy.170), channel_id=1, replica_groups=mesh['rep'=4,'ep'=8] {'ep'}, dimensions={0} | all-to-all | bytes 278528 | tf_op jit(solution)/shard_map/all_to_all | solution.py:223
  617.8 8.9 %all_to_all.49 = f32[8,1,288]{2,1,0:T(1,128)S(1)} all-to-all(f32[8,1,288]{2,1,0:T(1,128)S(1)} %all_to_all.38), channel_id=1, replica_groups=mesh['rep'=4,'ep'=8] {'ep'}, dimensions={0} | all-to-all | bytes 18432 | tf_op jit(solution)/shard_map/all_to_all | solution.py:223
  641.7 18.2 %collective-permute-done.46 = bf16[8,1,64,768]{3,2,0,1:T(8,128)(2,1)S(1)} collective-permute-done((bf16[8,1,64,768]{3,2,0,1:T(8,128)(2,1)S(1)}, bf16[8,1,64,768]{3,2,0,1:T(8,128)(2,1)S(1)}, u32[]{:S(2)}, u32[]{:S(2)}) %collective-permute-start.46) | collective-permute-done | bytes 786464 | tf_op jit(solution)/shard_map/ppermute | solution.py:180
  661.0 3.5 all-to-all-start.5
  664.6 3.3 add_convert_fusion.4
  670.3 2.5 collective-permute-start.51
  672.9 3.1 add_convert_fusion.6
  677.8 7.2 all-to-all-done.5
  686.3 2.4 collective-permute-start.47
  696.2 5.8 collective-permute-start.41
  702.0 19.3 %collective-permute-done.47 = bf16[1,3,64,2048]{3,2,1,0:T(8,128)(2,1)S(1)} collective-permute-done((bf16[1,3,64,2048]{3,2,1,0:T(8,128)(2,1)S(1)}, bf16[1,3,64,2048]{3,2,1,0:T(8,128)(2,1)S(1)}, u32[]{:S(2)}, u32[]{:S(2)}) %collective-permute-start.47) | collective-permute-done | bytes 786464 | tf_op jit(solution)/shard_map/ppermute | solution.py:180
  723.6 2.4 multiply_convert_fusion.2
  727.7 4.1 collective-permute-done.44
  735.3 2.4 maximum_select_fusion.1
  744.9 4.4 convert_element_type.544
  753.4 50.0 %reduce-scatter.6.cloned.1.call-done = bf16[512,2048]{1,0:T(8,128)(2,1)} async-done(((bf16[2048,2048]{1,0:T(8,128)(2,1)}), bf16[512,2048]{1,0:T(8,128)(2,1)}) %reduce-scatter.6.cloned.1.call-update) | async-done | bytes 2097168 | tf_op jit(solution)/shard_map/reduce_scatter | solution.py:729
  (651 shorter events, 206.6 us)
Async XLA Ops:
  7.2 32.9 %collective-permute-start.1 = (bf16[160,2048]{1,0:T(8,128)(2,1)}, bf16[160,2048]{1,0:T(8,128)(2,1)S(1)}, u32[]{:S(2)}, u32[]{:S(2)}) collective-permute-start(bf16[160,2048]{1,0:T(8,128)(2,1)} %param.18), channel_id=1, source_target_pairs={{0,1},{2,0},{4,2},{6,4},{7,6},{5,7},{3,5},{1,3},{8,9},{10,8},{12,1... | collective-permute-start | bytes 1966088 | tf_op jit(solution)/shard_map/ppermute | solution.py:88
  10.2 31.9 %collective-permute-start.2 = (bf16[160,2048]{1,0:T(8,128)(2,1)}, bf16[160,2048]{1,0:T(8,128)(2,1)}, u32[]{:S(2)}, u32[]{:S(2)}) collective-permute-start(bf16[160,2048]{1,0:T(8,128)(2,1)} %param.18), channel_id=1, source_target_pairs={{0,2},{2,4},{4,6},{6,7},{7,5},{5,3},{3,1},{1,0},{8,10},{10,12},{12... | collective-permute-start | bytes 1966088 | tf_op jit(solution)/shard_map/ppermute | solution.py:88
  14.8 16.5 %all-to-all-start.2 = ((bf16[8,52,128]{2,1,0:T(8,128)(2,1)}), bf16[8,52,128]{2,1,0:T(8,128)(2,1)S(1)}, u32[]{:S(2)}, u32[]{:S(2)}) async-start(bf16[8,52,128]{2,1,0:T(8,128)(2,1)} %broadcast_in_dim.188), calls=%async_computation.2 | async-start | bytes 229376 | tf_op jit(solution)/shard_map/all_to_all | solution.py:223
  21.0 109.2 %all-gather.4.cloned.1.call-start = ((), (), s32[]{:S(2)}) async-start(), calls=%async_computation.11 | async-start | bytes 2359296 | tf_op jit(solution)/shard_map/all_gather | solution.py:69
  31.3 65.3 %all-to-all-start = ((bf16[8,64,768]{2,1,0:T(8,128)(2,1)}), bf16[8,64,768]{2,1,0:T(8,128)(2,1)S(1)}, u32[]{:S(2)}, u32[]{:S(2)}) async-start(bf16[8,64,768]{2,1,0:T(8,128)(2,1)} %copy.125), calls=%async_computation | async-start | bytes 1572864 | tf_op jit(solution)/shard_map/all_to_all | solution.py:223
  36.4 193.7 %all-gather.6.cloned.1.call-start = ((), (), s32[]{:S(2)}) async-start(), calls=%async_computation.12 | async-start | bytes 5898240 | tf_op jit(solution)/shard_map/all_gather | solution.py:69
  40.1 46.7 %collective-permute-start.3 = (bf16[160,2048]{1,0:T(8,128)(2,1)S(1)}, bf16[160,2048]{1,0:T(8,128)(2,1)}, u32[]{:S(2)}, u32[]{:S(2)}) collective-permute-start(bf16[160,2048]{1,0:T(8,128)(2,1)S(1)} %collective-permute-done.1), channel_id=1, source_target_pairs={{0,1},{2,0},{4,2},{6,4},{7,6},{5,7},{3,5},{1,3},{8,9},{10,8},{12,1... | collective-permute-start | bytes 1966088 | tf_op jit(solution)/shard_map/ppermute | solution.py:88
  42.1 44.7 %collective-permute-start.4 = (bf16[160,2048]{1,0:T(8,128)(2,1)}, bf16[160,2048]{1,0:T(8,128)(2,1)}, u32[]{:S(2)}, u32[]{:S(2)}) collective-permute-start(bf16[160,2048]{1,0:T(8,128)(2,1)} %collective-permute-done.2), channel_id=1, source_target_pairs={{0,2},{2,4},{4,6},{6,7},{7,5},{5,3},{3,1},{1,0},{8,10},{10,12},{12... | collective-permute-start | bytes 1966088 | tf_op jit(solution)/shard_map/ppermute | solution.py:88
  86.8 25.1 %collective-permute-start.5 = (bf16[160,2048]{1,0:T(8,128)(2,1)}, bf16[160,2048]{1,0:T(8,128)(2,1)S(1)}, u32[]{:S(2)}, u32[]{:S(2)}) collective-permute-start(bf16[160,2048]{1,0:T(8,128)(2,1)} %collective-permute-done.3), channel_id=1, source_target_pairs={{0,1},{2,0},{4,2},{6,4},{7,6},{5,7},{3,5},{1,3},{8,9},{10,8},{12,1... | collective-permute-start | bytes 1966088 | tf_op jit(solution)/shard_map/ppermute | solution.py:88
  86.8 21.9 %collective-permute-start.6 = (bf16[160,2048]{1,0:T(8,128)(2,1)}, bf16[160,2048]{1,0:T(8,128)(2,1)}, u32[]{:S(2)}, u32[]{:S(2)}) collective-permute-start(bf16[160,2048]{1,0:T(8,128)(2,1)} %collective-permute-done.4), channel_id=1, source_target_pairs={{0,2},{2,4},{4,6},{6,7},{7,5},{5,3},{3,1},{1,0},{8,10},{10,12},{12... | collective-permute-start | bytes 1966088 | tf_op jit(solution)/shard_map/ppermute | solution.py:88
  96.7 18.6 %collective-permute-start.9 = (bf16[1,8,64,768]{3,2,1,0:T(8,128)(2,1)S(1)}, bf16[1,8,64,768]{3,2,1,0:T(8,128)(2,1)S(1)}, u32[]{:S(2)}, u32[]{:S(2)}) collective-permute-start(bf16[1,8,64,768]{3,2,1,0:T(8,128)(2,1)S(1)} %bitcast.183), channel_id=1, source_target_pairs={{0,16},{8,24},{16,0},{24,8},{1,17},{9,25},{17,1},{25,9},{2,18},{10... | collective-permute-start | bytes 2359304 | tf_op jit(solution)/shard_map/ppermute | solution.py:180
  109.7 9.4 %collective-permute-start.7 = (bf16[80,2048]{1,0:T(8,128)(2,1)S(1)}, bf16[80,2048]{1,0:T(8,128)(2,1)S(1)}, u32[]{:S(2)}, u32[]{:S(2)}) collective-permute-start(bf16[80,2048]{1,0:T(8,128)(2,1)S(1)} %slice.435), channel_id=1, source_target_pairs={{0,2},{2,4},{4,6},{6,7},{7,5},{5,3},{3,1},{1,0},{8,10},{10,12},{12... | collective-permute-start | bytes 983048 | tf_op jit(solution)/shard_map/ppermute | solution.py:88
  116.7 15.0 %collective-permute-start.10 = (bf16[2,8,64,768]{3,2,1,0:T(8,128)(2,1)}, bf16[2,8,64,768]{3,2,1,0:T(8,128)(2,1)}, u32[]{:S(2)}, u32[]{:S(2)}) collective-permute-start(bf16[2,8,64,768]{3,2,1,0:T(8,128)(2,1)} %maximum_select_fusion.3), channel_id=1, source_target_pairs={{0,8},{8,0},{16,24},{24,16},{1,9},{9,1},{17,25},{25,17},{2,10},{10... | collective-permute-start | bytes 4718600 | tf_op jit(solution)/shard_map/ppermute | solution.py:180
  130.2 47.3 %collective-permute-start = (bf16[2048,512]{1,0:T(8,128)(2,1)}, bf16[2048,512]{1,0:T(8,128)(2,1)S(1)}, u32[]{:S(2)}, u32[]{:S(2)}) collective-permute-start(bf16[2048,512]{1,0:T(8,128)(2,1)} %all-gather.4.cloned.1.call-done), channel_id=1, source_target_pairs={{0,16},{8,24},{16,0},{24,8},{1,17},{9,25},{17,1},{25,9},{2,18},{10... | collective-permute-start | bytes 6291464 | tf_op jit(solution)/shard_map/ppermute | solution.py:180
  131.7 89.0 %collective-permute-start.11 = (bf16[2048,512]{1,0:T(8,128)(2,1)}, bf16[2048,512]{1,0:T(8,128)(2,1)}, u32[]{:S(2)}, u32[]{:S(2)}) collective-permute-start(bf16[2048,512]{1,0:T(8,128)(2,1)} %all-gather.4.cloned.1.call-done), channel_id=1, source_target_pairs={{0,8},{8,0},{16,24},{24,16},{1,9},{9,1},{17,25},{25,17},{2,10},{10... | collective-permute-start | bytes 6291464 | tf_op jit(solution)/shard_map/ppermute | solution.py:180
  177.5 45.4 %collective-permute-start.12 = (bf16[2048,512]{1,0:T(8,128)(2,1)S(1)}, bf16[2048,512]{1,0:T(8,128)(2,1)}, u32[]{:S(2)}, u32[]{:S(2)}) collective-permute-start(bf16[2048,512]{1,0:T(8,128)(2,1)S(1)} %collective-permute-done), channel_id=1, source_target_pairs={{0,8},{8,0},{16,24},{24,16},{1,9},{9,1},{17,25},{25,17},{2,10},{10... | collective-permute-start | bytes 6291464 | tf_op jit(solution)/shard_map/ppermute | solution.py:180
  181.4 36.4 %all-to-all-start.1 = ((bf16[8,160,256]{2,1,0:T(8,128)(2,1)}), bf16[8,160,256]{2,1,0:T(8,128)(2,1)}, u32[]{:S(2)}, u32[]{:S(2)}) async-start(bf16[8,160,256]{2,1,0:T(8,128)(2,1)} %copy-done.47), calls=%async_computation.1 | async-start | bytes 1310720 | tf_op jit(solution)/shard_map/all_to_all | solution.py:223
  226.6 18.5 %collective-permute-start.13 = (bf16[160,2048]{1,0:T(8,128)(2,1)S(1)}, bf16[160,2048]{1,0:T(8,128)(2,1)S(1)}, u32[]{:S(2)}, u32[]{:S(2)}) collective-permute-start(bf16[160,2048]{1,0:T(8,128)(2,1)S(1)} %multiply_convert_fusion.3), channel_id=1, source_target_pairs={{0,2},{2,4},{4,6},{6,7},{7,5},{5,3},{3,1},{1,0},{8,10},{10,12},{12... | collective-permute-start | bytes 1966088 | tf_op jit(solution)/shard_map/ppermute | solution.py:88
  226.7 18.4 %collective-permute-start.14 = (bf16[160,2048]{1,0:T(8,128)(2,1)S(1)}, bf16[160,2048]{1,0:T(8,128)(2,1)S(1)}, u32[]{:S(2)}, u32[]{:S(2)}) collective-permute-start(bf16[160,2048]{1,0:T(8,128)(2,1)S(1)} %multiply_convert_fusion.3), channel_id=1, source_target_pairs={{0,1},{2,0},{4,2},{6,4},{7,6},{5,7},{3,5},{1,3},{8,9},{10,8},{12,1... | collective-permute-start | bytes 1966088 | tf_op jit(solution)/shard_map/ppermute | solution.py:88
  245.1 15.6 %collective-permute-start.15 = (bf16[160,2048]{1,0:T(8,128)(2,1)S(1)}, bf16[160,2048]{1,0:T(8,128)(2,1)}, u32[]{:S(2)}, u32[]{:S(2)}) collective-permute-start(bf16[160,2048]{1,0:T(8,128)(2,1)S(1)} %collective-permute-done.13), channel_id=1, source_target_pairs={{0,2},{2,4},{4,6},{6,7},{7,5},{5,3},{3,1},{1,0},{8,10},{10,12},{12... | collective-permute-start | bytes 1966088 | tf_op jit(solution)/shard_map/ppermute | solution.py:88
  245.2 15.9 %collective-permute-start.16 = (bf16[160,2048]{1,0:T(8,128)(2,1)S(1)}, bf16[160,2048]{1,0:T(8,128)(2,1)}, u32[]{:S(2)}, u32[]{:S(2)}) collective-permute-start(bf16[160,2048]{1,0:T(8,128)(2,1)S(1)} %collective-permute-done.14), channel_id=1, source_target_pairs={{0,1},{2,0},{4,2},{6,4},{7,6},{5,7},{3,5},{1,3},{8,9},{10,8},{12,1... | collective-permute-start | bytes 1966088 | tf_op jit(solution)/shard_map/ppermute | solution.py:88
  262.3 24.6 %collective-permute-start.18 = (bf16[160,2048]{1,0:T(8,128)(2,1)}, bf16[160,2048]{1,0:T(8,128)(2,1)S(1)}, u32[]{:S(2)}, u32[]{:S(2)}) collective-permute-start(bf16[160,2048]{1,0:T(8,128)(2,1)} %collective-permute-done.16), channel_id=1, source_target_pairs={{0,1},{2,0},{4,2},{6,4},{7,6},{5,7},{3,5},{1,3},{8,9},{10,8},{12,1... | collective-permute-start | bytes 1966088 | tf_op jit(solution)/shard_map/ppermute | solution.py:88
  263.7 23.1 %collective-permute-start.17 = (bf16[160,2048]{1,0:T(8,128)(2,1)}, bf16[160,2048]{1,0:T(8,128)(2,1)S(1)}, u32[]{:S(2)}, u32[]{:S(2)}) collective-permute-start(bf16[160,2048]{1,0:T(8,128)(2,1)} %collective-permute-done.15), channel_id=1, source_target_pairs={{0,2},{2,4},{4,6},{6,7},{7,5},{5,3},{3,1},{1,0},{8,10},{10,12},{12... | collective-permute-start | bytes 1966088 | tf_op jit(solution)/shard_map/ppermute | solution.py:88
  340.8 19.8 %collective-permute-start.21 = (bf16[80,2048]{1,0:T(8,128)(2,1)}, bf16[80,2048]{1,0:T(8,128)(2,1)}, u32[]{:S(2)}, u32[]{:S(2)}) collective-permute-start(bf16[80,2048]{1,0:T(8,128)(2,1)} %get-tuple-element.329), channel_id=1, source_target_pairs={{0,2},{2,4},{4,6},{6,7},{7,5},{5,3},{3,1},{1,0},{8,10},{10,12},{12... | collective-permute-start | bytes 983048 | tf_op jit(solution)/shard_map/ppermute | solution.py:88
  342.4 18.2 %collective-permute-start.22 = (bf16[80,2048]{1,0:T(8,128)(2,1)}, bf16[80,2048]{1,0:T(8,128)(2,1)}, u32[]{:S(2)}, u32[]{:S(2)}) collective-permute-start(bf16[80,2048]{1,0:T(8,128)(2,1)} %get-tuple-element.328), channel_id=1, source_target_pairs={{0,1},{2,0},{4,2},{6,4},{7,6},{5,7},{3,5},{1,3},{8,9},{10,8},{12,1... | collective-permute-start | bytes 983048 | tf_op jit(solution)/shard_map/ppermute | solution.py:88
  362.1 25.0 %collective-permute-start.24 = (bf16[160,2048]{1,0:T(8,128)(2,1)S(1)}, bf16[160,2048]{1,0:T(8,128)(2,1)}, u32[]{:S(2)}, u32[]{:S(2)}) collective-permute-start(bf16[160,2048]{1,0:T(8,128)(2,1)S(1)} %pad_maximum_fusion.7), channel_id=1, source_target_pairs={{0,1},{2,0},{4,2},{6,4},{7,6},{5,7},{3,5},{1,3},{8,9},{10,8},{12,1... | collective-permute-start | bytes 1966088 | tf_op jit(solution)/shard_map/ppermute | solution.py:88
  363.4 23.8 %collective-permute-start.23 = (bf16[160,2048]{1,0:T(8,128)(2,1)}, bf16[160,2048]{1,0:T(8,128)(2,1)S(1)}, u32[]{:S(2)}, u32[]{:S(2)}) collective-permute-start(bf16[160,2048]{1,0:T(8,128)(2,1)} %pad_maximum_fusion.6), channel_id=1, source_target_pairs={{0,2},{2,4},{4,6},{6,7},{7,5},{5,3},{3,1},{1,0},{8,10},{10,12},{12... | collective-permute-start | bytes 1966088 | tf_op jit(solution)/shard_map/ppermute | solution.py:88
  366.1 21.1 %all-to-all-start.3 = ((f32[8,160,2]{1,2,0:T(2,128)}), f32[8,160,2]{1,2,0:T(2,128)S(1)}, u32[]{:S(2)}, u32[]{:S(2)}) async-start(f32[8,160,2]{1,2,0:T(2,128)} %copy.160), calls=%async_computation.3 | async-start | bytes 32768 | tf_op jit(solution)/shard_map/all_to_all | solution.py:223
  370.2 218.2 %all-gather.8.cloned.1.call-start = ((), (), s32[]{:S(2)}) async-start(), calls=%async_computation.13 | async-start | bytes 5898240 | tf_op jit(solution)/shard_map/all_gather | solution.py:69
  389.5 21.4 %collective-permute-start.26 = (bf16[160,2048]{1,0:T(8,128)(2,1)}, bf16[160,2048]{1,0:T(8,128)(2,1)}, u32[]{:S(2)}, u32[]{:S(2)}) collective-permute-start(bf16[160,2048]{1,0:T(8,128)(2,1)} %add_convert_fusion.11), channel_id=1, source_target_pairs={{0,1},{2,0},{4,2},{6,4},{7,6},{5,7},{3,5},{1,3},{8,9},{10,8},{12,1... | collective-permute-start | bytes 1966088 | tf_op jit(solution)/shard_map/ppermute | solution.py:88
  393.6 17.3 %collective-permute-start.25 = (bf16[160,2048]{1,0:T(8,128)(2,1)}, bf16[160,2048]{1,0:T(8,128)(2,1)S(1)}, u32[]{:S(2)}, u32[]{:S(2)}) collective-permute-start(bf16[160,2048]{1,0:T(8,128)(2,1)} %add_convert_fusion.12), channel_id=1, source_target_pairs={{0,2},{2,4},{4,6},{6,7},{7,5},{5,3},{3,1},{1,0},{8,10},{10,12},{12... | collective-permute-start | bytes 1966088 | tf_op jit(solution)/shard_map/ppermute | solution.py:88
  414.0 19.1 %collective-permute-start.27 = (bf16[160,2048]{1,0:T(8,128)(2,1)}, bf16[160,2048]{1,0:T(8,128)(2,1)}, u32[]{:S(2)}, u32[]{:S(2)}) collective-permute-start(bf16[160,2048]{1,0:T(8,128)(2,1)} %get-tuple-element.325), channel_id=1, source_target_pairs={{0,2},{2,4},{4,6},{6,7},{7,5},{5,3},{3,1},{1,0},{8,10},{10,12},{12... | collective-permute-start | bytes 1966088 | tf_op jit(solution)/shard_map/ppermute | solution.py:88
  416.0 17.1 %collective-permute-start.28 = (bf16[160,2048]{1,0:T(8,128)(2,1)}, bf16[160,2048]{1,0:T(8,128)(2,1)}, u32[]{:S(2)}, u32[]{:S(2)}) collective-permute-start(bf16[160,2048]{1,0:T(8,128)(2,1)} %get-tuple-element.324), channel_id=1, source_target_pairs={{0,1},{2,0},{4,2},{6,4},{7,6},{5,7},{3,5},{1,3},{8,9},{10,8},{12,1... | collective-permute-start | bytes 1966088 | tf_op jit(solution)/shard_map/ppermute | solution.py:88
  437.3 307.6 %reduce-scatter.8.cloned.1.call-start = ((), (), s32[]{:S(2)}) async-start(), calls=%async_computation.16 | async-start | bytes 10485760 | tf_op jit(solution)/shard_map/reduce_scatter | solution.py:715
  437.9 311.5 %reduce-scatter.4.cloned.1.call-start = ((), (), s32[]{:S(2)}) async-start(), calls=%async_computation.14 | async-start | bytes 10485760 | tf_op jit(solution)/shard_map/reduce_scatter | solution.py:729
  449.6 36.4 %all-to-all-start.4 = ((bf16[8,160,256]{2,1,0:T(8,128)(2,1)}), bf16[8,160,256]{2,1,0:T(8,128)(2,1)S(1)}, u32[]{:S(2)}, u32[]{:S(2)}) async-start(bf16[8,160,256]{2,1,0:T(8,128)(2,1)} %bitcast.171), calls=%async_computation.4 | async-start | bytes 1310720 | tf_op jit(solution)/shard_map/all_to_all | solution.py:223
  455.5 347.9 %reduce-scatter.6.cloned.1.call-start = ((), (), s32[]{:S(2)}) async-start(), calls=%async_computation.15 | async-start | bytes 10485760 | tf_op jit(solution)/shard_map/reduce_scatter | solution.py:729
  487.7 10.4 %collective-permute-start.29 = (bf16[80,2048]{1,0:T(8,128)(2,1)S(1)}, bf16[80,2048]{1,0:T(8,128)(2,1)S(1)}, u32[]{:S(2)}, u32[]{:S(2)}) collective-permute-start(bf16[80,2048]{1,0:T(8,128)(2,1)S(1)} %get-tuple-element.306), channel_id=1, source_target_pairs={{0,2},{2,4},{4,6},{6,7},{7,5},{5,3},{3,1},{1,0},{8,10},{10,12},{12... | collective-permute-start | bytes 983048 | tf_op jit(solution)/shard_map/ppermute | solution.py:88
  487.7 14.7 %collective-permute-start.31 = (bf16[80,2048]{1,0:T(8,128)(2,1)S(1)}, bf16[80,2048]{1,0:T(8,128)(2,1)S(1)}, u32[]{:S(2)}, u32[]{:S(2)}) collective-permute-start(bf16[80,2048]{1,0:T(8,128)(2,1)S(1)} %get-tuple-element.304), channel_id=1, source_target_pairs={{0,1},{2,0},{4,2},{6,4},{7,6},{5,7},{3,5},{1,3},{8,9},{10,8},{12,1... | collective-permute-start | bytes 983048 | tf_op jit(solution)/shard_map/ppermute | solution.py:88
  510.8 40.3 %collective-permute-start.32 = (bf16[160,2048]{1,0:T(8,128)(2,1)S(1)}, bf16[160,2048]{1,0:T(8,128)(2,1)}, u32[]{:S(2)}, u32[]{:S(2)}) collective-permute-start(bf16[160,2048]{1,0:T(8,128)(2,1)S(1)} %pad_maximum_fusion.9), channel_id=1, source_target_pairs={{0,1},{2,0},{4,2},{6,4},{7,6},{5,7},{3,5},{1,3},{8,9},{10,8},{12,1... | collective-permute-start | bytes 1966088 | tf_op jit(solution)/shard_map/ppermute | solution.py:88
  516.6 34.6 %collective-permute-start.30 = (bf16[160,2048]{1,0:T(8,128)(2,1)}, bf16[160,2048]{1,0:T(8,128)(2,1)}, u32[]{:S(2)}, u32[]{:S(2)}) collective-permute-start(bf16[160,2048]{1,0:T(8,128)(2,1)} %pad_maximum_fusion.8), channel_id=1, source_target_pairs={{0,2},{2,4},{4,6},{6,7},{7,5},{5,3},{3,1},{1,0},{8,10},{10,12},{12... | collective-permute-start | bytes 1966088 | tf_op jit(solution)/shard_map/ppermute | solution.py:88
  561.0 11.9 %collective-permute-start.33 = (bf16[160,2048]{1,0:T(8,128)(2,1)}, bf16[160,2048]{1,0:T(8,128)(2,1)S(1)}, u32[]{:S(2)}, u32[]{:S(2)}) collective-permute-start(bf16[160,2048]{1,0:T(8,128)(2,1)} %get-tuple-element.302), channel_id=1, source_target_pairs={{0,2},{2,4},{4,6},{6,7},{7,5},{5,3},{3,1},{1,0},{8,10},{10,12},{12... | collective-permute-start | bytes 1966088 | tf_op jit(solution)/shard_map/ppermute | solution.py:88
  561.0 11.9 %collective-permute-start.34 = (bf16[160,2048]{1,0:T(8,128)(2,1)}, bf16[160,2048]{1,0:T(8,128)(2,1)}, u32[]{:S(2)}, u32[]{:S(2)}) collective-permute-start(bf16[160,2048]{1,0:T(8,128)(2,1)} %get-tuple-element.301), channel_id=1, source_target_pairs={{0,1},{2,0},{4,2},{6,4},{7,6},{5,7},{3,5},{1,3},{8,9},{10,8},{12,1... | collective-permute-start | bytes 1966088 | tf_op jit(solution)/shard_map/ppermute | solution.py:88
  586.2 12.4 %collective-permute-start.37 = (bf16[80,2048]{1,0:T(8,128)(2,1)S(1)}, bf16[80,2048]{1,0:T(8,128)(2,1)S(1)}, u32[]{:S(2)}, u32[]{:S(2)}) collective-permute-start(bf16[80,2048]{1,0:T(8,128)(2,1)S(1)} %get-tuple-element.298), channel_id=1, source_target_pairs={{0,2},{2,4},{4,6},{6,7},{7,5},{5,3},{3,1},{1,0},{8,10},{10,12},{12... | collective-permute-start | bytes 983048 | tf_op jit(solution)/shard_map/ppermute | solution.py:88
  586.2 12.4 %collective-permute-start.38 = (bf16[80,2048]{1,0:T(8,128)(2,1)S(1)}, bf16[80,2048]{1,0:T(8,128)(2,1)S(1)}, u32[]{:S(2)}, u32[]{:S(2)}) collective-permute-start(bf16[80,2048]{1,0:T(8,128)(2,1)S(1)} %get-tuple-element.297), channel_id=1, source_target_pairs={{0,1},{2,0},{4,2},{6,4},{7,6},{5,7},{3,5},{1,3},{8,9},{10,8},{12,1... | collective-permute-start | bytes 983048 | tf_op jit(solution)/shard_map/ppermute | solution.py:88
  600.2 34.4 %collective-permute-start.45 = (bf16[8,2,64,768]{3,2,0,1:T(8,128)(2,1)S(1)}, bf16[8,2,64,768]{3,2,0,1:T(8,128)(2,1)}, u32[]{:S(2)}, u32[]{:S(2)}) collective-permute-start(bf16[8,2,64,768]{3,2,0,1:T(8,128)(2,1)S(1)} %bitcast.218), channel_id=1, source_target_pairs={{0,8},{8,0},{16,24},{24,16},{1,9},{9,1},{17,25},{25,17},{2,10},{10... | collective-permute-start | bytes 4718600 | tf_op jit(solution)/shard_map/ppermute | solution.py:180
  614.7 12.1 %collective-permute-start.54 = (f32[4352]{0:T(1024)S(1)}, f32[4352]{0:T(1024)S(1)}, u32[]{:S(2)}, u32[]{:S(2)}) collective-permute-start(f32[4352]{0:T(1024)S(1)} %add.686), channel_id=1, source_target_pairs={{0,16},{8,24},{16,0},{24,8},{1,17},{9,25},{17,1},{25,9},{2,18},{10... | collective-permute-start | bytes 52232 | tf_op jit(solution)/shard_map/ppermute | solution.py:180
  629.8 48.0 %collective-permute-start.56 = (f32[288]{0:T(512)S(1)}, f32[288]{0:T(512)S(1)}, u32[]{:S(2)}, u32[]{:S(2)}) collective-permute-start(f32[288]{0:T(512)S(1)} %add.690), channel_id=1, source_target_pairs={{0,16},{8,24},{16,0},{24,8},{1,17},{9,25},{17,1},{25,9},{2,18},{10... | collective-permute-start | bytes 3464 | tf_op jit(solution)/shard_map/ppermute | solution.py:180
  631.4 9.5 %collective-permute-start.49 = (bf16[2,64,2048]{2,1,0:T(8,128)(2,1)S(1)}, bf16[2,64,2048]{2,1,0:T(8,128)(2,1)S(1)}, u32[]{:S(2)}, u32[]{:S(2)}) collective-permute-start(bf16[2,64,2048]{2,1,0:T(8,128)(2,1)S(1)} %dynamic-slice_bitcast_fusion), channel_id=1, source_target_pairs={{0,8},{8,0},{16,24},{24,16},{1,9},{9,1},{17,25},{25,17},{2,10},{10... | collective-permute-start | bytes 1572872 | tf_op jit(solution)/shard_map/ppermute | solution.py:180
  634.0 30.6 %collective-permute-start.42 = (bf16[160,2048]{1,0:T(8,128)(2,1)}, bf16[160,2048]{1,0:T(8,128)(2,1)}, u32[]{:S(2)}, u32[]{:S(2)}) collective-permute-start(bf16[160,2048]{1,0:T(8,128)(2,1)} %pad_maximum_fusion.11), channel_id=1, source_target_pairs={{0,1},{2,0},{4,2},{6,4},{7,6},{5,7},{3,5},{1,3},{8,9},{10,8},{12,1... | collective-permute-start | bytes 1966088 | tf_op jit(solution)/shard_map/ppermute | solution.py:88
  636.7 23.2 %collective-permute-start.46 = (bf16[8,1,64,768]{3,2,0,1:T(8,128)(2,1)S(1)}, bf16[8,1,64,768]{3,2,0,1:T(8,128)(2,1)S(1)}, u32[]{:S(2)}, u32[]{:S(2)}) collective-permute-start(bf16[8,1,64,768]{3,2,0,1:T(8,128)(2,1)S(1)} %constant_dynamic-slice_fusion.1), channel_id=1, source_target_pairs={{0,16},{8,24},{16,0},{24,8},{1,17},{9,25},{17,1},{25,9},{2,18},{10... | collective-permute-start | bytes 2359304 | tf_op jit(solution)/shard_map/ppermute | solution.py:180
  639.4 25.2 %collective-permute-start.39 = (bf16[160,2048]{1,0:T(8,128)(2,1)}, bf16[160,2048]{1,0:T(8,128)(2,1)}, u32[]{:S(2)}, u32[]{:S(2)}) collective-permute-start(bf16[160,2048]{1,0:T(8,128)(2,1)} %pad_maximum_fusion.10), channel_id=1, source_target_pairs={{0,2},{2,4},{4,6},{6,7},{7,5},{5,3},{3,1},{1,0},{8,10},{10,12},{12... | collective-permute-start | bytes 1966088 | tf_op jit(solution)/shard_map/ppermute | solution.py:88
  641.1 29.1 %collective-permute-start.50 = (bf16[1,64,2048]{2,1,0:T(8,128)(2,1)S(1)}, bf16[1,64,2048]{2,1,0:T(8,128)(2,1)S(1)}, u32[]{:S(2)}, u32[]{:S(2)}) collective-permute-start(bf16[1,64,2048]{2,1,0:T(8,128)(2,1)S(1)} %constant_dynamic-slice_fusion), channel_id=1, source_target_pairs={{0,16},{8,24},{16,0},{24,8},{1,17},{9,25},{17,1},{25,9},{2,18},{10... | collective-permute-start | bytes 786440 | tf_op jit(solution)/shard_map/ppermute | solution.py:180
  661.0 24.0 %all-to-all-start.5 = ((bf16[8,64,768]{2,1,0:T(8,128)(2,1)}), bf16[8,64,768]{2,1,0:T(8,128)(2,1)S(1)}, u32[]{:S(2)}, u32[]{:S(2)}) async-start(bf16[8,64,768]{2,1,0:T(8,128)(2,1)} %fusion.23), calls=%async_computation.5 | async-start | bytes 1572864 | tf_op jit(solution)/shard_map/all_to_all | solution.py:223
  667.9 24.8 %collective-permute-start.40 = (bf16[160,2048]{1,0:T(8,128)(2,1)}, bf16[160,2048]{1,0:T(8,128)(2,1)}, u32[]{:S(2)}, u32[]{:S(2)}) collective-permute-start(bf16[160,2048]{1,0:T(8,128)(2,1)} %get-tuple-element.291), channel_id=1, source_target_pairs={{0,2},{2,4},{4,6},{6,7},{7,5},{5,3},{3,1},{1,0},{8,10},{10,12},{12... | collective-permute-start | bytes 1966088 | tf_op jit(solution)/shard_map/ppermute | solution.py:88
  669.9 24.2 %collective-permute-start.43 = (bf16[160,2048]{1,0:T(8,128)(2,1)}, bf16[160,2048]{1,0:T(8,128)(2,1)}, u32[]{:S(2)}, u32[]{:S(2)}) collective-permute-start(bf16[160,2048]{1,0:T(8,128)(2,1)} %get-tuple-element.292), channel_id=1, source_target_pairs={{0,1},{2,0},{4,2},{6,4},{7,6},{5,7},{3,5},{1,3},{8,9},{10,8},{12,1... | collective-permute-start | bytes 1966088 | tf_op jit(solution)/shard_map/ppermute | solution.py:88
  670.3 19.6 %collective-permute-start.51 = (bf16[1,64,2048]{2,1,0:T(8,128)(2,1)S(1)}, bf16[1,64,2048]{2,1,0:T(8,128)(2,1)S(1)}, u32[]{:S(2)}, u32[]{:S(2)}) collective-permute-start(bf16[1,64,2048]{2,1,0:T(8,128)(2,1)S(1)} %add_convert_fusion.19), channel_id=1, source_target_pairs={{0,16},{8,24},{16,0},{24,8},{1,17},{9,25},{17,1},{25,9},{2,18},{10... | collective-permute-start | bytes 786440 | tf_op jit(solution)/shard_map/ppermute | solution.py:180
  675.9 47.7 %collective-permute-start.35 = (bf16[160,2048]{1,0:T(8,128)(2,1)}, bf16[160,2048]{1,0:T(8,128)(2,1)S(1)}, u32[]{:S(2)}, u32[]{:S(2)}) collective-permute-start(bf16[160,2048]{1,0:T(8,128)(2,1)} %get-tuple-element.299), channel_id=1, source_target_pairs={{0,2},{2,4},{4,6},{6,7},{7,5},{5,3},{3,1},{1,0},{8,10},{10,12},{12... | collective-permute-start | bytes 1966088 | tf_op jit(solution)/shard_map/ppermute | solution.py:88
  686.3 35.0 %collective-permute-start.47 = (bf16[1,3,64,2048]{3,2,1,0:T(8,128)(2,1)S(1)}, bf16[1,3,64,2048]{3,2,1,0:T(8,128)(2,1)S(1)}, u32[]{:S(2)}, u32[]{:S(2)}) collective-permute-start(bf16[1,3,64,2048]{3,2,1,0:T(8,128)(2,1)S(1)} %broadcast_in_dim_reshape.2), channel_id=1, source_target_pairs={{0,16},{8,24},{16,0},{24,8},{1,17},{9,25},{17,1},{25,9},{2,18},{10... | collective-permute-start | bytes 2359304 | tf_op jit(solution)/shard_map/ppermute | solution.py:180
  689.9 33.7 %collective-permute-start.36 = (bf16[160,2048]{1,0:T(8,128)(2,1)}, bf16[160,2048]{1,0:T(8,128)(2,1)S(1)}, u32[]{:S(2)}, u32[]{:S(2)}) collective-permute-start(bf16[160,2048]{1,0:T(8,128)(2,1)} %get-tuple-element.300), channel_id=1, source_target_pairs={{0,1},{2,0},{4,2},{6,4},{7,6},{5,7},{3,5},{1,3},{8,9},{10,8},{12,1... | collective-permute-start | bytes 1966088 | tf_op jit(solution)/shard_map/ppermute | solution.py:88
  692.7 33.3 %collective-permute-start.52 = (bf16[2,64,2048]{2,1,0:T(8,128)(2,1)S(1)}, bf16[2,64,2048]{2,1,0:T(8,128)(2,1)S(1)}, u32[]{:S(2)}, u32[]{:S(2)}) collective-permute-start(bf16[2,64,2048]{2,1,0:T(8,128)(2,1)S(1)} %maximum_select_fusion.8), channel_id=1, source_target_pairs={{0,8},{8,0},{16,24},{24,16},{1,9},{9,1},{17,25},{25,17},{2,10},{10... | collective-permute-start | bytes 1572872 | tf_op jit(solution)/shard_map/ppermute | solution.py:180
  696.2 31.5 %collective-permute-start.41 = (bf16[160,2048]{1,0:T(8,128)(2,1)S(1)}, bf16[160,2048]{1,0:T(8,128)(2,1)S(1)}, u32[]{:S(2)}, u32[]{:S(2)}) collective-permute-start(bf16[160,2048]{1,0:T(8,128)(2,1)S(1)} %get-tuple-element.289), channel_id=1, source_target_pairs={{0,2},{2,4},{4,6},{6,7},{7,5},{5,3},{3,1},{1,0},{8,10},{10,12},{12... | collective-permute-start | bytes 1966088 | tf_op jit(solution)/shard_map/ppermute | solution.py:88
  721.3 10.6 %collective-permute-start.44 = (bf16[160,2048]{1,0:T(8,128)(2,1)S(1)}, bf16[160,2048]{1,0:T(8,128)(2,1)S(1)}, u32[]{:S(2)}, u32[]{:S(2)}) collective-permute-start(bf16[160,2048]{1,0:T(8,128)(2,1)S(1)} %get-tuple-element.290), channel_id=1, source_target_pairs={{0,1},{2,0},{4,2},{6,4},{7,6},{5,7},{3,5},{1,3},{8,9},{10,8},{12,1... | collective-permute-start | bytes 1966088 | tf_op jit(solution)/shard_map/ppermute | solution.py:88
  723.6 11.7 %collective-permute-start.48 = (bf16[2,3,64,2048]{3,2,1,0:T(8,128)(2,1)}, bf16[2,3,64,2048]{3,2,1,0:T(8,128)(2,1)}, u32[]{:S(2)}, u32[]{:S(2)}) collective-permute-start(bf16[2,3,64,2048]{3,2,1,0:T(8,128)(2,1)} %maximum_select_fusion.5), channel_id=1, source_target_pairs={{0,8},{8,0},{16,24},{24,16},{1,9},{9,1},{17,25},{25,17},{2,10},{10... | collective-permute-start | bytes 4718600 | tf_op jit(solution)/shard_map/ppermute | solution.py:180
  (145 other events, 1467.4 us)
Sparse Core Ops, SparseCore 0:
  24.5 67.5 all-gather.3
  124.3 97.7 all-gather.5
  437.4 113.7 all-gather.7
  553.6 73.3 reduce-scatter.7
  629.6 101.3 reduce-scatter.3
  733.4 69.9 reduce-scatter.5

commit v5 on v4

--- a/solution.py
+++ b/solution.py
@@ -1,5 +1,3 @@
-import functools
-
 import jax
 import jax.numpy as jnp
 from jax import lax
@@ -119,36 +117,51 @@
     return blocks + [jnp.concatenate([onward, backward], axis=0)], results
 
 
-def ring_scatter(block, rows, fills=()):
-    count = lax.axis_size("ep")
-    half = count // 2
-    middle = rows // 2
-    fills = dict(fills)
-    slot = {offset: j for j, offset in enumerate(ring_slots(count))}
-    results = {}
-    far = block(slot[half], results)
-    onward, backward = far[:middle], far[middle:]
-    for step in range(1, half + 1):
-        sent = (onward, backward)
-        received = (ring_shift(onward, 1), ring_shift(backward, -1))
-        fill = fills[step](results) if step in fills else None
-        (onward, backward), results[step] = fill_window(fill, sent, received)
-        left = half - step
+class RingSum:
+    def __init__(self, block, rows):
+        count = lax.axis_size("ep")
+        self.block, self.middle, self.step = block, rows // 2, 0
+        self.half = count // 2
+        self.slot = {offset: j for j, offset in enumerate(ring_slots(count))}
+        far = block(self.slot[self.half])
+        self.sent = (far[: self.middle], far[self.middle :])
+
+    def start(self):
+        self.received = (ring_shift(self.sent[0], 1), ring_shift(self.sent[1], -1))
+
+    def finish(self):
+        self.step += 1
+        onward, backward = self.received
+        left = self.half - self.step
+        middle = self.middle
         if left:
-            up, down = block(slot[left], results), block(slot[-left], results)
-            if step == 1:
+            up, down = self.block(self.slot[left]), self.block(self.slot[-left])
+            if self.step == 1:
                 onward = jnp.concatenate([add_low(onward, up[:middle]), up[middle:]], axis=0)
                 backward = jnp.concatenate(
                     [down[:middle], add_low(backward, down[middle:])], axis=0
                 )
             else:
                 onward, backward = add_low(onward, up), add_low(backward, down)
-    total = (
-        block(slot[0], results).astype(wide_type)
-        + onward.astype(wide_type)
-        + backward.astype(wide_type)
-    )
-    return total, results
+        self.sent = (onward, backward)
+
+    def total(self):
+        return (
+            self.block(self.slot[0]).astype(wide_type)
+            + self.sent[0].astype(wide_type)
+            + self.sent[1].astype(wide_type)
+        )
+
+
+def window(rings, work, *inputs):
+    for ring in rings:
+        ring.start()
+    inputs, _ = tie(inputs, [ring.sent for ring in rings])
+    received, results = tie([ring.received for ring in rings], work(*inputs))
+    for ring, pair in zip(rings, received):
+        ring.received = pair
+        ring.finish()
+    return results
 
 
 def add_low(left, right):
@@ -403,17 +416,24 @@
     )
     token_all = jnp.concatenate(ring_gather(tokens)[0], axis=0)
     column_share = model_width // replica_count
-    output_share = gather_rows(
-        lax.dynamic_slice_in_dim(output_weight, replica * column_share, column_share, 1)
-    )
+    halves = 2 if column_share % 256 == 0 else 1
+    piece_width = column_share // halves
+    token_all, output_own = tie(token_all, output_weight)
+    output_shares = [
+        gather_rows(
+            lax.dynamic_slice_in_dim(
+                output_own, replica * column_share + half * piece_width, piece_width, 1
+            )
+        )
+        for half in range(halves)
+    ]
 
     def reorder_rows(rows, index):
         return reorder(
             rows.reshape(group_count, row_count, rows.shape[1]), index
         ).reshape(rows.shape)
 
-    token_late, cot_own = lax.optimization_barrier((token_all, cotangent))
-    token_all = token_late
+    output_shares[-1], cot_own = tie(output_shares[-1], cotangent)
     cot_ordered = gather_rows(cot_own)
     cot_all = reorder_rows(cot_ordered, device_of_slot)
 
@@ -458,23 +478,30 @@
     mixed_low = jnp.concatenate(mixed_parts, axis=1)
 
     mixed_ordered = reorder_rows(mixed_low, slot_of_device)
-    output_pieces = {0: output_share}
+    output_pieces = {(0, half): output_shares[half] for half in range(halves)}
     distance = replica_count // 2
     while distance:
-        for j in list(output_pieces):
-            output_pieces[j ^ distance] = rep_exchange(output_pieces[j], distance)
+        for j, half in list(output_pieces):
+            output_pieces[j ^ distance, half] = rep_exchange(output_pieces[j, half], distance)
         if distance == replica_count // 2:
-            output_pieces[distance], mixed_ordered = tie(output_pieces[distance], mixed_ordered)
+            for half in range(halves):
+                output_pieces[distance, half], mixed_ordered = tie(
+                    output_pieces[distance, half], mixed_ordered
+                )
         distance //= 2
+
+    def piece_start(j, half):
+        return (replica ^ j) * column_share + half * piece_width
+
     mixed_own = (
         swap_all(mixed_ordered.reshape(group_count, row_count, width_here))
         .transpose(1, 0, 2)
         .reshape(row_count, model_width)
     )
     attention = jnp.zeros((row_count, model_width), wide_type)
-    for j, piece in output_pieces.items():
+    for place, piece in output_pieces.items():
         attention = lax.dynamic_update_slice_in_dim(
-            attention, mm(mixed_own, piece, 1, 0), (replica ^ j) * column_share, 1
+            attention, mm(mixed_own, piece, 1, 0), piece_start(*place), 1
         )
     residual = tokens.astype(wide_type) + attention
     inverse_two = inverse_rms(residual)
@@ -528,17 +555,14 @@
     second_all = jnp.concatenate([rows_first, rows_last], axis=0)
     back_last = expert_back(gback_all, uback_all, gate_weight, up_weight, 1, chunks)
 
-    def back_first(results):
-        return (
-            lambda gback, uback: (
-                expert_back(gback, uback, gate_weight, up_weight, 0, chunks),
-            )
-        ), (gback_all, uback_all)
-
-    def back_block(slot, results):
-        part = back_last if slot >= blocks_here else results[1][0]
+    back_parts = {1: back_last}
+
+    def back_block(slot):
         start = (slot % blocks_here) * row_count
-        return part[start : start + row_count]
+        return back_parts[slot // blocks_here][start : start + row_count]
+
+    def grad_of(left, right):
+        return mm(left, right, 0, 0).astype(low_type)
 
     pair_lanes = jnp.concatenate([pair_first, pair_last], axis=1)
     pair_sent = (kept_here * jnp.sum(pair_lanes, axis=2).transpose(1, 0)).reshape(
@@ -547,66 +571,76 @@
     code_own = route_code
     gates_own = gate_table(second_input, code_own)
 
-    def grad_of(left, right):
-        return mm(left, right, 0, 0).astype(low_type)
-
-    def down_fill(results):
+    second_ring = RingSum(back_block, row_count)
+    second_ring.start()
+    (gback_tied, uback_tied), _ = tie((gback_all, uback_all), second_ring.sent)
+    second_ring.received, back_parts[0] = tie(
+        second_ring.received,
+        expert_back(gback_tied, uback_tied, gate_weight, up_weight, 0, chunks),
+    )
+    second_ring.finish()
+
+    def mixture_work(inner, pair):
         return (
-            lambda inner, pair: (grad_of(inner, cot_all), swap_all(reorder(pair, slot_of_device)))
-        ), (inner_all, pair_sent)
-
-    def gate_fill(results):
-        def work(gback, pair):
-            pair_grad = pair.transpose(1, 0, 2).reshape(row_count, expert_total)
-            chosen_grad = gates_own * (
-                pair_grad - jnp.sum(gates_own * pair_grad, axis=1, keepdims=True)
-            )
-            logits_grad = jnp.where(code_own > 0, chosen_grad, 0.0).astype(low_type)
-            router_back = mm(logits_grad, full_router, 1, 1)
-            return grad_of(second_all, gback), logits_grad, router_back
-
-        return work, (gback_all, results[2][1])
-
-    def up_fill(results):
-        return (lambda uback: (grad_of(second_all, uback),)), (uback_all,)
-
-    second_scattered, results = ring_scatter(
-        back_block, row_count, {1: back_first, 2: down_fill, 3: gate_fill, 4: up_fill}
-    )
-    down_part = results[2][0]
-    gate_part, logits_grad, router_back = results[3]
-    up_part = results[4][0]
-    router_part = mm(second_input, logits_grad, 0, 0)
+            mm(inner, flat_down, 1, 0).astype(low_type),
+            swap_all(reorder(pair, slot_of_device)),
+        )
+
+    mixture_part, pair_grad = window([second_ring], mixture_work, inner_all, pair_sent)
+    mixture_ring = RingSum(
+        lambda slot: mixture_part[slot * row_count : (slot + 1) * row_count], row_count
+    )
+
+    def down_work(inner, pair):
+        pair_grad = pair.transpose(1, 0, 2).reshape(row_count, expert_total)
+        chosen_grad = gates_own * (
+            pair_grad - jnp.sum(gates_own * pair_grad, axis=1, keepdims=True)
+        )
+        logits_grad = jnp.where(code_own > 0, chosen_grad, 0.0).astype(low_type)
+        router_back = mm(logits_grad, full_router, 1, 1)
+        router_part = mm(second_input, logits_grad, 0, 0)
+        return grad_of(inner, cot_all), router_back, router_part
+
+    down_part, router_back, router_part = window(
+        [second_ring, mixture_ring], down_work, inner_all, pair_grad
+    )
+    gate_part = window(
+        [second_ring, mixture_ring], lambda gback: grad_of(second_all, gback), gback_all
+    )
+    second_scattered = second_ring.total()
     second_grad = router_back + second_scattered
     upstream = valid_own * cotangent.astype(wide_type)
-    post_back, postnorm_part = norm_backward(residual, inverse_two, postnorm_gain, second_grad)
-    residual_grad = upstream + post_back
-    attention_low = residual_grad.astype(low_type)
+    def residual_work(second_grad):
+        post_back, postnorm_part = norm_backward(
+            residual, inverse_two, postnorm_gain, second_grad
+        )
+        residual_grad = upstream + post_back
+        attention_low = residual_grad.astype(low_type)
+        mixed_grad_own = jnp.zeros((row_count, model_width), wide_type)
+        for place, piece in output_pieces.items():
+            mixed_grad_own = mixed_grad_own + mm(
+                lax.dynamic_slice_in_dim(attention_low, piece_start(*place), piece_width, 1),
+                piece,
+                1,
+                1,
+            )
+        swap_sent = (
+            mixed_grad_own.astype(low_type)
+            .reshape(row_count, group_count, width_here)
+            .transpose(1, 0, 2)
+        )
+        return swap_sent, residual_grad, attention_low, jnp.sum(postnorm_part, axis=0)
+
+    swap_sent, residual_grad, attention_low, postnorm_part = window(
+        [mixture_ring], residual_work, second_grad
+    )
     attention_all = gather_rows(attention_low)
-    mixed_grad_own = jnp.zeros((row_count, model_width), wide_type)
-    for j, piece in output_pieces.items():
-        mixed_grad_own = mixed_grad_own + mm(
-            lax.dynamic_slice_in_dim(
-                attention_low, (replica ^ j) * column_share, column_share, 1
-            ),
-            piece,
-            1,
-            1,
-        )
-    swap_sent = (
-        mixed_grad_own.astype(low_type)
-        .reshape(row_count, group_count, width_here)
-        .transpose(1, 0, 2)
-    )
-    mixed_swapped, (mixture_part,) = fill_window(
-        ((lambda inner: (mm(inner, flat_down, 1, 0).astype(low_type),)), (inner_all,)),
-        swap_sent,
-        swap_all(swap_sent),
-    )
+    mixed_swapped = swap_all(swap_sent)
+    up_part = window([mixture_ring], lambda uback: grad_of(second_all, uback), uback_all)
+    mixture = mixture_ring.total()
+    layer_out = (valid_own * (residual + mixture)).astype(low_type)
+    mixed_swapped, up_part = tie(mixed_swapped, up_part)
     mixed_grad = reorder_rows(mixed_swapped.reshape(group_rows, width_here), device_of_slot)
-
-    def mixture_block(slot, results):
-        return mixture_part[slot * row_count : (slot + 1) * row_count]
 
     def head_backward(head, grad_head):
         (query_raw, key_raw, query_inverse, key_inverse, query_low, key_low, value_low, log_total) = (
@@ -636,69 +670,33 @@
             jnp.sum(key_gain_part, axis=0),
         )
 
-    def head_fill(head):
-        def fill(results):
-            start = head * head_dim
-            return functools.partial(head_backward, head), (
-                mixed_grad[:, start : start + head_dim],
-            )
-
-        return fill
-
-    mixture, results = ring_scatter(
-        mixture_block, row_count, {2 + head: head_fill(head) for head in range(heads_here)}
-    )
-    layer_out = (valid_own * (residual + mixture)).astype(low_type)
-    head_results = [results[2 + head] for head in range(heads_here)]
+    head_results = [
+        head_backward(head, mixed_grad[:, head * head_dim : (head + 1) * head_dim])
+        for head in range(heads_here)
+    ]
     sent = jnp.concatenate(
         [head_results[head][part] for part in range(3) for head in range(heads_here)], axis=1
     )
+    down_sum = lax.psum_scatter(
+        down_part.reshape(experts_here, hidden_here, model_width),
+        "rep",
+        scatter_dimension=1,
+        tiled=True,
+    )
+    sent, down_sum = tie(sent, down_sum)
     querynorm_part = sum(result[3] for result in head_results)
     keynorm_part = sum(result[4] for result in head_results)
     first_part = mm(sent, head_weight, 1, 1)
     prenorm_part = jnp.sum(first_part * token_wide * inverse_all, axis=0)
     first_low = first_part.astype(low_type)
 
-    def product_fill(results):
-        return (
-            lambda first, sent, mixed, attention: (grad_of(first, sent), grad_of(mixed, attention))
-        ), (first_all, sent, mixed_ordered, attention_all)
-
-    first_grad, results = ring_scatter(
-        lambda slot, results: first_low[slot * row_count : (slot + 1) * row_count],
-        row_count,
-        {1: product_fill},
-    )
-    head_part, output_part = results[1]
-    head_rows = swap_all(
-        rep_scatter(head_part.reshape(group_count, replica_count, share, 3 * width_here), 1)
-    )
-    head_rows = rep_gather(
-        head_rows.reshape(group_count, share, 3, width_here)
-        .transpose(2, 1, 0, 3)
-        .reshape(3, share, model_width)
-    )
-    query_grad, key_grad, value_grad = (
-        head_rows[:, block].reshape(width_here, model_width).astype(wide_type)
-        for block in range(3)
-    )
-    output_grad = (
-        rep_gather(rep_scatter(output_part.reshape(replica_count, share, model_width), 0))
-        .reshape(width_here, model_width)
-        .astype(wide_type)
-    )
-
-    first_grad, query_grad, key_grad, value_grad, output_grad = tie(
-        first_grad, query_grad, key_grad, value_grad, output_grad
-    )
-    token_own = tokens.astype(wide_type)
-    inverse_one = inverse_rms(token_own)
-    pre_back, _ = norm_backward(token_own, inverse_one, prenorm_gain, first_grad)
-    token_grad = residual_grad + pre_back
-
-    def small_sum(parts):
-        flat = jnp.concatenate([part.reshape(group_count, -1) for part in parts], axis=1)
-        total = rep_sum(jnp.sum(swap_all(flat), axis=0))
+    def small_swap(parts):
+        return swap_all(
+            jnp.concatenate([part.reshape(group_count, -1) for part in parts], axis=1)
+        )
+
+    def small_pieces(swapped, parts):
+        total = rep_sum(jnp.sum(swapped, axis=0))
         pieces, start = [], 0
         for part in parts:
             size = part.size // group_count
@@ -706,18 +704,69 @@
             start += size
         return pieces
 
-    router_grad, postnorm_grad = small_sum([router_part, jnp.sum(postnorm_part, axis=0)])
+    first_ring = RingSum(
+        lambda slot: first_low[slot * row_count : (slot + 1) * row_count], row_count
+    )
+    head_part, output_part = window(
+        [first_ring],
+        lambda first, sent, mixed, attention: (grad_of(first, sent), grad_of(mixed, attention)),
+        first_all,
+        sent,
+        mixed_ordered,
+        attention_all,
+    )
+    small_parts = [router_part, postnorm_part, prenorm_part, querynorm_part, keynorm_part]
+    head_rows, output_rows, small_swapped = window(
+        [first_ring],
+        lambda head, output, *small: (
+            rep_scatter(head, 1),
+            rep_scatter(output, 0),
+            small_swap(small),
+        ),
+        head_part.reshape(group_count, replica_count, share, 3 * width_here),
+        output_part.reshape(replica_count, share, model_width),
+        *small_parts,
+    )
+    head_rows, output_rows, small_sums = window(
+        [first_ring],
+        lambda head, output, small: (
+            swap_all(head)
+            .reshape(group_count, share, 3, width_here)
+            .transpose(2, 1, 0, 3)
+            .reshape(3, share, model_width),
+            rep_gather(output),
+            small_pieces(small, small_parts),
+        ),
+        head_rows,
+        output_rows,
+        small_swapped,
+    )
+    gate_sum = lax.psum_scatter(gate_part, "rep", scatter_dimension=0, tiled=True)
+    head_rows, gate_sum = tie(head_rows, gate_sum)
+    up_sum = lax.psum_scatter(up_part, "rep", scatter_dimension=0, tiled=True)
+    head_rows, output_grad = window(
+        [first_ring],
+        lambda head, output: (
+            rep_gather(head),
+            output.reshape(width_here, model_width).astype(wide_type),
+        ),
+        head_rows,
+        output_rows,
+    )
+    first_grad = first_ring.total()
+    query_grad, key_grad, value_grad = (
+        head_rows[:, block].reshape(width_here, model_width).astype(wide_type)
+        for block in range(3)
+    )
+    router_grad, postnorm_grad, prenorm_grad, querynorm_grad, keynorm_grad = small_sums
     router_grad = router_grad.reshape(width_here, expert_total)
-    prenorm_grad, querynorm_grad, keynorm_grad = small_sum(
-        [prenorm_part, querynorm_part, keynorm_part]
-    )
-
-    down_total = lax.psum_scatter(
-        down_part.reshape(experts_here, hidden_here, model_width),
-        "rep",
-        scatter_dimension=1,
-        tiled=True,
-    ).astype(wide_type)
+
+    token_own = tokens.astype(wide_type)
+    inverse_one = inverse_rms(token_own)
+    pre_back, _ = norm_backward(token_own, inverse_one, prenorm_gain, first_grad)
+    token_grad = residual_grad + pre_back
+
+    down_total = down_sum.astype(wide_type)
     gate_total, up_total = (
         jnp.stack(
             [
@@ -725,10 +774,7 @@
                 for e in range(experts_here)
             ]
         )
-        for total in (
-            lax.psum_scatter(part, "rep", scatter_dimension=0, tiled=True)
-            for part in (gate_part, up_part)
-        )
+        for total in (gate_sum, up_sum)
     )
     return (
         layer_out,

time: 825 us -> 851 us (1.032)
  waiting for transfers between devices: 269 us -> 296 us
  matrix products: 147 us -> 173 us
  blocking collectives: 20.2 us -> 0 us
  starting transfers between devices: 102 us -> 90 us
  other arithmetic: 110 us -> 120 us
    all_gather x3 -> x4, waiting for transfers between devices: 0.01 us -> 62.4 us  [gather_rows(): return lax.all_gather(values, 'ep', axis=0, tiled=True)]
    ppermute x40, waiting for transfers between devices: 106 us -> 49.8 us  [ring_shift(): return lax.ppermute(values, 'ep', pairs)]
    ppermute x17 -> x18, waiting for transfers between devices: 60.5 us -> 93.3 us  [rep_exchange(): lax.ppermute(values, 'rep', [(i, i ^ distance) for i in range(count)])]
    dot_general x35 -> x43, matrix products: 147 us -> 173 us  [mm(): lax.dot_general(left, right, (((left_dim,), (right_dim,)), ((), ())), pre...]
    all_to_all x2 -> x0, blocking collectives: 20.2 us -> none  [swap_all(): return lax.all_to_all(values, 'ep', split_axis=0, concat_axis=0, tiled=True)]
    reduce_scatter x2, waiting for transfers between devices: 50 us -> 36.3 us  [the longest x1 36.3 us: body(): up_sum = lax.psum_scatter(up_part, 'rep', scatter_dimension=0, tiled=True)]
    ppermute x40, starting transfers between devices: 59.4 us -> 45.7 us  [ring_shift(): return lax.ppermute(values, 'ep', pairs)]
    unnamed x330 -> x308, local copies, waits for them, and re-layouts: 37.5 us -> 31.3 us
  transfers between devices with their start and end apart: 69 -> 72, of which waited for: 23 -> 28; matrix products, arithmetic and copies ran while one was open for 36% -> 39% of each run, Pallas kernels for 4% -> 4%
where the time goes in v5:
time: 851 us; the launch traced here: 841 us
  waiting for transfers between devices  296 us (35%)
  matrix products  173 us (20%)
  other arithmetic  120 us (14%)
  starting transfers between devices  90 us (11%)
  Pallas kernels  72.7 us (9%)
  local copies, waits for them, and re-layouts  72.3 us (8%)
  between operations  17.2 us (2%)
    dot_general x43, matrix products, mm(): lax.dot_general(left, right, (((left_dim,), (right_dim,)), ((), ())), pre...  173 us
    ppermute x18, waiting for transfers between devices, rep_exchange(): lax.ppermute(values, 'rep', [(i, i ^ distance) for i in range(count)])  93.3 us
    all_gather x4, waiting for transfers between devices, gather_rows(): return lax.all_gather(values, 'ep', axis=0, tiled=True)  62.4 us
    all_to_all x7, waiting for transfers between devices, swap_all(): return lax.all_to_all(values, 'ep', split_axis=0, concat_axis=0, tiled=True)  53.6 us
    ppermute x40, waiting for transfers between devices, ring_shift(): return lax.ppermute(values, 'ep', pairs)  49.8 us
    ppermute x40, starting transfers between devices, ring_shift(): return lax.ppermute(values, 'ep', pairs)  45.7 us
    pallas_call x2, Pallas kernels, expert_pass(): pl.pallas_call(expert_kernel, grid=(experts, steps), in_specs=[pl.BlockSp...  39 us
    reduce_scatter x1, waiting for transfers between devices, body(): up_sum = lax.psum_scatter(up_part, 'rep', scatter_dimension=0, tiled=True)  36.3 us
  transfers between devices with their start and end apart: 72, of which 28 were waited for; matrix products, arithmetic and copies ran while one was open for 39% of the time, Pallas kernels for 4%

profile of v5, /device:TPU:0, one launch (start us, length us, event | category | flops | bytes accessed | tf_op | source)
XLA Modules:
  0.0 840.8 jit_solution(5648920754675378360)
XLA Ops:
  7.2 3.0 collective-permute-start
  14.2 6.2 all-to-all-start.2
  31.1 10.9 %collective-permute-done.2 = bf16[160,2048]{1,0:T(8,128)(2,1)S(1)} collective-permute-done((bf16[160,2048]{1,0:T(8,128)(2,1)S(1)}, bf16[160,2048]{1,0:T(8,128)(2,1)S(1)}, u32[]{:S(2)}, u32[]{:S(2)}) %collective-permute-start.2) | collective-permute-done | bytes 655392 | tf_op jit(solution)/shard_map/ppermute | solution.py:86
  47.9 10.0 %collective-permute-done.5 = bf16[160,2048]{1,0:T(8,128)(2,1)S(1)} collective-permute-done((bf16[160,2048]{1,0:T(8,128)(2,1)S(1)}, bf16[160,2048]{1,0:T(8,128)(2,1)S(1)}, u32[]{:S(2)}, u32[]{:S(2)}) %collective-permute-start.5) | collective-permute-done | bytes 655392 | tf_op jit(solution)/shard_map/ppermute | solution.py:86
  61.4 4.8 all-to-all-start
  75.9 9.6 %all-to-all-done = bf16[8,64,768]{2,1,0:T(8,128)(2,1)S(1)} async-done(((bf16[8,64,768]{2,1,0:T(8,128)(2,1)}), bf16[8,64,768]{2,1,0:T(8,128)(2,1)S(1)}, u32[]{:S(2)}, u32[]{:S(2)}) %all-to-all-start) | async-done | bytes 786464 | tf_op jit(solution)/shard_map/all_to_all | solution.py:236
  89.9 12.3 %collective-permute-done.10 = bf16[1,8,64,768]{3,2,1,0:T(8,128)(2,1)S(1)} collective-permute-done((bf16[1,8,64,768]{3,2,1,0:T(8,128)(2,1)S(1)}, bf16[1,8,64,768]{3,2,1,0:T(8,128)(2,1)S(1)}, u32[]{:S(2)}, u32[]{:S(2)}) %collective-permute-start.10) | collective-permute-done | bytes 786464 | tf_op jit(solution)/shard_map/ppermute | solution.py:193
  105.3 3.6 fusion
  109.0 3.7 fusion.2
  112.8 4.3 maximum_select_fusion
  117.3 5.6 fusion.126
  134.8 2.5 convolution_convert_fusion.7
  137.3 2.7 convolution_convert_fusion.6
  141.7 19.3 %all-gather.7.cloned.1.call-done = bf16[2048,256]{1,0:T(8,128)(2,1)} async-done(((bf16[256,256]{1,0:T(8,128)(2,1)}), bf16[2048,256]{1,0:T(8,128)(2,1)}) %all-gather.7.cloned.1.call-update) | async-done | bytes 1048592 | tf_op jit(solution)/shard_map/all_gather | solution.py:67
  162.9 25.4 %collective-permute-done.9 = bf16[2048,256]{1,0:T(8,128)(2,1)S(1)} collective-permute-done((bf16[2048,256]{1,0:T(8,128)(2,1)}, bf16[2048,256]{1,0:T(8,128)(2,1)S(1)}, u32[]{:S(2)}, u32[]{:S(2)}) %collective-permute-start.9) | collective-permute-done | bytes 1048608 | tf_op jit(solution)/shard_map/ppermute | solution.py:193
  188.3 4.0 all-to-all-start.1
  194.7 26.1 %all-to-all-done.1 = bf16[8,160,256]{2,1,0:T(8,128)(2,1)S(1)} async-done(((bf16[8,160,256]{2,1,0:T(8,128)(2,1)}), bf16[8,160,256]{2,1,0:T(8,128)(2,1)S(1)}, u32[]{:S(2)}, u32[]{:S(2)}) %all-to-all-start.1) | async-done | bytes 655392 | tf_op jit(solution)/shard_map/all_to_all | solution.py:236
  239.7 20.6 %all-gather.9.cloned.1.call-done = bf16[1280,2048]{1,0:T(8,128)(2,1)} async-done(((bf16[160,2048]{1,0:T(8,128)(2,1)}), bf16[1280,2048]{1,0:T(8,128)(2,1)}) %all-gather.9.cloned.1.call-update) | async-done | bytes 5242896 | tf_op jit(solution)/shard_map/all_gather | solution.py:67
  265.2 9.5 %fusion.133.stream_ref = f32[640,2048]{1,0:T(8,128)} fusion(bf16[640,2048]{1,0:T(8,128)(2,1)S(1)} %bitcast.243, bf16[2048,2048]{1,0:T(8,128)(2,1)} %bitcast.334), kind=kOutput, calls=%fused_computation.418 | convolution fusion | flops 5368709120 | bytes 16252928 | tf_op jit(solution)/shard_map/dot_general | solution.py:58
  278.3 9.5 %fusion.134.stream_ref = f32[640,2048]{1,0:T(8,128)} fusion(bf16[640,2048]{1,0:T(8,128)(2,1)S(1)} %bitcast.244, bf16[2048,2048]{1,0:T(8,128)(2,1)} %bitcast.335), kind=kOutput, calls=%fused_computation.419 | convolution fusion | flops 5368709120 | bytes 16252928 | tf_op jit(solution)/shard_map/dot_general | solution.py:58
  287.8 5.2 collective-permute-done.18
  298.7 19.6 %shard_map.281 = (bf16[1280,2048]{1,0:T(8,128)(2,1)}, bf16[1280,2048]{1,0:T(8,128)(2,1)}, bf16[1280,2048]{1,0:T(8,128)(2,1)}, f32[2,640,128]{2,1,0:T(8,128)}) custom-call(bf16[640,2048]{1,0:T(8,128)(2,1)} %copy-done.9, bf16[2,2048,1024]{2,1,0:T(8,128)(2,1)} %gate_ref.7, bf16[2,2048,1024]{2,1,0:T(8,128)(2,1)} %up_ref.7, f32[640,2048]{1,0:T(8,128)} %fusion.133.stream_ref, ...), custom_call_target="tpu_custom_call" | custom-call | flops 10737418240 | bytes 42991616 | tf_op jit(solution)/shard_map/pallas_call | solution.py:280
  322.2 6.2 collective-permute-done.22
  333.5 19.4 %shard_map.282 = (bf16[1280,2048]{1,0:T(8,128)(2,1)}, bf16[1280,2048]{1,0:T(8,128)(2,1)}, bf16[1280,2048]{1,0:T(8,128)(2,1)}, f32[2,640,128]{2,1,0:T(8,128)}) custom-call(bf16[640,2048]{1,0:T(8,128)(2,1)} %copy-done.27, bf16[2,2048,1024]{2,1,0:T(8,128)(2,1)} %gate_ref.7, ...), custom_call_target="tpu_custom_call", output_to_operand_aliasing={{0}: (5, {}), {1}: (6, {}), {2}: (7, {})} | custom-call | flops 10737418240 | bytes 42991616 | tf_op jit(solution)/shard_map/pallas_call | solution.py:280
  352.9 16.8 %shard_map.283 = bf16[640,2048]{1,0:T(8,128)(2,1)} custom-call(bf16[1280,2048]{1,0:T(8,128)(2,1)} %get-tuple-element.178.gback_ref, bf16[1280,2048]{1,0:T(8,128)(2,1)} %get-tuple-element.187.uback_ref, bf16[2,2048,1024]{2,1,0:T(8,128)(2,1)} %gate_ref.7, bf16[2,2048,1024]{2,1,0:T(8,128)(2,1)} %up_ref.7), custom_call_target="tpu_custom_call" | custom-call | flops 10737418240 | bytes 24641536 | tf_op jit(solution)/shard_map/pallas_call | solution.py:320
  374.8 16.9 %shard_map.284 = bf16[640,2048]{1,0:T(8,128)(2,1)} custom-call(bf16[1280,2048]{1,0:T(8,128)(2,1)} %get-tuple-element.178.gback_ref, bf16[1280,2048]{1,0:T(8,128)(2,1)} %get-tuple-element.187.uback_ref, bf16[2,2048,1024]{2,1,0:T(8,128)(2,1)} %gate_ref.7, bf16[2,2048,1024]{2,1,0:T(8,128)(2,1)} %up_ref.7), custom_call_target="tpu_custom_call" | custom-call | flops 10737418240 | bytes 24641536 | tf_op jit(solution)/shard_map/pallas_call | solution.py:320
  397.4 4.4 all-to-all-start.3
  402.3 16.5 %convolution_convert_fusion.3 = bf16[1280,2048]{1,0:T(8,128)(2,1)} fusion(bf16[1280,2048]{1,0:T(8,128)(2,1)} %get-tuple-element.171, bf16[2048,2048]{1,0:T(8,128)(2,1)} %bitcast.336), kind=kOutput, calls=%fused_computation.15 | convolution fusion | flops 10740039680 | bytes 18874368 | tf_op jit(solution)/shard_map/dot_general | solution.py:58
  428.6 16.7 %convolution_convert_fusion.2 = bf16[2048,2048]{1,0:T(8,128)(2,1)} fusion(bf16[1280,2048]{1,0:T(8,128)(2,1)} %get-tuple-element.171, bf16[1280,2048]{1,0:T(8,128)(2,1)} %bitcast.263), kind=kOutput, calls=%fused_computation.14 | convolution fusion | flops 10741612544 | bytes 18874368 | tf_op jit(solution)/shard_map/dot_general | solution.py:58
  457.3 2.8 add_convert_fusion.9
  462.1 16.8 %convolution_convert_fusion.1 = bf16[2048,2048]{1,0:T(8,128)(2,1)} fusion(bf16[1280,2048]{1,0:T(8,128)(2,1)} %copy-done.50, bf16[1280,2048]{1,0:T(8,128)(2,1)S(1)} %bitcast.209), kind=kOutput, calls=%fused_computation.13 | convolution fusion | flops 10741612544 | bytes 18874368 | tf_op jit(solution)/shard_map/dot_general | solution.py:58
  478.9 3.7 collective-permute-done.32
  482.6 3.3 add_convert_fusion.7
  506.7 3.3 add_convert_fusion.5
  512.1 4.4 all-to-all-start.4
  516.6 17.1 %convolution_convert_fusion = bf16[2048,2048]{1,0:T(8,128)(2,1)} fusion(bf16[1280,2048]{1,0:T(8,128)(2,1)} %copy-done.50, bf16[1280,2048]{1,0:T(8,128)(2,1)} %get-tuple-element.187.uback_ref), kind=kOutput, calls=%fused_computation.12 | convolution fusion | flops 10741612544 | bytes 18874368 | tf_op jit(solution)/shard_map/dot_general | solution.py:58
  535.5 7.1 multiply_reduce_fusion
  542.7 6.1 multiply_convert_fusion
  551.5 5.0 multiply_reduce_fusion.1
  556.5 4.1 multiply_convert_fusion.1
  564.8 3.0 fusion.52
  579.7 10.6 %fusion.4 = (f32[2048]{0:T(1024)}, bf16[1280,2048]{1,0:T(8,128)(2,1)S(1)}) fusion(bf16[1280,2048]{1,0:T(8,128)(2,1)} %constant_dynamic-update-slice_fusion, f32[1280]{0:T(1024)S(1)} %copy-done.88, bf16[1280,768]{0,1:T(8,128)(2,1)} %fusion.16, bf16[2048,768]{1,0:T(8,128)(2,1)} %bitcast.225), kind=kOutput, calls=%fused_computation.7 | convolution fusion | flops 4039636992 | bytes 15610880 | tf_op jit(solution)/shard_map/dot_general | solution.py:58
  594.7 22.4 %all-gather.11.cloned.1.call-done = bf16[1280,2048]{1,0:T(8,128)(2,1)} async-done(((bf16[160,2048]{1,0:T(8,128)(2,1)}), bf16[1280,2048]{1,0:T(8,128)(2,1)}) %all-gather.11.cloned.1.call-update) | async-done | bytes 5242896 | tf_op jit(solution)/shard_map/all_gather | solution.py:67
  617.2 7.6 convolution_convert_fusion.4
  631.4 3.2 collective-permute-done.46
  636.4 2.5 fusion.9
  649.6 4.4 all-to-all-start.5
  656.1 6.5 all-to-all-done.5
  663.2 24.8 %collective-permute-done.47 = bf16[1,64,2048]{2,1,0:T(8,128)(2,1)} collective-permute-done((bf16[1,64,2048]{2,1,0:T(8,128)(2,1)}, bf16[1,64,2048]{2,1,0:T(8,128)(2,1)}, u32[]{:S(2)}, u32[]{:S(2)}) %collective-permute-start.47) | collective-permute-done | bytes 262176 | tf_op jit(solution)/shard_map/ppermute | solution.py:193
  689.1 2.5 fusion.28
  691.5 3.1 add_convert_fusion.3
  694.6 2.6 collective-permute-start.50
  697.2 4.2 all-to-all-start.6
  705.1 4.9 collective-permute-done.53
  712.3 9.8 %all-to-all-done.6 = bf16[8,64,768]{2,1,0:T(8,128)(2,1)} async-done(((bf16[8,64,768]{2,1,0:T(8,128)(2,1)}), bf16[8,64,768]{2,1,0:T(8,128)(2,1)}, u32[]{:S(2)}, u32[]{:S(2)}) %all-to-all-start.6) | async-done | bytes 786464 | tf_op jit(solution)/shard_map/all_to_all | solution.py:236
  722.2 2.5 reshape.639
  729.8 4.0 add_convert_fusion.1
  734.0 3.1 multiply_convert_fusion.2
  737.0 2.5 convert_element_type.544
  739.6 20.3 %collective-permute-done.56 = bf16[1,3,64,2048]{3,2,1,0:T(8,128)(2,1)S(1)} collective-permute-done((bf16[1,3,64,2048]{3,2,1,0:T(8,128)(2,1)S(1)}, bf16[1,3,64,2048]{3,2,1,0:T(8,128)(2,1)S(1)}, u32[]{:S(2)}, u32[]{:S(2)}) %collective-permute-start.56) | collective-permute-done | bytes 786464 | tf_op jit(solution)/shard_map/ppermute | solution.py:193
  762.1 36.3 %reduce-scatter.8.cloned.1.call-done = bf16[512,2048]{1,0:T(8,128)(2,1)} async-done(((bf16[2048,2048]{1,0:T(8,128)(2,1)}), bf16[512,2048]{1,0:T(8,128)(2,1)}) %reduce-scatter.8.cloned.1.call-update) | async-done | bytes 2097168 | tf_op jit(solution)/shard_map/reduce_scatter | solution.py:746
  802.4 4.0 collective-permute-start.54
  814.3 6.7 collective-permute-done.54
  830.6 3.2 fusion.21
  (638 shorter events, 239.9 us)
Async XLA Ops:
  7.2 18.5 %collective-permute-start = (bf16[160,2048]{1,0:T(8,128)(2,1)}, bf16[160,2048]{1,0:T(8,128)(2,1)S(1)}, u32[]{:S(2)}, u32[]{:S(2)}) collective-permute-start(bf16[160,2048]{1,0:T(8,128)(2,1)} %param.18), channel_id=1, source_target_pairs={{0,1},{2,0},{4,2},{6,4},{7,6},{5,7},{3,5},{1,3},{8,9},{10,8},{12,1... | collective-permute-start | bytes 1966088 | tf_op jit(solution)/shard_map/ppermute | solution.py:86
  10.2 17.5 %collective-permute-start.1 = (bf16[160,2048]{1,0:T(8,128)(2,1)}, bf16[160,2048]{1,0:T(8,128)(2,1)S(1)}, u32[]{:S(2)}, u32[]{:S(2)}) collective-permute-start(bf16[160,2048]{1,0:T(8,128)(2,1)} %param.18), channel_id=1, source_target_pairs={{0,2},{2,4},{4,6},{6,7},{7,5},{5,3},{3,1},{1,0},{8,10},{10,12},{12... | collective-permute-start | bytes 1966088 | tf_op jit(solution)/shard_map/ppermute | solution.py:86
  14.2 47.2 %all-to-all-start.2 = ((bf16[8,52,128]{2,1,0:T(8,128)(2,1)}), bf16[8,52,128]{2,1,0:T(8,128)(2,1)S(1)}, u32[]{:S(2)}, u32[]{:S(2)}) async-start(bf16[8,52,128]{2,1,0:T(8,128)(2,1)} %broadcast_in_dim.194), calls=%async_computation.2 | async-start | bytes 229376 | tf_op jit(solution)/shard_map/all_to_all | solution.py:236
  25.7 16.3 %collective-permute-start.2 = (bf16[160,2048]{1,0:T(8,128)(2,1)S(1)}, bf16[160,2048]{1,0:T(8,128)(2,1)S(1)}, u32[]{:S(2)}, u32[]{:S(2)}) collective-permute-start(bf16[160,2048]{1,0:T(8,128)(2,1)S(1)} %collective-permute-done), channel_id=1, source_target_pairs={{0,1},{2,0},{4,2},{6,4},{7,6},{5,7},{3,5},{1,3},{8,9},{10,8},{12,1... | collective-permute-start | bytes 1966088 | tf_op jit(solution)/shard_map/ppermute | solution.py:86
  27.7 15.7 %collective-permute-start.3 = (bf16[160,2048]{1,0:T(8,128)(2,1)S(1)}, bf16[160,2048]{1,0:T(8,128)(2,1)S(1)}, u32[]{:S(2)}, u32[]{:S(2)}) collective-permute-start(bf16[160,2048]{1,0:T(8,128)(2,1)S(1)} %collective-permute-done.1), channel_id=1, source_target_pairs={{0,2},{2,4},{4,6},{6,7},{7,5},{5,3},{3,1},{1,0},{8,10},{10,12},{12... | collective-permute-start | bytes 1966088 | tf_op jit(solution)/shard_map/ppermute | solution.py:86
  42.0 17.9 %collective-permute-start.4 = (bf16[160,2048]{1,0:T(8,128)(2,1)S(1)}, bf16[160,2048]{1,0:T(8,128)(2,1)S(1)}, u32[]{:S(2)}, u32[]{:S(2)}) collective-permute-start(bf16[160,2048]{1,0:T(8,128)(2,1)S(1)} %collective-permute-done.2), channel_id=1, source_target_pairs={{0,1},{2,0},{4,2},{6,4},{7,6},{5,7},{3,5},{1,3},{8,9},{10,8},{12,1... | collective-permute-start | bytes 1966088 | tf_op jit(solution)/shard_map/ppermute | solution.py:86
  43.4 14.5 %collective-permute-start.5 = (bf16[160,2048]{1,0:T(8,128)(2,1)S(1)}, bf16[160,2048]{1,0:T(8,128)(2,1)S(1)}, u32[]{:S(2)}, u32[]{:S(2)}) collective-permute-start(bf16[160,2048]{1,0:T(8,128)(2,1)S(1)} %collective-permute-done.3), channel_id=1, source_target_pairs={{0,2},{2,4},{4,6},{6,7},{7,5},{5,3},{3,1},{1,0},{8,10},{10,12},{12... | collective-permute-start | bytes 1966088 | tf_op jit(solution)/shard_map/ppermute | solution.py:86
  58.6 9.4 %collective-permute-start.6 = (bf16[80,2048]{1,0:T(8,128)(2,1)}, bf16[80,2048]{1,0:T(8,128)(2,1)S(1)}, u32[]{:S(2)}, u32[]{:S(2)}) collective-permute-start(bf16[80,2048]{1,0:T(8,128)(2,1)} %slice.424), channel_id=1, source_target_pairs={{0,2},{2,4},{4,6},{6,7},{7,5},{5,3},{3,1},{1,0},{8,10},{10,12},{12... | collective-permute-start | bytes 983048 | tf_op jit(solution)/shard_map/ppermute | solution.py:86
  60.7 10.4 %collective-permute-start.7 = (bf16[80,2048]{1,0:T(8,128)(2,1)}, bf16[80,2048]{1,0:T(8,128)(2,1)}, u32[]{:S(2)}, u32[]{:S(2)}) collective-permute-start(bf16[80,2048]{1,0:T(8,128)(2,1)} %slice.425), channel_id=1, source_target_pairs={{0,1},{2,0},{4,2},{6,4},{7,6},{5,7},{3,5},{1,3},{8,9},{10,8},{12,1... | collective-permute-start | bytes 983048 | tf_op jit(solution)/shard_map/ppermute | solution.py:86
  61.4 24.2 %all-to-all-start = ((bf16[8,64,768]{2,1,0:T(8,128)(2,1)}), bf16[8,64,768]{2,1,0:T(8,128)(2,1)S(1)}, u32[]{:S(2)}, u32[]{:S(2)}) async-start(bf16[8,64,768]{2,1,0:T(8,128)(2,1)} %copy.125), calls=%async_computation | async-start | bytes 1572864 | tf_op jit(solution)/shard_map/all_to_all | solution.py:236
  66.2 62.4 %all-gather.5.cloned.1.call-start = ((), (), s32[]{:S(2)}) async-start(), calls=%async_computation.10 | async-start | bytes 1179648 | tf_op jit(solution)/shard_map/all_gather | solution.py:67
  74.6 86.4 %all-gather.7.cloned.1.call-start = ((), (), s32[]{:S(2)}) async-start(), calls=%async_computation.11 | async-start | bytes 1179648 | tf_op jit(solution)/shard_map/all_gather | solution.py:67
  85.6 16.7 %collective-permute-start.10 = (bf16[1,8,64,768]{3,2,1,0:T(8,128)(2,1)S(1)}, bf16[1,8,64,768]{3,2,1,0:T(8,128)(2,1)S(1)}, u32[]{:S(2)}, u32[]{:S(2)}) collective-permute-start(bf16[1,8,64,768]{3,2,1,0:T(8,128)(2,1)S(1)} %bitcast.202), channel_id=1, source_target_pairs={{0,16},{8,24},{16,0},{24,8},{1,17},{9,25},{17,1},{25,9},{2,18},{10... | collective-permute-start | bytes 2359304 | tf_op jit(solution)/shard_map/ppermute | solution.py:193
  108.9 151.4 %all-gather.9.cloned.1.call-start = ((), (), s32[]{:S(2)}) async-start(), calls=%async_computation.12 | async-start | bytes 5898240 | tf_op jit(solution)/shard_map/all_gather | solution.py:67
  140.0 48.3 %collective-permute-start.8 = (bf16[2048,256]{1,0:T(8,128)(2,1)}, bf16[2048,256]{1,0:T(8,128)(2,1)}, u32[]{:S(2)}, u32[]{:S(2)}) collective-permute-start(bf16[2048,256]{1,0:T(8,128)(2,1)} %all-gather.5.cloned.1.call-done), channel_id=1, source_target_pairs={{0,16},{8,24},{16,0},{24,8},{1,17},{9,25},{17,1},{25,9},{2,18},{10... | collective-permute-start | bytes 3145736 | tf_op jit(solution)/shard_map/ppermute | solution.py:193
  161.0 27.3 %collective-permute-start.9 = (bf16[2048,256]{1,0:T(8,128)(2,1)}, bf16[2048,256]{1,0:T(8,128)(2,1)S(1)}, u32[]{:S(2)}, u32[]{:S(2)}) collective-permute-start(bf16[2048,256]{1,0:T(8,128)(2,1)} %all-gather.7.cloned.1.call-done), channel_id=1, source_target_pairs={{0,16},{8,24},{16,0},{24,8},{1,17},{9,25},{17,1},{25,9},{2,18},{10... | collective-permute-start | bytes 3145736 | tf_op jit(solution)/shard_map/ppermute | solution.py:193
  188.3 32.4 %all-to-all-start.1 = ((bf16[8,160,256]{2,1,0:T(8,128)(2,1)}), bf16[8,160,256]{2,1,0:T(8,128)(2,1)S(1)}, u32[]{:S(2)}, u32[]{:S(2)}) async-start(bf16[8,160,256]{2,1,0:T(8,128)(2,1)} %copy-done.52), calls=%async_computation.1 | async-start | bytes 1310720 | tf_op jit(solution)/shard_map/all_to_all | solution.py:236
  193.7 35.9 %collective-permute-start.13 = (bf16[2048,256]{1,0:T(8,128)(2,1)}, bf16[2048,256]{1,0:T(8,128)(2,1)}, u32[]{:S(2)}, u32[]{:S(2)}) collective-permute-start(bf16[2048,256]{1,0:T(8,128)(2,1)} %all-gather.5.cloned.1.call-done), channel_id=1, source_target_pairs={{0,8},{8,0},{16,24},{24,16},{1,9},{9,1},{17,25},{25,17},{2,10},{10... | collective-permute-start | bytes 3145736 | tf_op jit(solution)/shard_map/ppermute | solution.py:193
  193.7 34.3 %collective-permute-start.12 = (bf16[2048,256]{1,0:T(8,128)(2,1)}, bf16[2048,256]{1,0:T(8,128)(2,1)}, u32[]{:S(2)}, u32[]{:S(2)}) collective-permute-start(bf16[2048,256]{1,0:T(8,128)(2,1)} %all-gather.7.cloned.1.call-done), channel_id=1, source_target_pairs={{0,8},{8,0},{16,24},{24,16},{1,9},{9,1},{17,25},{25,17},{2,10},{10... | collective-permute-start | bytes 3145736 | tf_op jit(solution)/shard_map/ppermute | solution.py:193
  194.2 37.0 %collective-permute-start.14 = (bf16[2048,256]{1,0:T(8,128)(2,1)S(1)}, bf16[2048,256]{1,0:T(8,128)(2,1)}, u32[]{:S(2)}, u32[]{:S(2)}) collective-permute-start(bf16[2048,256]{1,0:T(8,128)(2,1)S(1)} %collective-permute-done.9), channel_id=1, source_target_pairs={{0,8},{8,0},{16,24},{24,16},{1,9},{9,1},{17,25},{25,17},{2,10},{10... | collective-permute-start | bytes 3145736 | tf_op jit(solution)/shard_map/ppermute | solution.py:193
  194.2 38.6 %collective-permute-start.15 = (bf16[2048,256]{1,0:T(8,128)(2,1)}, bf16[2048,256]{1,0:T(8,128)(2,1)}, u32[]{:S(2)}, u32[]{:S(2)}) collective-permute-start(bf16[2048,256]{1,0:T(8,128)(2,1)} %collective-permute-done.8), channel_id=1, source_target_pairs={{0,8},{8,0},{16,24},{24,16},{1,9},{9,1},{17,25},{25,17},{2,10},{10... | collective-permute-start | bytes 3145736 | tf_op jit(solution)/shard_map/ppermute | solution.py:193
  236.1 39.2 %collective-permute-start.16 = (bf16[160,2048]{1,0:T(8,128)(2,1)S(1)}, bf16[160,2048]{1,0:T(8,128)(2,1)S(1)}, u32[]{:S(2)}, u32[]{:S(2)}) collective-permute-start(bf16[160,2048]{1,0:T(8,128)(2,1)S(1)} %multiply_convert_fusion.3), channel_id=1, source_target_pairs={{0,2},{2,4},{4,6},{6,7},{7,5},{5,3},{3,1},{1,0},{8,10},{10,12},{12... | collective-permute-start | bytes 1966088 | tf_op jit(solution)/shard_map/ppermute | solution.py:86
  236.2 39.0 %collective-permute-start.17 = (bf16[160,2048]{1,0:T(8,128)(2,1)S(1)}, bf16[160,2048]{1,0:T(8,128)(2,1)S(1)}, u32[]{:S(2)}, u32[]{:S(2)}) collective-permute-start(bf16[160,2048]{1,0:T(8,128)(2,1)S(1)} %multiply_convert_fusion.3), channel_id=1, source_target_pairs={{0,1},{2,0},{4,2},{6,4},{7,6},{5,7},{3,5},{1,3},{8,9},{10,8},{12,1... | collective-permute-start | bytes 1966088 | tf_op jit(solution)/shard_map/ppermute | solution.py:86
  275.3 17.7 %collective-permute-start.18 = (bf16[160,2048]{1,0:T(8,128)(2,1)S(1)}, bf16[160,2048]{1,0:T(8,128)(2,1)}, u32[]{:S(2)}, u32[]{:S(2)}) collective-permute-start(bf16[160,2048]{1,0:T(8,128)(2,1)S(1)} %collective-permute-done.16), channel_id=1, source_target_pairs={{0,2},{2,4},{4,6},{6,7},{7,5},{5,3},{3,1},{1,0},{8,10},{10,12},{12... | collective-permute-start | bytes 1966088 | tf_op jit(solution)/shard_map/ppermute | solution.py:86
  275.9 17.0 %collective-permute-start.19 = (bf16[160,2048]{1,0:T(8,128)(2,1)S(1)}, bf16[160,2048]{1,0:T(8,128)(2,1)}, u32[]{:S(2)}, u32[]{:S(2)}) collective-permute-start(bf16[160,2048]{1,0:T(8,128)(2,1)S(1)} %collective-permute-done.17), channel_id=1, source_target_pairs={{0,1},{2,0},{4,2},{6,4},{7,6},{5,7},{3,5},{1,3},{8,9},{10,8},{12,1... | collective-permute-start | bytes 1966088 | tf_op jit(solution)/shard_map/ppermute | solution.py:86
  294.2 24.1 %collective-permute-start.21 = (bf16[160,2048]{1,0:T(8,128)(2,1)}, bf16[160,2048]{1,0:T(8,128)(2,1)S(1)}, u32[]{:S(2)}, u32[]{:S(2)}) collective-permute-start(bf16[160,2048]{1,0:T(8,128)(2,1)} %collective-permute-done.19), channel_id=1, source_target_pairs={{0,1},{2,0},{4,2},{6,4},{7,6},{5,7},{3,5},{1,3},{8,9},{10,8},{12,1... | collective-permute-start | bytes 1966088 | tf_op jit(solution)/shard_map/ppermute | solution.py:86
  296.1 22.2 %collective-permute-start.20 = (bf16[160,2048]{1,0:T(8,128)(2,1)}, bf16[160,2048]{1,0:T(8,128)(2,1)S(1)}, u32[]{:S(2)}, u32[]{:S(2)}) collective-permute-start(bf16[160,2048]{1,0:T(8,128)(2,1)} %collective-permute-done.18), channel_id=1, source_target_pairs={{0,2},{2,4},{4,6},{6,7},{7,5},{5,3},{3,1},{1,0},{8,10},{10,12},{12... | collective-permute-start | bytes 1966088 | tf_op jit(solution)/shard_map/ppermute | solution.py:86
  372.0 19.8 %collective-permute-start.24 = (bf16[80,2048]{1,0:T(8,128)(2,1)}, bf16[80,2048]{1,0:T(8,128)(2,1)}, u32[]{:S(2)}, u32[]{:S(2)}) collective-permute-start(bf16[80,2048]{1,0:T(8,128)(2,1)} %get-tuple-element.402), channel_id=1, source_target_pairs={{0,2},{2,4},{4,6},{6,7},{7,5},{5,3},{3,1},{1,0},{8,10},{10,12},{12... | collective-permute-start | bytes 983048 | tf_op jit(solution)/shard_map/ppermute | solution.py:86
  373.5 18.4 %collective-permute-start.25 = (bf16[80,2048]{1,0:T(8,128)(2,1)}, bf16[80,2048]{1,0:T(8,128)(2,1)}, u32[]{:S(2)}, u32[]{:S(2)}) collective-permute-start(bf16[80,2048]{1,0:T(8,128)(2,1)} %get-tuple-element.401), channel_id=1, source_target_pairs={{0,1},{2,0},{4,2},{6,4},{7,6},{5,7},{3,5},{1,3},{8,9},{10,8},{12,1... | collective-permute-start | bytes 983048 | tf_op jit(solution)/shard_map/ppermute | solution.py:86
  393.5 25.4 %collective-permute-start.27 = (bf16[160,2048]{1,0:T(8,128)(2,1)S(1)}, bf16[160,2048]{1,0:T(8,128)(2,1)}, u32[]{:S(2)}, u32[]{:S(2)}) collective-permute-start(bf16[160,2048]{1,0:T(8,128)(2,1)S(1)} %pad_maximum_fusion.7), channel_id=1, source_target_pairs={{0,1},{2,0},{4,2},{6,4},{7,6},{5,7},{3,5},{1,3},{8,9},{10,8},{12,1... | collective-permute-start | bytes 1966088 | tf_op jit(solution)/shard_map/ppermute | solution.py:86
  395.8 23.1 %collective-permute-start.26 = (bf16[160,2048]{1,0:T(8,128)(2,1)}, bf16[160,2048]{1,0:T(8,128)(2,1)S(1)}, u32[]{:S(2)}, u32[]{:S(2)}) collective-permute-start(bf16[160,2048]{1,0:T(8,128)(2,1)} %pad_maximum_fusion.6), channel_id=1, source_target_pairs={{0,2},{2,4},{4,6},{6,7},{7,5},{5,3},{3,1},{1,0},{8,10},{10,12},{12... | collective-permute-start | bytes 1966088 | tf_op jit(solution)/shard_map/ppermute | solution.py:86
  397.4 21.4 %all-to-all-start.3 = ((f32[8,160,2]{1,2,0:T(2,128)}), f32[8,160,2]{1,2,0:T(2,128)S(1)}, u32[]{:S(2)}, u32[]{:S(2)}) async-start(f32[8,160,2]{1,2,0:T(2,128)} %copy.160), calls=%async_computation.3 | async-start | bytes 32768 | tf_op jit(solution)/shard_map/all_to_all | solution.py:236
  401.9 177.8 %reduce-scatter.4.cloned.1.call-start = ((), (), s32[]{:S(2)}) async-start(), calls=%async_computation.13 | async-start | bytes 10485760 | tf_op jit(solution)/shard_map/reduce_scatter | solution.py:680
  422.4 27.4 %collective-permute-start.29 = (bf16[160,2048]{1,0:T(8,128)(2,1)S(1)}, bf16[160,2048]{1,0:T(8,128)(2,1)}, u32[]{:S(2)}, u32[]{:S(2)}) collective-permute-start(bf16[160,2048]{1,0:T(8,128)(2,1)S(1)} %add_convert_fusion.11), channel_id=1, source_target_pairs={{0,1},{2,0},{4,2},{6,4},{7,6},{5,7},{3,5},{1,3},{8,9},{10,8},{12,1... | collective-permute-start | bytes 1966088 | tf_op jit(solution)/shard_map/ppermute | solution.py:86
  424.4 25.4 %collective-permute-start.30 = (bf16[80,2048]{1,0:T(8,128)(2,1)}, bf16[80,2048]{1,0:T(8,128)(2,1)}, u32[]{:S(2)}, u32[]{:S(2)}) collective-permute-start(bf16[80,2048]{1,0:T(8,128)(2,1)} %get-tuple-element.385), channel_id=1, source_target_pairs={{0,2},{2,4},{4,6},{6,7},{7,5},{5,3},{3,1},{1,0},{8,10},{10,12},{12... | collective-permute-start | bytes 983048 | tf_op jit(solution)/shard_map/ppermute | solution.py:86
  424.5 25.3 %collective-permute-start.31 = (bf16[80,2048]{1,0:T(8,128)(2,1)S(1)}, bf16[80,2048]{1,0:T(8,128)(2,1)}, u32[]{:S(2)}, u32[]{:S(2)}) collective-permute-start(bf16[80,2048]{1,0:T(8,128)(2,1)S(1)} %get-tuple-element.384), channel_id=1, source_target_pairs={{0,1},{2,0},{4,2},{6,4},{7,6},{5,7},{3,5},{1,3},{8,9},{10,8},{12,1... | collective-permute-start | bytes 983048 | tf_op jit(solution)/shard_map/ppermute | solution.py:86
  428.6 21.3 %collective-permute-start.28 = (bf16[160,2048]{1,0:T(8,128)(2,1)}, bf16[160,2048]{1,0:T(8,128)(2,1)S(1)}, u32[]{:S(2)}, u32[]{:S(2)}) collective-permute-start(bf16[160,2048]{1,0:T(8,128)(2,1)} %add_convert_fusion.12), channel_id=1, source_target_pairs={{0,2},{2,4},{4,6},{6,7},{7,5},{5,3},{3,1},{1,0},{8,10},{10,12},{12... | collective-permute-start | bytes 1966088 | tf_op jit(solution)/shard_map/ppermute | solution.py:86
  450.7 166.5 %all-gather.11.cloned.1.call-start = ((), (), s32[]{:S(2)}) async-start(), calls=%async_computation.14 | async-start | bytes 5898240 | tf_op jit(solution)/shard_map/all_gather | solution.py:67
  454.2 24.7 %collective-permute-start.35 = (bf16[160,2048]{1,0:T(8,128)(2,1)}, bf16[160,2048]{1,0:T(8,128)(2,1)}, u32[]{:S(2)}, u32[]{:S(2)}) collective-permute-start(bf16[160,2048]{1,0:T(8,128)(2,1)} %pad_maximum_fusion.9), channel_id=1, source_target_pairs={{0,1},{2,0},{4,2},{6,4},{7,6},{5,7},{3,5},{1,3},{8,9},{10,8},{12,1... | collective-permute-start | bytes 1966088 | tf_op jit(solution)/shard_map/ppermute | solution.py:86
  457.1 21.8 %collective-permute-start.34 = (bf16[160,2048]{1,0:T(8,128)(2,1)}, bf16[160,2048]{1,0:T(8,128)(2,1)}, u32[]{:S(2)}, u32[]{:S(2)}) collective-permute-start(bf16[160,2048]{1,0:T(8,128)(2,1)} %pad_maximum_fusion.8), channel_id=1, source_target_pairs={{0,2},{2,4},{4,6},{6,7},{7,5},{5,3},{3,1},{1,0},{8,10},{10,12},{12... | collective-permute-start | bytes 1966088 | tf_op jit(solution)/shard_map/ppermute | solution.py:86
  460.0 22.5 %collective-permute-start.32 = (bf16[160,2048]{1,0:T(8,128)(2,1)}, bf16[160,2048]{1,0:T(8,128)(2,1)S(1)}, u32[]{:S(2)}, u32[]{:S(2)}) collective-permute-start(bf16[160,2048]{1,0:T(8,128)(2,1)} %get-tuple-element.398), channel_id=1, source_target_pairs={{0,2},{2,4},{4,6},{6,7},{7,5},{5,3},{3,1},{1,0},{8,10},{10,12},{12... | collective-permute-start | bytes 1966088 | tf_op jit(solution)/shard_map/ppermute | solution.py:86
  462.0 20.6 %collective-permute-start.33 = (bf16[160,2048]{1,0:T(8,128)(2,1)}, bf16[160,2048]{1,0:T(8,128)(2,1)S(1)}, u32[]{:S(2)}, u32[]{:S(2)}) collective-permute-start(bf16[160,2048]{1,0:T(8,128)(2,1)} %get-tuple-element.397), channel_id=1, source_target_pairs={{0,1},{2,0},{4,2},{6,4},{7,6},{5,7},{3,5},{1,3},{8,9},{10,8},{12,1... | collective-permute-start | bytes 1966088 | tf_op jit(solution)/shard_map/ppermute | solution.py:86
  485.9 20.3 %collective-permute-start.36 = (bf16[160,2048]{1,0:T(8,128)(2,1)}, bf16[160,2048]{1,0:T(8,128)(2,1)}, u32[]{:S(2)}, u32[]{:S(2)}) collective-permute-start(bf16[160,2048]{1,0:T(8,128)(2,1)} %get-tuple-element.381), channel_id=1, source_target_pairs={{0,2},{2,4},{4,6},{6,7},{7,5},{5,3},{3,1},{1,0},{8,10},{10,12},{12... | collective-permute-start | bytes 1966088 | tf_op jit(solution)/shard_map/ppermute | solution.py:86
  486.1 20.0 %collective-permute-start.37 = (bf16[160,2048]{1,0:T(8,128)(2,1)}, bf16[160,2048]{1,0:T(8,128)(2,1)}, u32[]{:S(2)}, u32[]{:S(2)}) collective-permute-start(bf16[160,2048]{1,0:T(8,128)(2,1)} %get-tuple-element.380), channel_id=1, source_target_pairs={{0,1},{2,0},{4,2},{6,4},{7,6},{5,7},{3,5},{1,3},{8,9},{10,8},{12,1... | collective-permute-start | bytes 1966088 | tf_op jit(solution)/shard_map/ppermute | solution.py:86
  506.2 223.6 %reduce-scatter.6.cloned.1.call-start = ((), (), s32[]{:S(2)}) async-start(), calls=%async_computation.15 | async-start | bytes 10485760 | tf_op jit(solution)/shard_map/reduce_scatter | solution.py:744
  510.1 23.7 %collective-permute-start.38 = (bf16[160,2048]{1,0:T(8,128)(2,1)}, bf16[160,2048]{1,0:T(8,128)(2,1)S(1)}, u32[]{:S(2)}, u32[]{:S(2)}) collective-permute-start(bf16[160,2048]{1,0:T(8,128)(2,1)} %get-tuple-element.379), channel_id=1, source_target_pairs={{0,2},{2,4},{4,6},{6,7},{7,5},{5,3},{3,1},{1,0},{8,10},{10,12},{12... | collective-permute-start | bytes 1966088 | tf_op jit(solution)/shard_map/ppermute | solution.py:86
  510.1 23.6 %collective-permute-start.39 = (bf16[160,2048]{1,0:T(8,128)(2,1)}, bf16[160,2048]{1,0:T(8,128)(2,1)}, u32[]{:S(2)}, u32[]{:S(2)}) collective-permute-start(bf16[160,2048]{1,0:T(8,128)(2,1)} %get-tuple-element.378), channel_id=1, source_target_pairs={{0,1},{2,0},{4,2},{6,4},{7,6},{5,7},{3,5},{1,3},{8,9},{10,8},{12,1... | collective-permute-start | bytes 1966088 | tf_op jit(solution)/shard_map/ppermute | solution.py:86
  512.1 23.3 %all-to-all-start.4 = ((bf16[8,160,256]{2,1,0:T(8,128)(2,1)}), bf16[8,160,256]{2,1,0:T(8,128)(2,1)S(1)}, u32[]{:S(2)}, u32[]{:S(2)}) async-start(bf16[8,160,256]{2,1,0:T(8,128)(2,1)} %bitcast.183), calls=%async_computation.4 | async-start | bytes 1310720 | tf_op jit(solution)/shard_map/all_to_all | solution.py:236
  516.5 281.9 %reduce-scatter.8.cloned.1.call-start = ((), (), s32[]{:S(2)}) async-start(), calls=%async_computation.16 | async-start | bytes 10485760 | tf_op jit(solution)/shard_map/reduce_scatter | solution.py:746
  592.7 33.8 %collective-permute-start.40 = (bf16[80,2048]{1,0:T(8,128)(2,1)S(1)}, bf16[80,2048]{1,0:T(8,128)(2,1)}, u32[]{:S(2)}, u32[]{:S(2)}) collective-permute-start(bf16[80,2048]{1,0:T(8,128)(2,1)S(1)} %get-tuple-element.375), channel_id=1, source_target_pairs={{0,2},{2,4},{4,6},{6,7},{7,5},{5,3},{3,1},{1,0},{8,10},{10,12},{12... | collective-permute-start | bytes 983048 | tf_op jit(solution)/shard_map/ppermute | solution.py:86
  593.8 32.6 %collective-permute-start.41 = (bf16[80,2048]{1,0:T(8,128)(2,1)S(1)}, bf16[80,2048]{1,0:T(8,128)(2,1)}, u32[]{:S(2)}, u32[]{:S(2)}) collective-permute-start(bf16[80,2048]{1,0:T(8,128)(2,1)S(1)} %get-tuple-element.374), channel_id=1, source_target_pairs={{0,1},{2,0},{4,2},{6,4},{7,6},{5,7},{3,5},{1,3},{8,9},{10,8},{12,1... | collective-permute-start | bytes 983048 | tf_op jit(solution)/shard_map/ppermute | solution.py:86
  641.0 48.0 %collective-permute-start.45 = (bf16[8,1,64,768]{3,2,1,0:T(8,128)(2,1)}, bf16[8,1,64,768]{3,2,1,0:T(8,128)(2,1)}, u32[]{:S(2)}, u32[]{:S(2)}) collective-permute-start(bf16[8,1,64,768]{3,2,1,0:T(8,128)(2,1)} %constant_dynamic-slice_fusion.1), channel_id=1, source_target_pairs={{0,16},{8,24},{16,0},{24,8},{1,17},{9,25},{17,1},{25,9},{2,18},{10... | collective-permute-start | bytes 2359304 | tf_op jit(solution)/shard_map/ppermute | solution.py:193
  643.4 44.6 %collective-permute-start.47 = (bf16[1,64,2048]{2,1,0:T(8,128)(2,1)}, bf16[1,64,2048]{2,1,0:T(8,128)(2,1)}, u32[]{:S(2)}, u32[]{:S(2)}) collective-permute-start(bf16[1,64,2048]{2,1,0:T(8,128)(2,1)} %constant_dynamic-slice_fusion), channel_id=1, source_target_pairs={{0,16},{8,24},{16,0},{24,8},{1,17},{9,25},{17,1},{25,9},{2,18},{10... | collective-permute-start | bytes 786440 | tf_op jit(solution)/shard_map/ppermute | solution.py:193
  649.6 12.9 %all-to-all-start.5 = ((f32[8,1,4640]{2,1,0:T(1,128)}), f32[8,1,4640]{2,1,0:T(1,128)S(1)}, u32[]{:S(2)}, u32[]{:S(2)}) async-start(f32[8,1,4640]{2,1,0:T(1,128)} %copy.163), calls=%async_computation.6 | async-start | bytes 303104 | tf_op jit(solution)/shard_map/all_to_all | solution.py:236
  654.0 37.5 %collective-permute-start.43 = (bf16[160,2048]{1,0:T(8,128)(2,1)S(1)}, bf16[160,2048]{1,0:T(8,128)(2,1)S(1)}, u32[]{:S(2)}, u32[]{:S(2)}) collective-permute-start(bf16[160,2048]{1,0:T(8,128)(2,1)S(1)} %pad_maximum_fusion.11), channel_id=1, source_target_pairs={{0,1},{2,0},{4,2},{6,4},{7,6},{5,7},{3,5},{1,3},{8,9},{10,8},{12,1... | collective-permute-start | bytes 1966088 | tf_op jit(solution)/shard_map/ppermute | solution.py:86
  656.0 35.5 %collective-permute-start.42 = (bf16[160,2048]{1,0:T(8,128)(2,1)}, bf16[160,2048]{1,0:T(8,128)(2,1)}, u32[]{:S(2)}, u32[]{:S(2)}) collective-permute-start(bf16[160,2048]{1,0:T(8,128)(2,1)} %pad_maximum_fusion.10), channel_id=1, source_target_pairs={{0,2},{2,4},{4,6},{6,7},{7,5},{5,3},{3,1},{1,0},{8,10},{10,12},{12... | collective-permute-start | bytes 1966088 | tf_op jit(solution)/shard_map/ppermute | solution.py:86
  694.6 15.4 %collective-permute-start.50 = (bf16[1,64,2048]{2,1,0:T(8,128)(2,1)S(1)}, bf16[1,64,2048]{2,1,0:T(8,128)(2,1)S(1)}, u32[]{:S(2)}, u32[]{:S(2)}) collective-permute-start(bf16[1,64,2048]{2,1,0:T(8,128)(2,1)S(1)} %bitcast.247), channel_id=1, source_target_pairs={{0,16},{8,24},{16,0},{24,8},{1,17},{9,25},{17,1},{25,9},{2,18},{10... | collective-permute-start | bytes 786440 | tf_op jit(solution)/shard_map/ppermute | solution.py:193
  697.2 24.9 %all-to-all-start.6 = ((bf16[8,64,768]{2,1,0:T(8,128)(2,1)}), bf16[8,64,768]{2,1,0:T(8,128)(2,1)}, u32[]{:S(2)}, u32[]{:S(2)}) async-start(bf16[8,64,768]{2,1,0:T(8,128)(2,1)} %fusion.28), calls=%async_computation.7 | async-start | bytes 1572864 | tf_op jit(solution)/shard_map/all_to_all | solution.py:236
  702.8 24.9 %collective-permute-start.48 = (bf16[160,2048]{1,0:T(8,128)(2,1)}, bf16[160,2048]{1,0:T(8,128)(2,1)}, u32[]{:S(2)}, u32[]{:S(2)}) collective-permute-start(bf16[160,2048]{1,0:T(8,128)(2,1)} %get-tuple-element.371), channel_id=1, source_target_pairs={{0,2},{2,4},{4,6},{6,7},{7,5},{5,3},{3,1},{1,0},{8,10},{10,12},{12... | collective-permute-start | bytes 1966088 | tf_op jit(solution)/shard_map/ppermute | solution.py:86
  704.7 25.0 %collective-permute-start.49 = (bf16[160,2048]{1,0:T(8,128)(2,1)}, bf16[160,2048]{1,0:T(8,128)(2,1)}, u32[]{:S(2)}, u32[]{:S(2)}) collective-permute-start(bf16[160,2048]{1,0:T(8,128)(2,1)} %get-tuple-element.370), channel_id=1, source_target_pairs={{0,1},{2,0},{4,2},{6,4},{7,6},{5,7},{3,5},{1,3},{8,9},{10,8},{12,1... | collective-permute-start | bytes 1966088 | tf_op jit(solution)/shard_map/ppermute | solution.py:86
  733.8 26.0 %collective-permute-start.56 = (bf16[1,3,64,2048]{3,2,1,0:T(8,128)(2,1)S(1)}, bf16[1,3,64,2048]{3,2,1,0:T(8,128)(2,1)S(1)}, u32[]{:S(2)}, u32[]{:S(2)}) collective-permute-start(bf16[1,3,64,2048]{3,2,1,0:T(8,128)(2,1)S(1)} %bitcast.205), channel_id=1, source_target_pairs={{0,16},{8,24},{16,0},{24,8},{1,17},{9,25},{17,1},{25,9},{2,18},{10... | collective-permute-start | bytes 2359304 | tf_op jit(solution)/shard_map/ppermute | solution.py:193
  762.1 49.5 %collective-permute-start.57 = (bf16[2,3,64,2048]{3,2,1,0:T(8,128)(2,1)}, bf16[2,3,64,2048]{3,2,1,0:T(8,128)(2,1)}, u32[]{:S(2)}, u32[]{:S(2)}) collective-permute-start(bf16[2,3,64,2048]{3,2,1,0:T(8,128)(2,1)} %maximum_select_fusion.5), channel_id=1, source_target_pairs={{0,8},{8,0},{16,24},{24,16},{1,9},{9,1},{17,25},{25,17},{2,10},{10... | collective-permute-start | bytes 4718600 | tf_op jit(solution)/shard_map/ppermute | solution.py:193
  802.4 18.6 %collective-permute-start.54 = (bf16[160,2048]{1,0:T(8,128)(2,1)}, bf16[160,2048]{1,0:T(8,128)(2,1)}, u32[]{:S(2)}, u32[]{:S(2)}) collective-permute-start(bf16[160,2048]{1,0:T(8,128)(2,1)} %get-tuple-element.369), channel_id=1, source_target_pairs={{0,2},{2,4},{4,6},{6,7},{7,5},{5,3},{3,1},{1,0},{8,10},{10,12},{12... | collective-permute-start | bytes 1966088 | tf_op jit(solution)/shard_map/ppermute | solution.py:86
  806.4 16.7 %collective-permute-start.55 = (bf16[160,2048]{1,0:T(8,128)(2,1)}, bf16[160,2048]{1,0:T(8,128)(2,1)}, u32[]{:S(2)}, u32[]{:S(2)}) collective-permute-start(bf16[160,2048]{1,0:T(8,128)(2,1)} %get-tuple-element.368), channel_id=1, source_target_pairs={{0,1},{2,0},{4,2},{6,4},{7,6},{5,7},{3,5},{1,3},{8,9},{10,8},{12,1... | collective-permute-start | bytes 1966088 | tf_op jit(solution)/shard_map/ppermute | solution.py:86
  (140 other events, 885.4 us)
Sparse Core Ops, SparseCore 0:
  74.7 44.6 all-gather.4
  122.0 38.8 all-gather.6
  163.2 97.0 all-gather.8
  450.8 73.1 reduce-scatter.3
  526.3 90.8 all-gather.10
  619.8 99.1 reduce-scatter.5
  721.5 76.8 reduce-scatter.7

commit v6 on v5

--- a/solution.py
+++ b/solution.py
@@ -90,31 +90,36 @@
     return lax.optimization_barrier(arrays)
 
 
-def fill_window(fill, sent, received):
-    if fill is None:
-        return received, None
-    work, inputs = fill
-    inputs, _ = lax.optimization_barrier((inputs, sent))
-    return lax.optimization_barrier((received, work(*inputs)))
-
-
-def ring_gather(values, fills=()):
-    half = lax.axis_size("ep") // 2
-    middle = values.shape[0] // 2
-    fills = dict(fills)
-    onward, backward = values, values
-    blocks, results = [values], {}
-    for step in range(1, half + 1):
-        if step == half:
-            sent = (onward[:middle], backward[middle:])
+class RingGather:
+    def __init__(self, values):
+        self.middle = values.shape[0] // 2
+        self.half, self.step = lax.axis_size("ep") // 2, 0
+        self.sent = (values, values)
+        self.blocks = [values]
+
+    def start(self):
+        if self.step == self.half - 1:
+            self.sent = (self.sent[0][: self.middle], self.sent[1][self.middle :])
+        self.received = (ring_shift(self.sent[0], 1), ring_shift(self.sent[1], -1))
+
+    def finish(self):
+        self.step += 1
+        onward, backward = self.sent = self.received
+        if self.step < self.half:
+            self.blocks += [backward, onward]
         else:
-            sent = (onward, backward)
-        received = (ring_shift(sent[0], 1), ring_shift(sent[1], -1))
-        fill = fills[step](blocks, results) if step in fills else None
-        (onward, backward), results[step] = fill_window(fill, sent, received)
-        if step < half:
-            blocks = blocks + [backward, onward]
-    return blocks + [jnp.concatenate([onward, backward], axis=0)], results
+            self.blocks += [jnp.concatenate([onward, backward], axis=0)]
+
+
+class Exchange:
+    def __init__(self, values, distance):
+        self.sent, self.distance = values, distance
+
+    def start(self):
+        self.received = rep_exchange(self.sent, self.distance)
+
+    def finish(self):
+        pass
 
 
 class RingSum:
@@ -392,14 +397,6 @@
     small_sent = jnp.concatenate([route_code.astype(low_type), router_weight], axis=0)
 
     small_flat = small_sent.reshape(-1, head_dim)
-    small_all = swap_all(
-        jnp.broadcast_to(small_flat[None], (group_count,) + small_flat.shape)
-    ).reshape(group_count, row_count + width_here, expert_total)
-    code_all = reorder(small_all[:, :row_count], device_of_slot).reshape(
-        group_rows, expert_total
-    )
-    full_router = small_all[:, row_count:].reshape(model_width, expert_total)
-
     projections = jnp.concatenate(
         [
             lax.dynamic_slice_in_dim(piece, replica * share, share, 0).reshape(
@@ -409,100 +406,117 @@
         ],
         axis=2,
     ).transpose(1, 0, 2)
-    head_weight = (
-        rep_gather(swap_all(projections))
-        .transpose(1, 0, 2, 3)
-        .reshape(model_width, 3 * width_here)
-    )
-    token_all = jnp.concatenate(ring_gather(tokens)[0], axis=0)
-    column_share = model_width // replica_count
-    halves = 2 if column_share % 256 == 0 else 1
-    piece_width = column_share // halves
-    token_all, output_own = tie(token_all, output_weight)
-    output_shares = [
-        gather_rows(
-            lax.dynamic_slice_in_dim(
-                output_own, replica * column_share + half * piece_width, piece_width, 1
-            )
-        )
-        for half in range(halves)
-    ]
+    cosine, sine_part = rope_tables(position, head_dim)
+    chunks = 2
+    chunk_rows = group_rows // chunks
+    blocks_here = group_count // chunks
+
+    def chunk_of(array, chunk):
+        return array[chunk * chunk_rows : (chunk + 1) * chunk_rows]
+
+    def normed_rows(rows):
+        wide = rows.astype(wide_type)
+        return (wide * inverse_rms(wide) * prenorm_gain).astype(low_type)
+
+    def head_columns(values, block, head):
+        start = block * width_here + head * head_dim
+        return values[:, start : start + head_dim]
+
+    def project(first, weight, chunk):
+        raw = mm(first, weight, 1, 0)
+        turns = chunk_of(cosine, chunk), chunk_of(sine_part, chunk)
+        results = []
+        for head in range(heads_here):
+            for block, gain in ((0, querynorm_gain), (1, keynorm_gain)):
+                part = head_columns(raw, block, head)
+                normed = part * inverse_rms(part) * gain
+                turned = (normed * turns[0] + turn_half(normed) * turns[1]).astype(low_type)
+                results += [part, turned]
+            results.append(head_columns(raw, 2, head).astype(low_type))
+        return results
+
+    token_ring = RingGather(tokens)
+    swapped = window([token_ring], swap_all, projections)
+    head_pieces, small_all = window(
+        [token_ring],
+        lambda pieces, small: (
+            rep_gather(pieces),
+            swap_all(jnp.broadcast_to(small[None], (group_count,) + small.shape)),
+        ),
+        swapped,
+        small_flat,
+    )
+    head_weight, first_rows = window(
+        [token_ring],
+        lambda pieces, *blocks: (
+            pieces.transpose(1, 0, 2, 3).reshape(model_width, 3 * width_here),
+            normed_rows(jnp.concatenate(blocks, axis=0)),
+        ),
+        head_pieces,
+        *token_ring.blocks[:blocks_here],
+    )
+    early_heads = window(
+        [token_ring],
+        lambda first, weight: project(first, weight, 0),
+        first_rows,
+        head_weight,
+    )
+    token_blocks = token_ring.blocks
+    last_rows = normed_rows(jnp.concatenate(token_blocks[blocks_here:], axis=0))
+    late_heads = project(last_rows, head_weight, 1)
+    first_all = jnp.concatenate([first_rows, last_rows], axis=0)
+    token_all = jnp.concatenate(token_blocks, axis=0)
+    token_wide = token_all.astype(wide_type)
+    inverse_all = inverse_rms(token_wide)
+
+    small_all = small_all.reshape(group_count, row_count + width_here, expert_total)
+    code_all = reorder(small_all[:, :row_count], device_of_slot).reshape(
+        group_rows, expert_total
+    )
+    full_router = small_all[:, row_count:].reshape(model_width, expert_total)
 
     def reorder_rows(rows, index):
         return reorder(
             rows.reshape(group_count, row_count, rows.shape[1]), index
         ).reshape(rows.shape)
 
-    output_shares[-1], cot_own = tie(output_shares[-1], cotangent)
+    late_heads[0], cot_own = tie(late_heads[0], cotangent)
     cot_ordered = gather_rows(cot_own)
     cot_all = reorder_rows(cot_ordered, device_of_slot)
-
-    token_wide = token_all.astype(wide_type)
-    inverse_all = inverse_rms(token_wide)
-    first_all = (token_wide * inverse_all * prenorm_gain).astype(low_type)
-    raw = mm(first_all, head_weight, 1, 0)
-    cosine, sine_part = rope_tables(position, head_dim)
+    column_share = model_width // replica_count
+    cot_ordered, output_own = tie(cot_ordered, output_weight)
+    output_share = gather_rows(
+        lax.dynamic_slice_in_dim(output_own, replica * column_share, column_share, 1)
+    )
 
     hidden_here = down_weight.shape[1]
     flat_down = down_weight.reshape(experts_here * hidden_here, model_width)
 
     allowed = segment[:, None] == segment[None, :]
-
-    def head_columns(values, block, head):
-        start = block * width_here + head * head_dim
-        return values[:, start : start + head_dim]
 
     kept_heads = []
     mixed_parts = []
     for head in range(heads_here):
-        query_raw = head_columns(raw, 0, head)
-        key_raw = head_columns(raw, 1, head)
-        query_inverse = inverse_rms(query_raw)
-        key_inverse = inverse_rms(key_raw)
-        query_normed = query_raw * query_inverse * querynorm_gain
-        key_normed = key_raw * key_inverse * keynorm_gain
-        query_low = (query_normed * cosine + turn_half(query_normed) * sine_part).astype(
-            low_type
-        )
-        key_low = (key_normed * cosine + turn_half(key_normed) * sine_part).astype(low_type)
-        value_low = head_columns(raw, 2, head).astype(low_type)
+        query_raw, query_low, key_raw, key_low, value_low = (
+            jnp.concatenate([early_heads[5 * head + i], late_heads[5 * head + i]], axis=0)
+            for i in range(5)
+        )
         scores = jnp.where(allowed, mm(query_low, key_low, 1, 1) * score_scale, masked_value)
         top_score = jnp.max(scores, axis=-1, keepdims=True)
         powers = jnp.exp(scores - top_score)
         log_total = top_score + jnp.log(jnp.sum(powers, axis=-1, keepdims=True))
         weights_low = jnp.exp(scores - log_total).astype(low_type)
         mixed_parts.append(mm(weights_low, value_low, 1, 0).astype(low_type))
-        kept_heads.append(
-            (query_raw, key_raw, query_inverse, key_inverse, query_low, key_low, value_low, log_total)
-        )
+        kept_heads.append((query_raw, key_raw, query_low, key_low, value_low, log_total))
     mixed_low = jnp.concatenate(mixed_parts, axis=1)
 
-    mixed_ordered = reorder_rows(mixed_low, slot_of_device)
-    output_pieces = {(0, half): output_shares[half] for half in range(halves)}
-    distance = replica_count // 2
-    while distance:
-        for j, half in list(output_pieces):
-            output_pieces[j ^ distance, half] = rep_exchange(output_pieces[j, half], distance)
-        if distance == replica_count // 2:
-            for half in range(halves):
-                output_pieces[distance, half], mixed_ordered = tie(
-                    output_pieces[distance, half], mixed_ordered
-                )
-        distance //= 2
-
-    def piece_start(j, half):
-        return (replica ^ j) * column_share + half * piece_width
-
-    mixed_own = (
-        swap_all(mixed_ordered.reshape(group_count, row_count, width_here))
-        .transpose(1, 0, 2)
-        .reshape(row_count, model_width)
-    )
-    attention = jnp.zeros((row_count, model_width), wide_type)
-    for place, piece in output_pieces.items():
-        attention = lax.dynamic_update_slice_in_dim(
-            attention, mm(mixed_own, piece, 1, 0), piece_start(*place), 1
-        )
+    def slot_rows(array):
+        return lambda slot: array[slot * row_count : (slot + 1) * row_count]
+
+    attention_ring = RingSum(slot_rows(mm(mixed_low, output_weight, 1, 0).astype(low_type)), row_count)
+    for _ in range(group_count // 2):
+        window([attention_ring], lambda: ())
+    attention = attention_ring.total()
     residual = tokens.astype(wide_type) + attention
     inverse_two = inverse_rms(residual)
     second_input = (residual * inverse_two * postnorm_gain).astype(low_type)
@@ -513,16 +527,11 @@
         powers = jnp.exp(shifted - jnp.max(shifted, axis=1, keepdims=True))
         return powers / jnp.sum(powers, axis=1, keepdims=True)
 
-    chunks = 2
-    chunk_rows = group_rows // chunks
     kept_all = jnp.where(code_all > 1, valid_all, 0.0)
     kept_here = lax.dynamic_slice_in_dim(kept_all, device * experts_here, experts_here, 1)
 
-    def chunk_of(array, chunk):
-        return array[chunk * chunk_rows : (chunk + 1) * chunk_rows]
-
-    def stream_of(chunk):
-        return (lambda cot_part: (mm(cot_part, flat_down, 1, 1),)), (chunk_of(cot_all, chunk),)
+    def stream_of(cot_part):
+        return mm(cot_part, flat_down, 1, 1)
 
     def expert_chunk(chunk, rows, stream, *earlier):
         gates = gate_table(rows, chunk_of(code_all, chunk)) * chunk_of(kept_all, chunk)
@@ -531,29 +540,60 @@
             rows, gate_weight, up_weight, stream, gates_here, chunk, chunks, earlier
         )
 
-    blocks_here = group_count // chunks
-
-    def first_chunk(blocks, results):
-        rows = jnp.concatenate(blocks[:blocks_here], axis=0)
-        return (
-            lambda stream, rows: (rows,) + tuple(expert_chunk(0, rows, stream))
-        ), (results[1][0], rows)
-
-    blocks, results = ring_gather(
-        second_input,
-        {
-            1: lambda blocks, results: stream_of(0),
-            2: lambda blocks, results: stream_of(1),
-            3: first_chunk,
-        },
-    )
-    rows_first, *earlier, pair_first = results[3]
-    rows_last = jnp.concatenate(blocks[blocks_here:], axis=0)
-    inner_all, gback_all, uback_all, pair_last = expert_chunk(
-        1, rows_last, results[2][0], *earlier
+    halves = 2 if column_share % 256 == 0 else 1
+    piece_width = column_share // halves
+    shares = [output_share[:, i * piece_width : (i + 1) * piece_width] for i in range(halves)]
+    far = replica_count // 2
+
+    second_ring = RingGather(second_input)
+    stream_first = window([second_ring], lambda part: stream_of(part), chunk_of(cot_all, 0))
+    stream_last = window([second_ring], lambda part: stream_of(part), chunk_of(cot_all, 1))
+    rows_first = jnp.concatenate(second_ring.blocks[:blocks_here], axis=0)
+    exchanges = [Exchange(piece, far) for piece in shares]
+    *earlier, pair_first = window(
+        [second_ring, exchanges[0]],
+        lambda rows, stream: expert_chunk(0, rows, stream),
+        rows_first,
+        stream_first,
+    )
+    window([second_ring], lambda: ())
+    rows_last = jnp.concatenate(second_ring.blocks[blocks_here:], axis=0)
+    inner_all, gback_all, uback_all, pair_last = window(
+        exchanges[1:],
+        lambda rows, stream, *earlier: expert_chunk(1, rows, stream, *earlier),
+        rows_last,
+        stream_last,
+        *earlier,
     )
     second_all = jnp.concatenate([rows_first, rows_last], axis=0)
-    back_last = expert_back(gback_all, uback_all, gate_weight, up_weight, 1, chunks)
+    output_pieces = {}
+    for half in range(halves):
+        output_pieces[0, half] = shares[half]
+        output_pieces[far, half] = exchanges[half].received
+    near = []
+    distance = far // 2
+    while distance:
+        near += [
+            (j ^ distance, half, Exchange(output_pieces[j, half], distance))
+            for j, half in output_pieces
+        ]
+        if distance > 1:
+            for j, half, exchange in near:
+                window([exchange], lambda: ())
+                output_pieces[j, half] = exchange.received
+            near = []
+        distance //= 2
+    back_last = window(
+        [exchange for _, _, exchange in near],
+        lambda gback, uback: expert_back(gback, uback, gate_weight, up_weight, 1, chunks),
+        gback_all,
+        uback_all,
+    )
+    for j, half, exchange in near:
+        output_pieces[j, half] = exchange.received
+
+    def piece_start(j, half):
+        return (replica ^ j) * column_share + half * piece_width
 
     back_parts = {1: back_last}
 
@@ -571,14 +611,13 @@
     code_own = route_code
     gates_own = gate_table(second_input, code_own)
 
-    second_ring = RingSum(back_block, row_count)
-    second_ring.start()
-    (gback_tied, uback_tied), _ = tie((gback_all, uback_all), second_ring.sent)
-    second_ring.received, back_parts[0] = tie(
-        second_ring.received,
-        expert_back(gback_tied, uback_tied, gate_weight, up_weight, 0, chunks),
-    )
-    second_ring.finish()
+    back_ring = RingSum(back_block, row_count)
+    back_parts[0] = window(
+        [back_ring],
+        lambda gback, uback: expert_back(gback, uback, gate_weight, up_weight, 0, chunks),
+        gback_all,
+        uback_all,
+    )
 
     def mixture_work(inner, pair):
         return (
@@ -586,10 +625,8 @@
             swap_all(reorder(pair, slot_of_device)),
         )
 
-    mixture_part, pair_grad = window([second_ring], mixture_work, inner_all, pair_sent)
-    mixture_ring = RingSum(
-        lambda slot: mixture_part[slot * row_count : (slot + 1) * row_count], row_count
-    )
+    mixture_part, pair_grad = window([back_ring], mixture_work, inner_all, pair_sent)
+    mixture_ring = RingSum(slot_rows(mixture_part), row_count)
 
     def down_work(inner, pair):
         pair_grad = pair.transpose(1, 0, 2).reshape(row_count, expert_total)
@@ -602,12 +639,10 @@
         return grad_of(inner, cot_all), router_back, router_part
 
     down_part, router_back, router_part = window(
-        [second_ring, mixture_ring], down_work, inner_all, pair_grad
-    )
-    gate_part = window(
-        [second_ring, mixture_ring], lambda gback: grad_of(second_all, gback), gback_all
-    )
-    second_scattered = second_ring.total()
+        [back_ring, mixture_ring], down_work, inner_all, pair_grad
+    )
+    window([back_ring, mixture_ring], lambda: ())
+    second_scattered = back_ring.total()
     second_grad = router_back + second_scattered
     upstream = valid_own * cotangent.astype(wide_type)
     def residual_work(second_grad):
@@ -634,18 +669,24 @@
     swap_sent, residual_grad, attention_low, postnorm_part = window(
         [mixture_ring], residual_work, second_grad
     )
-    attention_all = gather_rows(attention_low)
-    mixed_swapped = swap_all(swap_sent)
-    up_part = window([mixture_ring], lambda uback: grad_of(second_all, uback), uback_all)
+    class Swap(Exchange):
+        def start(self):
+            self.received = swap_all(self.sent)
+
+    swap = Swap(swap_sent, 0)
+    gate_part, up_part = window(
+        [mixture_ring, swap],
+        lambda gback, uback: (grad_of(second_all, gback), grad_of(second_all, uback)),
+        gback_all,
+        uback_all,
+    )
     mixture = mixture_ring.total()
     layer_out = (valid_own * (residual + mixture)).astype(low_type)
-    mixed_swapped, up_part = tie(mixed_swapped, up_part)
-    mixed_grad = reorder_rows(mixed_swapped.reshape(group_rows, width_here), device_of_slot)
+    mixed_grad = reorder_rows(swap.received.reshape(group_rows, width_here), device_of_slot)
 
     def head_backward(head, grad_head):
-        (query_raw, key_raw, query_inverse, key_inverse, query_low, key_low, value_low, log_total) = (
-            kept_heads[head]
-        )
+        query_raw, key_raw, query_low, key_low, value_low, log_total = kept_heads[head]
+        query_inverse, key_inverse = inverse_rms(query_raw), inverse_rms(key_raw)
         scores = jnp.where(allowed, mm(query_low, key_low, 1, 1) * score_scale, masked_value)
         weights = jnp.exp(scores - log_total)
         weight_grad = mm(grad_head, value_low, 1, 1)
@@ -670,10 +711,16 @@
             jnp.sum(key_gain_part, axis=0),
         )
 
-    head_results = [
-        head_backward(head, mixed_grad[:, head * head_dim : (head + 1) * head_dim])
-        for head in range(heads_here)
-    ]
+    attention_gather = RingGather(attention_low)
+    head_results = []
+    for head in range(heads_here):
+        head_results.append(
+            window(
+                [attention_gather],
+                lambda grad_head: head_backward(head, grad_head),
+                mixed_grad[:, head * head_dim : (head + 1) * head_dim],
+            )
+        )
     sent = jnp.concatenate(
         [head_results[head][part] for part in range(3) for head in range(heads_here)], axis=1
     )
@@ -686,9 +733,14 @@
     sent, down_sum = tie(sent, down_sum)
     querynorm_part = sum(result[3] for result in head_results)
     keynorm_part = sum(result[4] for result in head_results)
-    first_part = mm(sent, head_weight, 1, 1)
-    prenorm_part = jnp.sum(first_part * token_wide * inverse_all, axis=0)
-    first_low = first_part.astype(low_type)
+    def first_work(sent):
+        first_part = mm(sent, head_weight, 1, 1)
+        prenorm_part = jnp.sum(first_part * token_wide * inverse_all, axis=0)
+        return first_part.astype(low_type), prenorm_part
+
+    while attention_gather.step < group_count // 2 - 2:
+        window([attention_gather], lambda: ())
+    first_low, prenorm_part = window([attention_gather], first_work, sent)
 
     def small_swap(parts):
         return swap_all(
@@ -704,17 +756,10 @@
             start += size
         return pieces
 
-    first_ring = RingSum(
-        lambda slot: first_low[slot * row_count : (slot + 1) * row_count], row_count
-    )
-    head_part, output_part = window(
-        [first_ring],
-        lambda first, sent, mixed, attention: (grad_of(first, sent), grad_of(mixed, attention)),
-        first_all,
-        sent,
-        mixed_ordered,
-        attention_all,
-    )
+    first_ring = RingSum(slot_rows(first_low), row_count)
+    head_part = window([attention_gather, first_ring], grad_of, first_all, sent)
+    attention_all = jnp.concatenate(attention_gather.blocks, axis=0)
+    output_part = grad_of(mixed_low, attention_all)
     small_parts = [router_part, postnorm_part, prenorm_part, querynorm_part, keynorm_part]
     head_rows, output_rows, small_swapped = window(
         [first_ring],

time: 851 us -> 871 us (1.024)
  waiting for transfers between devices: 296 us -> 254 us
  local copies, waits for them, and re-layouts: 72.3 us -> 114 us
  starting transfers between devices: 90 us -> 117 us
  matrix products: 173 us -> 147 us
  other arithmetic: 120 us -> 138 us
    ppermute x40 -> x56, waiting for transfers between devices: 49.8 us -> 135 us  [ring_shift(): return lax.ppermute(values, 'ep', pairs)]
    reduce_scatter x1, waiting for transfers between devices: 36.3 us -> 0.01 us  [body(): up_sum = lax.psum_scatter(up_part, 'rep', scatter_dimension=0, tiled=True)]
    all_gather x4 -> x2, waiting for transfers between devices: 62.4 us -> 26.4 us  [gather_rows(): return lax.all_gather(values, 'ep', axis=0, tiled=True)]
    all_to_all x7 -> x6, waiting for transfers between devices: 53.6 us -> 23.3 us  [swap_all(): return lax.all_to_all(values, 'ep', split_axis=0, concat_axis=0, tiled=True)]
    unnamed x308 -> x457, local copies, waits for them, and re-layouts: 31.3 us -> 60.1 us
    ppermute x40 -> x56, starting transfers between devices: 45.7 us -> 74 us  [ring_shift(): return lax.ppermute(values, 'ep', pairs)]
    dot_general x43 -> x37, matrix products: 173 us -> 147 us  [mm(): lax.dot_general(left, right, (((left_dim,), (right_dim,)), ((), ())), pre...]
    ppermute x18, waiting for transfers between devices: 93.3 us -> 68.9 us  [rep_exchange(): lax.ppermute(values, 'rep', [(i, i ^ distance) for i in range(count)])]
  transfers between devices with their start and end apart: 72 -> 85, of which waited for: 28 -> 32; matrix products, arithmetic and copies ran while one was open for 39% -> 41% of each run, Pallas kernels for 4% -> 8%
where the time goes in v6:
time: 871 us; the launch traced here: 861 us
  waiting for transfers between devices  254 us (29%)
  matrix products  147 us (17%)
  other arithmetic  138 us (16%)
  starting transfers between devices  117 us (13%)
  local copies, waits for them, and re-layouts  114 us (13%)
  Pallas kernels  72.7 us (8%)
  between operations  17.7 us (2%)
    dot_general x37, matrix products, mm(): lax.dot_general(left, right, (((left_dim,), (right_dim,)), ((), ())), pre...  147 us
    ppermute x56, waiting for transfers between devices, ring_shift(): return lax.ppermute(values, 'ep', pairs)  135 us
    ppermute x56, starting transfers between devices, ring_shift(): return lax.ppermute(values, 'ep', pairs)  74 us
    ppermute x18, waiting for transfers between devices, rep_exchange(): lax.ppermute(values, 'rep', [(i, i ^ distance) for i in range(count)])  68.9 us
    unnamed x457, local copies, waits for them, and re-layouts  60.1 us
    pallas_call x2, Pallas kernels, expert_pass(): pl.pallas_call(expert_kernel, grid=(experts, steps), in_specs=[pl.BlockSp...  39.1 us
    pallas_call x2, Pallas kernels, expert_back(): pl.pallas_call(expert_back_kernel, grid=(depth // width,), in_specs=[whol...  33.6 us
    all_to_all x6, starting transfers between devices, swap_all(): return lax.all_to_all(values, 'ep', split_axis=0, concat_axis=0, tiled=True)  33 us
  transfers between devices with their start and end apart: 85, of which 32 were waited for; matrix products, arithmetic and copies ran while one was open for 41% of the time, Pallas kernels for 8%

profile of v6, /device:TPU:0, one launch (start us, length us, event | category | flops | bytes accessed | tf_op | source)
XLA Modules:
  0.0 860.7 jit_solution(15297306767149667188)
XLA Ops:
  10.7 7.3 all-to-all-start
  21.1 23.7 %collective-permute-done = bf16[160,2048]{1,0:T(8,128)(2,1)S(1)} collective-permute-done((bf16[160,2048]{1,0:T(8,128)(2,1)S(1)}, bf16[160,2048]{1,0:T(8,128)(2,1)S(1)}, u32[]{:S(2)}, u32[]{:S(2)}) %collective-permute-start) | collective-permute-done | bytes 655392 | tf_op jit(solution)/shard_map/ppermute | solution.py:86
  49.2 16.2 %collective-permute-done.4 = bf16[1,8,64,768]{3,2,1,0:T(8,128)(2,1)} collective-permute-done((bf16[1,8,64,768]{3,2,1,0:T(8,128)(2,1)S(1)}, bf16[1,8,64,768]{3,2,1,0:T(8,128)(2,1)}, u32[]{:S(2)}, u32[]{:S(2)}) %collective-permute-start.4) | collective-permute-done | bytes 786464 | tf_op jit(solution)/shard_map/ppermute | solution.py:198
  65.4 2.8 maximum_select_fusion.3
  71.4 5.8 collective-permute-start.2
  77.9 5.5 all-to-all-start.1
  89.1 3.6 maximum_select_fusion
  92.8 5.1 all-to-all-done.1
  102.1 2.6 constant_dynamic-update-slice_fusion.56
  110.4 3.6 collective-permute-done.6
  129.0 3.1 fusion.131
  151.4 2.4 copy-done.7
  165.4 3.2 collective-permute-done.10
  168.6 8.1 collective-permute-done.11
  192.3 26.1 %collective-permute-done.13 = bf16[160,2048]{1,0:T(8,128)(2,1)} collective-permute-done((bf16[160,2048]{1,0:T(8,128)(2,1)S(1)}, bf16[160,2048]{1,0:T(8,128)(2,1)}, u32[]{:S(2)}, u32[]{:S(2)}) %collective-permute-start.13) | collective-permute-done | bytes 655392 | tf_op jit(solution)/shard_map/ppermute | solution.py:86
  218.4 3.1 add_convert_fusion.15
  221.4 4.4 collective-permute-start.14
  225.8 5.9 collective-permute-start.15
  232.1 16.3 %collective-permute-done.14 = bf16[160,2048]{1,0:T(8,128)(2,1)S(1)} collective-permute-done((bf16[160,2048]{1,0:T(8,128)(2,1)}, bf16[160,2048]{1,0:T(8,128)(2,1)S(1)}, u32[]{:S(2)}, u32[]{:S(2)}) %collective-permute-start.14) | collective-permute-done | bytes 655392 | tf_op jit(solution)/shard_map/ppermute | solution.py:86
  255.5 10.9 %collective-permute-done.16 = bf16[160,2048]{1,0:T(8,128)(2,1)S(1)} collective-permute-done((bf16[160,2048]{1,0:T(8,128)(2,1)S(1)}, bf16[160,2048]{1,0:T(8,128)(2,1)S(1)}, u32[]{:S(2)}, u32[]{:S(2)}) %collective-permute-start.16) | collective-permute-done | bytes 655392 | tf_op jit(solution)/shard_map/ppermute | solution.py:86
  278.6 9.5 %fusion.138.stream_ref = f32[640,2048]{1,0:T(8,128)} fusion(bf16[640,2048]{1,0:T(8,128)(2,1)S(1)} %bitcast.194, bf16[2048,2048]{1,0:T(8,128)(2,1)} %bitcast.284), kind=kOutput, calls=%fused_computation.500 | convolution fusion | flops 5368709120 | bytes 16252928 | tf_op jit(solution)/shard_map/dot_general | solution.py:58
  297.7 9.5 %fusion.139.stream_ref = f32[640,2048]{1,0:T(8,128)} fusion(bf16[640,2048]{1,0:T(8,128)(2,1)S(1)} %bitcast.195, bf16[2048,2048]{1,0:T(8,128)(2,1)} %bitcast.285), kind=kOutput, calls=%fused_computation.501 | convolution fusion | flops 5368709120 | bytes 16252928 | tf_op jit(solution)/shard_map/dot_general | solution.py:58
  316.5 2.7 pad_maximum_fusion.4.rows_ref
  319.2 26.4 %all-gather.5.cloned.1.call-done = bf16[2048,512]{1,0:T(8,128)(2,1)} async-done(((bf16[256,512]{1,0:T(8,128)(2,1)}), bf16[2048,512]{1,0:T(8,128)(2,1)}) %all-gather.5.cloned.1.call-update) | async-done | bytes 2097168 | tf_op jit(solution)/shard_map/all_gather | solution.py:67
  345.5 3.1 fusion.117
  353.0 19.6 %shard_map.281 = (bf16[1280,2048]{1,0:T(8,128)(2,1)}, bf16[1280,2048]{1,0:T(8,128)(2,1)}, bf16[1280,2048]{1,0:T(8,128)(2,1)}, f32[2,640,128]{2,1,0:T(8,128)}) custom-call(bf16[640,2048]{1,0:T(8,128)(2,1)} %pad_maximum_fusion.4.rows_ref, bf16[2,2048,1024]{2,1,0:T(8,128)(2,1)} %gate_ref.7, bf16[2,2048,1024]{2,1,0:T(8,128)(2,1)} %up_ref.7, ...), custom_call_target="tpu_custom_call" | custom-call | flops 10737418240 | bytes 42991616 | tf_op jit(solution)/shard_map/pallas_call | solution.py:285
  388.9 19.5 %shard_map.282 = (bf16[1280,2048]{1,0:T(8,128)(2,1)}, bf16[1280,2048]{1,0:T(8,128)(2,1)}, bf16[1280,2048]{1,0:T(8,128)(2,1)}, f32[2,640,128]{2,1,0:T(8,128)}) custom-call(bf16[640,2048]{1,0:T(8,128)(2,1)} %copy-done.48, bf16[2,2048,1024]{2,1,0:T(8,128)(2,1)} %gate_ref.7, ...), custom_call_target="tpu_custom_call", output_to_operand_aliasing={{0}: (5, {}), {1}: (6, {}), {2}: (7, {})} | custom-call | flops 10737418240 | bytes 42991616 | tf_op jit(solution)/shard_map/pallas_call | solution.py:285
  411.5 16.8 %shard_map.283 = bf16[640,2048]{1,0:T(8,128)(2,1)} custom-call(bf16[1280,2048]{1,0:T(8,128)(2,1)} %get-tuple-element.311.gback_ref, bf16[1280,2048]{1,0:T(8,128)(2,1)} %get-tuple-element.312.uback_ref, bf16[2,2048,1024]{2,1,0:T(8,128)(2,1)} %gate_ref.7, bf16[2,2048,1024]{2,1,0:T(8,128)(2,1)} %up_ref.7), custom_call_target="tpu_custom_call" | custom-call | flops 10737418240 | bytes 24641536 | tf_op jit(solution)/shard_map/pallas_call | solution.py:325
  432.2 16.8 %shard_map.284 = bf16[640,2048]{1,0:T(8,128)(2,1)} custom-call(bf16[1280,2048]{1,0:T(8,128)(2,1)} %get-tuple-element.311.gback_ref, bf16[1280,2048]{1,0:T(8,128)(2,1)} %get-tuple-element.312.uback_ref, bf16[2,2048,1024]{2,1,0:T(8,128)(2,1)} %gate_ref.7, bf16[2,2048,1024]{2,1,0:T(8,128)(2,1)} %up_ref.7), custom_call_target="tpu_custom_call" | custom-call | flops 10737418240 | bytes 24641536 | tf_op jit(solution)/shard_map/pallas_call | solution.py:325
  454.3 3.8 all-to-all-start.2
  458.7 16.5 %convolution_convert_fusion.3 = bf16[1280,2048]{1,0:T(8,128)(2,1)} fusion(bf16[1280,2048]{1,0:T(8,128)(2,1)} %get-tuple-element.292, bf16[2048,2048]{1,0:T(8,128)(2,1)} %bitcast.286), kind=kOutput, calls=%fused_computation.12 | convolution fusion | flops 10740039680 | bytes 18874368 | tf_op jit(solution)/shard_map/dot_general | solution.py:58
  485.2 16.7 %convolution_convert_fusion.2 = bf16[2048,2048]{1,0:T(8,128)(2,1)} fusion(bf16[1280,2048]{1,0:T(8,128)(2,1)} %get-tuple-element.292, bf16[1280,2048]{1,0:T(8,128)(2,1)} %bitcast.213), kind=kOutput, calls=%fused_computation.11 | convolution fusion | flops 10741612544 | bytes 18874368 | tf_op jit(solution)/shard_map/dot_general | solution.py:58
  509.8 2.9 add_convert_fusion.9
  515.5 9.2 %collective-permute-done.43 = bf16[160,2048]{1,0:T(8,128)(2,1)} collective-permute-done((bf16[160,2048]{1,0:T(8,128)(2,1)}, bf16[160,2048]{1,0:T(8,128)(2,1)}, u32[]{:S(2)}, u32[]{:S(2)}) %collective-permute-start.43) | collective-permute-done | bytes 655392 | tf_op jit(solution)/shard_map/ppermute | solution.py:86
  524.7 3.0 collective-permute-done.42
  527.7 10.3 %collective-permute-done.40 = bf16[160,2048]{1,0:T(8,128)(2,1)S(1)} collective-permute-done((bf16[160,2048]{1,0:T(8,128)(2,1)}, bf16[160,2048]{1,0:T(8,128)(2,1)S(1)}, u32[]{:S(2)}, u32[]{:S(2)}) %collective-permute-start.40) | collective-permute-done | bytes 655392 | tf_op jit(solution)/shard_map/ppermute | solution.py:86
  538.0 2.5 add_convert_fusion.7
  560.6 2.8 add_convert_fusion.5
  565.4 4.7 all-to-all-start.3
  570.2 16.7 %convolution_convert_fusion = bf16[2048,2048]{1,0:T(8,128)(2,1)} fusion(bf16[1280,2048]{1,0:T(8,128)(2,1)} %get-tuple-element.636, bf16[1280,2048]{1,0:T(8,128)(2,1)} %get-tuple-element.312.uback_ref), kind=kOutput, calls=%fused_computation.9 | convolution fusion | flops 10741612544 | bytes 18874368 | tf_op jit(solution)/shard_map/dot_general | solution.py:58
  586.9 16.6 %convolution_convert_fusion.1 = bf16[2048,2048]{1,0:T(8,128)(2,1)} fusion(bf16[1280,2048]{1,0:T(8,128)(2,1)} %get-tuple-element.636, bf16[1280,2048]{1,0:T(8,128)(2,1)} %get-tuple-element.311.gback_ref), kind=kOutput, calls=%fused_computation.10 | convolution fusion | flops 10741612544 | bytes 18874368 | tf_op jit(solution)/shard_map/dot_general | solution.py:58
  605.8 3.7 fusion.2
  609.9 3.3 pad_maximum_fusion
  643.2 3.7 multiply_reduce_fusion.5
  661.3 8.5 fusion.1
  674.1 7.4 convolution_convert_fusion.5
  687.1 5.2 convolution_convert_fusion.6
  693.5 3.4 collective-permute-done.62
  706.2 5.8 all-to-all-start.4
  714.1 6.4 all-to-all-done.4
  720.5 28.5 %collective-permute-done.63 = bf16[1,64,2048]{2,1,0:T(8,128)(2,1)} collective-permute-done((bf16[1,64,2048]{2,1,0:T(8,128)(2,1)}, bf16[1,64,2048]{2,1,0:T(8,128)(2,1)}, u32[]{:S(2)}, u32[]{:S(2)}) %collective-permute-start.63) | collective-permute-done | bytes 262176 | tf_op jit(solution)/shard_map/ppermute | solution.py:198
  752.4 3.1 add_convert_fusion.3
  755.4 2.4 collective-permute-start.66
  757.9 5.9 all-to-all-start.5
  767.2 4.0 collective-permute-done.69
  773.5 11.8 %all-to-all-done.5 = bf16[8,64,768]{2,1,0:T(8,128)(2,1)S(1)} async-done(((bf16[8,64,768]{2,1,0:T(8,128)(2,1)}), bf16[8,64,768]{2,1,0:T(8,128)(2,1)S(1)}, u32[]{:S(2)}, u32[]{:S(2)}) %all-to-all-start.5) | async-done | bytes 786464 | tf_op jit(solution)/shard_map/all_to_all | solution.py:241
  792.6 3.3 add_convert_fusion.1
  796.2 2.9 multiply_convert_fusion.2
  799.1 2.5 convert_element_type.662
  801.7 12.9 %collective-permute-done.72 = bf16[1,3,64,2048]{3,2,1,0:T(8,128)(2,1)S(1)} collective-permute-done((bf16[1,3,64,2048]{3,2,1,0:T(8,128)(2,1)S(1)}, bf16[1,3,64,2048]{3,2,1,0:T(8,128)(2,1)S(1)}, u32[]{:S(2)}, u32[]{:S(2)}) %collective-permute-start.72) | collective-permute-done | bytes 786464 | tf_op jit(solution)/shard_map/ppermute | solution.py:198
  820.8 5.1 collective-permute-start.70
  831.1 2.4 maximum_select_fusion.1
  834.0 7.0 collective-permute-done.70
  850.5 3.2 fusion.22
  (841 shorter events, 311.4 us)
Async XLA Ops:
  10.7 36.4 %all-to-all-start = ((bf16[8,64,768]{2,1,0:T(8,128)(2,1)}), bf16[8,64,768]{2,1,0:T(8,128)(2,1)S(1)}, u32[]{:S(2)}, u32[]{:S(2)}) async-start(bf16[8,64,768]{2,1,0:T(8,128)(2,1)} %copy.137), calls=%async_computation | async-start | bytes 1572864 | tf_op jit(solution)/shard_map/all_to_all | solution.py:241
  17.9 26.8 %collective-permute-start = (bf16[160,2048]{1,0:T(8,128)(2,1)S(1)}, bf16[160,2048]{1,0:T(8,128)(2,1)S(1)}, u32[]{:S(2)}, u32[]{:S(2)}) collective-permute-start(bf16[160,2048]{1,0:T(8,128)(2,1)S(1)} %copy-done.8), channel_id=1, source_target_pairs={{0,2},{2,4},{4,6},{6,7},{7,5},{5,3},{3,1},{1,0},{8,10},{10,12},{12... | collective-permute-start | bytes 1966088 | tf_op jit(solution)/shard_map/ppermute | solution.py:86
  19.9 27.2 %collective-permute-start.1 = (bf16[160,2048]{1,0:T(8,128)(2,1)S(1)}, bf16[160,2048]{1,0:T(8,128)(2,1)}, u32[]{:S(2)}, u32[]{:S(2)}) collective-permute-start(bf16[160,2048]{1,0:T(8,128)(2,1)S(1)} %copy-done.8), channel_id=1, source_target_pairs={{0,1},{2,0},{4,2},{6,4},{7,6},{5,7},{3,5},{1,3},{8,9},{10,8},{12,1... | collective-permute-start | bytes 1966088 | tf_op jit(solution)/shard_map/ppermute | solution.py:86
  47.1 18.2 %collective-permute-start.4 = (bf16[1,8,64,768]{3,2,1,0:T(8,128)(2,1)S(1)}, bf16[1,8,64,768]{3,2,1,0:T(8,128)(2,1)}, u32[]{:S(2)}, u32[]{:S(2)}) collective-permute-start(bf16[1,8,64,768]{3,2,1,0:T(8,128)(2,1)S(1)} %bitcast.167), channel_id=1, source_target_pairs={{0,16},{8,24},{16,0},{24,8},{1,17},{9,25},{17,1},{25,9},{2,18},{10... | collective-permute-start | bytes 2359304 | tf_op jit(solution)/shard_map/ppermute | solution.py:198
  68.1 21.0 %collective-permute-start.5 = (bf16[2,8,64,768]{3,2,1,0:T(8,128)(2,1)}, bf16[2,8,64,768]{3,2,1,0:T(8,128)(2,1)}, u32[]{:S(2)}, u32[]{:S(2)}) collective-permute-start(bf16[2,8,64,768]{3,2,1,0:T(8,128)(2,1)} %maximum_select_fusion.3), channel_id=1, source_target_pairs={{0,8},{8,0},{16,24},{24,16},{1,9},{9,1},{17,25},{25,17},{2,10},{10... | collective-permute-start | bytes 4718600 | tf_op jit(solution)/shard_map/ppermute | solution.py:198
  71.4 26.4 %collective-permute-start.2 = (bf16[160,2048]{1,0:T(8,128)(2,1)}, bf16[160,2048]{1,0:T(8,128)(2,1)}, u32[]{:S(2)}, u32[]{:S(2)}) collective-permute-start(bf16[160,2048]{1,0:T(8,128)(2,1)} %copy-done.25), channel_id=1, source_target_pairs={{0,2},{2,4},{4,6},{6,7},{7,5},{5,3},{3,1},{1,0},{8,10},{10,12},{12... | collective-permute-start | bytes 1966088 | tf_op jit(solution)/shard_map/ppermute | solution.py:86
  77.2 20.6 %collective-permute-start.3 = (bf16[160,2048]{1,0:T(8,128)(2,1)}, bf16[160,2048]{1,0:T(8,128)(2,1)}, u32[]{:S(2)}, u32[]{:S(2)}) collective-permute-start(bf16[160,2048]{1,0:T(8,128)(2,1)} %collective-permute-done.1), channel_id=1, source_target_pairs={{0,1},{2,0},{4,2},{6,4},{7,6},{5,7},{3,5},{1,3},{8,9},{10,8},{12,1... | collective-permute-start | bytes 1966088 | tf_op jit(solution)/shard_map/ppermute | solution.py:86
  77.9 20.0 %all-to-all-start.1 = ((bf16[8,52,128]{2,1,0:T(8,128)(2,1)}), bf16[8,52,128]{2,1,0:T(8,128)(2,1)S(1)}, u32[]{:S(2)}, u32[]{:S(2)}) async-start(bf16[8,52,128]{2,1,0:T(8,128)(2,1)} %broadcast_in_dim.202), calls=%async_computation.1 | async-start | bytes 229376 | tf_op jit(solution)/shard_map/all_to_all | solution.py:241
  83.3 190.5 %all-gather.3.cloned.1.call-start = ((), (), s32[]{:S(2)}) async-start(), calls=%async_computation.9 | async-start | bytes 5898240 | tf_op jit(solution)/shard_map/all_gather | solution.py:67
  97.8 16.2 %collective-permute-start.6 = (bf16[160,2048]{1,0:T(8,128)(2,1)}, bf16[160,2048]{1,0:T(8,128)(2,1)S(1)}, u32[]{:S(2)}, u32[]{:S(2)}) collective-permute-start(bf16[160,2048]{1,0:T(8,128)(2,1)} %collective-permute-done.2), channel_id=1, source_target_pairs={{0,2},{2,4},{4,6},{6,7},{7,5},{5,3},{3,1},{1,0},{8,10},{10,12},{12... | collective-permute-start | bytes 1966088 | tf_op jit(solution)/shard_map/ppermute | solution.py:86
  138.0 207.6 %all-gather.5.cloned.1.call-start = ((), (), s32[]{:S(2)}) async-start(), calls=%async_computation.10 | async-start | bytes 2359296 | tf_op jit(solution)/shard_map/all_gather | solution.py:67
  154.7 22.0 %collective-permute-start.11 = (bf16[80,2048]{1,0:T(8,128)(2,1)S(1)}, bf16[80,2048]{1,0:T(8,128)(2,1)}, u32[]{:S(2)}, u32[]{:S(2)}) collective-permute-start(bf16[80,2048]{1,0:T(8,128)(2,1)S(1)} %get-tuple-element.546), channel_id=1, source_target_pairs={{0,1},{2,0},{4,2},{6,4},{7,6},{5,7},{3,5},{1,3},{8,9},{10,8},{12,1... | collective-permute-start | bytes 983048 | tf_op jit(solution)/shard_map/ppermute | solution.py:86
  178.3 40.1 %collective-permute-start.13 = (bf16[160,2048]{1,0:T(8,128)(2,1)S(1)}, bf16[160,2048]{1,0:T(8,128)(2,1)}, u32[]{:S(2)}, u32[]{:S(2)}) collective-permute-start(bf16[160,2048]{1,0:T(8,128)(2,1)S(1)} %pad_maximum_fusion.7), channel_id=1, source_target_pairs={{0,1},{2,0},{4,2},{6,4},{7,6},{5,7},{3,5},{1,3},{8,9},{10,8},{12,1... | collective-permute-start | bytes 1966088 | tf_op jit(solution)/shard_map/ppermute | solution.py:86
  180.4 38.0 %collective-permute-start.12 = (bf16[160,2048]{1,0:T(8,128)(2,1)}, bf16[160,2048]{1,0:T(8,128)(2,1)S(1)}, u32[]{:S(2)}, u32[]{:S(2)}) collective-permute-start(bf16[160,2048]{1,0:T(8,128)(2,1)} %pad_maximum_fusion.6), channel_id=1, source_target_pairs={{0,2},{2,4},{4,6},{6,7},{7,5},{5,3},{3,1},{1,0},{8,10},{10,12},{12... | collective-permute-start | bytes 1966088 | tf_op jit(solution)/shard_map/ppermute | solution.py:86
  221.4 27.0 %collective-permute-start.14 = (bf16[160,2048]{1,0:T(8,128)(2,1)}, bf16[160,2048]{1,0:T(8,128)(2,1)S(1)}, u32[]{:S(2)}, u32[]{:S(2)}) collective-permute-start(bf16[160,2048]{1,0:T(8,128)(2,1)} %get-tuple-element.543), channel_id=1, source_target_pairs={{0,2},{2,4},{4,6},{6,7},{7,5},{5,3},{3,1},{1,0},{8,10},{10,12},{12... | collective-permute-start | bytes 1966088 | tf_op jit(solution)/shard_map/ppermute | solution.py:86
  225.8 24.3 %collective-permute-start.15 = (bf16[160,2048]{1,0:T(8,128)(2,1)}, bf16[160,2048]{1,0:T(8,128)(2,1)}, u32[]{:S(2)}, u32[]{:S(2)}) collective-permute-start(bf16[160,2048]{1,0:T(8,128)(2,1)} %get-tuple-element.542), channel_id=1, source_target_pairs={{0,1},{2,0},{4,2},{6,4},{7,6},{5,7},{3,5},{1,3},{8,9},{10,8},{12,1... | collective-permute-start | bytes 1966088 | tf_op jit(solution)/shard_map/ppermute | solution.py:86
  270.2 20.7 %collective-permute-start.19 = (bf16[160,2048]{1,0:T(8,128)(2,1)S(1)}, bf16[160,2048]{1,0:T(8,128)(2,1)S(1)}, u32[]{:S(2)}, u32[]{:S(2)}) collective-permute-start(bf16[160,2048]{1,0:T(8,128)(2,1)S(1)} %get-tuple-element.487), channel_id=1, source_target_pairs={{0,2},{2,4},{4,6},{6,7},{7,5},{5,3},{3,1},{1,0},{8,10},{10,12},{12... | collective-permute-start | bytes 1966088 | tf_op jit(solution)/shard_map/ppermute | solution.py:86
  271.6 19.3 %collective-permute-start.20 = (bf16[160,2048]{1,0:T(8,128)(2,1)S(1)}, bf16[160,2048]{1,0:T(8,128)(2,1)}, u32[]{:S(2)}, u32[]{:S(2)}) collective-permute-start(bf16[160,2048]{1,0:T(8,128)(2,1)S(1)} %get-tuple-element.487), channel_id=1, source_target_pairs={{0,1},{2,0},{4,2},{6,4},{7,6},{5,7},{3,5},{1,3},{8,9},{10,8},{12,1... | collective-permute-start | bytes 1966088 | tf_op jit(solution)/shard_map/ppermute | solution.py:86
  291.0 19.2 %collective-permute-start.21 = (bf16[160,2048]{1,0:T(8,128)(2,1)S(1)}, bf16[160,2048]{1,0:T(8,128)(2,1)}, u32[]{:S(2)}, u32[]{:S(2)}) collective-permute-start(bf16[160,2048]{1,0:T(8,128)(2,1)S(1)} %collective-permute-done.19), channel_id=1, source_target_pairs={{0,2},{2,4},{4,6},{6,7},{7,5},{5,3},{3,1},{1,0},{8,10},{10,12},{12... | collective-permute-start | bytes 1966088 | tf_op jit(solution)/shard_map/ppermute | solution.py:86
  292.4 17.7 %collective-permute-start.22 = (bf16[160,2048]{1,0:T(8,128)(2,1)}, bf16[160,2048]{1,0:T(8,128)(2,1)}, u32[]{:S(2)}, u32[]{:S(2)}) collective-permute-start(bf16[160,2048]{1,0:T(8,128)(2,1)} %collective-permute-done.20), channel_id=1, source_target_pairs={{0,1},{2,0},{4,2},{6,4},{7,6},{5,7},{3,5},{1,3},{8,9},{10,8},{12,1... | collective-permute-start | bytes 1966088 | tf_op jit(solution)/shard_map/ppermute | solution.py:86
  310.1 62.4 %collective-permute-start.23 = (bf16[160,2048]{1,0:T(8,128)(2,1)}, bf16[160,2048]{1,0:T(8,128)(2,1)S(1)}, u32[]{:S(2)}, u32[]{:S(2)}) collective-permute-start(bf16[160,2048]{1,0:T(8,128)(2,1)} %collective-permute-done.21), channel_id=1, source_target_pairs={{0,2},{2,4},{4,6},{6,7},{7,5},{5,3},{3,1},{1,0},{8,10},{10,12},{12... | collective-permute-start | bytes 1966088 | tf_op jit(solution)/shard_map/ppermute | solution.py:86
  311.5 61.4 %collective-permute-start.24 = (bf16[160,2048]{1,0:T(8,128)(2,1)}, bf16[160,2048]{1,0:T(8,128)(2,1)}, u32[]{:S(2)}, u32[]{:S(2)}) collective-permute-start(bf16[160,2048]{1,0:T(8,128)(2,1)} %collective-permute-done.22), channel_id=1, source_target_pairs={{0,1},{2,0},{4,2},{6,4},{7,6},{5,7},{3,5},{1,3},{8,9},{10,8},{12,1... | collective-permute-start | bytes 1966088 | tf_op jit(solution)/shard_map/ppermute | solution.py:86
  348.7 26.3 %collective-permute-start.25 = (bf16[2048,256]{1,0:T(8,128)(2,1)}, bf16[2048,256]{1,0:T(8,128)(2,1)}, u32[]{:S(2)}, u32[]{:S(2)}) collective-permute-start(bf16[2048,256]{1,0:T(8,128)(2,1)} %get-tuple-element.566), channel_id=1, source_target_pairs={{0,16},{8,24},{16,0},{24,8},{1,17},{9,25},{17,1},{25,9},{2,18},{10... | collective-permute-start | bytes 3145736 | tf_op jit(solution)/shard_map/ppermute | solution.py:198
  350.1 78.3 %collective-permute-start.18 = (bf16[2048,256]{1,0:T(8,128)(2,1)}, bf16[2048,256]{1,0:T(8,128)(2,1)}, u32[]{:S(2)}, u32[]{:S(2)}) collective-permute-start(bf16[2048,256]{1,0:T(8,128)(2,1)} %get-tuple-element.566), channel_id=1, source_target_pairs={{0,8},{8,0},{16,24},{24,16},{1,9},{9,1},{17,25},{25,17},{2,10},{10... | collective-permute-start | bytes 3145736 | tf_op jit(solution)/shard_map/ppermute | solution.py:198
  350.1 58.4 %collective-permute-start.28 = (bf16[2048,256]{1,0:T(8,128)(2,1)}, bf16[2048,256]{1,0:T(8,128)(2,1)S(1)}, u32[]{:S(2)}, u32[]{:S(2)}) collective-permute-start(bf16[2048,256]{1,0:T(8,128)(2,1)} %get-tuple-element.565), channel_id=1, source_target_pairs={{0,16},{8,24},{16,0},{24,8},{1,17},{9,25},{17,1},{25,9},{2,18},{10... | collective-permute-start | bytes 3145736 | tf_op jit(solution)/shard_map/ppermute | solution.py:198
  372.6 55.8 %collective-permute-start.27 = (bf16[2048,256]{1,0:T(8,128)(2,1)}, bf16[2048,256]{1,0:T(8,128)(2,1)}, u32[]{:S(2)}, u32[]{:S(2)}) collective-permute-start(bf16[2048,256]{1,0:T(8,128)(2,1)} %get-tuple-element.565), channel_id=1, source_target_pairs={{0,8},{8,0},{16,24},{24,16},{1,9},{9,1},{17,25},{25,17},{2,10},{10... | collective-permute-start | bytes 3145736 | tf_op jit(solution)/shard_map/ppermute | solution.py:198
  383.3 45.1 %collective-permute-start.26 = (bf16[2048,256]{1,0:T(8,128)(2,1)}, bf16[2048,256]{1,0:T(8,128)(2,1)}, u32[]{:S(2)}, u32[]{:S(2)}) collective-permute-start(bf16[2048,256]{1,0:T(8,128)(2,1)} %collective-permute-done.25), channel_id=1, source_target_pairs={{0,8},{8,0},{16,24},{24,16},{1,9},{9,1},{17,25},{25,17},{2,10},{10... | collective-permute-start | bytes 3145736 | tf_op jit(solution)/shard_map/ppermute | solution.py:198
  411.2 17.2 %collective-permute-start.31 = (bf16[2048,256]{1,0:T(8,128)(2,1)}, bf16[2048,256]{1,0:T(8,128)(2,1)S(1)}, u32[]{:S(2)}, u32[]{:S(2)}) collective-permute-start(bf16[2048,256]{1,0:T(8,128)(2,1)} %copy-done.88), channel_id=1, source_target_pairs={{0,8},{8,0},{16,24},{24,16},{1,9},{9,1},{17,25},{25,17},{2,10},{10... | collective-permute-start | bytes 3145736 | tf_op jit(solution)/shard_map/ppermute | solution.py:198
  430.1 18.9 %collective-permute-start.32 = (bf16[80,2048]{1,0:T(8,128)(2,1)S(1)}, bf16[80,2048]{1,0:T(8,128)(2,1)S(1)}, u32[]{:S(2)}, u32[]{:S(2)}) collective-permute-start(bf16[80,2048]{1,0:T(8,128)(2,1)S(1)} %get-tuple-element.558), channel_id=1, source_target_pairs={{0,2},{2,4},{4,6},{6,7},{7,5},{5,3},{3,1},{1,0},{8,10},{10,12},{12... | collective-permute-start | bytes 983048 | tf_op jit(solution)/shard_map/ppermute | solution.py:86
  431.2 17.8 %collective-permute-start.33 = (bf16[80,2048]{1,0:T(8,128)(2,1)S(1)}, bf16[80,2048]{1,0:T(8,128)(2,1)S(1)}, u32[]{:S(2)}, u32[]{:S(2)}) collective-permute-start(bf16[80,2048]{1,0:T(8,128)(2,1)S(1)} %get-tuple-element.557), channel_id=1, source_target_pairs={{0,1},{2,0},{4,2},{6,4},{7,6},{5,7},{3,5},{1,3},{8,9},{10,8},{12,1... | collective-permute-start | bytes 983048 | tf_op jit(solution)/shard_map/ppermute | solution.py:86
  450.4 24.9 %collective-permute-start.35 = (bf16[160,2048]{1,0:T(8,128)(2,1)S(1)}, bf16[160,2048]{1,0:T(8,128)(2,1)}, u32[]{:S(2)}, u32[]{:S(2)}) collective-permute-start(bf16[160,2048]{1,0:T(8,128)(2,1)S(1)} %pad_maximum_fusion.9), channel_id=1, source_target_pairs={{0,1},{2,0},{4,2},{6,4},{7,6},{5,7},{3,5},{1,3},{8,9},{10,8},{12,1... | collective-permute-start | bytes 1966088 | tf_op jit(solution)/shard_map/ppermute | solution.py:86
  452.8 22.4 %collective-permute-start.34 = (bf16[160,2048]{1,0:T(8,128)(2,1)}, bf16[160,2048]{1,0:T(8,128)(2,1)S(1)}, u32[]{:S(2)}, u32[]{:S(2)}) collective-permute-start(bf16[160,2048]{1,0:T(8,128)(2,1)} %pad_maximum_fusion.8), channel_id=1, source_target_pairs={{0,2},{2,4},{4,6},{6,7},{7,5},{5,3},{3,1},{1,0},{8,10},{10,12},{12... | collective-permute-start | bytes 1966088 | tf_op jit(solution)/shard_map/ppermute | solution.py:86
  454.3 20.9 %all-to-all-start.2 = ((f32[8,160,2]{1,2,0:T(2,128)}), f32[8,160,2]{1,2,0:T(2,128)S(1)}, u32[]{:S(2)}, u32[]{:S(2)}) async-start(f32[8,160,2]{1,2,0:T(2,128)} %copy.170), calls=%async_computation.2 | async-start | bytes 32768 | tf_op jit(solution)/shard_map/all_to_all | solution.py:241
  458.2 203.1 %reduce-scatter.4.cloned.1.call-start = ((), (), s32[]{:S(2)}) async-start(), calls=%async_computation.11 | async-start | bytes 10485760 | tf_op jit(solution)/shard_map/reduce_scatter | solution.py:727
  478.9 25.2 %collective-permute-start.37 = (bf16[160,2048]{1,0:T(8,128)(2,1)S(1)}, bf16[160,2048]{1,0:T(8,128)(2,1)}, u32[]{:S(2)}, u32[]{:S(2)}) collective-permute-start(bf16[160,2048]{1,0:T(8,128)(2,1)S(1)} %add_convert_fusion.11), channel_id=1, source_target_pairs={{0,1},{2,0},{4,2},{6,4},{7,6},{5,7},{3,5},{1,3},{8,9},{10,8},{12,1... | collective-permute-start | bytes 1966088 | tf_op jit(solution)/shard_map/ppermute | solution.py:86
  480.9 23.2 %collective-permute-start.38 = (bf16[80,2048]{1,0:T(8,128)(2,1)}, bf16[80,2048]{1,0:T(8,128)(2,1)}, u32[]{:S(2)}, u32[]{:S(2)}) collective-permute-start(bf16[80,2048]{1,0:T(8,128)(2,1)} %get-tuple-element.537), channel_id=1, source_target_pairs={{0,2},{2,4},{4,6},{6,7},{7,5},{5,3},{3,1},{1,0},{8,10},{10,12},{12... | collective-permute-start | bytes 983048 | tf_op jit(solution)/shard_map/ppermute | solution.py:86
  480.9 23.2 %collective-permute-start.39 = (bf16[80,2048]{1,0:T(8,128)(2,1)S(1)}, bf16[80,2048]{1,0:T(8,128)(2,1)}, u32[]{:S(2)}, u32[]{:S(2)}) collective-permute-start(bf16[80,2048]{1,0:T(8,128)(2,1)S(1)} %get-tuple-element.536), channel_id=1, source_target_pairs={{0,1},{2,0},{4,2},{6,4},{7,6},{5,7},{3,5},{1,3},{8,9},{10,8},{12,1... | collective-permute-start | bytes 983048 | tf_op jit(solution)/shard_map/ppermute | solution.py:86
  485.0 19.1 %collective-permute-start.36 = (bf16[160,2048]{1,0:T(8,128)(2,1)}, bf16[160,2048]{1,0:T(8,128)(2,1)}, u32[]{:S(2)}, u32[]{:S(2)}) collective-permute-start(bf16[160,2048]{1,0:T(8,128)(2,1)} %add_convert_fusion.12), channel_id=1, source_target_pairs={{0,2},{2,4},{4,6},{6,7},{7,5},{5,3},{3,1},{1,0},{8,10},{10,12},{12... | collective-permute-start | bytes 1966088 | tf_op jit(solution)/shard_map/ppermute | solution.py:86
  506.7 18.0 %collective-permute-start.43 = (bf16[160,2048]{1,0:T(8,128)(2,1)}, bf16[160,2048]{1,0:T(8,128)(2,1)}, u32[]{:S(2)}, u32[]{:S(2)}) collective-permute-start(bf16[160,2048]{1,0:T(8,128)(2,1)} %pad_maximum_fusion.11), channel_id=1, source_target_pairs={{0,1},{2,0},{4,2},{6,4},{7,6},{5,7},{3,5},{1,3},{8,9},{10,8},{12,1... | collective-permute-start | bytes 1966088 | tf_op jit(solution)/shard_map/ppermute | solution.py:86
  509.6 18.1 %collective-permute-start.42 = (bf16[160,2048]{1,0:T(8,128)(2,1)}, bf16[160,2048]{1,0:T(8,128)(2,1)}, u32[]{:S(2)}, u32[]{:S(2)}) collective-permute-start(bf16[160,2048]{1,0:T(8,128)(2,1)} %pad_maximum_fusion.10), channel_id=1, source_target_pairs={{0,2},{2,4},{4,6},{6,7},{7,5},{5,3},{3,1},{1,0},{8,10},{10,12},{12... | collective-permute-start | bytes 1966088 | tf_op jit(solution)/shard_map/ppermute | solution.py:86
  512.6 25.4 %collective-permute-start.40 = (bf16[160,2048]{1,0:T(8,128)(2,1)}, bf16[160,2048]{1,0:T(8,128)(2,1)S(1)}, u32[]{:S(2)}, u32[]{:S(2)}) collective-permute-start(bf16[160,2048]{1,0:T(8,128)(2,1)} %get-tuple-element.554), channel_id=1, source_target_pairs={{0,2},{2,4},{4,6},{6,7},{7,5},{5,3},{3,1},{1,0},{8,10},{10,12},{12... | collective-permute-start | bytes 1966088 | tf_op jit(solution)/shard_map/ppermute | solution.py:86
  514.7 23.3 %collective-permute-start.41 = (bf16[160,2048]{1,0:T(8,128)(2,1)}, bf16[160,2048]{1,0:T(8,128)(2,1)S(1)}, u32[]{:S(2)}, u32[]{:S(2)}) collective-permute-start(bf16[160,2048]{1,0:T(8,128)(2,1)} %get-tuple-element.553), channel_id=1, source_target_pairs={{0,1},{2,0},{4,2},{6,4},{7,6},{5,7},{3,5},{1,3},{8,9},{10,8},{12,1... | collective-permute-start | bytes 1966088 | tf_op jit(solution)/shard_map/ppermute | solution.py:86
  540.5 20.1 %collective-permute-start.44 = (bf16[160,2048]{1,0:T(8,128)(2,1)S(1)}, bf16[160,2048]{1,0:T(8,128)(2,1)S(1)}, u32[]{:S(2)}, u32[]{:S(2)}) collective-permute-start(bf16[160,2048]{1,0:T(8,128)(2,1)S(1)} %get-tuple-element.533), channel_id=1, source_target_pairs={{0,2},{2,4},{4,6},{6,7},{7,5},{5,3},{3,1},{1,0},{8,10},{10,12},{12... | collective-permute-start | bytes 1966088 | tf_op jit(solution)/shard_map/ppermute | solution.py:86
  541.0 19.6 %collective-permute-start.45 = (bf16[160,2048]{1,0:T(8,128)(2,1)S(1)}, bf16[160,2048]{1,0:T(8,128)(2,1)S(1)}, u32[]{:S(2)}, u32[]{:S(2)}) collective-permute-start(bf16[160,2048]{1,0:T(8,128)(2,1)S(1)} %get-tuple-element.532), channel_id=1, source_target_pairs={{0,1},{2,0},{4,2},{6,4},{7,6},{5,7},{3,5},{1,3},{8,9},{10,8},{12,1... | collective-permute-start | bytes 1966088 | tf_op jit(solution)/shard_map/ppermute | solution.py:86
  563.4 40.2 %collective-permute-start.46 = (bf16[160,2048]{1,0:T(8,128)(2,1)}, bf16[160,2048]{1,0:T(8,128)(2,1)}, u32[]{:S(2)}, u32[]{:S(2)}) collective-permute-start(bf16[160,2048]{1,0:T(8,128)(2,1)} %get-tuple-element.531), channel_id=1, source_target_pairs={{0,2},{2,4},{4,6},{6,7},{7,5},{5,3},{3,1},{1,0},{8,10},{10,12},{12... | collective-permute-start | bytes 1966088 | tf_op jit(solution)/shard_map/ppermute | solution.py:86
  563.9 39.8 %collective-permute-start.47 = (bf16[160,2048]{1,0:T(8,128)(2,1)}, bf16[160,2048]{1,0:T(8,128)(2,1)}, u32[]{:S(2)}, u32[]{:S(2)}) collective-permute-start(bf16[160,2048]{1,0:T(8,128)(2,1)} %get-tuple-element.530), channel_id=1, source_target_pairs={{0,1},{2,0},{4,2},{6,4},{7,6},{5,7},{3,5},{1,3},{8,9},{10,8},{12,1... | collective-permute-start | bytes 1966088 | tf_op jit(solution)/shard_map/ppermute | solution.py:86
  565.4 38.2 %all-to-all-start.3 = ((bf16[8,160,256]{2,1,0:T(8,128)(2,1)}), bf16[8,160,256]{2,1,0:T(8,128)(2,1)S(1)}, u32[]{:S(2)}, u32[]{:S(2)}) async-start(bf16[8,160,256]{2,1,0:T(8,128)(2,1)} %bitcast.156), calls=%async_computation.3 | async-start | bytes 1310720 | tf_op jit(solution)/shard_map/all_to_all | solution.py:241
  570.1 222.5 %reduce-scatter.6.cloned.1.call-start = ((), (), s32[]{:S(2)}) async-start(), calls=%async_computation.12 | async-start | bytes 10485760 | tf_op jit(solution)/shard_map/reduce_scatter | solution.py:789
  603.7 213.1 %reduce-scatter.8.cloned.1.call-start = ((), (), s32[]{:S(2)}) async-start(), calls=%async_computation.13 | async-start | bytes 10485760 | tf_op jit(solution)/shard_map/reduce_scatter | solution.py:791
  613.2 18.6 %collective-permute-start.48 = (bf16[160,2048]{1,0:T(8,128)(2,1)}, bf16[160,2048]{1,0:T(8,128)(2,1)}, u32[]{:S(2)}, u32[]{:S(2)}) collective-permute-start(bf16[160,2048]{1,0:T(8,128)(2,1)} %get-tuple-element.316), channel_id=1, source_target_pairs={{0,2},{2,4},{4,6},{6,7},{7,5},{5,3},{3,1},{1,0},{8,10},{10,12},{12... | collective-permute-start | bytes 1966088 | tf_op jit(solution)/shard_map/ppermute | solution.py:86
  615.2 16.6 %collective-permute-start.49 = (bf16[160,2048]{1,0:T(8,128)(2,1)}, bf16[160,2048]{1,0:T(8,128)(2,1)}, u32[]{:S(2)}, u32[]{:S(2)}) collective-permute-start(bf16[160,2048]{1,0:T(8,128)(2,1)} %get-tuple-element.316), channel_id=1, source_target_pairs={{0,1},{2,0},{4,2},{6,4},{7,6},{5,7},{3,5},{1,3},{8,9},{10,8},{12,1... | collective-permute-start | bytes 1966088 | tf_op jit(solution)/shard_map/ppermute | solution.py:86
  631.8 21.5 %collective-permute-start.50 = (bf16[160,2048]{1,0:T(8,128)(2,1)}, bf16[160,2048]{1,0:T(8,128)(2,1)}, u32[]{:S(2)}, u32[]{:S(2)}) collective-permute-start(bf16[160,2048]{1,0:T(8,128)(2,1)} %collective-permute-done.48), channel_id=1, source_target_pairs={{0,2},{2,4},{4,6},{6,7},{7,5},{5,3},{3,1},{1,0},{8,10},{10,12},{12... | collective-permute-start | bytes 1966088 | tf_op jit(solution)/shard_map/ppermute | solution.py:86
  633.7 19.6 %collective-permute-start.51 = (bf16[160,2048]{1,0:T(8,128)(2,1)}, bf16[160,2048]{1,0:T(8,128)(2,1)}, u32[]{:S(2)}, u32[]{:S(2)}) collective-permute-start(bf16[160,2048]{1,0:T(8,128)(2,1)} %collective-permute-done.49), channel_id=1, source_target_pairs={{0,1},{2,0},{4,2},{6,4},{7,6},{5,7},{3,5},{1,3},{8,9},{10,8},{12,1... | collective-permute-start | bytes 1966088 | tf_op jit(solution)/shard_map/ppermute | solution.py:86
  653.3 16.5 %collective-permute-start.52 = (bf16[160,2048]{1,0:T(8,128)(2,1)}, bf16[160,2048]{1,0:T(8,128)(2,1)S(1)}, u32[]{:S(2)}, u32[]{:S(2)}) collective-permute-start(bf16[160,2048]{1,0:T(8,128)(2,1)} %collective-permute-done.50), channel_id=1, source_target_pairs={{0,2},{2,4},{4,6},{6,7},{7,5},{5,3},{3,1},{1,0},{8,10},{10,12},{12... | collective-permute-start | bytes 1966088 | tf_op jit(solution)/shard_map/ppermute | solution.py:86
  701.4 48.7 %collective-permute-start.61 = (bf16[8,1,64,768]{3,2,1,0:T(8,128)(2,1)}, bf16[8,1,64,768]{3,2,1,0:T(8,128)(2,1)}, u32[]{:S(2)}, u32[]{:S(2)}) collective-permute-start(bf16[8,1,64,768]{3,2,1,0:T(8,128)(2,1)} %constant_dynamic-slice_fusion.1), channel_id=1, source_target_pairs={{0,16},{8,24},{16,0},{24,8},{1,17},{9,25},{17,1},{25,9},{2,18},{10... | collective-permute-start | bytes 2359304 | tf_op jit(solution)/shard_map/ppermute | solution.py:198
  704.0 45.0 %collective-permute-start.63 = (bf16[1,64,2048]{2,1,0:T(8,128)(2,1)}, bf16[1,64,2048]{2,1,0:T(8,128)(2,1)}, u32[]{:S(2)}, u32[]{:S(2)}) collective-permute-start(bf16[1,64,2048]{2,1,0:T(8,128)(2,1)} %constant_dynamic-slice_fusion), channel_id=1, source_target_pairs={{0,16},{8,24},{16,0},{24,8},{1,17},{9,25},{17,1},{25,9},{2,18},{10... | collective-permute-start | bytes 786440 | tf_op jit(solution)/shard_map/ppermute | solution.py:198
  712.0 40.3 %collective-permute-start.59 = (bf16[160,2048]{1,0:T(8,128)(2,1)}, bf16[160,2048]{1,0:T(8,128)(2,1)S(1)}, u32[]{:S(2)}, u32[]{:S(2)}) collective-permute-start(bf16[160,2048]{1,0:T(8,128)(2,1)} %pad_maximum_fusion.16), channel_id=1, source_target_pairs={{0,1},{2,0},{4,2},{6,4},{7,6},{5,7},{3,5},{1,3},{8,9},{10,8},{12,1... | collective-permute-start | bytes 1966088 | tf_op jit(solution)/shard_map/ppermute | solution.py:86
  714.0 38.3 %collective-permute-start.58 = (bf16[160,2048]{1,0:T(8,128)(2,1)}, bf16[160,2048]{1,0:T(8,128)(2,1)}, u32[]{:S(2)}, u32[]{:S(2)}) collective-permute-start(bf16[160,2048]{1,0:T(8,128)(2,1)} %pad_maximum_fusion.15), channel_id=1, source_target_pairs={{0,2},{2,4},{4,6},{6,7},{7,5},{5,3},{3,1},{1,0},{8,10},{10,12},{12... | collective-permute-start | bytes 1966088 | tf_op jit(solution)/shard_map/ppermute | solution.py:86
  757.9 27.4 %all-to-all-start.5 = ((bf16[8,64,768]{2,1,0:T(8,128)(2,1)}), bf16[8,64,768]{2,1,0:T(8,128)(2,1)S(1)}, u32[]{:S(2)}, u32[]{:S(2)}) async-start(bf16[8,64,768]{2,1,0:T(8,128)(2,1)} %fusion.29), calls=%async_computation.6 | async-start | bytes 1572864 | tf_op jit(solution)/shard_map/all_to_all | solution.py:241
  765.1 25.3 %collective-permute-start.64 = (bf16[160,2048]{1,0:T(8,128)(2,1)}, bf16[160,2048]{1,0:T(8,128)(2,1)}, u32[]{:S(2)}, u32[]{:S(2)}) collective-permute-start(bf16[160,2048]{1,0:T(8,128)(2,1)} %get-tuple-element.523), channel_id=1, source_target_pairs={{0,2},{2,4},{4,6},{6,7},{7,5},{5,3},{3,1},{1,0},{8,10},{10,12},{12... | collective-permute-start | bytes 1966088 | tf_op jit(solution)/shard_map/ppermute | solution.py:86
  767.2 25.5 %collective-permute-start.65 = (bf16[160,2048]{1,0:T(8,128)(2,1)}, bf16[160,2048]{1,0:T(8,128)(2,1)}, u32[]{:S(2)}, u32[]{:S(2)}) collective-permute-start(bf16[160,2048]{1,0:T(8,128)(2,1)} %get-tuple-element.522), channel_id=1, source_target_pairs={{0,1},{2,0},{4,2},{6,4},{7,6},{5,7},{3,5},{1,3},{8,9},{10,8},{12,1... | collective-permute-start | bytes 1966088 | tf_op jit(solution)/shard_map/ppermute | solution.py:86
  795.9 18.6 %collective-permute-start.72 = (bf16[1,3,64,2048]{3,2,1,0:T(8,128)(2,1)S(1)}, bf16[1,3,64,2048]{3,2,1,0:T(8,128)(2,1)S(1)}, u32[]{:S(2)}, u32[]{:S(2)}) collective-permute-start(bf16[1,3,64,2048]{3,2,1,0:T(8,128)(2,1)S(1)} %bitcast.170), channel_id=1, source_target_pairs={{0,16},{8,24},{16,0},{24,8},{1,17},{9,25},{17,1},{25,9},{2,18},{10... | collective-permute-start | bytes 2359304 | tf_op jit(solution)/shard_map/ppermute | solution.py:198
  820.8 20.1 %collective-permute-start.70 = (bf16[160,2048]{1,0:T(8,128)(2,1)}, bf16[160,2048]{1,0:T(8,128)(2,1)}, u32[]{:S(2)}, u32[]{:S(2)}) collective-permute-start(bf16[160,2048]{1,0:T(8,128)(2,1)} %get-tuple-element.521), channel_id=1, source_target_pairs={{0,2},{2,4},{4,6},{6,7},{7,5},{5,3},{3,1},{1,0},{8,10},{10,12},{12... | collective-permute-start | bytes 1966088 | tf_op jit(solution)/shard_map/ppermute | solution.py:86
  825.9 17.2 %collective-permute-start.71 = (bf16[160,2048]{1,0:T(8,128)(2,1)}, bf16[160,2048]{1,0:T(8,128)(2,1)}, u32[]{:S(2)}, u32[]{:S(2)}) collective-permute-start(bf16[160,2048]{1,0:T(8,128)(2,1)} %get-tuple-element.520), channel_id=1, source_target_pairs={{0,1},{2,0},{4,2},{6,4},{7,6},{5,7},{3,5},{1,3},{8,9},{10,8},{12,1... | collective-permute-start | bytes 1966088 | tf_op jit(solution)/shard_map/ppermute | solution.py:86
  (223 other events, 2086.3 us)
Sparse Core Ops, SparseCore 0:
  138.1 112.5 all-gather.2
  294.1 51.4 all-gather.4
  504.2 73.1 reduce-scatter.3
  603.8 73.0 reduce-scatter.5
  679.3 100.0 reduce-scatter.7

commit v7 on v6

--- a/solution.py
+++ b/solution.py
@@ -88,6 +88,10 @@
 
 def tie(*arrays):
     return lax.optimization_barrier(arrays)
+
+
+def after(value, *others):
+    return lax.optimization_barrier((value,) + others)[0]
 
 
 class RingGather:
@@ -397,6 +401,14 @@
     small_sent = jnp.concatenate([route_code.astype(low_type), router_weight], axis=0)
 
     small_flat = small_sent.reshape(-1, head_dim)
+    small_all = swap_all(
+        jnp.broadcast_to(small_flat[None], (group_count,) + small_flat.shape)
+    ).reshape(group_count, row_count + width_here, expert_total)
+    code_all = reorder(small_all[:, :row_count], device_of_slot).reshape(
+        group_rows, expert_total
+    )
+    full_router = small_all[:, row_count:].reshape(model_width, expert_total)
+
     projections = jnp.concatenate(
         [
             lax.dynamic_slice_in_dim(piece, replica * share, share, 0).reshape(
@@ -406,7 +418,15 @@
         ],
         axis=2,
     ).transpose(1, 0, 2)
-    cosine, sine_part = rope_tables(position, head_dim)
+    head_weight = (
+        rep_gather(swap_all(projections))
+        .transpose(1, 0, 2, 3)
+        .reshape(model_width, 3 * width_here)
+    )
+    column_share = model_width // replica_count
+    output_share = gather_rows(
+        lax.dynamic_slice_in_dim(output_weight, replica * column_share, column_share, 1)
+    )
     chunks = 2
     chunk_rows = group_rows // chunks
     blocks_here = group_count // chunks
@@ -414,109 +434,86 @@
     def chunk_of(array, chunk):
         return array[chunk * chunk_rows : (chunk + 1) * chunk_rows]
 
-    def normed_rows(rows):
-        wide = rows.astype(wide_type)
-        return (wide * inverse_rms(wide) * prenorm_gain).astype(low_type)
-
-    def head_columns(values, block, head):
-        start = block * width_here + head * head_dim
-        return values[:, start : start + head_dim]
-
-    def project(first, weight, chunk):
-        raw = mm(first, weight, 1, 0)
-        turns = chunk_of(cosine, chunk), chunk_of(sine_part, chunk)
-        results = []
-        for head in range(heads_here):
-            for block, gain in ((0, querynorm_gain), (1, keynorm_gain)):
-                part = head_columns(raw, block, head)
-                normed = part * inverse_rms(part) * gain
-                turned = (normed * turns[0] + turn_half(normed) * turns[1]).astype(low_type)
-                results += [part, turned]
-            results.append(head_columns(raw, 2, head).astype(low_type))
-        return results
-
-    token_ring = RingGather(tokens)
-    swapped = window([token_ring], swap_all, projections)
-    head_pieces, small_all = window(
-        [token_ring],
-        lambda pieces, small: (
-            rep_gather(pieces),
-            swap_all(jnp.broadcast_to(small[None], (group_count,) + small.shape)),
-        ),
-        swapped,
-        small_flat,
-    )
-    head_weight, first_rows = window(
-        [token_ring],
-        lambda pieces, *blocks: (
-            pieces.transpose(1, 0, 2, 3).reshape(model_width, 3 * width_here),
-            normed_rows(jnp.concatenate(blocks, axis=0)),
-        ),
-        head_pieces,
-        *token_ring.blocks[:blocks_here],
-    )
-    early_heads = window(
-        [token_ring],
-        lambda first, weight: project(first, weight, 0),
-        first_rows,
-        head_weight,
-    )
-    token_blocks = token_ring.blocks
-    last_rows = normed_rows(jnp.concatenate(token_blocks[blocks_here:], axis=0))
-    late_heads = project(last_rows, head_weight, 1)
-    first_all = jnp.concatenate([first_rows, last_rows], axis=0)
-    token_all = jnp.concatenate(token_blocks, axis=0)
-    token_wide = token_all.astype(wide_type)
-    inverse_all = inverse_rms(token_wide)
-
-    small_all = small_all.reshape(group_count, row_count + width_here, expert_total)
-    code_all = reorder(small_all[:, :row_count], device_of_slot).reshape(
-        group_rows, expert_total
-    )
-    full_router = small_all[:, row_count:].reshape(model_width, expert_total)
+    def gather_ring(values):
+        ring = RingGather(values)
+        for _ in range(group_count // 2):
+            ring.start()
+            ring.finish()
+        return ring.blocks
+
+    def slot_rows(array):
+        return lambda slot: array[slot * row_count : (slot + 1) * row_count]
 
     def reorder_rows(rows, index):
         return reorder(
             rows.reshape(group_count, row_count, rows.shape[1]), index
         ).reshape(rows.shape)
 
-    late_heads[0], cot_own = tie(late_heads[0], cotangent)
+    token_all = jnp.concatenate(gather_ring(tokens), axis=0)
+    token_late, cot_own = lax.optimization_barrier((token_all, cotangent))
+    token_all = token_late
     cot_ordered = gather_rows(cot_own)
     cot_all = reorder_rows(cot_ordered, device_of_slot)
-    column_share = model_width // replica_count
-    cot_ordered, output_own = tie(cot_ordered, output_weight)
-    output_share = gather_rows(
-        lax.dynamic_slice_in_dim(output_own, replica * column_share, column_share, 1)
-    )
+
+    token_wide = token_all.astype(wide_type)
+    inverse_all = inverse_rms(token_wide)
+    first_all = (token_wide * inverse_all * prenorm_gain).astype(low_type)
+    raw = mm(first_all, head_weight, 1, 0)
+    cosine, sine_part = rope_tables(position, head_dim)
 
     hidden_here = down_weight.shape[1]
     flat_down = down_weight.reshape(experts_here * hidden_here, model_width)
 
     allowed = segment[:, None] == segment[None, :]
+
+    def head_columns(values, block, head):
+        start = block * width_here + head * head_dim
+        return values[:, start : start + head_dim]
 
     kept_heads = []
     mixed_parts = []
     for head in range(heads_here):
-        query_raw, query_low, key_raw, key_low, value_low = (
-            jnp.concatenate([early_heads[5 * head + i], late_heads[5 * head + i]], axis=0)
-            for i in range(5)
-        )
+        query_raw = head_columns(raw, 0, head)
+        key_raw = head_columns(raw, 1, head)
+        query_inverse = inverse_rms(query_raw)
+        key_inverse = inverse_rms(key_raw)
+        query_normed = query_raw * query_inverse * querynorm_gain
+        key_normed = key_raw * key_inverse * keynorm_gain
+        query_low = (query_normed * cosine + turn_half(query_normed) * sine_part).astype(
+            low_type
+        )
+        key_low = (key_normed * cosine + turn_half(key_normed) * sine_part).astype(low_type)
+        value_low = head_columns(raw, 2, head).astype(low_type)
         scores = jnp.where(allowed, mm(query_low, key_low, 1, 1) * score_scale, masked_value)
         top_score = jnp.max(scores, axis=-1, keepdims=True)
         powers = jnp.exp(scores - top_score)
         log_total = top_score + jnp.log(jnp.sum(powers, axis=-1, keepdims=True))
         weights_low = jnp.exp(scores - log_total).astype(low_type)
         mixed_parts.append(mm(weights_low, value_low, 1, 0).astype(low_type))
-        kept_heads.append((query_raw, key_raw, query_low, key_low, value_low, log_total))
+        kept_heads.append(
+            (query_raw, key_raw, query_low, key_low, value_low, log_total)
+        )
     mixed_low = jnp.concatenate(mixed_parts, axis=1)
 
-    def slot_rows(array):
-        return lambda slot: array[slot * row_count : (slot + 1) * row_count]
-
-    attention_ring = RingSum(slot_rows(mm(mixed_low, output_weight, 1, 0).astype(low_type)), row_count)
-    for _ in range(group_count // 2):
-        window([attention_ring], lambda: ())
-    attention = attention_ring.total()
+    mixed_ordered = reorder_rows(mixed_low, slot_of_device)
+    output_pieces = {0: output_share}
+    distance = replica_count // 2
+    while distance:
+        for j in list(output_pieces):
+            output_pieces[j ^ distance] = rep_exchange(output_pieces[j], distance)
+        if distance == replica_count // 2:
+            output_pieces[distance] = after(output_pieces[distance], mixed_ordered)
+        distance //= 2
+    mixed_own = (
+        swap_all(mixed_ordered.reshape(group_count, row_count, width_here))
+        .transpose(1, 0, 2)
+        .reshape(row_count, model_width)
+    )
+    attention = jnp.zeros((row_count, model_width), wide_type)
+    for j, piece in output_pieces.items():
+        attention = lax.dynamic_update_slice_in_dim(
+            attention, mm(mixed_own, piece, 1, 0), (replica ^ j) * column_share, 1
+        )
     residual = tokens.astype(wide_type) + attention
     inverse_two = inverse_rms(residual)
     second_input = (residual * inverse_two * postnorm_gain).astype(low_type)
@@ -540,61 +537,23 @@
             rows, gate_weight, up_weight, stream, gates_here, chunk, chunks, earlier
         )
 
-    halves = 2 if column_share % 256 == 0 else 1
-    piece_width = column_share // halves
-    shares = [output_share[:, i * piece_width : (i + 1) * piece_width] for i in range(halves)]
-    far = replica_count // 2
-
     second_ring = RingGather(second_input)
     stream_first = window([second_ring], lambda part: stream_of(part), chunk_of(cot_all, 0))
     stream_last = window([second_ring], lambda part: stream_of(part), chunk_of(cot_all, 1))
     rows_first = jnp.concatenate(second_ring.blocks[:blocks_here], axis=0)
-    exchanges = [Exchange(piece, far) for piece in shares]
     *earlier, pair_first = window(
-        [second_ring, exchanges[0]],
+        [second_ring],
         lambda rows, stream: expert_chunk(0, rows, stream),
         rows_first,
         stream_first,
     )
     window([second_ring], lambda: ())
     rows_last = jnp.concatenate(second_ring.blocks[blocks_here:], axis=0)
-    inner_all, gback_all, uback_all, pair_last = window(
-        exchanges[1:],
-        lambda rows, stream, *earlier: expert_chunk(1, rows, stream, *earlier),
-        rows_last,
-        stream_last,
-        *earlier,
+    inner_all, gback_all, uback_all, pair_last = expert_chunk(
+        1, rows_last, stream_last, *earlier
     )
     second_all = jnp.concatenate([rows_first, rows_last], axis=0)
-    output_pieces = {}
-    for half in range(halves):
-        output_pieces[0, half] = shares[half]
-        output_pieces[far, half] = exchanges[half].received
-    near = []
-    distance = far // 2
-    while distance:
-        near += [
-            (j ^ distance, half, Exchange(output_pieces[j, half], distance))
-            for j, half in output_pieces
-        ]
-        if distance > 1:
-            for j, half, exchange in near:
-                window([exchange], lambda: ())
-                output_pieces[j, half] = exchange.received
-            near = []
-        distance //= 2
-    back_last = window(
-        [exchange for _, _, exchange in near],
-        lambda gback, uback: expert_back(gback, uback, gate_weight, up_weight, 1, chunks),
-        gback_all,
-        uback_all,
-    )
-    for j, half, exchange in near:
-        output_pieces[j, half] = exchange.received
-
-    def piece_start(j, half):
-        return (replica ^ j) * column_share + half * piece_width
-
+    back_last = expert_back(gback_all, uback_all, gate_weight, up_weight, 1, chunks)
     back_parts = {1: back_last}
 
     def back_block(slot):
@@ -641,7 +600,9 @@
     down_part, router_back, router_part = window(
         [back_ring, mixture_ring], down_work, inner_all, pair_grad
     )
-    window([back_ring, mixture_ring], lambda: ())
+    gate_part = window(
+        [back_ring, mixture_ring], lambda gback: grad_of(second_all, gback), gback_all
+    )
     second_scattered = back_ring.total()
     second_grad = router_back + second_scattered
     upstream = valid_own * cotangent.astype(wide_type)
@@ -652,9 +613,11 @@
         residual_grad = upstream + post_back
         attention_low = residual_grad.astype(low_type)
         mixed_grad_own = jnp.zeros((row_count, model_width), wide_type)
-        for place, piece in output_pieces.items():
+        for j, piece in output_pieces.items():
             mixed_grad_own = mixed_grad_own + mm(
-                lax.dynamic_slice_in_dim(attention_low, piece_start(*place), piece_width, 1),
+                lax.dynamic_slice_in_dim(
+                    attention_low, (replica ^ j) * column_share, column_share, 1
+                ),
                 piece,
                 1,
                 1,
@@ -674,11 +637,8 @@
             self.received = swap_all(self.sent)
 
     swap = Swap(swap_sent, 0)
-    gate_part, up_part = window(
-        [mixture_ring, swap],
-        lambda gback, uback: (grad_of(second_all, gback), grad_of(second_all, uback)),
-        gback_all,
-        uback_all,
+    up_part = window(
+        [mixture_ring, swap], lambda uback: grad_of(second_all, uback), uback_all
     )
     mixture = mixture_ring.total()
     layer_out = (valid_own * (residual + mixture)).astype(low_type)
@@ -757,48 +717,37 @@
         return pieces
 
     first_ring = RingSum(slot_rows(first_low), row_count)
-    head_part = window([attention_gather, first_ring], grad_of, first_all, sent)
+    head_part = window(
+        [attention_gather, first_ring],
+        grad_of,
+        first_all,
+        sent,
+    )
     attention_all = jnp.concatenate(attention_gather.blocks, axis=0)
-    output_part = grad_of(mixed_low, attention_all)
+    output_part = window([first_ring], grad_of, mixed_low, attention_all)
+    gate_sum = lax.psum_scatter(gate_part, "rep", scatter_dimension=0, tiled=True)
+    up_sum = lax.psum_scatter(up_part, "rep", scatter_dimension=0, tiled=True)
+    for _ in range(2, group_count // 2):
+        first_ring.start()
+        first_ring.finish()
+    first_grad = first_ring.total()
+    head_rows = rep_gather(
+        swap_all(
+            rep_scatter(
+                head_part.reshape(group_count, replica_count, share, 3 * width_here), 1
+            )
+        )
+        .reshape(group_count, share, 3, width_here)
+        .transpose(2, 1, 0, 3)
+        .reshape(3, share, model_width)
+    )
+    output_grad = (
+        rep_gather(rep_scatter(output_part.reshape(replica_count, share, model_width), 0))
+        .reshape(width_here, model_width)
+        .astype(wide_type)
+    )
     small_parts = [router_part, postnorm_part, prenorm_part, querynorm_part, keynorm_part]
-    head_rows, output_rows, small_swapped = window(
-        [first_ring],
-        lambda head, output, *small: (
-            rep_scatter(head, 1),
-            rep_scatter(output, 0),
-            small_swap(small),
-        ),
-        head_part.reshape(group_count, replica_count, share, 3 * width_here),
-        output_part.reshape(replica_count, share, model_width),
-        *small_parts,
-    )
-    head_rows, output_rows, small_sums = window(
-        [first_ring],
-        lambda head, output, small: (
-            swap_all(head)
-            .reshape(group_count, share, 3, width_here)
-            .transpose(2, 1, 0, 3)
-            .reshape(3, share, model_width),
-            rep_gather(output),
-            small_pieces(small, small_parts),
-        ),
-        head_rows,
-        output_rows,
-        small_swapped,
-    )
-    gate_sum = lax.psum_scatter(gate_part, "rep", scatter_dimension=0, tiled=True)
-    head_rows, gate_sum = tie(head_rows, gate_sum)
-    up_sum = lax.psum_scatter(up_part, "rep", scatter_dimension=0, tiled=True)
-    head_rows, output_grad = window(
-        [first_ring],
-        lambda head, output: (
-            rep_gather(head),
-            output.reshape(width_here, model_width).astype(wide_type),
-        ),
-        head_rows,
-        output_rows,
-    )
-    first_grad = first_ring.total()
+    small_sums = small_pieces(small_swap(small_parts), small_parts)
     query_grad, key_grad, value_grad = (
         head_rows[:, block].reshape(width_here, model_width).astype(wide_type)
         for block in range(3)

time: 871 us -> 734 us (0.84)
  waiting for transfers between devices: 254 us -> 170 us
  other arithmetic: 138 us -> 110 us
  starting transfers between devices: 117 us -> 101 us
  local copies, waits for them, and re-layouts: 114 us -> 101 us
    ppermute x56 -> x48, waiting for transfers between devices: 135 us -> 73.3 us  [ring_shift(): return lax.ppermute(values, 'ep', pairs)]
    all_to_all x6 -> x7, waiting for transfers between devices: 23.3 us -> 52.1 us  [swap_all(): return lax.all_to_all(values, 'ep', split_axis=0, concat_axis=0, tiled=True)]
    all_gather x2, waiting for transfers between devices: 26.4 us -> 0.01 us  [gather_rows(): return lax.all_gather(values, 'ep', axis=0, tiled=True)]
    ppermute x18 -> x15, waiting for transfers between devices: 68.9 us -> 44.5 us  [rep_exchange(): lax.ppermute(values, 'rep', [(i, i ^ distance) for i in range(count)])]
    ppermute x56 -> x48, starting transfers between devices: 74 us -> 58.5 us  [ring_shift(): return lax.ppermute(values, 'ep', pairs)]
    dynamic_slice x11, local copies, waits for them, and re-layouts: 11.2 us -> 0.68 us  [reorder(): lax.dynamic_slice_in_dim(blocks, index[i], 1, 0)]
    dot_general x37 -> x35, matrix products: 147 us -> 153 us  [mm(): lax.dot_general(left, right, (((left_dim,), (right_dim,)), ((), ())), pre...]
    convert_element_type x15 -> x13, other arithmetic: 31.2 us -> 25.6 us  [add_low(): return (left.astype(wide_type) + right.astype(wide_type)).astype(low_type)]
  transfers between devices with their start and end apart: 85 -> 75, of which waited for: 32 -> 19; matrix products, arithmetic and copies ran while one was open for 41% -> 45% of each run, Pallas kernels for 8% -> 5%
where the time goes in v7:
time: 734 us; the launch traced here: 724 us
  waiting for transfers between devices  170 us (23%)
  matrix products  153 us (21%)
  other arithmetic  110 us (15%)
  local copies, waits for them, and re-layouts  101 us (14%)
  starting transfers between devices  101 us (14%)
  Pallas kernels  72.6 us (10%)
  between operations  17.4 us (2%)
    dot_general x35, matrix products, mm(): lax.dot_general(left, right, (((left_dim,), (right_dim,)), ((), ())), pre...  153 us
    ppermute x48, waiting for transfers between devices, ring_shift(): return lax.ppermute(values, 'ep', pairs)  73.3 us
    unnamed x382, local copies, waits for them, and re-layouts  59.8 us
    ppermute x48, starting transfers between devices, ring_shift(): return lax.ppermute(values, 'ep', pairs)  58.5 us
    all_to_all x7, waiting for transfers between devices, swap_all(): return lax.all_to_all(values, 'ep', split_axis=0, concat_axis=0, tiled=True)  52.1 us
    ppermute x15, waiting for transfers between devices, rep_exchange(): lax.ppermute(values, 'rep', [(i, i ^ distance) for i in range(count)])  44.5 us
    pallas_call x2, Pallas kernels, expert_pass(): pl.pallas_call(expert_kernel, grid=(experts, steps), in_specs=[pl.BlockSp...  38.9 us
    all_to_all x7, starting transfers between devices, swap_all(): return lax.all_to_all(values, 'ep', split_axis=0, concat_axis=0, tiled=True)  34 us
  transfers between devices with their start and end apart: 75, of which 19 were waited for; matrix products, arithmetic and copies ran while one was open for 45% of the time, Pallas kernels for 5%

profile of v7, /device:TPU:0, one launch (start us, length us, event | category | flops | bytes accessed | tf_op | source)
XLA Modules:
  0.0 724.3 jit_solution(420091529791902530)
XLA Ops:
  7.2 3.0 collective-permute-start
  14.3 6.2 all-to-all-start.2
  31.3 4.0 all-to-all-start
  42.8 43.3 %collective-permute-done.2 = bf16[160,2048]{1,0:T(8,128)(2,1)} collective-permute-done((bf16[160,2048]{1,0:T(8,128)(2,1)}, bf16[160,2048]{1,0:T(8,128)(2,1)}, u32[]{:S(2)}, u32[]{:S(2)}) %collective-permute-start.2) | collective-permute-done | bytes 655392 | tf_op jit(solution)/shard_map/ppermute | solution.py:86
  86.1 8.1 %collective-permute-start.5 = (bf16[160,2048]{1,0:T(8,128)(2,1)}, bf16[160,2048]{1,0:T(8,128)(2,1)S(1)}, u32[]{:S(2)}, u32[]{:S(2)}) collective-permute-start(bf16[160,2048]{1,0:T(8,128)(2,1)} %collective-permute-done.3), channel_id=1, source_target_pairs={{0,2},{2,4},{4,6},{6,7},{7,5},{5,3},{3,1},{1,0},{8,10},{10,12},{12... | collective-permute-start | bytes 1966088 | tf_op jit(solution)/shard_map/ppermute | solution.py:86
  101.7 6.6 collective-permute-done.5
  108.3 2.3 collective-permute-start.6
  118.5 2.4 copy-done.10
  122.1 6.1 fusion.2
  129.6 3.5 maximum_select_fusion
  133.4 3.4 copy-done.27
  136.8 4.3 fusion.101
  160.2 15.3 %collective-permute-done.10 = bf16[2048,512]{1,0:T(8,128)(2,1)S(1)} collective-permute-done((bf16[2048,512]{1,0:T(8,128)(2,1)}, bf16[2048,512]{1,0:T(8,128)(2,1)S(1)}, u32[]{:S(2)}, u32[]{:S(2)}) %collective-permute-start.10) | collective-permute-done | bytes 2097184 | tf_op jit(solution)/shard_map/ppermute | solution.py:202
  176.2 4.2 all-to-all-start.1
  181.1 34.7 %all-to-all-done.1 = bf16[8,160,256]{2,1,0:T(8,128)(2,1)} async-done(((bf16[8,160,256]{2,1,0:T(8,128)(2,1)}), bf16[8,160,256]{2,1,0:T(8,128)(2,1)}, u32[]{:S(2)}, u32[]{:S(2)}) %all-to-all-start.1) | async-done | bytes 655392 | tf_op jit(solution)/shard_map/all_to_all | solution.py:245
  233.5 9.6 %fusion.108.stream_ref = f32[640,2048]{1,0:T(8,128)} fusion(bf16[640,2048]{1,0:T(8,128)(2,1)S(1)} %bitcast.211, bf16[2048,2048]{1,0:T(8,128)(2,1)} %bitcast.301), kind=kOutput, calls=%fused_computation.407 | convolution fusion | flops 5368709120 | bytes 16252928 | tf_op jit(solution)/shard_map/dot_general | solution.py:58
  246.0 9.7 %fusion.109.stream_ref = f32[640,2048]{1,0:T(8,128)} fusion(bf16[640,2048]{1,0:T(8,128)(2,1)S(1)} %bitcast.212, bf16[2048,2048]{1,0:T(8,128)(2,1)} %bitcast.302), kind=kOutput, calls=%fused_computation.408 | convolution fusion | flops 5368709120 | bytes 16252928 | tf_op jit(solution)/shard_map/dot_general | solution.py:58
  257.5 2.2 collective-permute-done.15
  267.6 19.4 %shard_map.281 = (bf16[1280,2048]{1,0:T(8,128)(2,1)}, bf16[1280,2048]{1,0:T(8,128)(2,1)}, bf16[1280,2048]{1,0:T(8,128)(2,1)}, f32[2,640,128]{2,1,0:T(8,128)}) custom-call(bf16[640,2048]{1,0:T(8,128)(2,1)} %copy-done.37, bf16[2,2048,1024]{2,1,0:T(8,128)(2,1)} %gate_ref.7, bf16[2,2048,1024]{2,1,0:T(8,128)(2,1)} %up_ref.7, f32[640,2048]{1,0:T(8,128)} %fusion.108.stream_ref, ...), custom_call_target="tpu_custom_call" | custom-call | flops 10737418240 | bytes 42991616 | tf_op jit(solution)/shard_map/pallas_call | solution.py:289
  291.3 3.3 collective-permute-done.19
  299.5 19.4 %shard_map.282 = (bf16[1280,2048]{1,0:T(8,128)(2,1)}, bf16[1280,2048]{1,0:T(8,128)(2,1)}, bf16[1280,2048]{1,0:T(8,128)(2,1)}, f32[2,640,128]{2,1,0:T(8,128)}) custom-call(bf16[640,2048]{1,0:T(8,128)(2,1)} %copy-done.31, bf16[2,2048,1024]{2,1,0:T(8,128)(2,1)} %gate_ref.7, ...), custom_call_target="tpu_custom_call", output_to_operand_aliasing={{0}: (5, {}), {1}: (6, {}), {2}: (7, {})} | custom-call | flops 10737418240 | bytes 42991616 | tf_op jit(solution)/shard_map/pallas_call | solution.py:289
  319.0 16.8 %shard_map.283 = bf16[640,2048]{1,0:T(8,128)(2,1)} custom-call(bf16[1280,2048]{1,0:T(8,128)(2,1)} %get-tuple-element.160.gback_ref, bf16[1280,2048]{1,0:T(8,128)(2,1)} %get-tuple-element.170.uback_ref, bf16[2,2048,1024]{2,1,0:T(8,128)(2,1)} %gate_ref.7, bf16[2,2048,1024]{2,1,0:T(8,128)(2,1)} %up_ref.7), custom_call_target="tpu_custom_call" | custom-call | flops 10737418240 | bytes 24641536 | tf_op jit(solution)/shard_map/pallas_call | solution.py:329
  335.8 2.2 fusion.90
  340.7 16.9 %shard_map.284 = bf16[640,2048]{1,0:T(8,128)(2,1)} custom-call(bf16[1280,2048]{1,0:T(8,128)(2,1)} %get-tuple-element.160.gback_ref, bf16[1280,2048]{1,0:T(8,128)(2,1)} %get-tuple-element.170.uback_ref, bf16[2,2048,1024]{2,1,0:T(8,128)(2,1)} %gate_ref.7, bf16[2,2048,1024]{2,1,0:T(8,128)(2,1)} %up_ref.7), custom_call_target="tpu_custom_call" | custom-call | flops 10737418240 | bytes 24641536 | tf_op jit(solution)/shard_map/pallas_call | solution.py:329
  363.4 4.8 all-to-all-start.3
  368.4 16.5 %convolution_convert_fusion.3 = bf16[1280,2048]{1,0:T(8,128)(2,1)} fusion(bf16[1280,2048]{1,0:T(8,128)(2,1)} %get-tuple-element.154, bf16[2048,2048]{1,0:T(8,128)(2,1)} %bitcast.303), kind=kOutput, calls=%fused_computation.15 | convolution fusion | flops 10740039680 | bytes 18874368 | tf_op jit(solution)/shard_map/dot_general | solution.py:58
  384.9 2.3 add_convert_fusion.11
  387.2 2.2 fusion.88
  393.5 2.3 add_convert_fusion.12
  395.9 16.8 %convolution_convert_fusion.2 = bf16[2048,2048]{1,0:T(8,128)(2,1)} fusion(bf16[1280,2048]{1,0:T(8,128)(2,1)} %get-tuple-element.154, bf16[1280,2048]{1,0:T(8,128)(2,1)} %bitcast.230), kind=kOutput, calls=%fused_computation.14 | convolution fusion | flops 10741612544 | bytes 18874368 | tf_op jit(solution)/shard_map/dot_general | solution.py:58
  420.2 2.9 add_convert_fusion.9
  425.2 16.9 %convolution_convert_fusion.1 = bf16[2048,2048]{1,0:T(8,128)(2,1)} fusion(bf16[1280,2048]{1,0:T(8,128)(2,1)} %get-tuple-element.407, bf16[1280,2048]{1,0:T(8,128)(2,1)S(1)} %bitcast.184), kind=kOutput, calls=%fused_computation.13 | convolution fusion | flops 10741612544 | bytes 18874368 | tf_op jit(solution)/shard_map/dot_general | solution.py:58
  443.7 3.4 collective-permute-done.29
  447.1 2.3 add_convert_fusion.7
  458.0 2.6 fusion.57
  460.6 2.4 fusion.11
  464.0 3.0 add_convert_fusion.5
  469.0 4.6 all-to-all-start.4
  476.0 16.7 %convolution_convert_fusion = bf16[2048,2048]{1,0:T(8,128)(2,1)} fusion(bf16[1280,2048]{1,0:T(8,128)(2,1)} %get-tuple-element.407, bf16[1280,2048]{1,0:T(8,128)(2,1)} %get-tuple-element.170.uback_ref), kind=kOutput, calls=%fused_computation.12 | convolution fusion | flops 10741612544 | bytes 18874368 | tf_op jit(solution)/shard_map/dot_general | solution.py:58
  493.6 3.1 all-to-all-done.4
  497.0 9.1 %multiply_reduce_fusion.1 = (f32[1280]{0:T(1024)S(1)}, f32[1280,1280]{0,1:T(8,128)}) fusion(f32[1280,1280]{0,1:T(8,128)} %copy-done.3, f32[1280]{0:T(1024)S(1)} %copy-done.72, bf16[1280,128]{1,0:T(8,128)(2,1)S(1)} %get-tuple-element.176, bf16[1280,768]{0,1:T(8,128)(2,1)} %copy-done.60), kind=kOutput, calls=%fused_computation.19 | convolution fusion | flops 424344320 | bytes 13772800 | tf_op jit(solution)/shard_map/dot_general | solution.py:58
  506.4 4.1 multiply_convert_fusion.1
  520.6 2.3 multiply_reduce_fusion
  539.8 2.4 multiply_convert_fusion.2
  553.9 9.8 %fusion.4 = (f32[2048]{0:T(1024)S(1)}, bf16[1280,2048]{1,0:T(8,128)(2,1)S(1)}) fusion(bf16[1280,2048]{1,0:T(8,128)(2,1)} %copy-done.10, f32[1280]{0:T(1024)S(1)} %copy-done.93, bf16[1280,768]{0,1:T(8,128)(2,1)} %constant_dynamic-update-slice_fusion.55, bf16[2048,768]{1,0:T(8,128)(2,1)} %bitcast.199), kind=kOutput, calls=%fused_computation.7 | convolution fusion | flops 4039636992 | bytes 15610880 | tf_op jit(solution)/shard_map/dot_general | solution.py:58
  572.3 4.7 all-to-all-start.6
  577.0 9.7 %convolution_convert_fusion.4 = bf16[2048,768]{1,0:T(8,128)(2,1)} fusion(bf16[1280,2048]{1,0:T(8,128)(2,1)} %fusion.2, bf16[1280,768]{0,1:T(8,128)(2,1)} %constant_dynamic-update-slice_fusion.55), kind=kOutput, calls=%fused_computation.26 | convolution fusion | flops 4028104704 | bytes 10354688 | tf_op jit(solution)/shard_map/dot_general | solution.py:58
  592.6 2.5 convert_element_type.544
  601.3 2.4 constant_dynamic-slice_fusion.3
  608.6 2.5 convolution_convert_fusion.5
  611.1 2.8 slice_bitcast_fusion.3
  613.9 2.8 collective-permute-done.48
  616.7 6.5 collective-permute-done.47
  626.1 3.0 add_convert_fusion.4
  632.7 18.8 %collective-permute-done.54 = bf16[8,1,64,768]{3,2,0,1:T(8,128)(2,1)S(1)} collective-permute-done((bf16[8,1,64,768]{3,2,0,1:T(8,128)(2,1)S(1)}, bf16[8,1,64,768]{3,2,0,1:T(8,128)(2,1)S(1)}, u32[]{:S(2)}, u32[]{:S(2)}) %collective-permute-start.54) | collective-permute-done | bytes 786464 | tf_op jit(solution)/shard_map/ppermute | solution.py:202
  652.5 5.5 all-to-all-start.5
  658.8 3.0 add_convert_fusion.3
  664.1 2.3 maximum_convert_fusion
  667.3 12.3 %all-to-all-done.5 = bf16[8,64,768]{2,1,0:T(8,128)(2,1)S(1)} async-done(((bf16[8,64,768]{2,1,0:T(8,128)(2,1)}), bf16[8,64,768]{2,1,0:T(8,128)(2,1)S(1)}, u32[]{:S(2)}, u32[]{:S(2)}) %all-to-all-start.5) | async-done | bytes 786464 | tf_op jit(solution)/shard_map/all_to_all | solution.py:245
  685.0 2.2 collective-permute-done.52
  689.3 8.3 %collective-permute-done.55 = bf16[1,3,64,2048]{3,2,1,0:T(8,128)(2,1)S(1)} collective-permute-done((bf16[1,3,64,2048]{3,2,1,0:T(8,128)(2,1)S(1)}, bf16[1,3,64,2048]{3,2,1,0:T(8,128)(2,1)S(1)}, u32[]{:S(2)}, u32[]{:S(2)}) %collective-permute-start.55) | collective-permute-done | bytes 786464 | tf_op jit(solution)/shard_map/ppermute | solution.py:202
  699.0 3.1 fusion.15
  703.8 2.3 maximum_convert_fusion.1
  709.6 2.4 maximum_select_fusion.1
  (712 shorter events, 232.0 us)
Async XLA Ops:
  7.2 31.3 %collective-permute-start = (bf16[160,2048]{1,0:T(8,128)(2,1)}, bf16[160,2048]{1,0:T(8,128)(2,1)}, u32[]{:S(2)}, u32[]{:S(2)}) collective-permute-start(bf16[160,2048]{1,0:T(8,128)(2,1)} %param.18), channel_id=1, source_target_pairs={{0,1},{2,0},{4,2},{6,4},{7,6},{5,7},{3,5},{1,3},{8,9},{10,8},{12,1... | collective-permute-start | bytes 1966088 | tf_op jit(solution)/shard_map/ppermute | solution.py:86
  10.2 30.3 %collective-permute-start.1 = (bf16[160,2048]{1,0:T(8,128)(2,1)}, bf16[160,2048]{1,0:T(8,128)(2,1)S(1)}, u32[]{:S(2)}, u32[]{:S(2)}) collective-permute-start(bf16[160,2048]{1,0:T(8,128)(2,1)} %param.18), channel_id=1, source_target_pairs={{0,2},{2,4},{4,6},{6,7},{7,5},{5,3},{3,1},{1,0},{8,10},{10,12},{12... | collective-permute-start | bytes 1966088 | tf_op jit(solution)/shard_map/ppermute | solution.py:86
  14.3 17.1 %all-to-all-start.2 = ((bf16[8,52,128]{2,1,0:T(8,128)(2,1)}), bf16[8,52,128]{2,1,0:T(8,128)(2,1)S(1)}, u32[]{:S(2)}, u32[]{:S(2)}) async-start(bf16[8,52,128]{2,1,0:T(8,128)(2,1)} %broadcast_in_dim.192), calls=%async_computation.2 | async-start | bytes 229376 | tf_op jit(solution)/shard_map/all_to_all | solution.py:245
  20.5 107.7 %all-gather.3.cloned.1.call-start = ((), (), s32[]{:S(2)}) async-start(), calls=%async_computation.10 | async-start | bytes 2359296 | tf_op jit(solution)/shard_map/all_gather | solution.py:67
  31.3 64.9 %all-to-all-start = ((bf16[8,64,768]{2,1,0:T(8,128)(2,1)}), bf16[8,64,768]{2,1,0:T(8,128)(2,1)S(1)}, u32[]{:S(2)}, u32[]{:S(2)}) async-start(bf16[8,64,768]{2,1,0:T(8,128)(2,1)} %copy.125), calls=%async_computation | async-start | bytes 1572864 | tf_op jit(solution)/shard_map/all_to_all | solution.py:245
  35.4 193.3 %all-gather.5.cloned.1.call-start = ((), (), s32[]{:S(2)}) async-start(), calls=%async_computation.11 | async-start | bytes 5898240 | tf_op jit(solution)/shard_map/all_gather | solution.py:67
  38.6 47.6 %collective-permute-start.2 = (bf16[160,2048]{1,0:T(8,128)(2,1)}, bf16[160,2048]{1,0:T(8,128)(2,1)}, u32[]{:S(2)}, u32[]{:S(2)}) collective-permute-start(bf16[160,2048]{1,0:T(8,128)(2,1)} %collective-permute-done), channel_id=1, source_target_pairs={{0,1},{2,0},{4,2},{6,4},{7,6},{5,7},{3,5},{1,3},{8,9},{10,8},{12,1... | collective-permute-start | bytes 1966088 | tf_op jit(solution)/shard_map/ppermute | solution.py:86
  40.5 45.6 %collective-permute-start.3 = (bf16[160,2048]{1,0:T(8,128)(2,1)S(1)}, bf16[160,2048]{1,0:T(8,128)(2,1)}, u32[]{:S(2)}, u32[]{:S(2)}) collective-permute-start(bf16[160,2048]{1,0:T(8,128)(2,1)S(1)} %collective-permute-done.1), channel_id=1, source_target_pairs={{0,2},{2,4},{4,6},{6,7},{7,5},{5,3},{3,1},{1,0},{8,10},{10,12},{12... | collective-permute-start | bytes 1966088 | tf_op jit(solution)/shard_map/ppermute | solution.py:86
  86.1 24.5 %collective-permute-start.4 = (bf16[160,2048]{1,0:T(8,128)(2,1)}, bf16[160,2048]{1,0:T(8,128)(2,1)S(1)}, u32[]{:S(2)}, u32[]{:S(2)}) collective-permute-start(bf16[160,2048]{1,0:T(8,128)(2,1)} %collective-permute-done.2), channel_id=1, source_target_pairs={{0,1},{2,0},{4,2},{6,4},{7,6},{5,7},{3,5},{1,3},{8,9},{10,8},{12,1... | collective-permute-start | bytes 1966088 | tf_op jit(solution)/shard_map/ppermute | solution.py:86
  86.1 22.1 %collective-permute-start.5 = (bf16[160,2048]{1,0:T(8,128)(2,1)}, bf16[160,2048]{1,0:T(8,128)(2,1)S(1)}, u32[]{:S(2)}, u32[]{:S(2)}) collective-permute-start(bf16[160,2048]{1,0:T(8,128)(2,1)} %collective-permute-done.3), channel_id=1, source_target_pairs={{0,2},{2,4},{4,6},{6,7},{7,5},{5,3},{3,1},{1,0},{8,10},{10,12},{12... | collective-permute-start | bytes 1966088 | tf_op jit(solution)/shard_map/ppermute | solution.py:86
  96.2 18.6 %collective-permute-start.8 = (bf16[1,8,64,768]{3,2,1,0:T(8,128)(2,1)S(1)}, bf16[1,8,64,768]{3,2,1,0:T(8,128)(2,1)S(1)}, u32[]{:S(2)}, u32[]{:S(2)}) collective-permute-start(bf16[1,8,64,768]{3,2,1,0:T(8,128)(2,1)S(1)} %bitcast.180), channel_id=1, source_target_pairs={{0,16},{8,24},{16,0},{24,8},{1,17},{9,25},{17,1},{25,9},{2,18},{10... | collective-permute-start | bytes 2359304 | tf_op jit(solution)/shard_map/ppermute | solution.py:202
  128.1 47.4 %collective-permute-start.10 = (bf16[2048,512]{1,0:T(8,128)(2,1)}, bf16[2048,512]{1,0:T(8,128)(2,1)S(1)}, u32[]{:S(2)}, u32[]{:S(2)}) collective-permute-start(bf16[2048,512]{1,0:T(8,128)(2,1)} %all-gather.3.cloned.1.call-done), channel_id=1, source_target_pairs={{0,16},{8,24},{16,0},{24,8},{1,17},{9,25},{17,1},{25,9},{2,18},{10... | collective-permute-start | bytes 6291464 | tf_op jit(solution)/shard_map/ppermute | solution.py:202
  129.6 89.1 %collective-permute-start.11 = (bf16[2048,512]{1,0:T(8,128)(2,1)}, bf16[2048,512]{1,0:T(8,128)(2,1)}, u32[]{:S(2)}, u32[]{:S(2)}) collective-permute-start(bf16[2048,512]{1,0:T(8,128)(2,1)} %all-gather.3.cloned.1.call-done), channel_id=1, source_target_pairs={{0,8},{8,0},{16,24},{24,16},{1,9},{9,1},{17,25},{25,17},{2,10},{10... | collective-permute-start | bytes 6291464 | tf_op jit(solution)/shard_map/ppermute | solution.py:202
  175.5 45.4 %collective-permute-start.12 = (bf16[2048,512]{1,0:T(8,128)(2,1)S(1)}, bf16[2048,512]{1,0:T(8,128)(2,1)}, u32[]{:S(2)}, u32[]{:S(2)}) collective-permute-start(bf16[2048,512]{1,0:T(8,128)(2,1)S(1)} %collective-permute-done.10), channel_id=1, source_target_pairs={{0,8},{8,0},{16,24},{24,16},{1,9},{9,1},{17,25},{25,17},{2,10},{10... | collective-permute-start | bytes 6291464 | tf_op jit(solution)/shard_map/ppermute | solution.py:202
  176.2 39.6 %all-to-all-start.1 = ((bf16[8,160,256]{2,1,0:T(8,128)(2,1)}), bf16[8,160,256]{2,1,0:T(8,128)(2,1)}, u32[]{:S(2)}, u32[]{:S(2)}) async-start(bf16[8,160,256]{2,1,0:T(8,128)(2,1)} %constant_dynamic-update-slice_fusion.9), calls=%async_computation.1 | async-start | bytes 1310720 | tf_op jit(solution)/shard_map/all_to_all | solution.py:245
  225.5 18.0 %collective-permute-start.13 = (bf16[160,2048]{1,0:T(8,128)(2,1)S(1)}, bf16[160,2048]{1,0:T(8,128)(2,1)S(1)}, u32[]{:S(2)}, u32[]{:S(2)}) collective-permute-start(bf16[160,2048]{1,0:T(8,128)(2,1)S(1)} %get-tuple-element.301), channel_id=1, source_target_pairs={{0,2},{2,4},{4,6},{6,7},{7,5},{5,3},{3,1},{1,0},{8,10},{10,12},{12... | collective-permute-start | bytes 1966088 | tf_op jit(solution)/shard_map/ppermute | solution.py:86
  225.5 18.0 %collective-permute-start.14 = (bf16[160,2048]{1,0:T(8,128)(2,1)S(1)}, bf16[160,2048]{1,0:T(8,128)(2,1)S(1)}, u32[]{:S(2)}, u32[]{:S(2)}) collective-permute-start(bf16[160,2048]{1,0:T(8,128)(2,1)S(1)} %get-tuple-element.301), channel_id=1, source_target_pairs={{0,1},{2,0},{4,2},{6,4},{7,6},{5,7},{3,5},{1,3},{8,9},{10,8},{12,1... | collective-permute-start | bytes 1966088 | tf_op jit(solution)/shard_map/ppermute | solution.py:86
  243.6 16.1 %collective-permute-start.15 = (bf16[160,2048]{1,0:T(8,128)(2,1)S(1)}, bf16[160,2048]{1,0:T(8,128)(2,1)}, u32[]{:S(2)}, u32[]{:S(2)}) collective-permute-start(bf16[160,2048]{1,0:T(8,128)(2,1)S(1)} %collective-permute-done.13), channel_id=1, source_target_pairs={{0,2},{2,4},{4,6},{6,7},{7,5},{5,3},{3,1},{1,0},{8,10},{10,12},{12... | collective-permute-start | bytes 1966088 | tf_op jit(solution)/shard_map/ppermute | solution.py:86
  243.6 16.0 %collective-permute-start.16 = (bf16[160,2048]{1,0:T(8,128)(2,1)S(1)}, bf16[160,2048]{1,0:T(8,128)(2,1)S(1)}, u32[]{:S(2)}, u32[]{:S(2)}) collective-permute-start(bf16[160,2048]{1,0:T(8,128)(2,1)S(1)} %collective-permute-done.14), channel_id=1, source_target_pairs={{0,1},{2,0},{4,2},{6,4},{7,6},{5,7},{3,5},{1,3},{8,9},{10,8},{12,1... | collective-permute-start | bytes 1966088 | tf_op jit(solution)/shard_map/ppermute | solution.py:86
  259.9 27.2 %collective-permute-start.18 = (bf16[160,2048]{1,0:T(8,128)(2,1)S(1)}, bf16[160,2048]{1,0:T(8,128)(2,1)S(1)}, u32[]{:S(2)}, u32[]{:S(2)}) collective-permute-start(bf16[160,2048]{1,0:T(8,128)(2,1)S(1)} %collective-permute-done.16), channel_id=1, source_target_pairs={{0,1},{2,0},{4,2},{6,4},{7,6},{5,7},{3,5},{1,3},{8,9},{10,8},{12,1... | collective-permute-start | bytes 1966088 | tf_op jit(solution)/shard_map/ppermute | solution.py:86
  261.7 25.4 %collective-permute-start.17 = (bf16[160,2048]{1,0:T(8,128)(2,1)}, bf16[160,2048]{1,0:T(8,128)(2,1)S(1)}, u32[]{:S(2)}, u32[]{:S(2)}) collective-permute-start(bf16[160,2048]{1,0:T(8,128)(2,1)} %collective-permute-done.15), channel_id=1, source_target_pairs={{0,2},{2,4},{4,6},{6,7},{7,5},{5,3},{3,1},{1,0},{8,10},{10,12},{12... | collective-permute-start | bytes 1966088 | tf_op jit(solution)/shard_map/ppermute | solution.py:86
  338.0 19.8 %collective-permute-start.21 = (bf16[80,2048]{1,0:T(8,128)(2,1)}, bf16[80,2048]{1,0:T(8,128)(2,1)}, u32[]{:S(2)}, u32[]{:S(2)}) collective-permute-start(bf16[80,2048]{1,0:T(8,128)(2,1)} %get-tuple-element.366), channel_id=1, source_target_pairs={{0,2},{2,4},{4,6},{6,7},{7,5},{5,3},{3,1},{1,0},{8,10},{10,12},{12... | collective-permute-start | bytes 983048 | tf_op jit(solution)/shard_map/ppermute | solution.py:86
  339.8 18.1 %collective-permute-start.22 = (bf16[80,2048]{1,0:T(8,128)(2,1)S(1)}, bf16[80,2048]{1,0:T(8,128)(2,1)}, u32[]{:S(2)}, u32[]{:S(2)}) collective-permute-start(bf16[80,2048]{1,0:T(8,128)(2,1)S(1)} %get-tuple-element.365), channel_id=1, source_target_pairs={{0,1},{2,0},{4,2},{6,4},{7,6},{5,7},{3,5},{1,3},{8,9},{10,8},{12,1... | collective-permute-start | bytes 983048 | tf_op jit(solution)/shard_map/ppermute | solution.py:86
  360.2 24.6 %collective-permute-start.24 = (bf16[160,2048]{1,0:T(8,128)(2,1)}, bf16[160,2048]{1,0:T(8,128)(2,1)}, u32[]{:S(2)}, u32[]{:S(2)}) collective-permute-start(bf16[160,2048]{1,0:T(8,128)(2,1)} %pad_maximum_fusion.7), channel_id=1, source_target_pairs={{0,1},{2,0},{4,2},{6,4},{7,6},{5,7},{3,5},{1,3},{8,9},{10,8},{12,1... | collective-permute-start | bytes 1966088 | tf_op jit(solution)/shard_map/ppermute | solution.py:86
  361.6 23.3 %collective-permute-start.23 = (bf16[160,2048]{1,0:T(8,128)(2,1)S(1)}, bf16[160,2048]{1,0:T(8,128)(2,1)}, u32[]{:S(2)}, u32[]{:S(2)}) collective-permute-start(bf16[160,2048]{1,0:T(8,128)(2,1)S(1)} %pad_maximum_fusion.6), channel_id=1, source_target_pairs={{0,2},{2,4},{4,6},{6,7},{7,5},{5,3},{3,1},{1,0},{8,10},{10,12},{12... | collective-permute-start | bytes 1966088 | tf_op jit(solution)/shard_map/ppermute | solution.py:86
  363.4 21.5 %all-to-all-start.3 = ((f32[8,160,2]{1,2,0:T(2,128)}), f32[8,160,2]{1,2,0:T(2,128)S(1)}, u32[]{:S(2)}, u32[]{:S(2)}) async-start(f32[8,160,2]{1,2,0:T(2,128)} %copy.160), calls=%async_computation.3 | async-start | bytes 32768 | tf_op jit(solution)/shard_map/all_to_all | solution.py:245
  368.2 185.8 %reduce-scatter.4.cloned.1.call-start = ((), (), s32[]{:S(2)}) async-start(), calls=%async_computation.12 | async-start | bytes 10485760 | tf_op jit(solution)/shard_map/reduce_scatter | solution.py:687
  389.5 24.1 %collective-permute-start.26 = (bf16[160,2048]{1,0:T(8,128)(2,1)}, bf16[160,2048]{1,0:T(8,128)(2,1)}, u32[]{:S(2)}, u32[]{:S(2)}) collective-permute-start(bf16[160,2048]{1,0:T(8,128)(2,1)} %add_convert_fusion.11), channel_id=1, source_target_pairs={{0,1},{2,0},{4,2},{6,4},{7,6},{5,7},{3,5},{1,3},{8,9},{10,8},{12,1... | collective-permute-start | bytes 1966088 | tf_op jit(solution)/shard_map/ppermute | solution.py:86
  391.4 22.1 %collective-permute-start.27 = (bf16[80,2048]{1,0:T(8,128)(2,1)}, bf16[80,2048]{1,0:T(8,128)(2,1)}, u32[]{:S(2)}, u32[]{:S(2)}) collective-permute-start(bf16[80,2048]{1,0:T(8,128)(2,1)} %get-tuple-element.343), channel_id=1, source_target_pairs={{0,2},{2,4},{4,6},{6,7},{7,5},{5,3},{3,1},{1,0},{8,10},{10,12},{12... | collective-permute-start | bytes 983048 | tf_op jit(solution)/shard_map/ppermute | solution.py:86
  391.5 22.1 %collective-permute-start.28 = (bf16[80,2048]{1,0:T(8,128)(2,1)S(1)}, bf16[80,2048]{1,0:T(8,128)(2,1)}, u32[]{:S(2)}, u32[]{:S(2)}) collective-permute-start(bf16[80,2048]{1,0:T(8,128)(2,1)S(1)} %get-tuple-element.342), channel_id=1, source_target_pairs={{0,1},{2,0},{4,2},{6,4},{7,6},{5,7},{3,5},{1,3},{8,9},{10,8},{12,1... | collective-permute-start | bytes 983048 | tf_op jit(solution)/shard_map/ppermute | solution.py:86
  395.8 17.8 %collective-permute-start.25 = (bf16[160,2048]{1,0:T(8,128)(2,1)}, bf16[160,2048]{1,0:T(8,128)(2,1)}, u32[]{:S(2)}, u32[]{:S(2)}) collective-permute-start(bf16[160,2048]{1,0:T(8,128)(2,1)} %add_convert_fusion.12), channel_id=1, source_target_pairs={{0,2},{2,4},{4,6},{6,7},{7,5},{5,3},{3,1},{1,0},{8,10},{10,12},{12... | collective-permute-start | bytes 1966088 | tf_op jit(solution)/shard_map/ppermute | solution.py:86
  413.6 197.5 %reduce-scatter.6.cloned.1.call-start = ((), (), s32[]{:S(2)}) async-start(), calls=%async_computation.13 | async-start | bytes 10485760 | tf_op jit(solution)/shard_map/reduce_scatter | solution.py:728
  417.1 26.6 %collective-permute-start.32 = (bf16[160,2048]{1,0:T(8,128)(2,1)}, bf16[160,2048]{1,0:T(8,128)(2,1)}, u32[]{:S(2)}, u32[]{:S(2)}) collective-permute-start(bf16[160,2048]{1,0:T(8,128)(2,1)} %pad_maximum_fusion.9), channel_id=1, source_target_pairs={{0,1},{2,0},{4,2},{6,4},{7,6},{5,7},{3,5},{1,3},{8,9},{10,8},{12,1... | collective-permute-start | bytes 1966088 | tf_op jit(solution)/shard_map/ppermute | solution.py:86
  420.0 23.7 %collective-permute-start.31 = (bf16[160,2048]{1,0:T(8,128)(2,1)}, bf16[160,2048]{1,0:T(8,128)(2,1)}, u32[]{:S(2)}, u32[]{:S(2)}) collective-permute-start(bf16[160,2048]{1,0:T(8,128)(2,1)} %pad_maximum_fusion.8), channel_id=1, source_target_pairs={{0,2},{2,4},{4,6},{6,7},{7,5},{5,3},{3,1},{1,0},{8,10},{10,12},{12... | collective-permute-start | bytes 1966088 | tf_op jit(solution)/shard_map/ppermute | solution.py:86
  423.2 23.9 %collective-permute-start.29 = (bf16[160,2048]{1,0:T(8,128)(2,1)}, bf16[160,2048]{1,0:T(8,128)(2,1)}, u32[]{:S(2)}, u32[]{:S(2)}) collective-permute-start(bf16[160,2048]{1,0:T(8,128)(2,1)} %get-tuple-element.362), channel_id=1, source_target_pairs={{0,2},{2,4},{4,6},{6,7},{7,5},{5,3},{3,1},{1,0},{8,10},{10,12},{12... | collective-permute-start | bytes 1966088 | tf_op jit(solution)/shard_map/ppermute | solution.py:86
  425.1 22.0 %collective-permute-start.30 = (bf16[160,2048]{1,0:T(8,128)(2,1)}, bf16[160,2048]{1,0:T(8,128)(2,1)}, u32[]{:S(2)}, u32[]{:S(2)}) collective-permute-start(bf16[160,2048]{1,0:T(8,128)(2,1)} %get-tuple-element.361), channel_id=1, source_target_pairs={{0,1},{2,0},{4,2},{6,4},{7,6},{5,7},{3,5},{1,3},{8,9},{10,8},{12,1... | collective-permute-start | bytes 1966088 | tf_op jit(solution)/shard_map/ppermute | solution.py:86
  449.5 14.5 %collective-permute-start.33 = (bf16[160,2048]{1,0:T(8,128)(2,1)S(1)}, bf16[160,2048]{1,0:T(8,128)(2,1)S(1)}, u32[]{:S(2)}, u32[]{:S(2)}) collective-permute-start(bf16[160,2048]{1,0:T(8,128)(2,1)S(1)} %get-tuple-element.339), channel_id=1, source_target_pairs={{0,2},{2,4},{4,6},{6,7},{7,5},{5,3},{3,1},{1,0},{8,10},{10,12},{12... | collective-permute-start | bytes 1966088 | tf_op jit(solution)/shard_map/ppermute | solution.py:86
  466.9 26.7 %collective-permute-start.35 = (bf16[160,2048]{1,0:T(8,128)(2,1)}, bf16[160,2048]{1,0:T(8,128)(2,1)S(1)}, u32[]{:S(2)}, u32[]{:S(2)}) collective-permute-start(bf16[160,2048]{1,0:T(8,128)(2,1)} %get-tuple-element.337), channel_id=1, source_target_pairs={{0,2},{2,4},{4,6},{6,7},{7,5},{5,3},{3,1},{1,0},{8,10},{10,12},{12... | collective-permute-start | bytes 1966088 | tf_op jit(solution)/shard_map/ppermute | solution.py:86
  466.9 26.7 %collective-permute-start.36 = (bf16[160,2048]{1,0:T(8,128)(2,1)}, bf16[160,2048]{1,0:T(8,128)(2,1)S(1)}, u32[]{:S(2)}, u32[]{:S(2)}) collective-permute-start(bf16[160,2048]{1,0:T(8,128)(2,1)} %get-tuple-element.336), channel_id=1, source_target_pairs={{0,1},{2,0},{4,2},{6,4},{7,6},{5,7},{3,5},{1,3},{8,9},{10,8},{12,1... | collective-permute-start | bytes 1966088 | tf_op jit(solution)/shard_map/ppermute | solution.py:86
  469.0 27.8 %all-to-all-start.4 = ((bf16[8,160,256]{2,1,0:T(8,128)(2,1)}), bf16[8,160,256]{2,1,0:T(8,128)(2,1)S(1)}, u32[]{:S(2)}, u32[]{:S(2)}) async-start(bf16[8,160,256]{2,1,0:T(8,128)(2,1)} %bitcast.166), calls=%async_computation.4 | async-start | bytes 1310720 | tf_op jit(solution)/shard_map/all_to_all | solution.py:245
  473.5 228.6 %reduce-scatter.8.cloned.1.call-start = ((), (), s32[]{:S(2)}) async-start(), calls=%async_computation.14 | async-start | bytes 10485760 | tf_op jit(solution)/shard_map/reduce_scatter | solution.py:729
  473.6 44.8 %collective-permute-start.37 = (bf16[160,2048]{1,0:T(8,128)(2,1)S(1)}, bf16[160,2048]{1,0:T(8,128)(2,1)}, u32[]{:S(2)}, u32[]{:S(2)}) collective-permute-start(bf16[160,2048]{1,0:T(8,128)(2,1)S(1)} %get-tuple-element.174), channel_id=1, source_target_pairs={{0,2},{2,4},{4,6},{6,7},{7,5},{5,3},{3,1},{1,0},{8,10},{10,12},{12... | collective-permute-start | bytes 1966088 | tf_op jit(solution)/shard_map/ppermute | solution.py:86
  475.5 42.9 %collective-permute-start.38 = (bf16[160,2048]{1,0:T(8,128)(2,1)S(1)}, bf16[160,2048]{1,0:T(8,128)(2,1)}, u32[]{:S(2)}, u32[]{:S(2)}) collective-permute-start(bf16[160,2048]{1,0:T(8,128)(2,1)S(1)} %get-tuple-element.174), channel_id=1, source_target_pairs={{0,1},{2,0},{4,2},{6,4},{7,6},{5,7},{3,5},{1,3},{8,9},{10,8},{12,1... | collective-permute-start | bytes 1966088 | tf_op jit(solution)/shard_map/ppermute | solution.py:86
  518.4 25.6 %collective-permute-start.39 = (bf16[160,2048]{1,0:T(8,128)(2,1)}, bf16[160,2048]{1,0:T(8,128)(2,1)}, u32[]{:S(2)}, u32[]{:S(2)}) collective-permute-start(bf16[160,2048]{1,0:T(8,128)(2,1)} %collective-permute-done.37), channel_id=1, source_target_pairs={{0,2},{2,4},{4,6},{6,7},{7,5},{5,3},{3,1},{1,0},{8,10},{10,12},{12... | collective-permute-start | bytes 1966088 | tf_op jit(solution)/shard_map/ppermute | solution.py:86
  518.4 25.5 %collective-permute-start.40 = (bf16[160,2048]{1,0:T(8,128)(2,1)}, bf16[160,2048]{1,0:T(8,128)(2,1)}, u32[]{:S(2)}, u32[]{:S(2)}) collective-permute-start(bf16[160,2048]{1,0:T(8,128)(2,1)} %collective-permute-done.38), channel_id=1, source_target_pairs={{0,1},{2,0},{4,2},{6,4},{7,6},{5,7},{3,5},{1,3},{8,9},{10,8},{12,1... | collective-permute-start | bytes 1966088 | tf_op jit(solution)/shard_map/ppermute | solution.py:86
  544.1 19.6 %collective-permute-start.41 = (bf16[160,2048]{1,0:T(8,128)(2,1)}, bf16[160,2048]{1,0:T(8,128)(2,1)S(1)}, u32[]{:S(2)}, u32[]{:S(2)}) collective-permute-start(bf16[160,2048]{1,0:T(8,128)(2,1)} %collective-permute-done.39), channel_id=1, source_target_pairs={{0,2},{2,4},{4,6},{6,7},{7,5},{5,3},{3,1},{1,0},{8,10},{10,12},{12... | collective-permute-start | bytes 1966088 | tf_op jit(solution)/shard_map/ppermute | solution.py:86
  544.6 19.2 %collective-permute-start.42 = (bf16[160,2048]{1,0:T(8,128)(2,1)}, bf16[160,2048]{1,0:T(8,128)(2,1)S(1)}, u32[]{:S(2)}, u32[]{:S(2)}) collective-permute-start(bf16[160,2048]{1,0:T(8,128)(2,1)} %collective-permute-done.40), channel_id=1, source_target_pairs={{0,1},{2,0},{4,2},{6,4},{7,6},{5,7},{3,5},{1,3},{8,9},{10,8},{12,1... | collective-permute-start | bytes 1966088 | tf_op jit(solution)/shard_map/ppermute | solution.py:86
  567.3 29.8 %collective-permute-start.45 = (bf16[80,2048]{1,0:T(8,128)(2,1)}, bf16[80,2048]{1,0:T(8,128)(2,1)}, u32[]{:S(2)}, u32[]{:S(2)}) collective-permute-start(bf16[80,2048]{1,0:T(8,128)(2,1)} %get-tuple-element.333), channel_id=1, source_target_pairs={{0,2},{2,4},{4,6},{6,7},{7,5},{5,3},{3,1},{1,0},{8,10},{10,12},{12... | collective-permute-start | bytes 983048 | tf_op jit(solution)/shard_map/ppermute | solution.py:86
  567.8 29.4 %collective-permute-start.46 = (bf16[80,2048]{1,0:T(8,128)(2,1)}, bf16[80,2048]{1,0:T(8,128)(2,1)}, u32[]{:S(2)}, u32[]{:S(2)}) collective-permute-start(bf16[80,2048]{1,0:T(8,128)(2,1)} %get-tuple-element.332), channel_id=1, source_target_pairs={{0,1},{2,0},{4,2},{6,4},{7,6},{5,7},{3,5},{1,3},{8,9},{10,8},{12,1... | collective-permute-start | bytes 983048 | tf_op jit(solution)/shard_map/ppermute | solution.py:86
  569.4 27.8 %collective-permute-start.43 = (bf16[80,2048]{1,0:T(8,128)(2,1)}, bf16[80,2048]{1,0:T(8,128)(2,1)}, u32[]{:S(2)}, u32[]{:S(2)}) collective-permute-start(bf16[80,2048]{1,0:T(8,128)(2,1)} %slice.417), channel_id=1, source_target_pairs={{0,2},{2,4},{4,6},{6,7},{7,5},{5,3},{3,1},{1,0},{8,10},{10,12},{12... | collective-permute-start | bytes 983048 | tf_op jit(solution)/shard_map/ppermute | solution.py:86
  569.8 27.3 %collective-permute-start.44 = (bf16[80,2048]{1,0:T(8,128)(2,1)}, bf16[80,2048]{1,0:T(8,128)(2,1)}, u32[]{:S(2)}, u32[]{:S(2)}) collective-permute-start(bf16[80,2048]{1,0:T(8,128)(2,1)} %slice.418), channel_id=1, source_target_pairs={{0,1},{2,0},{4,2},{6,4},{7,6},{5,7},{3,5},{1,3},{8,9},{10,8},{12,1... | collective-permute-start | bytes 983048 | tf_op jit(solution)/shard_map/ppermute | solution.py:86
  572.3 14.5 %all-to-all-start.6 = ((f32[8,1,4640]{2,1,0:T(1,128)}), f32[8,1,4640]{2,1,0:T(1,128)}, u32[]{:S(2)}, u32[]{:S(2)}) async-start(f32[8,1,4640]{2,1,0:T(1,128)} %copy.170), calls=%async_computation.7 | async-start | bytes 303104 | tf_op jit(solution)/shard_map/all_to_all | solution.py:245
  599.5 17.1 %collective-permute-start.48 = (bf16[160,2048]{1,0:T(8,128)(2,1)}, bf16[160,2048]{1,0:T(8,128)(2,1)}, u32[]{:S(2)}, u32[]{:S(2)}) collective-permute-start(bf16[160,2048]{1,0:T(8,128)(2,1)} %pad_maximum_fusion.11), channel_id=1, source_target_pairs={{0,1},{2,0},{4,2},{6,4},{7,6},{5,7},{3,5},{1,3},{8,9},{10,8},{12,1... | collective-permute-start | bytes 1966088 | tf_op jit(solution)/shard_map/ppermute | solution.py:86
  605.0 18.4 %collective-permute-start.53 = (bf16[8,2,64,768]{3,2,0,1:T(8,128)(2,1)}, bf16[8,2,64,768]{3,2,0,1:T(8,128)(2,1)}, u32[]{:S(2)}, u32[]{:S(2)}) collective-permute-start(bf16[8,2,64,768]{3,2,0,1:T(8,128)(2,1)} %bitcast.164), channel_id=1, source_target_pairs={{0,8},{8,0},{16,24},{24,16},{1,9},{9,1},{17,25},{25,17},{2,10},{10... | collective-permute-start | bytes 4718600 | tf_op jit(solution)/shard_map/ppermute | solution.py:202
  605.9 17.4 %collective-permute-start.47 = (bf16[160,2048]{1,0:T(8,128)(2,1)}, bf16[160,2048]{1,0:T(8,128)(2,1)S(1)}, u32[]{:S(2)}, u32[]{:S(2)}) collective-permute-start(bf16[160,2048]{1,0:T(8,128)(2,1)} %pad_maximum_fusion.10), channel_id=1, source_target_pairs={{0,2},{2,4},{4,6},{6,7},{7,5},{5,3},{3,1},{1,0},{8,10},{10,12},{12... | collective-permute-start | bytes 1966088 | tf_op jit(solution)/shard_map/ppermute | solution.py:86
  625.3 26.2 %collective-permute-start.54 = (bf16[8,1,64,768]{3,2,0,1:T(8,128)(2,1)S(1)}, bf16[8,1,64,768]{3,2,0,1:T(8,128)(2,1)S(1)}, u32[]{:S(2)}, u32[]{:S(2)}) collective-permute-start(bf16[8,1,64,768]{3,2,0,1:T(8,128)(2,1)S(1)} %constant_dynamic-slice_fusion.1), channel_id=1, source_target_pairs={{0,16},{8,24},{16,0},{24,8},{1,17},{9,25},{17,1},{25,9},{2,18},{10... | collective-permute-start | bytes 2359304 | tf_op jit(solution)/shard_map/ppermute | solution.py:202
  629.1 29.7 %collective-permute-start.49 = (bf16[160,2048]{1,0:T(8,128)(2,1)}, bf16[160,2048]{1,0:T(8,128)(2,1)S(1)}, u32[]{:S(2)}, u32[]{:S(2)}) collective-permute-start(bf16[160,2048]{1,0:T(8,128)(2,1)} %get-tuple-element.328), channel_id=1, source_target_pairs={{0,2},{2,4},{4,6},{6,7},{7,5},{5,3},{3,1},{1,0},{8,10},{10,12},{12... | collective-permute-start | bytes 1966088 | tf_op jit(solution)/shard_map/ppermute | solution.py:86
  629.5 29.3 %collective-permute-start.51 = (bf16[160,2048]{1,0:T(8,128)(2,1)}, bf16[160,2048]{1,0:T(8,128)(2,1)}, u32[]{:S(2)}, u32[]{:S(2)}) collective-permute-start(bf16[160,2048]{1,0:T(8,128)(2,1)} %get-tuple-element.329), channel_id=1, source_target_pairs={{0,1},{2,0},{4,2},{6,4},{7,6},{5,7},{3,5},{1,3},{8,9},{10,8},{12,1... | collective-permute-start | bytes 1966088 | tf_op jit(solution)/shard_map/ppermute | solution.py:86
  631.3 26.7 %collective-permute-start.58 = (bf16[1,64,2048]{2,1,0:T(8,128)(2,1)S(1)}, bf16[1,64,2048]{2,1,0:T(8,128)(2,1)S(1)}, u32[]{:S(2)}, u32[]{:S(2)}) collective-permute-start(bf16[1,64,2048]{2,1,0:T(8,128)(2,1)S(1)} %constant_dynamic-slice_fusion), channel_id=1, source_target_pairs={{0,16},{8,24},{16,0},{24,8},{1,17},{9,25},{17,1},{25,9},{2,18},{10... | collective-permute-start | bytes 786440 | tf_op jit(solution)/shard_map/ppermute | solution.py:202
  652.5 27.1 %all-to-all-start.5 = ((bf16[8,64,768]{2,1,0:T(8,128)(2,1)}), bf16[8,64,768]{2,1,0:T(8,128)(2,1)S(1)}, u32[]{:S(2)}, u32[]{:S(2)}) async-start(bf16[8,64,768]{2,1,0:T(8,128)(2,1)} %fusion.23), calls=%async_computation.6 | async-start | bytes 1572864 | tf_op jit(solution)/shard_map/all_to_all | solution.py:245
  661.8 23.1 %collective-permute-start.50 = (bf16[160,2048]{1,0:T(8,128)(2,1)}, bf16[160,2048]{1,0:T(8,128)(2,1)}, u32[]{:S(2)}, u32[]{:S(2)}) collective-permute-start(bf16[160,2048]{1,0:T(8,128)(2,1)} %get-tuple-element.326), channel_id=1, source_target_pairs={{0,2},{2,4},{4,6},{6,7},{7,5},{5,3},{3,1},{1,0},{8,10},{10,12},{12... | collective-permute-start | bytes 1966088 | tf_op jit(solution)/shard_map/ppermute | solution.py:86
  663.8 23.4 %collective-permute-start.52 = (bf16[160,2048]{1,0:T(8,128)(2,1)}, bf16[160,2048]{1,0:T(8,128)(2,1)}, u32[]{:S(2)}, u32[]{:S(2)}) collective-permute-start(bf16[160,2048]{1,0:T(8,128)(2,1)} %get-tuple-element.327), channel_id=1, source_target_pairs={{0,1},{2,0},{4,2},{6,4},{7,6},{5,7},{3,5},{1,3},{8,9},{10,8},{12,1... | collective-permute-start | bytes 1966088 | tf_op jit(solution)/shard_map/ppermute | solution.py:86
  667.3 38.8 %collective-permute-start.60 = (bf16[2,64,2048]{2,1,0:T(8,128)(2,1)}, bf16[2,64,2048]{2,1,0:T(8,128)(2,1)}, u32[]{:S(2)}, u32[]{:S(2)}) collective-permute-start(bf16[2,64,2048]{2,1,0:T(8,128)(2,1)} %maximum_select_fusion.8), channel_id=1, source_target_pairs={{0,8},{8,0},{16,24},{24,16},{1,9},{9,1},{17,25},{25,17},{2,10},{10... | collective-permute-start | bytes 1572872 | tf_op jit(solution)/shard_map/ppermute | solution.py:202
  681.0 16.6 %collective-permute-start.55 = (bf16[1,3,64,2048]{3,2,1,0:T(8,128)(2,1)S(1)}, bf16[1,3,64,2048]{3,2,1,0:T(8,128)(2,1)S(1)}, u32[]{:S(2)}, u32[]{:S(2)}) collective-permute-start(bf16[1,3,64,2048]{3,2,1,0:T(8,128)(2,1)S(1)} %broadcast_in_dim_reshape.2), channel_id=1, source_target_pairs={{0,16},{8,24},{16,0},{24,8},{1,17},{9,25},{17,1},{25,9},{2,18},{10... | collective-permute-start | bytes 2359304 | tf_op jit(solution)/shard_map/ppermute | solution.py:202
  (172 other events, 1684.0 us)
Sparse Core Ops, SparseCore 0:
  24.0 67.7 all-gather.2
  122.2 97.6 all-gather.4
  413.7 73.0 reduce-scatter.3
  489.5 71.7 reduce-scatter.5
  563.7 78.2 reduce-scatter.7

commit v8 on v7

--- a/solution.py
+++ b/solution.py
@@ -1,3 +1,5 @@
+import functools
+
 import jax
 import jax.numpy as jnp
 from jax import lax
@@ -206,31 +208,34 @@
     return (lax.axis_index("rep") // distance) % 2
 
 
-def rep_gather(values):
-    gathered = values[None]
-    distance = lax.axis_size("rep") // 2
-    while distance:
+def rep_distances():
+    count, distance, distances = lax.axis_size("rep"), 1, []
+    while distance < count:
+        distances.append(distance)
+        distance *= 2
+    return distances
+
+
+def rep_gather(gathered, distances):
+    for distance in distances:
+        shape = gathered.shape[1:]
         other = rep_exchange(gathered, distance)
         mine_first = jnp.stack([gathered, other], axis=1)
         other_first = jnp.stack([other, gathered], axis=1)
         gathered = jnp.where(rep_bit(distance) == 0, mine_first, other_first)
-        gathered = gathered.reshape((-1,) + values.shape)
-        distance //= 2
+        gathered = gathered.reshape((-1,) + shape)
     return gathered
 
 
-def rep_scatter(values, axis):
-    distance = 1
-    count = lax.axis_size("rep")
-    while distance < count:
+def rep_scatter(values, axis, distances):
+    for distance in distances:
         shape = values.shape
         pairs = values.reshape(shape[:axis] + (shape[axis] // 2, 2) + shape[axis + 1 :])
         bit = rep_bit(distance)
         keep = lax.dynamic_index_in_dim(pairs, bit, axis + 1, keepdims=False)
         send = lax.dynamic_index_in_dim(pairs, 1 - bit, axis + 1, keepdims=False)
         values = add_low(keep, rep_exchange(send, distance))
-        distance *= 2
-    return lax.index_in_dim(values, 0, axis, keepdims=False)
+    return values
 
 
 def rep_sum(values):
@@ -339,6 +344,93 @@
             transcendentals=0,
         ),
     )(gback, uback, gate_weight, up_weight)
+
+
+def attention_back_kernel(
+    block, scale, query_ref, key_ref, value_ref, grad_ref, total_ref, column_ref, line_ref,
+    query_raw_ref, key_raw_ref, gains_ref, cosine_ref, sine_ref, sent_ref, part_ref, key_sum, value_sum
+):
+    head, heads = pl.program_id(0), pl.num_programs(0)
+    rows, depth = query_ref.shape
+    lane = lax.broadcasted_iota(jnp.int32, (1, depth), 1)
+    sign = jnp.where(lane < depth // 2, 1.0, -1.0)
+    key_sum[...] = jnp.zeros_like(key_sum)
+    value_sum[...] = jnp.zeros_like(value_sum)
+
+    @pl.when(head == 0)
+    def _():
+        part_ref[...] = jnp.zeros_like(part_ref)
+
+    def finish(back, raw, gain, cosine, sine, row, column, which):
+        turned = back * cosine + pltpu.roll(back * sine, depth // 2, axis=1) * sign
+        inverse = lax.rsqrt(jnp.mean(raw * raw, axis=-1, keepdims=True) + 1e-5)
+        result, part = norm_backward(raw, inverse, gain, turned)
+        sent_ref[row, pl.ds(pl.multiple_of(column * depth, depth), depth)] = result.astype(low_type)
+        part_ref[which : which + 1, :] += jnp.sum(part, axis=0, keepdims=True)
+
+    @pl.loop(0, rows // block)
+    def _(step):
+        row = pl.ds(pl.multiple_of(step * block, block), block)
+        query, grad = query_ref[row, :], grad_ref[row, :]
+        scores = mm(query, key_ref[...], 1, 1) * scale
+        scores = jnp.where(column_ref[row, :] == line_ref[...], scores, masked_value)
+        weights = jnp.exp(scores - total_ref[row, pl.ds(0, 1)])
+        weight_grad = mm(grad, value_ref[...], 1, 1)
+        row_dot = jnp.sum(weights * weight_grad, axis=-1, keepdims=True)
+        score_grad = (weights * (weight_grad - row_dot)).astype(low_type)
+        key_sum[...] += mm(score_grad, query, 0, 0)
+        value_sum[...] += mm(weights.astype(low_type), grad, 0, 0)
+        query_back = mm(score_grad, key_ref[...], 1, 0) * scale
+        finish(query_back, query_raw_ref[row, :], gains_ref[0:1, :], cosine_ref[row, :], sine_ref[row, :], row, head, 0)
+
+    @pl.loop(0, rows // block)
+    def _(step):
+        row = pl.ds(pl.multiple_of(step * block, block), block)
+        finish(key_sum[row, :] * scale, key_raw_ref[row, :], gains_ref[1:2, :], cosine_ref[row, :], sine_ref[row, :], row, heads + head, 1)
+        sent_ref[row, pl.ds(pl.multiple_of((2 * heads + head) * depth, depth), depth)] = value_sum[row, :].astype(low_type)
+
+
+def attention_back(query, key, value, grad, totals, segment, query_raw, key_raw, gains, cosine, sine, block=256):
+    rows, width = query.shape
+    depth = cosine.shape[1]
+    heads = width // depth
+    by_head = pl.BlockSpec((rows, depth), lambda h: (0, h))
+    def whole(array):
+        return pl.BlockSpec(array.shape, lambda h: (0, 0))
+    column, line = segment[:, None], segment[None, :]
+    return pl.pallas_call(
+        functools.partial(attention_back_kernel, block, depth ** -0.5),
+        grid=(heads,),
+        in_specs=[by_head] * 4 + [pl.BlockSpec((None, rows, 1), lambda h: (h, 0, 0)), whole(column), whole(line), by_head, by_head, whole(gains), whole(cosine), whole(sine)],
+        out_specs=[pl.BlockSpec((rows, 3 * width), lambda h: (0, 0)), pl.BlockSpec((2, depth), lambda h: (0, 0))],
+        out_shape=[jax.ShapeDtypeStruct((rows, 3 * width), low_type), jax.ShapeDtypeStruct((2, depth), wide_type)],
+        scratch_shapes=[pltpu.VMEM((rows, depth), wide_type)] * 2,
+        compiler_params=pltpu.CompilerParams(vmem_limit_bytes=56 << 20),
+        cost_estimate=pl.CostEstimate(flops=10 * rows * rows * width, bytes_accessed=30 * rows * width, transcendentals=heads * rows * rows),
+    )(query, key, value, grad, totals, column, line, query_raw, key_raw, gains, cosine, sine)
+
+
+def block_product_kernel(left_ref, *refs):
+    out_ref = refs[-1]
+    rows = refs[0].shape[0]
+    total = None
+    for j, ref in enumerate(refs[:-1]):
+        term = mm(left_ref[j * rows : (j + 1) * rows, :], ref[...], 0, 0)
+        total = term if total is None else total + term
+    out_ref[...] = total.astype(low_type)
+
+
+def block_product(left, blocks):
+    rows, width = blocks[0].shape
+    tile = 512
+    return pl.pallas_call(
+        block_product_kernel,
+        grid=(width // tile,),
+        in_specs=[pl.BlockSpec(left.shape, lambda j: (0, 0))] + [pl.BlockSpec((rows, tile), lambda j: (0, j))] * len(blocks),
+        out_specs=pl.BlockSpec((left.shape[1], tile), lambda j: (0, j)),
+        out_shape=jax.ShapeDtypeStruct((left.shape[1], width), low_type),
+        cost_estimate=pl.CostEstimate(flops=2 * left.size * width, bytes_accessed=2 * left.size + 2 * len(blocks) * rows * width, transcendentals=0),
+    )(left, *blocks)
 
 
 def body(
@@ -400,15 +492,6 @@
         route_code = route_code + jnp.where(hit, 1 + kept, 0)
     small_sent = jnp.concatenate([route_code.astype(low_type), router_weight], axis=0)
 
-    small_flat = small_sent.reshape(-1, head_dim)
-    small_all = swap_all(
-        jnp.broadcast_to(small_flat[None], (group_count,) + small_flat.shape)
-    ).reshape(group_count, row_count + width_here, expert_total)
-    code_all = reorder(small_all[:, :row_count], device_of_slot).reshape(
-        group_rows, expert_total
-    )
-    full_router = small_all[:, row_count:].reshape(model_width, expert_total)
-
     projections = jnp.concatenate(
         [
             lax.dynamic_slice_in_dim(piece, replica * share, share, 0).reshape(
@@ -418,11 +501,22 @@
         ],
         axis=2,
     ).transpose(1, 0, 2)
+    scatter_order = rep_distances()
+    gather_order = scatter_order[::-1]
+    swapped = swap_all(projections)
     head_weight = (
-        rep_gather(swap_all(projections))
+        rep_gather(swapped[None], gather_order)
         .transpose(1, 0, 2, 3)
         .reshape(model_width, 3 * width_here)
     )
+    small_flat = after(small_sent.reshape(-1, head_dim), swapped)
+    small_all = swap_all(
+        jnp.broadcast_to(small_flat[None], (group_count,) + small_flat.shape)
+    ).reshape(group_count, row_count + width_here, expert_total)
+    code_all = reorder(small_all[:, :row_count], device_of_slot).reshape(
+        group_rows, expert_total
+    )
+    full_router = small_all[:, row_count:].reshape(model_width, expert_total)
     column_share = model_width // replica_count
     output_share = gather_rows(
         lax.dynamic_slice_in_dim(output_weight, replica * column_share, column_share, 1)
@@ -433,13 +527,6 @@
 
     def chunk_of(array, chunk):
         return array[chunk * chunk_rows : (chunk + 1) * chunk_rows]
-
-    def gather_ring(values):
-        ring = RingGather(values)
-        for _ in range(group_count // 2):
-            ring.start()
-            ring.finish()
-        return ring.blocks
 
     def slot_rows(array):
         return lambda slot: array[slot * row_count : (slot + 1) * row_count]
@@ -449,12 +536,26 @@
             rows.reshape(group_count, row_count, rows.shape[1]), index
         ).reshape(rows.shape)
 
-    token_all = jnp.concatenate(gather_ring(tokens), axis=0)
+    token_ring = RingGather(tokens)
+    for step in range(group_count // 2):
+        if step == group_count // 2 - 1:
+            token_ring.sent = (after(token_ring.sent[0], output_share), token_ring.sent[1])
+        token_ring.start()
+        token_ring.finish()
+    token_all = jnp.concatenate(token_ring.blocks, axis=0)
     token_late, cot_own = lax.optimization_barrier((token_all, cotangent))
     token_all = token_late
     cot_ordered = gather_rows(cot_own)
     cot_all = reorder_rows(cot_ordered, device_of_slot)
 
+    halves = 2 if column_share % 256 == 0 else 1
+    piece_width = column_share // halves
+    far = replica_count // 2
+    far_pieces = [
+        rep_exchange(output_share[:, i * piece_width : (i + 1) * piece_width], far)
+        for i in range(halves)
+    ]
+    head_weight = after(head_weight, far_pieces[0])
     token_wide = token_all.astype(wide_type)
     inverse_all = inverse_rms(token_wide)
     first_all = (token_wide * inverse_all * prenorm_gain).astype(low_type)
@@ -496,23 +597,23 @@
     mixed_low = jnp.concatenate(mixed_parts, axis=1)
 
     mixed_ordered = reorder_rows(mixed_low, slot_of_device)
-    output_pieces = {0: output_share}
-    distance = replica_count // 2
-    while distance:
-        for j in list(output_pieces):
-            output_pieces[j ^ distance] = rep_exchange(output_pieces[j], distance)
-        if distance == replica_count // 2:
-            output_pieces[distance] = after(output_pieces[distance], mixed_ordered)
-        distance //= 2
+    output_pieces = {(0, 0): output_share}
+    for i in range(halves):
+        output_pieces[far, i * piece_width] = after(far_pieces[i], mixed_ordered)
+    for distance in gather_order[1:]:
+        for j, start in list(output_pieces):
+            output_pieces[j ^ distance, start] = rep_exchange(
+                after(output_pieces[j, start], mixed_ordered), distance
+            )
     mixed_own = (
         swap_all(mixed_ordered.reshape(group_count, row_count, width_here))
         .transpose(1, 0, 2)
         .reshape(row_count, model_width)
     )
     attention = jnp.zeros((row_count, model_width), wide_type)
-    for j, piece in output_pieces.items():
+    for (j, start), piece in output_pieces.items():
         attention = lax.dynamic_update_slice_in_dim(
-            attention, mm(mixed_own, piece, 1, 0), (replica ^ j) * column_share, 1
+            attention, mm(mixed_own, piece, 1, 0), (replica ^ j) * column_share + start, 1
         )
     residual = tokens.astype(wide_type) + attention
     inverse_two = inverse_rms(residual)
@@ -613,10 +714,10 @@
         residual_grad = upstream + post_back
         attention_low = residual_grad.astype(low_type)
         mixed_grad_own = jnp.zeros((row_count, model_width), wide_type)
-        for j, piece in output_pieces.items():
+        for (j, start), piece in output_pieces.items():
             mixed_grad_own = mixed_grad_own + mm(
                 lax.dynamic_slice_in_dim(
-                    attention_low, (replica ^ j) * column_share, column_share, 1
+                    attention_low, (replica ^ j) * column_share + start, piece.shape[1], 1
                 ),
                 piece,
                 1,
@@ -644,46 +745,31 @@
     layer_out = (valid_own * (residual + mixture)).astype(low_type)
     mixed_grad = reorder_rows(swap.received.reshape(group_rows, width_here), device_of_slot)
 
-    def head_backward(head, grad_head):
-        query_raw, key_raw, query_low, key_low, value_low, log_total = kept_heads[head]
-        query_inverse, key_inverse = inverse_rms(query_raw), inverse_rms(key_raw)
-        scores = jnp.where(allowed, mm(query_low, key_low, 1, 1) * score_scale, masked_value)
-        weights = jnp.exp(scores - log_total)
-        weight_grad = mm(grad_head, value_low, 1, 1)
-        row_dot = jnp.sum(weights * weight_grad, axis=-1, keepdims=True)
-        score_grad = (weights * (weight_grad - row_dot)).astype(low_type)
-        query_back = mm(score_grad, key_low, 1, 0) * score_scale
-        key_back = mm(score_grad, query_low, 0, 0) * score_scale
-        value_back = mm(weights.astype(low_type), grad_head, 0, 0)
-        query_unturned = query_back * cosine + turn_back(query_back * sine_part)
-        key_unturned = key_back * cosine + turn_back(key_back * sine_part)
-        query_before, query_gain_part = norm_backward(
-            query_raw, query_inverse, querynorm_gain, query_unturned
-        )
-        key_before, key_gain_part = norm_backward(
-            key_raw, key_inverse, keynorm_gain, key_unturned
-        )
-        return (
-            query_before.astype(low_type),
-            key_before.astype(low_type),
-            value_back.astype(low_type),
-            jnp.sum(query_gain_part, axis=0),
-            jnp.sum(key_gain_part, axis=0),
-        )
-
+    query_raws, key_raws, query_lows, key_lows, value_lows = (
+        jnp.concatenate([kept[i] for kept in kept_heads], axis=1) for i in range(5)
+    )
+    log_totals = jnp.stack([kept[5] for kept in kept_heads])
     attention_gather = RingGather(attention_low)
-    head_results = []
-    for head in range(heads_here):
-        head_results.append(
-            window(
-                [attention_gather],
-                lambda grad_head: head_backward(head, grad_head),
-                mixed_grad[:, head * head_dim : (head + 1) * head_dim],
+    sent, gain_parts = window(
+        [attention_gather],
+        lambda grads: tuple(
+            attention_back(
+                query_lows,
+                key_lows,
+                value_lows,
+                grads,
+                log_totals,
+                segment,
+                query_raws,
+                key_raws,
+                jnp.stack([querynorm_gain, keynorm_gain]),
+                cosine,
+                sine_part,
             )
-        )
-    sent = jnp.concatenate(
-        [head_results[head][part] for part in range(3) for head in range(heads_here)], axis=1
-    )
+        ),
+        mixed_grad,
+    )
+    querynorm_part, keynorm_part = gain_parts[0], gain_parts[1]
     down_sum = lax.psum_scatter(
         down_part.reshape(experts_here, hidden_here, model_width),
         "rep",
@@ -691,16 +777,19 @@
         tiled=True,
     )
     sent, down_sum = tie(sent, down_sum)
-    querynorm_part = sum(result[3] for result in head_results)
-    keynorm_part = sum(result[4] for result in head_results)
-    def first_work(sent):
+
+    def first_work(sent, head):
         first_part = mm(sent, head_weight, 1, 1)
         prenorm_part = jnp.sum(first_part * token_wide * inverse_all, axis=0)
-        return first_part.astype(low_type), prenorm_part
-
-    while attention_gather.step < group_count // 2 - 2:
-        window([attention_gather], lambda: ())
-    first_low, prenorm_part = window([attention_gather], first_work, sent)
+        return first_part.astype(low_type), prenorm_part, rep_scatter(head, 1, scatter_order[:1])
+
+    head_part = window([attention_gather], grad_of, first_all, sent)
+    first_low, prenorm_part, head_part = window(
+        [attention_gather],
+        first_work,
+        sent,
+        head_part.reshape(group_count, replica_count, share, 3 * width_here),
+    )
 
     def small_swap(parts):
         return swap_all(
@@ -717,37 +806,53 @@
         return pieces
 
     first_ring = RingSum(slot_rows(first_low), row_count)
-    head_part = window(
+    small_parts = [router_part, postnorm_part, prenorm_part, querynorm_part, keynorm_part]
+    head_part, small_swapped = window(
         [attention_gather, first_ring],
-        grad_of,
-        first_all,
-        sent,
-    )
-    attention_all = jnp.concatenate(attention_gather.blocks, axis=0)
-    output_part = window([first_ring], grad_of, mixed_low, attention_all)
+        lambda head, *small: (rep_scatter(head, 1, scatter_order[1:]), small_swap(small)),
+        head_part,
+        *small_parts,
+    )
     gate_sum = lax.psum_scatter(gate_part, "rep", scatter_dimension=0, tiled=True)
     up_sum = lax.psum_scatter(up_part, "rep", scatter_dimension=0, tiled=True)
-    for _ in range(2, group_count // 2):
-        first_ring.start()
-        first_ring.finish()
+    head_swap = Swap(head_part.reshape(group_count, share, 3 * width_here), 0)
+    output_part = window(
+        [first_ring, head_swap],
+        lambda mixed, *blocks: block_product(mixed, blocks),
+        mixed_low,
+        *attention_gather.blocks,
+    )
+    head_rows, output_part, small_sums = window(
+        [first_ring],
+        lambda head, output, small: (
+            rep_gather(
+                head.reshape(group_count, share, 3, width_here)
+                .transpose(2, 1, 0, 3)
+                .reshape(1, 3, share, model_width),
+                gather_order[:-1],
+            ),
+            rep_scatter(output, 0, scatter_order[:1]),
+            small_pieces(small, small_parts),
+        ),
+        head_swap.received,
+        output_part.reshape(replica_count, share, model_width),
+        small_swapped,
+    )
+    head_rows, output_part = window(
+        [first_ring],
+        lambda head, output: (
+            rep_gather(head, gather_order[-1:]),
+            rep_scatter(output, 0, scatter_order[1:]),
+        ),
+        head_rows,
+        output_part,
+    )
     first_grad = first_ring.total()
-    head_rows = rep_gather(
-        swap_all(
-            rep_scatter(
-                head_part.reshape(group_count, replica_count, share, 3 * width_here), 1
-            )
-        )
-        .reshape(group_count, share, 3, width_here)
-        .transpose(2, 1, 0, 3)
-        .reshape(3, share, model_width)
-    )
     output_grad = (
-        rep_gather(rep_scatter(output_part.reshape(replica_count, share, model_width), 0))
+        rep_gather(output_part, gather_order)
         .reshape(width_here, model_width)
         .astype(wide_type)
     )
-    small_parts = [router_part, postnorm_part, prenorm_part, querynorm_part, keynorm_part]
-    small_sums = small_pieces(small_swap(small_parts), small_parts)
     query_grad, key_grad, value_grad = (
         head_rows[:, block].reshape(width_here, model_width).astype(wide_type)
         for block in range(3)

time: 734 us -> 729 us (level)
  Pallas kernels: 72.6 us -> 102 us
  matrix products: 153 us -> 136 us
  local copies, waits for them, and re-layouts: 101 us -> 87.8 us
  other arithmetic: 110 us -> 99.3 us
  starting transfers between devices: 101 us -> 110 us
    all_to_all x7, waiting for transfers between devices: 52.1 us -> 22.5 us  [swap_all(): return lax.all_to_all(values, 'ep', split_axis=0, concat_axis=0, tiled=True)]
    pallas_call x0 -> x2, Pallas kernels: none -> 29.2 us  [the longest x1 22.7 us: attention_back(): pl.pallas_call(functools.partial(attention_back_kernel, block, depth ** (...]
    unnamed x382 -> x320, local copies, waits for them, and re-layouts: 59.8 us -> 34.2 us
    dot_general x35 -> x30, matrix products: 153 us -> 136 us  [mm(): lax.dot_general(left, right, (((left_dim,), (right_dim,)), ((), ())), pre...]
    ppermute x48, waiting for transfers between devices: 73.3 us -> 89.5 us  [ring_shift(): return lax.ppermute(values, 'ep', pairs)]
    convert_element_type x6 -> x1, other arithmetic: 9.94 us -> 1.63 us  [body(): output_grad = rep_gather(output_part, gather_order).reshape(width_here, m...]
    ppermute x15 -> x17, waiting for transfers between devices: 44.5 us -> 51.3 us  [rep_exchange(): lax.ppermute(values, 'rep', [(i, i ^ distance) for i in range(count)])]
    convert_element_type x13 -> x14, other arithmetic: 25.6 us -> 31.3 us  [add_low(): return (left.astype(wide_type) + right.astype(wide_type)).astype(low_type)]
  transfers between devices with their start and end apart: 75 -> 77, of which waited for: 19 -> 28; matrix products, arithmetic and copies ran while one was open for 45% -> 41% of each run, Pallas kernels for 5% -> 9%
where the time goes in v8:
time: 729 us; the launch traced here: 721 us
  waiting for transfers between devices  169 us (23%)
  matrix products  136 us (19%)
  starting transfers between devices  110 us (15%)
  Pallas kernels  102 us (14%)
  other arithmetic  99.3 us (14%)
  local copies, waits for them, and re-layouts  87.8 us (12%)
  between operations  17.2 us (2%)
    dot_general x30, matrix products, mm(): lax.dot_general(left, right, (((left_dim,), (right_dim,)), ((), ())), pre...  136 us
    ppermute x48, waiting for transfers between devices, ring_shift(): return lax.ppermute(values, 'ep', pairs)  89.5 us
    ppermute x48, starting transfers between devices, ring_shift(): return lax.ppermute(values, 'ep', pairs)  64.9 us
    ppermute x17, waiting for transfers between devices, rep_exchange(): lax.ppermute(values, 'rep', [(i, i ^ distance) for i in range(count)])  51.3 us
    pallas_call x2, Pallas kernels, expert_pass(): pl.pallas_call(expert_kernel, grid=(experts, steps), in_specs=[pl.BlockSp...  39.1 us
    unnamed x320, local copies, waits for them, and re-layouts  34.2 us
    pallas_call x2, Pallas kernels, expert_back(): pl.pallas_call(expert_back_kernel, grid=(depth // width,), in_specs=[whol...  33.7 us
    all_to_all x7, starting transfers between devices, swap_all(): return lax.all_to_all(values, 'ep', split_axis=0, concat_axis=0, tiled=True)  33.6 us
  transfers between devices with their start and end apart: 77, of which 28 were waited for; matrix products, arithmetic and copies ran while one was open for 41% of the time, Pallas kernels for 9%

profile of v8, /device:TPU:0, one launch (start us, length us, event | category | flops | bytes accessed | tf_op | source)
XLA Modules:
  0.0 720.9 jit_solution(15646107001350678034)
XLA Ops:
  7.2 3.0 collective-permute-start
  14.5 6.2 all-to-all-start
  23.3 3.7 multiply_cosine_fusion
  27.0 2.9 collective-permute-done
  29.9 2.8 collective-permute-start.2
  32.7 4.5 collective-permute-start.3
  39.6 37.2 %collective-permute-done.2 = bf16[160,2048]{1,0:T(8,128)(2,1)} collective-permute-done((bf16[160,2048]{1,0:T(8,128)(2,1)S(1)}, bf16[160,2048]{1,0:T(8,128)(2,1)}, u32[]{:S(2)}, u32[]{:S(2)}) %collective-permute-start.2) | collective-permute-done | bytes 655392 | tf_op jit(solution)/shard_map/ppermute | solution.py:88
  76.8 6.5 collective-permute-start.5
  87.5 5.2 all-to-all-start.2
  94.8 8.0 %all-to-all-done.2 = bf16[8,52,128]{2,1,0:T(8,128)(2,1)S(1)} async-done(((bf16[8,52,128]{2,1,0:T(8,128)(2,1)}), bf16[8,52,128]{2,1,0:T(8,128)(2,1)S(1)}, u32[]{:S(2)}, u32[]{:S(2)}) %all-to-all-start.2) | async-done | bytes 106528 | tf_op jit(solution)/shard_map/all_to_all | solution.py:250
  123.3 3.0 fusion.71
  127.8 2.2 maximum_select_fusion
  133.7 3.6 fusion
  137.3 4.1 fusion.2
  141.4 10.1 %collective-permute-done.10 = bf16[2048,256]{1,0:T(8,128)(2,1)} collective-permute-done((bf16[2048,256]{1,0:T(8,128)(2,1)}, bf16[2048,256]{1,0:T(8,128)(2,1)}, u32[]{:S(2)}, u32[]{:S(2)}) %collective-permute-start.10) | collective-permute-done | bytes 1048608 | tf_op jit(solution)/shard_map/ppermute | solution.py:204
  151.6 4.3 fusion.77
  172.0 4.7 all-to-all-start.1
  179.5 22.4 %collective-permute-done.11 = bf16[2048,256]{1,0:T(8,128)(2,1)} collective-permute-done((bf16[2048,256]{1,0:T(8,128)(2,1)}, bf16[2048,256]{1,0:T(8,128)(2,1)}, u32[]{:S(2)}, u32[]{:S(2)}) %collective-permute-start.11) | collective-permute-done | bytes 1048608 | tf_op jit(solution)/shard_map/ppermute | solution.py:204
  202.4 10.2 %all-to-all-done.1 = bf16[8,160,256]{2,1,0:T(8,128)(2,1)} async-done(((bf16[8,160,256]{2,1,0:T(8,128)(2,1)}), bf16[8,160,256]{2,1,0:T(8,128)(2,1)}, u32[]{:S(2)}, u32[]{:S(2)}) %all-to-all-start.1) | async-done | bytes 655392 | tf_op jit(solution)/shard_map/all_to_all | solution.py:250
  228.5 5.6 all-gather.5.cloned.1.call-done
  238.9 9.5 %fusion.84.stream_ref = f32[640,2048]{1,0:T(8,128)} fusion(bf16[640,2048]{1,0:T(8,128)(2,1)S(1)} %bitcast.210, bf16[2048,2048]{1,0:T(8,128)(2,1)} %bitcast.300), kind=kOutput, calls=%fused_computation.349 | convolution fusion | flops 5368709120 | bytes 16252928 | tf_op jit(solution)/shard_map/dot_general | solution.py:60
  251.3 9.5 %fusion.85.stream_ref = f32[640,2048]{1,0:T(8,128)} fusion(bf16[640,2048]{1,0:T(8,128)(2,1)S(1)} %bitcast.211, bf16[2048,2048]{1,0:T(8,128)(2,1)} %bitcast.301), kind=kOutput, calls=%fused_computation.350 | convolution fusion | flops 5368709120 | bytes 16252928 | tf_op jit(solution)/shard_map/dot_general | solution.py:60
  262.6 2.5 collective-permute-done.17
  272.6 19.6 %shard_map.281 = (bf16[1280,2048]{1,0:T(8,128)(2,1)}, bf16[1280,2048]{1,0:T(8,128)(2,1)}, bf16[1280,2048]{1,0:T(8,128)(2,1)}, f32[2,640,128]{2,1,0:T(8,128)}) custom-call(bf16[640,2048]{1,0:T(8,128)(2,1)} %copy-done.31, bf16[2,2048,1024]{2,1,0:T(8,128)(2,1)} %gate_ref.7, bf16[2,2048,1024]{2,1,0:T(8,128)(2,1)} %up_ref.7, f32[640,2048]{1,0:T(8,128)} %fusion.84.stream_ref, ...), custom_call_target="tpu_custom_call" | custom-call | flops 10737418240 | bytes 42991616 | tf_op jit(solution)/shard_map/pallas_call | solution.py:294
  296.4 3.6 collective-permute-done.21
  305.7 19.4 %shard_map.282 = (bf16[1280,2048]{1,0:T(8,128)(2,1)}, bf16[1280,2048]{1,0:T(8,128)(2,1)}, bf16[1280,2048]{1,0:T(8,128)(2,1)}, f32[2,640,128]{2,1,0:T(8,128)}) custom-call(bf16[640,2048]{1,0:T(8,128)(2,1)} %copy-done.24, bf16[2,2048,1024]{2,1,0:T(8,128)(2,1)} %gate_ref.7, ...), custom_call_target="tpu_custom_call", output_to_operand_aliasing={{0}: (5, {}), {1}: (6, {}), {2}: (7, {})} | custom-call | flops 10737418240 | bytes 42991616 | tf_op jit(solution)/shard_map/pallas_call | solution.py:294
  325.1 16.8 %shard_map.283 = bf16[640,2048]{1,0:T(8,128)(2,1)} custom-call(bf16[1280,2048]{1,0:T(8,128)(2,1)} %get-tuple-element.205.gback_ref, bf16[1280,2048]{1,0:T(8,128)(2,1)} %get-tuple-element.215.uback_ref, bf16[2,2048,1024]{2,1,0:T(8,128)(2,1)} %gate_ref.7, bf16[2,2048,1024]{2,1,0:T(8,128)(2,1)} %up_ref.7), custom_call_target="tpu_custom_call" | custom-call | flops 10737418240 | bytes 24641536 | tf_op jit(solution)/shard_map/pallas_call | solution.py:334
  346.9 16.9 %shard_map.284 = bf16[640,2048]{1,0:T(8,128)(2,1)} custom-call(bf16[1280,2048]{1,0:T(8,128)(2,1)} %get-tuple-element.205.gback_ref, bf16[1280,2048]{1,0:T(8,128)(2,1)} %get-tuple-element.215.uback_ref, bf16[2,2048,1024]{2,1,0:T(8,128)(2,1)} %gate_ref.7, bf16[2,2048,1024]{2,1,0:T(8,128)(2,1)} %up_ref.7), custom_call_target="tpu_custom_call" | custom-call | flops 10737418240 | bytes 24641536 | tf_op jit(solution)/shard_map/pallas_call | solution.py:334
  369.5 4.1 all-to-all-start.3
  373.7 16.8 %convolution_convert_fusion.3 = bf16[1280,2048]{1,0:T(8,128)(2,1)} fusion(bf16[1280,2048]{1,0:T(8,128)(2,1)} %get-tuple-element.199, bf16[2048,2048]{1,0:T(8,128)(2,1)} %bitcast.302), kind=kOutput, calls=%fused_computation.15 | convolution fusion | flops 10740039680 | bytes 18874368 | tf_op jit(solution)/shard_map/dot_general | solution.py:60
  395.5 2.2 fusion.67
  399.9 16.8 %convolution_convert_fusion.2 = bf16[2048,2048]{1,0:T(8,128)(2,1)} fusion(bf16[1280,2048]{1,0:T(8,128)(2,1)} %get-tuple-element.199, bf16[1280,2048]{1,0:T(8,128)(2,1)} %bitcast.226), kind=kOutput, calls=%fused_computation.14 | convolution fusion | flops 10741612544 | bytes 18874368 | tf_op jit(solution)/shard_map/dot_general | solution.py:60
  423.6 2.8 add_convert_fusion.9
  428.4 18.5 %convolution_convert_fusion.1 = bf16[2048,2048]{1,0:T(8,128)(2,1)} fusion(bf16[1280,2048]{1,0:T(8,128)(2,1)} %get-tuple-element.465, bf16[1280,2048]{1,0:T(8,128)(2,1)} %get-tuple-element.205.gback_ref), kind=kOutput, calls=%fused_computation.13 | convolution fusion | flops 10741612544 | bytes 18874368 | tf_op jit(solution)/shard_map/dot_general | solution.py:60
  446.9 2.9 collective-permute-done.32
  459.7 2.4 fusion.34
  469.2 5.0 all-to-all-start.4
  474.2 3.4 add_convert_fusion.5
  479.7 16.8 %convolution_convert_fusion = bf16[2048,2048]{1,0:T(8,128)(2,1)} fusion(bf16[1280,2048]{1,0:T(8,128)(2,1)} %get-tuple-element.465, bf16[1280,2048]{1,0:T(8,128)(2,1)} %get-tuple-element.215.uback_ref), kind=kOutput, calls=%fused_computation.12 | convolution fusion | flops 10741612544 | bytes 18874368 | tf_op jit(solution)/shard_map/dot_general | solution.py:60
  510.3 22.7 %shard_map.285 = (bf16[1280,768]{1,0:T(8,128)(2,1)}, f32[2,128]{1,0:T(2,128)}) custom-call(bf16[1280,256]{1,0:T(8,128)(2,1)} %pad_maximum_fusion.11.query_ref, bf16[1280,256]{1,0:T(8,128)(2,1)} %pad_maximum_fusion.12.key_ref, bf16[1280,256]{1,0:T(8,128)(2,1)} %slice.439.value_ref, bf16[1280,256]{1,0:T(8,128)(2,1)} %bitcast.294, ...), custom_call_target="tpu_custom_call" | custom-call | flops 4194304000 | bytes 9830400 | tf_op jit(solution)/shard_map/pallas_call | solution.py:401
  535.3 7.5 %convolution_convert_fusion.4 = bf16[2048,768]{1,0:T(8,128)(2,1)S(1)} fusion(bf16[1280,2048]{1,0:T(8,128)(2,1)} %copy-done.19, bf16[1280,768]{1,0:T(8,128)(2,1)} %get-tuple-element.234), kind=kOutput, calls=%fused_computation.20 | convolution fusion | flops 4028104704 | bytes 10354688 | tf_op jit(solution)/shard_map/dot_general | solution.py:60
  549.4 8.5 %fusion.4 = (f32[2048]{0:T(1024)S(1)}, bf16[1280,2048]{1,0:T(8,128)(2,1)S(1)}) fusion(bf16[1280,2048]{1,0:T(8,128)(2,1)} %constant_dynamic-update-slice_fusion, f32[1280]{0:T(1024)S(1)} %copy-done.77, bf16[1280,768]{1,0:T(8,128)(2,1)} %get-tuple-element.234, bf16[2048,768]{1,0:T(8,128)(2,1)} %bitcast.205), kind=kOutput, calls=%fused_computation.7 | convolution fusion | flops 4039636992 | bytes 15610880 | tf_op jit(solution)/shard_map/dot_general | solution.py:60
  557.9 3.1 fusion.11
  561.0 3.8 collective-permute-done.43.refs_6_
  573.0 3.9 all-to-all-start.5
  581.0 4.4 all-to-all-done.5
  585.4 3.3 collective-permute-done.50
  588.6 2.4 add_convert_fusion
  591.1 4.2 collective-permute-done.49
  595.5 4.5 all-to-all-start.6
  606.7 6.4 shard_map.286
  613.1 13.2 %collective-permute-done.51 = bf16[160,2048]{1,0:T(8,128)(2,1)} collective-permute-done((bf16[160,2048]{1,0:T(8,128)(2,1)}, bf16[160,2048]{1,0:T(8,128)(2,1)}, u32[]{:S(2)}, u32[]{:S(2)}) %collective-permute-start.51) | collective-permute-done | bytes 655392 | tf_op jit(solution)/shard_map/ppermute | solution.py:88
  628.5 3.6 add_convert_fusion.3
  633.9 2.8 multiply_convert_fusion
  636.7 2.5 convert_element_type.506
  640.7 4.2 collective-permute-start.53
  644.9 2.5 reshape.573
  653.3 14.0 %collective-permute-done.55 = bf16[1,3,64,2048]{3,2,1,0:T(8,128)(2,1)S(1)} collective-permute-done((bf16[1,3,64,2048]{3,2,1,0:T(8,128)(2,1)S(1)}, bf16[1,3,64,2048]{3,2,1,0:T(8,128)(2,1)S(1)}, u32[]{:S(2)}, u32[]{:S(2)}) %collective-permute-start.55) | collective-permute-done | bytes 786464 | tf_op jit(solution)/shard_map/ppermute | solution.py:204
  667.6 3.3 add_convert_fusion.1
  672.7 2.3 maximum_convert_fusion
  678.5 2.3 maximum_convert_fusion.1
  685.0 2.4 maximum_select_fusion.1
  687.7 10.1 %collective-permute-done.60 = bf16[160,2048]{1,0:T(8,128)(2,1)S(1)} collective-permute-done((bf16[160,2048]{1,0:T(8,128)(2,1)}, bf16[160,2048]{1,0:T(8,128)(2,1)S(1)}, u32[]{:S(2)}, u32[]{:S(2)}) %collective-permute-start.60) | collective-permute-done | bytes 655392 | tf_op jit(solution)/shard_map/ppermute | solution.py:88
  704.8 2.7 fusion.21
  (638 shorter events, 223.9 us)
Async XLA Ops:
  7.2 113.8 %all-gather.3.cloned.1.call-start = ((), (), s32[]{:S(2)}) async-start(), calls=%async_computation.10 | async-start | bytes 2359296 | tf_op jit(solution)/shard_map/all_gather | solution.py:69
  7.2 22.6 %collective-permute-start = (bf16[160,2048]{1,0:T(8,128)(2,1)}, bf16[160,2048]{1,0:T(8,128)(2,1)S(1)}, u32[]{:S(2)}, u32[]{:S(2)}) collective-permute-start(bf16[160,2048]{1,0:T(8,128)(2,1)} %param.18), channel_id=1, source_target_pairs={{0,1},{2,0},{4,2},{6,4},{7,6},{5,7},{3,5},{1,3},{8,9},{10,8},{12,1... | collective-permute-start | bytes 1966088 | tf_op jit(solution)/shard_map/ppermute | solution.py:88
  10.2 22.5 %collective-permute-start.1 = (bf16[160,2048]{1,0:T(8,128)(2,1)}, bf16[160,2048]{1,0:T(8,128)(2,1)S(1)}, u32[]{:S(2)}, u32[]{:S(2)}) collective-permute-start(bf16[160,2048]{1,0:T(8,128)(2,1)} %param.18), channel_id=1, source_target_pairs={{0,2},{2,4},{4,6},{6,7},{7,5},{5,3},{3,1},{1,0},{8,10},{10,12},{12... | collective-permute-start | bytes 1966088 | tf_op jit(solution)/shard_map/ppermute | solution.py:88
  14.5 68.8 %all-to-all-start = ((bf16[8,64,768]{2,1,0:T(8,128)(2,1)}), bf16[8,64,768]{2,1,0:T(8,128)(2,1)S(1)}, u32[]{:S(2)}, u32[]{:S(2)}) async-start(bf16[8,64,768]{2,1,0:T(8,128)(2,1)} %copy.183), calls=%async_computation | async-start | bytes 1572864 | tf_op jit(solution)/shard_map/all_to_all | solution.py:250
  29.9 46.9 %collective-permute-start.2 = (bf16[160,2048]{1,0:T(8,128)(2,1)S(1)}, bf16[160,2048]{1,0:T(8,128)(2,1)}, u32[]{:S(2)}, u32[]{:S(2)}) collective-permute-start(bf16[160,2048]{1,0:T(8,128)(2,1)S(1)} %collective-permute-done), channel_id=1, source_target_pairs={{0,1},{2,0},{4,2},{6,4},{7,6},{5,7},{3,5},{1,3},{8,9},{10,8},{12,1... | collective-permute-start | bytes 1966088 | tf_op jit(solution)/shard_map/ppermute | solution.py:88
  32.7 44.1 %collective-permute-start.3 = (bf16[160,2048]{1,0:T(8,128)(2,1)S(1)}, bf16[160,2048]{1,0:T(8,128)(2,1)}, u32[]{:S(2)}, u32[]{:S(2)}) collective-permute-start(bf16[160,2048]{1,0:T(8,128)(2,1)S(1)} %collective-permute-done.1), channel_id=1, source_target_pairs={{0,2},{2,4},{4,6},{6,7},{7,5},{5,3},{3,1},{1,0},{8,10},{10,12},{12... | collective-permute-start | bytes 1966088 | tf_op jit(solution)/shard_map/ppermute | solution.py:88
  76.8 35.7 %collective-permute-start.4 = (bf16[160,2048]{1,0:T(8,128)(2,1)}, bf16[160,2048]{1,0:T(8,128)(2,1)}, u32[]{:S(2)}, u32[]{:S(2)}) collective-permute-start(bf16[160,2048]{1,0:T(8,128)(2,1)} %collective-permute-done.2), channel_id=1, source_target_pairs={{0,1},{2,0},{4,2},{6,4},{7,6},{5,7},{3,5},{1,3},{8,9},{10,8},{12,1... | collective-permute-start | bytes 1966088 | tf_op jit(solution)/shard_map/ppermute | solution.py:88
  76.8 40.5 %collective-permute-start.5 = (bf16[160,2048]{1,0:T(8,128)(2,1)}, bf16[160,2048]{1,0:T(8,128)(2,1)}, u32[]{:S(2)}, u32[]{:S(2)}) collective-permute-start(bf16[160,2048]{1,0:T(8,128)(2,1)} %collective-permute-done.3), channel_id=1, source_target_pairs={{0,2},{2,4},{4,6},{6,7},{7,5},{5,3},{3,1},{1,0},{8,10},{10,12},{12... | collective-permute-start | bytes 1966088 | tf_op jit(solution)/shard_map/ppermute | solution.py:88
  83.3 27.8 %collective-permute-start.8 = (bf16[1,8,64,768]{3,2,1,0:T(8,128)(2,1)S(1)}, bf16[1,8,64,768]{3,2,1,0:T(8,128)(2,1)S(1)}, u32[]{:S(2)}, u32[]{:S(2)}) collective-permute-start(bf16[1,8,64,768]{3,2,1,0:T(8,128)(2,1)S(1)} %bitcast.178), channel_id=1, source_target_pairs={{0,16},{8,24},{16,0},{24,8},{1,17},{9,25},{17,1},{25,9},{2,18},{10... | collective-permute-start | bytes 2359304 | tf_op jit(solution)/shard_map/ppermute | solution.py:204
  87.5 15.3 %all-to-all-start.2 = ((bf16[8,52,128]{2,1,0:T(8,128)(2,1)}), bf16[8,52,128]{2,1,0:T(8,128)(2,1)S(1)}, u32[]{:S(2)}, u32[]{:S(2)}) async-start(bf16[8,52,128]{2,1,0:T(8,128)(2,1)} %broadcast_in_dim.182), calls=%async_computation.2 | async-start | bytes 229376 | tf_op jit(solution)/shard_map/all_to_all | solution.py:250
  92.7 141.4 %all-gather.5.cloned.1.call-start = ((), (), s32[]{:S(2)}) async-start(), calls=%async_computation.11 | async-start | bytes 5898240 | tf_op jit(solution)/shard_map/all_gather | solution.py:69
  112.5 15.3 %collective-permute-start.9 = (bf16[2,8,64,768]{3,2,1,0:T(8,128)(2,1)}, bf16[2,8,64,768]{3,2,1,0:T(8,128)(2,1)}, u32[]{:S(2)}, u32[]{:S(2)}) collective-permute-start(bf16[2,8,64,768]{3,2,1,0:T(8,128)(2,1)} %maximum_select_fusion.3), channel_id=1, source_target_pairs={{0,8},{8,0},{16,24},{24,16},{1,9},{9,1},{17,25},{25,17},{2,10},{10... | collective-permute-start | bytes 4718600 | tf_op jit(solution)/shard_map/ppermute | solution.py:204
  114.3 18.6 %collective-permute-start.7 = (bf16[80,2048]{1,0:T(8,128)(2,1)}, bf16[80,2048]{1,0:T(8,128)(2,1)S(1)}, u32[]{:S(2)}, u32[]{:S(2)}) collective-permute-start(bf16[80,2048]{1,0:T(8,128)(2,1)} %slice.411), channel_id=1, source_target_pairs={{0,1},{2,0},{4,2},{6,4},{7,6},{5,7},{3,5},{1,3},{8,9},{10,8},{12,1... | collective-permute-start | bytes 983048 | tf_op jit(solution)/shard_map/ppermute | solution.py:88
  126.2 25.3 %collective-permute-start.10 = (bf16[2048,256]{1,0:T(8,128)(2,1)}, bf16[2048,256]{1,0:T(8,128)(2,1)}, u32[]{:S(2)}, u32[]{:S(2)}) collective-permute-start(bf16[2048,256]{1,0:T(8,128)(2,1)} %get-tuple-element.442), channel_id=1, source_target_pairs={{0,16},{8,24},{16,0},{24,8},{1,17},{9,25},{17,1},{25,9},{2,18},{10... | collective-permute-start | bytes 3145736 | tf_op jit(solution)/shard_map/ppermute | solution.py:204
  171.2 46.3 %collective-permute-start.12 = (bf16[2048,512]{1,0:T(8,128)(2,1)S(1)}, bf16[2048,512]{1,0:T(8,128)(2,1)}, u32[]{:S(2)}, u32[]{:S(2)}) collective-permute-start(bf16[2048,512]{1,0:T(8,128)(2,1)S(1)} %copy-done.4), channel_id=1, source_target_pairs={{0,8},{8,0},{16,24},{24,16},{1,9},{9,1},{17,25},{25,17},{2,10},{10... | collective-permute-start | bytes 6291464 | tf_op jit(solution)/shard_map/ppermute | solution.py:204
  172.0 40.5 %all-to-all-start.1 = ((bf16[8,160,256]{2,1,0:T(8,128)(2,1)}), bf16[8,160,256]{2,1,0:T(8,128)(2,1)}, u32[]{:S(2)}, u32[]{:S(2)}) async-start(bf16[8,160,256]{2,1,0:T(8,128)(2,1)} %copy-done.49), calls=%async_computation.1 | async-start | bytes 1310720 | tf_op jit(solution)/shard_map/all_to_all | solution.py:250
  176.7 25.1 %collective-permute-start.11 = (bf16[2048,256]{1,0:T(8,128)(2,1)}, bf16[2048,256]{1,0:T(8,128)(2,1)}, u32[]{:S(2)}, u32[]{:S(2)}) collective-permute-start(bf16[2048,256]{1,0:T(8,128)(2,1)} %get-tuple-element.441), channel_id=1, source_target_pairs={{0,16},{8,24},{16,0},{24,8},{1,17},{9,25},{17,1},{25,9},{2,18},{10... | collective-permute-start | bytes 3145736 | tf_op jit(solution)/shard_map/ppermute | solution.py:204
  201.9 17.8 %collective-permute-start.13 = (bf16[2048,256]{1,0:T(8,128)(2,1)}, bf16[2048,256]{1,0:T(8,128)(2,1)}, u32[]{:S(2)}, u32[]{:S(2)}) collective-permute-start(bf16[2048,256]{1,0:T(8,128)(2,1)} %collective-permute-done.10), channel_id=1, source_target_pairs={{0,8},{8,0},{16,24},{24,16},{1,9},{9,1},{17,25},{25,17},{2,10},{10... | collective-permute-start | bytes 3145736 | tf_op jit(solution)/shard_map/ppermute | solution.py:204
  201.9 19.4 %collective-permute-start.14 = (bf16[2048,256]{1,0:T(8,128)(2,1)}, bf16[2048,256]{1,0:T(8,128)(2,1)}, u32[]{:S(2)}, u32[]{:S(2)}) collective-permute-start(bf16[2048,256]{1,0:T(8,128)(2,1)} %collective-permute-done.11), channel_id=1, source_target_pairs={{0,8},{8,0},{16,24},{24,16},{1,9},{9,1},{17,25},{25,17},{2,10},{10... | collective-permute-start | bytes 3145736 | tf_op jit(solution)/shard_map/ppermute | solution.py:204
  225.4 23.5 %collective-permute-start.16 = (bf16[160,2048]{1,0:T(8,128)(2,1)S(1)}, bf16[160,2048]{1,0:T(8,128)(2,1)S(1)}, u32[]{:S(2)}, u32[]{:S(2)}) collective-permute-start(bf16[160,2048]{1,0:T(8,128)(2,1)S(1)} %get-tuple-element.373), channel_id=1, source_target_pairs={{0,1},{2,0},{4,2},{6,4},{7,6},{5,7},{3,5},{1,3},{8,9},{10,8},{12,1... | collective-permute-start | bytes 1966088 | tf_op jit(solution)/shard_map/ppermute | solution.py:88
  226.8 22.1 %collective-permute-start.15 = (bf16[160,2048]{1,0:T(8,128)(2,1)S(1)}, bf16[160,2048]{1,0:T(8,128)(2,1)S(1)}, u32[]{:S(2)}, u32[]{:S(2)}) collective-permute-start(bf16[160,2048]{1,0:T(8,128)(2,1)S(1)} %get-tuple-element.373), channel_id=1, source_target_pairs={{0,2},{2,4},{4,6},{6,7},{7,5},{5,3},{3,1},{1,0},{8,10},{10,12},{12... | collective-permute-start | bytes 1966088 | tf_op jit(solution)/shard_map/ppermute | solution.py:88
  248.9 16.2 %collective-permute-start.17 = (bf16[160,2048]{1,0:T(8,128)(2,1)S(1)}, bf16[160,2048]{1,0:T(8,128)(2,1)}, u32[]{:S(2)}, u32[]{:S(2)}) collective-permute-start(bf16[160,2048]{1,0:T(8,128)(2,1)S(1)} %collective-permute-done.15), channel_id=1, source_target_pairs={{0,2},{2,4},{4,6},{6,7},{7,5},{5,3},{3,1},{1,0},{8,10},{10,12},{12... | collective-permute-start | bytes 1966088 | tf_op jit(solution)/shard_map/ppermute | solution.py:88
  248.9 16.1 %collective-permute-start.18 = (bf16[160,2048]{1,0:T(8,128)(2,1)S(1)}, bf16[160,2048]{1,0:T(8,128)(2,1)S(1)}, u32[]{:S(2)}, u32[]{:S(2)}) collective-permute-start(bf16[160,2048]{1,0:T(8,128)(2,1)S(1)} %collective-permute-done.16), channel_id=1, source_target_pairs={{0,1},{2,0},{4,2},{6,4},{7,6},{5,7},{3,5},{1,3},{8,9},{10,8},{12,1... | collective-permute-start | bytes 1966088 | tf_op jit(solution)/shard_map/ppermute | solution.py:88
  265.1 27.2 %collective-permute-start.20 = (bf16[160,2048]{1,0:T(8,128)(2,1)S(1)}, bf16[160,2048]{1,0:T(8,128)(2,1)S(1)}, u32[]{:S(2)}, u32[]{:S(2)}) collective-permute-start(bf16[160,2048]{1,0:T(8,128)(2,1)S(1)} %collective-permute-done.18), channel_id=1, source_target_pairs={{0,1},{2,0},{4,2},{6,4},{7,6},{5,7},{3,5},{1,3},{8,9},{10,8},{12,1... | collective-permute-start | bytes 1966088 | tf_op jit(solution)/shard_map/ppermute | solution.py:88
  267.9 24.4 %collective-permute-start.19 = (bf16[160,2048]{1,0:T(8,128)(2,1)}, bf16[160,2048]{1,0:T(8,128)(2,1)S(1)}, u32[]{:S(2)}, u32[]{:S(2)}) collective-permute-start(bf16[160,2048]{1,0:T(8,128)(2,1)} %collective-permute-done.17), channel_id=1, source_target_pairs={{0,2},{2,4},{4,6},{6,7},{7,5},{5,3},{3,1},{1,0},{8,10},{10,12},{12... | collective-permute-start | bytes 1966088 | tf_op jit(solution)/shard_map/ppermute | solution.py:88
  344.1 19.9 %collective-permute-start.24 = (bf16[80,2048]{1,0:T(8,128)(2,1)}, bf16[80,2048]{1,0:T(8,128)(2,1)}, u32[]{:S(2)}, u32[]{:S(2)}) collective-permute-start(bf16[80,2048]{1,0:T(8,128)(2,1)} %get-tuple-element.433), channel_id=1, source_target_pairs={{0,1},{2,0},{4,2},{6,4},{7,6},{5,7},{3,5},{1,3},{8,9},{10,8},{12,1... | collective-permute-start | bytes 983048 | tf_op jit(solution)/shard_map/ppermute | solution.py:88
  344.5 19.5 %collective-permute-start.23 = (bf16[80,2048]{1,0:T(8,128)(2,1)S(1)}, bf16[80,2048]{1,0:T(8,128)(2,1)}, u32[]{:S(2)}, u32[]{:S(2)}) collective-permute-start(bf16[80,2048]{1,0:T(8,128)(2,1)S(1)} %get-tuple-element.434), channel_id=1, source_target_pairs={{0,2},{2,4},{4,6},{6,7},{7,5},{5,3},{3,1},{1,0},{8,10},{10,12},{12... | collective-permute-start | bytes 983048 | tf_op jit(solution)/shard_map/ppermute | solution.py:88
  366.4 24.1 %collective-permute-start.25 = (bf16[160,2048]{1,0:T(8,128)(2,1)}, bf16[160,2048]{1,0:T(8,128)(2,1)}, u32[]{:S(2)}, u32[]{:S(2)}) collective-permute-start(bf16[160,2048]{1,0:T(8,128)(2,1)} %pad_maximum_fusion.7), channel_id=1, source_target_pairs={{0,2},{2,4},{4,6},{6,7},{7,5},{5,3},{3,1},{1,0},{8,10},{10,12},{12... | collective-permute-start | bytes 1966088 | tf_op jit(solution)/shard_map/ppermute | solution.py:88
  368.2 22.3 %collective-permute-start.26 = (bf16[160,2048]{1,0:T(8,128)(2,1)S(1)}, bf16[160,2048]{1,0:T(8,128)(2,1)}, u32[]{:S(2)}, u32[]{:S(2)}) collective-permute-start(bf16[160,2048]{1,0:T(8,128)(2,1)S(1)} %pad_maximum_fusion.8), channel_id=1, source_target_pairs={{0,1},{2,0},{4,2},{6,4},{7,6},{5,7},{3,5},{1,3},{8,9},{10,8},{12,1... | collective-permute-start | bytes 1966088 | tf_op jit(solution)/shard_map/ppermute | solution.py:88
  369.5 20.9 %all-to-all-start.3 = ((f32[8,160,2]{1,2,0:T(2,128)}), f32[8,160,2]{1,2,0:T(2,128)S(1)}, u32[]{:S(2)}, u32[]{:S(2)}) async-start(f32[8,160,2]{1,2,0:T(2,128)} %copy.224), calls=%async_computation.3 | async-start | bytes 32768 | tf_op jit(solution)/shard_map/all_to_all | solution.py:250
  373.6 161.6 %reduce-scatter.4.cloned.1.call-start = ((), (), s32[]{:S(2)}) async-start(), calls=%async_computation.12 | async-start | bytes 10485760 | tf_op jit(solution)/shard_map/reduce_scatter | solution.py:773
  393.4 25.0 %collective-permute-start.27 = (bf16[160,2048]{1,0:T(8,128)(2,1)S(1)}, bf16[160,2048]{1,0:T(8,128)(2,1)}, u32[]{:S(2)}, u32[]{:S(2)}) collective-permute-start(bf16[160,2048]{1,0:T(8,128)(2,1)S(1)} %add_convert_fusion.12), channel_id=1, source_target_pairs={{0,2},{2,4},{4,6},{6,7},{7,5},{5,3},{3,1},{1,0},{8,10},{10,12},{12... | collective-permute-start | bytes 1966088 | tf_op jit(solution)/shard_map/ppermute | solution.py:88
  395.4 23.0 %collective-permute-start.28 = (bf16[160,2048]{1,0:T(8,128)(2,1)S(1)}, bf16[160,2048]{1,0:T(8,128)(2,1)}, u32[]{:S(2)}, u32[]{:S(2)}) collective-permute-start(bf16[160,2048]{1,0:T(8,128)(2,1)S(1)} %add_convert_fusion.11), channel_id=1, source_target_pairs={{0,1},{2,0},{4,2},{6,4},{7,6},{5,7},{3,5},{1,3},{8,9},{10,8},{12,1... | collective-permute-start | bytes 1966088 | tf_op jit(solution)/shard_map/ppermute | solution.py:88
  397.8 20.7 %collective-permute-start.30 = (bf16[80,2048]{1,0:T(8,128)(2,1)}, bf16[80,2048]{1,0:T(8,128)(2,1)}, u32[]{:S(2)}, u32[]{:S(2)}) collective-permute-start(bf16[80,2048]{1,0:T(8,128)(2,1)} %get-tuple-element.414), channel_id=1, source_target_pairs={{0,1},{2,0},{4,2},{6,4},{7,6},{5,7},{3,5},{1,3},{8,9},{10,8},{12,1... | collective-permute-start | bytes 983048 | tf_op jit(solution)/shard_map/ppermute | solution.py:88
  399.7 18.7 %collective-permute-start.29 = (bf16[80,2048]{1,0:T(8,128)(2,1)}, bf16[80,2048]{1,0:T(8,128)(2,1)}, u32[]{:S(2)}, u32[]{:S(2)}) collective-permute-start(bf16[80,2048]{1,0:T(8,128)(2,1)} %get-tuple-element.415), channel_id=1, source_target_pairs={{0,2},{2,4},{4,6},{6,7},{7,5},{5,3},{3,1},{1,0},{8,10},{10,12},{12... | collective-permute-start | bytes 983048 | tf_op jit(solution)/shard_map/ppermute | solution.py:88
  418.5 252.5 %reduce-scatter.6.cloned.1.call-start = ((), (), s32[]{:S(2)}) async-start(), calls=%async_computation.13 | async-start | bytes 10485760 | tf_op jit(solution)/shard_map/reduce_scatter | solution.py:816
  421.0 25.8 %collective-permute-start.33 = (bf16[160,2048]{1,0:T(8,128)(2,1)}, bf16[160,2048]{1,0:T(8,128)(2,1)S(1)}, u32[]{:S(2)}, u32[]{:S(2)}) collective-permute-start(bf16[160,2048]{1,0:T(8,128)(2,1)} %pad_maximum_fusion.9), channel_id=1, source_target_pairs={{0,2},{2,4},{4,6},{6,7},{7,5},{5,3},{3,1},{1,0},{8,10},{10,12},{12... | collective-permute-start | bytes 1966088 | tf_op jit(solution)/shard_map/ppermute | solution.py:88
  423.0 23.9 %collective-permute-start.34 = (bf16[160,2048]{1,0:T(8,128)(2,1)S(1)}, bf16[160,2048]{1,0:T(8,128)(2,1)}, u32[]{:S(2)}, u32[]{:S(2)}) collective-permute-start(bf16[160,2048]{1,0:T(8,128)(2,1)S(1)} %pad_maximum_fusion.10), channel_id=1, source_target_pairs={{0,1},{2,0},{4,2},{6,4},{7,6},{5,7},{3,5},{1,3},{8,9},{10,8},{12,1... | collective-permute-start | bytes 1966088 | tf_op jit(solution)/shard_map/ppermute | solution.py:88
  426.4 23.4 %collective-permute-start.32 = (bf16[160,2048]{1,0:T(8,128)(2,1)}, bf16[160,2048]{1,0:T(8,128)(2,1)S(1)}, u32[]{:S(2)}, u32[]{:S(2)}) collective-permute-start(bf16[160,2048]{1,0:T(8,128)(2,1)} %get-tuple-element.429), channel_id=1, source_target_pairs={{0,1},{2,0},{4,2},{6,4},{7,6},{5,7},{3,5},{1,3},{8,9},{10,8},{12,1... | collective-permute-start | bytes 1966088 | tf_op jit(solution)/shard_map/ppermute | solution.py:88
  428.4 21.4 %collective-permute-start.31 = (bf16[160,2048]{1,0:T(8,128)(2,1)}, bf16[160,2048]{1,0:T(8,128)(2,1)S(1)}, u32[]{:S(2)}, u32[]{:S(2)}) collective-permute-start(bf16[160,2048]{1,0:T(8,128)(2,1)} %get-tuple-element.430), channel_id=1, source_target_pairs={{0,2},{2,4},{4,6},{6,7},{7,5},{5,3},{3,1},{1,0},{8,10},{10,12},{12... | collective-permute-start | bytes 1966088 | tf_op jit(solution)/shard_map/ppermute | solution.py:88
  451.9 17.3 %collective-permute-start.36 = (bf16[160,2048]{1,0:T(8,128)(2,1)S(1)}, bf16[160,2048]{1,0:T(8,128)(2,1)}, u32[]{:S(2)}, u32[]{:S(2)}) collective-permute-start(bf16[160,2048]{1,0:T(8,128)(2,1)S(1)} %get-tuple-element.410), channel_id=1, source_target_pairs={{0,1},{2,0},{4,2},{6,4},{7,6},{5,7},{3,5},{1,3},{8,9},{10,8},{12,1... | collective-permute-start | bytes 1966088 | tf_op jit(solution)/shard_map/ppermute | solution.py:88
  452.4 16.8 %collective-permute-start.35 = (bf16[160,2048]{1,0:T(8,128)(2,1)S(1)}, bf16[160,2048]{1,0:T(8,128)(2,1)}, u32[]{:S(2)}, u32[]{:S(2)}) collective-permute-start(bf16[160,2048]{1,0:T(8,128)(2,1)S(1)} %get-tuple-element.411), channel_id=1, source_target_pairs={{0,2},{2,4},{4,6},{6,7},{7,5},{5,3},{3,1},{1,0},{8,10},{10,12},{12... | collective-permute-start | bytes 1966088 | tf_op jit(solution)/shard_map/ppermute | solution.py:88
  469.2 27.4 %all-to-all-start.4 = ((bf16[8,160,256]{2,1,0:T(8,128)(2,1)}), bf16[8,160,256]{2,1,0:T(8,128)(2,1)S(1)}, u32[]{:S(2)}, u32[]{:S(2)}) async-start(bf16[8,160,256]{2,1,0:T(8,128)(2,1)} %bitcast.212), calls=%async_computation.4 | async-start | bytes 1310720 | tf_op jit(solution)/shard_map/all_to_all | solution.py:250
  474.1 202.6 %reduce-scatter.8.cloned.1.call-start = ((), (), s32[]{:S(2)}) async-start(), calls=%async_computation.14 | async-start | bytes 10485760 | tf_op jit(solution)/shard_map/reduce_scatter | solution.py:817
  477.6 19.0 %collective-permute-start.38 = (bf16[160,2048]{1,0:T(8,128)(2,1)}, bf16[160,2048]{1,0:T(8,128)(2,1)}, u32[]{:S(2)}, u32[]{:S(2)}) collective-permute-start(bf16[160,2048]{1,0:T(8,128)(2,1)} %get-tuple-element.408), channel_id=1, source_target_pairs={{0,1},{2,0},{4,2},{6,4},{7,6},{5,7},{3,5},{1,3},{8,9},{10,8},{12,1... | collective-permute-start | bytes 1966088 | tf_op jit(solution)/shard_map/ppermute | solution.py:88
  479.5 17.1 %collective-permute-start.37 = (bf16[160,2048]{1,0:T(8,128)(2,1)}, bf16[160,2048]{1,0:T(8,128)(2,1)}, u32[]{:S(2)}, u32[]{:S(2)}) collective-permute-start(bf16[160,2048]{1,0:T(8,128)(2,1)} %get-tuple-element.409), channel_id=1, source_target_pairs={{0,2},{2,4},{4,6},{6,7},{7,5},{5,3},{3,1},{1,0},{8,10},{10,12},{12... | collective-permute-start | bytes 1966088 | tf_op jit(solution)/shard_map/ppermute | solution.py:88
  507.3 25.7 %collective-permute-start.40 = (bf16[160,2048]{1,0:T(8,128)(2,1)S(1)}, bf16[160,2048]{1,0:T(8,128)(2,1)}, u32[]{:S(2)}, u32[]{:S(2)}) collective-permute-start(bf16[160,2048]{1,0:T(8,128)(2,1)S(1)} %get-tuple-element.256.refs_0_), channel_id=1, source_target_pairs={{0,1},{2,0},{4,2},{6,4},{7,6},{5,7},{3,5},{1,3},{8,9},{10,8},{12,1... | collective-permute-start | bytes 1966088 | tf_op jit(solution)/shard_map/ppermute | solution.py:88
  509.2 23.8 %collective-permute-start.39 = (bf16[160,2048]{1,0:T(8,128)(2,1)S(1)}, bf16[160,2048]{1,0:T(8,128)(2,1)}, u32[]{:S(2)}, u32[]{:S(2)}) collective-permute-start(bf16[160,2048]{1,0:T(8,128)(2,1)S(1)} %get-tuple-element.256.refs_0_), channel_id=1, source_target_pairs={{0,2},{2,4},{4,6},{6,7},{7,5},{5,3},{3,1},{1,0},{8,10},{10,12},{12... | collective-permute-start | bytes 1966088 | tf_op jit(solution)/shard_map/ppermute | solution.py:88
  547.3 17.4 %collective-permute-start.43 = (bf16[160,2048]{1,0:T(8,128)(2,1)}, bf16[160,2048]{1,0:T(8,128)(2,1)S(1)}, u32[]{:S(2)}, u32[]{:S(2)}) collective-permute-start(bf16[160,2048]{1,0:T(8,128)(2,1)} %collective-permute-done.41.refs_4_), channel_id=1, source_target_pairs={{0,2},{2,4},{4,6},{6,7},{7,5},{5,3},{3,1},{1,0},{8,10},{10,12},{12... | collective-permute-start | bytes 1966088 | tf_op jit(solution)/shard_map/ppermute | solution.py:88
  548.9 17.1 %collective-permute-start.44 = (bf16[160,2048]{1,0:T(8,128)(2,1)}, bf16[160,2048]{1,0:T(8,128)(2,1)S(1)}, u32[]{:S(2)}, u32[]{:S(2)}) collective-permute-start(bf16[160,2048]{1,0:T(8,128)(2,1)} %copy-done.52), channel_id=1, source_target_pairs={{0,1},{2,0},{4,2},{6,4},{7,6},{5,7},{3,5},{1,3},{8,9},{10,8},{12,1... | collective-permute-start | bytes 1966088 | tf_op jit(solution)/shard_map/ppermute | solution.py:88
  569.4 19.2 %collective-permute-start.50 = (bf16[8,1,64,768]{3,2,1,0:T(8,128)(2,1)}, bf16[8,1,64,768]{3,2,1,0:T(8,128)(2,1)}, u32[]{:S(2)}, u32[]{:S(2)}) collective-permute-start(bf16[8,1,64,768]{3,2,1,0:T(8,128)(2,1)} %constant_dynamic-slice_fusion.1), channel_id=1, source_target_pairs={{0,16},{8,24},{16,0},{24,8},{1,17},{9,25},{17,1},{25,9},{2,18},{10... | collective-permute-start | bytes 2359304 | tf_op jit(solution)/shard_map/ppermute | solution.py:204
  576.9 14.2 %collective-permute-start.47 = (bf16[80,2048]{1,0:T(8,128)(2,1)}, bf16[80,2048]{1,0:T(8,128)(2,1)S(1)}, u32[]{:S(2)}, u32[]{:S(2)}) collective-permute-start(bf16[80,2048]{1,0:T(8,128)(2,1)} %slice.384), channel_id=1, source_target_pairs={{0,1},{2,0},{4,2},{6,4},{7,6},{5,7},{3,5},{1,3},{8,9},{10,8},{12,1... | collective-permute-start | bytes 983048 | tf_op jit(solution)/shard_map/ppermute | solution.py:88
  578.9 16.3 %collective-permute-start.49 = (bf16[80,2048]{1,0:T(8,128)(2,1)}, bf16[80,2048]{1,0:T(8,128)(2,1)}, u32[]{:S(2)}, u32[]{:S(2)}) collective-permute-start(bf16[80,2048]{1,0:T(8,128)(2,1)} %get-tuple-element.404), channel_id=1, source_target_pairs={{0,1},{2,0},{4,2},{6,4},{7,6},{5,7},{3,5},{1,3},{8,9},{10,8},{12,1... | collective-permute-start | bytes 983048 | tf_op jit(solution)/shard_map/ppermute | solution.py:88
  580.9 14.6 %collective-permute-start.48 = (bf16[80,2048]{1,0:T(8,128)(2,1)S(1)}, bf16[80,2048]{1,0:T(8,128)(2,1)}, u32[]{:S(2)}, u32[]{:S(2)}) collective-permute-start(bf16[80,2048]{1,0:T(8,128)(2,1)S(1)} %copy-done.53), channel_id=1, source_target_pairs={{0,2},{2,4},{4,6},{6,7},{7,5},{5,3},{3,1},{1,0},{8,10},{10,12},{12... | collective-permute-start | bytes 983048 | tf_op jit(solution)/shard_map/ppermute | solution.py:88
  595.5 33.0 %all-to-all-start.6 = ((bf16[8,64,768]{2,1,0:T(8,128)(2,1)}), bf16[8,64,768]{2,1,0:T(8,128)(2,1)S(1)}, u32[]{:S(2)}, u32[]{:S(2)}) async-start(bf16[8,64,768]{2,1,0:T(8,128)(2,1)} %bitcast.54), calls=%async_computation.7 | async-start | bytes 1572864 | tf_op jit(solution)/shard_map/all_to_all | solution.py:250
  602.6 23.8 %collective-permute-start.51 = (bf16[160,2048]{1,0:T(8,128)(2,1)}, bf16[160,2048]{1,0:T(8,128)(2,1)}, u32[]{:S(2)}, u32[]{:S(2)}) collective-permute-start(bf16[160,2048]{1,0:T(8,128)(2,1)} %pad_maximum_fusion.13), channel_id=1, source_target_pairs={{0,2},{2,4},{4,6},{6,7},{7,5},{5,3},{3,1},{1,0},{8,10},{10,12},{12... | collective-permute-start | bytes 1966088 | tf_op jit(solution)/shard_map/ppermute | solution.py:88
  605.5 23.0 %collective-permute-start.52 = (bf16[160,2048]{1,0:T(8,128)(2,1)}, bf16[160,2048]{1,0:T(8,128)(2,1)}, u32[]{:S(2)}, u32[]{:S(2)}) collective-permute-start(bf16[160,2048]{1,0:T(8,128)(2,1)} %pad_maximum_fusion.14), channel_id=1, source_target_pairs={{0,1},{2,0},{4,2},{6,4},{7,6},{5,7},{3,5},{1,3},{8,9},{10,8},{12,1... | collective-permute-start | bytes 1966088 | tf_op jit(solution)/shard_map/ppermute | solution.py:88
  633.1 18.3 %collective-permute-start.56 = (bf16[2,64,2048]{2,1,0:T(8,128)(2,1)}, bf16[2,64,2048]{2,1,0:T(8,128)(2,1)}, u32[]{:S(2)}, u32[]{:S(2)}) collective-permute-start(bf16[2,64,2048]{2,1,0:T(8,128)(2,1)} %dynamic-slice_bitcast_fusion.1), channel_id=1, source_target_pairs={{0,8},{8,0},{16,24},{24,16},{1,9},{9,1},{17,25},{25,17},{2,10},{10... | collective-permute-start | bytes 1572872 | tf_op jit(solution)/shard_map/ppermute | solution.py:204
  633.6 16.6 %collective-permute-start.58 = (f32[4640]{0:T(1024)S(1)}, f32[4640]{0:T(1024)S(1)}, u32[]{:S(2)}, u32[]{:S(2)}) collective-permute-start(f32[4640]{0:T(1024)S(1)} %add.694), channel_id=1, source_target_pairs={{0,16},{8,24},{16,0},{24,8},{1,17},{9,25},{17,1},{25,9},{2,18},{10... | collective-permute-start | bytes 55688 | tf_op jit(solution)/shard_map/ppermute | solution.py:204
  639.3 28.3 %collective-permute-start.54 = (bf16[160,2048]{1,0:T(8,128)(2,1)}, bf16[160,2048]{1,0:T(8,128)(2,1)}, u32[]{:S(2)}, u32[]{:S(2)}) collective-permute-start(bf16[160,2048]{1,0:T(8,128)(2,1)} %get-tuple-element.400), channel_id=1, source_target_pairs={{0,1},{2,0},{4,2},{6,4},{7,6},{5,7},{3,5},{1,3},{8,9},{10,8},{12,1... | collective-permute-start | bytes 1966088 | tf_op jit(solution)/shard_map/ppermute | solution.py:88
  640.7 26.9 %collective-permute-start.53 = (bf16[160,2048]{1,0:T(8,128)(2,1)}, bf16[160,2048]{1,0:T(8,128)(2,1)}, u32[]{:S(2)}, u32[]{:S(2)}) collective-permute-start(bf16[160,2048]{1,0:T(8,128)(2,1)} %get-tuple-element.401), channel_id=1, source_target_pairs={{0,2},{2,4},{4,6},{6,7},{7,5},{5,3},{3,1},{1,0},{8,10},{10,12},{12... | collective-permute-start | bytes 1966088 | tf_op jit(solution)/shard_map/ppermute | solution.py:88
  648.4 19.0 %collective-permute-start.55 = (bf16[1,3,64,2048]{3,2,1,0:T(8,128)(2,1)S(1)}, bf16[1,3,64,2048]{3,2,1,0:T(8,128)(2,1)S(1)}, u32[]{:S(2)}, u32[]{:S(2)}) collective-permute-start(bf16[1,3,64,2048]{3,2,1,0:T(8,128)(2,1)S(1)} %stack.127), channel_id=1, source_target_pairs={{0,16},{8,24},{16,0},{24,8},{1,17},{9,25},{17,1},{25,9},{2,18},{10... | collective-permute-start | bytes 2359304 | tf_op jit(solution)/shard_map/ppermute | solution.py:204
  680.8 17.1 %collective-permute-start.60 = (bf16[160,2048]{1,0:T(8,128)(2,1)}, bf16[160,2048]{1,0:T(8,128)(2,1)S(1)}, u32[]{:S(2)}, u32[]{:S(2)}) collective-permute-start(bf16[160,2048]{1,0:T(8,128)(2,1)} %get-tuple-element.398), channel_id=1, source_target_pairs={{0,1},{2,0},{4,2},{6,4},{7,6},{5,7},{3,5},{1,3},{8,9},{10,8},{12,1... | collective-permute-start | bytes 1966088 | tf_op jit(solution)/shard_map/ppermute | solution.py:88
  682.1 16.8 %collective-permute-start.59 = (bf16[160,2048]{1,0:T(8,128)(2,1)}, bf16[160,2048]{1,0:T(8,128)(2,1)S(1)}, u32[]{:S(2)}, u32[]{:S(2)}) collective-permute-start(bf16[160,2048]{1,0:T(8,128)(2,1)} %get-tuple-element.399), channel_id=1, source_target_pairs={{0,2},{2,4},{4,6},{6,7},{7,5},{5,3},{3,1},{1,0},{8,10},{10,12},{12... | collective-permute-start | bytes 1966088 | tf_op jit(solution)/shard_map/ppermute | solution.py:88
  (150 other events, 1039.4 us)
Sparse Core Ops, SparseCore 0:
  11.3 68.3 all-gather.2
  133.8 100.2 all-gather.4
  418.6 73.1 reduce-scatter.3
  494.5 71.6 reduce-scatter.5
  568.6 72.1 reduce-scatter.7

commit v9 on v8

--- a/solution.py
+++ b/solution.py
@@ -164,15 +164,15 @@
         )
 
 
-def window(rings, work, *inputs):
+def window(rings, work, *inputs, waits=()):
     for ring in rings:
         ring.start()
     inputs, _ = tie(inputs, [ring.sent for ring in rings])
-    received, results = tie([ring.received for ring in rings], work(*inputs))
+    received, waits, results = tie([ring.received for ring in rings], waits, work(*inputs))
     for ring, pair in zip(rings, received):
         ring.received = pair
         ring.finish()
-    return results
+    return (results, *waits) if waits else results
 
 
 def add_low(left, right):
@@ -347,13 +347,16 @@
 
 
 def attention_back_kernel(
-    block, scale, query_ref, key_ref, value_ref, grad_ref, total_ref, column_ref, line_ref,
-    query_raw_ref, key_raw_ref, gains_ref, cosine_ref, sine_ref, sent_ref, part_ref, key_sum, value_sum
+    block, scale, order_ref, query_ref, key_ref, value_ref, swapped_ref, total_ref, column_ref, line_ref,
+    query_raw_ref, key_raw_ref, gains_ref, cosine_ref, sine_ref, sent_ref, part_ref, key_sum, value_sum, grad_ref
 ):
     head, heads = pl.program_id(0), pl.num_programs(0)
     rows, depth = query_ref.shape
     lane = lax.broadcasted_iota(jnp.int32, (1, depth), 1)
     sign = jnp.where(lane < depth // 2, 1.0, -1.0)
+    share = swapped_ref.shape[1]
+    for slot in range(swapped_ref.shape[0]):
+        grad_ref[slot * share : (slot + 1) * share, :] = swapped_ref[order_ref[slot]]
     key_sum[...] = jnp.zeros_like(key_sum)
     value_sum[...] = jnp.zeros_like(value_sum)
 
@@ -390,24 +393,55 @@
         sent_ref[row, pl.ds(pl.multiple_of((2 * heads + head) * depth, depth), depth)] = value_sum[row, :].astype(low_type)
 
 
-def attention_back(query, key, value, grad, totals, segment, query_raw, key_raw, gains, cosine, sine, block=256):
-    rows, width = query.shape
-    depth = cosine.shape[1]
-    heads = width // depth
-    by_head = pl.BlockSpec((rows, depth), lambda h: (0, h))
+def attention_back(lows, swapped, order, totals, segment, raw, gains, cosine, sine, block=256):
+    rows, depth = cosine.shape
+    heads = lows.shape[1] // (3 * depth)
+    block = block if rows % block == 0 else rows
+
+    def by_head(start):
+        return pl.BlockSpec((rows, depth), lambda h, order: (0, start * heads + h))
+
     def whole(array):
-        return pl.BlockSpec(array.shape, lambda h: (0, 0))
+        return pl.BlockSpec(array.shape, lambda h, order: (0, 0))
+
     column, line = segment[:, None], segment[None, :]
     return pl.pallas_call(
-        functools.partial(attention_back_kernel, block, depth ** -0.5),
-        grid=(heads,),
-        in_specs=[by_head] * 4 + [pl.BlockSpec((None, rows, 1), lambda h: (h, 0, 0)), whole(column), whole(line), by_head, by_head, whole(gains), whole(cosine), whole(sine)],
-        out_specs=[pl.BlockSpec((rows, 3 * width), lambda h: (0, 0)), pl.BlockSpec((2, depth), lambda h: (0, 0))],
-        out_shape=[jax.ShapeDtypeStruct((rows, 3 * width), low_type), jax.ShapeDtypeStruct((2, depth), wide_type)],
-        scratch_shapes=[pltpu.VMEM((rows, depth), wide_type)] * 2,
+        functools.partial(attention_back_kernel, block, depth**-0.5),
+        grid_spec=pltpu.PrefetchScalarGridSpec(
+            num_scalar_prefetch=1,
+            grid=(heads,),
+            in_specs=[
+                by_head(0),
+                by_head(1),
+                by_head(2),
+                pl.BlockSpec(swapped.shape[:2] + (depth,), lambda h, order: (0, 0, h)),
+                pl.BlockSpec((None, rows, 1), lambda h, order: (h, 0, 0)),
+                whole(column),
+                whole(line),
+                by_head(0),
+                by_head(1),
+                whole(gains),
+                whole(cosine),
+                whole(sine),
+            ],
+            out_specs=[
+                pl.BlockSpec((rows, lows.shape[1]), lambda h, order: (0, 0)),
+                pl.BlockSpec((2, depth), lambda h, order: (0, 0)),
+            ],
+            scratch_shapes=[pltpu.VMEM((rows, depth), wide_type)] * 2
+            + [pltpu.VMEM((rows, depth), low_type)],
+        ),
+        out_shape=[
+            jax.ShapeDtypeStruct(lows.shape, low_type),
+            jax.ShapeDtypeStruct((2, depth), wide_type),
+        ],
         compiler_params=pltpu.CompilerParams(vmem_limit_bytes=56 << 20),
-        cost_estimate=pl.CostEstimate(flops=10 * rows * rows * width, bytes_accessed=30 * rows * width, transcendentals=heads * rows * rows),
-    )(query, key, value, grad, totals, column, line, query_raw, key_raw, gains, cosine, sine)
+        cost_estimate=pl.CostEstimate(
+            flops=10 * rows * rows * heads * depth,
+            bytes_accessed=30 * rows * heads * depth,
+            transcendentals=heads * rows * rows,
+        ),
+    )(order, lows, lows, lows, swapped, totals, column, line, raw, raw, gains, cosine, sine)
 
 
 def block_product_kernel(left_ref, *refs):
@@ -517,10 +551,6 @@
         group_rows, expert_total
     )
     full_router = small_all[:, row_count:].reshape(model_width, expert_total)
-    column_share = model_width // replica_count
-    output_share = gather_rows(
-        lax.dynamic_slice_in_dim(output_weight, replica * column_share, column_share, 1)
-    )
     chunks = 2
     chunk_rows = group_rows // chunks
     blocks_here = group_count // chunks
@@ -536,84 +566,94 @@
             rows.reshape(group_count, row_count, rows.shape[1]), index
         ).reshape(rows.shape)
 
-    token_ring = RingGather(tokens)
+    tokens_late, output_late, _ = tie(tokens, output_weight, swapped)
+    column_share = model_width // replica_count
+    output_share = gather_rows(
+        lax.dynamic_slice_in_dim(output_late, replica * column_share, column_share, 1)
+    )
+    token_ring = RingGather(tokens_late)
     for step in range(group_count // 2):
         if step == group_count // 2 - 1:
             token_ring.sent = (after(token_ring.sent[0], output_share), token_ring.sent[1])
         token_ring.start()
         token_ring.finish()
-    token_all = jnp.concatenate(token_ring.blocks, axis=0)
-    token_late, cot_own = lax.optimization_barrier((token_all, cotangent))
-    token_all = token_late
-    cot_ordered = gather_rows(cot_own)
-    cot_all = reorder_rows(cot_ordered, device_of_slot)
-
-    halves = 2 if column_share % 256 == 0 else 1
-    piece_width = column_share // halves
-    far = replica_count // 2
-    far_pieces = [
-        rep_exchange(output_share[:, i * piece_width : (i + 1) * piece_width], far)
-        for i in range(halves)
-    ]
-    head_weight = after(head_weight, far_pieces[0])
-    token_wide = token_all.astype(wide_type)
-    inverse_all = inverse_rms(token_wide)
-    first_all = (token_wide * inverse_all * prenorm_gain).astype(low_type)
-    raw = mm(first_all, head_weight, 1, 0)
     cosine, sine_part = rope_tables(position, head_dim)
 
     hidden_here = down_weight.shape[1]
     flat_down = down_weight.reshape(experts_here * hidden_here, model_width)
 
     allowed = segment[:, None] == segment[None, :]
+    far = replica_count // 2
+    steps = group_count // 2
+    part_rows = model_width // steps
+    far_parts = [
+        Exchange(output_share[i * part_rows : (i + 1) * part_rows], far) for i in range(steps)
+    ]
 
     def head_columns(values, block, head):
         start = block * width_here + head * head_dim
         return values[:, start : start + head_dim]
 
-    kept_heads = []
-    mixed_parts = []
-    for head in range(heads_here):
-        query_raw = head_columns(raw, 0, head)
-        key_raw = head_columns(raw, 1, head)
-        query_inverse = inverse_rms(query_raw)
-        key_inverse = inverse_rms(key_raw)
-        query_normed = query_raw * query_inverse * querynorm_gain
-        key_normed = key_raw * key_inverse * keynorm_gain
-        query_low = (query_normed * cosine + turn_half(query_normed) * sine_part).astype(
-            low_type
-        )
-        key_low = (key_normed * cosine + turn_half(key_normed) * sine_part).astype(low_type)
+    def project(weight, *blocks):
+        token_all = jnp.concatenate(blocks, axis=0)
+        token_wide = token_all.astype(wide_type)
+        first_all = (token_wide * inverse_rms(token_wide) * prenorm_gain).astype(low_type)
+        return token_all, first_all, mm(first_all, weight, 1, 0)
+
+    def attend(head, raw):
+        turned = []
+        for block, gain in ((0, querynorm_gain), (1, keynorm_gain)):
+            part = head_columns(raw, block, head)
+            normed = part * inverse_rms(part) * gain
+            turned.append((normed * cosine + turn_half(normed) * sine_part).astype(low_type))
         value_low = head_columns(raw, 2, head).astype(low_type)
-        scores = jnp.where(allowed, mm(query_low, key_low, 1, 1) * score_scale, masked_value)
+        scores = jnp.where(allowed, mm(*turned, 1, 1) * score_scale, masked_value)
         top_score = jnp.max(scores, axis=-1, keepdims=True)
         powers = jnp.exp(scores - top_score)
         log_total = top_score + jnp.log(jnp.sum(powers, axis=-1, keepdims=True))
         weights_low = jnp.exp(scores - log_total).astype(low_type)
-        mixed_parts.append(mm(weights_low, value_low, 1, 0).astype(low_type))
-        kept_heads.append(
-            (query_raw, key_raw, query_low, key_low, value_low, log_total)
-        )
-    mixed_low = jnp.concatenate(mixed_parts, axis=1)
-
-    mixed_ordered = reorder_rows(mixed_low, slot_of_device)
-    output_pieces = {(0, 0): output_share}
-    for i in range(halves):
-        output_pieces[far, i * piece_width] = after(far_pieces[i], mixed_ordered)
+        return (*turned, value_low, log_total, mm(weights_low, value_low, 1, 0).astype(low_type))
+
+    cot_ring = RingGather(after(cotangent, token_ring.received))
+    token_all, first_all, raw = window(
+        [cot_ring, far_parts[0]], project, head_weight, *token_ring.blocks
+    )
+    heads = []
+    for head in range(heads_here):
+        heads.append(
+            window(
+                [cot_ring, far_parts[1 + head]],
+                lambda raw, head=head: attend(head, raw),
+                raw,
+            )
+        )
+
+    def order_work(*mixed):
+        mixed_low = jnp.concatenate(mixed, axis=1)
+        return mixed_low, reorder_rows(mixed_low, slot_of_device)
+
+    mixed_low, mixed_ordered = window(
+        [cot_ring, *far_parts[1 + heads_here :]], order_work, *[head[4] for head in heads]
+    )
+    cot_all = jnp.concatenate(cot_ring.blocks, axis=0)
+    lows = jnp.concatenate([head[part] for part in range(3) for head in heads], axis=1)
+    log_totals = jnp.stack([head[3] for head in heads])
+    output_pieces = {
+        0: output_share,
+        far: jnp.concatenate([part.received for part in far_parts], axis=0),
+    }
     for distance in gather_order[1:]:
-        for j, start in list(output_pieces):
-            output_pieces[j ^ distance, start] = rep_exchange(
-                after(output_pieces[j, start], mixed_ordered), distance
-            )
+        for j in list(output_pieces):
+            output_pieces[j ^ distance] = rep_exchange(output_pieces[j], distance)
     mixed_own = (
         swap_all(mixed_ordered.reshape(group_count, row_count, width_here))
         .transpose(1, 0, 2)
         .reshape(row_count, model_width)
     )
     attention = jnp.zeros((row_count, model_width), wide_type)
-    for (j, start), piece in output_pieces.items():
+    for j, piece in output_pieces.items():
         attention = lax.dynamic_update_slice_in_dim(
-            attention, mm(mixed_own, piece, 1, 0), (replica ^ j) * column_share + start, 1
+            attention, mm(mixed_own, piece, 1, 0), (replica ^ j) * column_share, 1
         )
     residual = tokens.astype(wide_type) + attention
     inverse_two = inverse_rms(residual)
@@ -714,10 +754,10 @@
         residual_grad = upstream + post_back
         attention_low = residual_grad.astype(low_type)
         mixed_grad_own = jnp.zeros((row_count, model_width), wide_type)
-        for (j, start), piece in output_pieces.items():
+        for j, piece in output_pieces.items():
             mixed_grad_own = mixed_grad_own + mm(
                 lax.dynamic_slice_in_dim(
-                    attention_low, (replica ^ j) * column_share + start, piece.shape[1], 1
+                    attention_low, (replica ^ j) * column_share, column_share, 1
                 ),
                 piece,
                 1,
@@ -743,25 +783,19 @@
     )
     mixture = mixture_ring.total()
     layer_out = (valid_own * (residual + mixture)).astype(low_type)
-    mixed_grad = reorder_rows(swap.received.reshape(group_rows, width_here), device_of_slot)
-
-    query_raws, key_raws, query_lows, key_lows, value_lows = (
-        jnp.concatenate([kept[i] for kept in kept_heads], axis=1) for i in range(5)
-    )
-    log_totals = jnp.stack([kept[5] for kept in kept_heads])
+    mixed_grad = swap.received
+
     attention_gather = RingGather(attention_low)
     sent, gain_parts = window(
         [attention_gather],
         lambda grads: tuple(
             attention_back(
-                query_lows,
-                key_lows,
-                value_lows,
+                lows,
                 grads,
+                jnp.stack(device_of_slot),
                 log_totals,
                 segment,
-                query_raws,
-                key_raws,
+                raw,
                 jnp.stack([querynorm_gain, keynorm_gain]),
                 cosine,
                 sine_part,
@@ -780,7 +814,8 @@
 
     def first_work(sent, head):
         first_part = mm(sent, head_weight, 1, 1)
-        prenorm_part = jnp.sum(first_part * token_wide * inverse_all, axis=0)
+        token_wide = token_all.astype(wide_type)
+        prenorm_part = jnp.sum(first_part * token_wide * inverse_rms(token_wide), axis=0)
         return first_part.astype(low_type), prenorm_part, rep_scatter(head, 1, scatter_order[:1])
 
     head_part = window([attention_gather], grad_of, first_all, sent)
@@ -807,46 +842,43 @@
 
     first_ring = RingSum(slot_rows(first_low), row_count)
     small_parts = [router_part, postnorm_part, prenorm_part, querynorm_part, keynorm_part]
-    head_part, small_swapped = window(
-        [attention_gather, first_ring],
-        lambda head, *small: (rep_scatter(head, 1, scatter_order[1:]), small_swap(small)),
-        head_part,
-        *small_parts,
+    head_part = rep_scatter(head_part, 1, scatter_order[1:])
+    small_swapped = window(
+        [attention_gather, first_ring], lambda *small: small_swap(small), *small_parts
     )
     gate_sum = lax.psum_scatter(gate_part, "rep", scatter_dimension=0, tiled=True)
     up_sum = lax.psum_scatter(up_part, "rep", scatter_dimension=0, tiled=True)
-    head_swap = Swap(head_part.reshape(group_count, share, 3 * width_here), 0)
-    output_part = window(
-        [first_ring, head_swap],
+    output_part, head_part = window(
+        [first_ring],
         lambda mixed, *blocks: block_product(mixed, blocks),
         mixed_low,
         *attention_gather.blocks,
-    )
-    head_rows, output_part, small_sums = window(
+        waits=(head_part,),
+    )
+    head_rows = swap_all(head_part.reshape(group_count, share, 3 * width_here))
+    (output_part, small_sums), head_rows = window(
         [first_ring],
-        lambda head, output, small: (
-            rep_gather(
-                head.reshape(group_count, share, 3, width_here)
-                .transpose(2, 1, 0, 3)
-                .reshape(1, 3, share, model_width),
-                gather_order[:-1],
-            ),
+        lambda output, small: (
             rep_scatter(output, 0, scatter_order[:1]),
             small_pieces(small, small_parts),
         ),
-        head_swap.received,
         output_part.reshape(replica_count, share, model_width),
         small_swapped,
-    )
-    head_rows, output_part = window(
+        waits=(head_rows,),
+    )
+    head_rows = rep_gather(
+        head_rows.reshape(group_count, share, 3, width_here)
+        .transpose(2, 1, 0, 3)
+        .reshape(1, 3, share, model_width),
+        gather_order[:-1],
+    )
+    output_part, head_rows = window(
         [first_ring],
-        lambda head, output: (
-            rep_gather(head, gather_order[-1:]),
-            rep_scatter(output, 0, scatter_order[1:]),
-        ),
-        head_rows,
+        lambda output: rep_scatter(output, 0, scatter_order[1:]),
         output_part,
-    )
+        waits=(head_rows,),
+    )
+    head_rows = rep_gather(head_rows, gather_order[-1:])
     first_grad = first_ring.total()
     output_grad = (
         rep_gather(output_part, gather_order)

time: 729 us -> 707 us (0.970)
  waiting for transfers between devices: 169 us -> 158 us
  matrix products: 136 us -> 127 us
    ppermute x17 -> x18, waiting for transfers between devices: 51.3 us -> 23.2 us  [rep_exchange(): lax.ppermute(values, 'rep', [(i, i ^ distance) for i in range(count)])]
    ppermute x48 -> x56, waiting for transfers between devices: 89.5 us -> 103 us  [ring_shift(): return lax.ppermute(values, 'ep', pairs)]
    all_to_all x7, waiting for transfers between devices: 22.5 us -> 31.9 us  [swap_all(): return lax.all_to_all(values, 'ep', split_axis=0, concat_axis=0, tiled=True)]
    dot_general x30 -> x26, matrix products: 136 us -> 127 us  [mm(): lax.dot_general(left, right, (((left_dim,), (right_dim,)), ((), ())), pre...]
    ppermute x48 -> x56, starting transfers between devices: 64.9 us -> 68.3 us  [ring_shift(): return lax.ppermute(values, 'ep', pairs)]
    unnamed x320 -> x334, local copies, waits for them, and re-layouts: 34.2 us -> 35.9 us
  transfers between devices with their start and end apart: 77 -> 85, of which waited for: 28 -> 32; matrix products, arithmetic and copies ran while one was open for 41% -> 39% of each run, Pallas kernels for 9% -> 10%
where the time goes in v9:
time: 707 us; the launch traced here: 698 us
  waiting for transfers between devices  158 us (22%)
  matrix products  127 us (18%)
  starting transfers between devices  114 us (16%)
  Pallas kernels  103 us (15%)
  other arithmetic  92.9 us (13%)
  local copies, waits for them, and re-layouts  87 us (12%)
  between operations  16.8 us (2%)
    dot_general x26, matrix products, mm(): lax.dot_general(left, right, (((left_dim,), (right_dim,)), ((), ())), pre...  127 us
    ppermute x56, waiting for transfers between devices, ring_shift(): return lax.ppermute(values, 'ep', pairs)  103 us
    ppermute x56, starting transfers between devices, ring_shift(): return lax.ppermute(values, 'ep', pairs)  68.3 us
    pallas_call x2, Pallas kernels, expert_pass(): pl.pallas_call(expert_kernel, grid=(experts, steps), in_specs=[pl.BlockSp...  38.9 us
    unnamed x334, local copies, waits for them, and re-layouts  35.9 us
    pallas_call x2, Pallas kernels, expert_back(): pl.pallas_call(expert_back_kernel, grid=(depth // width,), in_specs=[whol...  33.7 us
    all_to_all x7, starting transfers between devices, swap_all(): return lax.all_to_all(values, 'ep', split_axis=0, concat_axis=0, tiled=True)  33.3 us
    all_to_all x7, waiting for transfers between devices, swap_all(): return lax.all_to_all(values, 'ep', split_axis=0, concat_axis=0, tiled=True)  31.9 us
  transfers between devices with their start and end apart: 85, of which 32 were waited for; matrix products, arithmetic and copies ran while one was open for 39% of the time, Pallas kernels for 10%

profile of v9, /device:TPU:0, one launch (start us, length us, event | category | flops | bytes accessed | tf_op | source)
XLA Modules:
  0.0 698.5 jit_solution(8463070210634486483)
XLA Ops:
  9.8 7.4 %all-to-all-start = ((bf16[8,64,768]{2,1,0:T(8,128)(2,1)}), bf16[8,64,768]{2,1,0:T(8,128)(2,1)S(1)}, u32[]{:S(2)}, u32[]{:S(2)}) async-start(bf16[8,64,768]{2,1,0:T(8,128)(2,1)} %copy.127), calls=%async_computation | async-start | bytes 1572864 | tf_op jit(solution)/shard_map/all_to_all | solution.py:250
  19.0 18.4 %all-to-all-done = bf16[8,64,768]{2,1,0:T(8,128)(2,1)S(1)} async-done(((bf16[8,64,768]{2,1,0:T(8,128)(2,1)}), bf16[8,64,768]{2,1,0:T(8,128)(2,1)S(1)}, u32[]{:S(2)}, u32[]{:S(2)}) %all-to-all-start) | async-done | bytes 786464 | tf_op jit(solution)/shard_map/all_to_all | solution.py:250
  39.2 3.7 multiply_cosine_fusion
  43.6 3.6 all-to-all-start.2
  51.3 5.3 all-to-all-done.2
  62.5 3.9 collective-permute-done.11
  71.4 3.8 collective-permute-start.1
  75.7 24.7 %collective-permute-done.1 = bf16[160,2048]{1,0:T(8,128)(2,1)} collective-permute-done((bf16[160,2048]{1,0:T(8,128)(2,1)}, bf16[160,2048]{1,0:T(8,128)(2,1)}, u32[]{:S(2)}, u32[]{:S(2)}) %collective-permute-start.1) | collective-permute-done | bytes 655392 | tf_op jit(solution)/shard_map/ppermute | solution.py:88
  100.4 4.0 collective-permute-start.2
  109.5 11.7 %collective-permute-done.6 = bf16[160,2048]{1,0:T(8,128)(2,1)S(1)} collective-permute-done((bf16[160,2048]{1,0:T(8,128)(2,1)}, bf16[160,2048]{1,0:T(8,128)(2,1)S(1)}, u32[]{:S(2)}, u32[]{:S(2)}) %collective-permute-start.6) | collective-permute-done | bytes 655392 | tf_op jit(solution)/shard_map/ppermute | solution.py:88
  125.9 2.3 maximum_select_fusion
  145.8 4.3 fusion.75.query_raw_ref.key_raw_ref
  163.1 2.4 collective-permute-done.13
  185.0 3.8 collective-permute-done.19
  190.2 4.4 all-to-all-start.1
  196.5 2.3 constant_dynamic-update-slice_fusion.44
  198.9 2.3 constant_dynamic-update-slice_fusion.43
  204.2 4.1 all-to-all-done.1
  220.6 7.4 %fusion.76.stream_ref = f32[640,2048]{1,0:T(8,128)} fusion(bf16[640,2048]{1,0:T(8,128)(2,1)S(1)} %copy-done.34, bf16[2048,2048]{1,0:T(8,128)(2,1)S(1)} %bitcast.293), kind=kOutput, calls=%fused_computation.341 | convolution fusion | flops 5368709120 | bytes 16252928 | tf_op jit(solution)/shard_map/dot_general | solution.py:60
  229.2 2.4 collective-permute-done.24
  235.1 8.9 %fusion.77.stream_ref = f32[640,2048]{1,0:T(8,128)} fusion(bf16[640,2048]{1,0:T(8,128)(2,1)} %get-tuple-element.219, bf16[2048,2048]{1,0:T(8,128)(2,1)S(1)} %bitcast.294), kind=kOutput, calls=%fused_computation.342 | convolution fusion | flops 5368709120 | bytes 16252928 | tf_op jit(solution)/shard_map/dot_general | solution.py:60
  246.1 2.7 collective-permute-done.27
  255.0 19.4 %shard_map.281 = (bf16[1280,2048]{1,0:T(8,128)(2,1)}, bf16[1280,2048]{1,0:T(8,128)(2,1)}, bf16[1280,2048]{1,0:T(8,128)(2,1)}, f32[2,640,128]{2,1,0:T(8,128)}) custom-call(bf16[640,2048]{1,0:T(8,128)(2,1)} %copy-done.35, bf16[2,2048,1024]{2,1,0:T(8,128)(2,1)} %gate_ref.7, bf16[2,2048,1024]{2,1,0:T(8,128)(2,1)} %up_ref.7, f32[640,2048]{1,0:T(8,128)} %fusion.76.stream_ref, ...), custom_call_target="tpu_custom_call" | custom-call | flops 10737418240 | bytes 42991616 | tf_op jit(solution)/shard_map/pallas_call | solution.py:294
  278.8 2.8 collective-permute-done.30
  288.0 19.4 %shard_map.282 = (bf16[1280,2048]{1,0:T(8,128)(2,1)}, bf16[1280,2048]{1,0:T(8,128)(2,1)}, bf16[1280,2048]{1,0:T(8,128)(2,1)}, f32[2,640,128]{2,1,0:T(8,128)}) custom-call(bf16[640,2048]{1,0:T(8,128)(2,1)} %copy-done.27, bf16[2,2048,1024]{2,1,0:T(8,128)(2,1)} %gate_ref.7, ...), custom_call_target="tpu_custom_call", output_to_operand_aliasing={{0}: (5, {}), {1}: (6, {}), {2}: (7, {})} | custom-call | flops 10737418240 | bytes 42991616 | tf_op jit(solution)/shard_map/pallas_call | solution.py:294
  307.5 16.8 %shard_map.283 = bf16[640,2048]{1,0:T(8,128)(2,1)} custom-call(bf16[1280,2048]{1,0:T(8,128)(2,1)} %get-tuple-element.260.gback_ref, bf16[1280,2048]{1,0:T(8,128)(2,1)} %get-tuple-element.270.uback_ref, bf16[2,2048,1024]{2,1,0:T(8,128)(2,1)} %gate_ref.7, bf16[2,2048,1024]{2,1,0:T(8,128)(2,1)} %up_ref.7), custom_call_target="tpu_custom_call" | custom-call | flops 10737418240 | bytes 24641536 | tf_op jit(solution)/shard_map/pallas_call | solution.py:334
  329.2 16.9 %shard_map.284 = bf16[640,2048]{1,0:T(8,128)(2,1)} custom-call(bf16[1280,2048]{1,0:T(8,128)(2,1)} %get-tuple-element.260.gback_ref, bf16[1280,2048]{1,0:T(8,128)(2,1)} %get-tuple-element.270.uback_ref, bf16[2,2048,1024]{2,1,0:T(8,128)(2,1)} %gate_ref.7, bf16[2,2048,1024]{2,1,0:T(8,128)(2,1)} %up_ref.7), custom_call_target="tpu_custom_call" | custom-call | flops 10737418240 | bytes 24641536 | tf_op jit(solution)/shard_map/pallas_call | solution.py:334
  351.9 3.3 all-to-all-start.3
  355.3 16.5 %convolution_convert_fusion.3 = bf16[1280,2048]{1,0:T(8,128)(2,1)} fusion(bf16[1280,2048]{1,0:T(8,128)(2,1)} %get-tuple-element.254, bf16[2048,2048]{1,0:T(8,128)(2,1)} %bitcast.290), kind=kOutput, calls=%fused_computation.17 | convolution fusion | flops 10740039680 | bytes 18874368 | tf_op jit(solution)/shard_map/dot_general | solution.py:60
  375.6 2.3 collective-permute-start.37
  381.7 16.7 %convolution_convert_fusion.2 = bf16[2048,2048]{1,0:T(8,128)(2,1)} fusion(bf16[1280,2048]{1,0:T(8,128)(2,1)} %get-tuple-element.254, bf16[1280,2048]{1,0:T(8,128)(2,1)} %get-tuple-element.519), kind=kOutput, calls=%fused_computation.16 | convolution fusion | flops 10741612544 | bytes 18874368 | tf_op jit(solution)/shard_map/dot_general | solution.py:60
  405.1 2.8 add_convert_fusion.9
  410.1 18.4 %convolution_convert_fusion.1 = bf16[2048,2048]{1,0:T(8,128)(2,1)} fusion(bf16[1280,2048]{1,0:T(8,128)(2,1)} %get-tuple-element.515, bf16[1280,2048]{1,0:T(8,128)(2,1)} %get-tuple-element.260.gback_ref), kind=kOutput, calls=%fused_computation.15 | convolution fusion | flops 10741612544 | bytes 18874368 | tf_op jit(solution)/shard_map/dot_general | solution.py:60
  428.5 2.5 collective-permute-done.40
  439.8 2.5 convolution_add_fusion.1
  442.3 2.4 fusion.31
  444.8 2.6 fusion.14
  448.3 2.8 add_convert_fusion.5
  453.1 4.6 all-to-all-start.4
  458.0 16.7 %convolution_convert_fusion = bf16[2048,2048]{1,0:T(8,128)(2,1)} fusion(bf16[1280,2048]{1,0:T(8,128)(2,1)} %get-tuple-element.515, bf16[1280,2048]{1,0:T(8,128)(2,1)} %get-tuple-element.270.uback_ref), kind=kOutput, calls=%fused_computation.14 | convolution fusion | flops 10741612544 | bytes 18874368 | tf_op jit(solution)/shard_map/dot_general | solution.py:60
  489.7 23.8 %shard_map.285 = (bf16[1280,768]{1,0:T(8,128)(2,1)}, f32[2,128]{1,0:T(2,128)}) custom-call(s32[8]{0:T(128)} %stack.164.order_ref, bf16[1280,768]{1,0:T(8,128)(2,1)} %constant_dynamic-update-slice_fusion.58.query_ref.key_ref.value_ref, bf16[1280,768]{1,0:T(8,128)(2,1)} %constant_dynamic-update-slice_fusion.58.query_ref.key_ref.value_ref, ...), custom_call_target="tpu_custom_call" | custom-call | flops 4194304000 | bytes 9830400 | tf_op jit(solution)/shard_map/pallas_call | solution.py:408
  516.0 7.5 %convolution_convert_fusion.4 = bf16[2048,768]{1,0:T(8,128)(2,1)S(1)} fusion(bf16[1280,2048]{1,0:T(8,128)(2,1)} %copy-done.20, bf16[1280,768]{1,0:T(8,128)(2,1)} %get-tuple-element.298), kind=kOutput, calls=%fused_computation.22 | convolution fusion | flops 4028104704 | bytes 10354688 | tf_op jit(solution)/shard_map/dot_general | solution.py:60
  524.5 2.3 collective-permute-done.51.refs_3_
  527.0 3.7 fusion.5
  532.9 6.6 fusion.4
  541.5 6.6 collective-permute-done.52.refs_6_
  558.0 3.7 all-to-all-start.5
  561.6 3.3 multiply_convert_fusion
  564.9 2.5 convert_element_type.510
  569.2 4.1 all-to-all-done.5
  579.6 3.0 slice_bitcast_fusion.3
  584.6 6.5 shard_map.286
  591.1 8.0 %collective-permute-done.61 = bf16[8,1,64,768]{3,2,1,0:T(8,128)(2,1)S(1)} collective-permute-done((bf16[8,1,64,768]{3,2,1,0:T(8,128)(2,1)}, bf16[8,1,64,768]{3,2,1,0:T(8,128)(2,1)S(1)}, u32[]{:S(2)}, u32[]{:S(2)}) %collective-permute-start.61) | collective-permute-done | bytes 786464 | tf_op jit(solution)/shard_map/ppermute | solution.py:204
  600.2 3.4 add_convert_fusion.3
  604.7 6.3 all-to-all-start.6
  612.8 2.3 maximum_convert_fusion
  618.4 20.8 %collective-permute-done.62 = bf16[160,2048]{1,0:T(8,128)(2,1)S(1)} collective-permute-done((bf16[160,2048]{1,0:T(8,128)(2,1)S(1)}, bf16[160,2048]{1,0:T(8,128)(2,1)S(1)}, u32[]{:S(2)}, u32[]{:S(2)}) %collective-permute-start.62) | collective-permute-done | bytes 655392 | tf_op jit(solution)/shard_map/ppermute | solution.py:88
  640.8 2.8 add_convert_fusion.1
  645.0 2.5 reshape.560
  651.0 2.3 maximum_convert_fusion.1
  653.3 5.7 collective-permute-start.67
  660.9 7.9 %collective-permute-done.69 = bf16[1,3,64,2048]{3,2,1,0:T(8,128)(2,1)} collective-permute-done((bf16[1,3,64,2048]{3,2,1,0:T(8,128)(2,1)S(1)}, bf16[1,3,64,2048]{3,2,1,0:T(8,128)(2,1)}, u32[]{:S(2)}, u32[]{:S(2)}) %collective-permute-start.69) | collective-permute-done | bytes 786464 | tf_op jit(solution)/shard_map/ppermute | solution.py:204
  677.4 3.4 collective-permute-done.72
  680.9 2.7 fusion.20
  (672 shorter events, 236.5 us)
Async XLA Ops:
  9.8 27.6 %all-to-all-start = ((bf16[8,64,768]{2,1,0:T(8,128)(2,1)}), bf16[8,64,768]{2,1,0:T(8,128)(2,1)S(1)}, u32[]{:S(2)}, u32[]{:S(2)}) async-start(bf16[8,64,768]{2,1,0:T(8,128)(2,1)} %copy.127), calls=%async_computation | async-start | bytes 1572864 | tf_op jit(solution)/shard_map/all_to_all | solution.py:250
  17.2 106.8 %all-gather.2.cloned.1.call-start = ((), (), s32[]{:S(2)}) async-start(), calls=%async_computation.10 | async-start | bytes 2359296 | tf_op jit(solution)/shard_map/all_gather | solution.py:69
  47.2 19.2 %collective-permute-start.11 = (bf16[1,8,64,768]{3,2,1,0:T(8,128)(2,1)S(1)}, bf16[1,8,64,768]{3,2,1,0:T(8,128)(2,1)S(1)}, u32[]{:S(2)}, u32[]{:S(2)}) collective-permute-start(bf16[1,8,64,768]{3,2,1,0:T(8,128)(2,1)S(1)} %bitcast.176), channel_id=1, source_target_pairs={{0,16},{8,24},{16,0},{24,8},{1,17},{9,25},{17,1},{25,9},{2,18},{10... | collective-permute-start | bytes 2359304 | tf_op jit(solution)/shard_map/ppermute | solution.py:204
  49.3 22.2 %collective-permute-start = (bf16[160,2048]{1,0:T(8,128)(2,1)S(1)}, bf16[160,2048]{1,0:T(8,128)(2,1)}, u32[]{:S(2)}, u32[]{:S(2)}) collective-permute-start(bf16[160,2048]{1,0:T(8,128)(2,1)S(1)} %copy-done.8), channel_id=1, source_target_pairs={{0,2},{2,4},{4,6},{6,7},{7,5},{5,3},{3,1},{1,0},{8,10},{10,12},{12... | collective-permute-start | bytes 1966088 | tf_op jit(solution)/shard_map/ppermute | solution.py:88
  51.3 24.0 %collective-permute-start.4 = (bf16[160,2048]{1,0:T(8,128)(2,1)S(1)}, bf16[160,2048]{1,0:T(8,128)(2,1)}, u32[]{:S(2)}, u32[]{:S(2)}) collective-permute-start(bf16[160,2048]{1,0:T(8,128)(2,1)S(1)} %copy-done.8), channel_id=1, source_target_pairs={{0,1},{2,0},{4,2},{6,4},{7,6},{5,7},{3,5},{1,3},{8,9},{10,8},{12,1... | collective-permute-start | bytes 1966088 | tf_op jit(solution)/shard_map/ppermute | solution.py:88
  67.7 58.1 %collective-permute-start.12 = (bf16[2,8,64,768]{3,2,1,0:T(8,128)(2,1)}, bf16[2,8,64,768]{3,2,1,0:T(8,128)(2,1)}, u32[]{:S(2)}, u32[]{:S(2)}) collective-permute-start(bf16[2,8,64,768]{3,2,1,0:T(8,128)(2,1)} %maximum_select_fusion.3), channel_id=1, source_target_pairs={{0,8},{8,0},{16,24},{24,16},{1,9},{9,1},{17,25},{25,17},{2,10},{10... | collective-permute-start | bytes 4718600 | tf_op jit(solution)/shard_map/ppermute | solution.py:204
  71.4 28.9 %collective-permute-start.1 = (bf16[160,2048]{1,0:T(8,128)(2,1)}, bf16[160,2048]{1,0:T(8,128)(2,1)}, u32[]{:S(2)}, u32[]{:S(2)}) collective-permute-start(bf16[160,2048]{1,0:T(8,128)(2,1)} %collective-permute-done), channel_id=1, source_target_pairs={{0,2},{2,4},{4,6},{6,7},{7,5},{5,3},{3,1},{1,0},{8,10},{10,12},{12... | collective-permute-start | bytes 1966088 | tf_op jit(solution)/shard_map/ppermute | solution.py:88
  75.3 29.3 %collective-permute-start.5 = (bf16[160,2048]{1,0:T(8,128)(2,1)}, bf16[160,2048]{1,0:T(8,128)(2,1)}, u32[]{:S(2)}, u32[]{:S(2)}) collective-permute-start(bf16[160,2048]{1,0:T(8,128)(2,1)} %collective-permute-done.4), channel_id=1, source_target_pairs={{0,1},{2,0},{4,2},{6,4},{7,6},{5,7},{3,5},{1,3},{8,9},{10,8},{12,1... | collective-permute-start | bytes 1966088 | tf_op jit(solution)/shard_map/ppermute | solution.py:88
  100.4 23.6 %collective-permute-start.2 = (bf16[160,2048]{1,0:T(8,128)(2,1)}, bf16[160,2048]{1,0:T(8,128)(2,1)}, u32[]{:S(2)}, u32[]{:S(2)}) collective-permute-start(bf16[160,2048]{1,0:T(8,128)(2,1)} %collective-permute-done.1), channel_id=1, source_target_pairs={{0,2},{2,4},{4,6},{6,7},{7,5},{5,3},{3,1},{1,0},{8,10},{10,12},{12... | collective-permute-start | bytes 1966088 | tf_op jit(solution)/shard_map/ppermute | solution.py:88
  104.5 16.7 %collective-permute-start.6 = (bf16[160,2048]{1,0:T(8,128)(2,1)}, bf16[160,2048]{1,0:T(8,128)(2,1)S(1)}, u32[]{:S(2)}, u32[]{:S(2)}) collective-permute-start(bf16[160,2048]{1,0:T(8,128)(2,1)} %collective-permute-done.5), channel_id=1, source_target_pairs={{0,1},{2,0},{4,2},{6,4},{7,6},{5,7},{3,5},{1,3},{8,9},{10,8},{12,1... | collective-permute-start | bytes 1966088 | tf_op jit(solution)/shard_map/ppermute | solution.py:88
  129.9 20.4 %collective-permute-start.10 = (bf16[512,512]{1,0:T(8,128)(2,1)S(1)}, bf16[512,512]{1,0:T(8,128)(2,1)S(1)}, u32[]{:S(2)}, u32[]{:S(2)}) collective-permute-start(bf16[512,512]{1,0:T(8,128)(2,1)S(1)} %get-tuple-element.486), channel_id=1, source_target_pairs={{0,16},{8,24},{16,0},{24,8},{1,17},{9,25},{17,1},{25,9},{2,18},{10... | collective-permute-start | bytes 1572872 | tf_op jit(solution)/shard_map/ppermute | solution.py:204
  131.8 31.2 %collective-permute-start.15 = (bf16[512,512]{1,0:T(8,128)(2,1)S(1)}, bf16[512,512]{1,0:T(8,128)(2,1)S(1)}, u32[]{:S(2)}, u32[]{:S(2)}) collective-permute-start(bf16[512,512]{1,0:T(8,128)(2,1)S(1)} %get-tuple-element.485), channel_id=1, source_target_pairs={{0,16},{8,24},{16,0},{24,8},{1,17},{9,25},{17,1},{25,9},{2,18},{10... | collective-permute-start | bytes 1572872 | tf_op jit(solution)/shard_map/ppermute | solution.py:204
  132.0 46.1 %collective-permute-start.18 = (bf16[512,512]{1,0:T(8,128)(2,1)S(1)}, bf16[512,512]{1,0:T(8,128)(2,1)S(1)}, u32[]{:S(2)}, u32[]{:S(2)}) collective-permute-start(bf16[512,512]{1,0:T(8,128)(2,1)S(1)} %get-tuple-element.484), channel_id=1, source_target_pairs={{0,16},{8,24},{16,0},{24,8},{1,17},{9,25},{17,1},{25,9},{2,18},{10... | collective-permute-start | bytes 1572872 | tf_op jit(solution)/shard_map/ppermute | solution.py:204
  133.8 17.0 %collective-permute-start.8 = (bf16[160,2048]{1,0:T(8,128)(2,1)S(1)}, bf16[160,2048]{1,0:T(8,128)(2,1)S(1)}, u32[]{:S(2)}, u32[]{:S(2)}) collective-permute-start(bf16[160,2048]{1,0:T(8,128)(2,1)S(1)} %copy-done.13), channel_id=1, source_target_pairs={{0,2},{2,4},{4,6},{6,7},{7,5},{5,3},{3,1},{1,0},{8,10},{10,12},{12... | collective-permute-start | bytes 1966088 | tf_op jit(solution)/shard_map/ppermute | solution.py:88
  135.6 15.2 %collective-permute-start.9 = (bf16[160,2048]{1,0:T(8,128)(2,1)S(1)}, bf16[160,2048]{1,0:T(8,128)(2,1)S(1)}, u32[]{:S(2)}, u32[]{:S(2)}) collective-permute-start(bf16[160,2048]{1,0:T(8,128)(2,1)S(1)} %copy-done.13), channel_id=1, source_target_pairs={{0,1},{2,0},{4,2},{6,4},{7,6},{5,7},{3,5},{1,3},{8,9},{10,8},{12,1... | collective-permute-start | bytes 1966088 | tf_op jit(solution)/shard_map/ppermute | solution.py:88
  150.3 34.7 %collective-permute-start.21 = (bf16[512,512]{1,0:T(8,128)(2,1)S(1)}, bf16[512,512]{1,0:T(8,128)(2,1)}, u32[]{:S(2)}, u32[]{:S(2)}) collective-permute-start(bf16[512,512]{1,0:T(8,128)(2,1)S(1)} %get-tuple-element.483), channel_id=1, source_target_pairs={{0,16},{8,24},{16,0},{24,8},{1,17},{9,25},{17,1},{25,9},{2,18},{10... | collective-permute-start | bytes 1572872 | tf_op jit(solution)/shard_map/ppermute | solution.py:204
  150.9 14.6 %collective-permute-start.14 = (bf16[160,2048]{1,0:T(8,128)(2,1)S(1)}, bf16[160,2048]{1,0:T(8,128)(2,1)S(1)}, u32[]{:S(2)}, u32[]{:S(2)}) collective-permute-start(bf16[160,2048]{1,0:T(8,128)(2,1)S(1)} %collective-permute-done.9), channel_id=1, source_target_pairs={{0,1},{2,0},{4,2},{6,4},{7,6},{5,7},{3,5},{1,3},{8,9},{10,8},{12,1... | collective-permute-start | bytes 1966088 | tf_op jit(solution)/shard_map/ppermute | solution.py:88
  163.0 49.4 %collective-permute-start.22 = (bf16[2048,512]{1,0:T(8,128)(2,1)S(1)}, bf16[2048,512]{1,0:T(8,128)(2,1)}, u32[]{:S(2)}, u32[]{:S(2)}) collective-permute-start(bf16[2048,512]{1,0:T(8,128)(2,1)S(1)} %copy-done.6), channel_id=1, source_target_pairs={{0,8},{8,0},{16,24},{24,16},{1,9},{9,1},{17,25},{25,17},{2,10},{10... | collective-permute-start | bytes 6291464 | tf_op jit(solution)/shard_map/ppermute | solution.py:204
  165.5 14.8 %collective-permute-start.16 = (bf16[160,2048]{1,0:T(8,128)(2,1)S(1)}, bf16[160,2048]{1,0:T(8,128)(2,1)S(1)}, u32[]{:S(2)}, u32[]{:S(2)}) collective-permute-start(bf16[160,2048]{1,0:T(8,128)(2,1)S(1)} %collective-permute-done.13), channel_id=1, source_target_pairs={{0,2},{2,4},{4,6},{6,7},{7,5},{5,3},{3,1},{1,0},{8,10},{10,12},{12... | collective-permute-start | bytes 1966088 | tf_op jit(solution)/shard_map/ppermute | solution.py:88
  166.7 14.9 %collective-permute-start.17 = (bf16[160,2048]{1,0:T(8,128)(2,1)S(1)}, bf16[160,2048]{1,0:T(8,128)(2,1)S(1)}, u32[]{:S(2)}, u32[]{:S(2)}) collective-permute-start(bf16[160,2048]{1,0:T(8,128)(2,1)S(1)} %collective-permute-done.14), channel_id=1, source_target_pairs={{0,1},{2,0},{4,2},{6,4},{7,6},{5,7},{3,5},{1,3},{8,9},{10,8},{12,1... | collective-permute-start | bytes 1966088 | tf_op jit(solution)/shard_map/ppermute | solution.py:88
  190.2 18.2 %all-to-all-start.1 = ((bf16[8,160,256]{2,1,0:T(8,128)(2,1)}), bf16[8,160,256]{2,1,0:T(8,128)(2,1)}, u32[]{:S(2)}, u32[]{:S(2)}) async-start(bf16[8,160,256]{2,1,0:T(8,128)(2,1)} %copy-done.58), calls=%async_computation.1 | async-start | bytes 1310720 | tf_op jit(solution)/shard_map/all_to_all | solution.py:250
  196.5 18.2 %collective-permute-start.23 = (bf16[2048,512]{1,0:T(8,128)(2,1)}, bf16[2048,512]{1,0:T(8,128)(2,1)}, u32[]{:S(2)}, u32[]{:S(2)}) collective-permute-start(bf16[2048,512]{1,0:T(8,128)(2,1)} %constant_dynamic-update-slice_fusion.18), channel_id=1, source_target_pairs={{0,8},{8,0},{16,24},{24,16},{1,9},{9,1},{17,25},{25,17},{2,10},{10... | collective-permute-start | bytes 6291464 | tf_op jit(solution)/shard_map/ppermute | solution.py:204
  249.1 25.3 %collective-permute-start.29 = (bf16[160,2048]{1,0:T(8,128)(2,1)S(1)}, bf16[160,2048]{1,0:T(8,128)(2,1)S(1)}, u32[]{:S(2)}, u32[]{:S(2)}) collective-permute-start(bf16[160,2048]{1,0:T(8,128)(2,1)S(1)} %collective-permute-done.27), channel_id=1, source_target_pairs={{0,1},{2,0},{4,2},{6,4},{7,6},{5,7},{3,5},{1,3},{8,9},{10,8},{12,1... | collective-permute-start | bytes 1966088 | tf_op jit(solution)/shard_map/ppermute | solution.py:88
  249.2 25.2 %collective-permute-start.28 = (bf16[160,2048]{1,0:T(8,128)(2,1)S(1)}, bf16[160,2048]{1,0:T(8,128)(2,1)S(1)}, u32[]{:S(2)}, u32[]{:S(2)}) collective-permute-start(bf16[160,2048]{1,0:T(8,128)(2,1)S(1)} %collective-permute-done.26), channel_id=1, source_target_pairs={{0,2},{2,4},{4,6},{6,7},{7,5},{5,3},{3,1},{1,0},{8,10},{10,12},{12... | collective-permute-start | bytes 1966088 | tf_op jit(solution)/shard_map/ppermute | solution.py:88
  326.5 19.9 %collective-permute-start.32 = (bf16[80,2048]{1,0:T(8,128)(2,1)}, bf16[80,2048]{1,0:T(8,128)(2,1)}, u32[]{:S(2)}, u32[]{:S(2)}) collective-permute-start(bf16[80,2048]{1,0:T(8,128)(2,1)} %get-tuple-element.476), channel_id=1, source_target_pairs={{0,2},{2,4},{4,6},{6,7},{7,5},{5,3},{3,1},{1,0},{8,10},{10,12},{12... | collective-permute-start | bytes 983048 | tf_op jit(solution)/shard_map/ppermute | solution.py:88
  328.0 18.4 %collective-permute-start.33 = (bf16[80,2048]{1,0:T(8,128)(2,1)S(1)}, bf16[80,2048]{1,0:T(8,128)(2,1)}, u32[]{:S(2)}, u32[]{:S(2)}) collective-permute-start(bf16[80,2048]{1,0:T(8,128)(2,1)S(1)} %get-tuple-element.475), channel_id=1, source_target_pairs={{0,1},{2,0},{4,2},{6,4},{7,6},{5,7},{3,5},{1,3},{8,9},{10,8},{12,1... | collective-permute-start | bytes 983048 | tf_op jit(solution)/shard_map/ppermute | solution.py:88
  348.7 23.1 %collective-permute-start.35 = (bf16[160,2048]{1,0:T(8,128)(2,1)}, bf16[160,2048]{1,0:T(8,128)(2,1)}, u32[]{:S(2)}, u32[]{:S(2)}) collective-permute-start(bf16[160,2048]{1,0:T(8,128)(2,1)} %pad_maximum_fusion.7), channel_id=1, source_target_pairs={{0,1},{2,0},{4,2},{6,4},{7,6},{5,7},{3,5},{1,3},{8,9},{10,8},{12,1... | collective-permute-start | bytes 1966088 | tf_op jit(solution)/shard_map/ppermute | solution.py:88
  349.1 22.8 %collective-permute-start.34 = (bf16[160,2048]{1,0:T(8,128)(2,1)S(1)}, bf16[160,2048]{1,0:T(8,128)(2,1)}, u32[]{:S(2)}, u32[]{:S(2)}) collective-permute-start(bf16[160,2048]{1,0:T(8,128)(2,1)S(1)} %pad_maximum_fusion.6), channel_id=1, source_target_pairs={{0,2},{2,4},{4,6},{6,7},{7,5},{5,3},{3,1},{1,0},{8,10},{10,12},{12... | collective-permute-start | bytes 1966088 | tf_op jit(solution)/shard_map/ppermute | solution.py:88
  351.9 19.9 %all-to-all-start.3 = ((f32[8,160,2]{1,2,0:T(2,128)}), f32[8,160,2]{1,2,0:T(2,128)S(1)}, u32[]{:S(2)}, u32[]{:S(2)}) async-start(f32[8,160,2]{1,2,0:T(2,128)} %copy.161), calls=%async_computation.3 | async-start | bytes 32768 | tf_op jit(solution)/shard_map/all_to_all | solution.py:250
  355.2 160.8 %reduce-scatter.4.cloned.1.call-start = ((), (), s32[]{:S(2)}) async-start(), calls=%async_computation.11 | async-start | bytes 10485760 | tf_op jit(solution)/shard_map/reduce_scatter | solution.py:807
  375.6 24.7 %collective-permute-start.37 = (bf16[160,2048]{1,0:T(8,128)(2,1)S(1)}, bf16[160,2048]{1,0:T(8,128)(2,1)}, u32[]{:S(2)}, u32[]{:S(2)}) collective-permute-start(bf16[160,2048]{1,0:T(8,128)(2,1)S(1)} %add_convert_fusion.11), channel_id=1, source_target_pairs={{0,1},{2,0},{4,2},{6,4},{7,6},{5,7},{3,5},{1,3},{8,9},{10,8},{12,1... | collective-permute-start | bytes 1966088 | tf_op jit(solution)/shard_map/ppermute | solution.py:88
  377.9 22.4 %collective-permute-start.38 = (bf16[80,2048]{1,0:T(8,128)(2,1)}, bf16[80,2048]{1,0:T(8,128)(2,1)}, u32[]{:S(2)}, u32[]{:S(2)}) collective-permute-start(bf16[80,2048]{1,0:T(8,128)(2,1)} %get-tuple-element.461), channel_id=1, source_target_pairs={{0,2},{2,4},{4,6},{6,7},{7,5},{5,3},{3,1},{1,0},{8,10},{10,12},{12... | collective-permute-start | bytes 983048 | tf_op jit(solution)/shard_map/ppermute | solution.py:88
  378.0 22.3 %collective-permute-start.39 = (bf16[80,2048]{1,0:T(8,128)(2,1)}, bf16[80,2048]{1,0:T(8,128)(2,1)}, u32[]{:S(2)}, u32[]{:S(2)}) collective-permute-start(bf16[80,2048]{1,0:T(8,128)(2,1)} %get-tuple-element.460), channel_id=1, source_target_pairs={{0,1},{2,0},{4,2},{6,4},{7,6},{5,7},{3,5},{1,3},{8,9},{10,8},{12,1... | collective-permute-start | bytes 983048 | tf_op jit(solution)/shard_map/ppermute | solution.py:88
  381.4 18.9 %collective-permute-start.36 = (bf16[160,2048]{1,0:T(8,128)(2,1)S(1)}, bf16[160,2048]{1,0:T(8,128)(2,1)}, u32[]{:S(2)}, u32[]{:S(2)}) collective-permute-start(bf16[160,2048]{1,0:T(8,128)(2,1)S(1)} %add_convert_fusion.12), channel_id=1, source_target_pairs={{0,2},{2,4},{4,6},{6,7},{7,5},{5,3},{3,1},{1,0},{8,10},{10,12},{12... | collective-permute-start | bytes 1966088 | tf_op jit(solution)/shard_map/ppermute | solution.py:88
  400.3 179.2 %reduce-scatter.6.cloned.1.call-start = ((), (), s32[]{:S(2)}) async-start(), calls=%async_computation.12 | async-start | bytes 10485760 | tf_op jit(solution)/shard_map/reduce_scatter | solution.py:849
  402.9 25.6 %collective-permute-start.43 = (bf16[160,2048]{1,0:T(8,128)(2,1)}, bf16[160,2048]{1,0:T(8,128)(2,1)S(1)}, u32[]{:S(2)}, u32[]{:S(2)}) collective-permute-start(bf16[160,2048]{1,0:T(8,128)(2,1)} %pad_maximum_fusion.9), channel_id=1, source_target_pairs={{0,1},{2,0},{4,2},{6,4},{7,6},{5,7},{3,5},{1,3},{8,9},{10,8},{12,1... | collective-permute-start | bytes 1966088 | tf_op jit(solution)/shard_map/ppermute | solution.py:88
  404.8 23.6 %collective-permute-start.42 = (bf16[160,2048]{1,0:T(8,128)(2,1)S(1)}, bf16[160,2048]{1,0:T(8,128)(2,1)}, u32[]{:S(2)}, u32[]{:S(2)}) collective-permute-start(bf16[160,2048]{1,0:T(8,128)(2,1)S(1)} %pad_maximum_fusion.8), channel_id=1, source_target_pairs={{0,2},{2,4},{4,6},{6,7},{7,5},{5,3},{3,1},{1,0},{8,10},{10,12},{12... | collective-permute-start | bytes 1966088 | tf_op jit(solution)/shard_map/ppermute | solution.py:88
  407.9 23.1 %collective-permute-start.40 = (bf16[160,2048]{1,0:T(8,128)(2,1)}, bf16[160,2048]{1,0:T(8,128)(2,1)S(1)}, u32[]{:S(2)}, u32[]{:S(2)}) collective-permute-start(bf16[160,2048]{1,0:T(8,128)(2,1)} %get-tuple-element.472), channel_id=1, source_target_pairs={{0,2},{2,4},{4,6},{6,7},{7,5},{5,3},{3,1},{1,0},{8,10},{10,12},{12... | collective-permute-start | bytes 1966088 | tf_op jit(solution)/shard_map/ppermute | solution.py:88
  409.8 21.2 %collective-permute-start.41 = (bf16[160,2048]{1,0:T(8,128)(2,1)}, bf16[160,2048]{1,0:T(8,128)(2,1)S(1)}, u32[]{:S(2)}, u32[]{:S(2)}) collective-permute-start(bf16[160,2048]{1,0:T(8,128)(2,1)} %get-tuple-element.471), channel_id=1, source_target_pairs={{0,1},{2,0},{4,2},{6,4},{7,6},{5,7},{3,5},{1,3},{8,9},{10,8},{12,1... | collective-permute-start | bytes 1966088 | tf_op jit(solution)/shard_map/ppermute | solution.py:88
  433.1 15.1 %collective-permute-start.44 = (bf16[160,2048]{1,0:T(8,128)(2,1)S(1)}, bf16[160,2048]{1,0:T(8,128)(2,1)S(1)}, u32[]{:S(2)}, u32[]{:S(2)}) collective-permute-start(bf16[160,2048]{1,0:T(8,128)(2,1)S(1)} %get-tuple-element.457), channel_id=1, source_target_pairs={{0,2},{2,4},{4,6},{6,7},{7,5},{5,3},{3,1},{1,0},{8,10},{10,12},{12... | collective-permute-start | bytes 1966088 | tf_op jit(solution)/shard_map/ppermute | solution.py:88
  433.2 15.1 %collective-permute-start.45 = (bf16[160,2048]{1,0:T(8,128)(2,1)S(1)}, bf16[160,2048]{1,0:T(8,128)(2,1)S(1)}, u32[]{:S(2)}, u32[]{:S(2)}) collective-permute-start(bf16[160,2048]{1,0:T(8,128)(2,1)S(1)} %get-tuple-element.456), channel_id=1, source_target_pairs={{0,1},{2,0},{4,2},{6,4},{7,6},{5,7},{3,5},{1,3},{8,9},{10,8},{12,1... | collective-permute-start | bytes 1966088 | tf_op jit(solution)/shard_map/ppermute | solution.py:88
  451.1 23.6 %collective-permute-start.46 = (bf16[160,2048]{1,0:T(8,128)(2,1)}, bf16[160,2048]{1,0:T(8,128)(2,1)}, u32[]{:S(2)}, u32[]{:S(2)}) collective-permute-start(bf16[160,2048]{1,0:T(8,128)(2,1)} %get-tuple-element.455), channel_id=1, source_target_pairs={{0,2},{2,4},{4,6},{6,7},{7,5},{5,3},{3,1},{1,0},{8,10},{10,12},{12... | collective-permute-start | bytes 1966088 | tf_op jit(solution)/shard_map/ppermute | solution.py:88
  451.1 23.6 %collective-permute-start.47 = (bf16[160,2048]{1,0:T(8,128)(2,1)}, bf16[160,2048]{1,0:T(8,128)(2,1)}, u32[]{:S(2)}, u32[]{:S(2)}) collective-permute-start(bf16[160,2048]{1,0:T(8,128)(2,1)} %get-tuple-element.454), channel_id=1, source_target_pairs={{0,1},{2,0},{4,2},{6,4},{7,6},{5,7},{3,5},{1,3},{8,9},{10,8},{12,1... | collective-permute-start | bytes 1966088 | tf_op jit(solution)/shard_map/ppermute | solution.py:88
  453.1 21.6 %all-to-all-start.4 = ((bf16[8,160,256]{2,1,0:T(8,128)(2,1)}), bf16[8,160,256]{2,1,0:T(8,128)(2,1)S(1)}, u32[]{:S(2)}, u32[]{:S(2)}) async-start(bf16[8,160,256]{2,1,0:T(8,128)(2,1)} %bitcast.201), calls=%async_computation.4 | async-start | bytes 1310720 | tf_op jit(solution)/shard_map/all_to_all | solution.py:250
  457.7 191.5 %reduce-scatter.8.cloned.1.call-start = ((), (), s32[]{:S(2)}) async-start(), calls=%async_computation.13 | async-start | bytes 10485760 | tf_op jit(solution)/shard_map/reduce_scatter | solution.py:850
  486.5 27.0 %collective-permute-start.48 = (bf16[160,2048]{1,0:T(8,128)(2,1)S(1)}, bf16[160,2048]{1,0:T(8,128)(2,1)}, u32[]{:S(2)}, u32[]{:S(2)}) collective-permute-start(bf16[160,2048]{1,0:T(8,128)(2,1)S(1)} %get-tuple-element.320.refs_0_), channel_id=1, source_target_pairs={{0,2},{2,4},{4,6},{6,7},{7,5},{5,3},{3,1},{1,0},{8,10},{10,12},{12... | collective-permute-start | bytes 1966088 | tf_op jit(solution)/shard_map/ppermute | solution.py:88
  488.6 25.0 %collective-permute-start.49 = (bf16[160,2048]{1,0:T(8,128)(2,1)S(1)}, bf16[160,2048]{1,0:T(8,128)(2,1)}, u32[]{:S(2)}, u32[]{:S(2)}) collective-permute-start(bf16[160,2048]{1,0:T(8,128)(2,1)S(1)} %get-tuple-element.320.refs_0_), channel_id=1, source_target_pairs={{0,1},{2,0},{4,2},{6,4},{7,6},{5,7},{3,5},{1,3},{8,9},{10,8},{12,1... | collective-permute-start | bytes 1966088 | tf_op jit(solution)/shard_map/ppermute | solution.py:88
  530.8 17.2 %collective-permute-start.52 = (bf16[160,2048]{1,0:T(8,128)(2,1)}, bf16[160,2048]{1,0:T(8,128)(2,1)S(1)}, u32[]{:S(2)}, u32[]{:S(2)}) collective-permute-start(bf16[160,2048]{1,0:T(8,128)(2,1)} %collective-permute-done.50.refs_4_), channel_id=1, source_target_pairs={{0,2},{2,4},{4,6},{6,7},{7,5},{5,3},{3,1},{1,0},{8,10},{10,12},{12... | collective-permute-start | bytes 1966088 | tf_op jit(solution)/shard_map/ppermute | solution.py:88
  532.3 16.9 %collective-permute-start.53 = (bf16[160,2048]{1,0:T(8,128)(2,1)}, bf16[160,2048]{1,0:T(8,128)(2,1)S(1)}, u32[]{:S(2)}, u32[]{:S(2)}) collective-permute-start(bf16[160,2048]{1,0:T(8,128)(2,1)} %copy-done.62), channel_id=1, source_target_pairs={{0,1},{2,0},{4,2},{6,4},{7,6},{5,7},{3,5},{1,3},{8,9},{10,8},{12,1... | collective-permute-start | bytes 1966088 | tf_op jit(solution)/shard_map/ppermute | solution.py:88
  551.8 22.1 %collective-permute-start.57 = (bf16[80,2048]{1,0:T(8,128)(2,1)}, bf16[80,2048]{1,0:T(8,128)(2,1)}, u32[]{:S(2)}, u32[]{:S(2)}) collective-permute-start(bf16[80,2048]{1,0:T(8,128)(2,1)} %get-tuple-element.451), channel_id=1, source_target_pairs={{0,2},{2,4},{4,6},{6,7},{7,5},{5,3},{3,1},{1,0},{8,10},{10,12},{12... | collective-permute-start | bytes 983048 | tf_op jit(solution)/shard_map/ppermute | solution.py:88
  553.3 20.6 %collective-permute-start.58 = (bf16[80,2048]{1,0:T(8,128)(2,1)}, bf16[80,2048]{1,0:T(8,128)(2,1)}, u32[]{:S(2)}, u32[]{:S(2)}) collective-permute-start(bf16[80,2048]{1,0:T(8,128)(2,1)} %get-tuple-element.450), channel_id=1, source_target_pairs={{0,1},{2,0},{4,2},{6,4},{7,6},{5,7},{3,5},{1,3},{8,9},{10,8},{12,1... | collective-permute-start | bytes 983048 | tf_op jit(solution)/shard_map/ppermute | solution.py:88
  553.9 20.1 %collective-permute-start.55 = (bf16[80,2048]{1,0:T(8,128)(2,1)}, bf16[80,2048]{1,0:T(8,128)(2,1)}, u32[]{:S(2)}, u32[]{:S(2)}) collective-permute-start(bf16[80,2048]{1,0:T(8,128)(2,1)} %slice.389), channel_id=1, source_target_pairs={{0,2},{2,4},{4,6},{6,7},{7,5},{5,3},{3,1},{1,0},{8,10},{10,12},{12... | collective-permute-start | bytes 983048 | tf_op jit(solution)/shard_map/ppermute | solution.py:88
  555.4 18.6 %collective-permute-start.56 = (bf16[80,2048]{1,0:T(8,128)(2,1)}, bf16[80,2048]{1,0:T(8,128)(2,1)}, u32[]{:S(2)}, u32[]{:S(2)}) collective-permute-start(bf16[80,2048]{1,0:T(8,128)(2,1)} %slice.390), channel_id=1, source_target_pairs={{0,1},{2,0},{4,2},{6,4},{7,6},{5,7},{3,5},{1,3},{8,9},{10,8},{12,1... | collective-permute-start | bytes 983048 | tf_op jit(solution)/shard_map/ppermute | solution.py:88
  558.0 15.3 %all-to-all-start.5 = ((f32[8,1,4640]{2,1,0:T(1,128)}), f32[8,1,4640]{2,1,0:T(1,128)S(1)}, u32[]{:S(2)}, u32[]{:S(2)}) async-start(f32[8,1,4640]{2,1,0:T(1,128)} %copy.167), calls=%async_computation.6 | async-start | bytes 303104 | tf_op jit(solution)/shard_map/all_to_all | solution.py:250
  568.4 30.7 %collective-permute-start.61 = (bf16[8,1,64,768]{3,2,1,0:T(8,128)(2,1)}, bf16[8,1,64,768]{3,2,1,0:T(8,128)(2,1)S(1)}, u32[]{:S(2)}, u32[]{:S(2)}) collective-permute-start(bf16[8,1,64,768]{3,2,1,0:T(8,128)(2,1)} %constant_dynamic-slice_fusion.1), channel_id=1, source_target_pairs={{0,16},{8,24},{16,0},{24,8},{1,17},{9,25},{17,1},{25,9},{2,18},{10... | collective-permute-start | bytes 2359304 | tf_op jit(solution)/shard_map/ppermute | solution.py:204
  576.5 23.7 %collective-permute-start.60 = (bf16[160,2048]{1,0:T(8,128)(2,1)}, bf16[160,2048]{1,0:T(8,128)(2,1)}, u32[]{:S(2)}, u32[]{:S(2)}) collective-permute-start(bf16[160,2048]{1,0:T(8,128)(2,1)} %pad_maximum_fusion.11), channel_id=1, source_target_pairs={{0,1},{2,0},{4,2},{6,4},{7,6},{5,7},{3,5},{1,3},{8,9},{10,8},{12,1... | collective-permute-start | bytes 1966088 | tf_op jit(solution)/shard_map/ppermute | solution.py:88
  578.8 21.4 %collective-permute-start.59 = (bf16[160,2048]{1,0:T(8,128)(2,1)}, bf16[160,2048]{1,0:T(8,128)(2,1)}, u32[]{:S(2)}, u32[]{:S(2)}) collective-permute-start(bf16[160,2048]{1,0:T(8,128)(2,1)} %pad_maximum_fusion.10), channel_id=1, source_target_pairs={{0,2},{2,4},{4,6},{6,7},{7,5},{5,3},{3,1},{1,0},{8,10},{10,12},{12... | collective-permute-start | bytes 1966088 | tf_op jit(solution)/shard_map/ppermute | solution.py:88
  604.7 36.1 %all-to-all-start.6 = ((bf16[8,64,768]{2,1,0:T(8,128)(2,1)}), bf16[8,64,768]{2,1,0:T(8,128)(2,1)}, u32[]{:S(2)}, u32[]{:S(2)}) async-start(bf16[8,64,768]{2,1,0:T(8,128)(2,1)} %bitcast.195), calls=%async_computation.7 | async-start | bytes 1572864 | tf_op jit(solution)/shard_map/all_to_all | solution.py:250
  615.1 24.2 %collective-permute-start.62 = (bf16[160,2048]{1,0:T(8,128)(2,1)S(1)}, bf16[160,2048]{1,0:T(8,128)(2,1)S(1)}, u32[]{:S(2)}, u32[]{:S(2)}) collective-permute-start(bf16[160,2048]{1,0:T(8,128)(2,1)S(1)} %copy-done.64), channel_id=1, source_target_pairs={{0,2},{2,4},{4,6},{6,7},{7,5},{5,3},{3,1},{1,0},{8,10},{10,12},{12... | collective-permute-start | bytes 1966088 | tf_op jit(solution)/shard_map/ppermute | solution.py:88
  616.9 23.9 %collective-permute-start.63 = (bf16[160,2048]{1,0:T(8,128)(2,1)S(1)}, bf16[160,2048]{1,0:T(8,128)(2,1)S(1)}, u32[]{:S(2)}, u32[]{:S(2)}) collective-permute-start(bf16[160,2048]{1,0:T(8,128)(2,1)S(1)} %copy-done.63), channel_id=1, source_target_pairs={{0,1},{2,0},{4,2},{6,4},{7,6},{5,7},{3,5},{1,3},{8,9},{10,8},{12,1... | collective-permute-start | bytes 1966088 | tf_op jit(solution)/shard_map/ppermute | solution.py:88
  643.6 16.2 %collective-permute-start.70 = (bf16[1,64,2048]{2,1,0:T(8,128)(2,1)S(1)}, bf16[1,64,2048]{2,1,0:T(8,128)(2,1)}, u32[]{:S(2)}, u32[]{:S(2)}) collective-permute-start(bf16[1,64,2048]{2,1,0:T(8,128)(2,1)S(1)} %constant_dynamic-slice_fusion), channel_id=1, source_target_pairs={{0,16},{8,24},{16,0},{24,8},{1,17},{9,25},{17,1},{25,9},{2,18},{10... | collective-permute-start | bytes 786440 | tf_op jit(solution)/shard_map/ppermute | solution.py:204
  648.5 20.3 %collective-permute-start.69 = (bf16[1,3,64,2048]{3,2,1,0:T(8,128)(2,1)S(1)}, bf16[1,3,64,2048]{3,2,1,0:T(8,128)(2,1)}, u32[]{:S(2)}, u32[]{:S(2)}) collective-permute-start(bf16[1,3,64,2048]{3,2,1,0:T(8,128)(2,1)S(1)} %stack.169), channel_id=1, source_target_pairs={{0,16},{8,24},{16,0},{24,8},{1,17},{9,25},{17,1},{25,9},{2,18},{10... | collective-permute-start | bytes 2359304 | tf_op jit(solution)/shard_map/ppermute | solution.py:204
  653.3 19.0 %collective-permute-start.67 = (bf16[160,2048]{1,0:T(8,128)(2,1)}, bf16[160,2048]{1,0:T(8,128)(2,1)S(1)}, u32[]{:S(2)}, u32[]{:S(2)}) collective-permute-start(bf16[160,2048]{1,0:T(8,128)(2,1)} %get-tuple-element.445), channel_id=1, source_target_pairs={{0,2},{2,4},{4,6},{6,7},{7,5},{5,3},{3,1},{1,0},{8,10},{10,12},{12... | collective-permute-start | bytes 1966088 | tf_op jit(solution)/shard_map/ppermute | solution.py:88
  659.0 15.4 %collective-permute-start.68 = (bf16[160,2048]{1,0:T(8,128)(2,1)}, bf16[160,2048]{1,0:T(8,128)(2,1)S(1)}, u32[]{:S(2)}, u32[]{:S(2)}) collective-permute-start(bf16[160,2048]{1,0:T(8,128)(2,1)} %get-tuple-element.444), channel_id=1, source_target_pairs={{0,1},{2,0},{4,2},{6,4},{7,6},{5,7},{3,5},{1,3},{8,9},{10,8},{12,1... | collective-permute-start | bytes 1966088 | tf_op jit(solution)/shard_map/ppermute | solution.py:88
  (164 other events, 1399.7 us)
Sparse Core Ops, SparseCore 0:
  39.2 62.9 all-gather.1
  400.5 72.9 reduce-scatter.3
  476.2 71.7 reduce-scatter.5
  550.4 82.2 reduce-scatter.7

commit v10 on v9

--- a/solution.py
+++ b/solution.py
@@ -347,10 +347,24 @@
 
 
 def attention_back_kernel(
-    block, scale, order_ref, query_ref, key_ref, value_ref, swapped_ref, total_ref, column_ref, line_ref,
-    query_raw_ref, key_raw_ref, gains_ref, cosine_ref, sine_ref, sent_ref, part_ref, key_sum, value_sum, grad_ref
+    block,
+    scale,
+    order_ref,
+    query_ref,
+    key_ref,
+    value_ref,
+    swapped_ref,
+    total_ref,
+    column_ref,
+    line_ref,
+    query_raw_ref,
+    key_raw_ref,
+    gains_ref,
+    cosine_ref,
+    sine_ref,
+    *refs,
 ):
-    head, heads = pl.program_id(0), pl.num_programs(0)
+    sent_ref, part_ref, key_sum, value_sum, grad_ref = refs[-5:]
     rows, depth = query_ref.shape
     lane = lax.broadcasted_iota(jnp.int32, (1, depth), 1)
     sign = jnp.where(lane < depth // 2, 1.0, -1.0)
@@ -359,16 +373,14 @@
         grad_ref[slot * share : (slot + 1) * share, :] = swapped_ref[order_ref[slot]]
     key_sum[...] = jnp.zeros_like(key_sum)
     value_sum[...] = jnp.zeros_like(value_sum)
-
-    @pl.when(head == 0)
-    def _():
-        part_ref[...] = jnp.zeros_like(part_ref)
-
-    def finish(back, raw, gain, cosine, sine, row, column, which):
-        turned = back * cosine + pltpu.roll(back * sine, depth // 2, axis=1) * sign
-        inverse = lax.rsqrt(jnp.mean(raw * raw, axis=-1, keepdims=True) + 1e-5)
-        result, part = norm_backward(raw, inverse, gain, turned)
-        sent_ref[row, pl.ds(pl.multiple_of(column * depth, depth), depth)] = result.astype(low_type)
+    part_ref[...] = jnp.zeros_like(part_ref)
+
+    def finish(back, raw, row, which):
+        turned = back * cosine_ref[row, :]
+        turned += pltpu.roll(back * sine_ref[row, :], depth // 2, axis=1) * sign
+        inverse = inverse_rms(raw)
+        result, part = norm_backward(raw, inverse, gains_ref[which : which + 1, :], turned)
+        sent_ref[row, which * depth : (which + 1) * depth] = result.astype(low_type)
         part_ref[which : which + 1, :] += jnp.sum(part, axis=0, keepdims=True)
 
     @pl.loop(0, rows // block)
@@ -377,71 +389,60 @@
         query, grad = query_ref[row, :], grad_ref[row, :]
         scores = mm(query, key_ref[...], 1, 1) * scale
         scores = jnp.where(column_ref[row, :] == line_ref[...], scores, masked_value)
-        weights = jnp.exp(scores - total_ref[row, pl.ds(0, 1)])
+        weights = jnp.exp(scores - total_ref[row, :])
         weight_grad = mm(grad, value_ref[...], 1, 1)
         row_dot = jnp.sum(weights * weight_grad, axis=-1, keepdims=True)
         score_grad = (weights * (weight_grad - row_dot)).astype(low_type)
         key_sum[...] += mm(score_grad, query, 0, 0)
         value_sum[...] += mm(weights.astype(low_type), grad, 0, 0)
-        query_back = mm(score_grad, key_ref[...], 1, 0) * scale
-        finish(query_back, query_raw_ref[row, :], gains_ref[0:1, :], cosine_ref[row, :], sine_ref[row, :], row, head, 0)
+        finish(mm(score_grad, key_ref[...], 1, 0) * scale, query_raw_ref[row, :], row, 0)
 
     @pl.loop(0, rows // block)
     def _(step):
         row = pl.ds(pl.multiple_of(step * block, block), block)
-        finish(key_sum[row, :] * scale, key_raw_ref[row, :], gains_ref[1:2, :], cosine_ref[row, :], sine_ref[row, :], row, heads + head, 1)
-        sent_ref[row, pl.ds(pl.multiple_of((2 * heads + head) * depth, depth), depth)] = value_sum[row, :].astype(low_type)
-
-
-def attention_back(lows, swapped, order, totals, segment, raw, gains, cosine, sine, block=256):
-    rows, depth = cosine.shape
-    heads = lows.shape[1] // (3 * depth)
-    block = block if rows % block == 0 else rows
-
-    def by_head(start):
-        return pl.BlockSpec((rows, depth), lambda h, order: (0, start * heads + h))
+        finish(key_sum[row, :] * scale, key_raw_ref[row, :], row, 1)
+        sent_ref[row, 2 * depth : 3 * depth] = value_sum[row, :].astype(low_type)
+
+
+def attention_back(head, kept, swapped, order, column, line, raw, gains, tables, earlier=()):
+    rows, depth = kept[0].shape
+    block = 256 if rows % 256 == 0 else rows
 
     def whole(array):
-        return pl.BlockSpec(array.shape, lambda h, order: (0, 0))
-
-    column, line = segment[:, None], segment[None, :]
+        return pl.BlockSpec(array.shape, lambda i, order: (0,) * array.ndim)
+
+    def columns(index):
+        return pl.BlockSpec((rows, depth), lambda i, order: (0, index))
+
+    operands = (*kept[:3], swapped, kept[3], column, line, raw, raw, gains, *tables)
+    specs = [whole(operand) for operand in operands]
+    specs[3] = pl.BlockSpec(swapped.shape[:2] + (depth,), lambda i, order: (0, 0, head))
+    specs[7], specs[8] = columns(3 * head), columns(3 * head + 1)
     return pl.pallas_call(
         functools.partial(attention_back_kernel, block, depth**-0.5),
         grid_spec=pltpu.PrefetchScalarGridSpec(
             num_scalar_prefetch=1,
-            grid=(heads,),
-            in_specs=[
-                by_head(0),
-                by_head(1),
-                by_head(2),
-                pl.BlockSpec(swapped.shape[:2] + (depth,), lambda h, order: (0, 0, h)),
-                pl.BlockSpec((None, rows, 1), lambda h, order: (h, 0, 0)),
-                whole(column),
-                whole(line),
-                by_head(0),
-                by_head(1),
-                whole(gains),
-                whole(cosine),
-                whole(sine),
-            ],
+            grid=(1,),
+            in_specs=specs + [pl.BlockSpec(memory_space=pl.ANY)] * len(earlier),
             out_specs=[
-                pl.BlockSpec((rows, lows.shape[1]), lambda h, order: (0, 0)),
-                pl.BlockSpec((2, depth), lambda h, order: (0, 0)),
+                pl.BlockSpec((rows, 3 * depth), lambda i, order: (0, head)),
+                pl.BlockSpec((2, depth), lambda i, order: (0, 0)),
             ],
             scratch_shapes=[pltpu.VMEM((rows, depth), wide_type)] * 2
             + [pltpu.VMEM((rows, depth), low_type)],
         ),
         out_shape=[
-            jax.ShapeDtypeStruct(lows.shape, low_type),
+            jax.ShapeDtypeStruct(raw.shape, low_type),
             jax.ShapeDtypeStruct((2, depth), wide_type),
         ],
+        input_output_aliases={1 + len(operands) + i: i for i in range(len(earlier))},
         compiler_params=pltpu.CompilerParams(vmem_limit_bytes=56 << 20),
         cost_estimate=pl.CostEstimate(
-            flops=10 * rows * rows * heads * depth,
-            bytes_accessed=30 * rows * heads * depth,
-            transcendentals=heads * rows * rows,
+            flops=10 * rows * rows * depth,
+            bytes_accessed=30 * rows * depth,
+            transcendentals=rows * rows,
         ),
-    )(order, lows, lows, lows, swapped, totals, column, line, raw, raw, gains, cosine, sine)
+    )(order, *operands, *earlier)
 
 
 def block_product_kernel(left_ref, *refs):
@@ -526,15 +527,19 @@
         route_code = route_code + jnp.where(hit, 1 + kept, 0)
     small_sent = jnp.concatenate([route_code.astype(low_type), router_weight], axis=0)
 
-    projections = jnp.concatenate(
-        [
-            lax.dynamic_slice_in_dim(piece, replica * share, share, 0).reshape(
-                share, group_count, width_here
-            )
-            for piece in (query_weight, key_weight, value_weight)
-        ],
-        axis=2,
-    ).transpose(1, 0, 2)
+    projections = (
+        jnp.stack(
+            [
+                lax.dynamic_slice_in_dim(piece, replica * share, share, 0).reshape(
+                    share, group_count, heads_here, head_dim
+                )
+                for piece in (query_weight, key_weight, value_weight)
+            ],
+            axis=3,
+        )
+        .reshape(share, group_count, 3 * width_here)
+        .transpose(1, 0, 2)
+    )
     scatter_order = rep_distances()
     gather_order = scatter_order[::-1]
     swapped = swap_all(projections)
@@ -543,7 +548,10 @@
         .transpose(1, 0, 2, 3)
         .reshape(model_width, 3 * width_here)
     )
-    small_flat = after(small_sent.reshape(-1, head_dim), swapped)
+    tokens_late, output_late, _ = tie(tokens, output_weight, swapped)
+    token_ring = RingGather(tokens_late)
+    token_ring.start()
+    small_flat = after(small_sent.reshape(-1, head_dim), token_ring.received)
     small_all = swap_all(
         jnp.broadcast_to(small_flat[None], (group_count,) + small_flat.shape)
     ).reshape(group_count, row_count + width_here, expert_total)
@@ -566,18 +574,17 @@
             rows.reshape(group_count, row_count, rows.shape[1]), index
         ).reshape(rows.shape)
 
-    tokens_late, output_late, _ = tie(tokens, output_weight, swapped)
     column_share = model_width // replica_count
     output_share = gather_rows(
         lax.dynamic_slice_in_dim(output_late, replica * column_share, column_share, 1)
     )
-    token_ring = RingGather(tokens_late)
-    for step in range(group_count // 2):
+    token_ring.finish()
+    for step in range(1, group_count // 2):
         if step == group_count // 2 - 1:
             token_ring.sent = (after(token_ring.sent[0], output_share), token_ring.sent[1])
         token_ring.start()
         token_ring.finish()
-    cosine, sine_part = rope_tables(position, head_dim)
+    cosine, sine_part = rope_tables(after(position, token_ring.blocks[1]), head_dim)
 
     hidden_here = down_weight.shape[1]
     flat_down = down_weight.reshape(experts_here * hidden_here, model_width)
@@ -591,7 +598,7 @@
     ]
 
     def head_columns(values, block, head):
-        start = block * width_here + head * head_dim
+        start = (3 * head + block) * head_dim
         return values[:, start : start + head_dim]
 
     def project(weight, *blocks):
@@ -630,14 +637,19 @@
 
     def order_work(*mixed):
         mixed_low = jnp.concatenate(mixed, axis=1)
-        return mixed_low, reorder_rows(mixed_low, slot_of_device)
-
-    mixed_low, mixed_ordered = window(
+        return (
+            mixed_low,
+            reorder_rows(mixed_low, slot_of_device),
+            segment[:, None],
+            segment[None, :],
+            jnp.stack([querynorm_gain, keynorm_gain]),
+            jnp.stack(device_of_slot),
+        )
+
+    mixed_low, mixed_ordered, segment_column, segment_line, norm_gains, slot_order = window(
         [cot_ring, *far_parts[1 + heads_here :]], order_work, *[head[4] for head in heads]
     )
     cot_all = jnp.concatenate(cot_ring.blocks, axis=0)
-    lows = jnp.concatenate([head[part] for part in range(3) for head in heads], axis=1)
-    log_totals = jnp.stack([head[3] for head in heads])
     output_pieces = {
         0: output_share,
         far: jnp.concatenate([part.received for part in far_parts], axis=0),
@@ -778,31 +790,38 @@
             self.received = swap_all(self.sent)
 
     swap = Swap(swap_sent, 0)
+    attention_gather = RingGather(attention_low)
     up_part = window(
-        [mixture_ring, swap], lambda uback: grad_of(second_all, uback), uback_all
+        [mixture_ring, swap, attention_gather],
+        lambda uback: grad_of(second_all, uback),
+        uback_all,
     )
     mixture = mixture_ring.total()
     layer_out = (valid_own * (residual + mixture)).astype(low_type)
     mixed_grad = swap.received
 
-    attention_gather = RingGather(attention_low)
-    sent, gain_parts = window(
-        [attention_gather],
-        lambda grads: tuple(
-            attention_back(
-                lows,
-                grads,
-                jnp.stack(device_of_slot),
-                log_totals,
-                segment,
-                raw,
-                jnp.stack([querynorm_gain, keynorm_gain]),
-                cosine,
-                sine_part,
+    sent, gain_parts = (), 0.0
+    for head in range(heads_here):
+
+        def head_work(grads, *earlier, head=head):
+            return tuple(
+                attention_back(
+                    head,
+                    heads[head][:4],
+                    grads,
+                    slot_order,
+                    segment_column,
+                    segment_line,
+                    raw,
+                    norm_gains,
+                    (cosine, sine_part),
+                    earlier,
+                )
             )
-        ),
-        mixed_grad,
-    )
+
+        *sent, gain_part = window([attention_gather], head_work, mixed_grad, *sent)
+        gain_parts = gain_parts + gain_part
+    (sent,) = sent
     querynorm_part, keynorm_part = gain_parts[0], gain_parts[1]
     down_sum = lax.psum_scatter(
         down_part.reshape(experts_here, hidden_here, model_width),
@@ -819,8 +838,10 @@
         return first_part.astype(low_type), prenorm_part, rep_scatter(head, 1, scatter_order[:1])
 
     head_part = window([attention_gather], grad_of, first_all, sent)
+    while attention_gather.step < group_count // 2:
+        window([attention_gather], lambda: ())
     first_low, prenorm_part, head_part = window(
-        [attention_gather],
+        [],
         first_work,
         sent,
         head_part.reshape(group_count, replica_count, share, 3 * width_here),
@@ -843,52 +864,52 @@
     first_ring = RingSum(slot_rows(first_low), row_count)
     small_parts = [router_part, postnorm_part, prenorm_part, querynorm_part, keynorm_part]
     head_part = rep_scatter(head_part, 1, scatter_order[1:])
-    small_swapped = window(
-        [attention_gather, first_ring], lambda *small: small_swap(small), *small_parts
-    )
-    gate_sum = lax.psum_scatter(gate_part, "rep", scatter_dimension=0, tiled=True)
-    up_sum = lax.psum_scatter(up_part, "rep", scatter_dimension=0, tiled=True)
-    output_part, head_part = window(
+    output_part = window(
         [first_ring],
         lambda mixed, *blocks: block_product(mixed, blocks),
         mixed_low,
         *attention_gather.blocks,
+    )
+    gate_sum = lax.psum_scatter(gate_part, "rep", scatter_dimension=0, tiled=True)
+    up_sum = lax.psum_scatter(up_part, "rep", scatter_dimension=0, tiled=True)
+    (small_swapped, output_part), head_part = window(
+        [first_ring],
+        lambda output, *small: (small_swap(small), rep_scatter(output, 0, scatter_order[:1])),
+        output_part.reshape(replica_count, share, model_width),
+        *small_parts,
         waits=(head_part,),
     )
     head_rows = swap_all(head_part.reshape(group_count, share, 3 * width_here))
     (output_part, small_sums), head_rows = window(
         [first_ring],
         lambda output, small: (
-            rep_scatter(output, 0, scatter_order[:1]),
+            rep_scatter(output, 0, scatter_order[1:]),
             small_pieces(small, small_parts),
         ),
-        output_part.reshape(replica_count, share, model_width),
+        output_part,
         small_swapped,
         waits=(head_rows,),
     )
     head_rows = rep_gather(
-        head_rows.reshape(group_count, share, 3, width_here)
-        .transpose(2, 1, 0, 3)
+        head_rows.reshape(group_count, share, heads_here, 3, head_dim)
+        .transpose(3, 1, 0, 2, 4)
         .reshape(1, 3, share, model_width),
         gather_order[:-1],
     )
-    output_part, head_rows = window(
+    output_rows, head_rows = window(
         [first_ring],
-        lambda output: rep_scatter(output, 0, scatter_order[1:]),
+        lambda output: rep_gather(output, gather_order[:-1]),
         output_part,
         waits=(head_rows,),
     )
     head_rows = rep_gather(head_rows, gather_order[-1:])
+    output_rows = rep_gather(output_rows, gather_order[-1:])
     first_grad = first_ring.total()
-    output_grad = (
-        rep_gather(output_part, gather_order)
-        .reshape(width_here, model_width)
-        .astype(wide_type)
-    )
     query_grad, key_grad, value_grad = (
         head_rows[:, block].reshape(width_here, model_width).astype(wide_type)
         for block in range(3)
     )
+    output_grad = output_rows.reshape(width_here, model_width).astype(wide_type)
     router_grad, postnorm_grad, prenorm_grad, querynorm_grad, keynorm_grad = small_sums
     router_grad = router_grad.reshape(width_here, expert_total)
 

time: 707 us -> 697 us (0.986)
  waiting for transfers between devices: 158 us -> 146 us
  local copies, waits for them, and re-layouts: 87 us -> 79.2 us
    ppermute x56, waiting for transfers between devices: 103 us -> 82.4 us  [ring_shift(): return lax.ppermute(values, 'ep', pairs)]
    all_to_all x7, waiting for transfers between devices: 31.9 us -> 42.3 us  [swap_all(): return lax.all_to_all(values, 'ep', split_axis=0, concat_axis=0, tiled=True)]
    unnamed x334 -> x316, local copies, waits for them, and re-layouts: 35.9 us -> 30.6 us
    pallas_call x1 -> x2, Pallas kernels: 23.8 us -> 27.2 us  [attention_back(): pl.pallas_call(functools.partial(attention_back_kernel, block, depth ** (...]
  transfers between devices with their start and end apart: 85 -> 85, of which waited for: 32 -> 28; matrix products, arithmetic and copies ran while one was open for 39% -> 38% of each run, Pallas kernels for 10% -> 10%
where the time goes in v10:
time: 697 us; the launch traced here: 687 us
  waiting for transfers between devices  146 us (21%)
  matrix products  128 us (18%)
  starting transfers between devices  118 us (17%)
  Pallas kernels  107 us (15%)
  other arithmetic  90 us (13%)
  local copies, waits for them, and re-layouts  79.2 us (11%)
  between operations  17.2 us (2%)
    dot_general x26, matrix products, mm(): lax.dot_general(left, right, (((left_dim,), (right_dim,)), ((), ())), pre...  128 us
    ppermute x56, waiting for transfers between devices, ring_shift(): return lax.ppermute(values, 'ep', pairs)  82.4 us
    ppermute x56, starting transfers between devices, ring_shift(): return lax.ppermute(values, 'ep', pairs)  68.7 us
    all_to_all x7, waiting for transfers between devices, swap_all(): return lax.all_to_all(values, 'ep', split_axis=0, concat_axis=0, tiled=True)  42.3 us
    pallas_call x2, Pallas kernels, expert_pass(): pl.pallas_call(expert_kernel, grid=(experts, steps), in_specs=[pl.BlockSp...  38.9 us
    all_to_all x7, starting transfers between devices, swap_all(): return lax.all_to_all(values, 'ep', split_axis=0, concat_axis=0, tiled=True)  34.2 us
    pallas_call x2, Pallas kernels, expert_back(): pl.pallas_call(expert_back_kernel, grid=(depth // width,), in_specs=[whol...  33.7 us
    unnamed x316, local copies, waits for them, and re-layouts  30.6 us
  transfers between devices with their start and end apart: 85, of which 28 were waited for; matrix products, arithmetic and copies ran while one was open for 38% of the time, Pallas kernels for 10%

profile of v10, /device:TPU:0, one launch (start us, length us, event | category | flops | bytes accessed | tf_op | source)
XLA Modules:
  0.0 686.6 jit_solution(18184008059226812627)
XLA Ops:
  11.5 7.3 %all-to-all-start = ((bf16[8,64,768]{2,1,0:T(8,128)(2,1)}), bf16[8,64,768]{2,1,0:T(8,128)(2,1)S(1)}, u32[]{:S(2)}, u32[]{:S(2)}) async-start(bf16[8,64,768]{2,1,0:T(8,128)(2,1)} %copy.138), calls=%async_computation | async-start | bytes 1572864 | tf_op jit(solution)/shard_map/all_to_all | solution.py:250
  19.9 19.0 %all-to-all-done = bf16[8,64,768]{2,1,0:T(8,128)(2,1)S(1)} async-done(((bf16[8,64,768]{2,1,0:T(8,128)(2,1)}), bf16[8,64,768]{2,1,0:T(8,128)(2,1)S(1)}, u32[]{:S(2)}, u32[]{:S(2)}) %all-to-all-start) | async-done | bytes 786464 | tf_op jit(solution)/shard_map/all_to_all | solution.py:250
  47.3 9.7 %collective-permute-done.4 = bf16[160,2048]{1,0:T(8,128)(2,1)} collective-permute-done((bf16[160,2048]{1,0:T(8,128)(2,1)S(1)}, bf16[160,2048]{1,0:T(8,128)(2,1)}, u32[]{:S(2)}, u32[]{:S(2)}) %collective-permute-start.4) | collective-permute-done | bytes 655392 | tf_op jit(solution)/shard_map/ppermute | solution.py:88
  59.9 4.1 all-to-all-start.2
  66.0 3.7 multiply_cosine_fusion
  79.3 10.4 %collective-permute-done.1 = bf16[160,2048]{1,0:T(8,128)(2,1)} collective-permute-done((bf16[160,2048]{1,0:T(8,128)(2,1)}, bf16[160,2048]{1,0:T(8,128)(2,1)}, u32[]{:S(2)}, u32[]{:S(2)}) %collective-permute-start.1) | collective-permute-done | bytes 655392 | tf_op jit(solution)/shard_map/ppermute | solution.py:88
  89.7 8.3 %collective-permute-start.2 = (bf16[160,2048]{1,0:T(8,128)(2,1)}, bf16[160,2048]{1,0:T(8,128)(2,1)S(1)}, u32[]{:S(2)}, u32[]{:S(2)}) collective-permute-start(bf16[160,2048]{1,0:T(8,128)(2,1)} %collective-permute-done.1), channel_id=1, source_target_pairs={{0,2},{2,4},{4,6},{6,7},{7,5},{5,3},{3,1},{1,0},{8,10},{10,12},{12... | collective-permute-start | bytes 1966088 | tf_op jit(solution)/shard_map/ppermute | solution.py:88
  98.0 2.5 collective-permute-done.5
  102.9 10.8 %collective-permute-done.6 = bf16[160,2048]{1,0:T(8,128)(2,1)S(1)} collective-permute-done((bf16[160,2048]{1,0:T(8,128)(2,1)}, bf16[160,2048]{1,0:T(8,128)(2,1)S(1)}, u32[]{:S(2)}, u32[]{:S(2)}) %collective-permute-start.6) | collective-permute-done | bytes 655392 | tf_op jit(solution)/shard_map/ppermute | solution.py:88
  116.8 2.3 maximum_select_fusion
  136.9 4.3 fusion.75.query_raw_ref.key_raw_ref
  156.1 2.2 collective-permute-start.16
  168.4 5.0 collective-permute-done.16
  178.8 6.1 collective-permute-done.19
  186.0 4.4 all-to-all-start.1
  192.4 2.3 constant_dynamic-update-slice_fusion.44
  194.7 2.3 constant_dynamic-update-slice_fusion.43
  200.0 6.5 all-to-all-done.1
  210.7 2.2 convolution_dynamic-update-slice_fusion.1
  218.9 7.3 %fusion.76.stream_ref = f32[640,2048]{1,0:T(8,128)} fusion(bf16[640,2048]{1,0:T(8,128)(2,1)S(1)} %copy-done.33, bf16[2048,2048]{1,0:T(8,128)(2,1)S(1)} %bitcast.276), kind=kOutput, calls=%fused_computation.332 | convolution fusion | flops 5368709120 | bytes 16252928 | tf_op jit(solution)/shard_map/dot_general | solution.py:60
  227.3 4.2 collective-permute-done.24
  233.5 8.9 %fusion.77.stream_ref = f32[640,2048]{1,0:T(8,128)} fusion(bf16[640,2048]{1,0:T(8,128)(2,1)} %get-tuple-element.233, bf16[2048,2048]{1,0:T(8,128)(2,1)S(1)} %bitcast.277), kind=kOutput, calls=%fused_computation.333 | convolution fusion | flops 5368709120 | bytes 16252928 | tf_op jit(solution)/shard_map/dot_general | solution.py:60
  242.5 2.7 collective-permute-done.26
  253.3 19.4 %shard_map.281 = (bf16[1280,2048]{1,0:T(8,128)(2,1)}, bf16[1280,2048]{1,0:T(8,128)(2,1)}, bf16[1280,2048]{1,0:T(8,128)(2,1)}, f32[2,640,128]{2,1,0:T(8,128)}) custom-call(bf16[640,2048]{1,0:T(8,128)(2,1)} %copy-done.34, bf16[2,2048,1024]{2,1,0:T(8,128)(2,1)} %gate_ref.7, bf16[2,2048,1024]{2,1,0:T(8,128)(2,1)} %up_ref.7, f32[640,2048]{1,0:T(8,128)} %fusion.76.stream_ref, ...), custom_call_target="tpu_custom_call" | custom-call | flops 10737418240 | bytes 42991616 | tf_op jit(solution)/shard_map/pallas_call | solution.py:294
  277.3 2.7 collective-permute-done.30
  286.6 19.4 %shard_map.282 = (bf16[1280,2048]{1,0:T(8,128)(2,1)}, bf16[1280,2048]{1,0:T(8,128)(2,1)}, bf16[1280,2048]{1,0:T(8,128)(2,1)}, f32[2,640,128]{2,1,0:T(8,128)}) custom-call(bf16[640,2048]{1,0:T(8,128)(2,1)} %copy-done.28, bf16[2,2048,1024]{2,1,0:T(8,128)(2,1)} %gate_ref.7, ...), custom_call_target="tpu_custom_call", output_to_operand_aliasing={{0}: (5, {}), {1}: (6, {}), {2}: (7, {})} | custom-call | flops 10737418240 | bytes 42991616 | tf_op jit(solution)/shard_map/pallas_call | solution.py:294
  306.0 16.8 %shard_map.283 = bf16[640,2048]{1,0:T(8,128)(2,1)} custom-call(bf16[1280,2048]{1,0:T(8,128)(2,1)} %get-tuple-element.274.gback_ref, bf16[1280,2048]{1,0:T(8,128)(2,1)} %get-tuple-element.285.uback_ref, bf16[2,2048,1024]{2,1,0:T(8,128)(2,1)} %gate_ref.7, bf16[2,2048,1024]{2,1,0:T(8,128)(2,1)} %up_ref.7), custom_call_target="tpu_custom_call" | custom-call | flops 10737418240 | bytes 24641536 | tf_op jit(solution)/shard_map/pallas_call | solution.py:334
  327.8 16.9 %shard_map.284 = bf16[640,2048]{1,0:T(8,128)(2,1)} custom-call(bf16[1280,2048]{1,0:T(8,128)(2,1)} %get-tuple-element.274.gback_ref, bf16[1280,2048]{1,0:T(8,128)(2,1)} %get-tuple-element.285.uback_ref, bf16[2,2048,1024]{2,1,0:T(8,128)(2,1)} %gate_ref.7, bf16[2,2048,1024]{2,1,0:T(8,128)(2,1)} %up_ref.7), custom_call_target="tpu_custom_call" | custom-call | flops 10737418240 | bytes 24641536 | tf_op jit(solution)/shard_map/pallas_call | solution.py:334
  350.5 3.3 all-to-all-start.3
  353.8 16.6 %convolution_convert_fusion.3 = bf16[1280,2048]{1,0:T(8,128)(2,1)} fusion(bf16[1280,2048]{1,0:T(8,128)(2,1)} %get-tuple-element.268, bf16[2048,2048]{1,0:T(8,128)(2,1)} %bitcast.273), kind=kOutput, calls=%fused_computation.17 | convolution fusion | flops 10740039680 | bytes 18874368 | tf_op jit(solution)/shard_map/dot_general | solution.py:60
  374.1 2.3 collective-permute-start.37
  380.1 16.7 %convolution_convert_fusion.2 = bf16[2048,2048]{1,0:T(8,128)(2,1)} fusion(bf16[1280,2048]{1,0:T(8,128)(2,1)} %get-tuple-element.268, bf16[1280,2048]{1,0:T(8,128)(2,1)} %get-tuple-element.545), kind=kOutput, calls=%fused_computation.16 | convolution fusion | flops 10741612544 | bytes 18874368 | tf_op jit(solution)/shard_map/dot_general | solution.py:60
  405.3 2.8 add_convert_fusion.9
  410.3 18.2 %convolution_convert_fusion.1 = bf16[2048,2048]{1,0:T(8,128)(2,1)} fusion(bf16[1280,2048]{1,0:T(8,128)(2,1)} %get-tuple-element.541, bf16[1280,2048]{1,0:T(8,128)(2,1)} %get-tuple-element.274.gback_ref), kind=kOutput, calls=%fused_computation.15 | convolution fusion | flops 10741612544 | bytes 18874368 | tf_op jit(solution)/shard_map/dot_general | solution.py:60
  440.7 2.4 convolution_add_fusion.1
  443.2 2.4 fusion.31
  445.6 2.4 fusion.14
  450.9 2.8 add_convert_fusion.5
  455.8 5.5 all-to-all-start.4
  461.5 16.7 %convolution_convert_fusion = bf16[2048,2048]{1,0:T(8,128)(2,1)} fusion(bf16[1280,2048]{1,0:T(8,128)(2,1)} %get-tuple-element.541, bf16[1280,2048]{1,0:T(8,128)(2,1)} %get-tuple-element.285.uback_ref), kind=kOutput, calls=%fused_computation.14 | convolution fusion | flops 10741612544 | bytes 18874368 | tf_op jit(solution)/shard_map/dot_general | solution.py:60
  478.4 13.9 %all-to-all-done.4.swapped_ref = bf16[8,160,256]{2,1,0:T(8,128)(2,1)S(1)} async-done(((bf16[8,160,256]{2,1,0:T(8,128)(2,1)}), bf16[8,160,256]{2,1,0:T(8,128)(2,1)S(1)}, u32[]{:S(2)}, u32[]{:S(2)}) %all-to-all-start.4) | async-done | bytes 655392 | tf_op jit(solution)/shard_map/all_to_all | solution.py:250
  497.3 13.8 %shard_map.285 = (bf16[1280,768]{1,0:T(8,128)(2,1)}, f32[2,128]{1,0:T(2,128)}) custom-call(s32[8]{0:T(128)} %stack.156.order_ref, bf16[1280,128]{1,0:T(8,128)(2,1)} %copy-done.50, bf16[1280,128]{1,0:T(8,128)(2,1)} %copy-done.49, bf16[1280,128]{1,0:T(8,128)(2,1)} %slice.506.value_ref, bf16[8,160,256]{2,1,0:T(8,128)(2,1)} %copy-done.12, ...), custom_call_target="tpu_custom_call" | custom-call | flops 2097152000 | bytes 4915200 | tf_op jit(solution)/shard_map/pallas_call | solution.py:421
  516.3 13.3 %shard_map.286 = (bf16[1280,768]{1,0:T(8,128)(2,1)}, f32[2,128]{1,0:T(2,128)}) custom-call(s32[8]{0:T(128)} %stack.156.order_ref, bf16[1280,128]{1,0:T(8,128)(2,1)} %copy-done.48, bf16[1280,128]{1,0:T(8,128)(2,1)} %copy-done.47, bf16[1280,128]{1,0:T(8,128)(2,1)} %slice.505.value_ref, ...), custom_call_target="tpu_custom_call", output_to_operand_aliasing={{0}: (13, {})} | custom-call | flops 2097152000 | bytes 4915200 | tf_op jit(solution)/shard_map/pallas_call | solution.py:421
  533.6 7.5 %convolution_convert_fusion.4 = bf16[2048,768]{1,0:T(8,128)(2,1)S(1)} fusion(bf16[1280,2048]{1,0:T(8,128)(2,1)} %copy-done.20, bf16[1280,768]{1,0:T(8,128)(2,1)} %get-tuple-element.323), kind=kOutput, calls=%fused_computation.22 | convolution fusion | flops 4028104704 | bytes 10354688 | tf_op jit(solution)/shard_map/dot_general | solution.py:60
  541.5 3.0 multiply_convert_fusion
  544.5 6.6 fusion.4
  555.5 2.5 convert_element_type.506
  559.0 3.5 collective-permute-start.61
  562.5 7.5 %shard_map.287 = bf16[256,2048]{1,0:T(8,128)(2,1)} custom-call(bf16[1280,256]{1,0:T(8,128)(2,1)} %copy-done.29, bf16[160,2048]{1,0:T(8,128)(2,1)} %copy-done.17, bf16[160,2048]{1,0:T(8,128)(2,1)} %collective-permute-done.49.refs_1_, bf16[160,2048]{1,0:T(8,128)(2,1)} %collective-permute-done.48.refs_2_, bf16[160,2048]{1,0:T(8,128)(2,1)} %copy-done.60, ...), custom_call_target="tpu_custom_call" | custom-call | flops 1342177280 | bytes 5898240 | tf_op jit(solution)/shard_map/pallas_call | solution.py:461
  576.3 5.0 all-to-all-start.5
  581.4 3.1 slice_bitcast_fusion.3
  586.5 2.9 all-to-all-done.5
  593.5 8.5 %collective-permute-done.60 = bf16[160,2048]{1,0:T(8,128)(2,1)} collective-permute-done((bf16[160,2048]{1,0:T(8,128)(2,1)}, bf16[160,2048]{1,0:T(8,128)(2,1)}, u32[]{:S(2)}, u32[]{:S(2)}) %collective-permute-start.60) | collective-permute-done | bytes 655392 | tf_op jit(solution)/shard_map/ppermute | solution.py:88
  603.3 4.7 all-to-all-start.6
  608.0 3.3 add_convert_fusion.3
  612.3 2.3 maximum_convert_fusion
  618.9 2.3 collective-permute-done.67
  622.3 8.8 %collective-permute-done.65 = bf16[1,64,2048]{2,1,0:T(8,128)(2,1)S(1)} collective-permute-done((bf16[1,64,2048]{2,1,0:T(8,128)(2,1)S(1)}, bf16[1,64,2048]{2,1,0:T(8,128)(2,1)S(1)}, u32[]{:S(2)}, u32[]{:S(2)}) %collective-permute-start.65) | collective-permute-done | bytes 262176 | tf_op jit(solution)/shard_map/ppermute | solution.py:204
  634.1 3.3 collective-permute-done.64
  639.5 3.0 add_convert_fusion.1
  646.0 4.5 collective-permute-start.68
  650.5 2.3 maximum_convert_fusion.1
  653.5 10.5 %collective-permute-done.71 = bf16[1,64,2048]{2,1,0:T(8,128)(2,1)} collective-permute-done((bf16[1,64,2048]{2,1,0:T(8,128)(2,1)S(1)}, bf16[1,64,2048]{2,1,0:T(8,128)(2,1)}, u32[]{:S(2)}, u32[]{:S(2)}) %collective-permute-start.71) | collective-permute-done | bytes 262176 | tf_op jit(solution)/shard_map/ppermute | solution.py:204
  669.1 2.7 fusion.20
  (660 shorter events, 226.5 us)
Async XLA Ops:
  11.5 27.4 %all-to-all-start = ((bf16[8,64,768]{2,1,0:T(8,128)(2,1)}), bf16[8,64,768]{2,1,0:T(8,128)(2,1)S(1)}, u32[]{:S(2)}, u32[]{:S(2)}) async-start(bf16[8,64,768]{2,1,0:T(8,128)(2,1)} %copy.138), calls=%async_computation | async-start | bytes 1572864 | tf_op jit(solution)/shard_map/all_to_all | solution.py:250
  18.7 96.6 %all-gather.2.cloned.1.call-start = ((), (), s32[]{:S(2)}) async-start(), calls=%async_computation.10 | async-start | bytes 2359296 | tf_op jit(solution)/shard_map/all_gather | solution.py:69
  38.9 18.2 %collective-permute-start.4 = (bf16[160,2048]{1,0:T(8,128)(2,1)S(1)}, bf16[160,2048]{1,0:T(8,128)(2,1)}, u32[]{:S(2)}, u32[]{:S(2)}) collective-permute-start(bf16[160,2048]{1,0:T(8,128)(2,1)S(1)} %copy-done.8), channel_id=1, source_target_pairs={{0,1},{2,0},{4,2},{6,4},{7,6},{5,7},{3,5},{1,3},{8,9},{10,8},{12,1... | collective-permute-start | bytes 1966088 | tf_op jit(solution)/shard_map/ppermute | solution.py:88
  40.3 18.9 %collective-permute-start = (bf16[160,2048]{1,0:T(8,128)(2,1)S(1)}, bf16[160,2048]{1,0:T(8,128)(2,1)}, u32[]{:S(2)}, u32[]{:S(2)}) collective-permute-start(bf16[160,2048]{1,0:T(8,128)(2,1)S(1)} %copy-done.8), channel_id=1, source_target_pairs={{0,2},{2,4},{4,6},{6,7},{7,5},{5,3},{3,1},{1,0},{8,10},{10,12},{12... | collective-permute-start | bytes 1966088 | tf_op jit(solution)/shard_map/ppermute | solution.py:88
  45.8 23.9 %collective-permute-start.11 = (bf16[1,8,64,768]{3,2,1,0:T(8,128)(2,1)S(1)}, bf16[1,8,64,768]{3,2,1,0:T(8,128)(2,1)S(1)}, u32[]{:S(2)}, u32[]{:S(2)}) collective-permute-start(bf16[1,8,64,768]{3,2,1,0:T(8,128)(2,1)S(1)} %bitcast.168), channel_id=1, source_target_pairs={{0,16},{8,24},{16,0},{24,8},{1,17},{9,25},{17,1},{25,9},{2,18},{10... | collective-permute-start | bytes 2359304 | tf_op jit(solution)/shard_map/ppermute | solution.py:204
  64.0 25.8 %collective-permute-start.1 = (bf16[160,2048]{1,0:T(8,128)(2,1)}, bf16[160,2048]{1,0:T(8,128)(2,1)}, u32[]{:S(2)}, u32[]{:S(2)}) collective-permute-start(bf16[160,2048]{1,0:T(8,128)(2,1)} %collective-permute-done), channel_id=1, source_target_pairs={{0,2},{2,4},{4,6},{6,7},{7,5},{5,3},{3,1},{1,0},{8,10},{10,12},{12... | collective-permute-start | bytes 1966088 | tf_op jit(solution)/shard_map/ppermute | solution.py:88
  66.0 34.5 %collective-permute-start.5 = (bf16[160,2048]{1,0:T(8,128)(2,1)}, bf16[160,2048]{1,0:T(8,128)(2,1)}, u32[]{:S(2)}, u32[]{:S(2)}) collective-permute-start(bf16[160,2048]{1,0:T(8,128)(2,1)} %collective-permute-done.4), channel_id=1, source_target_pairs={{0,1},{2,0},{4,2},{6,4},{7,6},{5,7},{3,5},{1,3},{8,9},{10,8},{12,1... | collective-permute-start | bytes 1966088 | tf_op jit(solution)/shard_map/ppermute | solution.py:88
  71.1 45.6 %collective-permute-start.12 = (bf16[2,8,64,768]{3,2,1,0:T(8,128)(2,1)}, bf16[2,8,64,768]{3,2,1,0:T(8,128)(2,1)}, u32[]{:S(2)}, u32[]{:S(2)}) collective-permute-start(bf16[2,8,64,768]{3,2,1,0:T(8,128)(2,1)} %maximum_select_fusion.3), channel_id=1, source_target_pairs={{0,8},{8,0},{16,24},{24,16},{1,9},{9,1},{17,25},{25,17},{2,10},{10... | collective-permute-start | bytes 4718600 | tf_op jit(solution)/shard_map/ppermute | solution.py:204
  89.7 25.6 %collective-permute-start.2 = (bf16[160,2048]{1,0:T(8,128)(2,1)}, bf16[160,2048]{1,0:T(8,128)(2,1)S(1)}, u32[]{:S(2)}, u32[]{:S(2)}) collective-permute-start(bf16[160,2048]{1,0:T(8,128)(2,1)} %collective-permute-done.1), channel_id=1, source_target_pairs={{0,2},{2,4},{4,6},{6,7},{7,5},{5,3},{3,1},{1,0},{8,10},{10,12},{12... | collective-permute-start | bytes 1966088 | tf_op jit(solution)/shard_map/ppermute | solution.py:88
  120.8 20.5 %collective-permute-start.10 = (bf16[512,512]{1,0:T(8,128)(2,1)S(1)}, bf16[512,512]{1,0:T(8,128)(2,1)S(1)}, u32[]{:S(2)}, u32[]{:S(2)}) collective-permute-start(bf16[512,512]{1,0:T(8,128)(2,1)S(1)} %get-tuple-element.512), channel_id=1, source_target_pairs={{0,16},{8,24},{16,0},{24,8},{1,17},{9,25},{17,1},{25,9},{2,18},{10... | collective-permute-start | bytes 1572872 | tf_op jit(solution)/shard_map/ppermute | solution.py:204
  122.4 33.5 %collective-permute-start.15 = (bf16[512,512]{1,0:T(8,128)(2,1)S(1)}, bf16[512,512]{1,0:T(8,128)(2,1)S(1)}, u32[]{:S(2)}, u32[]{:S(2)}) collective-permute-start(bf16[512,512]{1,0:T(8,128)(2,1)S(1)} %get-tuple-element.511), channel_id=1, source_target_pairs={{0,16},{8,24},{16,0},{24,8},{1,17},{9,25},{17,1},{25,9},{2,18},{10... | collective-permute-start | bytes 1572872 | tf_op jit(solution)/shard_map/ppermute | solution.py:204
  122.9 45.5 %collective-permute-start.18 = (bf16[512,512]{1,0:T(8,128)(2,1)S(1)}, bf16[512,512]{1,0:T(8,128)(2,1)S(1)}, u32[]{:S(2)}, u32[]{:S(2)}) collective-permute-start(bf16[512,512]{1,0:T(8,128)(2,1)S(1)} %get-tuple-element.510), channel_id=1, source_target_pairs={{0,16},{8,24},{16,0},{24,8},{1,17},{9,25},{17,1},{25,9},{2,18},{10... | collective-permute-start | bytes 1572872 | tf_op jit(solution)/shard_map/ppermute | solution.py:204
  126.0 16.9 %collective-permute-start.8 = (bf16[160,2048]{1,0:T(8,128)(2,1)S(1)}, bf16[160,2048]{1,0:T(8,128)(2,1)S(1)}, u32[]{:S(2)}, u32[]{:S(2)}) collective-permute-start(bf16[160,2048]{1,0:T(8,128)(2,1)S(1)} %copy-done.13), channel_id=1, source_target_pairs={{0,2},{2,4},{4,6},{6,7},{7,5},{5,3},{3,1},{1,0},{8,10},{10,12},{12... | collective-permute-start | bytes 1966088 | tf_op jit(solution)/shard_map/ppermute | solution.py:88
  127.3 15.5 %collective-permute-start.9 = (bf16[160,2048]{1,0:T(8,128)(2,1)S(1)}, bf16[160,2048]{1,0:T(8,128)(2,1)S(1)}, u32[]{:S(2)}, u32[]{:S(2)}) collective-permute-start(bf16[160,2048]{1,0:T(8,128)(2,1)S(1)} %copy-done.13), channel_id=1, source_target_pairs={{0,1},{2,0},{4,2},{6,4},{7,6},{5,7},{3,5},{1,3},{8,9},{10,8},{12,1... | collective-permute-start | bytes 1966088 | tf_op jit(solution)/shard_map/ppermute | solution.py:88
  141.4 37.4 %collective-permute-start.21 = (bf16[512,512]{1,0:T(8,128)(2,1)S(1)}, bf16[512,512]{1,0:T(8,128)(2,1)}, u32[]{:S(2)}, u32[]{:S(2)}) collective-permute-start(bf16[512,512]{1,0:T(8,128)(2,1)S(1)} %get-tuple-element.509), channel_id=1, source_target_pairs={{0,16},{8,24},{16,0},{24,8},{1,17},{9,25},{17,1},{25,9},{2,18},{10... | collective-permute-start | bytes 1572872 | tf_op jit(solution)/shard_map/ppermute | solution.py:204
  156.0 54.7 %collective-permute-start.22 = (bf16[2048,512]{1,0:T(8,128)(2,1)S(1)}, bf16[2048,512]{1,0:T(8,128)(2,1)}, u32[]{:S(2)}, u32[]{:S(2)}) collective-permute-start(bf16[2048,512]{1,0:T(8,128)(2,1)S(1)} %copy-done.6), channel_id=1, source_target_pairs={{0,8},{8,0},{16,24},{24,16},{1,9},{9,1},{17,25},{25,17},{2,10},{10... | collective-permute-start | bytes 6291464 | tf_op jit(solution)/shard_map/ppermute | solution.py:204
  156.1 17.4 %collective-permute-start.16 = (bf16[160,2048]{1,0:T(8,128)(2,1)S(1)}, bf16[160,2048]{1,0:T(8,128)(2,1)S(1)}, u32[]{:S(2)}, u32[]{:S(2)}) collective-permute-start(bf16[160,2048]{1,0:T(8,128)(2,1)S(1)} %collective-permute-done.13), channel_id=1, source_target_pairs={{0,2},{2,4},{4,6},{6,7},{7,5},{5,3},{3,1},{1,0},{8,10},{10,12},{12... | collective-permute-start | bytes 1966088 | tf_op jit(solution)/shard_map/ppermute | solution.py:88
  158.3 17.1 %collective-permute-start.17 = (bf16[160,2048]{1,0:T(8,128)(2,1)S(1)}, bf16[160,2048]{1,0:T(8,128)(2,1)S(1)}, u32[]{:S(2)}, u32[]{:S(2)}) collective-permute-start(bf16[160,2048]{1,0:T(8,128)(2,1)S(1)} %collective-permute-done.14), channel_id=1, source_target_pairs={{0,1},{2,0},{4,2},{6,4},{7,6},{5,7},{3,5},{1,3},{8,9},{10,8},{12,1... | collective-permute-start | bytes 1966088 | tf_op jit(solution)/shard_map/ppermute | solution.py:88
  186.0 20.6 %all-to-all-start.1 = ((bf16[8,160,256]{2,1,0:T(8,128)(2,1)}), bf16[8,160,256]{2,1,0:T(8,128)(2,1)}, u32[]{:S(2)}, u32[]{:S(2)}) async-start(bf16[8,160,256]{2,1,0:T(8,128)(2,1)} %copy-done.54), calls=%async_computation.1 | async-start | bytes 1310720 | tf_op jit(solution)/shard_map/all_to_all | solution.py:250
  192.4 20.6 %collective-permute-start.23 = (bf16[2048,512]{1,0:T(8,128)(2,1)}, bf16[2048,512]{1,0:T(8,128)(2,1)}, u32[]{:S(2)}, u32[]{:S(2)}) collective-permute-start(bf16[2048,512]{1,0:T(8,128)(2,1)} %constant_dynamic-update-slice_fusion.18), channel_id=1, source_target_pairs={{0,8},{8,0},{16,24},{24,16},{1,9},{9,1},{17,25},{25,17},{2,10},{10... | collective-permute-start | bytes 6291464 | tf_op jit(solution)/shard_map/ppermute | solution.py:204
  216.6 14.9 %collective-permute-start.24 = (bf16[160,2048]{1,0:T(8,128)(2,1)S(1)}, bf16[160,2048]{1,0:T(8,128)(2,1)S(1)}, u32[]{:S(2)}, u32[]{:S(2)}) collective-permute-start(bf16[160,2048]{1,0:T(8,128)(2,1)S(1)} %get-tuple-element.461), channel_id=1, source_target_pairs={{0,2},{2,4},{4,6},{6,7},{7,5},{5,3},{3,1},{1,0},{8,10},{10,12},{12... | collective-permute-start | bytes 1966088 | tf_op jit(solution)/shard_map/ppermute | solution.py:88
  232.5 14.7 %collective-permute-start.27 = (bf16[160,2048]{1,0:T(8,128)(2,1)S(1)}, bf16[160,2048]{1,0:T(8,128)(2,1)S(1)}, u32[]{:S(2)}, u32[]{:S(2)}) collective-permute-start(bf16[160,2048]{1,0:T(8,128)(2,1)S(1)} %collective-permute-done.25), channel_id=1, source_target_pairs={{0,1},{2,0},{4,2},{6,4},{7,6},{5,7},{3,5},{1,3},{8,9},{10,8},{12,1... | collective-permute-start | bytes 1966088 | tf_op jit(solution)/shard_map/ppermute | solution.py:88
  247.5 25.3 %collective-permute-start.29 = (bf16[160,2048]{1,0:T(8,128)(2,1)S(1)}, bf16[160,2048]{1,0:T(8,128)(2,1)S(1)}, u32[]{:S(2)}, u32[]{:S(2)}) collective-permute-start(bf16[160,2048]{1,0:T(8,128)(2,1)S(1)} %collective-permute-done.27), channel_id=1, source_target_pairs={{0,1},{2,0},{4,2},{6,4},{7,6},{5,7},{3,5},{1,3},{8,9},{10,8},{12,1... | collective-permute-start | bytes 1966088 | tf_op jit(solution)/shard_map/ppermute | solution.py:88
  247.6 25.2 %collective-permute-start.28 = (bf16[160,2048]{1,0:T(8,128)(2,1)S(1)}, bf16[160,2048]{1,0:T(8,128)(2,1)S(1)}, u32[]{:S(2)}, u32[]{:S(2)}) collective-permute-start(bf16[160,2048]{1,0:T(8,128)(2,1)S(1)} %collective-permute-done.26), channel_id=1, source_target_pairs={{0,2},{2,4},{4,6},{6,7},{7,5},{5,3},{3,1},{1,0},{8,10},{10,12},{12... | collective-permute-start | bytes 1966088 | tf_op jit(solution)/shard_map/ppermute | solution.py:88
  325.1 19.9 %collective-permute-start.32 = (bf16[80,2048]{1,0:T(8,128)(2,1)}, bf16[80,2048]{1,0:T(8,128)(2,1)}, u32[]{:S(2)}, u32[]{:S(2)}) collective-permute-start(bf16[80,2048]{1,0:T(8,128)(2,1)} %get-tuple-element.502), channel_id=1, source_target_pairs={{0,2},{2,4},{4,6},{6,7},{7,5},{5,3},{3,1},{1,0},{8,10},{10,12},{12... | collective-permute-start | bytes 983048 | tf_op jit(solution)/shard_map/ppermute | solution.py:88
  326.8 18.1 %collective-permute-start.33 = (bf16[80,2048]{1,0:T(8,128)(2,1)S(1)}, bf16[80,2048]{1,0:T(8,128)(2,1)}, u32[]{:S(2)}, u32[]{:S(2)}) collective-permute-start(bf16[80,2048]{1,0:T(8,128)(2,1)S(1)} %get-tuple-element.501), channel_id=1, source_target_pairs={{0,1},{2,0},{4,2},{6,4},{7,6},{5,7},{3,5},{1,3},{8,9},{10,8},{12,1... | collective-permute-start | bytes 983048 | tf_op jit(solution)/shard_map/ppermute | solution.py:88
  347.3 23.1 %collective-permute-start.35 = (bf16[160,2048]{1,0:T(8,128)(2,1)}, bf16[160,2048]{1,0:T(8,128)(2,1)}, u32[]{:S(2)}, u32[]{:S(2)}) collective-permute-start(bf16[160,2048]{1,0:T(8,128)(2,1)} %pad_maximum_fusion.7), channel_id=1, source_target_pairs={{0,1},{2,0},{4,2},{6,4},{7,6},{5,7},{3,5},{1,3},{8,9},{10,8},{12,1... | collective-permute-start | bytes 1966088 | tf_op jit(solution)/shard_map/ppermute | solution.py:88
  347.4 23.0 %collective-permute-start.34 = (bf16[160,2048]{1,0:T(8,128)(2,1)S(1)}, bf16[160,2048]{1,0:T(8,128)(2,1)}, u32[]{:S(2)}, u32[]{:S(2)}) collective-permute-start(bf16[160,2048]{1,0:T(8,128)(2,1)S(1)} %pad_maximum_fusion.6), channel_id=1, source_target_pairs={{0,2},{2,4},{4,6},{6,7},{7,5},{5,3},{3,1},{1,0},{8,10},{10,12},{12... | collective-permute-start | bytes 1966088 | tf_op jit(solution)/shard_map/ppermute | solution.py:88
  350.5 20.0 %all-to-all-start.3 = ((f32[8,160,2]{1,2,0:T(2,128)}), f32[8,160,2]{1,2,0:T(2,128)S(1)}, u32[]{:S(2)}, u32[]{:S(2)}) async-start(f32[8,160,2]{1,2,0:T(2,128)} %copy.172), calls=%async_computation.3 | async-start | bytes 32768 | tf_op jit(solution)/shard_map/all_to_all | solution.py:250
  353.8 179.8 %reduce-scatter.4.cloned.1.call-start = ((), (), s32[]{:S(2)}) async-start(), calls=%async_computation.11 | async-start | bytes 10485760 | tf_op jit(solution)/shard_map/reduce_scatter | solution.py:826
  374.1 27.3 %collective-permute-start.37 = (bf16[160,2048]{1,0:T(8,128)(2,1)S(1)}, bf16[160,2048]{1,0:T(8,128)(2,1)}, u32[]{:S(2)}, u32[]{:S(2)}) collective-permute-start(bf16[160,2048]{1,0:T(8,128)(2,1)S(1)} %add_convert_fusion.11), channel_id=1, source_target_pairs={{0,1},{2,0},{4,2},{6,4},{7,6},{5,7},{3,5},{1,3},{8,9},{10,8},{12,1... | collective-permute-start | bytes 1966088 | tf_op jit(solution)/shard_map/ppermute | solution.py:88
  376.4 25.0 %collective-permute-start.38 = (bf16[80,2048]{1,0:T(8,128)(2,1)}, bf16[80,2048]{1,0:T(8,128)(2,1)}, u32[]{:S(2)}, u32[]{:S(2)}) collective-permute-start(bf16[80,2048]{1,0:T(8,128)(2,1)} %get-tuple-element.487), channel_id=1, source_target_pairs={{0,2},{2,4},{4,6},{6,7},{7,5},{5,3},{3,1},{1,0},{8,10},{10,12},{12... | collective-permute-start | bytes 983048 | tf_op jit(solution)/shard_map/ppermute | solution.py:88
  376.5 24.8 %collective-permute-start.39 = (bf16[80,2048]{1,0:T(8,128)(2,1)S(1)}, bf16[80,2048]{1,0:T(8,128)(2,1)}, u32[]{:S(2)}, u32[]{:S(2)}) collective-permute-start(bf16[80,2048]{1,0:T(8,128)(2,1)S(1)} %get-tuple-element.486), channel_id=1, source_target_pairs={{0,1},{2,0},{4,2},{6,4},{7,6},{5,7},{3,5},{1,3},{8,9},{10,8},{12,1... | collective-permute-start | bytes 983048 | tf_op jit(solution)/shard_map/ppermute | solution.py:88
  379.9 21.5 %collective-permute-start.36 = (bf16[160,2048]{1,0:T(8,128)(2,1)S(1)}, bf16[160,2048]{1,0:T(8,128)(2,1)}, u32[]{:S(2)}, u32[]{:S(2)}) collective-permute-start(bf16[160,2048]{1,0:T(8,128)(2,1)S(1)} %add_convert_fusion.12), channel_id=1, source_target_pairs={{0,2},{2,4},{4,6},{6,7},{7,5},{5,3},{3,1},{1,0},{8,10},{10,12},{12... | collective-permute-start | bytes 1966088 | tf_op jit(solution)/shard_map/ppermute | solution.py:88
  401.4 180.0 %reduce-scatter.6.cloned.1.call-start = ((), (), s32[]{:S(2)}) async-start(), calls=%async_computation.12 | async-start | bytes 10485760 | tf_op jit(solution)/shard_map/reduce_scatter | solution.py:873
  403.1 25.3 %collective-permute-start.43 = (bf16[160,2048]{1,0:T(8,128)(2,1)S(1)}, bf16[160,2048]{1,0:T(8,128)(2,1)}, u32[]{:S(2)}, u32[]{:S(2)}) collective-permute-start(bf16[160,2048]{1,0:T(8,128)(2,1)S(1)} %pad_maximum_fusion.9), channel_id=1, source_target_pairs={{0,1},{2,0},{4,2},{6,4},{7,6},{5,7},{3,5},{1,3},{8,9},{10,8},{12,1... | collective-permute-start | bytes 1966088 | tf_op jit(solution)/shard_map/ppermute | solution.py:88
  405.1 23.4 %collective-permute-start.42 = (bf16[160,2048]{1,0:T(8,128)(2,1)S(1)}, bf16[160,2048]{1,0:T(8,128)(2,1)}, u32[]{:S(2)}, u32[]{:S(2)}) collective-permute-start(bf16[160,2048]{1,0:T(8,128)(2,1)S(1)} %pad_maximum_fusion.8), channel_id=1, source_target_pairs={{0,2},{2,4},{4,6},{6,7},{7,5},{5,3},{3,1},{1,0},{8,10},{10,12},{12... | collective-permute-start | bytes 1966088 | tf_op jit(solution)/shard_map/ppermute | solution.py:88
  408.1 21.9 %collective-permute-start.40 = (bf16[160,2048]{1,0:T(8,128)(2,1)}, bf16[160,2048]{1,0:T(8,128)(2,1)S(1)}, u32[]{:S(2)}, u32[]{:S(2)}) collective-permute-start(bf16[160,2048]{1,0:T(8,128)(2,1)} %get-tuple-element.498), channel_id=1, source_target_pairs={{0,2},{2,4},{4,6},{6,7},{7,5},{5,3},{3,1},{1,0},{8,10},{10,12},{12... | collective-permute-start | bytes 1966088 | tf_op jit(solution)/shard_map/ppermute | solution.py:88
  410.0 20.1 %collective-permute-start.41 = (bf16[160,2048]{1,0:T(8,128)(2,1)}, bf16[160,2048]{1,0:T(8,128)(2,1)S(1)}, u32[]{:S(2)}, u32[]{:S(2)}) collective-permute-start(bf16[160,2048]{1,0:T(8,128)(2,1)} %get-tuple-element.497), channel_id=1, source_target_pairs={{0,1},{2,0},{4,2},{6,4},{7,6},{5,7},{3,5},{1,3},{8,9},{10,8},{12,1... | collective-permute-start | bytes 1966088 | tf_op jit(solution)/shard_map/ppermute | solution.py:88
  433.9 15.0 %collective-permute-start.44 = (bf16[160,2048]{1,0:T(8,128)(2,1)S(1)}, bf16[160,2048]{1,0:T(8,128)(2,1)S(1)}, u32[]{:S(2)}, u32[]{:S(2)}) collective-permute-start(bf16[160,2048]{1,0:T(8,128)(2,1)S(1)} %get-tuple-element.483), channel_id=1, source_target_pairs={{0,2},{2,4},{4,6},{6,7},{7,5},{5,3},{3,1},{1,0},{8,10},{10,12},{12... | collective-permute-start | bytes 1966088 | tf_op jit(solution)/shard_map/ppermute | solution.py:88
  434.3 14.6 %collective-permute-start.45 = (bf16[160,2048]{1,0:T(8,128)(2,1)S(1)}, bf16[160,2048]{1,0:T(8,128)(2,1)S(1)}, u32[]{:S(2)}, u32[]{:S(2)}) collective-permute-start(bf16[160,2048]{1,0:T(8,128)(2,1)S(1)} %get-tuple-element.482), channel_id=1, source_target_pairs={{0,1},{2,0},{4,2},{6,4},{7,6},{5,7},{3,5},{1,3},{8,9},{10,8},{12,1... | collective-permute-start | bytes 1966088 | tf_op jit(solution)/shard_map/ppermute | solution.py:88
  448.9 29.5 %collective-permute-start.48 = (bf16[160,2048]{1,0:T(8,128)(2,1)S(1)}, bf16[160,2048]{1,0:T(8,128)(2,1)}, u32[]{:S(2)}, u32[]{:S(2)}) collective-permute-start(bf16[160,2048]{1,0:T(8,128)(2,1)S(1)} %get-tuple-element.331.refs_0_), channel_id=1, source_target_pairs={{0,2},{2,4},{4,6},{6,7},{7,5},{5,3},{3,1},{1,0},{8,10},{10,12},{12... | collective-permute-start | bytes 1966088 | tf_op jit(solution)/shard_map/ppermute | solution.py:88
  450.0 28.3 %collective-permute-start.49 = (bf16[160,2048]{1,0:T(8,128)(2,1)S(1)}, bf16[160,2048]{1,0:T(8,128)(2,1)}, u32[]{:S(2)}, u32[]{:S(2)}) collective-permute-start(bf16[160,2048]{1,0:T(8,128)(2,1)S(1)} %get-tuple-element.331.refs_0_), channel_id=1, source_target_pairs={{0,1},{2,0},{4,2},{6,4},{7,6},{5,7},{3,5},{1,3},{8,9},{10,8},{12,1... | collective-permute-start | bytes 1966088 | tf_op jit(solution)/shard_map/ppermute | solution.py:88
  453.8 24.4 %collective-permute-start.46 = (bf16[160,2048]{1,0:T(8,128)(2,1)}, bf16[160,2048]{1,0:T(8,128)(2,1)}, u32[]{:S(2)}, u32[]{:S(2)}) collective-permute-start(bf16[160,2048]{1,0:T(8,128)(2,1)} %get-tuple-element.481), channel_id=1, source_target_pairs={{0,2},{2,4},{4,6},{6,7},{7,5},{5,3},{3,1},{1,0},{8,10},{10,12},{12... | collective-permute-start | bytes 1966088 | tf_op jit(solution)/shard_map/ppermute | solution.py:88
  454.9 23.5 %collective-permute-start.47 = (bf16[160,2048]{1,0:T(8,128)(2,1)}, bf16[160,2048]{1,0:T(8,128)(2,1)}, u32[]{:S(2)}, u32[]{:S(2)}) collective-permute-start(bf16[160,2048]{1,0:T(8,128)(2,1)} %get-tuple-element.480), channel_id=1, source_target_pairs={{0,1},{2,0},{4,2},{6,4},{7,6},{5,7},{3,5},{1,3},{8,9},{10,8},{12,1... | collective-permute-start | bytes 1966088 | tf_op jit(solution)/shard_map/ppermute | solution.py:88
  455.8 36.5 %all-to-all-start.4 = ((bf16[8,160,256]{2,1,0:T(8,128)(2,1)}), bf16[8,160,256]{2,1,0:T(8,128)(2,1)S(1)}, u32[]{:S(2)}, u32[]{:S(2)}) async-start(bf16[8,160,256]{2,1,0:T(8,128)(2,1)} %bitcast.193), calls=%async_computation.4 | async-start | bytes 1310720 | tf_op jit(solution)/shard_map/all_to_all | solution.py:250
  461.3 183.0 %reduce-scatter.8.cloned.1.call-start = ((), (), s32[]{:S(2)}) async-start(), calls=%async_computation.13 | async-start | bytes 10485760 | tf_op jit(solution)/shard_map/reduce_scatter | solution.py:874
  493.1 18.1 %collective-permute-start.50 = (bf16[160,2048]{1,0:T(8,128)(2,1)}, bf16[160,2048]{1,0:T(8,128)(2,1)}, u32[]{:S(2)}, u32[]{:S(2)}) collective-permute-start(bf16[160,2048]{1,0:T(8,128)(2,1)} %collective-permute-done.48.refs_2_), channel_id=1, source_target_pairs={{0,2},{2,4},{4,6},{6,7},{7,5},{5,3},{3,1},{1,0},{8,10},{10,12},{12... | collective-permute-start | bytes 1966088 | tf_op jit(solution)/shard_map/ppermute | solution.py:88
  493.1 18.1 %collective-permute-start.51 = (bf16[160,2048]{1,0:T(8,128)(2,1)}, bf16[160,2048]{1,0:T(8,128)(2,1)S(1)}, u32[]{:S(2)}, u32[]{:S(2)}) collective-permute-start(bf16[160,2048]{1,0:T(8,128)(2,1)} %collective-permute-done.49.refs_1_), channel_id=1, source_target_pairs={{0,1},{2,0},{4,2},{6,4},{7,6},{5,7},{3,5},{1,3},{8,9},{10,8},{12,1... | collective-permute-start | bytes 1966088 | tf_op jit(solution)/shard_map/ppermute | solution.py:88
  512.0 17.6 %collective-permute-start.52 = (bf16[160,2048]{1,0:T(8,128)(2,1)}, bf16[160,2048]{1,0:T(8,128)(2,1)S(1)}, u32[]{:S(2)}, u32[]{:S(2)}) collective-permute-start(bf16[160,2048]{1,0:T(8,128)(2,1)} %collective-permute-done.50.refs_4_), channel_id=1, source_target_pairs={{0,2},{2,4},{4,6},{6,7},{7,5},{5,3},{3,1},{1,0},{8,10},{10,12},{12... | collective-permute-start | bytes 1966088 | tf_op jit(solution)/shard_map/ppermute | solution.py:88
  513.3 16.3 %collective-permute-start.53 = (bf16[160,2048]{1,0:T(8,128)(2,1)}, bf16[160,2048]{1,0:T(8,128)(2,1)S(1)}, u32[]{:S(2)}, u32[]{:S(2)}) collective-permute-start(bf16[160,2048]{1,0:T(8,128)(2,1)} %copy-done.60), channel_id=1, source_target_pairs={{0,1},{2,0},{4,2},{6,4},{7,6},{5,7},{3,5},{1,3},{8,9},{10,8},{12,1... | collective-permute-start | bytes 1966088 | tf_op jit(solution)/shard_map/ppermute | solution.py:88
  552.6 17.5 %collective-permute-start.57 = (bf16[80,2048]{1,0:T(8,128)(2,1)}, bf16[80,2048]{1,0:T(8,128)(2,1)}, u32[]{:S(2)}, u32[]{:S(2)}) collective-permute-start(bf16[80,2048]{1,0:T(8,128)(2,1)} %get-tuple-element.477), channel_id=1, source_target_pairs={{0,2},{2,4},{4,6},{6,7},{7,5},{5,3},{3,1},{1,0},{8,10},{10,12},{12... | collective-permute-start | bytes 983048 | tf_op jit(solution)/shard_map/ppermute | solution.py:88
  554.0 16.1 %collective-permute-start.58 = (bf16[80,2048]{1,0:T(8,128)(2,1)}, bf16[80,2048]{1,0:T(8,128)(2,1)}, u32[]{:S(2)}, u32[]{:S(2)}) collective-permute-start(bf16[80,2048]{1,0:T(8,128)(2,1)} %get-tuple-element.476), channel_id=1, source_target_pairs={{0,1},{2,0},{4,2},{6,4},{7,6},{5,7},{3,5},{1,3},{8,9},{10,8},{12,1... | collective-permute-start | bytes 983048 | tf_op jit(solution)/shard_map/ppermute | solution.py:88
  559.0 31.0 %collective-permute-start.61 = (bf16[8,1,64,768]{3,2,1,0:T(8,128)(2,1)}, bf16[8,1,64,768]{3,2,1,0:T(8,128)(2,1)}, u32[]{:S(2)}, u32[]{:S(2)}) collective-permute-start(bf16[8,1,64,768]{3,2,1,0:T(8,128)(2,1)} %constant_dynamic-slice_fusion.1), channel_id=1, source_target_pairs={{0,16},{8,24},{16,0},{24,8},{1,17},{9,25},{17,1},{25,9},{2,18},{10... | collective-permute-start | bytes 2359304 | tf_op jit(solution)/shard_map/ppermute | solution.py:204
  574.3 18.0 %collective-permute-start.62 = (bf16[2,64,2048]{2,1,0:T(8,128)(2,1)}, bf16[2,64,2048]{2,1,0:T(8,128)(2,1)}, u32[]{:S(2)}, u32[]{:S(2)}) collective-permute-start(bf16[2,64,2048]{2,1,0:T(8,128)(2,1)} %dynamic-slice_bitcast_fusion.1), channel_id=1, source_target_pairs={{0,8},{8,0},{16,24},{24,16},{1,9},{9,1},{17,25},{25,17},{2,10},{10... | collective-permute-start | bytes 1572872 | tf_op jit(solution)/shard_map/ppermute | solution.py:204
  584.5 17.6 %collective-permute-start.60 = (bf16[160,2048]{1,0:T(8,128)(2,1)}, bf16[160,2048]{1,0:T(8,128)(2,1)}, u32[]{:S(2)}, u32[]{:S(2)}) collective-permute-start(bf16[160,2048]{1,0:T(8,128)(2,1)} %pad_maximum_fusion.12), channel_id=1, source_target_pairs={{0,1},{2,0},{4,2},{6,4},{7,6},{5,7},{3,5},{1,3},{8,9},{10,8},{12,1... | collective-permute-start | bytes 1966088 | tf_op jit(solution)/shard_map/ppermute | solution.py:88
  586.5 16.8 %collective-permute-start.59 = (bf16[160,2048]{1,0:T(8,128)(2,1)}, bf16[160,2048]{1,0:T(8,128)(2,1)}, u32[]{:S(2)}, u32[]{:S(2)}) collective-permute-start(bf16[160,2048]{1,0:T(8,128)(2,1)} %pad_maximum_fusion.11), channel_id=1, source_target_pairs={{0,2},{2,4},{4,6},{6,7},{7,5},{5,3},{3,1},{1,0},{8,10},{10,12},{12... | collective-permute-start | bytes 1966088 | tf_op jit(solution)/shard_map/ppermute | solution.py:88
  603.3 34.1 %all-to-all-start.6 = ((bf16[8,64,768]{2,1,0:T(8,128)(2,1)}), bf16[8,64,768]{2,1,0:T(8,128)(2,1)S(1)}, u32[]{:S(2)}, u32[]{:S(2)}) async-start(bf16[8,64,768]{2,1,0:T(8,128)(2,1)} %bitcast.63), calls=%async_computation.7 | async-start | bytes 1572864 | tf_op jit(solution)/shard_map/all_to_all | solution.py:250
  614.6 19.5 %collective-permute-start.63 = (bf16[160,2048]{1,0:T(8,128)(2,1)S(1)}, bf16[160,2048]{1,0:T(8,128)(2,1)S(1)}, u32[]{:S(2)}, u32[]{:S(2)}) collective-permute-start(bf16[160,2048]{1,0:T(8,128)(2,1)S(1)} %copy-done.64), channel_id=1, source_target_pairs={{0,2},{2,4},{4,6},{6,7},{7,5},{5,3},{3,1},{1,0},{8,10},{10,12},{12... | collective-permute-start | bytes 1966088 | tf_op jit(solution)/shard_map/ppermute | solution.py:88
  616.7 20.8 %collective-permute-start.64 = (bf16[160,2048]{1,0:T(8,128)(2,1)S(1)}, bf16[160,2048]{1,0:T(8,128)(2,1)}, u32[]{:S(2)}, u32[]{:S(2)}) collective-permute-start(bf16[160,2048]{1,0:T(8,128)(2,1)S(1)} %copy-done.63), channel_id=1, source_target_pairs={{0,1},{2,0},{4,2},{6,4},{7,6},{5,7},{3,5},{1,3},{8,9},{10,8},{12,1... | collective-permute-start | bytes 1966088 | tf_op jit(solution)/shard_map/ppermute | solution.py:88
  639.1 26.0 %collective-permute-start.70 = (bf16[1,3,64,2048]{3,2,1,0:T(8,128)(2,1)S(1)}, bf16[1,3,64,2048]{3,2,1,0:T(8,128)(2,1)}, u32[]{:S(2)}, u32[]{:S(2)}) collective-permute-start(bf16[1,3,64,2048]{3,2,1,0:T(8,128)(2,1)S(1)} %stack.157), channel_id=1, source_target_pairs={{0,16},{8,24},{16,0},{24,8},{1,17},{9,25},{17,1},{25,9},{2,18},{10... | collective-permute-start | bytes 2359304 | tf_op jit(solution)/shard_map/ppermute | solution.py:204
  642.5 21.5 %collective-permute-start.71 = (bf16[1,64,2048]{2,1,0:T(8,128)(2,1)S(1)}, bf16[1,64,2048]{2,1,0:T(8,128)(2,1)}, u32[]{:S(2)}, u32[]{:S(2)}) collective-permute-start(bf16[1,64,2048]{2,1,0:T(8,128)(2,1)S(1)} %copy-done.53), channel_id=1, source_target_pairs={{0,16},{8,24},{16,0},{24,8},{1,17},{9,25},{17,1},{25,9},{2,18},{10... | collective-permute-start | bytes 786440 | tf_op jit(solution)/shard_map/ppermute | solution.py:204
  646.0 20.9 %collective-permute-start.68 = (bf16[160,2048]{1,0:T(8,128)(2,1)}, bf16[160,2048]{1,0:T(8,128)(2,1)S(1)}, u32[]{:S(2)}, u32[]{:S(2)}) collective-permute-start(bf16[160,2048]{1,0:T(8,128)(2,1)} %get-tuple-element.471), channel_id=1, source_target_pairs={{0,2},{2,4},{4,6},{6,7},{7,5},{5,3},{3,1},{1,0},{8,10},{10,12},{12... | collective-permute-start | bytes 1966088 | tf_op jit(solution)/shard_map/ppermute | solution.py:88
  650.5 16.4 %collective-permute-start.69 = (bf16[160,2048]{1,0:T(8,128)(2,1)}, bf16[160,2048]{1,0:T(8,128)(2,1)S(1)}, u32[]{:S(2)}, u32[]{:S(2)}) collective-permute-start(bf16[160,2048]{1,0:T(8,128)(2,1)} %get-tuple-element.470), channel_id=1, source_target_pairs={{0,1},{2,0},{4,2},{6,4},{7,6},{5,7},{3,5},{1,3},{8,9},{10,8},{12,1... | collective-permute-start | bytes 1966088 | tf_op jit(solution)/shard_map/ppermute | solution.py:88
  (159 other events, 1601.2 us)
Sparse Core Ops, SparseCore 0:
  42.8 57.6 all-gather.1
  401.5 74.2 reduce-scatter.3
  478.6 71.6 reduce-scatter.5
  552.8 78.9 reduce-scatter.7

commit v11 on v10

--- a/solution.py
+++ b/solution.py
@@ -724,12 +724,6 @@
     gates_own = gate_table(second_input, code_own)
 
     back_ring = RingSum(back_block, row_count)
-    back_parts[0] = window(
-        [back_ring],
-        lambda gback, uback: expert_back(gback, uback, gate_weight, up_weight, 0, chunks),
-        gback_all,
-        uback_all,
-    )
 
     def mixture_work(inner, pair):
         return (
@@ -739,6 +733,12 @@
 
     mixture_part, pair_grad = window([back_ring], mixture_work, inner_all, pair_sent)
     mixture_ring = RingSum(slot_rows(mixture_part), row_count)
+
+    def back_work(gback, uback, stage=back_parts):
+        stage[0] = expert_back(gback, uback, gate_weight, up_weight, 0, chunks)
+        return stage[0]
+
+    back_parts[0] = window([back_ring, mixture_ring], back_work, gback_all, uback_all)
 
     def down_work(inner, pair):
         pair_grad = pair.transpose(1, 0, 2).reshape(row_count, expert_total)
@@ -792,34 +792,43 @@
     swap = Swap(swap_sent, 0)
     attention_gather = RingGather(attention_low)
     up_part = window(
-        [mixture_ring, swap, attention_gather],
+        [swap, attention_gather],
         lambda uback: grad_of(second_all, uback),
         uback_all,
     )
     mixture = mixture_ring.total()
-    layer_out = (valid_own * (residual + mixture)).astype(low_type)
     mixed_grad = swap.received
 
-    sent, gain_parts = (), 0.0
+    head_width = 3 * head_dim
+
+    def head_grad(head, sent):
+        start = head * head_width
+        return grad_of(first_all, sent[:, start : start + head_width])
+
+    def chain_start(head_part):
+        shape = (group_count, replica_count, share, head_width)
+        return rep_scatter(head_part.reshape(shape), 1, scatter_order)
+
+    sent, gain_parts, chains = (), 0.0, []
     for head in range(heads_here):
 
         def head_work(grads, *earlier, head=head):
-            return tuple(
-                attention_back(
-                    head,
-                    heads[head][:4],
-                    grads,
-                    slot_order,
-                    segment_column,
-                    segment_line,
-                    raw,
-                    norm_gains,
-                    (cosine, sine_part),
-                    earlier,
-                )
+            part = [head_grad(head - 1, earlier[0])] if head else []
+            return part, attention_back(
+                head,
+                heads[head][:4],
+                grads,
+                slot_order,
+                segment_column,
+                segment_line,
+                raw,
+                norm_gains,
+                (cosine, sine_part),
+                earlier,
             )
 
-        *sent, gain_part = window([attention_gather], head_work, mixed_grad, *sent)
+        part, (*sent, gain_part) = window([attention_gather], head_work, mixed_grad, *sent)
+        chains += [chain_start(grad) for grad in part]
         gain_parts = gain_parts + gain_part
     (sent,) = sent
     querynorm_part, keynorm_part = gain_parts[0], gain_parts[1]
@@ -831,21 +840,19 @@
     )
     sent, down_sum = tie(sent, down_sum)
 
-    def first_work(sent, head):
+    def first_work(sent):
         first_part = mm(sent, head_weight, 1, 1)
         token_wide = token_all.astype(wide_type)
         prenorm_part = jnp.sum(first_part * token_wide * inverse_rms(token_wide), axis=0)
-        return first_part.astype(low_type), prenorm_part, rep_scatter(head, 1, scatter_order[:1])
-
-    head_part = window([attention_gather], grad_of, first_all, sent)
-    while attention_gather.step < group_count // 2:
+        return first_part.astype(low_type), prenorm_part
+
+    head_part = window([], functools.partial(head_grad, heads_here - 1), sent)
+    chains.append(chain_start(head_part))
+    first_low, prenorm_part = window(
+        [attention_gather] if attention_gather.step < steps else [], first_work, sent
+    )
+    while attention_gather.step < steps:
         window([attention_gather], lambda: ())
-    first_low, prenorm_part, head_part = window(
-        [],
-        first_work,
-        sent,
-        head_part.reshape(group_count, replica_count, share, 3 * width_here),
-    )
 
     def small_swap(parts):
         return swap_all(
@@ -863,45 +870,70 @@
 
     first_ring = RingSum(slot_rows(first_low), row_count)
     small_parts = [router_part, postnorm_part, prenorm_part, querynorm_part, keynorm_part]
-    head_part = rep_scatter(head_part, 1, scatter_order[1:])
-    output_part = window(
+    gate_sum = lax.psum_scatter(gate_part, "rep", scatter_dimension=0, tiled=True)
+    up_sum = lax.psum_scatter(up_part, "rep", scatter_dimension=0, tiled=True)
+
+    def split_experts(total):
+        return jnp.stack(
+            [
+                total[:, e * hidden_here : (e + 1) * hidden_here].astype(wide_type)
+                for e in range(experts_here)
+            ]
+        )
+
+    def chain_swap(part):
+        return swap_all(part.reshape(group_count, share, head_width))
+
+    def chain_gather(part):
+        rows = part.reshape(group_count, share, 3, head_dim).transpose(2, 1, 0, 3)
+        return rep_gather(rows[None], gather_order[:-1])
+
+    output_part, *chains[:-1] = window(
         [first_ring],
         lambda mixed, *blocks: block_product(mixed, blocks),
         mixed_low,
         *attention_gather.blocks,
-    )
-    gate_sum = lax.psum_scatter(gate_part, "rep", scatter_dimension=0, tiled=True)
-    up_sum = lax.psum_scatter(up_part, "rep", scatter_dimension=0, tiled=True)
-    (small_swapped, output_part), head_part = window(
+        waits=tuple(chains[:-1]),
+    )
+    swaps = [chain_swap(part) for part in chains[:-1]]
+    (output_part, down_total), last, *swaps = window(
         [first_ring],
-        lambda output, *small: (small_swap(small), rep_scatter(output, 0, scatter_order[:1])),
+        lambda output, down: (
+            rep_scatter(output, 0, scatter_order[:1]),
+            down.astype(wide_type),
+        ),
         output_part.reshape(replica_count, share, model_width),
+        down_sum,
+        waits=(chains[-1], *swaps),
+    )
+    gathers = [chain_gather(part) for part in swaps]
+    last = chain_swap(last)
+    (output_part, small_swapped, gate_total, layer_out), last, *gathers = window(
+        [first_ring],
+        lambda output, total, sums, *small: (
+            rep_scatter(output, 0, scatter_order[1:]),
+            small_swap(small),
+            split_experts(total),
+            (valid_own * (residual + sums)).astype(low_type),
+        ),
+        output_part,
+        gate_sum,
+        mixture,
         *small_parts,
-        waits=(head_part,),
-    )
-    head_rows = swap_all(head_part.reshape(group_count, share, 3 * width_here))
-    (output_part, small_sums), head_rows = window(
+        waits=(last, *gathers),
+    )
+    last = chain_gather(last)
+    (output_rows, small_sums), last = window(
         [first_ring],
         lambda output, small: (
-            rep_scatter(output, 0, scatter_order[1:]),
+            rep_gather(output, gather_order[:-1]),
             small_pieces(small, small_parts),
         ),
         output_part,
         small_swapped,
-        waits=(head_rows,),
-    )
-    head_rows = rep_gather(
-        head_rows.reshape(group_count, share, heads_here, 3, head_dim)
-        .transpose(3, 1, 0, 2, 4)
-        .reshape(1, 3, share, model_width),
-        gather_order[:-1],
-    )
-    output_rows, head_rows = window(
-        [first_ring],
-        lambda output: rep_gather(output, gather_order[:-1]),
-        output_part,
-        waits=(head_rows,),
-    )
+        waits=(last,),
+    )
+    head_rows = jnp.stack([*gathers, last], axis=4).reshape(-1, 3, share, model_width)
     head_rows = rep_gather(head_rows, gather_order[-1:])
     output_rows = rep_gather(output_rows, gather_order[-1:])
     first_grad = first_ring.total()
@@ -918,16 +950,7 @@
     pre_back, _ = norm_backward(token_own, inverse_one, prenorm_gain, first_grad)
     token_grad = residual_grad + pre_back
 
-    down_total = down_sum.astype(wide_type)
-    gate_total, up_total = (
-        jnp.stack(
-            [
-                total[:, e * hidden_here : (e + 1) * hidden_here].astype(wide_type)
-                for e in range(experts_here)
-            ]
-        )
-        for total in (gate_sum, up_sum)
-    )
+    up_total = split_experts(up_sum)
     return (
         layer_out,
         token_grad,

time: 697 us -> 739 us (1.060)
  other arithmetic: 90 us -> 106 us
  waiting for transfers between devices: 146 us -> 155 us
  local copies, waits for them, and re-layouts: 79.2 us -> 86.8 us
    ppermute x18 -> x21, waiting for transfers between devices: 21.6 us -> 50.8 us  [rep_exchange(): lax.ppermute(values, 'rep', [(i, i ^ distance) for i in range(count)])]
    all_to_all x7 -> x8, waiting for transfers between devices: 42.3 us -> 31.7 us  [swap_all(): return lax.all_to_all(values, 'ep', split_axis=0, concat_axis=0, tiled=True)]
    ppermute x56, waiting for transfers between devices: 82.4 us -> 72 us  [ring_shift(): return lax.ppermute(values, 'ep', pairs)]
    all_to_all x7 -> x8, starting transfers between devices: 34.2 us -> 39.6 us  [swap_all(): return lax.all_to_all(values, 'ep', split_axis=0, concat_axis=0, tiled=True)]
    dot_general x26 -> x27, matrix products: 128 us -> 133 us  [mm(): lax.dot_general(left, right, (((left_dim,), (right_dim,)), ((), ())), pre...]
    convert_element_type x14 -> x16, other arithmetic: 26.5 us -> 30.8 us  [add_low(): return (left.astype(wide_type) + right.astype(wide_type)).astype(low_type)]
    ppermute x18 -> x21, starting transfers between devices: 15.1 us -> 17.1 us  [rep_exchange(): lax.ppermute(values, 'rep', [(i, i ^ distance) for i in range(count)])]
    unnamed x316 -> x338, local copies, waits for them, and re-layouts: 30.6 us -> 32 us
  transfers between devices with their start and end apart: 85 -> 89, of which waited for: 28 -> 31; matrix products, arithmetic and copies ran while one was open for 38% -> 37% of each run, Pallas kernels for 10% -> 10%
where the time goes in v11:
time: 739 us; the launch traced here: 729 us
  waiting for transfers between devices  155 us (21%)
  matrix products  133 us (18%)
  starting transfers between devices  123 us (17%)
  Pallas kernels  108 us (15%)
  other arithmetic  106 us (14%)
  local copies, waits for them, and re-layouts  86.8 us (12%)
  between operations  17.4 us (2%)
    dot_general x27, matrix products, mm(): lax.dot_general(left, right, (((left_dim,), (right_dim,)), ((), ())), pre...  133 us
    ppermute x56, waiting for transfers between devices, ring_shift(): return lax.ppermute(values, 'ep', pairs)  72 us
    ppermute x56, starting transfers between devices, ring_shift(): return lax.ppermute(values, 'ep', pairs)  66.4 us
    ppermute x21, waiting for transfers between devices, rep_exchange(): lax.ppermute(values, 'rep', [(i, i ^ distance) for i in range(count)])  50.8 us
    all_to_all x8, starting transfers between devices, swap_all(): return lax.all_to_all(values, 'ep', split_axis=0, concat_axis=0, tiled=True)  39.6 us
    pallas_call x2, Pallas kernels, expert_pass(): pl.pallas_call(expert_kernel, grid=(experts, steps), in_specs=[pl.BlockSp...  39 us
    pallas_call x2, Pallas kernels, expert_back(): pl.pallas_call(expert_back_kernel, grid=(depth // width,), in_specs=[whol...  33.6 us
    unnamed x338, local copies, waits for them, and re-layouts  32 us
  transfers between devices with their start and end apart: 89, of which 31 were waited for; matrix products, arithmetic and copies ran while one was open for 37% of the time, Pallas kernels for 10%

profile of v11, /device:TPU:0, one launch (start us, length us, event | category | flops | bytes accessed | tf_op | source)
XLA Modules:
  0.0 729.0 jit_solution(1330417802679786145)
XLA Ops:
  11.5 7.3 all-to-all-start
  19.9 19.0 %all-to-all-done = bf16[8,64,768]{2,1,0:T(8,128)(2,1)S(1)} async-done(((bf16[8,64,768]{2,1,0:T(8,128)(2,1)}), bf16[8,64,768]{2,1,0:T(8,128)(2,1)S(1)}, u32[]{:S(2)}, u32[]{:S(2)}) %all-to-all-start) | async-done | bytes 786464 | tf_op jit(solution)/shard_map/all_to_all | solution.py:250
  47.2 9.8 %collective-permute-done.4 = bf16[160,2048]{1,0:T(8,128)(2,1)} collective-permute-done((bf16[160,2048]{1,0:T(8,128)(2,1)S(1)}, bf16[160,2048]{1,0:T(8,128)(2,1)}, u32[]{:S(2)}, u32[]{:S(2)}) %collective-permute-start.4) | collective-permute-done | bytes 655392 | tf_op jit(solution)/shard_map/ppermute | solution.py:88
  59.9 4.1 all-to-all-start.2
  66.0 3.7 multiply_cosine_fusion
  79.4 10.4 %collective-permute-done.1 = bf16[160,2048]{1,0:T(8,128)(2,1)} collective-permute-done((bf16[160,2048]{1,0:T(8,128)(2,1)}, bf16[160,2048]{1,0:T(8,128)(2,1)}, u32[]{:S(2)}, u32[]{:S(2)}) %collective-permute-start.1) | collective-permute-done | bytes 655392 | tf_op jit(solution)/shard_map/ppermute | solution.py:88
  89.7 8.3 %collective-permute-start.2 = (bf16[160,2048]{1,0:T(8,128)(2,1)}, bf16[160,2048]{1,0:T(8,128)(2,1)S(1)}, u32[]{:S(2)}, u32[]{:S(2)}) collective-permute-start(bf16[160,2048]{1,0:T(8,128)(2,1)} %collective-permute-done.1), channel_id=1, source_target_pairs={{0,2},{2,4},{4,6},{6,7},{7,5},{5,3},{3,1},{1,0},{8,10},{10,12},{12... | collective-permute-start | bytes 1966088 | tf_op jit(solution)/shard_map/ppermute | solution.py:88
  98.0 2.5 collective-permute-done.5
  102.9 10.9 %collective-permute-done.6 = bf16[160,2048]{1,0:T(8,128)(2,1)S(1)} collective-permute-done((bf16[160,2048]{1,0:T(8,128)(2,1)}, bf16[160,2048]{1,0:T(8,128)(2,1)S(1)}, u32[]{:S(2)}, u32[]{:S(2)}) %collective-permute-start.6) | collective-permute-done | bytes 655392 | tf_op jit(solution)/shard_map/ppermute | solution.py:88
  136.9 4.3 fusion.78.query_raw_ref.key_raw_ref
  168.4 4.0 collective-permute-done.16
  177.6 6.1 collective-permute-done.19
  184.8 4.4 all-to-all-start.1
  191.1 2.3 constant_dynamic-update-slice_fusion.44
  198.8 6.5 all-to-all-done.1
  217.6 7.4 %fusion.79.stream_ref = f32[640,2048]{1,0:T(8,128)} fusion(bf16[640,2048]{1,0:T(8,128)(2,1)S(1)} %copy-done.30, bf16[2048,2048]{1,0:T(8,128)(2,1)S(1)} %bitcast.298), kind=kOutput, calls=%fused_computation.349 | convolution fusion | flops 5368709120 | bytes 16252928 | tf_op jit(solution)/shard_map/dot_general | solution.py:60
  226.1 4.2 collective-permute-done.24
  232.3 9.0 %fusion.80.stream_ref = f32[640,2048]{1,0:T(8,128)} fusion(bf16[640,2048]{1,0:T(8,128)(2,1)} %get-tuple-element.238, bf16[2048,2048]{1,0:T(8,128)(2,1)S(1)} %bitcast.299), kind=kOutput, calls=%fused_computation.350 | convolution fusion | flops 5368709120 | bytes 16252928 | tf_op jit(solution)/shard_map/dot_general | solution.py:60
  241.4 2.6 collective-permute-done.26
  251.8 19.4 %shard_map.281 = (bf16[1280,2048]{1,0:T(8,128)(2,1)}, bf16[1280,2048]{1,0:T(8,128)(2,1)}, bf16[1280,2048]{1,0:T(8,128)(2,1)}, f32[2,640,128]{2,1,0:T(8,128)}) custom-call(bf16[640,2048]{1,0:T(8,128)(2,1)} %copy-done.31, bf16[2,2048,1024]{2,1,0:T(8,128)(2,1)} %gate_ref.7, bf16[2,2048,1024]{2,1,0:T(8,128)(2,1)} %up_ref.7, f32[640,2048]{1,0:T(8,128)} %fusion.79.stream_ref, ...), custom_call_target="tpu_custom_call" | custom-call | flops 10737418240 | bytes 42991616 | tf_op jit(solution)/shard_map/pallas_call | solution.py:294
  275.7 2.7 collective-permute-done.30
  285.1 19.5 %shard_map.282 = (bf16[1280,2048]{1,0:T(8,128)(2,1)}, bf16[1280,2048]{1,0:T(8,128)(2,1)}, bf16[1280,2048]{1,0:T(8,128)(2,1)}, f32[2,640,128]{2,1,0:T(8,128)}) custom-call(bf16[640,2048]{1,0:T(8,128)(2,1)} %copy-done.26, bf16[2,2048,1024]{2,1,0:T(8,128)(2,1)} %gate_ref.7, ...), custom_call_target="tpu_custom_call", output_to_operand_aliasing={{0}: (5, {}), {1}: (6, {}), {2}: (7, {})} | custom-call | flops 10737418240 | bytes 42991616 | tf_op jit(solution)/shard_map/pallas_call | solution.py:294
  306.7 16.8 %shard_map.283 = bf16[640,2048]{1,0:T(8,128)(2,1)} custom-call(bf16[1280,2048]{1,0:T(8,128)(2,1)} %get-tuple-element.281.gback_ref, bf16[1280,2048]{1,0:T(8,128)(2,1)} %get-tuple-element.290.uback_ref, bf16[2,2048,1024]{2,1,0:T(8,128)(2,1)} %gate_ref.7, bf16[2,2048,1024]{2,1,0:T(8,128)(2,1)} %up_ref.7), custom_call_target="tpu_custom_call" | custom-call | flops 10737418240 | bytes 24641536 | tf_op jit(solution)/shard_map/pallas_call | solution.py:334
  327.9 3.3 all-to-all-start.3
  331.3 16.5 %convolution_convert_fusion.3 = bf16[1280,2048]{1,0:T(8,128)(2,1)} fusion(bf16[1280,2048]{1,0:T(8,128)(2,1)} %get-tuple-element.274, bf16[2048,2048]{1,0:T(8,128)(2,1)} %bitcast.295), kind=kOutput, calls=%fused_computation.17 | convolution fusion | flops 10740039680 | bytes 18874368 | tf_op jit(solution)/shard_map/dot_general | solution.py:60
  357.0 16.8 %shard_map.284 = bf16[640,2048]{1,0:T(8,128)(2,1)} custom-call(bf16[1280,2048]{1,0:T(8,128)(2,1)} %get-tuple-element.281.gback_ref, bf16[1280,2048]{1,0:T(8,128)(2,1)} %get-tuple-element.290.uback_ref, bf16[2,2048,1024]{2,1,0:T(8,128)(2,1)} %gate_ref.7, bf16[2,2048,1024]{2,1,0:T(8,128)(2,1)} %up_ref.7), custom_call_target="tpu_custom_call" | custom-call | flops 10737418240 | bytes 24641536 | tf_op jit(solution)/shard_map/pallas_call | solution.py:334
  373.8 2.4 add_convert_fusion.10
  385.2 15.7 %convolution_convert_fusion.2 = bf16[2048,2048]{1,0:T(8,128)(2,1)} fusion(bf16[1280,2048]{1,0:T(8,128)(2,1)S(1)} %bitcast.188, bf16[1280,2048]{1,0:T(8,128)(2,1)} %get-tuple-element.545), kind=kOutput, calls=%fused_computation.16 | convolution fusion | flops 10741612544 | bytes 18874368 | tf_op jit(solution)/shard_map/dot_general | solution.py:60
  403.6 4.7 collective-permute-done.38
  408.4 3.4 add_convert_fusion.6
  413.9 2.7 add_convert_fusion.8
  418.8 18.3 %convolution_convert_fusion.1 = bf16[2048,2048]{1,0:T(8,128)(2,1)} fusion(bf16[1280,2048]{1,0:T(8,128)(2,1)} %get-tuple-element.541, bf16[1280,2048]{1,0:T(8,128)(2,1)} %get-tuple-element.281.gback_ref), kind=kOutput, calls=%fused_computation.15 | convolution fusion | flops 10741612544 | bytes 18874368 | tf_op jit(solution)/shard_map/dot_general | solution.py:60
  447.4 2.6 convolution_add_fusion.1
  450.0 2.4 fusion.34
  452.4 2.6 fusion.13
  460.5 5.1 all-to-all-start.4
  465.8 16.7 %convolution_convert_fusion = bf16[2048,2048]{1,0:T(8,128)(2,1)} fusion(bf16[1280,2048]{1,0:T(8,128)(2,1)} %get-tuple-element.541, bf16[1280,2048]{1,0:T(8,128)(2,1)} %get-tuple-element.290.uback_ref), kind=kOutput, calls=%fused_computation.14 | convolution fusion | flops 10741612544 | bytes 18874368 | tf_op jit(solution)/shard_map/dot_general | solution.py:60
  482.5 2.5 all-to-all-done.4.swapped_ref
  491.3 14.6 %shard_map.285 = (bf16[1280,768]{1,0:T(8,128)(2,1)}, f32[2,128]{1,0:T(2,128)}) custom-call(s32[8]{0:T(128)} %stack.171.order_ref, bf16[1280,128]{1,0:T(8,128)(2,1)} %copy-done.52, bf16[1280,128]{1,0:T(8,128)(2,1)} %copy-done.51, bf16[1280,128]{1,0:T(8,128)(2,1)} %slice.518.value_ref, bf16[8,160,256]{2,1,0:T(8,128)(2,1)} %copy-done.13, ...), custom_call_target="tpu_custom_call" | custom-call | flops 2097152000 | bytes 4915200 | tf_op jit(solution)/shard_map/pallas_call | solution.py:421
  506.8 2.4 collective-permute-start.53
  509.2 5.7 convolution_convert_fusion.5
  514.9 13.6 %shard_map.286 = (bf16[1280,768]{1,0:T(8,128)(2,1)}, f32[2,128]{1,0:T(2,128)}) custom-call(s32[8]{0:T(128)} %stack.171.order_ref, bf16[1280,128]{1,0:T(8,128)(2,1)} %copy-done.50, bf16[1280,128]{1,0:T(8,128)(2,1)} %copy-done.49, bf16[1280,128]{1,0:T(8,128)(2,1)} %slice.517.value_ref, ...), custom_call_target="tpu_custom_call", output_to_operand_aliasing={{0}: (13, {})} | custom-call | flops 2097152000 | bytes 4915200 | tf_op jit(solution)/shard_map/pallas_call | solution.py:421
  530.4 3.6 fusion.5
  536.4 2.5 collective-permute-start.59
  539.0 2.5 convert_add_fusion.3
  544.3 12.9 %collective-permute-done.59 = bf16[8,1,64,384]{3,2,0,1:T(8,128)(2,1)S(1)} collective-permute-done((bf16[8,1,64,384]{3,2,0,1:T(8,128)(2,1)S(1)}, bf16[8,1,64,384]{3,2,0,1:T(8,128)(2,1)S(1)}, u32[]{:S(2)}, u32[]{:S(2)}) %collective-permute-start.59) | collective-permute-done | bytes 393248 | tf_op jit(solution)/shard_map/ppermute | solution.py:204
  558.1 9.1 %fusion.4 = (f32[2048]{0:T(1024)}, bf16[1280,2048]{1,0:T(8,128)(2,1)S(1)}) fusion(bf16[1280,2048]{1,0:T(8,128)(2,1)} %copy-done.3, f32[1280]{0:T(1024)S(1)} %add_rsqrt_fusion, bf16[1280,768]{1,0:T(8,128)(2,1)} %get-tuple-element.322, bf16[2048,768]{1,0:T(8,128)(2,1)} %bitcast.206), kind=kOutput, calls=%fused_computation.8 | convolution fusion | flops 4039636992 | bytes 15610880 | tf_op jit(solution)/shard_map/dot_general | solution.py:60
  570.3 6.1 convolution_convert_fusion.4
  578.4 7.2 shard_map.287
  594.0 2.5 convert_element_type.510
  596.5 5.6 all-to-all-start.5
  607.0 16.6 %collective-permute-done.63 = bf16[8,1,64,384]{3,2,0,1:T(8,128)(2,1)S(1)} collective-permute-done((bf16[8,1,64,384]{3,2,0,1:T(8,128)(2,1)S(1)}, bf16[8,1,64,384]{3,2,0,1:T(8,128)(2,1)S(1)}, u32[]{:S(2)}, u32[]{:S(2)}) %collective-permute-start.63) | collective-permute-done | bytes 393248 | tf_op jit(solution)/shard_map/ppermute | solution.py:204
  624.4 3.4 add_convert_fusion.2
  633.5 6.0 all-to-all-start.7
  641.9 2.3 multiply_convert_fusion
  645.0 3.6 all-to-all-done.7
  648.6 4.0 all-to-all-start.6
  656.8 6.8 collective-permute-done.67
  665.9 3.4 add_convert_fusion
  677.8 4.6 collective-permute-done.72
  683.3 8.6 %collective-permute-done.71 = bf16[1,3,64,8,128]{4,1,2,3,0:T(4,128)(2,1)S(1)} collective-permute-done((bf16[1,3,64,8,128]{4,1,2,3,0:T(4,128)(2,1)S(1)}, bf16[1,3,64,8,128]{4,1,2,3,0:T(4,128)(2,1)S(1)}, u32[]{:S(2)}, u32[]{:S(2)}) %collective-permute-start.71) | collective-permute-done | bytes 393248 | tf_op jit(solution)/shard_map/ppermute | solution.py:204
  700.2 2.4 reshape.531
  702.6 2.4 stack_reshape.18
  708.1 2.9 fusion.21
  (702 shorter events, 255.4 us)
Async XLA Ops:
  11.5 27.4 %all-to-all-start = ((bf16[8,64,768]{2,1,0:T(8,128)(2,1)}), bf16[8,64,768]{2,1,0:T(8,128)(2,1)S(1)}, u32[]{:S(2)}, u32[]{:S(2)}) async-start(bf16[8,64,768]{2,1,0:T(8,128)(2,1)} %copy.136), calls=%async_computation | async-start | bytes 1572864 | tf_op jit(solution)/shard_map/all_to_all | solution.py:250
  18.7 96.6 %all-gather.2.cloned.1.call-start = ((), (), s32[]{:S(2)}) async-start(), calls=%async_computation.11 | async-start | bytes 2359296 | tf_op jit(solution)/shard_map/all_gather | solution.py:69
  38.9 18.2 %collective-permute-start.4 = (bf16[160,2048]{1,0:T(8,128)(2,1)S(1)}, bf16[160,2048]{1,0:T(8,128)(2,1)}, u32[]{:S(2)}, u32[]{:S(2)}) collective-permute-start(bf16[160,2048]{1,0:T(8,128)(2,1)S(1)} %copy-done.8), channel_id=1, source_target_pairs={{0,1},{2,0},{4,2},{6,4},{7,6},{5,7},{3,5},{1,3},{8,9},{10,8},{12,1... | collective-permute-start | bytes 1966088 | tf_op jit(solution)/shard_map/ppermute | solution.py:88
  40.3 18.9 %collective-permute-start = (bf16[160,2048]{1,0:T(8,128)(2,1)S(1)}, bf16[160,2048]{1,0:T(8,128)(2,1)}, u32[]{:S(2)}, u32[]{:S(2)}) collective-permute-start(bf16[160,2048]{1,0:T(8,128)(2,1)S(1)} %copy-done.8), channel_id=1, source_target_pairs={{0,2},{2,4},{4,6},{6,7},{7,5},{5,3},{3,1},{1,0},{8,10},{10,12},{12... | collective-permute-start | bytes 1966088 | tf_op jit(solution)/shard_map/ppermute | solution.py:88
  45.7 24.0 %collective-permute-start.11 = (bf16[1,8,64,768]{3,2,1,0:T(8,128)(2,1)S(1)}, bf16[1,8,64,768]{3,2,1,0:T(8,128)(2,1)S(1)}, u32[]{:S(2)}, u32[]{:S(2)}) collective-permute-start(bf16[1,8,64,768]{3,2,1,0:T(8,128)(2,1)S(1)} %bitcast.184), channel_id=1, source_target_pairs={{0,16},{8,24},{16,0},{24,8},{1,17},{9,25},{17,1},{25,9},{2,18},{10... | collective-permute-start | bytes 2359304 | tf_op jit(solution)/shard_map/ppermute | solution.py:204
  64.0 25.8 %collective-permute-start.1 = (bf16[160,2048]{1,0:T(8,128)(2,1)}, bf16[160,2048]{1,0:T(8,128)(2,1)}, u32[]{:S(2)}, u32[]{:S(2)}) collective-permute-start(bf16[160,2048]{1,0:T(8,128)(2,1)} %collective-permute-done), channel_id=1, source_target_pairs={{0,2},{2,4},{4,6},{6,7},{7,5},{5,3},{3,1},{1,0},{8,10},{10,12},{12... | collective-permute-start | bytes 1966088 | tf_op jit(solution)/shard_map/ppermute | solution.py:88
  66.0 34.5 %collective-permute-start.5 = (bf16[160,2048]{1,0:T(8,128)(2,1)}, bf16[160,2048]{1,0:T(8,128)(2,1)}, u32[]{:S(2)}, u32[]{:S(2)}) collective-permute-start(bf16[160,2048]{1,0:T(8,128)(2,1)} %collective-permute-done.4), channel_id=1, source_target_pairs={{0,1},{2,0},{4,2},{6,4},{7,6},{5,7},{3,5},{1,3},{8,9},{10,8},{12,1... | collective-permute-start | bytes 1966088 | tf_op jit(solution)/shard_map/ppermute | solution.py:88
  71.1 45.6 %collective-permute-start.12 = (bf16[2,8,64,768]{3,2,1,0:T(8,128)(2,1)}, bf16[2,8,64,768]{3,2,1,0:T(8,128)(2,1)}, u32[]{:S(2)}, u32[]{:S(2)}) collective-permute-start(bf16[2,8,64,768]{3,2,1,0:T(8,128)(2,1)} %maximum_select_fusion.3), channel_id=1, source_target_pairs={{0,8},{8,0},{16,24},{24,16},{1,9},{9,1},{17,25},{25,17},{2,10},{10... | collective-permute-start | bytes 4718600 | tf_op jit(solution)/shard_map/ppermute | solution.py:204
  89.7 25.6 %collective-permute-start.2 = (bf16[160,2048]{1,0:T(8,128)(2,1)}, bf16[160,2048]{1,0:T(8,128)(2,1)S(1)}, u32[]{:S(2)}, u32[]{:S(2)}) collective-permute-start(bf16[160,2048]{1,0:T(8,128)(2,1)} %collective-permute-done.1), channel_id=1, source_target_pairs={{0,2},{2,4},{4,6},{6,7},{7,5},{5,3},{3,1},{1,0},{8,10},{10,12},{12... | collective-permute-start | bytes 1966088 | tf_op jit(solution)/shard_map/ppermute | solution.py:88
  120.8 20.5 %collective-permute-start.10 = (bf16[512,512]{1,0:T(8,128)(2,1)S(1)}, bf16[512,512]{1,0:T(8,128)(2,1)S(1)}, u32[]{:S(2)}, u32[]{:S(2)}) collective-permute-start(bf16[512,512]{1,0:T(8,128)(2,1)S(1)} %get-tuple-element.508), channel_id=1, source_target_pairs={{0,16},{8,24},{16,0},{24,8},{1,17},{9,25},{17,1},{25,9},{2,18},{10... | collective-permute-start | bytes 1572872 | tf_op jit(solution)/shard_map/ppermute | solution.py:204
  122.4 32.5 %collective-permute-start.15 = (bf16[512,512]{1,0:T(8,128)(2,1)S(1)}, bf16[512,512]{1,0:T(8,128)(2,1)S(1)}, u32[]{:S(2)}, u32[]{:S(2)}) collective-permute-start(bf16[512,512]{1,0:T(8,128)(2,1)S(1)} %get-tuple-element.507), channel_id=1, source_target_pairs={{0,16},{8,24},{16,0},{24,8},{1,17},{9,25},{17,1},{25,9},{2,18},{10... | collective-permute-start | bytes 1572872 | tf_op jit(solution)/shard_map/ppermute | solution.py:204
  122.9 45.5 %collective-permute-start.18 = (bf16[512,512]{1,0:T(8,128)(2,1)S(1)}, bf16[512,512]{1,0:T(8,128)(2,1)S(1)}, u32[]{:S(2)}, u32[]{:S(2)}) collective-permute-start(bf16[512,512]{1,0:T(8,128)(2,1)S(1)} %get-tuple-element.506), channel_id=1, source_target_pairs={{0,16},{8,24},{16,0},{24,8},{1,17},{9,25},{17,1},{25,9},{2,18},{10... | collective-permute-start | bytes 1572872 | tf_op jit(solution)/shard_map/ppermute | solution.py:204
  126.0 16.8 %collective-permute-start.8 = (bf16[160,2048]{1,0:T(8,128)(2,1)S(1)}, bf16[160,2048]{1,0:T(8,128)(2,1)S(1)}, u32[]{:S(2)}, u32[]{:S(2)}) collective-permute-start(bf16[160,2048]{1,0:T(8,128)(2,1)S(1)} %copy-done.14), channel_id=1, source_target_pairs={{0,2},{2,4},{4,6},{6,7},{7,5},{5,3},{3,1},{1,0},{8,10},{10,12},{12... | collective-permute-start | bytes 1966088 | tf_op jit(solution)/shard_map/ppermute | solution.py:88
  141.3 36.2 %collective-permute-start.21 = (bf16[512,512]{1,0:T(8,128)(2,1)S(1)}, bf16[512,512]{1,0:T(8,128)(2,1)}, u32[]{:S(2)}, u32[]{:S(2)}) collective-permute-start(bf16[512,512]{1,0:T(8,128)(2,1)S(1)} %get-tuple-element.505), channel_id=1, source_target_pairs={{0,16},{8,24},{16,0},{24,8},{1,17},{9,25},{17,1},{25,9},{2,18},{10... | collective-permute-start | bytes 1572872 | tf_op jit(solution)/shard_map/ppermute | solution.py:204
  154.9 54.5 %collective-permute-start.22 = (bf16[2048,512]{1,0:T(8,128)(2,1)S(1)}, bf16[2048,512]{1,0:T(8,128)(2,1)}, u32[]{:S(2)}, u32[]{:S(2)}) collective-permute-start(bf16[2048,512]{1,0:T(8,128)(2,1)S(1)} %copy-done.6), channel_id=1, source_target_pairs={{0,8},{8,0},{16,24},{24,16},{1,9},{9,1},{17,25},{25,17},{2,10},{10... | collective-permute-start | bytes 6291464 | tf_op jit(solution)/shard_map/ppermute | solution.py:204
  155.9 16.5 %collective-permute-start.16 = (bf16[160,2048]{1,0:T(8,128)(2,1)S(1)}, bf16[160,2048]{1,0:T(8,128)(2,1)S(1)}, u32[]{:S(2)}, u32[]{:S(2)}) collective-permute-start(bf16[160,2048]{1,0:T(8,128)(2,1)S(1)} %collective-permute-done.13), channel_id=1, source_target_pairs={{0,2},{2,4},{4,6},{6,7},{7,5},{5,3},{3,1},{1,0},{8,10},{10,12},{12... | collective-permute-start | bytes 1966088 | tf_op jit(solution)/shard_map/ppermute | solution.py:88
  157.1 17.1 %collective-permute-start.17 = (bf16[160,2048]{1,0:T(8,128)(2,1)S(1)}, bf16[160,2048]{1,0:T(8,128)(2,1)S(1)}, u32[]{:S(2)}, u32[]{:S(2)}) collective-permute-start(bf16[160,2048]{1,0:T(8,128)(2,1)S(1)} %collective-permute-done.14), channel_id=1, source_target_pairs={{0,1},{2,0},{4,2},{6,4},{7,6},{5,7},{3,5},{1,3},{8,9},{10,8},{12,1... | collective-permute-start | bytes 1966088 | tf_op jit(solution)/shard_map/ppermute | solution.py:88
  184.8 20.5 %all-to-all-start.1 = ((bf16[8,160,256]{2,1,0:T(8,128)(2,1)}), bf16[8,160,256]{2,1,0:T(8,128)(2,1)}, u32[]{:S(2)}, u32[]{:S(2)}) async-start(bf16[8,160,256]{2,1,0:T(8,128)(2,1)} %copy-done.55), calls=%async_computation.1 | async-start | bytes 1310720 | tf_op jit(solution)/shard_map/all_to_all | solution.py:250
  191.1 20.6 %collective-permute-start.23 = (bf16[2048,512]{1,0:T(8,128)(2,1)}, bf16[2048,512]{1,0:T(8,128)(2,1)}, u32[]{:S(2)}, u32[]{:S(2)}) collective-permute-start(bf16[2048,512]{1,0:T(8,128)(2,1)} %constant_dynamic-update-slice_fusion.18), channel_id=1, source_target_pairs={{0,8},{8,0},{16,24},{24,16},{1,9},{9,1},{17,25},{25,17},{2,10},{10... | collective-permute-start | bytes 6291464 | tf_op jit(solution)/shard_map/ppermute | solution.py:204
  246.0 25.3 %collective-permute-start.29 = (bf16[160,2048]{1,0:T(8,128)(2,1)S(1)}, bf16[160,2048]{1,0:T(8,128)(2,1)S(1)}, u32[]{:S(2)}, u32[]{:S(2)}) collective-permute-start(bf16[160,2048]{1,0:T(8,128)(2,1)S(1)} %collective-permute-done.27), channel_id=1, source_target_pairs={{0,1},{2,0},{4,2},{6,4},{7,6},{5,7},{3,5},{1,3},{8,9},{10,8},{12,1... | collective-permute-start | bytes 1966088 | tf_op jit(solution)/shard_map/ppermute | solution.py:88
  246.5 24.8 %collective-permute-start.28 = (bf16[160,2048]{1,0:T(8,128)(2,1)S(1)}, bf16[160,2048]{1,0:T(8,128)(2,1)S(1)}, u32[]{:S(2)}, u32[]{:S(2)}) collective-permute-start(bf16[160,2048]{1,0:T(8,128)(2,1)S(1)} %collective-permute-done.26), channel_id=1, source_target_pairs={{0,2},{2,4},{4,6},{6,7},{7,5},{5,3},{3,1},{1,0},{8,10},{10,12},{12... | collective-permute-start | bytes 1966088 | tf_op jit(solution)/shard_map/ppermute | solution.py:88
  324.8 23.0 %collective-permute-start.32 = (bf16[80,2048]{1,0:T(8,128)(2,1)S(1)}, bf16[80,2048]{1,0:T(8,128)(2,1)S(1)}, u32[]{:S(2)}, u32[]{:S(2)}) collective-permute-start(bf16[80,2048]{1,0:T(8,128)(2,1)S(1)} %get-tuple-element.498), channel_id=1, source_target_pairs={{0,2},{2,4},{4,6},{6,7},{7,5},{5,3},{3,1},{1,0},{8,10},{10,12},{12... | collective-permute-start | bytes 983048 | tf_op jit(solution)/shard_map/ppermute | solution.py:88
  326.6 21.2 %collective-permute-start.33 = (bf16[80,2048]{1,0:T(8,128)(2,1)S(1)}, bf16[80,2048]{1,0:T(8,128)(2,1)}, u32[]{:S(2)}, u32[]{:S(2)}) collective-permute-start(bf16[80,2048]{1,0:T(8,128)(2,1)S(1)} %get-tuple-element.497), channel_id=1, source_target_pairs={{0,1},{2,0},{4,2},{6,4},{7,6},{5,7},{3,5},{1,3},{8,9},{10,8},{12,1... | collective-permute-start | bytes 983048 | tf_op jit(solution)/shard_map/ppermute | solution.py:88
  327.9 19.9 %all-to-all-start.3 = ((f32[8,160,2]{1,2,0:T(2,128)}), f32[8,160,2]{1,2,0:T(2,128)S(1)}, u32[]{:S(2)}, u32[]{:S(2)}) async-start(f32[8,160,2]{1,2,0:T(2,128)} %copy.170), calls=%async_computation.3 | async-start | bytes 32768 | tf_op jit(solution)/shard_map/all_to_all | solution.py:250
  331.3 226.8 %reduce-scatter.4.cloned.1.call-start = ((), (), s32[]{:S(2)}) async-start(), calls=%async_computation.12 | async-start | bytes 10485760 | tf_op jit(solution)/shard_map/reduce_scatter | solution.py:835
  351.6 22.2 %collective-permute-start.35 = (bf16[160,2048]{1,0:T(8,128)(2,1)S(1)}, bf16[160,2048]{1,0:T(8,128)(2,1)}, u32[]{:S(2)}, u32[]{:S(2)}) collective-permute-start(bf16[160,2048]{1,0:T(8,128)(2,1)S(1)} %pad_maximum_fusion.8), channel_id=1, source_target_pairs={{0,1},{2,0},{4,2},{6,4},{7,6},{5,7},{3,5},{1,3},{8,9},{10,8},{12,1... | collective-permute-start | bytes 1966088 | tf_op jit(solution)/shard_map/ppermute | solution.py:88
  354.4 19.4 %collective-permute-start.34 = (bf16[160,2048]{1,0:T(8,128)(2,1)}, bf16[160,2048]{1,0:T(8,128)(2,1)}, u32[]{:S(2)}, u32[]{:S(2)}) collective-permute-start(bf16[160,2048]{1,0:T(8,128)(2,1)} %pad_maximum_fusion.7), channel_id=1, source_target_pairs={{0,2},{2,4},{4,6},{6,7},{7,5},{5,3},{3,1},{1,0},{8,10},{10,12},{12... | collective-permute-start | bytes 1966088 | tf_op jit(solution)/shard_map/ppermute | solution.py:88
  354.5 19.2 %collective-permute-start.36 = (bf16[80,2048]{1,0:T(8,128)(2,1)}, bf16[80,2048]{1,0:T(8,128)(2,1)S(1)}, u32[]{:S(2)}, u32[]{:S(2)}) collective-permute-start(bf16[80,2048]{1,0:T(8,128)(2,1)} %get-tuple-element.483), channel_id=1, source_target_pairs={{0,2},{2,4},{4,6},{6,7},{7,5},{5,3},{3,1},{1,0},{8,10},{10,12},{12... | collective-permute-start | bytes 983048 | tf_op jit(solution)/shard_map/ppermute | solution.py:88
  356.4 17.3 %collective-permute-start.37 = (bf16[80,2048]{1,0:T(8,128)(2,1)}, bf16[80,2048]{1,0:T(8,128)(2,1)}, u32[]{:S(2)}, u32[]{:S(2)}) collective-permute-start(bf16[80,2048]{1,0:T(8,128)(2,1)} %get-tuple-element.482), channel_id=1, source_target_pairs={{0,1},{2,0},{4,2},{6,4},{7,6},{5,7},{3,5},{1,3},{8,9},{10,8},{12,1... | collective-permute-start | bytes 983048 | tf_op jit(solution)/shard_map/ppermute | solution.py:88
  380.1 23.3 %collective-permute-start.41 = (bf16[160,2048]{1,0:T(8,128)(2,1)S(1)}, bf16[160,2048]{1,0:T(8,128)(2,1)}, u32[]{:S(2)}, u32[]{:S(2)}) collective-permute-start(bf16[160,2048]{1,0:T(8,128)(2,1)S(1)} %pad_maximum_fusion.10), channel_id=1, source_target_pairs={{0,1},{2,0},{4,2},{6,4},{7,6},{5,7},{3,5},{1,3},{8,9},{10,8},{12,1... | collective-permute-start | bytes 1966088 | tf_op jit(solution)/shard_map/ppermute | solution.py:88
  382.9 20.5 %collective-permute-start.40 = (bf16[160,2048]{1,0:T(8,128)(2,1)}, bf16[160,2048]{1,0:T(8,128)(2,1)}, u32[]{:S(2)}, u32[]{:S(2)}) collective-permute-start(bf16[160,2048]{1,0:T(8,128)(2,1)} %pad_maximum_fusion.9), channel_id=1, source_target_pairs={{0,2},{2,4},{4,6},{6,7},{7,5},{5,3},{3,1},{1,0},{8,10},{10,12},{12... | collective-permute-start | bytes 1966088 | tf_op jit(solution)/shard_map/ppermute | solution.py:88
  383.0 20.6 %collective-permute-start.39 = (bf16[160,2048]{1,0:T(8,128)(2,1)}, bf16[160,2048]{1,0:T(8,128)(2,1)S(1)}, u32[]{:S(2)}, u32[]{:S(2)}) collective-permute-start(bf16[160,2048]{1,0:T(8,128)(2,1)} %add_convert_fusion.10), channel_id=1, source_target_pairs={{0,1},{2,0},{4,2},{6,4},{7,6},{5,7},{3,5},{1,3},{8,9},{10,8},{12,1... | collective-permute-start | bytes 1966088 | tf_op jit(solution)/shard_map/ppermute | solution.py:88
  384.9 23.4 %collective-permute-start.38 = (bf16[160,2048]{1,0:T(8,128)(2,1)}, bf16[160,2048]{1,0:T(8,128)(2,1)}, u32[]{:S(2)}, u32[]{:S(2)}) collective-permute-start(bf16[160,2048]{1,0:T(8,128)(2,1)} %add_convert_fusion.11), channel_id=1, source_target_pairs={{0,2},{2,4},{4,6},{6,7},{7,5},{5,3},{3,1},{1,0},{8,10},{10,12},{12... | collective-permute-start | bytes 1966088 | tf_op jit(solution)/shard_map/ppermute | solution.py:88
  408.3 221.5 %reduce-scatter.6.cloned.1.call-start = ((), (), s32[]{:S(2)}) async-start(), calls=%async_computation.13 | async-start | bytes 10485760 | tf_op jit(solution)/shard_map/reduce_scatter | solution.py:873
  411.8 25.2 %collective-permute-start.44 = (bf16[160,2048]{1,0:T(8,128)(2,1)}, bf16[160,2048]{1,0:T(8,128)(2,1)S(1)}, u32[]{:S(2)}, u32[]{:S(2)}) collective-permute-start(bf16[160,2048]{1,0:T(8,128)(2,1)} %get-tuple-element.479), channel_id=1, source_target_pairs={{0,2},{2,4},{4,6},{6,7},{7,5},{5,3},{3,1},{1,0},{8,10},{10,12},{12... | collective-permute-start | bytes 1966088 | tf_op jit(solution)/shard_map/ppermute | solution.py:88
  412.0 25.1 %collective-permute-start.45 = (bf16[160,2048]{1,0:T(8,128)(2,1)}, bf16[160,2048]{1,0:T(8,128)(2,1)}, u32[]{:S(2)}, u32[]{:S(2)}) collective-permute-start(bf16[160,2048]{1,0:T(8,128)(2,1)} %get-tuple-element.478), channel_id=1, source_target_pairs={{0,1},{2,0},{4,2},{6,4},{7,6},{5,7},{3,5},{1,3},{8,9},{10,8},{12,1... | collective-permute-start | bytes 1966088 | tf_op jit(solution)/shard_map/ppermute | solution.py:88
  416.6 21.4 %collective-permute-start.42 = (bf16[160,2048]{1,0:T(8,128)(2,1)}, bf16[160,2048]{1,0:T(8,128)(2,1)S(1)}, u32[]{:S(2)}, u32[]{:S(2)}) collective-permute-start(bf16[160,2048]{1,0:T(8,128)(2,1)} %get-tuple-element.494), channel_id=1, source_target_pairs={{0,2},{2,4},{4,6},{6,7},{7,5},{5,3},{3,1},{1,0},{8,10},{10,12},{12... | collective-permute-start | bytes 1966088 | tf_op jit(solution)/shard_map/ppermute | solution.py:88
  416.7 21.2 %collective-permute-start.43 = (bf16[160,2048]{1,0:T(8,128)(2,1)}, bf16[160,2048]{1,0:T(8,128)(2,1)S(1)}, u32[]{:S(2)}, u32[]{:S(2)}) collective-permute-start(bf16[160,2048]{1,0:T(8,128)(2,1)} %get-tuple-element.493), channel_id=1, source_target_pairs={{0,1},{2,0},{4,2},{6,4},{7,6},{5,7},{3,5},{1,3},{8,9},{10,8},{12,1... | collective-permute-start | bytes 1966088 | tf_op jit(solution)/shard_map/ppermute | solution.py:88
  440.7 16.6 %collective-permute-start.46 = (bf16[160,2048]{1,0:T(8,128)(2,1)S(1)}, bf16[160,2048]{1,0:T(8,128)(2,1)S(1)}, u32[]{:S(2)}, u32[]{:S(2)}) collective-permute-start(bf16[160,2048]{1,0:T(8,128)(2,1)S(1)} %get-tuple-element.477), channel_id=1, source_target_pairs={{0,2},{2,4},{4,6},{6,7},{7,5},{5,3},{3,1},{1,0},{8,10},{10,12},{12... | collective-permute-start | bytes 1966088 | tf_op jit(solution)/shard_map/ppermute | solution.py:88
  440.9 16.5 %collective-permute-start.47 = (bf16[160,2048]{1,0:T(8,128)(2,1)S(1)}, bf16[160,2048]{1,0:T(8,128)(2,1)S(1)}, u32[]{:S(2)}, u32[]{:S(2)}) collective-permute-start(bf16[160,2048]{1,0:T(8,128)(2,1)S(1)} %get-tuple-element.476), channel_id=1, source_target_pairs={{0,1},{2,0},{4,2},{6,4},{7,6},{5,7},{3,5},{1,3},{8,9},{10,8},{12,1... | collective-permute-start | bytes 1966088 | tf_op jit(solution)/shard_map/ppermute | solution.py:88
  458.2 24.3 %collective-permute-start.48 = (bf16[160,2048]{1,0:T(8,128)(2,1)S(1)}, bf16[160,2048]{1,0:T(8,128)(2,1)}, u32[]{:S(2)}, u32[]{:S(2)}) collective-permute-start(bf16[160,2048]{1,0:T(8,128)(2,1)S(1)} %get-tuple-element.330.refs_0_), channel_id=1, source_target_pairs={{0,2},{2,4},{4,6},{6,7},{7,5},{5,3},{3,1},{1,0},{8,10},{10,12},{12... | collective-permute-start | bytes 1966088 | tf_op jit(solution)/shard_map/ppermute | solution.py:88
  459.1 23.4 %collective-permute-start.49 = (bf16[160,2048]{1,0:T(8,128)(2,1)S(1)}, bf16[160,2048]{1,0:T(8,128)(2,1)}, u32[]{:S(2)}, u32[]{:S(2)}) collective-permute-start(bf16[160,2048]{1,0:T(8,128)(2,1)S(1)} %get-tuple-element.330.refs_0_), channel_id=1, source_target_pairs={{0,1},{2,0},{4,2},{6,4},{7,6},{5,7},{3,5},{1,3},{8,9},{10,8},{12,1... | collective-permute-start | bytes 1966088 | tf_op jit(solution)/shard_map/ppermute | solution.py:88
  460.5 24.6 %all-to-all-start.4 = ((bf16[8,160,256]{2,1,0:T(8,128)(2,1)}), bf16[8,160,256]{2,1,0:T(8,128)(2,1)S(1)}, u32[]{:S(2)}, u32[]{:S(2)}) async-start(bf16[8,160,256]{2,1,0:T(8,128)(2,1)} %bitcast.209), calls=%async_computation.4 | async-start | bytes 1310720 | tf_op jit(solution)/shard_map/all_to_all | solution.py:250
  465.6 227.2 %reduce-scatter.8.cloned.1.call-start = ((), (), s32[]{:S(2)}) async-start(), calls=%async_computation.14 | async-start | bytes 10485760 | tf_op jit(solution)/shard_map/reduce_scatter | solution.py:874
  485.9 20.0 %collective-permute-start.50 = (bf16[160,2048]{1,0:T(8,128)(2,1)}, bf16[160,2048]{1,0:T(8,128)(2,1)S(1)}, u32[]{:S(2)}, u32[]{:S(2)}) collective-permute-start(bf16[160,2048]{1,0:T(8,128)(2,1)} %collective-permute-done.48.refs_2_), channel_id=1, source_target_pairs={{0,2},{2,4},{4,6},{6,7},{7,5},{5,3},{3,1},{1,0},{8,10},{10,12},{12... | collective-permute-start | bytes 1966088 | tf_op jit(solution)/shard_map/ppermute | solution.py:88
  485.9 20.0 %collective-permute-start.51 = (bf16[160,2048]{1,0:T(8,128)(2,1)}, bf16[160,2048]{1,0:T(8,128)(2,1)S(1)}, u32[]{:S(2)}, u32[]{:S(2)}) collective-permute-start(bf16[160,2048]{1,0:T(8,128)(2,1)} %collective-permute-done.49.refs_1_), channel_id=1, source_target_pairs={{0,1},{2,0},{4,2},{6,4},{7,6},{5,7},{3,5},{1,3},{8,9},{10,8},{12,1... | collective-permute-start | bytes 1966088 | tf_op jit(solution)/shard_map/ppermute | solution.py:88
  506.8 21.7 %collective-permute-start.52 = (bf16[160,2048]{1,0:T(8,128)(2,1)}, bf16[160,2048]{1,0:T(8,128)(2,1)S(1)}, u32[]{:S(2)}, u32[]{:S(2)}) collective-permute-start(bf16[160,2048]{1,0:T(8,128)(2,1)} %copy-done.63), channel_id=1, source_target_pairs={{0,2},{2,4},{4,6},{6,7},{7,5},{5,3},{3,1},{1,0},{8,10},{10,12},{12... | collective-permute-start | bytes 1966088 | tf_op jit(solution)/shard_map/ppermute | solution.py:88
  506.8 21.7 %collective-permute-start.53 = (bf16[160,2048]{1,0:T(8,128)(2,1)S(1)}, bf16[160,2048]{1,0:T(8,128)(2,1)S(1)}, u32[]{:S(2)}, u32[]{:S(2)}) collective-permute-start(bf16[160,2048]{1,0:T(8,128)(2,1)S(1)} %collective-permute-done.51.refs_3_), channel_id=1, source_target_pairs={{0,1},{2,0},{4,2},{6,4},{7,6},{5,7},{3,5},{1,3},{8,9},{10,8},{12,1... | collective-permute-start | bytes 1966088 | tf_op jit(solution)/shard_map/ppermute | solution.py:88
  536.4 20.8 %collective-permute-start.59 = (bf16[8,1,64,384]{3,2,0,1:T(8,128)(2,1)S(1)}, bf16[8,1,64,384]{3,2,0,1:T(8,128)(2,1)S(1)}, u32[]{:S(2)}, u32[]{:S(2)}) collective-permute-start(bf16[8,1,64,384]{3,2,0,1:T(8,128)(2,1)S(1)} %constant_dynamic-slice_fusion.4), channel_id=1, source_target_pairs={{0,16},{8,24},{16,0},{24,8},{1,17},{9,25},{17,1},{25,9},{2,18},{10... | collective-permute-start | bytes 1179656 | tf_op jit(solution)/shard_map/ppermute | solution.py:204
  542.2 25.0 %collective-permute-start.54 = (bf16[80,2048]{1,0:T(8,128)(2,1)}, bf16[80,2048]{1,0:T(8,128)(2,1)S(1)}, u32[]{:S(2)}, u32[]{:S(2)}) collective-permute-start(bf16[80,2048]{1,0:T(8,128)(2,1)} %slice.394), channel_id=1, source_target_pairs={{0,2},{2,4},{4,6},{6,7},{7,5},{5,3},{3,1},{1,0},{8,10},{10,12},{12... | collective-permute-start | bytes 983048 | tf_op jit(solution)/shard_map/ppermute | solution.py:88
  542.6 24.6 %collective-permute-start.55 = (bf16[80,2048]{1,0:T(8,128)(2,1)S(1)}, bf16[80,2048]{1,0:T(8,128)(2,1)S(1)}, u32[]{:S(2)}, u32[]{:S(2)}) collective-permute-start(bf16[80,2048]{1,0:T(8,128)(2,1)S(1)} %slice.395), channel_id=1, source_target_pairs={{0,1},{2,0},{4,2},{6,4},{7,6},{5,7},{3,5},{1,3},{8,9},{10,8},{12,1... | collective-permute-start | bytes 983048 | tf_op jit(solution)/shard_map/ppermute | solution.py:88
  568.2 17.5 %collective-permute-start.56 = (bf16[80,2048]{1,0:T(8,128)(2,1)}, bf16[80,2048]{1,0:T(8,128)(2,1)}, u32[]{:S(2)}, u32[]{:S(2)}) collective-permute-start(bf16[80,2048]{1,0:T(8,128)(2,1)} %get-tuple-element.473), channel_id=1, source_target_pairs={{0,2},{2,4},{4,6},{6,7},{7,5},{5,3},{3,1},{1,0},{8,10},{10,12},{12... | collective-permute-start | bytes 983048 | tf_op jit(solution)/shard_map/ppermute | solution.py:88
  568.7 17.0 %collective-permute-start.57 = (bf16[80,2048]{1,0:T(8,128)(2,1)}, bf16[80,2048]{1,0:T(8,128)(2,1)}, u32[]{:S(2)}, u32[]{:S(2)}) collective-permute-start(bf16[80,2048]{1,0:T(8,128)(2,1)} %get-tuple-element.472), channel_id=1, source_target_pairs={{0,1},{2,0},{4,2},{6,4},{7,6},{5,7},{3,5},{1,3},{8,9},{10,8},{12,1... | collective-permute-start | bytes 983048 | tf_op jit(solution)/shard_map/ppermute | solution.py:88
  578.4 23.7 %collective-permute-start.62 = (bf16[8,2,64,384]{3,2,0,1:T(8,128)(2,1)}, bf16[8,2,64,384]{3,2,0,1:T(8,128)(2,1)}, u32[]{:S(2)}, u32[]{:S(2)}) collective-permute-start(bf16[8,2,64,384]{3,2,0,1:T(8,128)(2,1)} %bitcast.172), channel_id=1, source_target_pairs={{0,8},{8,0},{16,24},{24,16},{1,9},{9,1},{17,25},{25,17},{2,10},{10... | collective-permute-start | bytes 2359304 | tf_op jit(solution)/shard_map/ppermute | solution.py:204
  591.9 32.5 %collective-permute-start.61 = (bf16[160,2048]{1,0:T(8,128)(2,1)}, bf16[160,2048]{1,0:T(8,128)(2,1)}, u32[]{:S(2)}, u32[]{:S(2)}) collective-permute-start(bf16[160,2048]{1,0:T(8,128)(2,1)} %pad_maximum_fusion.13), channel_id=1, source_target_pairs={{0,1},{2,0},{4,2},{6,4},{7,6},{5,7},{3,5},{1,3},{8,9},{10,8},{12,1... | collective-permute-start | bytes 1966088 | tf_op jit(solution)/shard_map/ppermute | solution.py:88
  593.4 31.0 %collective-permute-start.60 = (bf16[160,2048]{1,0:T(8,128)(2,1)}, bf16[160,2048]{1,0:T(8,128)(2,1)}, u32[]{:S(2)}, u32[]{:S(2)}) collective-permute-start(bf16[160,2048]{1,0:T(8,128)(2,1)} %pad_maximum_fusion.12), channel_id=1, source_target_pairs={{0,2},{2,4},{4,6},{6,7},{7,5},{5,3},{3,1},{1,0},{8,10},{10,12},{12... | collective-permute-start | bytes 1966088 | tf_op jit(solution)/shard_map/ppermute | solution.py:88
  596.5 27.9 %all-to-all-start.5 = ((bf16[8,64,384]{2,1,0:T(8,128)(2,1)}), bf16[8,64,384]{2,1,0:T(8,128)(2,1)S(1)}, u32[]{:S(2)}, u32[]{:S(2)}) async-start(bf16[8,64,384]{2,1,0:T(8,128)(2,1)} %bitcast.219), calls=%async_computation.6 | async-start | bytes 786432 | tf_op jit(solution)/shard_map/all_to_all | solution.py:250
  603.5 20.0 %collective-permute-start.63 = (bf16[8,1,64,384]{3,2,0,1:T(8,128)(2,1)S(1)}, bf16[8,1,64,384]{3,2,0,1:T(8,128)(2,1)S(1)}, u32[]{:S(2)}, u32[]{:S(2)}) collective-permute-start(bf16[8,1,64,384]{3,2,0,1:T(8,128)(2,1)S(1)} %constant_dynamic-slice_fusion.1), channel_id=1, source_target_pairs={{0,16},{8,24},{16,0},{24,8},{1,17},{9,25},{17,1},{25,9},{2,18},{10... | collective-permute-start | bytes 1179656 | tf_op jit(solution)/shard_map/ppermute | solution.py:204
  627.8 38.0 %collective-permute-start.65 = (bf16[160,2048]{1,0:T(8,128)(2,1)}, bf16[160,2048]{1,0:T(8,128)(2,1)}, u32[]{:S(2)}, u32[]{:S(2)}) collective-permute-start(bf16[160,2048]{1,0:T(8,128)(2,1)} %get-tuple-element.469), channel_id=1, source_target_pairs={{0,2},{2,4},{4,6},{6,7},{7,5},{5,3},{3,1},{1,0},{8,10},{10,12},{12... | collective-permute-start | bytes 1966088 | tf_op jit(solution)/shard_map/ppermute | solution.py:88
  629.9 36.0 %collective-permute-start.66 = (bf16[160,2048]{1,0:T(8,128)(2,1)}, bf16[160,2048]{1,0:T(8,128)(2,1)}, u32[]{:S(2)}, u32[]{:S(2)}) collective-permute-start(bf16[160,2048]{1,0:T(8,128)(2,1)} %get-tuple-element.468), channel_id=1, source_target_pairs={{0,1},{2,0},{4,2},{6,4},{7,6},{5,7},{3,5},{1,3},{8,9},{10,8},{12,1... | collective-permute-start | bytes 1966088 | tf_op jit(solution)/shard_map/ppermute | solution.py:88
  644.5 19.0 %collective-permute-start.67 = (bf16[1,3,64,8,128]{4,1,2,3,0:T(4,128)(2,1)S(1)}, bf16[1,3,64,8,128]{4,1,2,3,0:T(4,128)(2,1)}, u32[]{:S(2)}, u32[]{:S(2)}) collective-permute-start(bf16[1,3,64,8,128]{4,1,2,3,0:T(4,128)(2,1)S(1)} %bitcast.212), channel_id=1, source_target_pairs={{0,16},{8,24},{16,0},{24,8},{1,17},{9,25},{17,1},{25,9},{2,18},{10... | collective-permute-start | bytes 1179656 | tf_op jit(solution)/shard_map/ppermute | solution.py:204
  648.6 17.3 %all-to-all-start.6 = ((bf16[8,64,384]{2,1,0:T(8,128)(2,1)}), bf16[8,64,384]{2,1,0:T(8,128)(2,1)S(1)}, u32[]{:S(2)}, u32[]{:S(2)}) async-start(bf16[8,64,384]{2,1,0:T(8,128)(2,1)} %bitcast.220), calls=%async_computation.7 | async-start | bytes 786432 | tf_op jit(solution)/shard_map/all_to_all | solution.py:250
  671.0 25.8 %collective-permute-start.69 = (bf16[160,2048]{1,0:T(8,128)(2,1)}, bf16[160,2048]{1,0:T(8,128)(2,1)S(1)}, u32[]{:S(2)}, u32[]{:S(2)}) collective-permute-start(bf16[160,2048]{1,0:T(8,128)(2,1)} %get-tuple-element.467), channel_id=1, source_target_pairs={{0,2},{2,4},{4,6},{6,7},{7,5},{5,3},{3,1},{1,0},{8,10},{10,12},{12... | collective-permute-start | bytes 1966088 | tf_op jit(solution)/shard_map/ppermute | solution.py:88
  672.7 24.1 %collective-permute-start.70 = (bf16[160,2048]{1,0:T(8,128)(2,1)}, bf16[160,2048]{1,0:T(8,128)(2,1)}, u32[]{:S(2)}, u32[]{:S(2)}) collective-permute-start(bf16[160,2048]{1,0:T(8,128)(2,1)} %get-tuple-element.466), channel_id=1, source_target_pairs={{0,1},{2,0},{4,2},{6,4},{7,6},{5,7},{3,5},{1,3},{8,9},{10,8},{12,1... | collective-permute-start | bytes 1966088 | tf_op jit(solution)/shard_map/ppermute | solution.py:88
  (174 other events, 1842.5 us)
Sparse Core Ops, SparseCore 0:
  42.8 57.6 all-gather.1
  408.5 72.9 reduce-scatter.3
  484.2 80.1 reduce-scatter.5
  566.9 86.3 reduce-scatter.7

commit v12 on v10

--- a/solution.py
+++ b/solution.py
@@ -724,12 +724,6 @@
     gates_own = gate_table(second_input, code_own)
 
     back_ring = RingSum(back_block, row_count)
-    back_parts[0] = window(
-        [back_ring],
-        lambda gback, uback: expert_back(gback, uback, gate_weight, up_weight, 0, chunks),
-        gback_all,
-        uback_all,
-    )
 
     def mixture_work(inner, pair):
         return (
@@ -739,6 +733,12 @@
 
     mixture_part, pair_grad = window([back_ring], mixture_work, inner_all, pair_sent)
     mixture_ring = RingSum(slot_rows(mixture_part), row_count)
+
+    def back_work(gback, uback):
+        back_parts[0] = expert_back(gback, uback, gate_weight, up_weight, 0, chunks)
+        return back_parts[0]
+
+    back_parts[0] = window([back_ring, mixture_ring], back_work, gback_all, uback_all)
 
     def down_work(inner, pair):
         pair_grad = pair.transpose(1, 0, 2).reshape(row_count, expert_total)
@@ -792,12 +792,11 @@
     swap = Swap(swap_sent, 0)
     attention_gather = RingGather(attention_low)
     up_part = window(
-        [mixture_ring, swap, attention_gather],
+        [swap, attention_gather],
         lambda uback: grad_of(second_all, uback),
         uback_all,
     )
     mixture = mixture_ring.total()
-    layer_out = (valid_own * (residual + mixture)).astype(low_type)
     mixed_grad = swap.received
 
     sent, gain_parts = (), 0.0
@@ -872,22 +871,39 @@
     )
     gate_sum = lax.psum_scatter(gate_part, "rep", scatter_dimension=0, tiled=True)
     up_sum = lax.psum_scatter(up_part, "rep", scatter_dimension=0, tiled=True)
-    (small_swapped, output_part), head_part = window(
+    def split_experts(total):
+        return jnp.stack(
+            [
+                total[:, e * hidden_here : (e + 1) * hidden_here].astype(wide_type)
+                for e in range(experts_here)
+            ]
+        )
+
+    (small_swapped, output_part, down_total), head_part = window(
         [first_ring],
-        lambda output, *small: (small_swap(small), rep_scatter(output, 0, scatter_order[:1])),
+        lambda output, down, *small: (
+            small_swap(small),
+            rep_scatter(output, 0, scatter_order[:1]),
+            down.astype(wide_type),
+        ),
         output_part.reshape(replica_count, share, model_width),
+        down_sum,
         *small_parts,
         waits=(head_part,),
     )
     head_rows = swap_all(head_part.reshape(group_count, share, 3 * width_here))
-    (output_part, small_sums), head_rows = window(
+    (output_part, small_sums, gate_total, layer_out), head_rows = window(
         [first_ring],
-        lambda output, small: (
+        lambda output, small, total, sums: (
             rep_scatter(output, 0, scatter_order[1:]),
             small_pieces(small, small_parts),
+            split_experts(total),
+            (valid_own * (residual + sums)).astype(low_type),
         ),
         output_part,
         small_swapped,
+        gate_sum,
+        mixture,
         waits=(head_rows,),
     )
     head_rows = rep_gather(
@@ -918,16 +934,7 @@
     pre_back, _ = norm_backward(token_own, inverse_one, prenorm_gain, first_grad)
     token_grad = residual_grad + pre_back
 
-    down_total = down_sum.astype(wide_type)
-    gate_total, up_total = (
-        jnp.stack(
-            [
-                total[:, e * hidden_here : (e + 1) * hidden_here].astype(wide_type)
-                for e in range(experts_here)
-            ]
-        )
-        for total in (gate_sum, up_sum)
-    )
+    up_total = split_experts(up_sum)
     return (
         layer_out,
         token_grad,

time: 697 us -> 690 us (0.990)
  waiting for transfers between devices: 146 us -> 136 us
  other arithmetic: 90 us -> 97.9 us
    all_to_all x7, waiting for transfers between devices: 42.3 us -> 33.6 us  [swap_all(): return lax.all_to_all(values, 'ep', split_axis=0, concat_axis=0, tiled=True)]
    unnamed x316 -> x328, local copies, waits for them, and re-layouts: 30.6 us -> 31.7 us
  transfers between devices with their start and end apart: 85 -> 85, of which waited for: 28 -> 29; matrix products, arithmetic and copies ran while one was open for 38% -> 38% of each run, Pallas kernels for 10% -> 10%
where the time goes in v12:
time: 690 us; the launch traced here: 680 us
  waiting for transfers between devices  136 us (20%)
  matrix products  127 us (18%)
  starting transfers between devices  115 us (17%)
  Pallas kernels  107 us (16%)
  other arithmetic  97.9 us (14%)
  local copies, waits for them, and re-layouts  80 us (12%)
  between operations  17.5 us (3%)
    dot_general x26, matrix products, mm(): lax.dot_general(left, right, (((left_dim,), (right_dim,)), ((), ())), pre...  127 us
    ppermute x56, waiting for transfers between devices, ring_shift(): return lax.ppermute(values, 'ep', pairs)  80.7 us
    ppermute x56, starting transfers between devices, ring_shift(): return lax.ppermute(values, 'ep', pairs)  65.8 us
    pallas_call x2, Pallas kernels, expert_pass(): pl.pallas_call(expert_kernel, grid=(experts, steps), in_specs=[pl.BlockSp...  39 us
    all_to_all x7, starting transfers between devices, swap_all(): return lax.all_to_all(values, 'ep', split_axis=0, concat_axis=0, tiled=True)  34.6 us
    pallas_call x2, Pallas kernels, expert_back(): pl.pallas_call(expert_back_kernel, grid=(depth // width,), in_specs=[whol...  33.6 us
    all_to_all x7, waiting for transfers between devices, swap_all(): return lax.all_to_all(values, 'ep', split_axis=0, concat_axis=0, tiled=True)  33.6 us
    unnamed x328, local copies, waits for them, and re-layouts  31.7 us
  transfers between devices with their start and end apart: 85, of which 29 were waited for; matrix products, arithmetic and copies ran while one was open for 38% of the time, Pallas kernels for 10%

profile of v12, /device:TPU:0, one launch (start us, length us, event | category | flops | bytes accessed | tf_op | source)
XLA Modules:
  0.0 680.1 jit_solution(5366058957569430537)
XLA Ops:
  11.5 7.3 %all-to-all-start = ((bf16[8,64,768]{2,1,0:T(8,128)(2,1)}), bf16[8,64,768]{2,1,0:T(8,128)(2,1)S(1)}, u32[]{:S(2)}, u32[]{:S(2)}) async-start(bf16[8,64,768]{2,1,0:T(8,128)(2,1)} %copy.138), calls=%async_computation | async-start | bytes 1572864 | tf_op jit(solution)/shard_map/all_to_all | solution.py:250
  19.9 19.0 %all-to-all-done = bf16[8,64,768]{2,1,0:T(8,128)(2,1)S(1)} async-done(((bf16[8,64,768]{2,1,0:T(8,128)(2,1)}), bf16[8,64,768]{2,1,0:T(8,128)(2,1)S(1)}, u32[]{:S(2)}, u32[]{:S(2)}) %all-to-all-start) | async-done | bytes 786464 | tf_op jit(solution)/shard_map/all_to_all | solution.py:250
  47.3 9.7 %collective-permute-done.4 = bf16[160,2048]{1,0:T(8,128)(2,1)} collective-permute-done((bf16[160,2048]{1,0:T(8,128)(2,1)S(1)}, bf16[160,2048]{1,0:T(8,128)(2,1)}, u32[]{:S(2)}, u32[]{:S(2)}) %collective-permute-start.4) | collective-permute-done | bytes 655392 | tf_op jit(solution)/shard_map/ppermute | solution.py:88
  59.9 4.1 all-to-all-start.2
  66.0 3.7 multiply_cosine_fusion
  79.3 10.4 %collective-permute-done.1 = bf16[160,2048]{1,0:T(8,128)(2,1)} collective-permute-done((bf16[160,2048]{1,0:T(8,128)(2,1)}, bf16[160,2048]{1,0:T(8,128)(2,1)}, u32[]{:S(2)}, u32[]{:S(2)}) %collective-permute-start.1) | collective-permute-done | bytes 655392 | tf_op jit(solution)/shard_map/ppermute | solution.py:88
  89.7 8.3 %collective-permute-start.2 = (bf16[160,2048]{1,0:T(8,128)(2,1)}, bf16[160,2048]{1,0:T(8,128)(2,1)S(1)}, u32[]{:S(2)}, u32[]{:S(2)}) collective-permute-start(bf16[160,2048]{1,0:T(8,128)(2,1)} %collective-permute-done.1), channel_id=1, source_target_pairs={{0,2},{2,4},{4,6},{6,7},{7,5},{5,3},{3,1},{1,0},{8,10},{10,12},{12... | collective-permute-start | bytes 1966088 | tf_op jit(solution)/shard_map/ppermute | solution.py:88
  98.0 2.5 collective-permute-done.5
  102.8 10.9 %collective-permute-done.6 = bf16[160,2048]{1,0:T(8,128)(2,1)S(1)} collective-permute-done((bf16[160,2048]{1,0:T(8,128)(2,1)}, bf16[160,2048]{1,0:T(8,128)(2,1)S(1)}, u32[]{:S(2)}, u32[]{:S(2)}) %collective-permute-start.6) | collective-permute-done | bytes 655392 | tf_op jit(solution)/shard_map/ppermute | solution.py:88
  116.8 2.3 maximum_select_fusion
  136.8 4.3 fusion.75.query_raw_ref.key_raw_ref
  168.1 4.0 collective-permute-done.16
  177.4 6.1 collective-permute-done.19
  184.6 4.6 all-to-all-start.1
  191.2 2.3 constant_dynamic-update-slice_fusion.44
  193.5 2.3 constant_dynamic-update-slice_fusion.43
  198.9 6.5 all-to-all-done.1
  217.7 7.4 %fusion.76.stream_ref = f32[640,2048]{1,0:T(8,128)} fusion(bf16[640,2048]{1,0:T(8,128)(2,1)S(1)} %copy-done.31, bf16[2048,2048]{1,0:T(8,128)(2,1)S(1)} %bitcast.276), kind=kOutput, calls=%fused_computation.333 | convolution fusion | flops 5368709120 | bytes 16252928 | tf_op jit(solution)/shard_map/dot_general | solution.py:60
  226.1 4.2 collective-permute-done.24
  232.4 8.9 %fusion.77.stream_ref = f32[640,2048]{1,0:T(8,128)} fusion(bf16[640,2048]{1,0:T(8,128)(2,1)} %get-tuple-element.239, bf16[2048,2048]{1,0:T(8,128)(2,1)S(1)} %bitcast.277), kind=kOutput, calls=%fused_computation.334 | convolution fusion | flops 5368709120 | bytes 16252928 | tf_op jit(solution)/shard_map/dot_general | solution.py:60
  241.4 2.6 collective-permute-done.26
  251.9 19.4 %shard_map.281 = (bf16[1280,2048]{1,0:T(8,128)(2,1)}, bf16[1280,2048]{1,0:T(8,128)(2,1)}, bf16[1280,2048]{1,0:T(8,128)(2,1)}, f32[2,640,128]{2,1,0:T(8,128)}) custom-call(bf16[640,2048]{1,0:T(8,128)(2,1)} %copy-done.32, bf16[2,2048,1024]{2,1,0:T(8,128)(2,1)} %gate_ref.7, bf16[2,2048,1024]{2,1,0:T(8,128)(2,1)} %up_ref.7, f32[640,2048]{1,0:T(8,128)} %fusion.76.stream_ref, ...), custom_call_target="tpu_custom_call" | custom-call | flops 10737418240 | bytes 42991616 | tf_op jit(solution)/shard_map/pallas_call | solution.py:294
  275.7 2.8 collective-permute-done.30
  285.1 19.5 %shard_map.282 = (bf16[1280,2048]{1,0:T(8,128)(2,1)}, bf16[1280,2048]{1,0:T(8,128)(2,1)}, bf16[1280,2048]{1,0:T(8,128)(2,1)}, f32[2,640,128]{2,1,0:T(8,128)}) custom-call(bf16[640,2048]{1,0:T(8,128)(2,1)} %copy-done.26, bf16[2,2048,1024]{2,1,0:T(8,128)(2,1)} %gate_ref.7, ...), custom_call_target="tpu_custom_call", output_to_operand_aliasing={{0}: (5, {}), {1}: (6, {}), {2}: (7, {})} | custom-call | flops 10737418240 | bytes 42991616 | tf_op jit(solution)/shard_map/pallas_call | solution.py:294
  306.7 16.8 %shard_map.283 = bf16[640,2048]{1,0:T(8,128)(2,1)} custom-call(bf16[1280,2048]{1,0:T(8,128)(2,1)} %get-tuple-element.282.gback_ref, bf16[1280,2048]{1,0:T(8,128)(2,1)} %get-tuple-element.291.uback_ref, bf16[2,2048,1024]{2,1,0:T(8,128)(2,1)} %gate_ref.7, bf16[2,2048,1024]{2,1,0:T(8,128)(2,1)} %up_ref.7), custom_call_target="tpu_custom_call" | custom-call | flops 10737418240 | bytes 24641536 | tf_op jit(solution)/shard_map/pallas_call | solution.py:334
  328.0 3.3 all-to-all-start.3
  331.3 16.6 %convolution_convert_fusion.3 = bf16[1280,2048]{1,0:T(8,128)(2,1)} fusion(bf16[1280,2048]{1,0:T(8,128)(2,1)} %get-tuple-element.275, bf16[2048,2048]{1,0:T(8,128)(2,1)} %bitcast.273), kind=kOutput, calls=%fused_computation.17 | convolution fusion | flops 10740039680 | bytes 18874368 | tf_op jit(solution)/shard_map/dot_general | solution.py:60
  356.8 16.8 %shard_map.284 = bf16[640,2048]{1,0:T(8,128)(2,1)} custom-call(bf16[1280,2048]{1,0:T(8,128)(2,1)} %get-tuple-element.282.gback_ref, bf16[1280,2048]{1,0:T(8,128)(2,1)} %get-tuple-element.291.uback_ref, bf16[2,2048,1024]{2,1,0:T(8,128)(2,1)} %gate_ref.7, bf16[2,2048,1024]{2,1,0:T(8,128)(2,1)} %up_ref.7), custom_call_target="tpu_custom_call" | custom-call | flops 10737418240 | bytes 24641536 | tf_op jit(solution)/shard_map/pallas_call | solution.py:334
  373.6 2.4 add_convert_fusion.11
  376.1 2.3 add_convert_fusion.12
  385.1 15.7 %convolution_convert_fusion.2 = bf16[2048,2048]{1,0:T(8,128)(2,1)} fusion(bf16[1280,2048]{1,0:T(8,128)(2,1)S(1)} %bitcast.171, bf16[1280,2048]{1,0:T(8,128)(2,1)} %get-tuple-element.557), kind=kOutput, calls=%fused_computation.16 | convolution fusion | flops 10741612544 | bytes 18874368 | tf_op jit(solution)/shard_map/dot_general | solution.py:60
  403.4 4.7 collective-permute-done.38
  408.3 3.4 add_convert_fusion.7
  413.7 2.7 add_convert_fusion.9
  416.5 2.3 collective-permute-start.43
  418.8 18.4 %convolution_convert_fusion.1 = bf16[2048,2048]{1,0:T(8,128)(2,1)} fusion(bf16[1280,2048]{1,0:T(8,128)(2,1)} %get-tuple-element.553, bf16[1280,2048]{1,0:T(8,128)(2,1)} %get-tuple-element.282.gback_ref), kind=kOutput, calls=%fused_computation.15 | convolution fusion | flops 10741612544 | bytes 18874368 | tf_op jit(solution)/shard_map/dot_general | solution.py:60
  447.3 2.6 convolution_add_fusion.1
  449.9 2.4 fusion.31
  452.3 2.6 fusion.14
  460.3 5.1 all-to-all-start.4
  465.6 16.7 %convolution_convert_fusion = bf16[2048,2048]{1,0:T(8,128)(2,1)} fusion(bf16[1280,2048]{1,0:T(8,128)(2,1)} %get-tuple-element.553, bf16[1280,2048]{1,0:T(8,128)(2,1)} %get-tuple-element.291.uback_ref), kind=kOutput, calls=%fused_computation.14 | convolution fusion | flops 10741612544 | bytes 18874368 | tf_op jit(solution)/shard_map/dot_general | solution.py:60
  482.3 2.6 all-to-all-done.4.swapped_ref
  490.0 14.6 %shard_map.285 = (bf16[1280,768]{1,0:T(8,128)(2,1)}, f32[2,128]{1,0:T(2,128)}) custom-call(s32[8]{0:T(128)} %stack.156.order_ref, bf16[1280,128]{1,0:T(8,128)(2,1)} %copy-done.50, bf16[1280,128]{1,0:T(8,128)(2,1)} %copy-done.49, bf16[1280,128]{1,0:T(8,128)(2,1)} %slice.505.value_ref, bf16[8,160,256]{2,1,0:T(8,128)(2,1)} %copy-done.13, ...), custom_call_target="tpu_custom_call" | custom-call | flops 2097152000 | bytes 4915200 | tf_op jit(solution)/shard_map/pallas_call | solution.py:421
  508.9 13.3 %shard_map.286 = (bf16[1280,768]{1,0:T(8,128)(2,1)}, f32[2,128]{1,0:T(2,128)}) custom-call(s32[8]{0:T(128)} %stack.156.order_ref, bf16[1280,128]{1,0:T(8,128)(2,1)} %copy-done.48, bf16[1280,128]{1,0:T(8,128)(2,1)} %copy-done.47, bf16[1280,128]{1,0:T(8,128)(2,1)} %slice.504.value_ref, ...), custom_call_target="tpu_custom_call", output_to_operand_aliasing={{0}: (13, {})} | custom-call | flops 2097152000 | bytes 4915200 | tf_op jit(solution)/shard_map/pallas_call | solution.py:421
  526.0 7.7 %convolution_convert_fusion.4 = bf16[2048,768]{1,0:T(8,128)(2,1)S(1)} fusion(bf16[1280,2048]{1,0:T(8,128)(2,1)} %copy-done.21, bf16[1280,768]{1,0:T(8,128)(2,1)} %get-tuple-element.326), kind=kOutput, calls=%fused_computation.22 | convolution fusion | flops 4028104704 | bytes 10354688 | tf_op jit(solution)/shard_map/dot_general | solution.py:60
  534.0 3.7 fusion.5
  538.3 7.3 %fusion.4 = (f32[2048]{0:T(1024)}, bf16[1280,2048]{1,0:T(8,128)(2,1)S(1)}) fusion(bf16[1280,2048]{1,0:T(8,128)(2,1)} %copy-done.3, f32[1280]{0:T(1024)S(1)} %add_rsqrt_fusion, bf16[1280,768]{1,0:T(8,128)(2,1)S(1)} %copy-done.37, bf16[2048,768]{1,0:T(8,128)(2,1)S(1)} %bitcast.188), kind=kOutput, calls=%fused_computation.8 | convolution fusion | flops 4039636992 | bytes 15610880 | tf_op jit(solution)/shard_map/dot_general | solution.py:60
  552.0 2.5 collective-permute-start.61
  554.5 6.4 shard_map.287
  568.7 5.7 all-to-all-start.5
  574.3 3.1 convert_add_fusion.2
  579.7 2.6 convert_element_type.476
  583.0 2.4 add_convert_fusion
  587.4 7.5 %collective-permute-done.60 = bf16[160,2048]{1,0:T(8,128)(2,1)} collective-permute-done((bf16[160,2048]{1,0:T(8,128)(2,1)S(1)}, bf16[160,2048]{1,0:T(8,128)(2,1)}, u32[]{:S(2)}, u32[]{:S(2)}) %collective-permute-start.60) | collective-permute-done | bytes 655392 | tf_op jit(solution)/shard_map/ppermute | solution.py:88
  596.4 3.3 add_convert_fusion.3
  601.8 4.5 all-to-all-start.6
  606.3 2.5 multiply_convert_fusion
  613.0 2.3 maximum_convert_fusion
  615.2 11.1 %collective-permute-done.67 = f32[4640]{0:T(1024)S(1)} collective-permute-done((f32[4640]{0:T(1024)S(1)}, f32[4640]{0:T(1024)S(1)}, u32[]{:S(2)}, u32[]{:S(2)}) %collective-permute-start.67) | collective-permute-done | bytes 18592 | tf_op jit(solution)/shard_map/ppermute | solution.py:204
  627.6 5.5 all-to-all-done.6
  635.1 3.3 add_convert_fusion.1
  643.9 2.3 maximum_convert_fusion.1
  647.0 10.3 %collective-permute-done.71 = bf16[1,64,2048]{2,1,0:T(8,128)(2,1)} collective-permute-done((bf16[1,64,2048]{2,1,0:T(8,128)(2,1)S(1)}, bf16[1,64,2048]{2,1,0:T(8,128)(2,1)}, u32[]{:S(2)}, u32[]{:S(2)}) %collective-permute-start.71) | collective-permute-done | bytes 262176 | tf_op jit(solution)/shard_map/ppermute | solution.py:204
  662.4 2.7 fusion.20
  (673 shorter events, 227.4 us)
Async XLA Ops:
  11.5 27.4 %all-to-all-start = ((bf16[8,64,768]{2,1,0:T(8,128)(2,1)}), bf16[8,64,768]{2,1,0:T(8,128)(2,1)S(1)}, u32[]{:S(2)}, u32[]{:S(2)}) async-start(bf16[8,64,768]{2,1,0:T(8,128)(2,1)} %copy.138), calls=%async_computation | async-start | bytes 1572864 | tf_op jit(solution)/shard_map/all_to_all | solution.py:250
  18.7 96.6 %all-gather.2.cloned.1.call-start = ((), (), s32[]{:S(2)}) async-start(), calls=%async_computation.10 | async-start | bytes 2359296 | tf_op jit(solution)/shard_map/all_gather | solution.py:69
  38.9 18.2 %collective-permute-start.4 = (bf16[160,2048]{1,0:T(8,128)(2,1)S(1)}, bf16[160,2048]{1,0:T(8,128)(2,1)}, u32[]{:S(2)}, u32[]{:S(2)}) collective-permute-start(bf16[160,2048]{1,0:T(8,128)(2,1)S(1)} %copy-done.8), channel_id=1, source_target_pairs={{0,1},{2,0},{4,2},{6,4},{7,6},{5,7},{3,5},{1,3},{8,9},{10,8},{12,1... | collective-permute-start | bytes 1966088 | tf_op jit(solution)/shard_map/ppermute | solution.py:88
  40.3 18.9 %collective-permute-start = (bf16[160,2048]{1,0:T(8,128)(2,1)S(1)}, bf16[160,2048]{1,0:T(8,128)(2,1)}, u32[]{:S(2)}, u32[]{:S(2)}) collective-permute-start(bf16[160,2048]{1,0:T(8,128)(2,1)S(1)} %copy-done.8), channel_id=1, source_target_pairs={{0,2},{2,4},{4,6},{6,7},{7,5},{5,3},{3,1},{1,0},{8,10},{10,12},{12... | collective-permute-start | bytes 1966088 | tf_op jit(solution)/shard_map/ppermute | solution.py:88
  45.8 23.9 %collective-permute-start.11 = (bf16[1,8,64,768]{3,2,1,0:T(8,128)(2,1)S(1)}, bf16[1,8,64,768]{3,2,1,0:T(8,128)(2,1)S(1)}, u32[]{:S(2)}, u32[]{:S(2)}) collective-permute-start(bf16[1,8,64,768]{3,2,1,0:T(8,128)(2,1)S(1)} %bitcast.166), channel_id=1, source_target_pairs={{0,16},{8,24},{16,0},{24,8},{1,17},{9,25},{17,1},{25,9},{2,18},{10... | collective-permute-start | bytes 2359304 | tf_op jit(solution)/shard_map/ppermute | solution.py:204
  64.0 25.8 %collective-permute-start.1 = (bf16[160,2048]{1,0:T(8,128)(2,1)}, bf16[160,2048]{1,0:T(8,128)(2,1)}, u32[]{:S(2)}, u32[]{:S(2)}) collective-permute-start(bf16[160,2048]{1,0:T(8,128)(2,1)} %collective-permute-done), channel_id=1, source_target_pairs={{0,2},{2,4},{4,6},{6,7},{7,5},{5,3},{3,1},{1,0},{8,10},{10,12},{12... | collective-permute-start | bytes 1966088 | tf_op jit(solution)/shard_map/ppermute | solution.py:88
  66.0 34.5 %collective-permute-start.5 = (bf16[160,2048]{1,0:T(8,128)(2,1)}, bf16[160,2048]{1,0:T(8,128)(2,1)}, u32[]{:S(2)}, u32[]{:S(2)}) collective-permute-start(bf16[160,2048]{1,0:T(8,128)(2,1)} %collective-permute-done.4), channel_id=1, source_target_pairs={{0,1},{2,0},{4,2},{6,4},{7,6},{5,7},{3,5},{1,3},{8,9},{10,8},{12,1... | collective-permute-start | bytes 1966088 | tf_op jit(solution)/shard_map/ppermute | solution.py:88
  71.1 45.6 %collective-permute-start.12 = (bf16[2,8,64,768]{3,2,1,0:T(8,128)(2,1)}, bf16[2,8,64,768]{3,2,1,0:T(8,128)(2,1)}, u32[]{:S(2)}, u32[]{:S(2)}) collective-permute-start(bf16[2,8,64,768]{3,2,1,0:T(8,128)(2,1)} %maximum_select_fusion.3), channel_id=1, source_target_pairs={{0,8},{8,0},{16,24},{24,16},{1,9},{9,1},{17,25},{25,17},{2,10},{10... | collective-permute-start | bytes 4718600 | tf_op jit(solution)/shard_map/ppermute | solution.py:204
  89.7 25.6 %collective-permute-start.2 = (bf16[160,2048]{1,0:T(8,128)(2,1)}, bf16[160,2048]{1,0:T(8,128)(2,1)S(1)}, u32[]{:S(2)}, u32[]{:S(2)}) collective-permute-start(bf16[160,2048]{1,0:T(8,128)(2,1)} %collective-permute-done.1), channel_id=1, source_target_pairs={{0,2},{2,4},{4,6},{6,7},{7,5},{5,3},{3,1},{1,0},{8,10},{10,12},{12... | collective-permute-start | bytes 1966088 | tf_op jit(solution)/shard_map/ppermute | solution.py:88
  120.9 20.4 %collective-permute-start.10 = (bf16[512,512]{1,0:T(8,128)(2,1)S(1)}, bf16[512,512]{1,0:T(8,128)(2,1)S(1)}, u32[]{:S(2)}, u32[]{:S(2)}) collective-permute-start(bf16[512,512]{1,0:T(8,128)(2,1)S(1)} %get-tuple-element.524), channel_id=1, source_target_pairs={{0,16},{8,24},{16,0},{24,8},{1,17},{9,25},{17,1},{25,9},{2,18},{10... | collective-permute-start | bytes 1572872 | tf_op jit(solution)/shard_map/ppermute | solution.py:204
  122.4 32.2 %collective-permute-start.15 = (bf16[512,512]{1,0:T(8,128)(2,1)S(1)}, bf16[512,512]{1,0:T(8,128)(2,1)S(1)}, u32[]{:S(2)}, u32[]{:S(2)}) collective-permute-start(bf16[512,512]{1,0:T(8,128)(2,1)S(1)} %get-tuple-element.523), channel_id=1, source_target_pairs={{0,16},{8,24},{16,0},{24,8},{1,17},{9,25},{17,1},{25,9},{2,18},{10... | collective-permute-start | bytes 1572872 | tf_op jit(solution)/shard_map/ppermute | solution.py:204
  123.0 45.2 %collective-permute-start.18 = (bf16[512,512]{1,0:T(8,128)(2,1)S(1)}, bf16[512,512]{1,0:T(8,128)(2,1)S(1)}, u32[]{:S(2)}, u32[]{:S(2)}) collective-permute-start(bf16[512,512]{1,0:T(8,128)(2,1)S(1)} %get-tuple-element.522), channel_id=1, source_target_pairs={{0,16},{8,24},{16,0},{24,8},{1,17},{9,25},{17,1},{25,9},{2,18},{10... | collective-permute-start | bytes 1572872 | tf_op jit(solution)/shard_map/ppermute | solution.py:204
  126.0 16.7 %collective-permute-start.8 = (bf16[160,2048]{1,0:T(8,128)(2,1)S(1)}, bf16[160,2048]{1,0:T(8,128)(2,1)S(1)}, u32[]{:S(2)}, u32[]{:S(2)}) collective-permute-start(bf16[160,2048]{1,0:T(8,128)(2,1)S(1)} %copy-done.14), channel_id=1, source_target_pairs={{0,2},{2,4},{4,6},{6,7},{7,5},{5,3},{3,1},{1,0},{8,10},{10,12},{12... | collective-permute-start | bytes 1966088 | tf_op jit(solution)/shard_map/ppermute | solution.py:88
  127.3 15.4 %collective-permute-start.9 = (bf16[160,2048]{1,0:T(8,128)(2,1)S(1)}, bf16[160,2048]{1,0:T(8,128)(2,1)S(1)}, u32[]{:S(2)}, u32[]{:S(2)}) collective-permute-start(bf16[160,2048]{1,0:T(8,128)(2,1)S(1)} %copy-done.14), channel_id=1, source_target_pairs={{0,1},{2,0},{4,2},{6,4},{7,6},{5,7},{3,5},{1,3},{8,9},{10,8},{12,1... | collective-permute-start | bytes 1966088 | tf_op jit(solution)/shard_map/ppermute | solution.py:88
  141.3 36.1 %collective-permute-start.21 = (bf16[512,512]{1,0:T(8,128)(2,1)S(1)}, bf16[512,512]{1,0:T(8,128)(2,1)}, u32[]{:S(2)}, u32[]{:S(2)}) collective-permute-start(bf16[512,512]{1,0:T(8,128)(2,1)S(1)} %get-tuple-element.521), channel_id=1, source_target_pairs={{0,16},{8,24},{16,0},{24,8},{1,17},{9,25},{17,1},{25,9},{2,18},{10... | collective-permute-start | bytes 1572872 | tf_op jit(solution)/shard_map/ppermute | solution.py:204
  154.6 54.8 %collective-permute-start.22 = (bf16[2048,512]{1,0:T(8,128)(2,1)S(1)}, bf16[2048,512]{1,0:T(8,128)(2,1)}, u32[]{:S(2)}, u32[]{:S(2)}) collective-permute-start(bf16[2048,512]{1,0:T(8,128)(2,1)S(1)} %copy-done.6), channel_id=1, source_target_pairs={{0,8},{8,0},{16,24},{24,16},{1,9},{9,1},{17,25},{25,17},{2,10},{10... | collective-permute-start | bytes 6291464 | tf_op jit(solution)/shard_map/ppermute | solution.py:204
  155.6 16.5 %collective-permute-start.16 = (bf16[160,2048]{1,0:T(8,128)(2,1)S(1)}, bf16[160,2048]{1,0:T(8,128)(2,1)S(1)}, u32[]{:S(2)}, u32[]{:S(2)}) collective-permute-start(bf16[160,2048]{1,0:T(8,128)(2,1)S(1)} %collective-permute-done.13), channel_id=1, source_target_pairs={{0,2},{2,4},{4,6},{6,7},{7,5},{5,3},{3,1},{1,0},{8,10},{10,12},{12... | collective-permute-start | bytes 1966088 | tf_op jit(solution)/shard_map/ppermute | solution.py:88
  156.9 17.1 %collective-permute-start.17 = (bf16[160,2048]{1,0:T(8,128)(2,1)S(1)}, bf16[160,2048]{1,0:T(8,128)(2,1)S(1)}, u32[]{:S(2)}, u32[]{:S(2)}) collective-permute-start(bf16[160,2048]{1,0:T(8,128)(2,1)S(1)} %collective-permute-done.14), channel_id=1, source_target_pairs={{0,1},{2,0},{4,2},{6,4},{7,6},{5,7},{3,5},{1,3},{8,9},{10,8},{12,1... | collective-permute-start | bytes 1966088 | tf_op jit(solution)/shard_map/ppermute | solution.py:88
  184.6 20.8 %all-to-all-start.1 = ((bf16[8,160,256]{2,1,0:T(8,128)(2,1)}), bf16[8,160,256]{2,1,0:T(8,128)(2,1)}, u32[]{:S(2)}, u32[]{:S(2)}) async-start(bf16[8,160,256]{2,1,0:T(8,128)(2,1)} %copy-done.53), calls=%async_computation.1 | async-start | bytes 1310720 | tf_op jit(solution)/shard_map/all_to_all | solution.py:250
  191.2 20.6 %collective-permute-start.23 = (bf16[2048,512]{1,0:T(8,128)(2,1)}, bf16[2048,512]{1,0:T(8,128)(2,1)}, u32[]{:S(2)}, u32[]{:S(2)}) collective-permute-start(bf16[2048,512]{1,0:T(8,128)(2,1)} %constant_dynamic-update-slice_fusion.18), channel_id=1, source_target_pairs={{0,8},{8,0},{16,24},{24,16},{1,9},{9,1},{17,25},{25,17},{2,10},{10... | collective-permute-start | bytes 6291464 | tf_op jit(solution)/shard_map/ppermute | solution.py:204
  215.4 14.9 %collective-permute-start.24 = (bf16[160,2048]{1,0:T(8,128)(2,1)S(1)}, bf16[160,2048]{1,0:T(8,128)(2,1)S(1)}, u32[]{:S(2)}, u32[]{:S(2)}) collective-permute-start(bf16[160,2048]{1,0:T(8,128)(2,1)S(1)} %get-tuple-element.473), channel_id=1, source_target_pairs={{0,2},{2,4},{4,6},{6,7},{7,5},{5,3},{3,1},{1,0},{8,10},{10,12},{12... | collective-permute-start | bytes 1966088 | tf_op jit(solution)/shard_map/ppermute | solution.py:88
  231.2 14.6 %collective-permute-start.27 = (bf16[160,2048]{1,0:T(8,128)(2,1)S(1)}, bf16[160,2048]{1,0:T(8,128)(2,1)S(1)}, u32[]{:S(2)}, u32[]{:S(2)}) collective-permute-start(bf16[160,2048]{1,0:T(8,128)(2,1)S(1)} %collective-permute-done.25), channel_id=1, source_target_pairs={{0,1},{2,0},{4,2},{6,4},{7,6},{5,7},{3,5},{1,3},{8,9},{10,8},{12,1... | collective-permute-start | bytes 1966088 | tf_op jit(solution)/shard_map/ppermute | solution.py:88
  246.0 25.3 %collective-permute-start.29 = (bf16[160,2048]{1,0:T(8,128)(2,1)S(1)}, bf16[160,2048]{1,0:T(8,128)(2,1)S(1)}, u32[]{:S(2)}, u32[]{:S(2)}) collective-permute-start(bf16[160,2048]{1,0:T(8,128)(2,1)S(1)} %collective-permute-done.27), channel_id=1, source_target_pairs={{0,1},{2,0},{4,2},{6,4},{7,6},{5,7},{3,5},{1,3},{8,9},{10,8},{12,1... | collective-permute-start | bytes 1966088 | tf_op jit(solution)/shard_map/ppermute | solution.py:88
  246.5 24.8 %collective-permute-start.28 = (bf16[160,2048]{1,0:T(8,128)(2,1)S(1)}, bf16[160,2048]{1,0:T(8,128)(2,1)S(1)}, u32[]{:S(2)}, u32[]{:S(2)}) collective-permute-start(bf16[160,2048]{1,0:T(8,128)(2,1)S(1)} %collective-permute-done.26), channel_id=1, source_target_pairs={{0,2},{2,4},{4,6},{6,7},{7,5},{5,3},{3,1},{1,0},{8,10},{10,12},{12... | collective-permute-start | bytes 1966088 | tf_op jit(solution)/shard_map/ppermute | solution.py:88
  324.9 23.1 %collective-permute-start.32 = (bf16[80,2048]{1,0:T(8,128)(2,1)S(1)}, bf16[80,2048]{1,0:T(8,128)(2,1)S(1)}, u32[]{:S(2)}, u32[]{:S(2)}) collective-permute-start(bf16[80,2048]{1,0:T(8,128)(2,1)S(1)} %get-tuple-element.514), channel_id=1, source_target_pairs={{0,2},{2,4},{4,6},{6,7},{7,5},{5,3},{3,1},{1,0},{8,10},{10,12},{12... | collective-permute-start | bytes 983048 | tf_op jit(solution)/shard_map/ppermute | solution.py:88
  326.6 21.3 %collective-permute-start.33 = (bf16[80,2048]{1,0:T(8,128)(2,1)S(1)}, bf16[80,2048]{1,0:T(8,128)(2,1)}, u32[]{:S(2)}, u32[]{:S(2)}) collective-permute-start(bf16[80,2048]{1,0:T(8,128)(2,1)S(1)} %get-tuple-element.513), channel_id=1, source_target_pairs={{0,1},{2,0},{4,2},{6,4},{7,6},{5,7},{3,5},{1,3},{8,9},{10,8},{12,1... | collective-permute-start | bytes 983048 | tf_op jit(solution)/shard_map/ppermute | solution.py:88
  328.0 20.0 %all-to-all-start.3 = ((f32[8,160,2]{1,2,0:T(2,128)}), f32[8,160,2]{1,2,0:T(2,128)S(1)}, u32[]{:S(2)}, u32[]{:S(2)}) async-start(f32[8,160,2]{1,2,0:T(2,128)} %copy.172), calls=%async_computation.3 | async-start | bytes 32768 | tf_op jit(solution)/shard_map/all_to_all | solution.py:250
  331.3 194.7 %reduce-scatter.4.cloned.1.call-start = ((), (), s32[]{:S(2)}) async-start(), calls=%async_computation.11 | async-start | bytes 10485760 | tf_op jit(solution)/shard_map/reduce_scatter | solution.py:825
  351.6 22.0 %collective-permute-start.35 = (bf16[160,2048]{1,0:T(8,128)(2,1)S(1)}, bf16[160,2048]{1,0:T(8,128)(2,1)}, u32[]{:S(2)}, u32[]{:S(2)}) collective-permute-start(bf16[160,2048]{1,0:T(8,128)(2,1)S(1)} %pad_maximum_fusion.7), channel_id=1, source_target_pairs={{0,1},{2,0},{4,2},{6,4},{7,6},{5,7},{3,5},{1,3},{8,9},{10,8},{12,1... | collective-permute-start | bytes 1966088 | tf_op jit(solution)/shard_map/ppermute | solution.py:88
  354.4 19.2 %collective-permute-start.34 = (bf16[160,2048]{1,0:T(8,128)(2,1)}, bf16[160,2048]{1,0:T(8,128)(2,1)}, u32[]{:S(2)}, u32[]{:S(2)}) collective-permute-start(bf16[160,2048]{1,0:T(8,128)(2,1)} %pad_maximum_fusion.6), channel_id=1, source_target_pairs={{0,2},{2,4},{4,6},{6,7},{7,5},{5,3},{3,1},{1,0},{8,10},{10,12},{12... | collective-permute-start | bytes 1966088 | tf_op jit(solution)/shard_map/ppermute | solution.py:88
  354.6 19.0 %collective-permute-start.36 = (bf16[80,2048]{1,0:T(8,128)(2,1)}, bf16[80,2048]{1,0:T(8,128)(2,1)S(1)}, u32[]{:S(2)}, u32[]{:S(2)}) collective-permute-start(bf16[80,2048]{1,0:T(8,128)(2,1)} %get-tuple-element.499), channel_id=1, source_target_pairs={{0,2},{2,4},{4,6},{6,7},{7,5},{5,3},{3,1},{1,0},{8,10},{10,12},{12... | collective-permute-start | bytes 983048 | tf_op jit(solution)/shard_map/ppermute | solution.py:88
  356.4 17.2 %collective-permute-start.37 = (bf16[80,2048]{1,0:T(8,128)(2,1)}, bf16[80,2048]{1,0:T(8,128)(2,1)}, u32[]{:S(2)}, u32[]{:S(2)}) collective-permute-start(bf16[80,2048]{1,0:T(8,128)(2,1)} %get-tuple-element.498), channel_id=1, source_target_pairs={{0,1},{2,0},{4,2},{6,4},{7,6},{5,7},{3,5},{1,3},{8,9},{10,8},{12,1... | collective-permute-start | bytes 983048 | tf_op jit(solution)/shard_map/ppermute | solution.py:88
  379.9 23.3 %collective-permute-start.41 = (bf16[160,2048]{1,0:T(8,128)(2,1)S(1)}, bf16[160,2048]{1,0:T(8,128)(2,1)}, u32[]{:S(2)}, u32[]{:S(2)}) collective-permute-start(bf16[160,2048]{1,0:T(8,128)(2,1)S(1)} %pad_maximum_fusion.9), channel_id=1, source_target_pairs={{0,1},{2,0},{4,2},{6,4},{7,6},{5,7},{3,5},{1,3},{8,9},{10,8},{12,1... | collective-permute-start | bytes 1966088 | tf_op jit(solution)/shard_map/ppermute | solution.py:88
  382.7 20.5 %collective-permute-start.40 = (bf16[160,2048]{1,0:T(8,128)(2,1)}, bf16[160,2048]{1,0:T(8,128)(2,1)}, u32[]{:S(2)}, u32[]{:S(2)}) collective-permute-start(bf16[160,2048]{1,0:T(8,128)(2,1)} %pad_maximum_fusion.8), channel_id=1, source_target_pairs={{0,2},{2,4},{4,6},{6,7},{7,5},{5,3},{3,1},{1,0},{8,10},{10,12},{12... | collective-permute-start | bytes 1966088 | tf_op jit(solution)/shard_map/ppermute | solution.py:88
  382.9 20.6 %collective-permute-start.39 = (bf16[160,2048]{1,0:T(8,128)(2,1)}, bf16[160,2048]{1,0:T(8,128)(2,1)S(1)}, u32[]{:S(2)}, u32[]{:S(2)}) collective-permute-start(bf16[160,2048]{1,0:T(8,128)(2,1)} %add_convert_fusion.11), channel_id=1, source_target_pairs={{0,1},{2,0},{4,2},{6,4},{7,6},{5,7},{3,5},{1,3},{8,9},{10,8},{12,1... | collective-permute-start | bytes 1966088 | tf_op jit(solution)/shard_map/ppermute | solution.py:88
  384.8 23.4 %collective-permute-start.38 = (bf16[160,2048]{1,0:T(8,128)(2,1)}, bf16[160,2048]{1,0:T(8,128)(2,1)}, u32[]{:S(2)}, u32[]{:S(2)}) collective-permute-start(bf16[160,2048]{1,0:T(8,128)(2,1)} %add_convert_fusion.12), channel_id=1, source_target_pairs={{0,2},{2,4},{4,6},{6,7},{7,5},{5,3},{3,1},{1,0},{8,10},{10,12},{12... | collective-permute-start | bytes 1966088 | tf_op jit(solution)/shard_map/ppermute | solution.py:88
  408.2 193.6 %reduce-scatter.6.cloned.1.call-start = ((), (), s32[]{:S(2)}) async-start(), calls=%async_computation.12 | async-start | bytes 10485760 | tf_op jit(solution)/shard_map/reduce_scatter | solution.py:872
  411.7 25.5 %collective-permute-start.44 = (bf16[160,2048]{1,0:T(8,128)(2,1)}, bf16[160,2048]{1,0:T(8,128)(2,1)S(1)}, u32[]{:S(2)}, u32[]{:S(2)}) collective-permute-start(bf16[160,2048]{1,0:T(8,128)(2,1)} %get-tuple-element.495), channel_id=1, source_target_pairs={{0,2},{2,4},{4,6},{6,7},{7,5},{5,3},{3,1},{1,0},{8,10},{10,12},{12... | collective-permute-start | bytes 1966088 | tf_op jit(solution)/shard_map/ppermute | solution.py:88
  411.8 25.4 %collective-permute-start.45 = (bf16[160,2048]{1,0:T(8,128)(2,1)}, bf16[160,2048]{1,0:T(8,128)(2,1)}, u32[]{:S(2)}, u32[]{:S(2)}) collective-permute-start(bf16[160,2048]{1,0:T(8,128)(2,1)} %get-tuple-element.494), channel_id=1, source_target_pairs={{0,1},{2,0},{4,2},{6,4},{7,6},{5,7},{3,5},{1,3},{8,9},{10,8},{12,1... | collective-permute-start | bytes 1966088 | tf_op jit(solution)/shard_map/ppermute | solution.py:88
  416.4 21.4 %collective-permute-start.42 = (bf16[160,2048]{1,0:T(8,128)(2,1)}, bf16[160,2048]{1,0:T(8,128)(2,1)S(1)}, u32[]{:S(2)}, u32[]{:S(2)}) collective-permute-start(bf16[160,2048]{1,0:T(8,128)(2,1)} %get-tuple-element.510), channel_id=1, source_target_pairs={{0,2},{2,4},{4,6},{6,7},{7,5},{5,3},{3,1},{1,0},{8,10},{10,12},{12... | collective-permute-start | bytes 1966088 | tf_op jit(solution)/shard_map/ppermute | solution.py:88
  416.5 21.3 %collective-permute-start.43 = (bf16[160,2048]{1,0:T(8,128)(2,1)}, bf16[160,2048]{1,0:T(8,128)(2,1)S(1)}, u32[]{:S(2)}, u32[]{:S(2)}) collective-permute-start(bf16[160,2048]{1,0:T(8,128)(2,1)} %get-tuple-element.509), channel_id=1, source_target_pairs={{0,1},{2,0},{4,2},{6,4},{7,6},{5,7},{3,5},{1,3},{8,9},{10,8},{12,1... | collective-permute-start | bytes 1966088 | tf_op jit(solution)/shard_map/ppermute | solution.py:88
  440.6 16.6 %collective-permute-start.46 = (bf16[160,2048]{1,0:T(8,128)(2,1)S(1)}, bf16[160,2048]{1,0:T(8,128)(2,1)S(1)}, u32[]{:S(2)}, u32[]{:S(2)}) collective-permute-start(bf16[160,2048]{1,0:T(8,128)(2,1)S(1)} %get-tuple-element.493), channel_id=1, source_target_pairs={{0,2},{2,4},{4,6},{6,7},{7,5},{5,3},{3,1},{1,0},{8,10},{10,12},{12... | collective-permute-start | bytes 1966088 | tf_op jit(solution)/shard_map/ppermute | solution.py:88
  440.8 16.4 %collective-permute-start.47 = (bf16[160,2048]{1,0:T(8,128)(2,1)S(1)}, bf16[160,2048]{1,0:T(8,128)(2,1)S(1)}, u32[]{:S(2)}, u32[]{:S(2)}) collective-permute-start(bf16[160,2048]{1,0:T(8,128)(2,1)S(1)} %get-tuple-element.492), channel_id=1, source_target_pairs={{0,1},{2,0},{4,2},{6,4},{7,6},{5,7},{3,5},{1,3},{8,9},{10,8},{12,1... | collective-permute-start | bytes 1966088 | tf_op jit(solution)/shard_map/ppermute | solution.py:88
  458.0 24.3 %collective-permute-start.48 = (bf16[160,2048]{1,0:T(8,128)(2,1)S(1)}, bf16[160,2048]{1,0:T(8,128)(2,1)}, u32[]{:S(2)}, u32[]{:S(2)}) collective-permute-start(bf16[160,2048]{1,0:T(8,128)(2,1)S(1)} %get-tuple-element.334.refs_0_), channel_id=1, source_target_pairs={{0,2},{2,4},{4,6},{6,7},{7,5},{5,3},{3,1},{1,0},{8,10},{10,12},{12... | collective-permute-start | bytes 1966088 | tf_op jit(solution)/shard_map/ppermute | solution.py:88
  459.0 23.3 %collective-permute-start.49 = (bf16[160,2048]{1,0:T(8,128)(2,1)S(1)}, bf16[160,2048]{1,0:T(8,128)(2,1)}, u32[]{:S(2)}, u32[]{:S(2)}) collective-permute-start(bf16[160,2048]{1,0:T(8,128)(2,1)S(1)} %get-tuple-element.334.refs_0_), channel_id=1, source_target_pairs={{0,1},{2,0},{4,2},{6,4},{7,6},{5,7},{3,5},{1,3},{8,9},{10,8},{12,1... | collective-permute-start | bytes 1966088 | tf_op jit(solution)/shard_map/ppermute | solution.py:88
  460.3 24.6 %all-to-all-start.4 = ((bf16[8,160,256]{2,1,0:T(8,128)(2,1)}), bf16[8,160,256]{2,1,0:T(8,128)(2,1)S(1)}, u32[]{:S(2)}, u32[]{:S(2)}) async-start(bf16[8,160,256]{2,1,0:T(8,128)(2,1)} %bitcast.193), calls=%async_computation.4 | async-start | bytes 1310720 | tf_op jit(solution)/shard_map/all_to_all | solution.py:250
  465.4 174.7 %reduce-scatter.8.cloned.1.call-start = ((), (), s32[]{:S(2)}) async-start(), calls=%async_computation.13 | async-start | bytes 10485760 | tf_op jit(solution)/shard_map/reduce_scatter | solution.py:873
  485.7 18.9 %collective-permute-start.50 = (bf16[160,2048]{1,0:T(8,128)(2,1)}, bf16[160,2048]{1,0:T(8,128)(2,1)S(1)}, u32[]{:S(2)}, u32[]{:S(2)}) collective-permute-start(bf16[160,2048]{1,0:T(8,128)(2,1)} %collective-permute-done.48.refs_2_), channel_id=1, source_target_pairs={{0,2},{2,4},{4,6},{6,7},{7,5},{5,3},{3,1},{1,0},{8,10},{10,12},{12... | collective-permute-start | bytes 1966088 | tf_op jit(solution)/shard_map/ppermute | solution.py:88
  485.7 18.9 %collective-permute-start.51 = (bf16[160,2048]{1,0:T(8,128)(2,1)}, bf16[160,2048]{1,0:T(8,128)(2,1)S(1)}, u32[]{:S(2)}, u32[]{:S(2)}) collective-permute-start(bf16[160,2048]{1,0:T(8,128)(2,1)} %collective-permute-done.49.refs_1_), channel_id=1, source_target_pairs={{0,1},{2,0},{4,2},{6,4},{7,6},{5,7},{3,5},{1,3},{8,9},{10,8},{12,1... | collective-permute-start | bytes 1966088 | tf_op jit(solution)/shard_map/ppermute | solution.py:88
  505.7 16.5 %collective-permute-start.52 = (bf16[160,2048]{1,0:T(8,128)(2,1)}, bf16[160,2048]{1,0:T(8,128)(2,1)S(1)}, u32[]{:S(2)}, u32[]{:S(2)}) collective-permute-start(bf16[160,2048]{1,0:T(8,128)(2,1)} %copy-done.59), channel_id=1, source_target_pairs={{0,2},{2,4},{4,6},{6,7},{7,5},{5,3},{3,1},{1,0},{8,10},{10,12},{12... | collective-permute-start | bytes 1966088 | tf_op jit(solution)/shard_map/ppermute | solution.py:88
  506.3 15.9 %collective-permute-start.53 = (bf16[160,2048]{1,0:T(8,128)(2,1)}, bf16[160,2048]{1,0:T(8,128)(2,1)S(1)}, u32[]{:S(2)}, u32[]{:S(2)}) collective-permute-start(bf16[160,2048]{1,0:T(8,128)(2,1)} %copy-done.60), channel_id=1, source_target_pairs={{0,1},{2,0},{4,2},{6,4},{7,6},{5,7},{3,5},{1,3},{8,9},{10,8},{12,1... | collective-permute-start | bytes 1966088 | tf_op jit(solution)/shard_map/ppermute | solution.py:88
  552.0 31.0 %collective-permute-start.61 = (bf16[8,1,64,768]{3,2,1,0:T(8,128)(2,1)}, bf16[8,1,64,768]{3,2,1,0:T(8,128)(2,1)}, u32[]{:S(2)}, u32[]{:S(2)}) collective-permute-start(bf16[8,1,64,768]{3,2,1,0:T(8,128)(2,1)} %constant_dynamic-slice_fusion.1), channel_id=1, source_target_pairs={{0,16},{8,24},{16,0},{24,8},{1,17},{9,25},{17,1},{25,9},{2,18},{10... | collective-permute-start | bytes 2359304 | tf_op jit(solution)/shard_map/ppermute | solution.py:204
  565.2 20.3 %collective-permute-start.62 = (bf16[2,64,2048]{2,1,0:T(8,128)(2,1)}, bf16[2,64,2048]{2,1,0:T(8,128)(2,1)}, u32[]{:S(2)}, u32[]{:S(2)}) collective-permute-start(bf16[2,64,2048]{2,1,0:T(8,128)(2,1)} %dynamic-slice_bitcast_fusion.1), channel_id=1, source_target_pairs={{0,8},{8,0},{16,24},{24,16},{1,9},{9,1},{17,25},{25,17},{2,10},{10... | collective-permute-start | bytes 1572872 | tf_op jit(solution)/shard_map/ppermute | solution.py:204
  577.4 17.5 %collective-permute-start.60 = (bf16[160,2048]{1,0:T(8,128)(2,1)S(1)}, bf16[160,2048]{1,0:T(8,128)(2,1)}, u32[]{:S(2)}, u32[]{:S(2)}) collective-permute-start(bf16[160,2048]{1,0:T(8,128)(2,1)S(1)} %copy-done.55), channel_id=1, source_target_pairs={{0,1},{2,0},{4,2},{6,4},{7,6},{5,7},{3,5},{1,3},{8,9},{10,8},{12,1... | collective-permute-start | bytes 1966088 | tf_op jit(solution)/shard_map/ppermute | solution.py:88
  579.4 17.0 %collective-permute-start.59 = (bf16[160,2048]{1,0:T(8,128)(2,1)}, bf16[160,2048]{1,0:T(8,128)(2,1)}, u32[]{:S(2)}, u32[]{:S(2)}) collective-permute-start(bf16[160,2048]{1,0:T(8,128)(2,1)} %pad_maximum_fusion.11), channel_id=1, source_target_pairs={{0,2},{2,4},{4,6},{6,7},{7,5},{5,3},{3,1},{1,0},{8,10},{10,12},{12... | collective-permute-start | bytes 1966088 | tf_op jit(solution)/shard_map/ppermute | solution.py:88
  599.8 27.8 %collective-permute-start.63 = (bf16[160,2048]{1,0:T(8,128)(2,1)}, bf16[160,2048]{1,0:T(8,128)(2,1)}, u32[]{:S(2)}, u32[]{:S(2)}) collective-permute-start(bf16[160,2048]{1,0:T(8,128)(2,1)} %get-tuple-element.485), channel_id=1, source_target_pairs={{0,2},{2,4},{4,6},{6,7},{7,5},{5,3},{3,1},{1,0},{8,10},{10,12},{12... | collective-permute-start | bytes 1966088 | tf_op jit(solution)/shard_map/ppermute | solution.py:88
  599.9 27.7 %collective-permute-start.64 = (bf16[160,2048]{1,0:T(8,128)(2,1)}, bf16[160,2048]{1,0:T(8,128)(2,1)}, u32[]{:S(2)}, u32[]{:S(2)}) collective-permute-start(bf16[160,2048]{1,0:T(8,128)(2,1)} %get-tuple-element.484), channel_id=1, source_target_pairs={{0,1},{2,0},{4,2},{6,4},{7,6},{5,7},{3,5},{1,3},{8,9},{10,8},{12,1... | collective-permute-start | bytes 1966088 | tf_op jit(solution)/shard_map/ppermute | solution.py:88
  601.8 31.3 %all-to-all-start.6 = ((bf16[8,64,768]{2,1,0:T(8,128)(2,1)}), bf16[8,64,768]{2,1,0:T(8,128)(2,1)S(1)}, u32[]{:S(2)}, u32[]{:S(2)}) async-start(bf16[8,64,768]{2,1,0:T(8,128)(2,1)} %bitcast.63), calls=%async_computation.7 | async-start | bytes 1572864 | tf_op jit(solution)/shard_map/all_to_all | solution.py:250
  610.8 16.7 %collective-permute-start.65 = (bf16[1,64,2048]{2,1,0:T(8,128)(2,1)S(1)}, bf16[1,64,2048]{2,1,0:T(8,128)(2,1)S(1)}, u32[]{:S(2)}, u32[]{:S(2)}) collective-permute-start(bf16[1,64,2048]{2,1,0:T(8,128)(2,1)S(1)} %constant_dynamic-slice_fusion), channel_id=1, source_target_pairs={{0,16},{8,24},{16,0},{24,8},{1,17},{9,25},{17,1},{25,9},{2,18},{10... | collective-permute-start | bytes 786440 | tf_op jit(solution)/shard_map/ppermute | solution.py:204
  611.1 15.2 %collective-permute-start.67 = (f32[4640]{0:T(1024)S(1)}, f32[4640]{0:T(1024)S(1)}, u32[]{:S(2)}, u32[]{:S(2)}) collective-permute-start(f32[4640]{0:T(1024)S(1)} %add.652), channel_id=1, source_target_pairs={{0,16},{8,24},{16,0},{24,8},{1,17},{9,25},{17,1},{25,9},{2,18},{10... | collective-permute-start | bytes 55688 | tf_op jit(solution)/shard_map/ppermute | solution.py:204
  634.7 23.7 %collective-permute-start.70 = (bf16[1,3,64,2048]{3,2,1,0:T(8,128)(2,1)S(1)}, bf16[1,3,64,2048]{3,2,1,0:T(8,128)(2,1)}, u32[]{:S(2)}, u32[]{:S(2)}) collective-permute-start(bf16[1,3,64,2048]{3,2,1,0:T(8,128)(2,1)S(1)} %stack.161), channel_id=1, source_target_pairs={{0,16},{8,24},{16,0},{24,8},{1,17},{9,25},{17,1},{25,9},{2,18},{10... | collective-permute-start | bytes 2359304 | tf_op jit(solution)/shard_map/ppermute | solution.py:204
  638.4 18.9 %collective-permute-start.71 = (bf16[1,64,2048]{2,1,0:T(8,128)(2,1)S(1)}, bf16[1,64,2048]{2,1,0:T(8,128)(2,1)}, u32[]{:S(2)}, u32[]{:S(2)}) collective-permute-start(bf16[1,64,2048]{2,1,0:T(8,128)(2,1)S(1)} %add_convert_fusion.19), channel_id=1, source_target_pairs={{0,16},{8,24},{16,0},{24,8},{1,17},{9,25},{17,1},{25,9},{2,18},{10... | collective-permute-start | bytes 786440 | tf_op jit(solution)/shard_map/ppermute | solution.py:204
  641.8 18.3 %collective-permute-start.68 = (bf16[160,2048]{1,0:T(8,128)(2,1)}, bf16[160,2048]{1,0:T(8,128)(2,1)S(1)}, u32[]{:S(2)}, u32[]{:S(2)}) collective-permute-start(bf16[160,2048]{1,0:T(8,128)(2,1)} %get-tuple-element.483), channel_id=1, source_target_pairs={{0,2},{2,4},{4,6},{6,7},{7,5},{5,3},{3,1},{1,0},{8,10},{10,12},{12... | collective-permute-start | bytes 1966088 | tf_op jit(solution)/shard_map/ppermute | solution.py:88
  642.2 18.0 %collective-permute-start.69 = (bf16[160,2048]{1,0:T(8,128)(2,1)}, bf16[160,2048]{1,0:T(8,128)(2,1)S(1)}, u32[]{:S(2)}, u32[]{:S(2)}) collective-permute-start(bf16[160,2048]{1,0:T(8,128)(2,1)} %get-tuple-element.482), channel_id=1, source_target_pairs={{0,1},{2,0},{4,2},{6,4},{7,6},{5,7},{3,5},{1,3},{8,9},{10,8},{12,1... | collective-permute-start | bytes 1966088 | tf_op jit(solution)/shard_map/ppermute | solution.py:88
  (165 other events, 1762.5 us)
Sparse Core Ops, SparseCore 0:
  42.8 57.6 all-gather.1
  408.3 72.9 reduce-scatter.3
  484.1 71.7 reduce-scatter.5
  558.3 77.9 reduce-scatter.7

commit v13 on v12

--- a/solution.py
+++ b/solution.py
@@ -443,6 +443,99 @@
             transcendentals=rows * rows,
         ),
     )(order, *operands, *earlier)
+
+
+def output_forward_kernel(starts_ref, mixed_ref, token_ref, gain_ref, *refs):
+    residual_ref, normed_ref, total = refs[-3:]
+    step = pl.program_id(0)
+
+    @pl.when(step == 0)
+    def _():
+        total[...] = token_ref[...].astype(wide_type)
+
+    for j, piece_ref in enumerate(refs[:-3]):
+        width = piece_ref.shape[1]
+        columns = pl.ds(pl.multiple_of(starts_ref[j], width), width)
+        total[:, columns] += mm(mixed_ref[0], piece_ref[...], 1, 0)
+
+    @pl.when(step == pl.num_programs(0) - 1)
+    def _():
+        residual = total[...]
+        residual_ref[...] = residual
+        normed_ref[...] = (residual * inverse_rms(residual) * gain_ref[...]).astype(low_type)
+
+
+def output_forward(swapped, tokens, gain, pieces, starts):
+    count, rows, width = swapped.shape
+    depth = tokens.shape[1]
+    whole = pl.BlockSpec((rows, depth), lambda i, starts: (0, 0))
+    return pl.pallas_call(
+        output_forward_kernel,
+        grid_spec=pltpu.PrefetchScalarGridSpec(
+            num_scalar_prefetch=1,
+            grid=(count,),
+            in_specs=[
+                pl.BlockSpec((1, rows, width), lambda i, starts: (i, 0, 0)),
+                whole,
+                pl.BlockSpec((1, depth), lambda i, starts: (0, 0)),
+            ]
+            + [
+                pl.BlockSpec((width, piece.shape[1]), lambda i, starts: (i, 0))
+                for piece in pieces
+            ],
+            out_specs=[whole, whole],
+            scratch_shapes=[pltpu.VMEM((rows, depth), wide_type)],
+        ),
+        out_shape=[
+            jax.ShapeDtypeStruct((rows, depth), wide_type),
+            jax.ShapeDtypeStruct((rows, depth), low_type),
+        ],
+        compiler_params=pltpu.CompilerParams(vmem_limit_bytes=40 << 20),
+        cost_estimate=pl.CostEstimate(
+            flops=2 * rows * depth * depth,
+            bytes_accessed=2 * depth * depth + 10 * rows * depth,
+            transcendentals=0,
+        ),
+    )(starts, swapped, tokens, gain[None, :], *pieces)
+
+
+def output_back_kernel(starts_ref, grad_ref, *refs):
+    out_ref = refs[-1]
+    total = None
+    for j, piece_ref in enumerate(refs[:-1]):
+        width = piece_ref.shape[1]
+        columns = pl.ds(pl.multiple_of(starts_ref[j], width), width)
+        term = mm(grad_ref[:, columns], piece_ref[...], 1, 1)
+        total = term if total is None else total + term
+    width = out_ref.shape[2]
+    for i in range(out_ref.shape[0]):
+        out_ref[i] = total[:, i * width : (i + 1) * width].astype(low_type)
+
+
+def output_back(grads, pieces, starts, count):
+    rows, depth = grads.shape
+    width = depth // count
+    group = 2 if count % 2 == 0 else 1
+    return pl.pallas_call(
+        output_back_kernel,
+        grid_spec=pltpu.PrefetchScalarGridSpec(
+            num_scalar_prefetch=1,
+            grid=(count // group,),
+            in_specs=[pl.BlockSpec((rows, depth), lambda i, starts: (0, 0))]
+            + [
+                pl.BlockSpec((group * width, piece.shape[1]), lambda i, starts: (i, 0))
+                for piece in pieces
+            ],
+            out_specs=pl.BlockSpec((group, rows, width), lambda i, starts: (i, 0, 0)),
+        ),
+        out_shape=jax.ShapeDtypeStruct((count, rows, width), low_type),
+        compiler_params=pltpu.CompilerParams(vmem_limit_bytes=40 << 20),
+        cost_estimate=pl.CostEstimate(
+            flops=2 * rows * depth * depth,
+            bytes_accessed=2 * depth * depth + 4 * rows * depth,
+            transcendentals=0,
+        ),
+    )(starts, grads, *pieces)
 
 
 def block_product_kernel(left_ref, *refs):
@@ -551,14 +644,6 @@
     tokens_late, output_late, _ = tie(tokens, output_weight, swapped)
     token_ring = RingGather(tokens_late)
     token_ring.start()
-    small_flat = after(small_sent.reshape(-1, head_dim), token_ring.received)
-    small_all = swap_all(
-        jnp.broadcast_to(small_flat[None], (group_count,) + small_flat.shape)
-    ).reshape(group_count, row_count + width_here, expert_total)
-    code_all = reorder(small_all[:, :row_count], device_of_slot).reshape(
-        group_rows, expert_total
-    )
-    full_router = small_all[:, row_count:].reshape(model_width, expert_total)
     chunks = 2
     chunk_rows = group_rows // chunks
     blocks_here = group_count // chunks
@@ -657,19 +742,24 @@
     for distance in gather_order[1:]:
         for j in list(output_pieces):
             output_pieces[j ^ distance] = rep_exchange(output_pieces[j], distance)
-    mixed_own = (
-        swap_all(mixed_ordered.reshape(group_count, row_count, width_here))
-        .transpose(1, 0, 2)
-        .reshape(row_count, model_width)
-    )
-    attention = jnp.zeros((row_count, model_width), wide_type)
-    for j, piece in output_pieces.items():
-        attention = lax.dynamic_update_slice_in_dim(
-            attention, mm(mixed_own, piece, 1, 0), (replica ^ j) * column_share, 1
-        )
-    residual = tokens.astype(wide_type) + attention
+    small_flat = after(small_sent.reshape(-1, head_dim), mixed_ordered)
+    small_all = swap_all(
+        jnp.broadcast_to(small_flat[None], (group_count,) + small_flat.shape)
+    ).reshape(group_count, row_count + width_here, expert_total)
+    code_all = reorder(small_all[:, :row_count], device_of_slot).reshape(
+        group_rows, expert_total
+    )
+    full_router = small_all[:, row_count:].reshape(model_width, expert_total)
+    piece_starts = jnp.stack([(replica ^ j) * column_share for j in output_pieces])
+    piece_list = list(output_pieces.values())
+    residual, second_input = output_forward(
+        swap_all(mixed_ordered.reshape(group_count, row_count, width_here)),
+        tokens,
+        postnorm_gain,
+        piece_list,
+        piece_starts,
+    )
     inverse_two = inverse_rms(residual)
-    second_input = (residual * inverse_two * postnorm_gain).astype(low_type)
 
     def gate_table(rows, code):
         logits = mm(rows, full_router, 1, 0)
@@ -765,21 +855,7 @@
         )
         residual_grad = upstream + post_back
         attention_low = residual_grad.astype(low_type)
-        mixed_grad_own = jnp.zeros((row_count, model_width), wide_type)
-        for j, piece in output_pieces.items():
-            mixed_grad_own = mixed_grad_own + mm(
-                lax.dynamic_slice_in_dim(
-                    attention_low, (replica ^ j) * column_share, column_share, 1
-                ),
-                piece,
-                1,
-                1,
-            )
-        swap_sent = (
-            mixed_grad_own.astype(low_type)
-            .reshape(row_count, group_count, width_here)
-            .transpose(1, 0, 2)
-        )
+        swap_sent = output_back(attention_low, piece_list, piece_starts, group_count)
         return swap_sent, residual_grad, attention_low, jnp.sum(postnorm_part, axis=0)
 
     swap_sent, residual_grad, attention_low, postnorm_part = window(
@@ -796,7 +872,6 @@
         lambda uback: grad_of(second_all, uback),
         uback_all,
     )
-    mixture = mixture_ring.total()
     mixed_grad = swap.received
 
     sent, gain_parts = (), 0.0
@@ -879,31 +954,33 @@
             ]
         )
 
-    (small_swapped, output_part, down_total), head_part = window(
+    (output_part, down_total), head_part = window(
         [first_ring],
-        lambda output, down, *small: (
-            small_swap(small),
+        lambda output, down: (
             rep_scatter(output, 0, scatter_order[:1]),
             down.astype(wide_type),
         ),
         output_part.reshape(replica_count, share, model_width),
         down_sum,
-        *small_parts,
         waits=(head_part,),
     )
     head_rows = swap_all(head_part.reshape(group_count, share, 3 * width_here))
-    (output_part, small_sums, gate_total, layer_out), head_rows = window(
+    def layer_work(own, *sums):
+        mixture = sum((part.astype(wide_type) for part in sums), own.astype(wide_type))
+        return (valid_own * (residual + mixture)).astype(low_type)
+
+    (output_part, small_swapped, gate_total, layer_out), head_rows = window(
         [first_ring],
-        lambda output, small, total, sums: (
+        lambda output, total, sums, *small: (
             rep_scatter(output, 0, scatter_order[1:]),
-            small_pieces(small, small_parts),
+            small_swap(small),
             split_experts(total),
-            (valid_own * (residual + sums)).astype(low_type),
+            layer_work(*sums),
         ),
         output_part,
-        small_swapped,
         gate_sum,
-        mixture,
+        (mixture_part[:row_count], *mixture_ring.sent),
+        *small_parts,
         waits=(head_rows,),
     )
     head_rows = rep_gather(
@@ -912,10 +989,14 @@
         .reshape(1, 3, share, model_width),
         gather_order[:-1],
     )
-    output_rows, head_rows = window(
+    (output_rows, small_sums), head_rows = window(
         [first_ring],
-        lambda output: rep_gather(output, gather_order[:-1]),
+        lambda output, small: (
+            rep_gather(output, gather_order[:-1]),
+            small_pieces(small, small_parts),
+        ),
         output_part,
+        small_swapped,
         waits=(head_rows,),
     )
     head_rows = rep_gather(head_rows, gather_order[-1:])

time: 690 us -> 736 us (1.067)
  waiting for transfers between devices: 136 us -> 161 us
  local copies, waits for them, and re-layouts: 80 us -> 96.9 us
  Pallas kernels: 107 us -> 121 us
  other arithmetic: 97.9 us -> 108 us
  matrix products: 127 us -> 117 us
  starting transfers between devices: 115 us -> 106 us
    all_to_all x7, waiting for transfers between devices: 33.6 us -> 60.2 us  [swap_all(): return lax.all_to_all(values, 'ep', split_axis=0, concat_axis=0, tiled=True)]
    pallas_call x0 -> x2, Pallas kernels: none -> 13.8 us  [the longest x1 7.55 us: output_forward(): pl.pallas_call(output_forward_kernel, grid_spec=pltpu.PrefetchScalarGridS...]
    ppermute x56, waiting for transfers between devices: 80.7 us -> 68.6 us  [ring_shift(): return lax.ppermute(values, 'ep', pairs)]
    ppermute x18, waiting for transfers between devices: 21.5 us -> 32.4 us  [rep_exchange(): lax.ppermute(values, 'rep', [(i, i ^ distance) for i in range(count)])]
    dot_general x26 -> x18, matrix products: 127 us -> 117 us  [mm(): lax.dot_general(left, right, (((left_dim,), (right_dim,)), ((), ())), pre...]
    unnamed x328 -> x269, local copies, waits for them, and re-layouts: 31.7 us -> 39.3 us
  transfers between devices with their start and end apart: 85 -> 85, of which waited for: 29 -> 30; matrix products, arithmetic and copies ran while one was open for 38% -> 39% of each run, Pallas kernels for 10% -> 11%
where the time goes in v13:
time: 736 us; the launch traced here: 727 us
  waiting for transfers between devices  161 us (22%)
  Pallas kernels  121 us (16%)
  matrix products  117 us (16%)
  other arithmetic  108 us (15%)
  starting transfers between devices  106 us (14%)
  local copies, waits for them, and re-layouts  96.9 us (13%)
  between operations  16.4 us (2%)
    dot_general x18, matrix products, mm(): lax.dot_general(left, right, (((left_dim,), (right_dim,)), ((), ())), pre...  117 us
    ppermute x56, waiting for transfers between devices, ring_shift(): return lax.ppermute(values, 'ep', pairs)  68.6 us
    ppermute x56, starting transfers between devices, ring_shift(): return lax.ppermute(values, 'ep', pairs)  65 us
    all_to_all x7, waiting for transfers between devices, swap_all(): return lax.all_to_all(values, 'ep', split_axis=0, concat_axis=0, tiled=True)  60.2 us
    unnamed x269, local copies, waits for them, and re-layouts  39.3 us
    pallas_call x2, Pallas kernels, expert_pass(): pl.pallas_call(expert_kernel, grid=(experts, steps), in_specs=[pl.BlockSp...  38.9 us
    pallas_call x2, Pallas kernels, expert_back(): pl.pallas_call(expert_back_kernel, grid=(depth // width,), in_specs=[whol...  33.6 us
    ppermute x18, waiting for transfers between devices, rep_exchange(): lax.ppermute(values, 'rep', [(i, i ^ distance) for i in range(count)])  32.4 us
  transfers between devices with their start and end apart: 85, of which 30 were waited for; matrix products, arithmetic and copies ran while one was open for 39% of the time, Pallas kernels for 11%

profile of v13, /device:TPU:0, one launch (start us, length us, event | category | flops | bytes accessed | tf_op | source)
XLA Modules:
  0.0 726.7 jit_solution(5665529066595509626)
XLA Ops:
  11.4 7.3 all-to-all-start
  18.8 20.1 %all-to-all-done = bf16[8,64,768]{2,1,0:T(8,128)(2,1)S(1)} async-done(((bf16[8,64,768]{2,1,0:T(8,128)(2,1)}), bf16[8,64,768]{2,1,0:T(8,128)(2,1)S(1)}, u32[]{:S(2)}, u32[]{:S(2)}) %all-to-all-start) | async-done | bytes 786464 | tf_op jit(solution)/shard_map/all_to_all | solution.py:250
  45.0 13.5 %collective-permute-done.11 = bf16[1,8,64,768]{3,2,1,0:T(8,128)(2,1)S(1)} collective-permute-done((bf16[1,8,64,768]{3,2,1,0:T(8,128)(2,1)S(1)}, bf16[1,8,64,768]{3,2,1,0:T(8,128)(2,1)S(1)}, u32[]{:S(2)}, u32[]{:S(2)}) %collective-permute-start.11) | collective-permute-done | bytes 786464 | tf_op jit(solution)/shard_map/ppermute | solution.py:204
  61.1 3.5 collective-permute-done
  64.6 2.5 collective-permute-start.1
  70.3 21.7 %collective-permute-done.1 = bf16[160,2048]{1,0:T(8,128)(2,1)} collective-permute-done((bf16[160,2048]{1,0:T(8,128)(2,1)S(1)}, bf16[160,2048]{1,0:T(8,128)(2,1)}, u32[]{:S(2)}, u32[]{:S(2)}) %collective-permute-start.1) | collective-permute-done | bytes 655392 | tf_op jit(solution)/shard_map/ppermute | solution.py:88
  92.0 3.4 collective-permute-start.2
  95.5 4.7 collective-permute-done.5
  102.5 3.7 multiply_cosine_fusion
  108.0 6.5 collective-permute-done.6
  116.1 2.4 collective-permute-start.7
  139.0 4.3 fusion.63.query_raw_ref.key_raw_ref
  170.4 4.2 collective-permute-done.16
  187.8 5.2 all-to-all-start.2
  194.7 5.6 all-to-all-done.2
  200.3 3.5 all-to-all-start.1
  213.1 7.4 %all-to-all-done.1.mixed_ref = bf16[8,160,256]{2,1,0:T(8,128)(2,1)S(1)} async-done(((bf16[8,160,256]{2,1,0:T(8,128)(2,1)}), bf16[8,160,256]{2,1,0:T(8,128)(2,1)S(1)}, u32[]{:S(2)}, u32[]{:S(2)}) %all-to-all-start.1) | async-done | bytes 655392 | tf_op jit(solution)/shard_map/all_to_all | solution.py:250
  223.6 7.5 %shard_map.281 = (f32[160,2048]{1,0:T(8,128)S(1)}, bf16[160,2048]{1,0:T(8,128)(2,1)S(1)}) custom-call(s32[4]{0:T(128)S(1)} %pad_add_fusion.starts_ref, bf16[8,160,256]{2,1,0:T(8,128)(2,1)S(1)} %copy-done.8, bf16[160,2048]{1,0:T(8,128)(2,1)S(1)} %copy-done.4, f32[1,2048]{1,0:T(1,128)S(1)} %bitcast.142, bf16[2048,512]{1,0:T(8,128)(2,1)S(1)} %copy-done.2, ...), custom_call_target="tpu_custom_call" | custom-call | flops 1342177280 | bytes 11665408 | tf_op jit(solution)/shard_map/pallas_call | solution.py:472
  233.3 9.7 %fusion.64.stream_ref = f32[640,2048]{1,0:T(8,128)} fusion(bf16[640,2048]{1,0:T(8,128)(2,1)S(1)} %copy-done.32, bf16[2048,2048]{1,0:T(8,128)(2,1)} %bitcast.247), kind=kOutput, calls=%fused_computation.312 | convolution fusion | flops 5368709120 | bytes 16252928 | tf_op jit(solution)/shard_map/dot_general | solution.py:60
  248.5 9.6 %fusion.65.stream_ref = f32[640,2048]{1,0:T(8,128)} fusion(bf16[640,2048]{1,0:T(8,128)(2,1)S(1)} %copy-done.64, bf16[2048,2048]{1,0:T(8,128)(2,1)} %bitcast.248), kind=kOutput, calls=%fused_computation.313 | convolution fusion | flops 5368709120 | bytes 16252928 | tf_op jit(solution)/shard_map/dot_general | solution.py:60
  258.2 3.0 collective-permute-done.26
  271.4 19.4 %shard_map.282 = (bf16[1280,2048]{1,0:T(8,128)(2,1)}, bf16[1280,2048]{1,0:T(8,128)(2,1)}, bf16[1280,2048]{1,0:T(8,128)(2,1)}, f32[2,640,128]{2,1,0:T(8,128)}) custom-call(bf16[640,2048]{1,0:T(8,128)(2,1)} %copy-done.33, bf16[2,2048,1024]{2,1,0:T(8,128)(2,1)} %gate_ref.7, bf16[2,2048,1024]{2,1,0:T(8,128)(2,1)} %up_ref.7, f32[640,2048]{1,0:T(8,128)} %fusion.64.stream_ref, ...), custom_call_target="tpu_custom_call" | custom-call | flops 10737418240 | bytes 42991616 | tf_op jit(solution)/shard_map/pallas_call | solution.py:294
  298.0 3.0 collective-permute-done.31
  305.4 19.4 %shard_map.283 = (bf16[1280,2048]{1,0:T(8,128)(2,1)}, bf16[1280,2048]{1,0:T(8,128)(2,1)}, bf16[1280,2048]{1,0:T(8,128)(2,1)}, f32[2,640,128]{2,1,0:T(8,128)}) custom-call(bf16[640,2048]{1,0:T(8,128)(2,1)} %copy-done.26, bf16[2,2048,1024]{2,1,0:T(8,128)(2,1)} %gate_ref.7, ...), custom_call_target="tpu_custom_call", output_to_operand_aliasing={{0}: (5, {}), {1}: (6, {}), {2}: (7, {})} | custom-call | flops 10737418240 | bytes 42991616 | tf_op jit(solution)/shard_map/pallas_call | solution.py:294
  324.8 16.8 %shard_map.284 = bf16[640,2048]{1,0:T(8,128)(2,1)} custom-call(bf16[1280,2048]{1,0:T(8,128)(2,1)} %get-tuple-element.287.gback_ref, bf16[1280,2048]{1,0:T(8,128)(2,1)} %get-tuple-element.297.uback_ref, bf16[2,2048,1024]{2,1,0:T(8,128)(2,1)} %gate_ref.7, bf16[2,2048,1024]{2,1,0:T(8,128)(2,1)} %up_ref.7), custom_call_target="tpu_custom_call" | custom-call | flops 10737418240 | bytes 24641536 | tf_op jit(solution)/shard_map/pallas_call | solution.py:334
  341.6 2.5 fusion.48
  347.7 2.4 bitcast_multiply_fusion
  352.1 3.4 all-to-all-start.3
  355.5 16.5 %convolution_convert_fusion.3 = bf16[1280,2048]{1,0:T(8,128)(2,1)} fusion(bf16[1280,2048]{1,0:T(8,128)(2,1)} %get-tuple-element.280, bf16[2048,2048]{1,0:T(8,128)(2,1)} %bitcast.249), kind=kOutput, calls=%fused_computation.17 | convolution fusion | flops 10740039680 | bytes 18874368 | tf_op jit(solution)/shard_map/dot_general | solution.py:60
  380.6 16.8 %shard_map.285 = bf16[640,2048]{1,0:T(8,128)(2,1)} custom-call(bf16[1280,2048]{1,0:T(8,128)(2,1)} %get-tuple-element.287.gback_ref, bf16[1280,2048]{1,0:T(8,128)(2,1)} %get-tuple-element.297.uback_ref, bf16[2,2048,1024]{2,1,0:T(8,128)(2,1)} %gate_ref.7, bf16[2,2048,1024]{2,1,0:T(8,128)(2,1)} %up_ref.7), custom_call_target="tpu_custom_call" | custom-call | flops 10737418240 | bytes 24641536 | tf_op jit(solution)/shard_map/pallas_call | solution.py:334
  408.9 16.7 %convolution_convert_fusion.2 = bf16[2048,2048]{1,0:T(8,128)(2,1)} fusion(bf16[1280,2048]{1,0:T(8,128)(2,1)} %get-tuple-element.280, bf16[1280,2048]{1,0:T(8,128)(2,1)} %get-tuple-element.561), kind=kOutput, calls=%fused_computation.16 | convolution fusion | flops 10741612544 | bytes 18874368 | tf_op jit(solution)/shard_map/dot_general | solution.py:60
  427.7 2.5 fusion.62
  430.3 3.3 add_convert_fusion.9
  435.6 3.9 add_convert_fusion.7
  441.9 18.2 %convolution_convert_fusion.1 = bf16[2048,2048]{1,0:T(8,128)(2,1)} fusion(bf16[1280,2048]{1,0:T(8,128)(2,1)} %get-tuple-element.557, bf16[1280,2048]{1,0:T(8,128)(2,1)} %get-tuple-element.287.gback_ref), kind=kOutput, calls=%fused_computation.15 | convolution fusion | flops 10741612544 | bytes 18874368 | tf_op jit(solution)/shard_map/dot_general | solution.py:60
  461.1 2.4 add_convert_fusion.5
  469.8 6.3 shard_map.286
  476.1 2.6 collective-permute-done.46
  478.7 2.7 collective-permute-done.47
  483.3 5.0 all-to-all-start.4
  488.6 16.7 %convolution_convert_fusion = bf16[2048,2048]{1,0:T(8,128)(2,1)} fusion(bf16[1280,2048]{1,0:T(8,128)(2,1)} %get-tuple-element.557, bf16[1280,2048]{1,0:T(8,128)(2,1)} %get-tuple-element.297.uback_ref), kind=kOutput, calls=%fused_computation.14 | convolution fusion | flops 10741612544 | bytes 18874368 | tf_op jit(solution)/shard_map/dot_general | solution.py:60
  505.3 5.2 all-to-all-done.4.swapped_ref
  515.5 14.7 %shard_map.287 = (bf16[1280,768]{1,0:T(8,128)(2,1)}, f32[2,128]{1,0:T(2,128)}) custom-call(s32[8]{0:T(128)} %stack.176.order_ref, bf16[1280,128]{1,0:T(8,128)(2,1)} %copy-done.45, bf16[1280,128]{1,0:T(8,128)(2,1)} %copy-done.44, bf16[1280,128]{1,0:T(8,128)(2,1)} %slice.504.value_ref, bf16[8,160,256]{2,1,0:T(8,128)(2,1)} %copy-done.14, ...), custom_call_target="tpu_custom_call" | custom-call | flops 2097152000 | bytes 4915200 | tf_op jit(solution)/shard_map/pallas_call | solution.py:421
  534.2 13.3 %shard_map.288 = (bf16[1280,768]{1,0:T(8,128)(2,1)}, f32[2,128]{1,0:T(2,128)}) custom-call(s32[8]{0:T(128)} %stack.176.order_ref, bf16[1280,128]{1,0:T(8,128)(2,1)} %copy-done.43, bf16[1280,128]{1,0:T(8,128)(2,1)} %copy-done.42, bf16[1280,128]{1,0:T(8,128)(2,1)} %slice.503.value_ref, ...), custom_call_target="tpu_custom_call", output_to_operand_aliasing={{0}: (13, {})} | custom-call | flops 2097152000 | bytes 4915200 | tf_op jit(solution)/shard_map/pallas_call | solution.py:421
  551.4 7.5 %convolution_convert_fusion.4 = bf16[2048,768]{1,0:T(8,128)(2,1)S(1)} fusion(bf16[1280,2048]{1,0:T(8,128)(2,1)} %copy-done.20, bf16[1280,768]{1,0:T(8,128)(2,1)} %get-tuple-element.332), kind=kOutput, calls=%fused_computation.22 | convolution fusion | flops 4028104704 | bytes 10354688 | tf_op jit(solution)/shard_map/dot_general | solution.py:60
  559.2 3.8 fusion.5
  563.2 7.2 fusion.4
  578.7 6.4 shard_map.289
  591.6 4.3 convert_element_type.466
  600.2 6.4 collective-permute-done.59
  606.8 2.8 add_convert_fusion.3
  615.6 3.5 all-to-all-start.6
  622.8 4.9 all-to-all-done.6
  627.7 3.5 all-to-all-start.5
  631.2 2.7 multiply_convert_fusion
  639.9 17.0 %all-to-all-done.5 = bf16[8,64,768]{2,1,0:T(8,128)(2,1)S(1)} async-done(((bf16[8,64,768]{2,1,0:T(8,128)(2,1)}), bf16[8,64,768]{2,1,0:T(8,128)(2,1)S(1)}, u32[]{:S(2)}, u32[]{:S(2)}) %all-to-all-start.5) | async-done | bytes 786464 | tf_op jit(solution)/shard_map/all_to_all | solution.py:250
  656.9 3.6 add_convert_fusion.1
  662.3 2.5 reshape.485
  666.4 3.1 stack.181
  676.8 13.8 %collective-permute-done.71 = f32[4640]{0:T(1024)S(1)} collective-permute-done((f32[4640]{0:T(1024)S(1)}, f32[4640]{0:T(1024)S(1)}, u32[]{:S(2)}, u32[]{:S(2)}) %collective-permute-start.71) | collective-permute-done | bytes 18592 | tf_op jit(solution)/shard_map/ppermute | solution.py:204
  691.7 4.0 collective-permute-done.69
  698.4 2.6 fusion.15
  705.1 3.1 fusion.18
  711.5 2.5 maximum_select_fusion.1
  (604 shorter events, 242.2 us)
Async XLA Ops:
  11.4 27.4 %all-to-all-start = ((bf16[8,64,768]{2,1,0:T(8,128)(2,1)}), bf16[8,64,768]{2,1,0:T(8,128)(2,1)S(1)}, u32[]{:S(2)}, u32[]{:S(2)}) async-start(bf16[8,64,768]{2,1,0:T(8,128)(2,1)} %copy.131), calls=%async_computation | async-start | bytes 1572864 | tf_op jit(solution)/shard_map/all_to_all | solution.py:250
  18.7 99.7 %all-gather.2.cloned.1.call-start = ((), (), s32[]{:S(2)}) async-start(), calls=%async_computation.10 | async-start | bytes 2359296 | tf_op jit(solution)/shard_map/all_gather | solution.py:69
  40.6 17.9 %collective-permute-start.11 = (bf16[1,8,64,768]{3,2,1,0:T(8,128)(2,1)S(1)}, bf16[1,8,64,768]{3,2,1,0:T(8,128)(2,1)S(1)}, u32[]{:S(2)}, u32[]{:S(2)}) collective-permute-start(bf16[1,8,64,768]{3,2,1,0:T(8,128)(2,1)S(1)} %bitcast.146), channel_id=1, source_target_pairs={{0,16},{8,24},{16,0},{24,8},{1,17},{9,25},{17,1},{25,9},{2,18},{10... | collective-permute-start | bytes 2359304 | tf_op jit(solution)/shard_map/ppermute | solution.py:204
  42.6 22.0 %collective-permute-start = (bf16[160,2048]{1,0:T(8,128)(2,1)S(1)}, bf16[160,2048]{1,0:T(8,128)(2,1)S(1)}, u32[]{:S(2)}, u32[]{:S(2)}) collective-permute-start(bf16[160,2048]{1,0:T(8,128)(2,1)S(1)} %copy-done.3), channel_id=1, source_target_pairs={{0,2},{2,4},{4,6},{6,7},{7,5},{5,3},{3,1},{1,0},{8,10},{10,12},{12... | collective-permute-start | bytes 1966088 | tf_op jit(solution)/shard_map/ppermute | solution.py:88
  43.0 24.1 %collective-permute-start.4 = (bf16[160,2048]{1,0:T(8,128)(2,1)S(1)}, bf16[160,2048]{1,0:T(8,128)(2,1)}, u32[]{:S(2)}, u32[]{:S(2)}) collective-permute-start(bf16[160,2048]{1,0:T(8,128)(2,1)S(1)} %copy-done.3), channel_id=1, source_target_pairs={{0,1},{2,0},{4,2},{6,4},{7,6},{5,7},{3,5},{1,3},{8,9},{10,8},{12,1... | collective-permute-start | bytes 1966088 | tf_op jit(solution)/shard_map/ppermute | solution.py:88
  59.9 59.6 %collective-permute-start.12 = (bf16[2,8,64,768]{3,2,1,0:T(8,128)(2,1)}, bf16[2,8,64,768]{3,2,1,0:T(8,128)(2,1)}, u32[]{:S(2)}, u32[]{:S(2)}) collective-permute-start(bf16[2,8,64,768]{3,2,1,0:T(8,128)(2,1)} %maximum_select_fusion.3), channel_id=1, source_target_pairs={{0,8},{8,0},{16,24},{24,16},{1,9},{9,1},{17,25},{25,17},{2,10},{10... | collective-permute-start | bytes 4718600 | tf_op jit(solution)/shard_map/ppermute | solution.py:204
  64.6 27.4 %collective-permute-start.1 = (bf16[160,2048]{1,0:T(8,128)(2,1)S(1)}, bf16[160,2048]{1,0:T(8,128)(2,1)}, u32[]{:S(2)}, u32[]{:S(2)}) collective-permute-start(bf16[160,2048]{1,0:T(8,128)(2,1)S(1)} %collective-permute-done), channel_id=1, source_target_pairs={{0,2},{2,4},{4,6},{6,7},{7,5},{5,3},{3,1},{1,0},{8,10},{10,12},{12... | collective-permute-start | bytes 1966088 | tf_op jit(solution)/shard_map/ppermute | solution.py:88
  67.1 33.1 %collective-permute-start.5 = (bf16[160,2048]{1,0:T(8,128)(2,1)}, bf16[160,2048]{1,0:T(8,128)(2,1)}, u32[]{:S(2)}, u32[]{:S(2)}) collective-permute-start(bf16[160,2048]{1,0:T(8,128)(2,1)} %collective-permute-done.4), channel_id=1, source_target_pairs={{0,1},{2,0},{4,2},{6,4},{7,6},{5,7},{3,5},{1,3},{8,9},{10,8},{12,1... | collective-permute-start | bytes 1966088 | tf_op jit(solution)/shard_map/ppermute | solution.py:88
  92.0 26.4 %collective-permute-start.2 = (bf16[160,2048]{1,0:T(8,128)(2,1)}, bf16[160,2048]{1,0:T(8,128)(2,1)}, u32[]{:S(2)}, u32[]{:S(2)}) collective-permute-start(bf16[160,2048]{1,0:T(8,128)(2,1)} %collective-permute-done.1), channel_id=1, source_target_pairs={{0,2},{2,4},{4,6},{6,7},{7,5},{5,3},{3,1},{1,0},{8,10},{10,12},{12... | collective-permute-start | bytes 1966088 | tf_op jit(solution)/shard_map/ppermute | solution.py:88
  123.6 20.8 %collective-permute-start.10 = (bf16[512,512]{1,0:T(8,128)(2,1)S(1)}, bf16[512,512]{1,0:T(8,128)(2,1)S(1)}, u32[]{:S(2)}, u32[]{:S(2)}) collective-permute-start(bf16[512,512]{1,0:T(8,128)(2,1)S(1)} %get-tuple-element.528), channel_id=1, source_target_pairs={{0,16},{8,24},{16,0},{24,8},{1,17},{9,25},{17,1},{25,9},{2,18},{10... | collective-permute-start | bytes 1572872 | tf_op jit(solution)/shard_map/ppermute | solution.py:204
  123.6 33.5 %collective-permute-start.15 = (bf16[512,512]{1,0:T(8,128)(2,1)S(1)}, bf16[512,512]{1,0:T(8,128)(2,1)S(1)}, u32[]{:S(2)}, u32[]{:S(2)}) collective-permute-start(bf16[512,512]{1,0:T(8,128)(2,1)S(1)} %get-tuple-element.527), channel_id=1, source_target_pairs={{0,16},{8,24},{16,0},{24,8},{1,17},{9,25},{17,1},{25,9},{2,18},{10... | collective-permute-start | bytes 1572872 | tf_op jit(solution)/shard_map/ppermute | solution.py:204
  125.7 44.7 %collective-permute-start.18 = (bf16[512,512]{1,0:T(8,128)(2,1)S(1)}, bf16[512,512]{1,0:T(8,128)(2,1)S(1)}, u32[]{:S(2)}, u32[]{:S(2)}) collective-permute-start(bf16[512,512]{1,0:T(8,128)(2,1)S(1)} %get-tuple-element.526), channel_id=1, source_target_pairs={{0,16},{8,24},{16,0},{24,8},{1,17},{9,25},{17,1},{25,9},{2,18},{10... | collective-permute-start | bytes 1572872 | tf_op jit(solution)/shard_map/ppermute | solution.py:204
  128.5 15.9 %collective-permute-start.8 = (bf16[160,2048]{1,0:T(8,128)(2,1)S(1)}, bf16[160,2048]{1,0:T(8,128)(2,1)S(1)}, u32[]{:S(2)}, u32[]{:S(2)}) collective-permute-start(bf16[160,2048]{1,0:T(8,128)(2,1)S(1)} %copy-done.15), channel_id=1, source_target_pairs={{0,2},{2,4},{4,6},{6,7},{7,5},{5,3},{3,1},{1,0},{8,10},{10,12},{12... | collective-permute-start | bytes 1966088 | tf_op jit(solution)/shard_map/ppermute | solution.py:88
  129.6 14.9 %collective-permute-start.9 = (bf16[160,2048]{1,0:T(8,128)(2,1)S(1)}, bf16[160,2048]{1,0:T(8,128)(2,1)S(1)}, u32[]{:S(2)}, u32[]{:S(2)}) collective-permute-start(bf16[160,2048]{1,0:T(8,128)(2,1)S(1)} %copy-done.15), channel_id=1, source_target_pairs={{0,1},{2,0},{4,2},{6,4},{7,6},{5,7},{3,5},{1,3},{8,9},{10,8},{12,1... | collective-permute-start | bytes 1966088 | tf_op jit(solution)/shard_map/ppermute | solution.py:88
  144.3 41.1 %collective-permute-start.21 = (bf16[512,512]{1,0:T(8,128)(2,1)S(1)}, bf16[512,512]{1,0:T(8,128)(2,1)S(1)}, u32[]{:S(2)}, u32[]{:S(2)}) collective-permute-start(bf16[512,512]{1,0:T(8,128)(2,1)S(1)} %get-tuple-element.525), channel_id=1, source_target_pairs={{0,16},{8,24},{16,0},{24,8},{1,17},{9,25},{17,1},{25,9},{2,18},{10... | collective-permute-start | bytes 1572872 | tf_op jit(solution)/shard_map/ppermute | solution.py:204
  157.2 55.9 %collective-permute-start.22 = (bf16[2048,512]{1,0:T(8,128)(2,1)S(1)}, bf16[2048,512]{1,0:T(8,128)(2,1)}, u32[]{:S(2)}, u32[]{:S(2)}) collective-permute-start(bf16[2048,512]{1,0:T(8,128)(2,1)S(1)} %copy-done.2), channel_id=1, source_target_pairs={{0,8},{8,0},{16,24},{24,16},{1,9},{9,1},{17,25},{25,17},{2,10},{10... | collective-permute-start | bytes 6291464 | tf_op jit(solution)/shard_map/ppermute | solution.py:204
  157.3 17.3 %collective-permute-start.16 = (bf16[160,2048]{1,0:T(8,128)(2,1)S(1)}, bf16[160,2048]{1,0:T(8,128)(2,1)S(1)}, u32[]{:S(2)}, u32[]{:S(2)}) collective-permute-start(bf16[160,2048]{1,0:T(8,128)(2,1)S(1)} %collective-permute-done.13), channel_id=1, source_target_pairs={{0,2},{2,4},{4,6},{6,7},{7,5},{5,3},{3,1},{1,0},{8,10},{10,12},{12... | collective-permute-start | bytes 1966088 | tf_op jit(solution)/shard_map/ppermute | solution.py:88
  158.3 16.8 %collective-permute-start.17 = (bf16[160,2048]{1,0:T(8,128)(2,1)S(1)}, bf16[160,2048]{1,0:T(8,128)(2,1)S(1)}, u32[]{:S(2)}, u32[]{:S(2)}) collective-permute-start(bf16[160,2048]{1,0:T(8,128)(2,1)S(1)} %collective-permute-done.14), channel_id=1, source_target_pairs={{0,1},{2,0},{4,2},{6,4},{7,6},{5,7},{3,5},{1,3},{8,9},{10,8},{12,1... | collective-permute-start | bytes 1966088 | tf_op jit(solution)/shard_map/ppermute | solution.py:88
  187.1 34.3 %collective-permute-start.23 = (bf16[2048,512]{1,0:T(8,128)(2,1)}, bf16[2048,512]{1,0:T(8,128)(2,1)}, u32[]{:S(2)}, u32[]{:S(2)}) collective-permute-start(bf16[2048,512]{1,0:T(8,128)(2,1)} %constant_dynamic-update-slice_fusion.18.refs_1_), channel_id=1, source_target_pairs={{0,8},{8,0},{16,24},{24,16},{1,9},{9,1},{17,25},{25,17},{2,10},{10... | collective-permute-start | bytes 6291464 | tf_op jit(solution)/shard_map/ppermute | solution.py:204
  200.3 20.2 %all-to-all-start.1 = ((bf16[8,160,256]{2,1,0:T(8,128)(2,1)}), bf16[8,160,256]{2,1,0:T(8,128)(2,1)S(1)}, u32[]{:S(2)}, u32[]{:S(2)}) async-start(bf16[8,160,256]{2,1,0:T(8,128)(2,1)} %bitcast.28), calls=%async_computation.1 | async-start | bytes 1310720 | tf_op jit(solution)/shard_map/all_to_all | solution.py:250
  231.1 15.3 %collective-permute-start.24 = (bf16[160,2048]{1,0:T(8,128)(2,1)S(1)}, bf16[160,2048]{1,0:T(8,128)(2,1)S(1)}, u32[]{:S(2)}, u32[]{:S(2)}) collective-permute-start(bf16[160,2048]{1,0:T(8,128)(2,1)S(1)} %get-tuple-element.238), channel_id=1, source_target_pairs={{0,2},{2,4},{4,6},{6,7},{7,5},{5,3},{3,1},{1,0},{8,10},{10,12},{12... | collective-permute-start | bytes 1966088 | tf_op jit(solution)/shard_map/ppermute | solution.py:88
  231.7 14.7 %collective-permute-start.25 = (bf16[160,2048]{1,0:T(8,128)(2,1)S(1)}, bf16[160,2048]{1,0:T(8,128)(2,1)S(1)}, u32[]{:S(2)}, u32[]{:S(2)}) collective-permute-start(bf16[160,2048]{1,0:T(8,128)(2,1)S(1)} %get-tuple-element.238), channel_id=1, source_target_pairs={{0,1},{2,0},{4,2},{6,4},{7,6},{5,7},{3,5},{1,3},{8,9},{10,8},{12,1... | collective-permute-start | bytes 1966088 | tf_op jit(solution)/shard_map/ppermute | solution.py:88
  246.4 14.7 %collective-permute-start.26 = (bf16[160,2048]{1,0:T(8,128)(2,1)S(1)}, bf16[160,2048]{1,0:T(8,128)(2,1)}, u32[]{:S(2)}, u32[]{:S(2)}) collective-permute-start(bf16[160,2048]{1,0:T(8,128)(2,1)S(1)} %collective-permute-done.24), channel_id=1, source_target_pairs={{0,2},{2,4},{4,6},{6,7},{7,5},{5,3},{3,1},{1,0},{8,10},{10,12},{12... | collective-permute-start | bytes 1966088 | tf_op jit(solution)/shard_map/ppermute | solution.py:88
  247.7 15.3 %collective-permute-start.27 = (bf16[160,2048]{1,0:T(8,128)(2,1)S(1)}, bf16[160,2048]{1,0:T(8,128)(2,1)S(1)}, u32[]{:S(2)}, u32[]{:S(2)}) collective-permute-start(bf16[160,2048]{1,0:T(8,128)(2,1)S(1)} %collective-permute-done.25), channel_id=1, source_target_pairs={{0,1},{2,0},{4,2},{6,4},{7,6},{5,7},{3,5},{1,3},{8,9},{10,8},{12,1... | collective-permute-start | bytes 1966088 | tf_op jit(solution)/shard_map/ppermute | solution.py:88
  263.0 27.8 %collective-permute-start.29 = (bf16[160,2048]{1,0:T(8,128)(2,1)S(1)}, bf16[160,2048]{1,0:T(8,128)(2,1)}, u32[]{:S(2)}, u32[]{:S(2)}) collective-permute-start(bf16[160,2048]{1,0:T(8,128)(2,1)S(1)} %collective-permute-done.27), channel_id=1, source_target_pairs={{0,1},{2,0},{4,2},{6,4},{7,6},{5,7},{3,5},{1,3},{8,9},{10,8},{12,1... | collective-permute-start | bytes 1966088 | tf_op jit(solution)/shard_map/ppermute | solution.py:88
  263.4 27.4 %collective-permute-start.28 = (bf16[160,2048]{1,0:T(8,128)(2,1)}, bf16[160,2048]{1,0:T(8,128)(2,1)S(1)}, u32[]{:S(2)}, u32[]{:S(2)}) collective-permute-start(bf16[160,2048]{1,0:T(8,128)(2,1)} %collective-permute-done.26), channel_id=1, source_target_pairs={{0,2},{2,4},{4,6},{6,7},{7,5},{5,3},{3,1},{1,0},{8,10},{10,12},{12... | collective-permute-start | bytes 1966088 | tf_op jit(solution)/shard_map/ppermute | solution.py:88
  344.1 28.0 %collective-permute-start.32 = (bf16[80,2048]{1,0:T(8,128)(2,1)}, bf16[80,2048]{1,0:T(8,128)(2,1)}, u32[]{:S(2)}, u32[]{:S(2)}) collective-permute-start(bf16[80,2048]{1,0:T(8,128)(2,1)} %get-tuple-element.518), channel_id=1, source_target_pairs={{0,2},{2,4},{4,6},{6,7},{7,5},{5,3},{3,1},{1,0},{8,10},{10,12},{12... | collective-permute-start | bytes 983048 | tf_op jit(solution)/shard_map/ppermute | solution.py:88
  345.9 26.2 %collective-permute-start.33 = (bf16[80,2048]{1,0:T(8,128)(2,1)}, bf16[80,2048]{1,0:T(8,128)(2,1)}, u32[]{:S(2)}, u32[]{:S(2)}) collective-permute-start(bf16[80,2048]{1,0:T(8,128)(2,1)} %get-tuple-element.517), channel_id=1, source_target_pairs={{0,1},{2,0},{4,2},{6,4},{7,6},{5,7},{3,5},{1,3},{8,9},{10,8},{12,1... | collective-permute-start | bytes 983048 | tf_op jit(solution)/shard_map/ppermute | solution.py:88
  352.1 19.9 %all-to-all-start.3 = ((f32[8,160,2]{1,2,0:T(2,128)}), f32[8,160,2]{1,2,0:T(2,128)S(1)}, u32[]{:S(2)}, u32[]{:S(2)}) async-start(f32[8,160,2]{1,2,0:T(2,128)} %copy.164), calls=%async_computation.3 | async-start | bytes 32768 | tf_op jit(solution)/shard_map/all_to_all | solution.py:250
  355.5 195.9 %reduce-scatter.4.cloned.1.call-start = ((), (), s32[]{:S(2)}) async-start(), calls=%async_computation.11 | async-start | bytes 10485760 | tf_op jit(solution)/shard_map/reduce_scatter | solution.py:900
  374.6 22.7 %collective-permute-start.34 = (bf16[160,2048]{1,0:T(8,128)(2,1)S(1)}, bf16[160,2048]{1,0:T(8,128)(2,1)S(1)}, u32[]{:S(2)}, u32[]{:S(2)}) collective-permute-start(bf16[160,2048]{1,0:T(8,128)(2,1)S(1)} %pad_maximum_fusion.6), channel_id=1, source_target_pairs={{0,2},{2,4},{4,6},{6,7},{7,5},{5,3},{3,1},{1,0},{8,10},{10,12},{12... | collective-permute-start | bytes 1966088 | tf_op jit(solution)/shard_map/ppermute | solution.py:88
  376.7 20.7 %collective-permute-start.35 = (bf16[160,2048]{1,0:T(8,128)(2,1)S(1)}, bf16[160,2048]{1,0:T(8,128)(2,1)S(1)}, u32[]{:S(2)}, u32[]{:S(2)}) collective-permute-start(bf16[160,2048]{1,0:T(8,128)(2,1)S(1)} %pad_maximum_fusion.7), channel_id=1, source_target_pairs={{0,1},{2,0},{4,2},{6,4},{7,6},{5,7},{3,5},{1,3},{8,9},{10,8},{12,1... | collective-permute-start | bytes 1966088 | tf_op jit(solution)/shard_map/ppermute | solution.py:88
  378.3 19.1 %collective-permute-start.36 = (bf16[80,2048]{1,0:T(8,128)(2,1)S(1)}, bf16[80,2048]{1,0:T(8,128)(2,1)S(1)}, u32[]{:S(2)}, u32[]{:S(2)}) collective-permute-start(bf16[80,2048]{1,0:T(8,128)(2,1)S(1)} %get-tuple-element.503), channel_id=1, source_target_pairs={{0,2},{2,4},{4,6},{6,7},{7,5},{5,3},{3,1},{1,0},{8,10},{10,12},{12... | collective-permute-start | bytes 983048 | tf_op jit(solution)/shard_map/ppermute | solution.py:88
  380.3 17.1 %collective-permute-start.37 = (bf16[80,2048]{1,0:T(8,128)(2,1)S(1)}, bf16[80,2048]{1,0:T(8,128)(2,1)S(1)}, u32[]{:S(2)}, u32[]{:S(2)}) collective-permute-start(bf16[80,2048]{1,0:T(8,128)(2,1)S(1)} %get-tuple-element.502), channel_id=1, source_target_pairs={{0,1},{2,0},{4,2},{6,4},{7,6},{5,7},{3,5},{1,3},{8,9},{10,8},{12,1... | collective-permute-start | bytes 983048 | tf_op jit(solution)/shard_map/ppermute | solution.py:88
  399.5 30.6 %collective-permute-start.38 = (bf16[160,2048]{1,0:T(8,128)(2,1)}, bf16[160,2048]{1,0:T(8,128)(2,1)}, u32[]{:S(2)}, u32[]{:S(2)}) collective-permute-start(bf16[160,2048]{1,0:T(8,128)(2,1)} %add_convert_fusion.12), channel_id=1, source_target_pairs={{0,2},{2,4},{4,6},{6,7},{7,5},{5,3},{3,1},{1,0},{8,10},{10,12},{12... | collective-permute-start | bytes 1966088 | tf_op jit(solution)/shard_map/ppermute | solution.py:88
  403.6 26.6 %collective-permute-start.39 = (bf16[160,2048]{1,0:T(8,128)(2,1)}, bf16[160,2048]{1,0:T(8,128)(2,1)}, u32[]{:S(2)}, u32[]{:S(2)}) collective-permute-start(bf16[160,2048]{1,0:T(8,128)(2,1)} %add_convert_fusion.11), channel_id=1, source_target_pairs={{0,1},{2,0},{4,2},{6,4},{7,6},{5,7},{3,5},{1,3},{8,9},{10,8},{12,1... | collective-permute-start | bytes 1966088 | tf_op jit(solution)/shard_map/ppermute | solution.py:88
  405.9 24.3 %collective-permute-start.40 = (bf16[160,2048]{1,0:T(8,128)(2,1)}, bf16[160,2048]{1,0:T(8,128)(2,1)}, u32[]{:S(2)}, u32[]{:S(2)}) collective-permute-start(bf16[160,2048]{1,0:T(8,128)(2,1)} %pad_maximum_fusion.8), channel_id=1, source_target_pairs={{0,2},{2,4},{4,6},{6,7},{7,5},{5,3},{3,1},{1,0},{8,10},{10,12},{12... | collective-permute-start | bytes 1966088 | tf_op jit(solution)/shard_map/ppermute | solution.py:88
  408.7 21.5 %collective-permute-start.41 = (bf16[160,2048]{1,0:T(8,128)(2,1)}, bf16[160,2048]{1,0:T(8,128)(2,1)}, u32[]{:S(2)}, u32[]{:S(2)}) collective-permute-start(bf16[160,2048]{1,0:T(8,128)(2,1)} %pad_maximum_fusion.9), channel_id=1, source_target_pairs={{0,1},{2,0},{4,2},{6,4},{7,6},{5,7},{3,5},{1,3},{8,9},{10,8},{12,1... | collective-permute-start | bytes 1966088 | tf_op jit(solution)/shard_map/ppermute | solution.py:88
  430.2 179.4 %reduce-scatter.6.cloned.1.call-start = ((), (), s32[]{:S(2)}) async-start(), calls=%async_computation.12 | async-start | bytes 10485760 | tf_op jit(solution)/shard_map/reduce_scatter | solution.py:947
  433.6 26.6 %collective-permute-start.42 = (bf16[160,2048]{1,0:T(8,128)(2,1)}, bf16[160,2048]{1,0:T(8,128)(2,1)}, u32[]{:S(2)}, u32[]{:S(2)}) collective-permute-start(bf16[160,2048]{1,0:T(8,128)(2,1)} %get-tuple-element.514), channel_id=1, source_target_pairs={{0,2},{2,4},{4,6},{6,7},{7,5},{5,3},{3,1},{1,0},{8,10},{10,12},{12... | collective-permute-start | bytes 1966088 | tf_op jit(solution)/shard_map/ppermute | solution.py:88
  435.5 24.7 %collective-permute-start.43 = (bf16[160,2048]{1,0:T(8,128)(2,1)}, bf16[160,2048]{1,0:T(8,128)(2,1)}, u32[]{:S(2)}, u32[]{:S(2)}) collective-permute-start(bf16[160,2048]{1,0:T(8,128)(2,1)} %get-tuple-element.513), channel_id=1, source_target_pairs={{0,1},{2,0},{4,2},{6,4},{7,6},{5,7},{3,5},{1,3},{8,9},{10,8},{12,1... | collective-permute-start | bytes 1966088 | tf_op jit(solution)/shard_map/ppermute | solution.py:88
  439.5 20.7 %collective-permute-start.44 = (bf16[160,2048]{1,0:T(8,128)(2,1)}, bf16[160,2048]{1,0:T(8,128)(2,1)}, u32[]{:S(2)}, u32[]{:S(2)}) collective-permute-start(bf16[160,2048]{1,0:T(8,128)(2,1)} %get-tuple-element.499), channel_id=1, source_target_pairs={{0,2},{2,4},{4,6},{6,7},{7,5},{5,3},{3,1},{1,0},{8,10},{10,12},{12... | collective-permute-start | bytes 1966088 | tf_op jit(solution)/shard_map/ppermute | solution.py:88
  441.5 18.7 %collective-permute-start.45 = (bf16[160,2048]{1,0:T(8,128)(2,1)}, bf16[160,2048]{1,0:T(8,128)(2,1)}, u32[]{:S(2)}, u32[]{:S(2)}) collective-permute-start(bf16[160,2048]{1,0:T(8,128)(2,1)} %get-tuple-element.498), channel_id=1, source_target_pairs={{0,1},{2,0},{4,2},{6,4},{7,6},{5,7},{3,5},{1,3},{8,9},{10,8},{12,1... | collective-permute-start | bytes 1966088 | tf_op jit(solution)/shard_map/ppermute | solution.py:88
  463.5 15.2 %collective-permute-start.46 = (bf16[160,2048]{1,0:T(8,128)(2,1)S(1)}, bf16[160,2048]{1,0:T(8,128)(2,1)}, u32[]{:S(2)}, u32[]{:S(2)}) collective-permute-start(bf16[160,2048]{1,0:T(8,128)(2,1)S(1)} %get-tuple-element.497), channel_id=1, source_target_pairs={{0,2},{2,4},{4,6},{6,7},{7,5},{5,3},{3,1},{1,0},{8,10},{10,12},{12... | collective-permute-start | bytes 1966088 | tf_op jit(solution)/shard_map/ppermute | solution.py:88
  465.4 15.9 %collective-permute-start.47 = (bf16[160,2048]{1,0:T(8,128)(2,1)S(1)}, bf16[160,2048]{1,0:T(8,128)(2,1)}, u32[]{:S(2)}, u32[]{:S(2)}) collective-permute-start(bf16[160,2048]{1,0:T(8,128)(2,1)S(1)} %get-tuple-element.496), channel_id=1, source_target_pairs={{0,1},{2,0},{4,2},{6,4},{7,6},{5,7},{3,5},{1,3},{8,9},{10,8},{12,1... | collective-permute-start | bytes 1966088 | tf_op jit(solution)/shard_map/ppermute | solution.py:88
  481.3 23.9 %collective-permute-start.48 = (bf16[160,2048]{1,0:T(8,128)(2,1)}, bf16[160,2048]{1,0:T(8,128)(2,1)S(1)}, u32[]{:S(2)}, u32[]{:S(2)}) collective-permute-start(bf16[160,2048]{1,0:T(8,128)(2,1)} %get-tuple-element.340.grad_ref.refs_0_), channel_id=1, source_target_pairs={{0,2},{2,4},{4,6},{6,7},{7,5},{5,3},{3,1},{1,0},{8,10},{10,12},{12... | collective-permute-start | bytes 1966088 | tf_op jit(solution)/shard_map/ppermute | solution.py:88
  482.7 22.5 %collective-permute-start.49 = (bf16[160,2048]{1,0:T(8,128)(2,1)}, bf16[160,2048]{1,0:T(8,128)(2,1)S(1)}, u32[]{:S(2)}, u32[]{:S(2)}) collective-permute-start(bf16[160,2048]{1,0:T(8,128)(2,1)} %get-tuple-element.340.grad_ref.refs_0_), channel_id=1, source_target_pairs={{0,1},{2,0},{4,2},{6,4},{7,6},{5,7},{3,5},{1,3},{8,9},{10,8},{12,1... | collective-permute-start | bytes 1966088 | tf_op jit(solution)/shard_map/ppermute | solution.py:88
  483.3 27.1 %all-to-all-start.4 = ((bf16[8,160,256]{2,1,0:T(8,128)(2,1)}), bf16[8,160,256]{2,1,0:T(8,128)(2,1)S(1)}, u32[]{:S(2)}, u32[]{:S(2)}) async-start(bf16[8,160,256]{2,1,0:T(8,128)(2,1)} %copy-done.9), calls=%async_computation.4 | async-start | bytes 1310720 | tf_op jit(solution)/shard_map/all_to_all | solution.py:250
  488.3 172.3 %reduce-scatter.8.cloned.1.call-start = ((), (), s32[]{:S(2)}) async-start(), calls=%async_computation.13 | async-start | bytes 10485760 | tf_op jit(solution)/shard_map/reduce_scatter | solution.py:948
  511.3 18.9 %collective-permute-start.50 = (bf16[160,2048]{1,0:T(8,128)(2,1)S(1)}, bf16[160,2048]{1,0:T(8,128)(2,1)}, u32[]{:S(2)}, u32[]{:S(2)}) collective-permute-start(bf16[160,2048]{1,0:T(8,128)(2,1)S(1)} %collective-permute-done.48.refs_2_), channel_id=1, source_target_pairs={{0,2},{2,4},{4,6},{6,7},{7,5},{5,3},{3,1},{1,0},{8,10},{10,12},{12... | collective-permute-start | bytes 1966088 | tf_op jit(solution)/shard_map/ppermute | solution.py:88
  511.3 18.9 %collective-permute-start.51 = (bf16[160,2048]{1,0:T(8,128)(2,1)S(1)}, bf16[160,2048]{1,0:T(8,128)(2,1)S(1)}, u32[]{:S(2)}, u32[]{:S(2)}) collective-permute-start(bf16[160,2048]{1,0:T(8,128)(2,1)S(1)} %collective-permute-done.49.refs_1_), channel_id=1, source_target_pairs={{0,1},{2,0},{4,2},{6,4},{7,6},{5,7},{3,5},{1,3},{8,9},{10,8},{12,1... | collective-permute-start | bytes 1966088 | tf_op jit(solution)/shard_map/ppermute | solution.py:88
  531.1 16.4 %collective-permute-start.52 = (bf16[160,2048]{1,0:T(8,128)(2,1)}, bf16[160,2048]{1,0:T(8,128)(2,1)S(1)}, u32[]{:S(2)}, u32[]{:S(2)}) collective-permute-start(bf16[160,2048]{1,0:T(8,128)(2,1)} %collective-permute-done.50.refs_4_), channel_id=1, source_target_pairs={{0,2},{2,4},{4,6},{6,7},{7,5},{5,3},{3,1},{1,0},{8,10},{10,12},{12... | collective-permute-start | bytes 1966088 | tf_op jit(solution)/shard_map/ppermute | solution.py:88
  531.1 16.5 %collective-permute-start.53 = (bf16[160,2048]{1,0:T(8,128)(2,1)}, bf16[160,2048]{1,0:T(8,128)(2,1)S(1)}, u32[]{:S(2)}, u32[]{:S(2)}) collective-permute-start(bf16[160,2048]{1,0:T(8,128)(2,1)} %copy-done.56), channel_id=1, source_target_pairs={{0,1},{2,0},{4,2},{6,4},{7,6},{5,7},{3,5},{1,3},{8,9},{10,8},{12,1... | collective-permute-start | bytes 1966088 | tf_op jit(solution)/shard_map/ppermute | solution.py:88
  577.5 19.3 %collective-permute-start.61 = (bf16[8,1,64,768]{3,2,1,0:T(8,128)(2,1)}, bf16[8,1,64,768]{3,2,1,0:T(8,128)(2,1)}, u32[]{:S(2)}, u32[]{:S(2)}) collective-permute-start(bf16[8,1,64,768]{3,2,1,0:T(8,128)(2,1)} %constant_dynamic-slice_fusion.1), channel_id=1, source_target_pairs={{0,16},{8,24},{16,0},{24,8},{1,17},{9,25},{17,1},{25,9},{2,18},{10... | collective-permute-start | bytes 2359304 | tf_op jit(solution)/shard_map/ppermute | solution.py:204
  589.3 17.3 %collective-permute-start.59 = (bf16[160,2048]{1,0:T(8,128)(2,1)}, bf16[160,2048]{1,0:T(8,128)(2,1)S(1)}, u32[]{:S(2)}, u32[]{:S(2)}) collective-permute-start(bf16[160,2048]{1,0:T(8,128)(2,1)} %pad_maximum_fusion.11), channel_id=1, source_target_pairs={{0,2},{2,4},{4,6},{6,7},{7,5},{5,3},{3,1},{1,0},{8,10},{10,12},{12... | collective-permute-start | bytes 1966088 | tf_op jit(solution)/shard_map/ppermute | solution.py:88
  589.3 17.5 %collective-permute-start.60 = (bf16[160,2048]{1,0:T(8,128)(2,1)}, bf16[160,2048]{1,0:T(8,128)(2,1)S(1)}, u32[]{:S(2)}, u32[]{:S(2)}) collective-permute-start(bf16[160,2048]{1,0:T(8,128)(2,1)} %pad_maximum_fusion.12), channel_id=1, source_target_pairs={{0,1},{2,0},{4,2},{6,4},{7,6},{5,7},{3,5},{1,3},{8,9},{10,8},{12,1... | collective-permute-start | bytes 1966088 | tf_op jit(solution)/shard_map/ppermute | solution.py:88
  619.1 19.2 %collective-permute-start.63 = (bf16[160,2048]{1,0:T(8,128)(2,1)}, bf16[160,2048]{1,0:T(8,128)(2,1)}, u32[]{:S(2)}, u32[]{:S(2)}) collective-permute-start(bf16[160,2048]{1,0:T(8,128)(2,1)} %get-tuple-element.489), channel_id=1, source_target_pairs={{0,2},{2,4},{4,6},{6,7},{7,5},{5,3},{3,1},{1,0},{8,10},{10,12},{12... | collective-permute-start | bytes 1966088 | tf_op jit(solution)/shard_map/ppermute | solution.py:88
  621.1 18.8 %collective-permute-start.64 = (bf16[160,2048]{1,0:T(8,128)(2,1)}, bf16[160,2048]{1,0:T(8,128)(2,1)}, u32[]{:S(2)}, u32[]{:S(2)}) collective-permute-start(bf16[160,2048]{1,0:T(8,128)(2,1)} %get-tuple-element.488), channel_id=1, source_target_pairs={{0,1},{2,0},{4,2},{6,4},{7,6},{5,7},{3,5},{1,3},{8,9},{10,8},{12,1... | collective-permute-start | bytes 1966088 | tf_op jit(solution)/shard_map/ppermute | solution.py:88
  627.7 29.2 %all-to-all-start.5 = ((bf16[8,64,768]{2,1,0:T(8,128)(2,1)}), bf16[8,64,768]{2,1,0:T(8,128)(2,1)S(1)}, u32[]{:S(2)}, u32[]{:S(2)}) async-start(bf16[8,64,768]{2,1,0:T(8,128)(2,1)} %bitcast.165), calls=%async_computation.6 | async-start | bytes 1572864 | tf_op jit(solution)/shard_map/all_to_all | solution.py:250
  669.6 27.1 %collective-permute-start.68 = (bf16[1,3,64,2048]{3,2,1,0:T(8,128)(2,1)}, bf16[1,3,64,2048]{3,2,1,0:T(8,128)(2,1)S(1)}, u32[]{:S(2)}, u32[]{:S(2)}) collective-permute-start(bf16[1,3,64,2048]{3,2,1,0:T(8,128)(2,1)} %stack.181), channel_id=1, source_target_pairs={{0,16},{8,24},{16,0},{24,8},{1,17},{9,25},{17,1},{25,9},{2,18},{10... | collective-permute-start | bytes 2359304 | tf_op jit(solution)/shard_map/ppermute | solution.py:204
  670.4 20.2 %collective-permute-start.71 = (f32[4640]{0:T(1024)S(1)}, f32[4640]{0:T(1024)S(1)}, u32[]{:S(2)}, u32[]{:S(2)}) collective-permute-start(f32[4640]{0:T(1024)S(1)} %add.623), channel_id=1, source_target_pairs={{0,16},{8,24},{16,0},{24,8},{1,17},{9,25},{17,1},{25,9},{2,18},{10... | collective-permute-start | bytes 55688 | tf_op jit(solution)/shard_map/ppermute | solution.py:204
  674.0 24.4 %collective-permute-start.66 = (bf16[160,2048]{1,0:T(8,128)(2,1)S(1)}, bf16[160,2048]{1,0:T(8,128)(2,1)S(1)}, u32[]{:S(2)}, u32[]{:S(2)}) collective-permute-start(bf16[160,2048]{1,0:T(8,128)(2,1)S(1)} %copy-done.58), channel_id=1, source_target_pairs={{0,2},{2,4},{4,6},{6,7},{7,5},{5,3},{3,1},{1,0},{8,10},{10,12},{12... | collective-permute-start | bytes 1966088 | tf_op jit(solution)/shard_map/ppermute | solution.py:88
  674.0 24.4 %collective-permute-start.67 = (bf16[160,2048]{1,0:T(8,128)(2,1)S(1)}, bf16[160,2048]{1,0:T(8,128)(2,1)S(1)}, u32[]{:S(2)}, u32[]{:S(2)}) collective-permute-start(bf16[160,2048]{1,0:T(8,128)(2,1)S(1)} %copy-done.57), channel_id=1, source_target_pairs={{0,1},{2,0},{4,2},{6,4},{7,6},{5,7},{3,5},{1,3},{8,9},{10,8},{12,1... | collective-permute-start | bytes 1966088 | tf_op jit(solution)/shard_map/ppermute | solution.py:88
  676.0 19.7 %collective-permute-start.69 = (bf16[1,64,2048]{2,1,0:T(8,128)(2,1)S(1)}, bf16[1,64,2048]{2,1,0:T(8,128)(2,1)S(1)}, u32[]{:S(2)}, u32[]{:S(2)}) collective-permute-start(bf16[1,64,2048]{2,1,0:T(8,128)(2,1)S(1)} %copy-done.49), channel_id=1, source_target_pairs={{0,16},{8,24},{16,0},{24,8},{1,17},{9,25},{17,1},{25,9},{2,18},{10... | collective-permute-start | bytes 786440 | tf_op jit(solution)/shard_map/ppermute | solution.py:204
  (136 other events, 1849.8 us)
Sparse Core Ops, SparseCore 0:
  40.7 62.2 all-gather.1
  430.3 72.7 reduce-scatter.3
  505.9 71.7 reduce-scatter.5
  580.1 77.3 reduce-scatter.7

commit v14 on v12

--- a/solution.py
+++ b/solution.py
@@ -548,8 +548,8 @@
         .transpose(1, 0, 2, 3)
         .reshape(model_width, 3 * width_here)
     )
-    tokens_late, output_late, _ = tie(tokens, output_weight, swapped)
-    token_ring = RingGather(tokens_late)
+    output_late = after(output_weight, swapped)
+    token_ring = RingGather(tokens)
     token_ring.start()
     small_flat = after(small_sent.reshape(-1, head_dim), token_ring.received)
     small_all = swap_all(
@@ -604,8 +604,9 @@
     def project(weight, *blocks):
         token_all = jnp.concatenate(blocks, axis=0)
         token_wide = token_all.astype(wide_type)
-        first_all = (token_wide * inverse_rms(token_wide) * prenorm_gain).astype(low_type)
-        return token_all, first_all, mm(first_all, weight, 1, 0)
+        inverse = inverse_rms(token_wide)
+        first_all = (token_wide * inverse * prenorm_gain).astype(low_type)
+        return token_all, inverse, first_all, mm(first_all, weight, 1, 0)
 
     def attend(head, raw):
         turned = []
@@ -622,7 +623,7 @@
         return (*turned, value_low, log_total, mm(weights_low, value_low, 1, 0).astype(low_type))
 
     cot_ring = RingGather(after(cotangent, token_ring.received))
-    token_all, first_all, raw = window(
+    token_all, inverse_all, first_all, raw = window(
         [cot_ring, far_parts[0]], project, head_weight, *token_ring.blocks
     )
     heads = []
@@ -796,7 +797,6 @@
         lambda uback: grad_of(second_all, uback),
         uback_all,
     )
-    mixture = mixture_ring.total()
     mixed_grad = swap.received
 
     sent, gain_parts = (), 0.0
@@ -833,7 +833,7 @@
     def first_work(sent, head):
         first_part = mm(sent, head_weight, 1, 1)
         token_wide = token_all.astype(wide_type)
-        prenorm_part = jnp.sum(first_part * token_wide * inverse_rms(token_wide), axis=0)
+        prenorm_part = jnp.sum(first_part * token_wide * inverse_all, axis=0)
         return first_part.astype(low_type), prenorm_part, rep_scatter(head, 1, scatter_order[:1])
 
     head_part = window([attention_gather], grad_of, first_all, sent)
@@ -892,18 +892,22 @@
         waits=(head_part,),
     )
     head_rows = swap_all(head_part.reshape(group_count, share, 3 * width_here))
+    def layer_work(own, *sums):
+        mixture = sum((part.astype(wide_type) for part in sums), own.astype(wide_type))
+        return (valid_own * (residual + mixture)).astype(low_type)
+
     (output_part, small_sums, gate_total, layer_out), head_rows = window(
         [first_ring],
         lambda output, small, total, sums: (
             rep_scatter(output, 0, scatter_order[1:]),
             small_pieces(small, small_parts),
             split_experts(total),
-            (valid_own * (residual + sums)).astype(low_type),
+            layer_work(*sums),
         ),
         output_part,
         small_swapped,
         gate_sum,
-        mixture,
+        (mixture_part[:row_count], *mixture_ring.sent),
         waits=(head_rows,),
     )
     head_rows = rep_gather(

time: 690 us -> 710 us (1.029)
  other arithmetic: 97.9 us -> 110 us
  local copies, waits for them, and re-layouts: 80 us -> 88.7 us
    ppermute x56, waiting for transfers between devices: 80.7 us -> 63.5 us  [ring_shift(): return lax.ppermute(values, 'ep', pairs)]
    reduce_sum x0 -> x1, other arithmetic: none -> 13.5 us  [first_work(): prenorm_part = jnp.sum(first_part * token_wide * inverse_all, axis=0)]
    all_to_all x7, starting transfers between devices: 34.6 us -> 42.7 us  [swap_all(): return lax.all_to_all(values, 'ep', split_axis=0, concat_axis=0, tiled=True)]
    all_to_all x7, waiting for transfers between devices: 33.6 us -> 41.4 us  [swap_all(): return lax.all_to_all(values, 'ep', split_axis=0, concat_axis=0, tiled=True)]
    unnamed x328 -> x330, local copies, waits for them, and re-layouts: 31.7 us -> 34.5 us
  transfers between devices with their start and end apart: 85 -> 85, of which waited for: 29 -> 26; matrix products, arithmetic and copies ran while one was open for 38% -> 40% of each run, Pallas kernels for 10% -> 10%
where the time goes in v14:
time: 710 us; the launch traced here: 700 us
  waiting for transfers between devices  129 us (18%)
  matrix products  127 us (18%)
  starting transfers between devices  121 us (17%)
  other arithmetic  110 us (15%)
  Pallas kernels  108 us (15%)
  local copies, waits for them, and re-layouts  88.7 us (12%)
  between operations  17 us (2%)
    dot_general x26, matrix products, mm(): lax.dot_general(left, right, (((left_dim,), (right_dim,)), ((), ())), pre...  127 us
    ppermute x56, starting transfers between devices, ring_shift(): return lax.ppermute(values, 'ep', pairs)  65.3 us
    ppermute x56, waiting for transfers between devices, ring_shift(): return lax.ppermute(values, 'ep', pairs)  63.5 us
    all_to_all x7, starting transfers between devices, swap_all(): return lax.all_to_all(values, 'ep', split_axis=0, concat_axis=0, tiled=True)  42.7 us
    all_to_all x7, waiting for transfers between devices, swap_all(): return lax.all_to_all(values, 'ep', split_axis=0, concat_axis=0, tiled=True)  41.4 us
    pallas_call x2, Pallas kernels, expert_pass(): pl.pallas_call(expert_kernel, grid=(experts, steps), in_specs=[pl.BlockSp...  39 us
    unnamed x330, local copies, waits for them, and re-layouts  34.5 us
    pallas_call x2, Pallas kernels, expert_back(): pl.pallas_call(expert_back_kernel, grid=(depth // width,), in_specs=[whol...  33.6 us
  transfers between devices with their start and end apart: 85, of which 26 were waited for; matrix products, arithmetic and copies ran while one was open for 40% of the time, Pallas kernels for 10%

profile of v14, /device:TPU:0, one launch (start us, length us, event | category | flops | bytes accessed | tf_op | source)
XLA Modules:
  0.0 699.7 jit_solution(7078695847746205799)
XLA Ops:
  11.5 7.3 %all-to-all-start = ((bf16[8,64,768]{2,1,0:T(8,128)(2,1)}), bf16[8,64,768]{2,1,0:T(8,128)(2,1)S(1)}, u32[]{:S(2)}, u32[]{:S(2)}) async-start(bf16[8,64,768]{2,1,0:T(8,128)(2,1)} %copy.138), calls=%async_computation | async-start | bytes 1572864 | tf_op jit(solution)/shard_map/all_to_all | solution.py:250
  21.5 18.8 %all-to-all-done = bf16[8,64,768]{2,1,0:T(8,128)(2,1)S(1)} async-done(((bf16[8,64,768]{2,1,0:T(8,128)(2,1)}), bf16[8,64,768]{2,1,0:T(8,128)(2,1)S(1)}, u32[]{:S(2)}, u32[]{:S(2)}) %all-to-all-start) | async-done | bytes 786464 | tf_op jit(solution)/shard_map/all_to_all | solution.py:250
  48.6 11.5 %all-to-all-start.2 = ((bf16[8,52,128]{2,1,0:T(8,128)(2,1)}), bf16[8,52,128]{2,1,0:T(8,128)(2,1)S(1)}, u32[]{:S(2)}, u32[]{:S(2)}) async-start(bf16[8,52,128]{2,1,0:T(8,128)(2,1)} %broadcast_in_dim.188), calls=%async_computation.2 | async-start | bytes 229376 | tf_op jit(solution)/shard_map/all_to_all | solution.py:250
  61.7 3.7 multiply_cosine_fusion
  73.3 4.9 collective-permute-done.11
  81.8 10.3 %collective-permute-done.1 = bf16[160,2048]{1,0:T(8,128)(2,1)} collective-permute-done((bf16[160,2048]{1,0:T(8,128)(2,1)}, bf16[160,2048]{1,0:T(8,128)(2,1)}, u32[]{:S(2)}, u32[]{:S(2)}) %collective-permute-start.1) | collective-permute-done | bytes 655392 | tf_op jit(solution)/shard_map/ppermute | solution.py:88
  92.2 4.5 collective-permute-start.2
  96.6 3.0 collective-permute-done.5
  102.2 10.7 %collective-permute-done.6 = bf16[160,2048]{1,0:T(8,128)(2,1)S(1)} collective-permute-done((bf16[160,2048]{1,0:T(8,128)(2,1)}, bf16[160,2048]{1,0:T(8,128)(2,1)S(1)}, u32[]{:S(2)}, u32[]{:S(2)}) %collective-permute-start.6) | collective-permute-done | bytes 655392 | tf_op jit(solution)/shard_map/ppermute | solution.py:88
  118.9 2.3 maximum_select_fusion
  128.0 3.3 collective-permute-start.9
  140.9 4.3 fusion.72.query_raw_ref.key_raw_ref
  171.6 4.0 collective-permute-done.16
  178.9 6.1 collective-permute-done.19
  185.7 4.8 all-to-all-start.1
  192.5 2.3 constant_dynamic-update-slice_fusion.44
  194.8 2.3 constant_dynamic-update-slice_fusion.43
  200.1 6.7 all-to-all-done.1
  219.2 7.4 %fusion.73.stream_ref = f32[640,2048]{1,0:T(8,128)} fusion(bf16[640,2048]{1,0:T(8,128)(2,1)S(1)} %copy-done.31, bf16[2048,2048]{1,0:T(8,128)(2,1)S(1)} %bitcast.276), kind=kOutput, calls=%fused_computation.327 | convolution fusion | flops 5368709120 | bytes 16252928 | tf_op jit(solution)/shard_map/dot_general | solution.py:60
  227.7 4.1 collective-permute-done.24
  233.8 8.9 %fusion.74.stream_ref = f32[640,2048]{1,0:T(8,128)} fusion(bf16[640,2048]{1,0:T(8,128)(2,1)} %get-tuple-element.240, bf16[2048,2048]{1,0:T(8,128)(2,1)S(1)} %bitcast.277), kind=kOutput, calls=%fused_computation.328 | convolution fusion | flops 5368709120 | bytes 16252928 | tf_op jit(solution)/shard_map/dot_general | solution.py:60
  242.9 3.1 collective-permute-done.26
  253.9 19.5 %shard_map.281 = (bf16[1280,2048]{1,0:T(8,128)(2,1)}, bf16[1280,2048]{1,0:T(8,128)(2,1)}, bf16[1280,2048]{1,0:T(8,128)(2,1)}, f32[2,640,128]{2,1,0:T(8,128)}) custom-call(bf16[640,2048]{1,0:T(8,128)(2,1)} %copy-done.32, bf16[2,2048,1024]{2,1,0:T(8,128)(2,1)} %gate_ref.7, bf16[2,2048,1024]{2,1,0:T(8,128)(2,1)} %up_ref.7, f32[640,2048]{1,0:T(8,128)} %fusion.73.stream_ref, ...), custom_call_target="tpu_custom_call" | custom-call | flops 10737418240 | bytes 42991616 | tf_op jit(solution)/shard_map/pallas_call | solution.py:294
  277.7 2.8 collective-permute-done.30
  287.0 19.5 %shard_map.282 = (bf16[1280,2048]{1,0:T(8,128)(2,1)}, bf16[1280,2048]{1,0:T(8,128)(2,1)}, bf16[1280,2048]{1,0:T(8,128)(2,1)}, f32[2,640,128]{2,1,0:T(8,128)}) custom-call(bf16[640,2048]{1,0:T(8,128)(2,1)} %copy-done.25, bf16[2,2048,1024]{2,1,0:T(8,128)(2,1)} %gate_ref.7, ...), custom_call_target="tpu_custom_call", output_to_operand_aliasing={{0}: (5, {}), {1}: (6, {}), {2}: (7, {})} | custom-call | flops 10737418240 | bytes 42991616 | tf_op jit(solution)/shard_map/pallas_call | solution.py:294
  308.6 16.8 %shard_map.283 = bf16[640,2048]{1,0:T(8,128)(2,1)} custom-call(bf16[1280,2048]{1,0:T(8,128)(2,1)} %get-tuple-element.283.gback_ref, bf16[1280,2048]{1,0:T(8,128)(2,1)} %get-tuple-element.292.uback_ref, bf16[2,2048,1024]{2,1,0:T(8,128)(2,1)} %gate_ref.7, bf16[2,2048,1024]{2,1,0:T(8,128)(2,1)} %up_ref.7), custom_call_target="tpu_custom_call" | custom-call | flops 10737418240 | bytes 24641536 | tf_op jit(solution)/shard_map/pallas_call | solution.py:334
  329.9 3.3 all-to-all-start.3
  333.3 16.5 %convolution_convert_fusion.3 = bf16[1280,2048]{1,0:T(8,128)(2,1)} fusion(bf16[1280,2048]{1,0:T(8,128)(2,1)} %get-tuple-element.276, bf16[2048,2048]{1,0:T(8,128)(2,1)} %bitcast.273), kind=kOutput, calls=%fused_computation.13 | convolution fusion | flops 10740039680 | bytes 18874368 | tf_op jit(solution)/shard_map/dot_general | solution.py:60
  358.7 16.8 %shard_map.284 = bf16[640,2048]{1,0:T(8,128)(2,1)} custom-call(bf16[1280,2048]{1,0:T(8,128)(2,1)} %get-tuple-element.283.gback_ref, bf16[1280,2048]{1,0:T(8,128)(2,1)} %get-tuple-element.292.uback_ref, bf16[2,2048,1024]{2,1,0:T(8,128)(2,1)} %gate_ref.7, bf16[2,2048,1024]{2,1,0:T(8,128)(2,1)} %up_ref.7), custom_call_target="tpu_custom_call" | custom-call | flops 10737418240 | bytes 24641536 | tf_op jit(solution)/shard_map/pallas_call | solution.py:334
  375.5 2.4 add_convert_fusion.11
  378.0 2.3 add_convert_fusion.12
  386.9 15.7 %convolution_convert_fusion.2 = bf16[2048,2048]{1,0:T(8,128)(2,1)} fusion(bf16[1280,2048]{1,0:T(8,128)(2,1)S(1)} %bitcast.171, bf16[1280,2048]{1,0:T(8,128)(2,1)} %get-tuple-element.561), kind=kOutput, calls=%fused_computation.12 | convolution fusion | flops 10741612544 | bytes 18874368 | tf_op jit(solution)/shard_map/dot_general | solution.py:60
  406.2 3.9 collective-permute-done.38
  410.1 3.4 add_convert_fusion.7
  415.6 2.8 add_convert_fusion.9
  418.4 2.4 collective-permute-start.43
  420.8 18.3 %convolution_convert_fusion.1 = bf16[2048,2048]{1,0:T(8,128)(2,1)} fusion(bf16[1280,2048]{1,0:T(8,128)(2,1)} %get-tuple-element.557, bf16[1280,2048]{1,0:T(8,128)(2,1)} %get-tuple-element.283.gback_ref), kind=kOutput, calls=%fused_computation.11 | convolution fusion | flops 10741612544 | bytes 18874368 | tf_op jit(solution)/shard_map/dot_general | solution.py:60
  449.5 2.5 convolution_add_fusion.1
  452.0 2.4 fusion.28
  454.4 2.5 fusion.11
  460.6 5.5 all-to-all-start.4
  466.3 16.7 %convolution_convert_fusion = bf16[2048,2048]{1,0:T(8,128)(2,1)} fusion(bf16[1280,2048]{1,0:T(8,128)(2,1)} %get-tuple-element.557, bf16[1280,2048]{1,0:T(8,128)(2,1)} %get-tuple-element.292.uback_ref), kind=kOutput, calls=%fused_computation.10 | convolution fusion | flops 10741612544 | bytes 18874368 | tf_op jit(solution)/shard_map/dot_general | solution.py:60
  483.1 3.3 all-to-all-done.4.swapped_ref
  491.5 14.8 %shard_map.285 = (bf16[1280,768]{1,0:T(8,128)(2,1)}, f32[2,128]{1,0:T(2,128)}) custom-call(s32[8]{0:T(128)} %stack.156.order_ref, bf16[1280,128]{1,0:T(8,128)(2,1)} %copy-done.47, bf16[1280,128]{1,0:T(8,128)(2,1)} %copy-done.46, bf16[1280,128]{1,0:T(8,128)(2,1)} %slice.504.value_ref, bf16[8,160,256]{2,1,0:T(8,128)(2,1)} %copy-done.12, ...), custom_call_target="tpu_custom_call" | custom-call | flops 2097152000 | bytes 4915200 | tf_op jit(solution)/shard_map/pallas_call | solution.py:421
  510.3 13.4 %shard_map.286 = (bf16[1280,768]{1,0:T(8,128)(2,1)}, f32[2,128]{1,0:T(2,128)}) custom-call(s32[8]{0:T(128)} %stack.156.order_ref, bf16[1280,128]{1,0:T(8,128)(2,1)} %copy-done.45, bf16[1280,128]{1,0:T(8,128)(2,1)} %copy-done.44, bf16[1280,128]{1,0:T(8,128)(2,1)} %slice.503.value_ref, ...), custom_call_target="tpu_custom_call", output_to_operand_aliasing={{0}: (13, {})} | custom-call | flops 2097152000 | bytes 4915200 | tf_op jit(solution)/shard_map/pallas_call | solution.py:421
  528.8 7.7 %convolution_convert_fusion.4 = bf16[2048,768]{1,0:T(8,128)(2,1)S(1)} fusion(bf16[1280,2048]{1,0:T(8,128)(2,1)} %copy-done.20, bf16[1280,768]{1,0:T(8,128)(2,1)} %get-tuple-element.327), kind=kOutput, calls=%fused_computation.18 | convolution fusion | flops 4028104704 | bytes 10354688 | tf_op jit(solution)/shard_map/dot_general | solution.py:60
  540.1 6.9 fusion.75
  547.0 13.5 %multiply_reduce_fusion = (f32[2048]{0:T(1024)S(1)}, bf16[1280,2048]{1,0:T(8,128)(2,1)}) fusion(f32[1280,2048]{1,0:T(8,128)} %fusion.75, bf16[1280,2048]{1,0:T(8,128)(2,1)} %copy-done.3, f32[1280]{0:T(1024)S(1)} %reduce.1), kind=kLoop, calls=%fused_computation.5 | loop fusion | flops 13105152 | bytes 20984832 | tf_op jit(solution)/shard_map/reduce_sum | solution.py:836
  560.5 2.3 fusion.9
  562.8 2.9 fusion.54
  569.8 2.4 collective-permute-start.61
  572.2 6.9 shard_map.287
  586.7 6.0 all-to-all-start.5
  594.7 4.2 convert_element_type.476
  601.8 2.5 add_convert_fusion
  606.3 5.9 collective-permute-done.60
  613.0 3.4 add_convert_fusion.3
  618.6 4.4 all-to-all-start.6
  623.0 2.7 multiply_convert_fusion
  632.2 8.0 %collective-permute-done.67 = f32[4640]{0:T(1024)S(1)} collective-permute-done((f32[4640]{0:T(1024)S(1)}, f32[4640]{0:T(1024)S(1)}, u32[]{:S(2)}, u32[]{:S(2)}) %collective-permute-start.67) | collective-permute-done | bytes 18592 | tf_op jit(solution)/shard_map/ppermute | solution.py:204
  641.5 10.4 %all-to-all-done.6 = bf16[8,64,768]{2,1,0:T(8,128)(2,1)S(1)} async-done(((bf16[8,64,768]{2,1,0:T(8,128)(2,1)}), bf16[8,64,768]{2,1,0:T(8,128)(2,1)S(1)}, u32[]{:S(2)}, u32[]{:S(2)}) %all-to-all-start.6) | async-done | bytes 786464 | tf_op jit(solution)/shard_map/all_to_all | solution.py:250
  653.8 3.3 add_convert_fusion.1
  665.8 11.1 %collective-permute-done.71 = bf16[1,64,2048]{2,1,0:T(8,128)(2,1)} collective-permute-done((bf16[1,64,2048]{2,1,0:T(8,128)(2,1)S(1)}, bf16[1,64,2048]{2,1,0:T(8,128)(2,1)}, u32[]{:S(2)}, u32[]{:S(2)}) %collective-permute-start.71) | collective-permute-done | bytes 262176 | tf_op jit(solution)/shard_map/ppermute | solution.py:204
  682.0 2.7 fusion.17
  (677 shorter events, 233.6 us)
Async XLA Ops:
  11.5 28.8 %all-to-all-start = ((bf16[8,64,768]{2,1,0:T(8,128)(2,1)}), bf16[8,64,768]{2,1,0:T(8,128)(2,1)S(1)}, u32[]{:S(2)}, u32[]{:S(2)}) async-start(bf16[8,64,768]{2,1,0:T(8,128)(2,1)} %copy.138), calls=%async_computation | async-start | bytes 1572864 | tf_op jit(solution)/shard_map/all_to_all | solution.py:250
  18.7 98.4 %all-gather.2.cloned.1.call-start = ((), (), s32[]{:S(2)}) async-start(), calls=%async_computation.10 | async-start | bytes 2359296 | tf_op jit(solution)/shard_map/all_gather | solution.py:69
  18.8 29.1 %collective-permute-start.4 = (bf16[160,2048]{1,0:T(8,128)(2,1)S(1)}, bf16[160,2048]{1,0:T(8,128)(2,1)}, u32[]{:S(2)}, u32[]{:S(2)}) collective-permute-start(bf16[160,2048]{1,0:T(8,128)(2,1)S(1)} %copy-done.8), channel_id=1, source_target_pairs={{0,1},{2,0},{4,2},{6,4},{7,6},{5,7},{3,5},{1,3},{8,9},{10,8},{12,1... | collective-permute-start | bytes 1966088 | tf_op jit(solution)/shard_map/ppermute | solution.py:88
  20.8 27.1 %collective-permute-start = (bf16[160,2048]{1,0:T(8,128)(2,1)S(1)}, bf16[160,2048]{1,0:T(8,128)(2,1)}, u32[]{:S(2)}, u32[]{:S(2)}) collective-permute-start(bf16[160,2048]{1,0:T(8,128)(2,1)S(1)} %copy-done.8), channel_id=1, source_target_pairs={{0,2},{2,4},{4,6},{6,7},{7,5},{5,3},{3,1},{1,0},{8,10},{10,12},{12... | collective-permute-start | bytes 1966088 | tf_op jit(solution)/shard_map/ppermute | solution.py:88
  48.6 18.9 %all-to-all-start.2 = ((bf16[8,52,128]{2,1,0:T(8,128)(2,1)}), bf16[8,52,128]{2,1,0:T(8,128)(2,1)S(1)}, u32[]{:S(2)}, u32[]{:S(2)}) async-start(bf16[8,52,128]{2,1,0:T(8,128)(2,1)} %broadcast_in_dim.188), calls=%async_computation.2 | async-start | bytes 229376 | tf_op jit(solution)/shard_map/all_to_all | solution.py:250
  60.1 18.2 %collective-permute-start.11 = (bf16[1,8,64,768]{3,2,1,0:T(8,128)(2,1)S(1)}, bf16[1,8,64,768]{3,2,1,0:T(8,128)(2,1)S(1)}, u32[]{:S(2)}, u32[]{:S(2)}) collective-permute-start(bf16[1,8,64,768]{3,2,1,0:T(8,128)(2,1)S(1)} %bitcast.166), channel_id=1, source_target_pairs={{0,16},{8,24},{16,0},{24,8},{1,17},{9,25},{17,1},{25,9},{2,18},{10... | collective-permute-start | bytes 2359304 | tf_op jit(solution)/shard_map/ppermute | solution.py:204
  65.4 26.8 %collective-permute-start.1 = (bf16[160,2048]{1,0:T(8,128)(2,1)}, bf16[160,2048]{1,0:T(8,128)(2,1)}, u32[]{:S(2)}, u32[]{:S(2)}) collective-permute-start(bf16[160,2048]{1,0:T(8,128)(2,1)} %collective-permute-done), channel_id=1, source_target_pairs={{0,2},{2,4},{4,6},{6,7},{7,5},{5,3},{3,1},{1,0},{8,10},{10,12},{12... | collective-permute-start | bytes 1966088 | tf_op jit(solution)/shard_map/ppermute | solution.py:88
  67.4 32.3 %collective-permute-start.5 = (bf16[160,2048]{1,0:T(8,128)(2,1)}, bf16[160,2048]{1,0:T(8,128)(2,1)}, u32[]{:S(2)}, u32[]{:S(2)}) collective-permute-start(bf16[160,2048]{1,0:T(8,128)(2,1)} %collective-permute-done.4), channel_id=1, source_target_pairs={{0,1},{2,0},{4,2},{6,4},{7,6},{5,7},{3,5},{1,3},{8,9},{10,8},{12,1... | collective-permute-start | bytes 1966088 | tf_op jit(solution)/shard_map/ppermute | solution.py:88
  79.7 39.2 %collective-permute-start.12 = (bf16[2,8,64,768]{3,2,1,0:T(8,128)(2,1)}, bf16[2,8,64,768]{3,2,1,0:T(8,128)(2,1)}, u32[]{:S(2)}, u32[]{:S(2)}) collective-permute-start(bf16[2,8,64,768]{3,2,1,0:T(8,128)(2,1)} %maximum_select_fusion.3), channel_id=1, source_target_pairs={{0,8},{8,0},{16,24},{24,16},{1,9},{9,1},{17,25},{25,17},{2,10},{10... | collective-permute-start | bytes 4718600 | tf_op jit(solution)/shard_map/ppermute | solution.py:204
  92.2 25.0 %collective-permute-start.2 = (bf16[160,2048]{1,0:T(8,128)(2,1)}, bf16[160,2048]{1,0:T(8,128)(2,1)}, u32[]{:S(2)}, u32[]{:S(2)}) collective-permute-start(bf16[160,2048]{1,0:T(8,128)(2,1)} %collective-permute-done.1), channel_id=1, source_target_pairs={{0,2},{2,4},{4,6},{6,7},{7,5},{5,3},{3,1},{1,0},{8,10},{10,12},{12... | collective-permute-start | bytes 1966088 | tf_op jit(solution)/shard_map/ppermute | solution.py:88
  123.0 23.0 %collective-permute-start.10 = (bf16[512,512]{1,0:T(8,128)(2,1)S(1)}, bf16[512,512]{1,0:T(8,128)(2,1)S(1)}, u32[]{:S(2)}, u32[]{:S(2)}) collective-permute-start(bf16[512,512]{1,0:T(8,128)(2,1)S(1)} %get-tuple-element.528), channel_id=1, source_target_pairs={{0,16},{8,24},{16,0},{24,8},{1,17},{9,25},{17,1},{25,9},{2,18},{10... | collective-permute-start | bytes 1572872 | tf_op jit(solution)/shard_map/ppermute | solution.py:204
  124.4 33.6 %collective-permute-start.15 = (bf16[512,512]{1,0:T(8,128)(2,1)S(1)}, bf16[512,512]{1,0:T(8,128)(2,1)S(1)}, u32[]{:S(2)}, u32[]{:S(2)}) collective-permute-start(bf16[512,512]{1,0:T(8,128)(2,1)S(1)} %get-tuple-element.527), channel_id=1, source_target_pairs={{0,16},{8,24},{16,0},{24,8},{1,17},{9,25},{17,1},{25,9},{2,18},{10... | collective-permute-start | bytes 1572872 | tf_op jit(solution)/shard_map/ppermute | solution.py:204
  125.1 46.5 %collective-permute-start.18 = (bf16[512,512]{1,0:T(8,128)(2,1)S(1)}, bf16[512,512]{1,0:T(8,128)(2,1)S(1)}, u32[]{:S(2)}, u32[]{:S(2)}) collective-permute-start(bf16[512,512]{1,0:T(8,128)(2,1)S(1)} %get-tuple-element.526), channel_id=1, source_target_pairs={{0,16},{8,24},{16,0},{24,8},{1,17},{9,25},{17,1},{25,9},{2,18},{10... | collective-permute-start | bytes 1572872 | tf_op jit(solution)/shard_map/ppermute | solution.py:204
  127.0 19.1 %collective-permute-start.8 = (bf16[160,2048]{1,0:T(8,128)(2,1)S(1)}, bf16[160,2048]{1,0:T(8,128)(2,1)S(1)}, u32[]{:S(2)}, u32[]{:S(2)}) collective-permute-start(bf16[160,2048]{1,0:T(8,128)(2,1)S(1)} %copy-done.13), channel_id=1, source_target_pairs={{0,2},{2,4},{4,6},{6,7},{7,5},{5,3},{3,1},{1,0},{8,10},{10,12},{12... | collective-permute-start | bytes 1966088 | tf_op jit(solution)/shard_map/ppermute | solution.py:88
  128.0 18.1 %collective-permute-start.9 = (bf16[160,2048]{1,0:T(8,128)(2,1)S(1)}, bf16[160,2048]{1,0:T(8,128)(2,1)S(1)}, u32[]{:S(2)}, u32[]{:S(2)}) collective-permute-start(bf16[160,2048]{1,0:T(8,128)(2,1)S(1)} %copy-done.13), channel_id=1, source_target_pairs={{0,1},{2,0},{4,2},{6,4},{7,6},{5,7},{3,5},{1,3},{8,9},{10,8},{12,1... | collective-permute-start | bytes 1966088 | tf_op jit(solution)/shard_map/ppermute | solution.py:88
  146.0 32.9 %collective-permute-start.21 = (bf16[512,512]{1,0:T(8,128)(2,1)S(1)}, bf16[512,512]{1,0:T(8,128)(2,1)}, u32[]{:S(2)}, u32[]{:S(2)}) collective-permute-start(bf16[512,512]{1,0:T(8,128)(2,1)S(1)} %get-tuple-element.525), channel_id=1, source_target_pairs={{0,16},{8,24},{16,0},{24,8},{1,17},{9,25},{17,1},{25,9},{2,18},{10... | collective-permute-start | bytes 1572872 | tf_op jit(solution)/shard_map/ppermute | solution.py:204
  158.0 53.0 %collective-permute-start.22 = (bf16[2048,512]{1,0:T(8,128)(2,1)S(1)}, bf16[2048,512]{1,0:T(8,128)(2,1)}, u32[]{:S(2)}, u32[]{:S(2)}) collective-permute-start(bf16[2048,512]{1,0:T(8,128)(2,1)S(1)} %copy-done.6), channel_id=1, source_target_pairs={{0,8},{8,0},{16,24},{24,16},{1,9},{9,1},{17,25},{25,17},{2,10},{10... | collective-permute-start | bytes 6291464 | tf_op jit(solution)/shard_map/ppermute | solution.py:204
  159.1 16.5 %collective-permute-start.16 = (bf16[160,2048]{1,0:T(8,128)(2,1)S(1)}, bf16[160,2048]{1,0:T(8,128)(2,1)S(1)}, u32[]{:S(2)}, u32[]{:S(2)}) collective-permute-start(bf16[160,2048]{1,0:T(8,128)(2,1)S(1)} %collective-permute-done.13), channel_id=1, source_target_pairs={{0,2},{2,4},{4,6},{6,7},{7,5},{5,3},{3,1},{1,0},{8,10},{10,12},{12... | collective-permute-start | bytes 1966088 | tf_op jit(solution)/shard_map/ppermute | solution.py:88
  159.1 16.5 %collective-permute-start.17 = (bf16[160,2048]{1,0:T(8,128)(2,1)S(1)}, bf16[160,2048]{1,0:T(8,128)(2,1)S(1)}, u32[]{:S(2)}, u32[]{:S(2)}) collective-permute-start(bf16[160,2048]{1,0:T(8,128)(2,1)S(1)} %collective-permute-done.14), channel_id=1, source_target_pairs={{0,1},{2,0},{4,2},{6,4},{7,6},{5,7},{3,5},{1,3},{8,9},{10,8},{12,1... | collective-permute-start | bytes 1966088 | tf_op jit(solution)/shard_map/ppermute | solution.py:88
  185.7 21.2 %all-to-all-start.1 = ((bf16[8,160,256]{2,1,0:T(8,128)(2,1)}), bf16[8,160,256]{2,1,0:T(8,128)(2,1)}, u32[]{:S(2)}, u32[]{:S(2)}) async-start(bf16[8,160,256]{2,1,0:T(8,128)(2,1)} %copy-done.50), calls=%async_computation.1 | async-start | bytes 1310720 | tf_op jit(solution)/shard_map/all_to_all | solution.py:250
  192.5 20.8 %collective-permute-start.23 = (bf16[2048,512]{1,0:T(8,128)(2,1)}, bf16[2048,512]{1,0:T(8,128)(2,1)}, u32[]{:S(2)}, u32[]{:S(2)}) collective-permute-start(bf16[2048,512]{1,0:T(8,128)(2,1)} %constant_dynamic-update-slice_fusion.18), channel_id=1, source_target_pairs={{0,8},{8,0},{16,24},{24,16},{1,9},{9,1},{17,25},{25,17},{2,10},{10... | collective-permute-start | bytes 6291464 | tf_op jit(solution)/shard_map/ppermute | solution.py:204
  216.9 14.9 %collective-permute-start.24 = (bf16[160,2048]{1,0:T(8,128)(2,1)S(1)}, bf16[160,2048]{1,0:T(8,128)(2,1)S(1)}, u32[]{:S(2)}, u32[]{:S(2)}) collective-permute-start(bf16[160,2048]{1,0:T(8,128)(2,1)S(1)} %get-tuple-element.477), channel_id=1, source_target_pairs={{0,2},{2,4},{4,6},{6,7},{7,5},{5,3},{3,1},{1,0},{8,10},{10,12},{12... | collective-permute-start | bytes 1966088 | tf_op jit(solution)/shard_map/ppermute | solution.py:88
  233.0 14.8 %collective-permute-start.27 = (bf16[160,2048]{1,0:T(8,128)(2,1)S(1)}, bf16[160,2048]{1,0:T(8,128)(2,1)S(1)}, u32[]{:S(2)}, u32[]{:S(2)}) collective-permute-start(bf16[160,2048]{1,0:T(8,128)(2,1)S(1)} %collective-permute-done.25), channel_id=1, source_target_pairs={{0,1},{2,0},{4,2},{6,4},{7,6},{5,7},{3,5},{1,3},{8,9},{10,8},{12,1... | collective-permute-start | bytes 1966088 | tf_op jit(solution)/shard_map/ppermute | solution.py:88
  248.0 25.3 %collective-permute-start.29 = (bf16[160,2048]{1,0:T(8,128)(2,1)S(1)}, bf16[160,2048]{1,0:T(8,128)(2,1)S(1)}, u32[]{:S(2)}, u32[]{:S(2)}) collective-permute-start(bf16[160,2048]{1,0:T(8,128)(2,1)S(1)} %collective-permute-done.27), channel_id=1, source_target_pairs={{0,1},{2,0},{4,2},{6,4},{7,6},{5,7},{3,5},{1,3},{8,9},{10,8},{12,1... | collective-permute-start | bytes 1966088 | tf_op jit(solution)/shard_map/ppermute | solution.py:88
  248.1 25.2 %collective-permute-start.28 = (bf16[160,2048]{1,0:T(8,128)(2,1)S(1)}, bf16[160,2048]{1,0:T(8,128)(2,1)S(1)}, u32[]{:S(2)}, u32[]{:S(2)}) collective-permute-start(bf16[160,2048]{1,0:T(8,128)(2,1)S(1)} %collective-permute-done.26), channel_id=1, source_target_pairs={{0,2},{2,4},{4,6},{6,7},{7,5},{5,3},{3,1},{1,0},{8,10},{10,12},{12... | collective-permute-start | bytes 1966088 | tf_op jit(solution)/shard_map/ppermute | solution.py:88
  326.8 23.0 %collective-permute-start.32 = (bf16[80,2048]{1,0:T(8,128)(2,1)S(1)}, bf16[80,2048]{1,0:T(8,128)(2,1)S(1)}, u32[]{:S(2)}, u32[]{:S(2)}) collective-permute-start(bf16[80,2048]{1,0:T(8,128)(2,1)S(1)} %get-tuple-element.518), channel_id=1, source_target_pairs={{0,2},{2,4},{4,6},{6,7},{7,5},{5,3},{3,1},{1,0},{8,10},{10,12},{12... | collective-permute-start | bytes 983048 | tf_op jit(solution)/shard_map/ppermute | solution.py:88
  328.6 21.2 %collective-permute-start.33 = (bf16[80,2048]{1,0:T(8,128)(2,1)S(1)}, bf16[80,2048]{1,0:T(8,128)(2,1)}, u32[]{:S(2)}, u32[]{:S(2)}) collective-permute-start(bf16[80,2048]{1,0:T(8,128)(2,1)S(1)} %get-tuple-element.517), channel_id=1, source_target_pairs={{0,1},{2,0},{4,2},{6,4},{7,6},{5,7},{3,5},{1,3},{8,9},{10,8},{12,1... | collective-permute-start | bytes 983048 | tf_op jit(solution)/shard_map/ppermute | solution.py:88
  329.9 19.9 %all-to-all-start.3 = ((f32[8,160,2]{1,2,0:T(2,128)}), f32[8,160,2]{1,2,0:T(2,128)S(1)}, u32[]{:S(2)}, u32[]{:S(2)}) async-start(f32[8,160,2]{1,2,0:T(2,128)} %copy.172), calls=%async_computation.3 | async-start | bytes 32768 | tf_op jit(solution)/shard_map/all_to_all | solution.py:250
  333.2 195.5 %reduce-scatter.4.cloned.1.call-start = ((), (), s32[]{:S(2)}) async-start(), calls=%async_computation.11 | async-start | bytes 10485760 | tf_op jit(solution)/shard_map/reduce_scatter | solution.py:825
  353.5 22.0 %collective-permute-start.35 = (bf16[160,2048]{1,0:T(8,128)(2,1)S(1)}, bf16[160,2048]{1,0:T(8,128)(2,1)}, u32[]{:S(2)}, u32[]{:S(2)}) collective-permute-start(bf16[160,2048]{1,0:T(8,128)(2,1)S(1)} %pad_maximum_fusion.7), channel_id=1, source_target_pairs={{0,1},{2,0},{4,2},{6,4},{7,6},{5,7},{3,5},{1,3},{8,9},{10,8},{12,1... | collective-permute-start | bytes 1966088 | tf_op jit(solution)/shard_map/ppermute | solution.py:88
  356.3 19.2 %collective-permute-start.34 = (bf16[160,2048]{1,0:T(8,128)(2,1)}, bf16[160,2048]{1,0:T(8,128)(2,1)}, u32[]{:S(2)}, u32[]{:S(2)}) collective-permute-start(bf16[160,2048]{1,0:T(8,128)(2,1)} %pad_maximum_fusion.6), channel_id=1, source_target_pairs={{0,2},{2,4},{4,6},{6,7},{7,5},{5,3},{3,1},{1,0},{8,10},{10,12},{12... | collective-permute-start | bytes 1966088 | tf_op jit(solution)/shard_map/ppermute | solution.py:88
  356.5 19.0 %collective-permute-start.36 = (bf16[80,2048]{1,0:T(8,128)(2,1)}, bf16[80,2048]{1,0:T(8,128)(2,1)S(1)}, u32[]{:S(2)}, u32[]{:S(2)}) collective-permute-start(bf16[80,2048]{1,0:T(8,128)(2,1)} %get-tuple-element.503), channel_id=1, source_target_pairs={{0,2},{2,4},{4,6},{6,7},{7,5},{5,3},{3,1},{1,0},{8,10},{10,12},{12... | collective-permute-start | bytes 983048 | tf_op jit(solution)/shard_map/ppermute | solution.py:88
  358.4 17.1 %collective-permute-start.37 = (bf16[80,2048]{1,0:T(8,128)(2,1)}, bf16[80,2048]{1,0:T(8,128)(2,1)}, u32[]{:S(2)}, u32[]{:S(2)}) collective-permute-start(bf16[80,2048]{1,0:T(8,128)(2,1)} %get-tuple-element.502), channel_id=1, source_target_pairs={{0,1},{2,0},{4,2},{6,4},{7,6},{5,7},{3,5},{1,3},{8,9},{10,8},{12,1... | collective-permute-start | bytes 983048 | tf_op jit(solution)/shard_map/ppermute | solution.py:88
  381.8 23.4 %collective-permute-start.41 = (bf16[160,2048]{1,0:T(8,128)(2,1)S(1)}, bf16[160,2048]{1,0:T(8,128)(2,1)}, u32[]{:S(2)}, u32[]{:S(2)}) collective-permute-start(bf16[160,2048]{1,0:T(8,128)(2,1)S(1)} %pad_maximum_fusion.9), channel_id=1, source_target_pairs={{0,1},{2,0},{4,2},{6,4},{7,6},{5,7},{3,5},{1,3},{8,9},{10,8},{12,1... | collective-permute-start | bytes 1966088 | tf_op jit(solution)/shard_map/ppermute | solution.py:88
  384.6 20.6 %collective-permute-start.40 = (bf16[160,2048]{1,0:T(8,128)(2,1)}, bf16[160,2048]{1,0:T(8,128)(2,1)}, u32[]{:S(2)}, u32[]{:S(2)}) collective-permute-start(bf16[160,2048]{1,0:T(8,128)(2,1)} %pad_maximum_fusion.8), channel_id=1, source_target_pairs={{0,2},{2,4},{4,6},{6,7},{7,5},{5,3},{3,1},{1,0},{8,10},{10,12},{12... | collective-permute-start | bytes 1966088 | tf_op jit(solution)/shard_map/ppermute | solution.py:88
  384.8 21.4 %collective-permute-start.39 = (bf16[160,2048]{1,0:T(8,128)(2,1)}, bf16[160,2048]{1,0:T(8,128)(2,1)S(1)}, u32[]{:S(2)}, u32[]{:S(2)}) collective-permute-start(bf16[160,2048]{1,0:T(8,128)(2,1)} %add_convert_fusion.11), channel_id=1, source_target_pairs={{0,1},{2,0},{4,2},{6,4},{7,6},{5,7},{3,5},{1,3},{8,9},{10,8},{12,1... | collective-permute-start | bytes 1966088 | tf_op jit(solution)/shard_map/ppermute | solution.py:88
  386.6 23.4 %collective-permute-start.38 = (bf16[160,2048]{1,0:T(8,128)(2,1)}, bf16[160,2048]{1,0:T(8,128)(2,1)}, u32[]{:S(2)}, u32[]{:S(2)}) collective-permute-start(bf16[160,2048]{1,0:T(8,128)(2,1)} %add_convert_fusion.12), channel_id=1, source_target_pairs={{0,2},{2,4},{4,6},{6,7},{7,5},{5,3},{3,1},{1,0},{8,10},{10,12},{12... | collective-permute-start | bytes 1966088 | tf_op jit(solution)/shard_map/ppermute | solution.py:88
  410.1 208.5 %reduce-scatter.6.cloned.1.call-start = ((), (), s32[]{:S(2)}) async-start(), calls=%async_computation.12 | async-start | bytes 10485760 | tf_op jit(solution)/shard_map/reduce_scatter | solution.py:872
  413.6 25.6 %collective-permute-start.44 = (bf16[160,2048]{1,0:T(8,128)(2,1)}, bf16[160,2048]{1,0:T(8,128)(2,1)S(1)}, u32[]{:S(2)}, u32[]{:S(2)}) collective-permute-start(bf16[160,2048]{1,0:T(8,128)(2,1)} %get-tuple-element.499), channel_id=1, source_target_pairs={{0,2},{2,4},{4,6},{6,7},{7,5},{5,3},{3,1},{1,0},{8,10},{10,12},{12... | collective-permute-start | bytes 1966088 | tf_op jit(solution)/shard_map/ppermute | solution.py:88
  413.7 25.4 %collective-permute-start.45 = (bf16[160,2048]{1,0:T(8,128)(2,1)}, bf16[160,2048]{1,0:T(8,128)(2,1)}, u32[]{:S(2)}, u32[]{:S(2)}) collective-permute-start(bf16[160,2048]{1,0:T(8,128)(2,1)} %get-tuple-element.498), channel_id=1, source_target_pairs={{0,1},{2,0},{4,2},{6,4},{7,6},{5,7},{3,5},{1,3},{8,9},{10,8},{12,1... | collective-permute-start | bytes 1966088 | tf_op jit(solution)/shard_map/ppermute | solution.py:88
  418.4 20.7 %collective-permute-start.42 = (bf16[160,2048]{1,0:T(8,128)(2,1)}, bf16[160,2048]{1,0:T(8,128)(2,1)S(1)}, u32[]{:S(2)}, u32[]{:S(2)}) collective-permute-start(bf16[160,2048]{1,0:T(8,128)(2,1)} %get-tuple-element.514), channel_id=1, source_target_pairs={{0,2},{2,4},{4,6},{6,7},{7,5},{5,3},{3,1},{1,0},{8,10},{10,12},{12... | collective-permute-start | bytes 1966088 | tf_op jit(solution)/shard_map/ppermute | solution.py:88
  418.4 20.7 %collective-permute-start.43 = (bf16[160,2048]{1,0:T(8,128)(2,1)}, bf16[160,2048]{1,0:T(8,128)(2,1)S(1)}, u32[]{:S(2)}, u32[]{:S(2)}) collective-permute-start(bf16[160,2048]{1,0:T(8,128)(2,1)} %get-tuple-element.513), channel_id=1, source_target_pairs={{0,1},{2,0},{4,2},{6,4},{7,6},{5,7},{3,5},{1,3},{8,9},{10,8},{12,1... | collective-permute-start | bytes 1966088 | tf_op jit(solution)/shard_map/ppermute | solution.py:88
  442.8 14.9 %collective-permute-start.46 = (bf16[160,2048]{1,0:T(8,128)(2,1)S(1)}, bf16[160,2048]{1,0:T(8,128)(2,1)S(1)}, u32[]{:S(2)}, u32[]{:S(2)}) collective-permute-start(bf16[160,2048]{1,0:T(8,128)(2,1)S(1)} %get-tuple-element.497), channel_id=1, source_target_pairs={{0,2},{2,4},{4,6},{6,7},{7,5},{5,3},{3,1},{1,0},{8,10},{10,12},{12... | collective-permute-start | bytes 1966088 | tf_op jit(solution)/shard_map/ppermute | solution.py:88
  442.9 14.8 %collective-permute-start.47 = (bf16[160,2048]{1,0:T(8,128)(2,1)S(1)}, bf16[160,2048]{1,0:T(8,128)(2,1)S(1)}, u32[]{:S(2)}, u32[]{:S(2)}) collective-permute-start(bf16[160,2048]{1,0:T(8,128)(2,1)S(1)} %get-tuple-element.496), channel_id=1, source_target_pairs={{0,1},{2,0},{4,2},{6,4},{7,6},{5,7},{3,5},{1,3},{8,9},{10,8},{12,1... | collective-permute-start | bytes 1966088 | tf_op jit(solution)/shard_map/ppermute | solution.py:88
  458.6 24.4 %collective-permute-start.48 = (bf16[160,2048]{1,0:T(8,128)(2,1)S(1)}, bf16[160,2048]{1,0:T(8,128)(2,1)}, u32[]{:S(2)}, u32[]{:S(2)}) collective-permute-start(bf16[160,2048]{1,0:T(8,128)(2,1)S(1)} %get-tuple-element.336.refs_0_), channel_id=1, source_target_pairs={{0,2},{2,4},{4,6},{6,7},{7,5},{5,3},{3,1},{1,0},{8,10},{10,12},{12... | collective-permute-start | bytes 1966088 | tf_op jit(solution)/shard_map/ppermute | solution.py:88
  459.0 24.1 %collective-permute-start.49 = (bf16[160,2048]{1,0:T(8,128)(2,1)S(1)}, bf16[160,2048]{1,0:T(8,128)(2,1)}, u32[]{:S(2)}, u32[]{:S(2)}) collective-permute-start(bf16[160,2048]{1,0:T(8,128)(2,1)S(1)} %get-tuple-element.336.refs_0_), channel_id=1, source_target_pairs={{0,1},{2,0},{4,2},{6,4},{7,6},{5,7},{3,5},{1,3},{8,9},{10,8},{12,1... | collective-permute-start | bytes 1966088 | tf_op jit(solution)/shard_map/ppermute | solution.py:88
  460.6 25.7 %all-to-all-start.4 = ((bf16[8,160,256]{2,1,0:T(8,128)(2,1)}), bf16[8,160,256]{2,1,0:T(8,128)(2,1)S(1)}, u32[]{:S(2)}, u32[]{:S(2)}) async-start(bf16[8,160,256]{2,1,0:T(8,128)(2,1)} %bitcast.193), calls=%async_computation.4 | async-start | bytes 1310720 | tf_op jit(solution)/shard_map/all_to_all | solution.py:250
  466.1 192.7 %reduce-scatter.8.cloned.1.call-start = ((), (), s32[]{:S(2)}) async-start(), calls=%async_computation.13 | async-start | bytes 10485760 | tf_op jit(solution)/shard_map/reduce_scatter | solution.py:873
  487.2 19.1 %collective-permute-start.50 = (bf16[160,2048]{1,0:T(8,128)(2,1)}, bf16[160,2048]{1,0:T(8,128)(2,1)}, u32[]{:S(2)}, u32[]{:S(2)}) collective-permute-start(bf16[160,2048]{1,0:T(8,128)(2,1)} %collective-permute-done.48.refs_2_), channel_id=1, source_target_pairs={{0,2},{2,4},{4,6},{6,7},{7,5},{5,3},{3,1},{1,0},{8,10},{10,12},{12... | collective-permute-start | bytes 1966088 | tf_op jit(solution)/shard_map/ppermute | solution.py:88
  487.4 18.8 %collective-permute-start.51 = (bf16[160,2048]{1,0:T(8,128)(2,1)}, bf16[160,2048]{1,0:T(8,128)(2,1)S(1)}, u32[]{:S(2)}, u32[]{:S(2)}) collective-permute-start(bf16[160,2048]{1,0:T(8,128)(2,1)} %collective-permute-done.49.refs_1_), channel_id=1, source_target_pairs={{0,1},{2,0},{4,2},{6,4},{7,6},{5,7},{3,5},{1,3},{8,9},{10,8},{12,1... | collective-permute-start | bytes 1966088 | tf_op jit(solution)/shard_map/ppermute | solution.py:88
  507.1 16.6 %collective-permute-start.52 = (bf16[160,2048]{1,0:T(8,128)(2,1)}, bf16[160,2048]{1,0:T(8,128)(2,1)S(1)}, u32[]{:S(2)}, u32[]{:S(2)}) collective-permute-start(bf16[160,2048]{1,0:T(8,128)(2,1)} %collective-permute-done.50.refs_4_), channel_id=1, source_target_pairs={{0,2},{2,4},{4,6},{6,7},{7,5},{5,3},{3,1},{1,0},{8,10},{10,12},{12... | collective-permute-start | bytes 1966088 | tf_op jit(solution)/shard_map/ppermute | solution.py:88
  508.0 15.7 %collective-permute-start.53 = (bf16[160,2048]{1,0:T(8,128)(2,1)}, bf16[160,2048]{1,0:T(8,128)(2,1)S(1)}, u32[]{:S(2)}, u32[]{:S(2)}) collective-permute-start(bf16[160,2048]{1,0:T(8,128)(2,1)} %copy-done.57), channel_id=1, source_target_pairs={{0,1},{2,0},{4,2},{6,4},{7,6},{5,7},{3,5},{1,3},{8,9},{10,8},{12,1... | collective-permute-start | bytes 1966088 | tf_op jit(solution)/shard_map/ppermute | solution.py:88
  539.4 21.1 %collective-permute-start.56 = (bf16[8,2,64,768]{3,2,1,0:T(8,128)(2,1)}, bf16[8,2,64,768]{3,2,1,0:T(8,128)(2,1)}, u32[]{:S(2)}, u32[]{:S(2)}) collective-permute-start(bf16[8,2,64,768]{3,2,1,0:T(8,128)(2,1)} %dynamic-slice_bitcast_fusion), channel_id=1, source_target_pairs={{0,8},{8,0},{16,24},{24,16},{1,9},{9,1},{17,25},{25,17},{2,10},{10... | collective-permute-start | bytes 4718600 | tf_op jit(solution)/shard_map/ppermute | solution.py:204
  569.8 32.0 %collective-permute-start.61 = (bf16[8,1,64,768]{3,2,1,0:T(8,128)(2,1)}, bf16[8,1,64,768]{3,2,1,0:T(8,128)(2,1)}, u32[]{:S(2)}, u32[]{:S(2)}) collective-permute-start(bf16[8,1,64,768]{3,2,1,0:T(8,128)(2,1)} %constant_dynamic-slice_fusion.1), channel_id=1, source_target_pairs={{0,16},{8,24},{16,0},{24,8},{1,17},{9,25},{17,1},{25,9},{2,18},{10... | collective-permute-start | bytes 2359304 | tf_op jit(solution)/shard_map/ppermute | solution.py:204
  583.3 21.0 %collective-permute-start.62 = (bf16[2,64,2048]{2,1,0:T(8,128)(2,1)}, bf16[2,64,2048]{2,1,0:T(8,128)(2,1)}, u32[]{:S(2)}, u32[]{:S(2)}) collective-permute-start(bf16[2,64,2048]{2,1,0:T(8,128)(2,1)} %dynamic-slice_bitcast_fusion.1), channel_id=1, source_target_pairs={{0,8},{8,0},{16,24},{24,16},{1,9},{9,1},{17,25},{25,17},{2,10},{10... | collective-permute-start | bytes 1572872 | tf_op jit(solution)/shard_map/ppermute | solution.py:204
  592.7 19.5 %collective-permute-start.60 = (bf16[160,2048]{1,0:T(8,128)(2,1)}, bf16[160,2048]{1,0:T(8,128)(2,1)S(1)}, u32[]{:S(2)}, u32[]{:S(2)}) collective-permute-start(bf16[160,2048]{1,0:T(8,128)(2,1)} %pad_maximum_fusion.12), channel_id=1, source_target_pairs={{0,1},{2,0},{4,2},{6,4},{7,6},{5,7},{3,5},{1,3},{8,9},{10,8},{12,1... | collective-permute-start | bytes 1966088 | tf_op jit(solution)/shard_map/ppermute | solution.py:88
  594.7 17.6 %collective-permute-start.59 = (bf16[160,2048]{1,0:T(8,128)(2,1)}, bf16[160,2048]{1,0:T(8,128)(2,1)}, u32[]{:S(2)}, u32[]{:S(2)}) collective-permute-start(bf16[160,2048]{1,0:T(8,128)(2,1)} %pad_maximum_fusion.11), channel_id=1, source_target_pairs={{0,2},{2,4},{4,6},{6,7},{7,5},{5,3},{3,1},{1,0},{8,10},{10,12},{12... | collective-permute-start | bytes 1966088 | tf_op jit(solution)/shard_map/ppermute | solution.py:88
  616.4 25.1 %collective-permute-start.63 = (bf16[160,2048]{1,0:T(8,128)(2,1)}, bf16[160,2048]{1,0:T(8,128)(2,1)}, u32[]{:S(2)}, u32[]{:S(2)}) collective-permute-start(bf16[160,2048]{1,0:T(8,128)(2,1)} %get-tuple-element.489), channel_id=1, source_target_pairs={{0,2},{2,4},{4,6},{6,7},{7,5},{5,3},{3,1},{1,0},{8,10},{10,12},{12... | collective-permute-start | bytes 1966088 | tf_op jit(solution)/shard_map/ppermute | solution.py:88
  618.6 22.8 %collective-permute-start.64 = (bf16[160,2048]{1,0:T(8,128)(2,1)}, bf16[160,2048]{1,0:T(8,128)(2,1)}, u32[]{:S(2)}, u32[]{:S(2)}) collective-permute-start(bf16[160,2048]{1,0:T(8,128)(2,1)} %get-tuple-element.488), channel_id=1, source_target_pairs={{0,1},{2,0},{4,2},{6,4},{7,6},{5,7},{3,5},{1,3},{8,9},{10,8},{12,1... | collective-permute-start | bytes 1966088 | tf_op jit(solution)/shard_map/ppermute | solution.py:88
  618.6 33.2 %all-to-all-start.6 = ((bf16[8,64,768]{2,1,0:T(8,128)(2,1)}), bf16[8,64,768]{2,1,0:T(8,128)(2,1)S(1)}, u32[]{:S(2)}, u32[]{:S(2)}) async-start(bf16[8,64,768]{2,1,0:T(8,128)(2,1)} %bitcast.63), calls=%async_computation.7 | async-start | bytes 1572864 | tf_op jit(solution)/shard_map/all_to_all | solution.py:250
  653.5 24.5 %collective-permute-start.70 = (bf16[1,3,64,2048]{3,2,1,0:T(8,128)(2,1)S(1)}, bf16[1,3,64,2048]{3,2,1,0:T(8,128)(2,1)}, u32[]{:S(2)}, u32[]{:S(2)}) collective-permute-start(bf16[1,3,64,2048]{3,2,1,0:T(8,128)(2,1)S(1)} %stack.161), channel_id=1, source_target_pairs={{0,16},{8,24},{16,0},{24,8},{1,17},{9,25},{17,1},{25,9},{2,18},{10... | collective-permute-start | bytes 2359304 | tf_op jit(solution)/shard_map/ppermute | solution.py:204
  657.1 19.8 %collective-permute-start.71 = (bf16[1,64,2048]{2,1,0:T(8,128)(2,1)S(1)}, bf16[1,64,2048]{2,1,0:T(8,128)(2,1)}, u32[]{:S(2)}, u32[]{:S(2)}) collective-permute-start(bf16[1,64,2048]{2,1,0:T(8,128)(2,1)S(1)} %add_convert_fusion.19), channel_id=1, source_target_pairs={{0,16},{8,24},{16,0},{24,8},{1,17},{9,25},{17,1},{25,9},{2,18},{10... | collective-permute-start | bytes 786440 | tf_op jit(solution)/shard_map/ppermute | solution.py:204
  660.6 19.1 %collective-permute-start.68 = (bf16[160,2048]{1,0:T(8,128)(2,1)}, bf16[160,2048]{1,0:T(8,128)(2,1)S(1)}, u32[]{:S(2)}, u32[]{:S(2)}) collective-permute-start(bf16[160,2048]{1,0:T(8,128)(2,1)} %get-tuple-element.487), channel_id=1, source_target_pairs={{0,2},{2,4},{4,6},{6,7},{7,5},{5,3},{3,1},{1,0},{8,10},{10,12},{12... | collective-permute-start | bytes 1966088 | tf_op jit(solution)/shard_map/ppermute | solution.py:88
  660.7 19.1 %collective-permute-start.69 = (bf16[160,2048]{1,0:T(8,128)(2,1)}, bf16[160,2048]{1,0:T(8,128)(2,1)S(1)}, u32[]{:S(2)}, u32[]{:S(2)}) collective-permute-start(bf16[160,2048]{1,0:T(8,128)(2,1)} %get-tuple-element.486), channel_id=1, source_target_pairs={{0,1},{2,0},{4,2},{6,4},{7,6},{5,7},{3,5},{1,3},{8,9},{10,8},{12,1... | collective-permute-start | bytes 1966088 | tf_op jit(solution)/shard_map/ppermute | solution.py:88
  (167 other events, 1827.5 us)
Sparse Core Ops, SparseCore 0:
  42.1 59.5 all-gather.1
  410.2 72.1 reduce-scatter.3
  485.1 71.7 reduce-scatter.5
  559.3 79.2 reduce-scatter.7

commit v15 on v14

--- a/solution.py
+++ b/solution.py
@@ -551,14 +551,6 @@
     output_late = after(output_weight, swapped)
     token_ring = RingGather(tokens)
     token_ring.start()
-    small_flat = after(small_sent.reshape(-1, head_dim), token_ring.received)
-    small_all = swap_all(
-        jnp.broadcast_to(small_flat[None], (group_count,) + small_flat.shape)
-    ).reshape(group_count, row_count + width_here, expert_total)
-    code_all = reorder(small_all[:, :row_count], device_of_slot).reshape(
-        group_rows, expert_total
-    )
-    full_router = small_all[:, row_count:].reshape(model_width, expert_total)
     chunks = 2
     chunk_rows = group_rows // chunks
     blocks_here = group_count // chunks
@@ -604,9 +596,8 @@
     def project(weight, *blocks):
         token_all = jnp.concatenate(blocks, axis=0)
         token_wide = token_all.astype(wide_type)
-        inverse = inverse_rms(token_wide)
-        first_all = (token_wide * inverse * prenorm_gain).astype(low_type)
-        return token_all, inverse, first_all, mm(first_all, weight, 1, 0)
+        first_all = (token_wide * inverse_rms(token_wide) * prenorm_gain).astype(low_type)
+        return token_all, first_all, mm(first_all, weight, 1, 0)
 
     def attend(head, raw):
         turned = []
@@ -623,7 +614,7 @@
         return (*turned, value_low, log_total, mm(weights_low, value_low, 1, 0).astype(low_type))
 
     cot_ring = RingGather(after(cotangent, token_ring.received))
-    token_all, inverse_all, first_all, raw = window(
+    token_all, first_all, raw = window(
         [cot_ring, far_parts[0]], project, head_weight, *token_ring.blocks
     )
     heads = []
@@ -636,7 +627,7 @@
             )
         )
 
-    def order_work(*mixed):
+    def order_work(small, *mixed):
         mixed_low = jnp.concatenate(mixed, axis=1)
         return (
             mixed_low,
@@ -645,11 +636,28 @@
             segment[None, :],
             jnp.stack([querynorm_gain, keynorm_gain]),
             jnp.stack(device_of_slot),
-        )
-
-    mixed_low, mixed_ordered, segment_column, segment_line, norm_gains, slot_order = window(
-        [cot_ring, *far_parts[1 + heads_here :]], order_work, *[head[4] for head in heads]
-    )
+            swap_all(jnp.broadcast_to(small[None], (group_count,) + small.shape)),
+        )
+
+    (
+        mixed_low,
+        mixed_ordered,
+        segment_column,
+        segment_line,
+        norm_gains,
+        slot_order,
+        small_all,
+    ) = window(
+        [cot_ring, *far_parts[1 + heads_here :]],
+        order_work,
+        small_sent.reshape(-1, head_dim),
+        *[head[4] for head in heads],
+    )
+    small_all = small_all.reshape(group_count, row_count + width_here, expert_total)
+    code_all = reorder(small_all[:, :row_count], device_of_slot).reshape(
+        group_rows, expert_total
+    )
+    full_router = small_all[:, row_count:].reshape(model_width, expert_total)
     cot_all = jnp.concatenate(cot_ring.blocks, axis=0)
     output_pieces = {
         0: output_share,
@@ -833,7 +841,7 @@
     def first_work(sent, head):
         first_part = mm(sent, head_weight, 1, 1)
         token_wide = token_all.astype(wide_type)
-        prenorm_part = jnp.sum(first_part * token_wide * inverse_all, axis=0)
+        prenorm_part = jnp.sum(first_part * token_wide * inverse_rms(token_wide), axis=0)
         return first_part.astype(low_type), prenorm_part, rep_scatter(head, 1, scatter_order[:1])
 
     head_part = window([attention_gather], grad_of, first_all, sent)

time: 710 us -> 689 us (0.970)
  waiting for transfers between devices: 129 us -> 153 us
  starting transfers between devices: 121 us -> 99 us
  other arithmetic: 110 us -> 97.4 us
  local copies, waits for them, and re-layouts: 88.7 us -> 78.5 us
    ppermute x56, waiting for transfers between devices: 63.5 us -> 87.7 us  [ring_shift(): return lax.ppermute(values, 'ep', pairs)]
    reduce_sum x1 -> x0, other arithmetic: 13.5 us -> none  [first_work(): prenorm_part = jnp.sum(first_part * token_wide * inverse_all, axis=0)]
    all_to_all x7, starting transfers between devices: 42.7 us -> 30.9 us  [swap_all(): return lax.all_to_all(values, 'ep', split_axis=0, concat_axis=0, tiled=True)]
    ppermute x56, starting transfers between devices: 65.3 us -> 56.3 us  [ring_shift(): return lax.ppermute(values, 'ep', pairs)]
    unnamed x330 -> x310, local copies, waits for them, and re-layouts: 34.5 us -> 30.1 us
  transfers between devices with their start and end apart: 85 -> 85, of which waited for: 26 -> 29; matrix products, arithmetic and copies ran while one was open for 40% -> 39% of each run, Pallas kernels for 10% -> 10%
where the time goes in v15:
time: 689 us; the launch traced here: 681 us
  waiting for transfers between devices  153 us (22%)
  matrix products  129 us (19%)
  Pallas kernels  107 us (16%)
  starting transfers between devices  99 us (14%)
  other arithmetic  97.4 us (14%)
  local copies, waits for them, and re-layouts  78.5 us (11%)
  between operations  17.2 us (2%)
    dot_general x26, matrix products, mm(): lax.dot_general(left, right, (((left_dim,), (right_dim,)), ((), ())), pre...  129 us
    ppermute x56, waiting for transfers between devices, ring_shift(): return lax.ppermute(values, 'ep', pairs)  87.7 us
    ppermute x56, starting transfers between devices, ring_shift(): return lax.ppermute(values, 'ep', pairs)  56.3 us
    all_to_all x7, waiting for transfers between devices, swap_all(): return lax.all_to_all(values, 'ep', split_axis=0, concat_axis=0, tiled=True)  45.6 us
    pallas_call x2, Pallas kernels, expert_pass(): pl.pallas_call(expert_kernel, grid=(experts, steps), in_specs=[pl.BlockSp...  38.9 us
    pallas_call x2, Pallas kernels, expert_back(): pl.pallas_call(expert_back_kernel, grid=(depth // width,), in_specs=[whol...  33.7 us
    all_to_all x7, starting transfers between devices, swap_all(): return lax.all_to_all(values, 'ep', split_axis=0, concat_axis=0, tiled=True)  30.9 us
    convert_element_type x14, other arithmetic, add_low(): return (left.astype(wide_type) + right.astype(wide_type)).astype(low_type)  30.6 us
  transfers between devices with their start and end apart: 85, of which 29 were waited for; matrix products, arithmetic and copies ran while one was open for 39% of the time, Pallas kernels for 10%

profile of v15, /device:TPU:0, one launch (start us, length us, event | category | flops | bytes accessed | tf_op | source)
XLA Modules:
  0.0 680.7 jit_solution(4401342073358181967)
XLA Ops:
  11.4 7.3 %all-to-all-start = ((bf16[8,64,768]{2,1,0:T(8,128)(2,1)}), bf16[8,64,768]{2,1,0:T(8,128)(2,1)S(1)}, u32[]{:S(2)}, u32[]{:S(2)}) async-start(bf16[8,64,768]{2,1,0:T(8,128)(2,1)} %copy.138), calls=%async_computation | async-start | bytes 1572864 | tf_op jit(solution)/shard_map/all_to_all | solution.py:250
  18.8 20.1 %all-to-all-done = bf16[8,64,768]{2,1,0:T(8,128)(2,1)S(1)} async-done(((bf16[8,64,768]{2,1,0:T(8,128)(2,1)}), bf16[8,64,768]{2,1,0:T(8,128)(2,1)S(1)}, u32[]{:S(2)}, u32[]{:S(2)}) %all-to-all-start) | async-done | bytes 786464 | tf_op jit(solution)/shard_map/all_to_all | solution.py:250
  44.8 22.2 %collective-permute-done.4 = bf16[160,2048]{1,0:T(8,128)(2,1)S(1)} collective-permute-done((bf16[160,2048]{1,0:T(8,128)(2,1)S(1)}, bf16[160,2048]{1,0:T(8,128)(2,1)S(1)}, u32[]{:S(2)}, u32[]{:S(2)}) %collective-permute-start.4) | collective-permute-done | bytes 655392 | tf_op jit(solution)/shard_map/ppermute | solution.py:88
  70.9 30.3 %collective-permute-done.5 = bf16[160,2048]{1,0:T(8,128)(2,1)} collective-permute-done((bf16[160,2048]{1,0:T(8,128)(2,1)S(1)}, bf16[160,2048]{1,0:T(8,128)(2,1)}, u32[]{:S(2)}, u32[]{:S(2)}) %collective-permute-start.5) | collective-permute-done | bytes 655392 | tf_op jit(solution)/shard_map/ppermute | solution.py:88
  106.0 3.7 multiply_cosine_fusion
  109.7 4.9 collective-permute-done.6
  117.2 2.3 collective-permute-done.2
  120.6 2.3 maximum_select_fusion
  129.0 2.2 collective-permute-start.9
  139.8 4.3 fusion.75.query_raw_ref.key_raw_ref
  179.3 5.1 all-to-all-start.1
  184.6 2.6 constant_dynamic-update-slice_fusion.43
  193.0 4.2 all-to-all-start.2
  205.3 5.6 all-to-all-done.2
  212.7 2.1 convolution_dynamic-update-slice_fusion.2
  214.9 2.2 convolution_dynamic-update-slice_fusion.1
  223.0 9.7 %fusion.76.stream_ref = f32[640,2048]{1,0:T(8,128)} fusion(bf16[640,2048]{1,0:T(8,128)(2,1)S(1)} %copy-done.31, bf16[2048,2048]{1,0:T(8,128)(2,1)} %bitcast.273), kind=kOutput, calls=%fused_computation.332 | convolution fusion | flops 5368709120 | bytes 16252928 | tf_op jit(solution)/shard_map/dot_general | solution.py:60
  236.8 9.6 %fusion.77.stream_ref = f32[640,2048]{1,0:T(8,128)} fusion(bf16[640,2048]{1,0:T(8,128)(2,1)S(1)} %copy-done.60, bf16[2048,2048]{1,0:T(8,128)(2,1)} %bitcast.274), kind=kOutput, calls=%fused_computation.333 | convolution fusion | flops 5368709120 | bytes 16252928 | tf_op jit(solution)/shard_map/dot_general | solution.py:60
  247.3 3.5 collective-permute-done.27
  251.2 2.2 collective-permute-start.28
  257.1 19.4 %shard_map.281 = (bf16[1280,2048]{1,0:T(8,128)(2,1)}, bf16[1280,2048]{1,0:T(8,128)(2,1)}, bf16[1280,2048]{1,0:T(8,128)(2,1)}, f32[2,640,128]{2,1,0:T(8,128)}) custom-call(bf16[640,2048]{1,0:T(8,128)(2,1)} %copy-done.32, bf16[2,2048,1024]{2,1,0:T(8,128)(2,1)} %gate_ref.7, bf16[2,2048,1024]{2,1,0:T(8,128)(2,1)} %up_ref.7, f32[640,2048]{1,0:T(8,128)} %fusion.76.stream_ref, ...), custom_call_target="tpu_custom_call" | custom-call | flops 10737418240 | bytes 42991616 | tf_op jit(solution)/shard_map/pallas_call | solution.py:294
  280.8 2.9 collective-permute-done.30
  290.0 19.4 %shard_map.282 = (bf16[1280,2048]{1,0:T(8,128)(2,1)}, bf16[1280,2048]{1,0:T(8,128)(2,1)}, bf16[1280,2048]{1,0:T(8,128)(2,1)}, f32[2,640,128]{2,1,0:T(8,128)}) custom-call(bf16[640,2048]{1,0:T(8,128)(2,1)} %copy-done.26, bf16[2,2048,1024]{2,1,0:T(8,128)(2,1)} %gate_ref.7, ...), custom_call_target="tpu_custom_call", output_to_operand_aliasing={{0}: (5, {}), {1}: (6, {}), {2}: (7, {})} | custom-call | flops 10737418240 | bytes 42991616 | tf_op jit(solution)/shard_map/pallas_call | solution.py:294
  309.5 16.8 %shard_map.283 = bf16[640,2048]{1,0:T(8,128)(2,1)} custom-call(bf16[1280,2048]{1,0:T(8,128)(2,1)} %get-tuple-element.284.gback_ref, bf16[1280,2048]{1,0:T(8,128)(2,1)} %get-tuple-element.293.uback_ref, bf16[2,2048,1024]{2,1,0:T(8,128)(2,1)} %gate_ref.7, bf16[2,2048,1024]{2,1,0:T(8,128)(2,1)} %up_ref.7), custom_call_target="tpu_custom_call" | custom-call | flops 10737418240 | bytes 24641536 | tf_op jit(solution)/shard_map/pallas_call | solution.py:334
  326.3 2.4 fusion.60
  332.7 3.3 all-to-all-start.3
  336.3 16.5 %convolution_convert_fusion.3 = bf16[1280,2048]{1,0:T(8,128)(2,1)} fusion(bf16[1280,2048]{1,0:T(8,128)(2,1)} %get-tuple-element.277, bf16[2048,2048]{1,0:T(8,128)(2,1)} %bitcast.275), kind=kOutput, calls=%fused_computation.17 | convolution fusion | flops 10740039680 | bytes 18874368 | tf_op jit(solution)/shard_map/dot_general | solution.py:60
  357.3 2.3 fusion.58
  361.6 16.9 %shard_map.284 = bf16[640,2048]{1,0:T(8,128)(2,1)} custom-call(bf16[1280,2048]{1,0:T(8,128)(2,1)} %get-tuple-element.284.gback_ref, bf16[1280,2048]{1,0:T(8,128)(2,1)} %get-tuple-element.293.uback_ref, bf16[2,2048,1024]{2,1,0:T(8,128)(2,1)} %gate_ref.7, bf16[2,2048,1024]{2,1,0:T(8,128)(2,1)} %up_ref.7), custom_call_target="tpu_custom_call" | custom-call | flops 10737418240 | bytes 24641536 | tf_op jit(solution)/shard_map/pallas_call | solution.py:334
  378.5 2.3 add_convert_fusion.12
  382.6 2.3 add_convert_fusion.11
  389.9 15.7 %convolution_convert_fusion.2 = bf16[2048,2048]{1,0:T(8,128)(2,1)} fusion(bf16[1280,2048]{1,0:T(8,128)(2,1)S(1)} %bitcast.171, bf16[1280,2048]{1,0:T(8,128)(2,1)} %get-tuple-element.561), kind=kOutput, calls=%fused_computation.16 | convolution fusion | flops 10741612544 | bytes 18874368 | tf_op jit(solution)/shard_map/dot_general | solution.py:60
  408.4 3.1 add_convert_fusion.9
  413.5 3.6 add_convert_fusion.7
  417.1 2.2 collective-permute-start.44
  419.6 18.1 %convolution_convert_fusion.1 = bf16[2048,2048]{1,0:T(8,128)(2,1)} fusion(bf16[1280,2048]{1,0:T(8,128)(2,1)} %get-tuple-element.557, bf16[1280,2048]{1,0:T(8,128)(2,1)} %get-tuple-element.284.gback_ref), kind=kOutput, calls=%fused_computation.15 | convolution fusion | flops 10741612544 | bytes 18874368 | tf_op jit(solution)/shard_map/dot_general | solution.py:60
  447.4 2.5 convolution_add_fusion.1
  449.9 2.4 fusion.31
  452.3 2.5 fusion.14
  455.7 2.4 collective-permute-done.46
  461.9 3.8 all-to-all-start.4
  465.9 16.7 %convolution_convert_fusion = bf16[2048,2048]{1,0:T(8,128)(2,1)} fusion(bf16[1280,2048]{1,0:T(8,128)(2,1)} %get-tuple-element.557, bf16[1280,2048]{1,0:T(8,128)(2,1)} %get-tuple-element.293.uback_ref), kind=kOutput, calls=%fused_computation.14 | convolution fusion | flops 10741612544 | bytes 18874368 | tf_op jit(solution)/shard_map/dot_general | solution.py:60
  482.6 5.2 all-to-all-done.4.swapped_ref
  493.0 14.7 %shard_map.285 = (bf16[1280,768]{1,0:T(8,128)(2,1)}, f32[2,128]{1,0:T(2,128)}) custom-call(s32[8]{0:T(128)} %stack.156.order_ref, bf16[1280,128]{1,0:T(8,128)(2,1)} %copy-done.46, bf16[1280,128]{1,0:T(8,128)(2,1)} %copy-done.45, bf16[1280,128]{1,0:T(8,128)(2,1)} %slice.504.value_ref, bf16[8,160,256]{2,1,0:T(8,128)(2,1)} %copy-done.13, ...), custom_call_target="tpu_custom_call" | custom-call | flops 2097152000 | bytes 4915200 | tf_op jit(solution)/shard_map/pallas_call | solution.py:421
  511.9 13.3 %shard_map.286 = (bf16[1280,768]{1,0:T(8,128)(2,1)}, f32[2,128]{1,0:T(2,128)}) custom-call(s32[8]{0:T(128)} %stack.156.order_ref, bf16[1280,128]{1,0:T(8,128)(2,1)} %copy-done.44, bf16[1280,128]{1,0:T(8,128)(2,1)} %copy-done.43, bf16[1280,128]{1,0:T(8,128)(2,1)} %slice.503.value_ref, ...), custom_call_target="tpu_custom_call", output_to_operand_aliasing={{0}: (13, {})} | custom-call | flops 2097152000 | bytes 4915200 | tf_op jit(solution)/shard_map/pallas_call | solution.py:421
  526.8 2.2 collective-permute-start.55
  529.0 7.5 %convolution_convert_fusion.4 = bf16[2048,768]{1,0:T(8,128)(2,1)S(1)} fusion(bf16[1280,2048]{1,0:T(8,128)(2,1)} %copy-done.21, bf16[1280,768]{1,0:T(8,128)(2,1)} %get-tuple-element.328), kind=kOutput, calls=%fused_computation.22 | convolution fusion | flops 4028104704 | bytes 10354688 | tf_op jit(solution)/shard_map/dot_general | solution.py:60
  536.8 3.8 fusion.5
  541.2 7.2 %fusion.4 = (f32[2048]{0:T(1024)}, bf16[1280,2048]{1,0:T(8,128)(2,1)S(1)}) fusion(bf16[1280,2048]{1,0:T(8,128)(2,1)} %copy-done.3, f32[1280]{0:T(1024)S(1)} %add_rsqrt_fusion, bf16[1280,768]{1,0:T(8,128)(2,1)S(1)} %copy-done.35, bf16[2048,768]{1,0:T(8,128)(2,1)S(1)} %bitcast.188), kind=kOutput, calls=%fused_computation.8 | convolution fusion | flops 4039636992 | bytes 15610880 | tf_op jit(solution)/shard_map/dot_general | solution.py:60
  555.4 6.4 shard_map.287
  569.7 3.4 all-to-all-start.5
  575.4 4.1 convert_element_type.476
  581.5 2.4 add_convert_fusion
  585.9 6.2 collective-permute-done.59
  593.6 3.3 add_convert_fusion.3
  599.0 3.9 all-to-all-start.6
  604.9 2.7 multiply_convert_fusion
  609.1 2.3 maximum_convert_fusion
  611.4 7.5 %collective-permute-done.67 = f32[4640]{0:T(1024)S(1)} collective-permute-done((f32[4640]{0:T(1024)S(1)}, f32[4640]{0:T(1024)S(1)}, u32[]{:S(2)}, u32[]{:S(2)}) %collective-permute-start.67) | collective-permute-done | bytes 18592 | tf_op jit(solution)/shard_map/ppermute | solution.py:204
  621.1 10.7 %all-to-all-done.6 = bf16[8,64,768]{2,1,0:T(8,128)(2,1)S(1)} async-done(((bf16[8,64,768]{2,1,0:T(8,128)(2,1)}), bf16[8,64,768]{2,1,0:T(8,128)(2,1)S(1)}, u32[]{:S(2)}, u32[]{:S(2)}) %all-to-all-start.6) | async-done | bytes 786464 | tf_op jit(solution)/shard_map/all_to_all | solution.py:250
  634.4 3.3 add_convert_fusion.1
  642.6 2.3 maximum_convert_fusion.1
  645.7 11.2 %collective-permute-done.71 = bf16[1,64,2048]{2,1,0:T(8,128)(2,1)} collective-permute-done((bf16[1,64,2048]{2,1,0:T(8,128)(2,1)S(1)}, bf16[1,64,2048]{2,1,0:T(8,128)(2,1)}, u32[]{:S(2)}, u32[]{:S(2)}) %collective-permute-start.71) | collective-permute-done | bytes 262176 | tf_op jit(solution)/shard_map/ppermute | solution.py:204
  662.0 2.7 fusion.20
  (655 shorter events, 213.1 us)
Async XLA Ops:
  11.4 27.4 %all-to-all-start = ((bf16[8,64,768]{2,1,0:T(8,128)(2,1)}), bf16[8,64,768]{2,1,0:T(8,128)(2,1)S(1)}, u32[]{:S(2)}, u32[]{:S(2)}) async-start(bf16[8,64,768]{2,1,0:T(8,128)(2,1)} %copy.138), calls=%async_computation | async-start | bytes 1572864 | tf_op jit(solution)/shard_map/all_to_all | solution.py:250
  18.7 100.8 %all-gather.2.cloned.1.call-start = ((), (), s32[]{:S(2)}) async-start(), calls=%async_computation.10 | async-start | bytes 2359296 | tf_op jit(solution)/shard_map/all_gather | solution.py:69
  40.6 26.5 %collective-permute-start.11 = (bf16[1,8,64,768]{3,2,1,0:T(8,128)(2,1)S(1)}, bf16[1,8,64,768]{3,2,1,0:T(8,128)(2,1)S(1)}, u32[]{:S(2)}, u32[]{:S(2)}) collective-permute-start(bf16[1,8,64,768]{3,2,1,0:T(8,128)(2,1)S(1)} %bitcast.166), channel_id=1, source_target_pairs={{0,16},{8,24},{16,0},{24,8},{1,17},{9,25},{17,1},{25,9},{2,18},{10... | collective-permute-start | bytes 2359304 | tf_op jit(solution)/shard_map/ppermute | solution.py:204
  42.2 24.9 %collective-permute-start.4 = (bf16[160,2048]{1,0:T(8,128)(2,1)S(1)}, bf16[160,2048]{1,0:T(8,128)(2,1)S(1)}, u32[]{:S(2)}, u32[]{:S(2)}) collective-permute-start(bf16[160,2048]{1,0:T(8,128)(2,1)S(1)} %copy-done.8), channel_id=1, source_target_pairs={{0,1},{2,0},{4,2},{6,4},{7,6},{5,7},{3,5},{1,3},{8,9},{10,8},{12,1... | collective-permute-start | bytes 1966088 | tf_op jit(solution)/shard_map/ppermute | solution.py:88
  43.5 25.2 %collective-permute-start = (bf16[160,2048]{1,0:T(8,128)(2,1)S(1)}, bf16[160,2048]{1,0:T(8,128)(2,1)}, u32[]{:S(2)}, u32[]{:S(2)}) collective-permute-start(bf16[160,2048]{1,0:T(8,128)(2,1)S(1)} %copy-done.8), channel_id=1, source_target_pairs={{0,2},{2,4},{4,6},{6,7},{7,5},{5,3},{3,1},{1,0},{8,10},{10,12},{12... | collective-permute-start | bytes 1966088 | tf_op jit(solution)/shard_map/ppermute | solution.py:88
  67.1 34.1 %collective-permute-start.5 = (bf16[160,2048]{1,0:T(8,128)(2,1)S(1)}, bf16[160,2048]{1,0:T(8,128)(2,1)}, u32[]{:S(2)}, u32[]{:S(2)}) collective-permute-start(bf16[160,2048]{1,0:T(8,128)(2,1)S(1)} %collective-permute-done.4), channel_id=1, source_target_pairs={{0,1},{2,0},{4,2},{6,4},{7,6},{5,7},{3,5},{1,3},{8,9},{10,8},{12,1... | collective-permute-start | bytes 1966088 | tf_op jit(solution)/shard_map/ppermute | solution.py:88
  68.7 51.9 %collective-permute-start.12 = (bf16[2,8,64,768]{3,2,1,0:T(8,128)(2,1)}, bf16[2,8,64,768]{3,2,1,0:T(8,128)(2,1)}, u32[]{:S(2)}, u32[]{:S(2)}) collective-permute-start(bf16[2,8,64,768]{3,2,1,0:T(8,128)(2,1)} %maximum_select_fusion.3), channel_id=1, source_target_pairs={{0,8},{8,0},{16,24},{24,16},{1,9},{9,1},{17,25},{25,17},{2,10},{10... | collective-permute-start | bytes 4718600 | tf_op jit(solution)/shard_map/ppermute | solution.py:204
  68.8 35.5 %collective-permute-start.1 = (bf16[160,2048]{1,0:T(8,128)(2,1)}, bf16[160,2048]{1,0:T(8,128)(2,1)}, u32[]{:S(2)}, u32[]{:S(2)}) collective-permute-start(bf16[160,2048]{1,0:T(8,128)(2,1)} %collective-permute-done), channel_id=1, source_target_pairs={{0,2},{2,4},{4,6},{6,7},{7,5},{5,3},{3,1},{1,0},{8,10},{10,12},{12... | collective-permute-start | bytes 1966088 | tf_op jit(solution)/shard_map/ppermute | solution.py:88
  104.2 15.3 %collective-permute-start.2 = (bf16[160,2048]{1,0:T(8,128)(2,1)}, bf16[160,2048]{1,0:T(8,128)(2,1)}, u32[]{:S(2)}, u32[]{:S(2)}) collective-permute-start(bf16[160,2048]{1,0:T(8,128)(2,1)} %collective-permute-done.1), channel_id=1, source_target_pairs={{0,2},{2,4},{4,6},{6,7},{7,5},{5,3},{3,1},{1,0},{8,10},{10,12},{12... | collective-permute-start | bytes 1966088 | tf_op jit(solution)/shard_map/ppermute | solution.py:88
  125.4 18.8 %collective-permute-start.10 = (bf16[512,512]{1,0:T(8,128)(2,1)S(1)}, bf16[512,512]{1,0:T(8,128)(2,1)S(1)}, u32[]{:S(2)}, u32[]{:S(2)}) collective-permute-start(bf16[512,512]{1,0:T(8,128)(2,1)S(1)} %get-tuple-element.528), channel_id=1, source_target_pairs={{0,16},{8,24},{16,0},{24,8},{1,17},{9,25},{17,1},{25,9},{2,18},{10... | collective-permute-start | bytes 1572872 | tf_op jit(solution)/shard_map/ppermute | solution.py:204
  126.5 30.2 %collective-permute-start.15 = (bf16[512,512]{1,0:T(8,128)(2,1)S(1)}, bf16[512,512]{1,0:T(8,128)(2,1)S(1)}, u32[]{:S(2)}, u32[]{:S(2)}) collective-permute-start(bf16[512,512]{1,0:T(8,128)(2,1)S(1)} %get-tuple-element.527), channel_id=1, source_target_pairs={{0,16},{8,24},{16,0},{24,8},{1,17},{9,25},{17,1},{25,9},{2,18},{10... | collective-permute-start | bytes 1572872 | tf_op jit(solution)/shard_map/ppermute | solution.py:204
  127.4 45.3 %collective-permute-start.18 = (bf16[512,512]{1,0:T(8,128)(2,1)S(1)}, bf16[512,512]{1,0:T(8,128)(2,1)S(1)}, u32[]{:S(2)}, u32[]{:S(2)}) collective-permute-start(bf16[512,512]{1,0:T(8,128)(2,1)S(1)} %get-tuple-element.526), channel_id=1, source_target_pairs={{0,16},{8,24},{16,0},{24,8},{1,17},{9,25},{17,1},{25,9},{2,18},{10... | collective-permute-start | bytes 1572872 | tf_op jit(solution)/shard_map/ppermute | solution.py:204
  129.0 15.8 %collective-permute-start.8 = (bf16[160,2048]{1,0:T(8,128)(2,1)S(1)}, bf16[160,2048]{1,0:T(8,128)(2,1)S(1)}, u32[]{:S(2)}, u32[]{:S(2)}) collective-permute-start(bf16[160,2048]{1,0:T(8,128)(2,1)S(1)} %copy-done.14), channel_id=1, source_target_pairs={{0,2},{2,4},{4,6},{6,7},{7,5},{5,3},{3,1},{1,0},{8,10},{10,12},{12... | collective-permute-start | bytes 1966088 | tf_op jit(solution)/shard_map/ppermute | solution.py:88
  129.0 15.8 %collective-permute-start.9 = (bf16[160,2048]{1,0:T(8,128)(2,1)S(1)}, bf16[160,2048]{1,0:T(8,128)(2,1)S(1)}, u32[]{:S(2)}, u32[]{:S(2)}) collective-permute-start(bf16[160,2048]{1,0:T(8,128)(2,1)S(1)} %copy-done.14), channel_id=1, source_target_pairs={{0,1},{2,0},{4,2},{6,4},{7,6},{5,7},{3,5},{1,3},{8,9},{10,8},{12,1... | collective-permute-start | bytes 1966088 | tf_op jit(solution)/shard_map/ppermute | solution.py:88
  144.2 45.4 %collective-permute-start.21 = (bf16[512,512]{1,0:T(8,128)(2,1)}, bf16[512,512]{1,0:T(8,128)(2,1)}, u32[]{:S(2)}, u32[]{:S(2)}) collective-permute-start(bf16[512,512]{1,0:T(8,128)(2,1)} %get-tuple-element.525), channel_id=1, source_target_pairs={{0,16},{8,24},{16,0},{24,8},{1,17},{9,25},{17,1},{25,9},{2,18},{10... | collective-permute-start | bytes 1572872 | tf_op jit(solution)/shard_map/ppermute | solution.py:204
  156.7 58.1 %collective-permute-start.22 = (bf16[2048,512]{1,0:T(8,128)(2,1)S(1)}, bf16[2048,512]{1,0:T(8,128)(2,1)}, u32[]{:S(2)}, u32[]{:S(2)}) collective-permute-start(bf16[2048,512]{1,0:T(8,128)(2,1)S(1)} %copy-done.6), channel_id=1, source_target_pairs={{0,8},{8,0},{16,24},{24,16},{1,9},{9,1},{17,25},{25,17},{2,10},{10... | collective-permute-start | bytes 6291464 | tf_op jit(solution)/shard_map/ppermute | solution.py:204
  159.0 15.2 %collective-permute-start.16 = (bf16[160,2048]{1,0:T(8,128)(2,1)S(1)}, bf16[160,2048]{1,0:T(8,128)(2,1)S(1)}, u32[]{:S(2)}, u32[]{:S(2)}) collective-permute-start(bf16[160,2048]{1,0:T(8,128)(2,1)S(1)} %collective-permute-done.13), channel_id=1, source_target_pairs={{0,2},{2,4},{4,6},{6,7},{7,5},{5,3},{3,1},{1,0},{8,10},{10,12},{12... | collective-permute-start | bytes 1966088 | tf_op jit(solution)/shard_map/ppermute | solution.py:88
  159.9 15.1 %collective-permute-start.17 = (bf16[160,2048]{1,0:T(8,128)(2,1)S(1)}, bf16[160,2048]{1,0:T(8,128)(2,1)S(1)}, u32[]{:S(2)}, u32[]{:S(2)}) collective-permute-start(bf16[160,2048]{1,0:T(8,128)(2,1)S(1)} %collective-permute-done.14), channel_id=1, source_target_pairs={{0,1},{2,0},{4,2},{6,4},{7,6},{5,7},{3,5},{1,3},{8,9},{10,8},{12,1... | collective-permute-start | bytes 1966088 | tf_op jit(solution)/shard_map/ppermute | solution.py:88
  175.8 15.8 %collective-permute-start.19 = (bf16[80,2048]{1,0:T(8,128)(2,1)}, bf16[80,2048]{1,0:T(8,128)(2,1)}, u32[]{:S(2)}, u32[]{:S(2)}) collective-permute-start(bf16[80,2048]{1,0:T(8,128)(2,1)} %slice.340), channel_id=1, source_target_pairs={{0,2},{2,4},{4,6},{6,7},{7,5},{5,3},{3,1},{1,0},{8,10},{10,12},{12... | collective-permute-start | bytes 983048 | tf_op jit(solution)/shard_map/ppermute | solution.py:88
  177.3 14.3 %collective-permute-start.20 = (bf16[80,2048]{1,0:T(8,128)(2,1)}, bf16[80,2048]{1,0:T(8,128)(2,1)}, u32[]{:S(2)}, u32[]{:S(2)}) collective-permute-start(bf16[80,2048]{1,0:T(8,128)(2,1)} %slice.341), channel_id=1, source_target_pairs={{0,1},{2,0},{4,2},{6,4},{7,6},{5,7},{3,5},{1,3},{8,9},{10,8},{12,1... | collective-permute-start | bytes 983048 | tf_op jit(solution)/shard_map/ppermute | solution.py:88
  193.0 17.9 %all-to-all-start.2 = ((bf16[8,160,256]{2,1,0:T(8,128)(2,1)}), bf16[8,160,256]{2,1,0:T(8,128)(2,1)}, u32[]{:S(2)}, u32[]{:S(2)}) async-start(bf16[8,160,256]{2,1,0:T(8,128)(2,1)} %copy-done.48), calls=%async_computation.2 | async-start | bytes 1310720 | tf_op jit(solution)/shard_map/all_to_all | solution.py:250
  199.1 17.9 %collective-permute-start.23 = (bf16[2048,512]{1,0:T(8,128)(2,1)}, bf16[2048,512]{1,0:T(8,128)(2,1)}, u32[]{:S(2)}, u32[]{:S(2)}) collective-permute-start(bf16[2048,512]{1,0:T(8,128)(2,1)} %constant_dynamic-update-slice_fusion.18), channel_id=1, source_target_pairs={{0,8},{8,0},{16,24},{24,16},{1,9},{9,1},{17,25},{25,17},{2,10},{10... | collective-permute-start | bytes 6291464 | tf_op jit(solution)/shard_map/ppermute | solution.py:204
  236.2 14.6 %collective-permute-start.27 = (bf16[160,2048]{1,0:T(8,128)(2,1)S(1)}, bf16[160,2048]{1,0:T(8,128)(2,1)S(1)}, u32[]{:S(2)}, u32[]{:S(2)}) collective-permute-start(bf16[160,2048]{1,0:T(8,128)(2,1)S(1)} %collective-permute-done.25), channel_id=1, source_target_pairs={{0,1},{2,0},{4,2},{6,4},{7,6},{5,7},{3,5},{1,3},{8,9},{10,8},{12,1... | collective-permute-start | bytes 1966088 | tf_op jit(solution)/shard_map/ppermute | solution.py:88
  250.9 25.7 %collective-permute-start.29 = (bf16[160,2048]{1,0:T(8,128)(2,1)S(1)}, bf16[160,2048]{1,0:T(8,128)(2,1)S(1)}, u32[]{:S(2)}, u32[]{:S(2)}) collective-permute-start(bf16[160,2048]{1,0:T(8,128)(2,1)S(1)} %collective-permute-done.27), channel_id=1, source_target_pairs={{0,1},{2,0},{4,2},{6,4},{7,6},{5,7},{3,5},{1,3},{8,9},{10,8},{12,1... | collective-permute-start | bytes 1966088 | tf_op jit(solution)/shard_map/ppermute | solution.py:88
  251.2 25.4 %collective-permute-start.28 = (bf16[160,2048]{1,0:T(8,128)(2,1)S(1)}, bf16[160,2048]{1,0:T(8,128)(2,1)S(1)}, u32[]{:S(2)}, u32[]{:S(2)}) collective-permute-start(bf16[160,2048]{1,0:T(8,128)(2,1)S(1)} %collective-permute-done.26), channel_id=1, source_target_pairs={{0,2},{2,4},{4,6},{6,7},{7,5},{5,3},{3,1},{1,0},{8,10},{10,12},{12... | collective-permute-start | bytes 1966088 | tf_op jit(solution)/shard_map/ppermute | solution.py:88
  328.7 24.1 %collective-permute-start.32 = (bf16[80,2048]{1,0:T(8,128)(2,1)}, bf16[80,2048]{1,0:T(8,128)(2,1)}, u32[]{:S(2)}, u32[]{:S(2)}) collective-permute-start(bf16[80,2048]{1,0:T(8,128)(2,1)} %get-tuple-element.518), channel_id=1, source_target_pairs={{0,2},{2,4},{4,6},{6,7},{7,5},{5,3},{3,1},{1,0},{8,10},{10,12},{12... | collective-permute-start | bytes 983048 | tf_op jit(solution)/shard_map/ppermute | solution.py:88
  330.4 22.4 %collective-permute-start.33 = (bf16[80,2048]{1,0:T(8,128)(2,1)}, bf16[80,2048]{1,0:T(8,128)(2,1)}, u32[]{:S(2)}, u32[]{:S(2)}) collective-permute-start(bf16[80,2048]{1,0:T(8,128)(2,1)} %get-tuple-element.517), channel_id=1, source_target_pairs={{0,1},{2,0},{4,2},{6,4},{7,6},{5,7},{3,5},{1,3},{8,9},{10,8},{12,1... | collective-permute-start | bytes 983048 | tf_op jit(solution)/shard_map/ppermute | solution.py:88
  332.7 20.1 %all-to-all-start.3 = ((f32[8,160,2]{1,2,0:T(2,128)}), f32[8,160,2]{1,2,0:T(2,128)S(1)}, u32[]{:S(2)}, u32[]{:S(2)}) async-start(f32[8,160,2]{1,2,0:T(2,128)} %copy.172), calls=%async_computation.3 | async-start | bytes 32768 | tf_op jit(solution)/shard_map/all_to_all | solution.py:250
  336.0 193.0 %reduce-scatter.4.cloned.1.call-start = ((), (), s32[]{:S(2)}) async-start(), calls=%async_computation.11 | async-start | bytes 10485760 | tf_op jit(solution)/shard_map/reduce_scatter | solution.py:833
  354.4 24.1 %collective-permute-start.34 = (bf16[160,2048]{1,0:T(8,128)(2,1)S(1)}, bf16[160,2048]{1,0:T(8,128)(2,1)}, u32[]{:S(2)}, u32[]{:S(2)}) collective-permute-start(bf16[160,2048]{1,0:T(8,128)(2,1)S(1)} %pad_maximum_fusion.6), channel_id=1, source_target_pairs={{0,2},{2,4},{4,6},{6,7},{7,5},{5,3},{3,1},{1,0},{8,10},{10,12},{12... | collective-permute-start | bytes 1966088 | tf_op jit(solution)/shard_map/ppermute | solution.py:88
  357.2 21.3 %collective-permute-start.35 = (bf16[160,2048]{1,0:T(8,128)(2,1)}, bf16[160,2048]{1,0:T(8,128)(2,1)}, u32[]{:S(2)}, u32[]{:S(2)}) collective-permute-start(bf16[160,2048]{1,0:T(8,128)(2,1)} %pad_maximum_fusion.7), channel_id=1, source_target_pairs={{0,1},{2,0},{4,2},{6,4},{7,6},{5,7},{3,5},{1,3},{8,9},{10,8},{12,1... | collective-permute-start | bytes 1966088 | tf_op jit(solution)/shard_map/ppermute | solution.py:88
  359.6 18.9 %collective-permute-start.36 = (bf16[80,2048]{1,0:T(8,128)(2,1)}, bf16[80,2048]{1,0:T(8,128)(2,1)}, u32[]{:S(2)}, u32[]{:S(2)}) collective-permute-start(bf16[80,2048]{1,0:T(8,128)(2,1)} %get-tuple-element.503), channel_id=1, source_target_pairs={{0,2},{2,4},{4,6},{6,7},{7,5},{5,3},{3,1},{1,0},{8,10},{10,12},{12... | collective-permute-start | bytes 983048 | tf_op jit(solution)/shard_map/ppermute | solution.py:88
  361.5 17.0 %collective-permute-start.37 = (bf16[80,2048]{1,0:T(8,128)(2,1)S(1)}, bf16[80,2048]{1,0:T(8,128)(2,1)}, u32[]{:S(2)}, u32[]{:S(2)}) collective-permute-start(bf16[80,2048]{1,0:T(8,128)(2,1)S(1)} %get-tuple-element.502), channel_id=1, source_target_pairs={{0,1},{2,0},{4,2},{6,4},{7,6},{5,7},{3,5},{1,3},{8,9},{10,8},{12,1... | collective-permute-start | bytes 983048 | tf_op jit(solution)/shard_map/ppermute | solution.py:88
  380.8 26.6 %collective-permute-start.38 = (bf16[160,2048]{1,0:T(8,128)(2,1)}, bf16[160,2048]{1,0:T(8,128)(2,1)}, u32[]{:S(2)}, u32[]{:S(2)}) collective-permute-start(bf16[160,2048]{1,0:T(8,128)(2,1)} %add_convert_fusion.12), channel_id=1, source_target_pairs={{0,2},{2,4},{4,6},{6,7},{7,5},{5,3},{3,1},{1,0},{8,10},{10,12},{12... | collective-permute-start | bytes 1966088 | tf_op jit(solution)/shard_map/ppermute | solution.py:88
  385.0 22.4 %collective-permute-start.39 = (bf16[160,2048]{1,0:T(8,128)(2,1)}, bf16[160,2048]{1,0:T(8,128)(2,1)}, u32[]{:S(2)}, u32[]{:S(2)}) collective-permute-start(bf16[160,2048]{1,0:T(8,128)(2,1)} %add_convert_fusion.11), channel_id=1, source_target_pairs={{0,1},{2,0},{4,2},{6,4},{7,6},{5,7},{3,5},{1,3},{8,9},{10,8},{12,1... | collective-permute-start | bytes 1966088 | tf_op jit(solution)/shard_map/ppermute | solution.py:88
  386.7 20.7 %collective-permute-start.40 = (bf16[160,2048]{1,0:T(8,128)(2,1)S(1)}, bf16[160,2048]{1,0:T(8,128)(2,1)}, u32[]{:S(2)}, u32[]{:S(2)}) collective-permute-start(bf16[160,2048]{1,0:T(8,128)(2,1)S(1)} %pad_maximum_fusion.8), channel_id=1, source_target_pairs={{0,2},{2,4},{4,6},{6,7},{7,5},{5,3},{3,1},{1,0},{8,10},{10,12},{12... | collective-permute-start | bytes 1966088 | tf_op jit(solution)/shard_map/ppermute | solution.py:88
  389.5 18.9 %collective-permute-start.41 = (bf16[160,2048]{1,0:T(8,128)(2,1)}, bf16[160,2048]{1,0:T(8,128)(2,1)}, u32[]{:S(2)}, u32[]{:S(2)}) collective-permute-start(bf16[160,2048]{1,0:T(8,128)(2,1)} %pad_maximum_fusion.9), channel_id=1, source_target_pairs={{0,1},{2,0},{4,2},{6,4},{7,6},{5,7},{3,5},{1,3},{8,9},{10,8},{12,1... | collective-permute-start | bytes 1966088 | tf_op jit(solution)/shard_map/ppermute | solution.py:88
  408.4 194.5 %reduce-scatter.6.cloned.1.call-start = ((), (), s32[]{:S(2)}) async-start(), calls=%async_computation.12 | async-start | bytes 10485760 | tf_op jit(solution)/shard_map/reduce_scatter | solution.py:880
  411.5 26.2 %collective-permute-start.42 = (bf16[160,2048]{1,0:T(8,128)(2,1)}, bf16[160,2048]{1,0:T(8,128)(2,1)S(1)}, u32[]{:S(2)}, u32[]{:S(2)}) collective-permute-start(bf16[160,2048]{1,0:T(8,128)(2,1)} %get-tuple-element.514), channel_id=1, source_target_pairs={{0,2},{2,4},{4,6},{6,7},{7,5},{5,3},{3,1},{1,0},{8,10},{10,12},{12... | collective-permute-start | bytes 1966088 | tf_op jit(solution)/shard_map/ppermute | solution.py:88
  412.9 24.7 %collective-permute-start.43 = (bf16[160,2048]{1,0:T(8,128)(2,1)S(1)}, bf16[160,2048]{1,0:T(8,128)(2,1)S(1)}, u32[]{:S(2)}, u32[]{:S(2)}) collective-permute-start(bf16[160,2048]{1,0:T(8,128)(2,1)S(1)} %get-tuple-element.513), channel_id=1, source_target_pairs={{0,1},{2,0},{4,2},{6,4},{7,6},{5,7},{3,5},{1,3},{8,9},{10,8},{12,1... | collective-permute-start | bytes 1966088 | tf_op jit(solution)/shard_map/ppermute | solution.py:88
  417.1 20.6 %collective-permute-start.44 = (bf16[160,2048]{1,0:T(8,128)(2,1)}, bf16[160,2048]{1,0:T(8,128)(2,1)S(1)}, u32[]{:S(2)}, u32[]{:S(2)}) collective-permute-start(bf16[160,2048]{1,0:T(8,128)(2,1)} %get-tuple-element.499), channel_id=1, source_target_pairs={{0,2},{2,4},{4,6},{6,7},{7,5},{5,3},{3,1},{1,0},{8,10},{10,12},{12... | collective-permute-start | bytes 1966088 | tf_op jit(solution)/shard_map/ppermute | solution.py:88
  419.3 18.6 %collective-permute-start.45 = (bf16[160,2048]{1,0:T(8,128)(2,1)}, bf16[160,2048]{1,0:T(8,128)(2,1)}, u32[]{:S(2)}, u32[]{:S(2)}) collective-permute-start(bf16[160,2048]{1,0:T(8,128)(2,1)} %get-tuple-element.498), channel_id=1, source_target_pairs={{0,1},{2,0},{4,2},{6,4},{7,6},{5,7},{3,5},{1,3},{8,9},{10,8},{12,1... | collective-permute-start | bytes 1966088 | tf_op jit(solution)/shard_map/ppermute | solution.py:88
  440.7 17.3 %collective-permute-start.46 = (bf16[160,2048]{1,0:T(8,128)(2,1)S(1)}, bf16[160,2048]{1,0:T(8,128)(2,1)S(1)}, u32[]{:S(2)}, u32[]{:S(2)}) collective-permute-start(bf16[160,2048]{1,0:T(8,128)(2,1)S(1)} %get-tuple-element.497), channel_id=1, source_target_pairs={{0,2},{2,4},{4,6},{6,7},{7,5},{5,3},{3,1},{1,0},{8,10},{10,12},{12... | collective-permute-start | bytes 1966088 | tf_op jit(solution)/shard_map/ppermute | solution.py:88
  442.3 17.5 %collective-permute-start.47 = (bf16[160,2048]{1,0:T(8,128)(2,1)S(1)}, bf16[160,2048]{1,0:T(8,128)(2,1)S(1)}, u32[]{:S(2)}, u32[]{:S(2)}) collective-permute-start(bf16[160,2048]{1,0:T(8,128)(2,1)S(1)} %get-tuple-element.496), channel_id=1, source_target_pairs={{0,1},{2,0},{4,2},{6,4},{7,6},{5,7},{3,5},{1,3},{8,9},{10,8},{12,1... | collective-permute-start | bytes 1966088 | tf_op jit(solution)/shard_map/ppermute | solution.py:88
  459.9 22.7 %collective-permute-start.48 = (bf16[160,2048]{1,0:T(8,128)(2,1)S(1)}, bf16[160,2048]{1,0:T(8,128)(2,1)}, u32[]{:S(2)}, u32[]{:S(2)}) collective-permute-start(bf16[160,2048]{1,0:T(8,128)(2,1)S(1)} %get-tuple-element.336.refs_0_), channel_id=1, source_target_pairs={{0,2},{2,4},{4,6},{6,7},{7,5},{5,3},{3,1},{1,0},{8,10},{10,12},{12... | collective-permute-start | bytes 1966088 | tf_op jit(solution)/shard_map/ppermute | solution.py:88
  461.2 21.4 %collective-permute-start.49 = (bf16[160,2048]{1,0:T(8,128)(2,1)S(1)}, bf16[160,2048]{1,0:T(8,128)(2,1)}, u32[]{:S(2)}, u32[]{:S(2)}) collective-permute-start(bf16[160,2048]{1,0:T(8,128)(2,1)S(1)} %get-tuple-element.336.refs_0_), channel_id=1, source_target_pairs={{0,1},{2,0},{4,2},{6,4},{7,6},{5,7},{3,5},{1,3},{8,9},{10,8},{12,1... | collective-permute-start | bytes 1966088 | tf_op jit(solution)/shard_map/ppermute | solution.py:88
  461.9 26.0 %all-to-all-start.4 = ((bf16[8,160,256]{2,1,0:T(8,128)(2,1)}), bf16[8,160,256]{2,1,0:T(8,128)(2,1)S(1)}, u32[]{:S(2)}, u32[]{:S(2)}) async-start(bf16[8,160,256]{2,1,0:T(8,128)(2,1)} %bitcast.193), calls=%async_computation.4 | async-start | bytes 1310720 | tf_op jit(solution)/shard_map/all_to_all | solution.py:250
  465.7 173.1 %reduce-scatter.8.cloned.1.call-start = ((), (), s32[]{:S(2)}) async-start(), calls=%async_computation.13 | async-start | bytes 10485760 | tf_op jit(solution)/shard_map/reduce_scatter | solution.py:881
  488.7 19.0 %collective-permute-start.50 = (bf16[160,2048]{1,0:T(8,128)(2,1)}, bf16[160,2048]{1,0:T(8,128)(2,1)S(1)}, u32[]{:S(2)}, u32[]{:S(2)}) collective-permute-start(bf16[160,2048]{1,0:T(8,128)(2,1)} %collective-permute-done.48.refs_2_), channel_id=1, source_target_pairs={{0,2},{2,4},{4,6},{6,7},{7,5},{5,3},{3,1},{1,0},{8,10},{10,12},{12... | collective-permute-start | bytes 1966088 | tf_op jit(solution)/shard_map/ppermute | solution.py:88
  488.7 19.0 %collective-permute-start.51 = (bf16[160,2048]{1,0:T(8,128)(2,1)}, bf16[160,2048]{1,0:T(8,128)(2,1)S(1)}, u32[]{:S(2)}, u32[]{:S(2)}) collective-permute-start(bf16[160,2048]{1,0:T(8,128)(2,1)} %collective-permute-done.49.refs_1_), channel_id=1, source_target_pairs={{0,1},{2,0},{4,2},{6,4},{7,6},{5,7},{3,5},{1,3},{8,9},{10,8},{12,1... | collective-permute-start | bytes 1966088 | tf_op jit(solution)/shard_map/ppermute | solution.py:88
  508.8 16.5 %collective-permute-start.52 = (bf16[160,2048]{1,0:T(8,128)(2,1)}, bf16[160,2048]{1,0:T(8,128)(2,1)S(1)}, u32[]{:S(2)}, u32[]{:S(2)}) collective-permute-start(bf16[160,2048]{1,0:T(8,128)(2,1)} %copy-done.56), channel_id=1, source_target_pairs={{0,2},{2,4},{4,6},{6,7},{7,5},{5,3},{3,1},{1,0},{8,10},{10,12},{12... | collective-permute-start | bytes 1966088 | tf_op jit(solution)/shard_map/ppermute | solution.py:88
  508.8 16.5 %collective-permute-start.53 = (bf16[160,2048]{1,0:T(8,128)(2,1)}, bf16[160,2048]{1,0:T(8,128)(2,1)S(1)}, u32[]{:S(2)}, u32[]{:S(2)}) collective-permute-start(bf16[160,2048]{1,0:T(8,128)(2,1)} %copy-done.57), channel_id=1, source_target_pairs={{0,1},{2,0},{4,2},{6,4},{7,6},{5,7},{3,5},{1,3},{8,9},{10,8},{12,1... | collective-permute-start | bytes 1966088 | tf_op jit(solution)/shard_map/ppermute | solution.py:88
  554.5 27.0 %collective-permute-start.61 = (bf16[8,1,64,768]{3,2,1,0:T(8,128)(2,1)}, bf16[8,1,64,768]{3,2,1,0:T(8,128)(2,1)}, u32[]{:S(2)}, u32[]{:S(2)}) collective-permute-start(bf16[8,1,64,768]{3,2,1,0:T(8,128)(2,1)} %constant_dynamic-slice_fusion.1), channel_id=1, source_target_pairs={{0,16},{8,24},{16,0},{24,8},{1,17},{9,25},{17,1},{25,9},{2,18},{10... | collective-permute-start | bytes 2359304 | tf_op jit(solution)/shard_map/ppermute | solution.py:204
  567.3 16.7 %collective-permute-start.62 = (bf16[2,64,2048]{2,1,0:T(8,128)(2,1)}, bf16[2,64,2048]{2,1,0:T(8,128)(2,1)}, u32[]{:S(2)}, u32[]{:S(2)}) collective-permute-start(bf16[2,64,2048]{2,1,0:T(8,128)(2,1)} %dynamic-slice_bitcast_fusion.1), channel_id=1, source_target_pairs={{0,8},{8,0},{16,24},{24,16},{1,9},{9,1},{17,25},{25,17},{2,10},{10... | collective-permute-start | bytes 1572872 | tf_op jit(solution)/shard_map/ppermute | solution.py:204
  573.1 19.0 %collective-permute-start.59 = (bf16[160,2048]{1,0:T(8,128)(2,1)S(1)}, bf16[160,2048]{1,0:T(8,128)(2,1)}, u32[]{:S(2)}, u32[]{:S(2)}) collective-permute-start(bf16[160,2048]{1,0:T(8,128)(2,1)S(1)} %copy-done.53), channel_id=1, source_target_pairs={{0,2},{2,4},{4,6},{6,7},{7,5},{5,3},{3,1},{1,0},{8,10},{10,12},{12... | collective-permute-start | bytes 1966088 | tf_op jit(solution)/shard_map/ppermute | solution.py:88
  575.0 18.6 %collective-permute-start.60 = (bf16[160,2048]{1,0:T(8,128)(2,1)}, bf16[160,2048]{1,0:T(8,128)(2,1)}, u32[]{:S(2)}, u32[]{:S(2)}) collective-permute-start(bf16[160,2048]{1,0:T(8,128)(2,1)} %pad_maximum_fusion.12), channel_id=1, source_target_pairs={{0,1},{2,0},{4,2},{6,4},{7,6},{5,7},{3,5},{1,3},{8,9},{10,8},{12,1... | collective-permute-start | bytes 1966088 | tf_op jit(solution)/shard_map/ppermute | solution.py:88
  597.0 24.1 %collective-permute-start.63 = (bf16[160,2048]{1,0:T(8,128)(2,1)}, bf16[160,2048]{1,0:T(8,128)(2,1)}, u32[]{:S(2)}, u32[]{:S(2)}) collective-permute-start(bf16[160,2048]{1,0:T(8,128)(2,1)} %get-tuple-element.489), channel_id=1, source_target_pairs={{0,2},{2,4},{4,6},{6,7},{7,5},{5,3},{3,1},{1,0},{8,10},{10,12},{12... | collective-permute-start | bytes 1966088 | tf_op jit(solution)/shard_map/ppermute | solution.py:88
  598.5 22.6 %collective-permute-start.64 = (bf16[160,2048]{1,0:T(8,128)(2,1)}, bf16[160,2048]{1,0:T(8,128)(2,1)}, u32[]{:S(2)}, u32[]{:S(2)}) collective-permute-start(bf16[160,2048]{1,0:T(8,128)(2,1)} %get-tuple-element.488), channel_id=1, source_target_pairs={{0,1},{2,0},{4,2},{6,4},{7,6},{5,7},{3,5},{1,3},{8,9},{10,8},{12,1... | collective-permute-start | bytes 1966088 | tf_op jit(solution)/shard_map/ppermute | solution.py:88
  599.0 32.8 %all-to-all-start.6 = ((bf16[8,64,768]{2,1,0:T(8,128)(2,1)}), bf16[8,64,768]{2,1,0:T(8,128)(2,1)S(1)}, u32[]{:S(2)}, u32[]{:S(2)}) async-start(bf16[8,64,768]{2,1,0:T(8,128)(2,1)} %bitcast.63), calls=%async_computation.7 | async-start | bytes 1572864 | tf_op jit(solution)/shard_map/all_to_all | solution.py:250
  603.8 16.2 %collective-permute-start.65 = (bf16[1,64,2048]{2,1,0:T(8,128)(2,1)S(1)}, bf16[1,64,2048]{2,1,0:T(8,128)(2,1)}, u32[]{:S(2)}, u32[]{:S(2)}) collective-permute-start(bf16[1,64,2048]{2,1,0:T(8,128)(2,1)S(1)} %constant_dynamic-slice_fusion), channel_id=1, source_target_pairs={{0,16},{8,24},{16,0},{24,8},{1,17},{9,25},{17,1},{25,9},{2,18},{10... | collective-permute-start | bytes 786440 | tf_op jit(solution)/shard_map/ppermute | solution.py:204
  633.4 24.6 %collective-permute-start.70 = (bf16[1,3,64,2048]{3,2,1,0:T(8,128)(2,1)S(1)}, bf16[1,3,64,2048]{3,2,1,0:T(8,128)(2,1)}, u32[]{:S(2)}, u32[]{:S(2)}) collective-permute-start(bf16[1,3,64,2048]{3,2,1,0:T(8,128)(2,1)S(1)} %stack.161), channel_id=1, source_target_pairs={{0,16},{8,24},{16,0},{24,8},{1,17},{9,25},{17,1},{25,9},{2,18},{10... | collective-permute-start | bytes 2359304 | tf_op jit(solution)/shard_map/ppermute | solution.py:204
  637.7 19.2 %collective-permute-start.71 = (bf16[1,64,2048]{2,1,0:T(8,128)(2,1)S(1)}, bf16[1,64,2048]{2,1,0:T(8,128)(2,1)}, u32[]{:S(2)}, u32[]{:S(2)}) collective-permute-start(bf16[1,64,2048]{2,1,0:T(8,128)(2,1)S(1)} %add_convert_fusion.19), channel_id=1, source_target_pairs={{0,16},{8,24},{16,0},{24,8},{1,17},{9,25},{17,1},{25,9},{2,18},{10... | collective-permute-start | bytes 786440 | tf_op jit(solution)/shard_map/ppermute | solution.py:204
  640.5 19.3 %collective-permute-start.68 = (bf16[160,2048]{1,0:T(8,128)(2,1)}, bf16[160,2048]{1,0:T(8,128)(2,1)S(1)}, u32[]{:S(2)}, u32[]{:S(2)}) collective-permute-start(bf16[160,2048]{1,0:T(8,128)(2,1)} %get-tuple-element.487), channel_id=1, source_target_pairs={{0,2},{2,4},{4,6},{6,7},{7,5},{5,3},{3,1},{1,0},{8,10},{10,12},{12... | collective-permute-start | bytes 1966088 | tf_op jit(solution)/shard_map/ppermute | solution.py:88
  640.6 19.2 %collective-permute-start.69 = (bf16[160,2048]{1,0:T(8,128)(2,1)}, bf16[160,2048]{1,0:T(8,128)(2,1)S(1)}, u32[]{:S(2)}, u32[]{:S(2)}) collective-permute-start(bf16[160,2048]{1,0:T(8,128)(2,1)} %get-tuple-element.486), channel_id=1, source_target_pairs={{0,1},{2,0},{4,2},{6,4},{7,6},{5,7},{3,5},{1,3},{8,9},{10,8},{12,1... | collective-permute-start | bytes 1966088 | tf_op jit(solution)/shard_map/ppermute | solution.py:88
  (157 other events, 2297.5 us)
Sparse Core Ops, SparseCore 0:
  40.7 62.9 all-gather.1
  408.5 71.8 reduce-scatter.3
  483.2 71.7 reduce-scatter.5
  557.4 77.7 reduce-scatter.7

commit v16 on v14

--- a/solution.py
+++ b/solution.py
@@ -443,6 +443,41 @@
             transcendentals=rows * rows,
         ),
     )(order, *operands, *earlier)
+
+
+def first_product_kernel(sent_ref, weight_ref, token_ref, inverse_ref, out_ref, part_ref):
+    first = mm(sent_ref[...], weight_ref[...], 1, 1)
+    out_ref[...] = first.astype(low_type)
+    scaled = token_ref[...].astype(wide_type) * inverse_ref[...]
+    part_ref[...] = jnp.sum(first * scaled, axis=0, keepdims=True)
+
+
+def first_product(sent, weight, tokens, inverse):
+    rows, depth = tokens.shape
+    width = 256
+    tile = pl.BlockSpec((rows, width), lambda j: (0, j))
+    first, part = pl.pallas_call(
+        first_product_kernel,
+        grid=(depth // width,),
+        in_specs=[
+            pl.BlockSpec(sent.shape, lambda j: (0, 0)),
+            pl.BlockSpec((width, weight.shape[1]), lambda j: (j, 0)),
+            tile,
+            pl.BlockSpec((rows, 1), lambda j: (0, 0)),
+        ],
+        out_specs=[tile, pl.BlockSpec((1, width), lambda j: (0, j))],
+        out_shape=[
+            jax.ShapeDtypeStruct((rows, depth), low_type),
+            jax.ShapeDtypeStruct((1, depth), wide_type),
+        ],
+        compiler_params=pltpu.CompilerParams(vmem_limit_bytes=40 << 20),
+        cost_estimate=pl.CostEstimate(
+            flops=2 * sent.size * depth,
+            bytes_accessed=2 * (sent.size + weight.size) + 4 * rows * depth,
+            transcendentals=0,
+        ),
+    )(sent, weight, tokens, inverse)
+    return first, part[0]
 
 
 def block_product_kernel(left_ref, *refs):
@@ -548,8 +583,8 @@
         .transpose(1, 0, 2, 3)
         .reshape(model_width, 3 * width_here)
     )
-    output_late = after(output_weight, swapped)
-    token_ring = RingGather(tokens)
+    tokens_late, output_late, _ = tie(tokens, output_weight, swapped)
+    token_ring = RingGather(tokens_late)
     token_ring.start()
     small_flat = after(small_sent.reshape(-1, head_dim), token_ring.received)
     small_all = swap_all(
@@ -831,10 +866,10 @@
     sent, down_sum = tie(sent, down_sum)
 
     def first_work(sent, head):
-        first_part = mm(sent, head_weight, 1, 1)
-        token_wide = token_all.astype(wide_type)
-        prenorm_part = jnp.sum(first_part * token_wide * inverse_all, axis=0)
-        return first_part.astype(low_type), prenorm_part, rep_scatter(head, 1, scatter_order[:1])
+        return (
+            *first_product(sent, head_weight, token_all, inverse_all),
+            rep_scatter(head, 1, scatter_order[:1]),
+        )
 
     head_part = window([attention_gather], grad_of, first_all, sent)
     while attention_gather.step < group_count // 2:

time: 710 us -> 695 us (0.979)
  other arithmetic: 110 us -> 94.9 us
  matrix products: 127 us -> 119 us
  Pallas kernels: 108 us -> 116 us
  waiting for transfers between devices: 129 us -> 137 us
    ppermute x56, waiting for transfers between devices: 63.5 us -> 78.2 us  [ring_shift(): return lax.ppermute(values, 'ep', pairs)]
    reduce_sum x1 -> x0, other arithmetic: 13.5 us -> none  [first_work(): prenorm_part = jnp.sum(first_part * token_wide * inverse_all, axis=0)]
    pallas_call x0 -> x1, Pallas kernels: none -> 8.7 us  [first_product(): pl.pallas_call(first_product_kernel, grid=(depth // width,), in_specs=[pl...]
    all_to_all x7, starting transfers between devices: 42.7 us -> 34.4 us  [swap_all(): return lax.all_to_all(values, 'ep', split_axis=0, concat_axis=0, tiled=True)]
    dot_general x26 -> x25, matrix products: 127 us -> 119 us  [mm(): lax.dot_general(left, right, (((left_dim,), (right_dim,)), ((), ())), pre...]
    unnamed x330 -> x334, local copies, waits for them, and re-layouts: 34.5 us -> 35.5 us
  transfers between devices with their start and end apart: 85 -> 85, of which waited for: 26 -> 29; matrix products, arithmetic and copies ran while one was open for 40% -> 37% of each run, Pallas kernels for 10% -> 12%
where the time goes in v16:
time: 695 us; the launch traced here: 685 us
  waiting for transfers between devices  137 us (20%)
  matrix products  119 us (17%)
  Pallas kernels  116 us (17%)
  starting transfers between devices  115 us (17%)
  other arithmetic  94.9 us (14%)
  local copies, waits for them, and re-layouts  86 us (12%)
  between operations  17.3 us (2%)
    dot_general x25, matrix products, mm(): lax.dot_general(left, right, (((left_dim,), (right_dim,)), ((), ())), pre...  119 us
    ppermute x56, waiting for transfers between devices, ring_shift(): return lax.ppermute(values, 'ep', pairs)  78.2 us
    ppermute x56, starting transfers between devices, ring_shift(): return lax.ppermute(values, 'ep', pairs)  66.5 us
    pallas_call x2, Pallas kernels, expert_pass(): pl.pallas_call(expert_kernel, grid=(experts, steps), in_specs=[pl.BlockSp...  39 us
    all_to_all x7, waiting for transfers between devices, swap_all(): return lax.all_to_all(values, 'ep', split_axis=0, concat_axis=0, tiled=True)  36.8 us
    unnamed x334, local copies, waits for them, and re-layouts  35.5 us
    all_to_all x7, starting transfers between devices, swap_all(): return lax.all_to_all(values, 'ep', split_axis=0, concat_axis=0, tiled=True)  34.4 us
    pallas_call x2, Pallas kernels, expert_back(): pl.pallas_call(expert_back_kernel, grid=(depth // width,), in_specs=[whol...  33.6 us
  transfers between devices with their start and end apart: 85, of which 29 were waited for; matrix products, arithmetic and copies ran while one was open for 37% of the time, Pallas kernels for 12%

profile of v16, /device:TPU:0, one launch (start us, length us, event | category | flops | bytes accessed | tf_op | source)
XLA Modules:
  0.0 684.7 jit_solution(16195883606952573322)
XLA Ops:
  11.5 7.3 %all-to-all-start = ((bf16[8,64,768]{2,1,0:T(8,128)(2,1)}), bf16[8,64,768]{2,1,0:T(8,128)(2,1)S(1)}, u32[]{:S(2)}, u32[]{:S(2)}) async-start(bf16[8,64,768]{2,1,0:T(8,128)(2,1)} %copy.143), calls=%async_computation | async-start | bytes 1572864 | tf_op jit(solution)/shard_map/all_to_all | solution.py:250
  19.9 19.0 %all-to-all-done = bf16[8,64,768]{2,1,0:T(8,128)(2,1)S(1)} async-done(((bf16[8,64,768]{2,1,0:T(8,128)(2,1)}), bf16[8,64,768]{2,1,0:T(8,128)(2,1)S(1)}, u32[]{:S(2)}, u32[]{:S(2)}) %all-to-all-start) | async-done | bytes 786464 | tf_op jit(solution)/shard_map/all_to_all | solution.py:250
  47.2 9.8 %collective-permute-done.4 = bf16[160,2048]{1,0:T(8,128)(2,1)} collective-permute-done((bf16[160,2048]{1,0:T(8,128)(2,1)S(1)}, bf16[160,2048]{1,0:T(8,128)(2,1)}, u32[]{:S(2)}, u32[]{:S(2)}) %collective-permute-start.4) | collective-permute-done | bytes 655392 | tf_op jit(solution)/shard_map/ppermute | solution.py:88
  59.9 4.1 all-to-all-start.2
  66.0 3.7 multiply_cosine_fusion
  79.3 10.4 %collective-permute-done.1 = bf16[160,2048]{1,0:T(8,128)(2,1)} collective-permute-done((bf16[160,2048]{1,0:T(8,128)(2,1)}, bf16[160,2048]{1,0:T(8,128)(2,1)}, u32[]{:S(2)}, u32[]{:S(2)}) %collective-permute-start.1) | collective-permute-done | bytes 655392 | tf_op jit(solution)/shard_map/ppermute | solution.py:88
  89.7 8.3 %collective-permute-start.2 = (bf16[160,2048]{1,0:T(8,128)(2,1)}, bf16[160,2048]{1,0:T(8,128)(2,1)S(1)}, u32[]{:S(2)}, u32[]{:S(2)}) collective-permute-start(bf16[160,2048]{1,0:T(8,128)(2,1)} %collective-permute-done.1), channel_id=1, source_target_pairs={{0,2},{2,4},{4,6},{6,7},{7,5},{5,3},{3,1},{1,0},{8,10},{10,12},{12... | collective-permute-start | bytes 1966088 | tf_op jit(solution)/shard_map/ppermute | solution.py:88
  98.0 2.5 collective-permute-done.5
  102.8 10.9 %collective-permute-done.6 = bf16[160,2048]{1,0:T(8,128)(2,1)S(1)} collective-permute-done((bf16[160,2048]{1,0:T(8,128)(2,1)}, bf16[160,2048]{1,0:T(8,128)(2,1)S(1)}, u32[]{:S(2)}, u32[]{:S(2)}) %collective-permute-start.6) | collective-permute-done | bytes 655392 | tf_op jit(solution)/shard_map/ppermute | solution.py:88
  116.8 2.3 maximum_select_fusion
  137.0 4.3 fusion.72.query_raw_ref.key_raw_ref
  169.3 4.0 collective-permute-done.16
  177.6 5.9 collective-permute-done.19
  184.9 4.4 all-to-all-start.1
  191.2 2.3 constant_dynamic-update-slice_fusion.44
  193.5 2.3 constant_dynamic-update-slice_fusion.43
  198.9 6.3 all-to-all-done.1
  209.2 2.2 convolution_dynamic-update-slice_fusion.1
  217.4 7.4 %fusion.73.stream_ref = f32[640,2048]{1,0:T(8,128)} fusion(bf16[640,2048]{1,0:T(8,128)(2,1)S(1)} %copy-done.34, bf16[2048,2048]{1,0:T(8,128)(2,1)S(1)} %bitcast.275), kind=kOutput, calls=%fused_computation.326 | convolution fusion | flops 5368709120 | bytes 16252928 | tf_op jit(solution)/shard_map/dot_general | solution.py:60
  225.9 4.2 collective-permute-done.24
  232.1 8.9 %fusion.74.stream_ref = f32[640,2048]{1,0:T(8,128)} fusion(bf16[640,2048]{1,0:T(8,128)(2,1)} %get-tuple-element.244, bf16[2048,2048]{1,0:T(8,128)(2,1)S(1)} %bitcast.276), kind=kOutput, calls=%fused_computation.327 | convolution fusion | flops 5368709120 | bytes 16252928 | tf_op jit(solution)/shard_map/dot_general | solution.py:60
  241.1 2.6 collective-permute-done.26
  251.6 19.4 %shard_map.281 = (bf16[1280,2048]{1,0:T(8,128)(2,1)}, bf16[1280,2048]{1,0:T(8,128)(2,1)}, bf16[1280,2048]{1,0:T(8,128)(2,1)}, f32[2,640,128]{2,1,0:T(8,128)}) custom-call(bf16[640,2048]{1,0:T(8,128)(2,1)} %copy-done.35, bf16[2,2048,1024]{2,1,0:T(8,128)(2,1)} %gate_ref.7, bf16[2,2048,1024]{2,1,0:T(8,128)(2,1)} %up_ref.7, f32[640,2048]{1,0:T(8,128)} %fusion.73.stream_ref, ...), custom_call_target="tpu_custom_call" | custom-call | flops 10737418240 | bytes 42991616 | tf_op jit(solution)/shard_map/pallas_call | solution.py:294
  275.5 2.7 collective-permute-done.30
  278.2 2.3 collective-permute-done.31
  285.0 19.5 %shard_map.282 = (bf16[1280,2048]{1,0:T(8,128)(2,1)}, bf16[1280,2048]{1,0:T(8,128)(2,1)}, bf16[1280,2048]{1,0:T(8,128)(2,1)}, f32[2,640,128]{2,1,0:T(8,128)}) custom-call(bf16[640,2048]{1,0:T(8,128)(2,1)} %copy-done.29, bf16[2,2048,1024]{2,1,0:T(8,128)(2,1)} %gate_ref.7, ...), custom_call_target="tpu_custom_call", output_to_operand_aliasing={{0}: (5, {}), {1}: (6, {}), {2}: (7, {})} | custom-call | flops 10737418240 | bytes 42991616 | tf_op jit(solution)/shard_map/pallas_call | solution.py:294
  306.6 16.8 %shard_map.283 = bf16[640,2048]{1,0:T(8,128)(2,1)} custom-call(bf16[1280,2048]{1,0:T(8,128)(2,1)} %get-tuple-element.287.gback_ref, bf16[1280,2048]{1,0:T(8,128)(2,1)} %get-tuple-element.296.uback_ref, bf16[2,2048,1024]{2,1,0:T(8,128)(2,1)} %gate_ref.7, bf16[2,2048,1024]{2,1,0:T(8,128)(2,1)} %up_ref.7), custom_call_target="tpu_custom_call" | custom-call | flops 10737418240 | bytes 24641536 | tf_op jit(solution)/shard_map/pallas_call | solution.py:334
  327.9 3.3 all-to-all-start.3
  331.3 16.5 %convolution_convert_fusion.3 = bf16[1280,2048]{1,0:T(8,128)(2,1)} fusion(bf16[1280,2048]{1,0:T(8,128)(2,1)} %get-tuple-element.280, bf16[2048,2048]{1,0:T(8,128)(2,1)} %bitcast.272), kind=kOutput, calls=%fused_computation.12 | convolution fusion | flops 10740039680 | bytes 18874368 | tf_op jit(solution)/shard_map/dot_general | solution.py:60
  347.8 2.3 fusion.55
  356.9 16.8 %shard_map.284 = bf16[640,2048]{1,0:T(8,128)(2,1)} custom-call(bf16[1280,2048]{1,0:T(8,128)(2,1)} %get-tuple-element.287.gback_ref, bf16[1280,2048]{1,0:T(8,128)(2,1)} %get-tuple-element.296.uback_ref, bf16[2,2048,1024]{2,1,0:T(8,128)(2,1)} %gate_ref.7, bf16[2,2048,1024]{2,1,0:T(8,128)(2,1)} %up_ref.7), custom_call_target="tpu_custom_call" | custom-call | flops 10737418240 | bytes 24641536 | tf_op jit(solution)/shard_map/pallas_call | solution.py:334
  373.8 2.4 add_convert_fusion.11
  376.2 2.3 add_convert_fusion.12
  385.2 15.7 %convolution_convert_fusion.2 = bf16[2048,2048]{1,0:T(8,128)(2,1)} fusion(bf16[1280,2048]{1,0:T(8,128)(2,1)S(1)} %bitcast.173, bf16[1280,2048]{1,0:T(8,128)(2,1)} %get-tuple-element.565), kind=kOutput, calls=%fused_computation.11 | convolution fusion | flops 10741612544 | bytes 18874368 | tf_op jit(solution)/shard_map/dot_general | solution.py:60
  403.7 4.6 collective-permute-done.38
  408.4 3.4 add_convert_fusion.7
  413.9 3.1 add_convert_fusion.9
  419.1 18.5 %convolution_convert_fusion.1 = bf16[2048,2048]{1,0:T(8,128)(2,1)} fusion(bf16[1280,2048]{1,0:T(8,128)(2,1)} %get-tuple-element.561, bf16[1280,2048]{1,0:T(8,128)(2,1)} %get-tuple-element.287.gback_ref), kind=kOutput, calls=%fused_computation.10 | convolution fusion | flops 10741612544 | bytes 18874368 | tf_op jit(solution)/shard_map/dot_general | solution.py:60
  447.3 2.6 convolution_add_fusion.1
  449.9 2.4 fusion.28
  452.3 2.6 fusion.11
  460.5 5.0 all-to-all-start.4
  465.8 16.7 %convolution_convert_fusion = bf16[2048,2048]{1,0:T(8,128)(2,1)} fusion(bf16[1280,2048]{1,0:T(8,128)(2,1)} %get-tuple-element.561, bf16[1280,2048]{1,0:T(8,128)(2,1)} %get-tuple-element.296.uback_ref), kind=kOutput, calls=%fused_computation.9 | convolution fusion | flops 10741612544 | bytes 18874368 | tf_op jit(solution)/shard_map/dot_general | solution.py:60
  482.5 2.7 all-to-all-done.4.swapped_ref
  490.3 14.8 %shard_map.285 = (bf16[1280,768]{1,0:T(8,128)(2,1)}, f32[2,128]{1,0:T(2,128)}) custom-call(s32[8]{0:T(128)} %stack.156.order_ref, bf16[1280,128]{1,0:T(8,128)(2,1)} %copy-done.51, bf16[1280,128]{1,0:T(8,128)(2,1)} %copy-done.50, bf16[1280,128]{1,0:T(8,128)(2,1)} %slice.504.value_ref, bf16[8,160,256]{2,1,0:T(8,128)(2,1)} %copy-done.16, ...), custom_call_target="tpu_custom_call" | custom-call | flops 2097152000 | bytes 4915200 | tf_op jit(solution)/shard_map/pallas_call | solution.py:421
  509.3 13.3 %shard_map.286 = (bf16[1280,768]{1,0:T(8,128)(2,1)}, f32[2,128]{1,0:T(2,128)}) custom-call(s32[8]{0:T(128)} %stack.156.order_ref, bf16[1280,128]{1,0:T(8,128)(2,1)} %copy-done.49, bf16[1280,128]{1,0:T(8,128)(2,1)} %copy-done.48, bf16[1280,128]{1,0:T(8,128)(2,1)} %slice.503.value_ref, ...), custom_call_target="tpu_custom_call", output_to_operand_aliasing={{0}: (13, {})} | custom-call | flops 2097152000 | bytes 4915200 | tf_op jit(solution)/shard_map/pallas_call | solution.py:421
  524.3 2.4 collective-permute-start.55
  526.7 7.7 %convolution_convert_fusion.4 = bf16[2048,768]{1,0:T(8,128)(2,1)S(1)} fusion(bf16[1280,2048]{1,0:T(8,128)(2,1)} %copy-done.24, bf16[1280,768]{1,0:T(8,128)(2,1)} %get-tuple-element.331.sent_ref), kind=kOutput, calls=%fused_computation.17 | convolution fusion | flops 4028104704 | bytes 10354688 | tf_op jit(solution)/shard_map/dot_general | solution.py:60
  539.7 8.7 %shard_map.287 = (bf16[1280,2048]{1,0:T(8,128)(2,1)S(1)}, f32[1,2048]{1,0:T(1,128)S(1)}) custom-call(bf16[1280,768]{1,0:T(8,128)(2,1)S(1)} %copy-done.5, bf16[2048,768]{1,0:T(8,128)(2,1)S(1)} %bitcast.159, bf16[1280,2048]{1,0:T(8,128)(2,1)} %copy-done.10, f32[1280,1]{1,0:T(8,128)S(1)} %copy.183.inverse_ref), custom_call_target="tpu_custom_call" | custom-call | flops 4026531840 | bytes 15597568 | tf_op jit(solution)/shard_map/pallas_call | solution.py:459
  548.4 3.1 fusion.9
  558.2 6.4 shard_map.288
  573.3 5.8 all-to-all-start.5
  581.1 4.6 convert_element_type.468
  592.3 6.3 collective-permute-done.60
  598.7 3.4 add_convert_fusion.3
  604.3 4.5 all-to-all-start.6
  608.9 2.7 multiply_convert_fusion
  615.7 2.3 maximum_convert_fusion
  618.0 11.1 %collective-permute-done.67 = f32[4640]{0:T(1024)S(1)} collective-permute-done((f32[4640]{0:T(1024)S(1)}, f32[4640]{0:T(1024)S(1)}, u32[]{:S(2)}, u32[]{:S(2)}) %collective-permute-start.67) | collective-permute-done | bytes 18592 | tf_op jit(solution)/shard_map/ppermute | solution.py:204
  630.4 6.9 %all-to-all-done.6 = bf16[8,64,768]{2,1,0:T(8,128)(2,1)S(1)} async-done(((bf16[8,64,768]{2,1,0:T(8,128)(2,1)}), bf16[8,64,768]{2,1,0:T(8,128)(2,1)S(1)}, u32[]{:S(2)}, u32[]{:S(2)}) %all-to-all-start.6) | async-done | bytes 786464 | tf_op jit(solution)/shard_map/all_to_all | solution.py:250
  639.6 3.3 add_convert_fusion.1
  648.1 2.3 maximum_convert_fusion.1
  651.2 11.0 %collective-permute-done.71 = bf16[1,64,2048]{2,1,0:T(8,128)(2,1)} collective-permute-done((bf16[1,64,2048]{2,1,0:T(8,128)(2,1)S(1)}, bf16[1,64,2048]{2,1,0:T(8,128)(2,1)}, u32[]{:S(2)}, u32[]{:S(2)}) %collective-permute-start.71) | collective-permute-done | bytes 262176 | tf_op jit(solution)/shard_map/ppermute | solution.py:204
  667.3 2.7 fusion.17
  (680 shorter events, 229.5 us)
Async XLA Ops:
  11.5 27.4 %all-to-all-start = ((bf16[8,64,768]{2,1,0:T(8,128)(2,1)}), bf16[8,64,768]{2,1,0:T(8,128)(2,1)S(1)}, u32[]{:S(2)}, u32[]{:S(2)}) async-start(bf16[8,64,768]{2,1,0:T(8,128)(2,1)} %copy.143), calls=%async_computation | async-start | bytes 1572864 | tf_op jit(solution)/shard_map/all_to_all | solution.py:250
  18.7 96.6 %all-gather.2.cloned.1.call-start = ((), (), s32[]{:S(2)}) async-start(), calls=%async_computation.10 | async-start | bytes 2359296 | tf_op jit(solution)/shard_map/all_gather | solution.py:69
  38.9 18.2 %collective-permute-start.4 = (bf16[160,2048]{1,0:T(8,128)(2,1)S(1)}, bf16[160,2048]{1,0:T(8,128)(2,1)}, u32[]{:S(2)}, u32[]{:S(2)}) collective-permute-start(bf16[160,2048]{1,0:T(8,128)(2,1)S(1)} %copy-done.13), channel_id=1, source_target_pairs={{0,1},{2,0},{4,2},{6,4},{7,6},{5,7},{3,5},{1,3},{8,9},{10,8},{12,1... | collective-permute-start | bytes 1966088 | tf_op jit(solution)/shard_map/ppermute | solution.py:88
  40.3 18.9 %collective-permute-start = (bf16[160,2048]{1,0:T(8,128)(2,1)S(1)}, bf16[160,2048]{1,0:T(8,128)(2,1)}, u32[]{:S(2)}, u32[]{:S(2)}) collective-permute-start(bf16[160,2048]{1,0:T(8,128)(2,1)S(1)} %copy-done.13), channel_id=1, source_target_pairs={{0,2},{2,4},{4,6},{6,7},{7,5},{5,3},{3,1},{1,0},{8,10},{10,12},{12... | collective-permute-start | bytes 1966088 | tf_op jit(solution)/shard_map/ppermute | solution.py:88
  45.7 24.0 %collective-permute-start.11 = (bf16[1,8,64,768]{3,2,1,0:T(8,128)(2,1)S(1)}, bf16[1,8,64,768]{3,2,1,0:T(8,128)(2,1)S(1)}, u32[]{:S(2)}, u32[]{:S(2)}) collective-permute-start(bf16[1,8,64,768]{3,2,1,0:T(8,128)(2,1)S(1)} %bitcast.168), channel_id=1, source_target_pairs={{0,16},{8,24},{16,0},{24,8},{1,17},{9,25},{17,1},{25,9},{2,18},{10... | collective-permute-start | bytes 2359304 | tf_op jit(solution)/shard_map/ppermute | solution.py:204
  64.0 25.8 %collective-permute-start.1 = (bf16[160,2048]{1,0:T(8,128)(2,1)}, bf16[160,2048]{1,0:T(8,128)(2,1)}, u32[]{:S(2)}, u32[]{:S(2)}) collective-permute-start(bf16[160,2048]{1,0:T(8,128)(2,1)} %collective-permute-done), channel_id=1, source_target_pairs={{0,2},{2,4},{4,6},{6,7},{7,5},{5,3},{3,1},{1,0},{8,10},{10,12},{12... | collective-permute-start | bytes 1966088 | tf_op jit(solution)/shard_map/ppermute | solution.py:88
  66.0 34.5 %collective-permute-start.5 = (bf16[160,2048]{1,0:T(8,128)(2,1)}, bf16[160,2048]{1,0:T(8,128)(2,1)}, u32[]{:S(2)}, u32[]{:S(2)}) collective-permute-start(bf16[160,2048]{1,0:T(8,128)(2,1)} %collective-permute-done.4), channel_id=1, source_target_pairs={{0,1},{2,0},{4,2},{6,4},{7,6},{5,7},{3,5},{1,3},{8,9},{10,8},{12,1... | collective-permute-start | bytes 1966088 | tf_op jit(solution)/shard_map/ppermute | solution.py:88
  71.1 45.6 %collective-permute-start.12 = (bf16[2,8,64,768]{3,2,1,0:T(8,128)(2,1)}, bf16[2,8,64,768]{3,2,1,0:T(8,128)(2,1)}, u32[]{:S(2)}, u32[]{:S(2)}) collective-permute-start(bf16[2,8,64,768]{3,2,1,0:T(8,128)(2,1)} %maximum_select_fusion.3), channel_id=1, source_target_pairs={{0,8},{8,0},{16,24},{24,16},{1,9},{9,1},{17,25},{25,17},{2,10},{10... | collective-permute-start | bytes 4718600 | tf_op jit(solution)/shard_map/ppermute | solution.py:204
  89.7 25.6 %collective-permute-start.2 = (bf16[160,2048]{1,0:T(8,128)(2,1)}, bf16[160,2048]{1,0:T(8,128)(2,1)S(1)}, u32[]{:S(2)}, u32[]{:S(2)}) collective-permute-start(bf16[160,2048]{1,0:T(8,128)(2,1)} %collective-permute-done.1), channel_id=1, source_target_pairs={{0,2},{2,4},{4,6},{6,7},{7,5},{5,3},{3,1},{1,0},{8,10},{10,12},{12... | collective-permute-start | bytes 1966088 | tf_op jit(solution)/shard_map/ppermute | solution.py:88
  120.8 21.2 %collective-permute-start.10 = (bf16[512,512]{1,0:T(8,128)(2,1)S(1)}, bf16[512,512]{1,0:T(8,128)(2,1)S(1)}, u32[]{:S(2)}, u32[]{:S(2)}) collective-permute-start(bf16[512,512]{1,0:T(8,128)(2,1)S(1)} %get-tuple-element.532), channel_id=1, source_target_pairs={{0,16},{8,24},{16,0},{24,8},{1,17},{9,25},{17,1},{25,9},{2,18},{10... | collective-permute-start | bytes 1572872 | tf_op jit(solution)/shard_map/ppermute | solution.py:204
  122.4 33.4 %collective-permute-start.15 = (bf16[512,512]{1,0:T(8,128)(2,1)S(1)}, bf16[512,512]{1,0:T(8,128)(2,1)S(1)}, u32[]{:S(2)}, u32[]{:S(2)}) collective-permute-start(bf16[512,512]{1,0:T(8,128)(2,1)S(1)} %get-tuple-element.531), channel_id=1, source_target_pairs={{0,16},{8,24},{16,0},{24,8},{1,17},{9,25},{17,1},{25,9},{2,18},{10... | collective-permute-start | bytes 1572872 | tf_op jit(solution)/shard_map/ppermute | solution.py:204
  122.9 46.3 %collective-permute-start.18 = (bf16[512,512]{1,0:T(8,128)(2,1)S(1)}, bf16[512,512]{1,0:T(8,128)(2,1)S(1)}, u32[]{:S(2)}, u32[]{:S(2)}) collective-permute-start(bf16[512,512]{1,0:T(8,128)(2,1)S(1)} %get-tuple-element.530), channel_id=1, source_target_pairs={{0,16},{8,24},{16,0},{24,8},{1,17},{9,25},{17,1},{25,9},{2,18},{10... | collective-permute-start | bytes 1572872 | tf_op jit(solution)/shard_map/ppermute | solution.py:204
  126.0 17.6 %collective-permute-start.8 = (bf16[160,2048]{1,0:T(8,128)(2,1)S(1)}, bf16[160,2048]{1,0:T(8,128)(2,1)S(1)}, u32[]{:S(2)}, u32[]{:S(2)}) collective-permute-start(bf16[160,2048]{1,0:T(8,128)(2,1)S(1)} %copy-done.17), channel_id=1, source_target_pairs={{0,2},{2,4},{4,6},{6,7},{7,5},{5,3},{3,1},{1,0},{8,10},{10,12},{12... | collective-permute-start | bytes 1966088 | tf_op jit(solution)/shard_map/ppermute | solution.py:88
  127.3 16.2 %collective-permute-start.9 = (bf16[160,2048]{1,0:T(8,128)(2,1)S(1)}, bf16[160,2048]{1,0:T(8,128)(2,1)S(1)}, u32[]{:S(2)}, u32[]{:S(2)}) collective-permute-start(bf16[160,2048]{1,0:T(8,128)(2,1)S(1)} %copy-done.17), channel_id=1, source_target_pairs={{0,1},{2,0},{4,2},{6,4},{7,6},{5,7},{3,5},{1,3},{8,9},{10,8},{12,1... | collective-permute-start | bytes 1966088 | tf_op jit(solution)/shard_map/ppermute | solution.py:88
  142.1 35.5 %collective-permute-start.21 = (bf16[512,512]{1,0:T(8,128)(2,1)S(1)}, bf16[512,512]{1,0:T(8,128)(2,1)}, u32[]{:S(2)}, u32[]{:S(2)}) collective-permute-start(bf16[512,512]{1,0:T(8,128)(2,1)S(1)} %get-tuple-element.529), channel_id=1, source_target_pairs={{0,16},{8,24},{16,0},{24,8},{1,17},{9,25},{17,1},{25,9},{2,18},{10... | collective-permute-start | bytes 1572872 | tf_op jit(solution)/shard_map/ppermute | solution.py:204
  155.8 53.5 %collective-permute-start.22 = (bf16[2048,512]{1,0:T(8,128)(2,1)S(1)}, bf16[2048,512]{1,0:T(8,128)(2,1)}, u32[]{:S(2)}, u32[]{:S(2)}) collective-permute-start(bf16[2048,512]{1,0:T(8,128)(2,1)S(1)} %copy-done.11), channel_id=1, source_target_pairs={{0,8},{8,0},{16,24},{24,16},{1,9},{9,1},{17,25},{25,17},{2,10},{10... | collective-permute-start | bytes 6291464 | tf_op jit(solution)/shard_map/ppermute | solution.py:204
  156.7 16.5 %collective-permute-start.16 = (bf16[160,2048]{1,0:T(8,128)(2,1)S(1)}, bf16[160,2048]{1,0:T(8,128)(2,1)S(1)}, u32[]{:S(2)}, u32[]{:S(2)}) collective-permute-start(bf16[160,2048]{1,0:T(8,128)(2,1)S(1)} %collective-permute-done.13), channel_id=1, source_target_pairs={{0,2},{2,4},{4,6},{6,7},{7,5},{5,3},{3,1},{1,0},{8,10},{10,12},{12... | collective-permute-start | bytes 1966088 | tf_op jit(solution)/shard_map/ppermute | solution.py:88
  157.3 17.0 %collective-permute-start.17 = (bf16[160,2048]{1,0:T(8,128)(2,1)S(1)}, bf16[160,2048]{1,0:T(8,128)(2,1)S(1)}, u32[]{:S(2)}, u32[]{:S(2)}) collective-permute-start(bf16[160,2048]{1,0:T(8,128)(2,1)S(1)} %collective-permute-done.14), channel_id=1, source_target_pairs={{0,1},{2,0},{4,2},{6,4},{7,6},{5,7},{3,5},{1,3},{8,9},{10,8},{12,1... | collective-permute-start | bytes 1966088 | tf_op jit(solution)/shard_map/ppermute | solution.py:88
  184.9 20.3 %all-to-all-start.1 = ((bf16[8,160,256]{2,1,0:T(8,128)(2,1)}), bf16[8,160,256]{2,1,0:T(8,128)(2,1)}, u32[]{:S(2)}, u32[]{:S(2)}) async-start(bf16[8,160,256]{2,1,0:T(8,128)(2,1)} %copy-done.54), calls=%async_computation.1 | async-start | bytes 1310720 | tf_op jit(solution)/shard_map/all_to_all | solution.py:250
  191.2 20.3 %collective-permute-start.23 = (bf16[2048,512]{1,0:T(8,128)(2,1)}, bf16[2048,512]{1,0:T(8,128)(2,1)}, u32[]{:S(2)}, u32[]{:S(2)}) collective-permute-start(bf16[2048,512]{1,0:T(8,128)(2,1)} %constant_dynamic-update-slice_fusion.18), channel_id=1, source_target_pairs={{0,8},{8,0},{16,24},{24,16},{1,9},{9,1},{17,25},{25,17},{2,10},{10... | collective-permute-start | bytes 6291464 | tf_op jit(solution)/shard_map/ppermute | solution.py:204
  215.2 14.9 %collective-permute-start.24 = (bf16[160,2048]{1,0:T(8,128)(2,1)S(1)}, bf16[160,2048]{1,0:T(8,128)(2,1)S(1)}, u32[]{:S(2)}, u32[]{:S(2)}) collective-permute-start(bf16[160,2048]{1,0:T(8,128)(2,1)S(1)} %get-tuple-element.483), channel_id=1, source_target_pairs={{0,2},{2,4},{4,6},{6,7},{7,5},{5,3},{3,1},{1,0},{8,10},{10,12},{12... | collective-permute-start | bytes 1966088 | tf_op jit(solution)/shard_map/ppermute | solution.py:88
  230.9 14.6 %collective-permute-start.27 = (bf16[160,2048]{1,0:T(8,128)(2,1)S(1)}, bf16[160,2048]{1,0:T(8,128)(2,1)S(1)}, u32[]{:S(2)}, u32[]{:S(2)}) collective-permute-start(bf16[160,2048]{1,0:T(8,128)(2,1)S(1)} %collective-permute-done.25), channel_id=1, source_target_pairs={{0,1},{2,0},{4,2},{6,4},{7,6},{5,7},{3,5},{1,3},{8,9},{10,8},{12,1... | collective-permute-start | bytes 1966088 | tf_op jit(solution)/shard_map/ppermute | solution.py:88
  245.7 25.3 %collective-permute-start.29 = (bf16[160,2048]{1,0:T(8,128)(2,1)S(1)}, bf16[160,2048]{1,0:T(8,128)(2,1)S(1)}, u32[]{:S(2)}, u32[]{:S(2)}) collective-permute-start(bf16[160,2048]{1,0:T(8,128)(2,1)S(1)} %collective-permute-done.27), channel_id=1, source_target_pairs={{0,1},{2,0},{4,2},{6,4},{7,6},{5,7},{3,5},{1,3},{8,9},{10,8},{12,1... | collective-permute-start | bytes 1966088 | tf_op jit(solution)/shard_map/ppermute | solution.py:88
  246.3 24.8 %collective-permute-start.28 = (bf16[160,2048]{1,0:T(8,128)(2,1)S(1)}, bf16[160,2048]{1,0:T(8,128)(2,1)S(1)}, u32[]{:S(2)}, u32[]{:S(2)}) collective-permute-start(bf16[160,2048]{1,0:T(8,128)(2,1)S(1)} %collective-permute-done.26), channel_id=1, source_target_pairs={{0,2},{2,4},{4,6},{6,7},{7,5},{5,3},{3,1},{1,0},{8,10},{10,12},{12... | collective-permute-start | bytes 1966088 | tf_op jit(solution)/shard_map/ppermute | solution.py:88
  324.8 23.0 %collective-permute-start.32 = (bf16[80,2048]{1,0:T(8,128)(2,1)S(1)}, bf16[80,2048]{1,0:T(8,128)(2,1)S(1)}, u32[]{:S(2)}, u32[]{:S(2)}) collective-permute-start(bf16[80,2048]{1,0:T(8,128)(2,1)S(1)} %get-tuple-element.522), channel_id=1, source_target_pairs={{0,2},{2,4},{4,6},{6,7},{7,5},{5,3},{3,1},{1,0},{8,10},{10,12},{12... | collective-permute-start | bytes 983048 | tf_op jit(solution)/shard_map/ppermute | solution.py:88
  326.6 21.2 %collective-permute-start.33 = (bf16[80,2048]{1,0:T(8,128)(2,1)S(1)}, bf16[80,2048]{1,0:T(8,128)(2,1)}, u32[]{:S(2)}, u32[]{:S(2)}) collective-permute-start(bf16[80,2048]{1,0:T(8,128)(2,1)S(1)} %get-tuple-element.521), channel_id=1, source_target_pairs={{0,1},{2,0},{4,2},{6,4},{7,6},{5,7},{3,5},{1,3},{8,9},{10,8},{12,1... | collective-permute-start | bytes 983048 | tf_op jit(solution)/shard_map/ppermute | solution.py:88
  327.9 19.9 %all-to-all-start.3 = ((f32[8,160,2]{1,2,0:T(2,128)}), f32[8,160,2]{1,2,0:T(2,128)S(1)}, u32[]{:S(2)}, u32[]{:S(2)}) async-start(f32[8,160,2]{1,2,0:T(2,128)} %copy.177), calls=%async_computation.3 | async-start | bytes 32768 | tf_op jit(solution)/shard_map/all_to_all | solution.py:250
  331.2 195.5 %reduce-scatter.4.cloned.1.call-start = ((), (), s32[]{:S(2)}) async-start(), calls=%async_computation.11 | async-start | bytes 10485760 | tf_op jit(solution)/shard_map/reduce_scatter | solution.py:860
  351.5 22.2 %collective-permute-start.35 = (bf16[160,2048]{1,0:T(8,128)(2,1)S(1)}, bf16[160,2048]{1,0:T(8,128)(2,1)}, u32[]{:S(2)}, u32[]{:S(2)}) collective-permute-start(bf16[160,2048]{1,0:T(8,128)(2,1)S(1)} %pad_maximum_fusion.7), channel_id=1, source_target_pairs={{0,1},{2,0},{4,2},{6,4},{7,6},{5,7},{3,5},{1,3},{8,9},{10,8},{12,1... | collective-permute-start | bytes 1966088 | tf_op jit(solution)/shard_map/ppermute | solution.py:88
  354.4 19.4 %collective-permute-start.34 = (bf16[160,2048]{1,0:T(8,128)(2,1)}, bf16[160,2048]{1,0:T(8,128)(2,1)}, u32[]{:S(2)}, u32[]{:S(2)}) collective-permute-start(bf16[160,2048]{1,0:T(8,128)(2,1)} %pad_maximum_fusion.6), channel_id=1, source_target_pairs={{0,2},{2,4},{4,6},{6,7},{7,5},{5,3},{3,1},{1,0},{8,10},{10,12},{12... | collective-permute-start | bytes 1966088 | tf_op jit(solution)/shard_map/ppermute | solution.py:88
  354.5 19.2 %collective-permute-start.36 = (bf16[80,2048]{1,0:T(8,128)(2,1)}, bf16[80,2048]{1,0:T(8,128)(2,1)S(1)}, u32[]{:S(2)}, u32[]{:S(2)}) collective-permute-start(bf16[80,2048]{1,0:T(8,128)(2,1)} %get-tuple-element.507), channel_id=1, source_target_pairs={{0,2},{2,4},{4,6},{6,7},{7,5},{5,3},{3,1},{1,0},{8,10},{10,12},{12... | collective-permute-start | bytes 983048 | tf_op jit(solution)/shard_map/ppermute | solution.py:88
  356.4 17.4 %collective-permute-start.37 = (bf16[80,2048]{1,0:T(8,128)(2,1)}, bf16[80,2048]{1,0:T(8,128)(2,1)}, u32[]{:S(2)}, u32[]{:S(2)}) collective-permute-start(bf16[80,2048]{1,0:T(8,128)(2,1)} %get-tuple-element.506), channel_id=1, source_target_pairs={{0,1},{2,0},{4,2},{6,4},{7,6},{5,7},{3,5},{1,3},{8,9},{10,8},{12,1... | collective-permute-start | bytes 983048 | tf_op jit(solution)/shard_map/ppermute | solution.py:88
  380.1 22.3 %collective-permute-start.41 = (bf16[160,2048]{1,0:T(8,128)(2,1)S(1)}, bf16[160,2048]{1,0:T(8,128)(2,1)}, u32[]{:S(2)}, u32[]{:S(2)}) collective-permute-start(bf16[160,2048]{1,0:T(8,128)(2,1)S(1)} %pad_maximum_fusion.9), channel_id=1, source_target_pairs={{0,1},{2,0},{4,2},{6,4},{7,6},{5,7},{3,5},{1,3},{8,9},{10,8},{12,1... | collective-permute-start | bytes 1966088 | tf_op jit(solution)/shard_map/ppermute | solution.py:88
  382.9 19.5 %collective-permute-start.40 = (bf16[160,2048]{1,0:T(8,128)(2,1)}, bf16[160,2048]{1,0:T(8,128)(2,1)}, u32[]{:S(2)}, u32[]{:S(2)}) collective-permute-start(bf16[160,2048]{1,0:T(8,128)(2,1)} %pad_maximum_fusion.8), channel_id=1, source_target_pairs={{0,2},{2,4},{4,6},{6,7},{7,5},{5,3},{3,1},{1,0},{8,10},{10,12},{12... | collective-permute-start | bytes 1966088 | tf_op jit(solution)/shard_map/ppermute | solution.py:88
  383.0 20.7 %collective-permute-start.39 = (bf16[160,2048]{1,0:T(8,128)(2,1)}, bf16[160,2048]{1,0:T(8,128)(2,1)}, u32[]{:S(2)}, u32[]{:S(2)}) collective-permute-start(bf16[160,2048]{1,0:T(8,128)(2,1)} %add_convert_fusion.11), channel_id=1, source_target_pairs={{0,1},{2,0},{4,2},{6,4},{7,6},{5,7},{3,5},{1,3},{8,9},{10,8},{12,1... | collective-permute-start | bytes 1966088 | tf_op jit(solution)/shard_map/ppermute | solution.py:88
  384.9 23.4 %collective-permute-start.38 = (bf16[160,2048]{1,0:T(8,128)(2,1)}, bf16[160,2048]{1,0:T(8,128)(2,1)}, u32[]{:S(2)}, u32[]{:S(2)}) collective-permute-start(bf16[160,2048]{1,0:T(8,128)(2,1)} %add_convert_fusion.12), channel_id=1, source_target_pairs={{0,2},{2,4},{4,6},{6,7},{7,5},{5,3},{3,1},{1,0},{8,10},{10,12},{12... | collective-permute-start | bytes 1966088 | tf_op jit(solution)/shard_map/ppermute | solution.py:88
  408.3 196.0 %reduce-scatter.6.cloned.1.call-start = ((), (), s32[]{:S(2)}) async-start(), calls=%async_computation.12 | async-start | bytes 10485760 | tf_op jit(solution)/shard_map/reduce_scatter | solution.py:907
  411.8 25.7 %collective-permute-start.44 = (bf16[160,2048]{1,0:T(8,128)(2,1)}, bf16[160,2048]{1,0:T(8,128)(2,1)}, u32[]{:S(2)}, u32[]{:S(2)}) collective-permute-start(bf16[160,2048]{1,0:T(8,128)(2,1)} %get-tuple-element.503), channel_id=1, source_target_pairs={{0,2},{2,4},{4,6},{6,7},{7,5},{5,3},{3,1},{1,0},{8,10},{10,12},{12... | collective-permute-start | bytes 1966088 | tf_op jit(solution)/shard_map/ppermute | solution.py:88
  412.0 25.6 %collective-permute-start.45 = (bf16[160,2048]{1,0:T(8,128)(2,1)}, bf16[160,2048]{1,0:T(8,128)(2,1)}, u32[]{:S(2)}, u32[]{:S(2)}) collective-permute-start(bf16[160,2048]{1,0:T(8,128)(2,1)} %get-tuple-element.502), channel_id=1, source_target_pairs={{0,1},{2,0},{4,2},{6,4},{7,6},{5,7},{3,5},{1,3},{8,9},{10,8},{12,1... | collective-permute-start | bytes 1966088 | tf_op jit(solution)/shard_map/ppermute | solution.py:88
  416.9 20.9 %collective-permute-start.42 = (bf16[160,2048]{1,0:T(8,128)(2,1)}, bf16[160,2048]{1,0:T(8,128)(2,1)S(1)}, u32[]{:S(2)}, u32[]{:S(2)}) collective-permute-start(bf16[160,2048]{1,0:T(8,128)(2,1)} %get-tuple-element.518), channel_id=1, source_target_pairs={{0,2},{2,4},{4,6},{6,7},{7,5},{5,3},{3,1},{1,0},{8,10},{10,12},{12... | collective-permute-start | bytes 1966088 | tf_op jit(solution)/shard_map/ppermute | solution.py:88
  416.9 20.9 %collective-permute-start.43 = (bf16[160,2048]{1,0:T(8,128)(2,1)}, bf16[160,2048]{1,0:T(8,128)(2,1)S(1)}, u32[]{:S(2)}, u32[]{:S(2)}) collective-permute-start(bf16[160,2048]{1,0:T(8,128)(2,1)} %get-tuple-element.517), channel_id=1, source_target_pairs={{0,1},{2,0},{4,2},{6,4},{7,6},{5,7},{3,5},{1,3},{8,9},{10,8},{12,1... | collective-permute-start | bytes 1966088 | tf_op jit(solution)/shard_map/ppermute | solution.py:88
  440.7 16.6 %collective-permute-start.46 = (bf16[160,2048]{1,0:T(8,128)(2,1)S(1)}, bf16[160,2048]{1,0:T(8,128)(2,1)S(1)}, u32[]{:S(2)}, u32[]{:S(2)}) collective-permute-start(bf16[160,2048]{1,0:T(8,128)(2,1)S(1)} %get-tuple-element.501), channel_id=1, source_target_pairs={{0,2},{2,4},{4,6},{6,7},{7,5},{5,3},{3,1},{1,0},{8,10},{10,12},{12... | collective-permute-start | bytes 1966088 | tf_op jit(solution)/shard_map/ppermute | solution.py:88
  440.9 16.5 %collective-permute-start.47 = (bf16[160,2048]{1,0:T(8,128)(2,1)S(1)}, bf16[160,2048]{1,0:T(8,128)(2,1)S(1)}, u32[]{:S(2)}, u32[]{:S(2)}) collective-permute-start(bf16[160,2048]{1,0:T(8,128)(2,1)S(1)} %get-tuple-element.500), channel_id=1, source_target_pairs={{0,1},{2,0},{4,2},{6,4},{7,6},{5,7},{3,5},{1,3},{8,9},{10,8},{12,1... | collective-permute-start | bytes 1966088 | tf_op jit(solution)/shard_map/ppermute | solution.py:88
  458.2 24.3 %collective-permute-start.48 = (bf16[160,2048]{1,0:T(8,128)(2,1)S(1)}, bf16[160,2048]{1,0:T(8,128)(2,1)S(1)}, u32[]{:S(2)}, u32[]{:S(2)}) collective-permute-start(bf16[160,2048]{1,0:T(8,128)(2,1)S(1)} %get-tuple-element.342.refs_0_), channel_id=1, source_target_pairs={{0,2},{2,4},{4,6},{6,7},{7,5},{5,3},{3,1},{1,0},{8,10},{10,12},{12... | collective-permute-start | bytes 1966088 | tf_op jit(solution)/shard_map/ppermute | solution.py:88
  459.0 23.5 %collective-permute-start.49 = (bf16[160,2048]{1,0:T(8,128)(2,1)S(1)}, bf16[160,2048]{1,0:T(8,128)(2,1)S(1)}, u32[]{:S(2)}, u32[]{:S(2)}) collective-permute-start(bf16[160,2048]{1,0:T(8,128)(2,1)S(1)} %get-tuple-element.342.refs_0_), channel_id=1, source_target_pairs={{0,1},{2,0},{4,2},{6,4},{7,6},{5,7},{3,5},{1,3},{8,9},{10,8},{12,1... | collective-permute-start | bytes 1966088 | tf_op jit(solution)/shard_map/ppermute | solution.py:88
  460.5 24.7 %all-to-all-start.4 = ((bf16[8,160,256]{2,1,0:T(8,128)(2,1)}), bf16[8,160,256]{2,1,0:T(8,128)(2,1)S(1)}, u32[]{:S(2)}, u32[]{:S(2)}) async-start(bf16[8,160,256]{2,1,0:T(8,128)(2,1)} %bitcast.156), calls=%async_computation.4 | async-start | bytes 1310720 | tf_op jit(solution)/shard_map/all_to_all | solution.py:250
  465.6 178.8 %reduce-scatter.8.cloned.1.call-start = ((), (), s32[]{:S(2)}) async-start(), calls=%async_computation.13 | async-start | bytes 10485760 | tf_op jit(solution)/shard_map/reduce_scatter | solution.py:908
  486.0 19.0 %collective-permute-start.50 = (bf16[160,2048]{1,0:T(8,128)(2,1)S(1)}, bf16[160,2048]{1,0:T(8,128)(2,1)S(1)}, u32[]{:S(2)}, u32[]{:S(2)}) collective-permute-start(bf16[160,2048]{1,0:T(8,128)(2,1)S(1)} %collective-permute-done.48.refs_2_), channel_id=1, source_target_pairs={{0,2},{2,4},{4,6},{6,7},{7,5},{5,3},{3,1},{1,0},{8,10},{10,12},{12... | collective-permute-start | bytes 1966088 | tf_op jit(solution)/shard_map/ppermute | solution.py:88
  486.0 19.0 %collective-permute-start.51 = (bf16[160,2048]{1,0:T(8,128)(2,1)S(1)}, bf16[160,2048]{1,0:T(8,128)(2,1)S(1)}, u32[]{:S(2)}, u32[]{:S(2)}) collective-permute-start(bf16[160,2048]{1,0:T(8,128)(2,1)S(1)} %collective-permute-done.49.refs_1_), channel_id=1, source_target_pairs={{0,1},{2,0},{4,2},{6,4},{7,6},{5,7},{3,5},{1,3},{8,9},{10,8},{12,1... | collective-permute-start | bytes 1966088 | tf_op jit(solution)/shard_map/ppermute | solution.py:88
  506.2 16.4 %collective-permute-start.52 = (bf16[160,2048]{1,0:T(8,128)(2,1)}, bf16[160,2048]{1,0:T(8,128)(2,1)S(1)}, u32[]{:S(2)}, u32[]{:S(2)}) collective-permute-start(bf16[160,2048]{1,0:T(8,128)(2,1)} %copy-done.61), channel_id=1, source_target_pairs={{0,2},{2,4},{4,6},{6,7},{7,5},{5,3},{3,1},{1,0},{8,10},{10,12},{12... | collective-permute-start | bytes 1966088 | tf_op jit(solution)/shard_map/ppermute | solution.py:88
  506.2 16.5 %collective-permute-start.53 = (bf16[160,2048]{1,0:T(8,128)(2,1)}, bf16[160,2048]{1,0:T(8,128)(2,1)S(1)}, u32[]{:S(2)}, u32[]{:S(2)}) collective-permute-start(bf16[160,2048]{1,0:T(8,128)(2,1)} %copy-done.62), channel_id=1, source_target_pairs={{0,1},{2,0},{4,2},{6,4},{7,6},{5,7},{3,5},{1,3},{8,9},{10,8},{12,1... | collective-permute-start | bytes 1966088 | tf_op jit(solution)/shard_map/ppermute | solution.py:88
  556.3 33.0 %collective-permute-start.61 = (bf16[8,1,64,768]{3,2,1,0:T(8,128)(2,1)}, bf16[8,1,64,768]{3,2,1,0:T(8,128)(2,1)S(1)}, u32[]{:S(2)}, u32[]{:S(2)}) collective-permute-start(bf16[8,1,64,768]{3,2,1,0:T(8,128)(2,1)} %constant_dynamic-slice_fusion.1), channel_id=1, source_target_pairs={{0,16},{8,24},{16,0},{24,8},{1,17},{9,25},{17,1},{25,9},{2,18},{10... | collective-permute-start | bytes 2359304 | tf_op jit(solution)/shard_map/ppermute | solution.py:204
  568.8 21.5 %collective-permute-start.62 = (bf16[2,64,2048]{2,1,0:T(8,128)(2,1)}, bf16[2,64,2048]{2,1,0:T(8,128)(2,1)}, u32[]{:S(2)}, u32[]{:S(2)}) collective-permute-start(bf16[2,64,2048]{2,1,0:T(8,128)(2,1)} %dynamic-slice_bitcast_fusion.1), channel_id=1, source_target_pairs={{0,8},{8,0},{16,24},{24,16},{1,9},{9,1},{17,25},{25,17},{2,10},{10... | collective-permute-start | bytes 1572872 | tf_op jit(solution)/shard_map/ppermute | solution.py:204
  579.1 19.6 %collective-permute-start.60 = (bf16[160,2048]{1,0:T(8,128)(2,1)}, bf16[160,2048]{1,0:T(8,128)(2,1)}, u32[]{:S(2)}, u32[]{:S(2)}) collective-permute-start(bf16[160,2048]{1,0:T(8,128)(2,1)} %pad_maximum_fusion.12), channel_id=1, source_target_pairs={{0,1},{2,0},{4,2},{6,4},{7,6},{5,7},{3,5},{1,3},{8,9},{10,8},{12,1... | collective-permute-start | bytes 1966088 | tf_op jit(solution)/shard_map/ppermute | solution.py:88
  581.1 17.6 %collective-permute-start.59 = (bf16[160,2048]{1,0:T(8,128)(2,1)}, bf16[160,2048]{1,0:T(8,128)(2,1)}, u32[]{:S(2)}, u32[]{:S(2)}) collective-permute-start(bf16[160,2048]{1,0:T(8,128)(2,1)} %pad_maximum_fusion.11), channel_id=1, source_target_pairs={{0,2},{2,4},{4,6},{6,7},{7,5},{5,3},{3,1},{1,0},{8,10},{10,12},{12... | collective-permute-start | bytes 1966088 | tf_op jit(solution)/shard_map/ppermute | solution.py:88
  602.1 28.3 %collective-permute-start.63 = (bf16[160,2048]{1,0:T(8,128)(2,1)}, bf16[160,2048]{1,0:T(8,128)(2,1)}, u32[]{:S(2)}, u32[]{:S(2)}) collective-permute-start(bf16[160,2048]{1,0:T(8,128)(2,1)} %get-tuple-element.493), channel_id=1, source_target_pairs={{0,2},{2,4},{4,6},{6,7},{7,5},{5,3},{3,1},{1,0},{8,10},{10,12},{12... | collective-permute-start | bytes 1966088 | tf_op jit(solution)/shard_map/ppermute | solution.py:88
  604.3 26.0 %collective-permute-start.64 = (bf16[160,2048]{1,0:T(8,128)(2,1)}, bf16[160,2048]{1,0:T(8,128)(2,1)}, u32[]{:S(2)}, u32[]{:S(2)}) collective-permute-start(bf16[160,2048]{1,0:T(8,128)(2,1)} %get-tuple-element.492), channel_id=1, source_target_pairs={{0,1},{2,0},{4,2},{6,4},{7,6},{5,7},{3,5},{1,3},{8,9},{10,8},{12,1... | collective-permute-start | bytes 1966088 | tf_op jit(solution)/shard_map/ppermute | solution.py:88
  604.3 33.0 %all-to-all-start.6 = ((bf16[8,64,768]{2,1,0:T(8,128)(2,1)}), bf16[8,64,768]{2,1,0:T(8,128)(2,1)S(1)}, u32[]{:S(2)}, u32[]{:S(2)}) async-start(bf16[8,64,768]{2,1,0:T(8,128)(2,1)} %bitcast.64), calls=%async_computation.7 | async-start | bytes 1572864 | tf_op jit(solution)/shard_map/all_to_all | solution.py:250
  613.6 16.7 %collective-permute-start.65 = (bf16[1,64,2048]{2,1,0:T(8,128)(2,1)S(1)}, bf16[1,64,2048]{2,1,0:T(8,128)(2,1)S(1)}, u32[]{:S(2)}, u32[]{:S(2)}) collective-permute-start(bf16[1,64,2048]{2,1,0:T(8,128)(2,1)S(1)} %constant_dynamic-slice_fusion), channel_id=1, source_target_pairs={{0,16},{8,24},{16,0},{24,8},{1,17},{9,25},{17,1},{25,9},{2,18},{10... | collective-permute-start | bytes 786440 | tf_op jit(solution)/shard_map/ppermute | solution.py:204
  614.2 14.9 %collective-permute-start.67 = (f32[4640]{0:T(1024)S(1)}, f32[4640]{0:T(1024)S(1)}, u32[]{:S(2)}, u32[]{:S(2)}) collective-permute-start(f32[4640]{0:T(1024)S(1)} %add.646), channel_id=1, source_target_pairs={{0,16},{8,24},{16,0},{24,8},{1,17},{9,25},{17,1},{25,9},{2,18},{10... | collective-permute-start | bytes 55688 | tf_op jit(solution)/shard_map/ppermute | solution.py:204
  638.9 24.3 %collective-permute-start.70 = (bf16[1,3,64,2048]{3,2,1,0:T(8,128)(2,1)S(1)}, bf16[1,3,64,2048]{3,2,1,0:T(8,128)(2,1)}, u32[]{:S(2)}, u32[]{:S(2)}) collective-permute-start(bf16[1,3,64,2048]{3,2,1,0:T(8,128)(2,1)S(1)} %stack.161), channel_id=1, source_target_pairs={{0,16},{8,24},{16,0},{24,8},{1,17},{9,25},{17,1},{25,9},{2,18},{10... | collective-permute-start | bytes 2359304 | tf_op jit(solution)/shard_map/ppermute | solution.py:204
  642.8 19.3 %collective-permute-start.71 = (bf16[1,64,2048]{2,1,0:T(8,128)(2,1)S(1)}, bf16[1,64,2048]{2,1,0:T(8,128)(2,1)}, u32[]{:S(2)}, u32[]{:S(2)}) collective-permute-start(bf16[1,64,2048]{2,1,0:T(8,128)(2,1)S(1)} %add_convert_fusion.19), channel_id=1, source_target_pairs={{0,16},{8,24},{16,0},{24,8},{1,17},{9,25},{17,1},{25,9},{2,18},{10... | collective-permute-start | bytes 786440 | tf_op jit(solution)/shard_map/ppermute | solution.py:204
  646.0 19.0 %collective-permute-start.68 = (bf16[160,2048]{1,0:T(8,128)(2,1)}, bf16[160,2048]{1,0:T(8,128)(2,1)S(1)}, u32[]{:S(2)}, u32[]{:S(2)}) collective-permute-start(bf16[160,2048]{1,0:T(8,128)(2,1)} %get-tuple-element.491), channel_id=1, source_target_pairs={{0,2},{2,4},{4,6},{6,7},{7,5},{5,3},{3,1},{1,0},{8,10},{10,12},{12... | collective-permute-start | bytes 1966088 | tf_op jit(solution)/shard_map/ppermute | solution.py:88
  646.3 18.7 %collective-permute-start.69 = (bf16[160,2048]{1,0:T(8,128)(2,1)}, bf16[160,2048]{1,0:T(8,128)(2,1)S(1)}, u32[]{:S(2)}, u32[]{:S(2)}) collective-permute-start(bf16[160,2048]{1,0:T(8,128)(2,1)} %get-tuple-element.490), channel_id=1, source_target_pairs={{0,1},{2,0},{4,2},{6,4},{7,6},{5,7},{3,5},{1,3},{8,9},{10,8},{12,1... | collective-permute-start | bytes 1966088 | tf_op jit(solution)/shard_map/ppermute | solution.py:88
  (169 other events, 1776.4 us)
Sparse Core Ops, SparseCore 0:
  42.8 57.6 all-gather.1
  408.5 72.8 reduce-scatter.3
  484.1 71.7 reduce-scatter.5
  558.3 78.3 reduce-scatter.7

commit v17 on v12

--- a/solution.py
+++ b/solution.py
@@ -796,7 +796,6 @@
         lambda uback: grad_of(second_all, uback),
         uback_all,
     )
-    mixture = mixture_ring.total()
     mixed_grad = swap.received
 
     sent, gain_parts = (), 0.0
@@ -892,18 +891,22 @@
         waits=(head_part,),
     )
     head_rows = swap_all(head_part.reshape(group_count, share, 3 * width_here))
+    def layer_work(own, *sums):
+        mixture = sum((part.astype(wide_type) for part in sums), own.astype(wide_type))
+        return (valid_own * (residual + mixture)).astype(low_type)
+
     (output_part, small_sums, gate_total, layer_out), head_rows = window(
         [first_ring],
         lambda output, small, total, sums: (
             rep_scatter(output, 0, scatter_order[1:]),
             small_pieces(small, small_parts),
             split_experts(total),
-            (valid_own * (residual + sums)).astype(low_type),
+            layer_work(*sums),
         ),
         output_part,
         small_swapped,
         gate_sum,
-        mixture,
+        (mixture_part[:row_count], *mixture_ring.sent),
         waits=(head_rows,),
     )
     head_rows = rep_gather(

time: 690 us -> 691 us (level)
    unnamed x328 -> x326, local copies, waits for them, and re-layouts: 31.7 us -> 32.1 us
  transfers between devices with their start and end apart: 85 -> 85, of which waited for: 29 -> 30; matrix products, arithmetic and copies ran while one was open for 38% -> 38% of each run, Pallas kernels for 10% -> 10%
where the time goes in v17:
time: 691 us; the launch traced here: 681 us
  waiting for transfers between devices  137 us (20%)
  matrix products  127 us (18%)
  starting transfers between devices  115 us (17%)
  Pallas kernels  107 us (15%)
  other arithmetic  96.5 us (14%)
  local copies, waits for them, and re-layouts  80.4 us (12%)
  between operations  17.5 us (3%)
    dot_general x26, matrix products, mm(): lax.dot_general(left, right, (((left_dim,), (right_dim,)), ((), ())), pre...  127 us
    ppermute x56, waiting for transfers between devices, ring_shift(): return lax.ppermute(values, 'ep', pairs)  77.2 us
    ppermute x56, starting transfers between devices, ring_shift(): return lax.ppermute(values, 'ep', pairs)  66.3 us
    pallas_call x2, Pallas kernels, expert_pass(): pl.pallas_call(expert_kernel, grid=(experts, steps), in_specs=[pl.BlockSp...  39 us
    all_to_all x7, waiting for transfers between devices, swap_all(): return lax.all_to_all(values, 'ep', split_axis=0, concat_axis=0, tiled=True)  37.8 us
    all_to_all x7, starting transfers between devices, swap_all(): return lax.all_to_all(values, 'ep', split_axis=0, concat_axis=0, tiled=True)  35 us
    pallas_call x2, Pallas kernels, expert_back(): pl.pallas_call(expert_back_kernel, grid=(depth // width,), in_specs=[whol...  33.6 us
    unnamed x326, local copies, waits for them, and re-layouts  32.1 us
  transfers between devices with their start and end apart: 85, of which 30 were waited for; matrix products, arithmetic and copies ran while one was open for 38% of the time, Pallas kernels for 10%

profile of v17, /device:TPU:0, one launch (start us, length us, event | category | flops | bytes accessed | tf_op | source)
XLA Modules:
  0.0 681.1 jit_solution(4139120920821026122)
XLA Ops:
  11.5 7.3 %all-to-all-start = ((bf16[8,64,768]{2,1,0:T(8,128)(2,1)}), bf16[8,64,768]{2,1,0:T(8,128)(2,1)S(1)}, u32[]{:S(2)}, u32[]{:S(2)}) async-start(bf16[8,64,768]{2,1,0:T(8,128)(2,1)} %copy.138), calls=%async_computation | async-start | bytes 1572864 | tf_op jit(solution)/shard_map/all_to_all | solution.py:250
  19.9 19.0 %all-to-all-done = bf16[8,64,768]{2,1,0:T(8,128)(2,1)S(1)} async-done(((bf16[8,64,768]{2,1,0:T(8,128)(2,1)}), bf16[8,64,768]{2,1,0:T(8,128)(2,1)S(1)}, u32[]{:S(2)}, u32[]{:S(2)}) %all-to-all-start) | async-done | bytes 786464 | tf_op jit(solution)/shard_map/all_to_all | solution.py:250
  47.3 9.7 %collective-permute-done.4 = bf16[160,2048]{1,0:T(8,128)(2,1)} collective-permute-done((bf16[160,2048]{1,0:T(8,128)(2,1)S(1)}, bf16[160,2048]{1,0:T(8,128)(2,1)}, u32[]{:S(2)}, u32[]{:S(2)}) %collective-permute-start.4) | collective-permute-done | bytes 655392 | tf_op jit(solution)/shard_map/ppermute | solution.py:88
  59.9 4.1 all-to-all-start.2
  66.0 3.7 multiply_cosine_fusion
  79.3 10.4 %collective-permute-done.1 = bf16[160,2048]{1,0:T(8,128)(2,1)} collective-permute-done((bf16[160,2048]{1,0:T(8,128)(2,1)}, bf16[160,2048]{1,0:T(8,128)(2,1)}, u32[]{:S(2)}, u32[]{:S(2)}) %collective-permute-start.1) | collective-permute-done | bytes 655392 | tf_op jit(solution)/shard_map/ppermute | solution.py:88
  89.7 8.3 %collective-permute-start.2 = (bf16[160,2048]{1,0:T(8,128)(2,1)}, bf16[160,2048]{1,0:T(8,128)(2,1)S(1)}, u32[]{:S(2)}, u32[]{:S(2)}) collective-permute-start(bf16[160,2048]{1,0:T(8,128)(2,1)} %collective-permute-done.1), channel_id=1, source_target_pairs={{0,2},{2,4},{4,6},{6,7},{7,5},{5,3},{3,1},{1,0},{8,10},{10,12},{12... | collective-permute-start | bytes 1966088 | tf_op jit(solution)/shard_map/ppermute | solution.py:88
  98.0 2.5 collective-permute-done.5
  102.9 10.9 %collective-permute-done.6 = bf16[160,2048]{1,0:T(8,128)(2,1)S(1)} collective-permute-done((bf16[160,2048]{1,0:T(8,128)(2,1)}, bf16[160,2048]{1,0:T(8,128)(2,1)S(1)}, u32[]{:S(2)}, u32[]{:S(2)}) %collective-permute-start.6) | collective-permute-done | bytes 655392 | tf_op jit(solution)/shard_map/ppermute | solution.py:88
  116.8 2.3 maximum_select_fusion
  136.8 4.3 fusion.75.query_raw_ref.key_raw_ref
  168.1 3.9 collective-permute-done.16
  177.3 6.1 collective-permute-done.19
  184.6 4.6 all-to-all-start.1
  191.2 2.3 constant_dynamic-update-slice_fusion.44
  193.5 2.3 constant_dynamic-update-slice_fusion.43
  198.8 6.5 all-to-all-done.1
  209.5 2.2 convolution_dynamic-update-slice_fusion.1
  217.7 7.4 %fusion.76.stream_ref = f32[640,2048]{1,0:T(8,128)} fusion(bf16[640,2048]{1,0:T(8,128)(2,1)S(1)} %copy-done.31, bf16[2048,2048]{1,0:T(8,128)(2,1)S(1)} %bitcast.276), kind=kOutput, calls=%fused_computation.332 | convolution fusion | flops 5368709120 | bytes 16252928 | tf_op jit(solution)/shard_map/dot_general | solution.py:60
  226.1 4.2 collective-permute-done.24
  232.3 9.0 %fusion.77.stream_ref = f32[640,2048]{1,0:T(8,128)} fusion(bf16[640,2048]{1,0:T(8,128)(2,1)} %get-tuple-element.241, bf16[2048,2048]{1,0:T(8,128)(2,1)S(1)} %bitcast.277), kind=kOutput, calls=%fused_computation.333 | convolution fusion | flops 5368709120 | bytes 16252928 | tf_op jit(solution)/shard_map/dot_general | solution.py:60
  241.4 2.6 collective-permute-done.26
  252.1 19.4 %shard_map.281 = (bf16[1280,2048]{1,0:T(8,128)(2,1)}, bf16[1280,2048]{1,0:T(8,128)(2,1)}, bf16[1280,2048]{1,0:T(8,128)(2,1)}, f32[2,640,128]{2,1,0:T(8,128)}) custom-call(bf16[640,2048]{1,0:T(8,128)(2,1)} %copy-done.32, bf16[2,2048,1024]{2,1,0:T(8,128)(2,1)} %gate_ref.7, bf16[2,2048,1024]{2,1,0:T(8,128)(2,1)} %up_ref.7, f32[640,2048]{1,0:T(8,128)} %fusion.76.stream_ref, ...), custom_call_target="tpu_custom_call" | custom-call | flops 10737418240 | bytes 42991616 | tf_op jit(solution)/shard_map/pallas_call | solution.py:294
  275.9 2.8 collective-permute-done.30
  285.4 19.5 %shard_map.282 = (bf16[1280,2048]{1,0:T(8,128)(2,1)}, bf16[1280,2048]{1,0:T(8,128)(2,1)}, bf16[1280,2048]{1,0:T(8,128)(2,1)}, f32[2,640,128]{2,1,0:T(8,128)}) custom-call(bf16[640,2048]{1,0:T(8,128)(2,1)} %copy-done.26, bf16[2,2048,1024]{2,1,0:T(8,128)(2,1)} %gate_ref.7, ...), custom_call_target="tpu_custom_call", output_to_operand_aliasing={{0}: (5, {}), {1}: (6, {}), {2}: (7, {})} | custom-call | flops 10737418240 | bytes 42991616 | tf_op jit(solution)/shard_map/pallas_call | solution.py:294
  306.9 16.8 %shard_map.283 = bf16[640,2048]{1,0:T(8,128)(2,1)} custom-call(bf16[1280,2048]{1,0:T(8,128)(2,1)} %get-tuple-element.284.gback_ref, bf16[1280,2048]{1,0:T(8,128)(2,1)} %get-tuple-element.293.uback_ref, bf16[2,2048,1024]{2,1,0:T(8,128)(2,1)} %gate_ref.7, bf16[2,2048,1024]{2,1,0:T(8,128)(2,1)} %up_ref.7), custom_call_target="tpu_custom_call" | custom-call | flops 10737418240 | bytes 24641536 | tf_op jit(solution)/shard_map/pallas_call | solution.py:334
  328.2 3.3 all-to-all-start.3
  331.6 16.5 %convolution_convert_fusion.3 = bf16[1280,2048]{1,0:T(8,128)(2,1)} fusion(bf16[1280,2048]{1,0:T(8,128)(2,1)} %get-tuple-element.277, bf16[2048,2048]{1,0:T(8,128)(2,1)} %bitcast.273), kind=kOutput, calls=%fused_computation.17 | convolution fusion | flops 10740039680 | bytes 18874368 | tf_op jit(solution)/shard_map/dot_general | solution.py:60
  357.0 16.8 %shard_map.284 = bf16[640,2048]{1,0:T(8,128)(2,1)} custom-call(bf16[1280,2048]{1,0:T(8,128)(2,1)} %get-tuple-element.284.gback_ref, bf16[1280,2048]{1,0:T(8,128)(2,1)} %get-tuple-element.293.uback_ref, bf16[2,2048,1024]{2,1,0:T(8,128)(2,1)} %gate_ref.7, bf16[2,2048,1024]{2,1,0:T(8,128)(2,1)} %up_ref.7), custom_call_target="tpu_custom_call" | custom-call | flops 10737418240 | bytes 24641536 | tf_op jit(solution)/shard_map/pallas_call | solution.py:334
  373.8 2.4 add_convert_fusion.11
  376.3 2.3 add_convert_fusion.12
  385.3 15.7 %convolution_convert_fusion.2 = bf16[2048,2048]{1,0:T(8,128)(2,1)} fusion(bf16[1280,2048]{1,0:T(8,128)(2,1)S(1)} %bitcast.171, bf16[1280,2048]{1,0:T(8,128)(2,1)} %get-tuple-element.561), kind=kOutput, calls=%fused_computation.16 | convolution fusion | flops 10741612544 | bytes 18874368 | tf_op jit(solution)/shard_map/dot_general | solution.py:60
  404.2 4.2 collective-permute-done.38
  408.5 3.4 add_convert_fusion.7
  413.9 2.7 add_convert_fusion.9
  416.7 2.3 collective-permute-start.43
  419.0 18.4 %convolution_convert_fusion.1 = bf16[2048,2048]{1,0:T(8,128)(2,1)} fusion(bf16[1280,2048]{1,0:T(8,128)(2,1)} %get-tuple-element.557, bf16[1280,2048]{1,0:T(8,128)(2,1)} %get-tuple-element.284.gback_ref), kind=kOutput, calls=%fused_computation.15 | convolution fusion | flops 10741612544 | bytes 18874368 | tf_op jit(solution)/shard_map/dot_general | solution.py:60
  447.6 2.6 convolution_add_fusion.1
  450.1 2.4 fusion.31
  452.6 2.6 fusion.14
  459.5 5.5 all-to-all-start.4
  465.2 16.7 %convolution_convert_fusion = bf16[2048,2048]{1,0:T(8,128)(2,1)} fusion(bf16[1280,2048]{1,0:T(8,128)(2,1)} %get-tuple-element.557, bf16[1280,2048]{1,0:T(8,128)(2,1)} %get-tuple-element.293.uback_ref), kind=kOutput, calls=%fused_computation.14 | convolution fusion | flops 10741612544 | bytes 18874368 | tf_op jit(solution)/shard_map/dot_general | solution.py:60
  481.9 3.1 all-to-all-done.4.swapped_ref
  490.2 14.6 %shard_map.285 = (bf16[1280,768]{1,0:T(8,128)(2,1)}, f32[2,128]{1,0:T(2,128)}) custom-call(s32[8]{0:T(128)} %stack.156.order_ref, bf16[1280,128]{1,0:T(8,128)(2,1)} %copy-done.49, bf16[1280,128]{1,0:T(8,128)(2,1)} %copy-done.48, bf16[1280,128]{1,0:T(8,128)(2,1)} %slice.504.value_ref, bf16[8,160,256]{2,1,0:T(8,128)(2,1)} %copy-done.13, ...), custom_call_target="tpu_custom_call" | custom-call | flops 2097152000 | bytes 4915200 | tf_op jit(solution)/shard_map/pallas_call | solution.py:421
  509.0 13.3 %shard_map.286 = (bf16[1280,768]{1,0:T(8,128)(2,1)}, f32[2,128]{1,0:T(2,128)}) custom-call(s32[8]{0:T(128)} %stack.156.order_ref, bf16[1280,128]{1,0:T(8,128)(2,1)} %copy-done.47, bf16[1280,128]{1,0:T(8,128)(2,1)} %copy-done.46, bf16[1280,128]{1,0:T(8,128)(2,1)} %slice.503.value_ref, ...), custom_call_target="tpu_custom_call", output_to_operand_aliasing={{0}: (13, {})} | custom-call | flops 2097152000 | bytes 4915200 | tf_op jit(solution)/shard_map/pallas_call | solution.py:421
  526.1 7.7 %convolution_convert_fusion.4 = bf16[2048,768]{1,0:T(8,128)(2,1)S(1)} fusion(bf16[1280,2048]{1,0:T(8,128)(2,1)} %copy-done.21, bf16[1280,768]{1,0:T(8,128)(2,1)} %get-tuple-element.328), kind=kOutput, calls=%fused_computation.22 | convolution fusion | flops 4028104704 | bytes 10354688 | tf_op jit(solution)/shard_map/dot_general | solution.py:60
  534.2 3.7 fusion.5
  538.5 7.3 %fusion.4 = (f32[2048]{0:T(1024)}, bf16[1280,2048]{1,0:T(8,128)(2,1)S(1)}) fusion(bf16[1280,2048]{1,0:T(8,128)(2,1)} %copy-done.3, f32[1280]{0:T(1024)S(1)} %add_rsqrt_fusion, bf16[1280,768]{1,0:T(8,128)(2,1)S(1)} %copy-done.36, bf16[2048,768]{1,0:T(8,128)(2,1)S(1)} %bitcast.188), kind=kOutput, calls=%fused_computation.8 | convolution fusion | flops 4039636992 | bytes 15610880 | tf_op jit(solution)/shard_map/dot_general | solution.py:60
  554.3 6.4 shard_map.287
  568.3 6.1 all-to-all-start.5
  576.7 4.1 convert_element_type.476
  583.6 2.4 add_convert_fusion
  588.0 5.9 collective-permute-done.60
  594.8 3.3 add_convert_fusion.3
  598.1 2.5 collective-permute-start.63
  600.6 4.1 all-to-all-start.6
  604.7 2.7 multiply_convert_fusion
  611.6 2.3 maximum_convert_fusion
  613.9 11.1 %collective-permute-done.67 = f32[4640]{0:T(1024)S(1)} collective-permute-done((f32[4640]{0:T(1024)S(1)}, f32[4640]{0:T(1024)S(1)}, u32[]{:S(2)}, u32[]{:S(2)}) %collective-permute-start.67) | collective-permute-done | bytes 18592 | tf_op jit(solution)/shard_map/ppermute | solution.py:204
  626.2 7.2 %all-to-all-done.6 = bf16[8,64,768]{2,1,0:T(8,128)(2,1)S(1)} async-done(((bf16[8,64,768]{2,1,0:T(8,128)(2,1)}), bf16[8,64,768]{2,1,0:T(8,128)(2,1)S(1)}, u32[]{:S(2)}, u32[]{:S(2)}) %all-to-all-start.6) | async-done | bytes 786464 | tf_op jit(solution)/shard_map/all_to_all | solution.py:250
  635.3 3.4 add_convert_fusion.1
  644.2 2.3 maximum_convert_fusion.1
  647.3 11.0 %collective-permute-done.71 = bf16[1,64,2048]{2,1,0:T(8,128)(2,1)} collective-permute-done((bf16[1,64,2048]{2,1,0:T(8,128)(2,1)S(1)}, bf16[1,64,2048]{2,1,0:T(8,128)(2,1)}, u32[]{:S(2)}, u32[]{:S(2)}) %collective-permute-start.71) | collective-permute-done | bytes 262176 | tf_op jit(solution)/shard_map/ppermute | solution.py:204
  663.4 2.7 fusion.20
  (672 shorter events, 226.4 us)
Async XLA Ops:
  11.5 27.4 %all-to-all-start = ((bf16[8,64,768]{2,1,0:T(8,128)(2,1)}), bf16[8,64,768]{2,1,0:T(8,128)(2,1)S(1)}, u32[]{:S(2)}, u32[]{:S(2)}) async-start(bf16[8,64,768]{2,1,0:T(8,128)(2,1)} %copy.138), calls=%async_computation | async-start | bytes 1572864 | tf_op jit(solution)/shard_map/all_to_all | solution.py:250
  18.7 96.6 %all-gather.2.cloned.1.call-start = ((), (), s32[]{:S(2)}) async-start(), calls=%async_computation.10 | async-start | bytes 2359296 | tf_op jit(solution)/shard_map/all_gather | solution.py:69
  38.9 18.2 %collective-permute-start.4 = (bf16[160,2048]{1,0:T(8,128)(2,1)S(1)}, bf16[160,2048]{1,0:T(8,128)(2,1)}, u32[]{:S(2)}, u32[]{:S(2)}) collective-permute-start(bf16[160,2048]{1,0:T(8,128)(2,1)S(1)} %copy-done.8), channel_id=1, source_target_pairs={{0,1},{2,0},{4,2},{6,4},{7,6},{5,7},{3,5},{1,3},{8,9},{10,8},{12,1... | collective-permute-start | bytes 1966088 | tf_op jit(solution)/shard_map/ppermute | solution.py:88
  40.3 18.9 %collective-permute-start = (bf16[160,2048]{1,0:T(8,128)(2,1)S(1)}, bf16[160,2048]{1,0:T(8,128)(2,1)}, u32[]{:S(2)}, u32[]{:S(2)}) collective-permute-start(bf16[160,2048]{1,0:T(8,128)(2,1)S(1)} %copy-done.8), channel_id=1, source_target_pairs={{0,2},{2,4},{4,6},{6,7},{7,5},{5,3},{3,1},{1,0},{8,10},{10,12},{12... | collective-permute-start | bytes 1966088 | tf_op jit(solution)/shard_map/ppermute | solution.py:88
  45.8 24.0 %collective-permute-start.11 = (bf16[1,8,64,768]{3,2,1,0:T(8,128)(2,1)S(1)}, bf16[1,8,64,768]{3,2,1,0:T(8,128)(2,1)S(1)}, u32[]{:S(2)}, u32[]{:S(2)}) collective-permute-start(bf16[1,8,64,768]{3,2,1,0:T(8,128)(2,1)S(1)} %bitcast.166), channel_id=1, source_target_pairs={{0,16},{8,24},{16,0},{24,8},{1,17},{9,25},{17,1},{25,9},{2,18},{10... | collective-permute-start | bytes 2359304 | tf_op jit(solution)/shard_map/ppermute | solution.py:204
  64.0 25.8 %collective-permute-start.1 = (bf16[160,2048]{1,0:T(8,128)(2,1)}, bf16[160,2048]{1,0:T(8,128)(2,1)}, u32[]{:S(2)}, u32[]{:S(2)}) collective-permute-start(bf16[160,2048]{1,0:T(8,128)(2,1)} %collective-permute-done), channel_id=1, source_target_pairs={{0,2},{2,4},{4,6},{6,7},{7,5},{5,3},{3,1},{1,0},{8,10},{10,12},{12... | collective-permute-start | bytes 1966088 | tf_op jit(solution)/shard_map/ppermute | solution.py:88
  66.0 34.5 %collective-permute-start.5 = (bf16[160,2048]{1,0:T(8,128)(2,1)}, bf16[160,2048]{1,0:T(8,128)(2,1)}, u32[]{:S(2)}, u32[]{:S(2)}) collective-permute-start(bf16[160,2048]{1,0:T(8,128)(2,1)} %collective-permute-done.4), channel_id=1, source_target_pairs={{0,1},{2,0},{4,2},{6,4},{7,6},{5,7},{3,5},{1,3},{8,9},{10,8},{12,1... | collective-permute-start | bytes 1966088 | tf_op jit(solution)/shard_map/ppermute | solution.py:88
  71.1 45.6 %collective-permute-start.12 = (bf16[2,8,64,768]{3,2,1,0:T(8,128)(2,1)}, bf16[2,8,64,768]{3,2,1,0:T(8,128)(2,1)}, u32[]{:S(2)}, u32[]{:S(2)}) collective-permute-start(bf16[2,8,64,768]{3,2,1,0:T(8,128)(2,1)} %maximum_select_fusion.3), channel_id=1, source_target_pairs={{0,8},{8,0},{16,24},{24,16},{1,9},{9,1},{17,25},{25,17},{2,10},{10... | collective-permute-start | bytes 4718600 | tf_op jit(solution)/shard_map/ppermute | solution.py:204
  89.7 25.6 %collective-permute-start.2 = (bf16[160,2048]{1,0:T(8,128)(2,1)}, bf16[160,2048]{1,0:T(8,128)(2,1)S(1)}, u32[]{:S(2)}, u32[]{:S(2)}) collective-permute-start(bf16[160,2048]{1,0:T(8,128)(2,1)} %collective-permute-done.1), channel_id=1, source_target_pairs={{0,2},{2,4},{4,6},{6,7},{7,5},{5,3},{3,1},{1,0},{8,10},{10,12},{12... | collective-permute-start | bytes 1966088 | tf_op jit(solution)/shard_map/ppermute | solution.py:88
  120.9 20.4 %collective-permute-start.10 = (bf16[512,512]{1,0:T(8,128)(2,1)S(1)}, bf16[512,512]{1,0:T(8,128)(2,1)S(1)}, u32[]{:S(2)}, u32[]{:S(2)}) collective-permute-start(bf16[512,512]{1,0:T(8,128)(2,1)S(1)} %get-tuple-element.528), channel_id=1, source_target_pairs={{0,16},{8,24},{16,0},{24,8},{1,17},{9,25},{17,1},{25,9},{2,18},{10... | collective-permute-start | bytes 1572872 | tf_op jit(solution)/shard_map/ppermute | solution.py:204
  122.4 32.2 %collective-permute-start.15 = (bf16[512,512]{1,0:T(8,128)(2,1)S(1)}, bf16[512,512]{1,0:T(8,128)(2,1)S(1)}, u32[]{:S(2)}, u32[]{:S(2)}) collective-permute-start(bf16[512,512]{1,0:T(8,128)(2,1)S(1)} %get-tuple-element.527), channel_id=1, source_target_pairs={{0,16},{8,24},{16,0},{24,8},{1,17},{9,25},{17,1},{25,9},{2,18},{10... | collective-permute-start | bytes 1572872 | tf_op jit(solution)/shard_map/ppermute | solution.py:204
  123.0 45.2 %collective-permute-start.18 = (bf16[512,512]{1,0:T(8,128)(2,1)S(1)}, bf16[512,512]{1,0:T(8,128)(2,1)S(1)}, u32[]{:S(2)}, u32[]{:S(2)}) collective-permute-start(bf16[512,512]{1,0:T(8,128)(2,1)S(1)} %get-tuple-element.526), channel_id=1, source_target_pairs={{0,16},{8,24},{16,0},{24,8},{1,17},{9,25},{17,1},{25,9},{2,18},{10... | collective-permute-start | bytes 1572872 | tf_op jit(solution)/shard_map/ppermute | solution.py:204
  126.0 16.8 %collective-permute-start.8 = (bf16[160,2048]{1,0:T(8,128)(2,1)S(1)}, bf16[160,2048]{1,0:T(8,128)(2,1)S(1)}, u32[]{:S(2)}, u32[]{:S(2)}) collective-permute-start(bf16[160,2048]{1,0:T(8,128)(2,1)S(1)} %copy-done.14), channel_id=1, source_target_pairs={{0,2},{2,4},{4,6},{6,7},{7,5},{5,3},{3,1},{1,0},{8,10},{10,12},{12... | collective-permute-start | bytes 1966088 | tf_op jit(solution)/shard_map/ppermute | solution.py:88
  127.3 15.4 %collective-permute-start.9 = (bf16[160,2048]{1,0:T(8,128)(2,1)S(1)}, bf16[160,2048]{1,0:T(8,128)(2,1)S(1)}, u32[]{:S(2)}, u32[]{:S(2)}) collective-permute-start(bf16[160,2048]{1,0:T(8,128)(2,1)S(1)} %copy-done.14), channel_id=1, source_target_pairs={{0,1},{2,0},{4,2},{6,4},{7,6},{5,7},{3,5},{1,3},{8,9},{10,8},{12,1... | collective-permute-start | bytes 1966088 | tf_op jit(solution)/shard_map/ppermute | solution.py:88
  141.3 36.1 %collective-permute-start.21 = (bf16[512,512]{1,0:T(8,128)(2,1)S(1)}, bf16[512,512]{1,0:T(8,128)(2,1)}, u32[]{:S(2)}, u32[]{:S(2)}) collective-permute-start(bf16[512,512]{1,0:T(8,128)(2,1)S(1)} %get-tuple-element.525), channel_id=1, source_target_pairs={{0,16},{8,24},{16,0},{24,8},{1,17},{9,25},{17,1},{25,9},{2,18},{10... | collective-permute-start | bytes 1572872 | tf_op jit(solution)/shard_map/ppermute | solution.py:204
  154.6 54.8 %collective-permute-start.22 = (bf16[2048,512]{1,0:T(8,128)(2,1)S(1)}, bf16[2048,512]{1,0:T(8,128)(2,1)}, u32[]{:S(2)}, u32[]{:S(2)}) collective-permute-start(bf16[2048,512]{1,0:T(8,128)(2,1)S(1)} %copy-done.6), channel_id=1, source_target_pairs={{0,8},{8,0},{16,24},{24,16},{1,9},{9,1},{17,25},{25,17},{2,10},{10... | collective-permute-start | bytes 6291464 | tf_op jit(solution)/shard_map/ppermute | solution.py:204
  155.6 16.4 %collective-permute-start.16 = (bf16[160,2048]{1,0:T(8,128)(2,1)S(1)}, bf16[160,2048]{1,0:T(8,128)(2,1)S(1)}, u32[]{:S(2)}, u32[]{:S(2)}) collective-permute-start(bf16[160,2048]{1,0:T(8,128)(2,1)S(1)} %collective-permute-done.13), channel_id=1, source_target_pairs={{0,2},{2,4},{4,6},{6,7},{7,5},{5,3},{3,1},{1,0},{8,10},{10,12},{12... | collective-permute-start | bytes 1966088 | tf_op jit(solution)/shard_map/ppermute | solution.py:88
  156.9 17.1 %collective-permute-start.17 = (bf16[160,2048]{1,0:T(8,128)(2,1)S(1)}, bf16[160,2048]{1,0:T(8,128)(2,1)S(1)}, u32[]{:S(2)}, u32[]{:S(2)}) collective-permute-start(bf16[160,2048]{1,0:T(8,128)(2,1)S(1)} %collective-permute-done.14), channel_id=1, source_target_pairs={{0,1},{2,0},{4,2},{6,4},{7,6},{5,7},{3,5},{1,3},{8,9},{10,8},{12,1... | collective-permute-start | bytes 1966088 | tf_op jit(solution)/shard_map/ppermute | solution.py:88
  184.6 20.8 %all-to-all-start.1 = ((bf16[8,160,256]{2,1,0:T(8,128)(2,1)}), bf16[8,160,256]{2,1,0:T(8,128)(2,1)}, u32[]{:S(2)}, u32[]{:S(2)}) async-start(bf16[8,160,256]{2,1,0:T(8,128)(2,1)} %copy-done.52), calls=%async_computation.1 | async-start | bytes 1310720 | tf_op jit(solution)/shard_map/all_to_all | solution.py:250
  191.1 20.6 %collective-permute-start.23 = (bf16[2048,512]{1,0:T(8,128)(2,1)}, bf16[2048,512]{1,0:T(8,128)(2,1)}, u32[]{:S(2)}, u32[]{:S(2)}) collective-permute-start(bf16[2048,512]{1,0:T(8,128)(2,1)} %constant_dynamic-update-slice_fusion.18), channel_id=1, source_target_pairs={{0,8},{8,0},{16,24},{24,16},{1,9},{9,1},{17,25},{25,17},{2,10},{10... | collective-permute-start | bytes 6291464 | tf_op jit(solution)/shard_map/ppermute | solution.py:204
  215.4 14.9 %collective-permute-start.24 = (bf16[160,2048]{1,0:T(8,128)(2,1)S(1)}, bf16[160,2048]{1,0:T(8,128)(2,1)S(1)}, u32[]{:S(2)}, u32[]{:S(2)}) collective-permute-start(bf16[160,2048]{1,0:T(8,128)(2,1)S(1)} %get-tuple-element.477), channel_id=1, source_target_pairs={{0,2},{2,4},{4,6},{6,7},{7,5},{5,3},{3,1},{1,0},{8,10},{10,12},{12... | collective-permute-start | bytes 1966088 | tf_op jit(solution)/shard_map/ppermute | solution.py:88
  231.3 14.7 %collective-permute-start.27 = (bf16[160,2048]{1,0:T(8,128)(2,1)S(1)}, bf16[160,2048]{1,0:T(8,128)(2,1)S(1)}, u32[]{:S(2)}, u32[]{:S(2)}) collective-permute-start(bf16[160,2048]{1,0:T(8,128)(2,1)S(1)} %collective-permute-done.25), channel_id=1, source_target_pairs={{0,1},{2,0},{4,2},{6,4},{7,6},{5,7},{3,5},{1,3},{8,9},{10,8},{12,1... | collective-permute-start | bytes 1966088 | tf_op jit(solution)/shard_map/ppermute | solution.py:88
  246.2 25.3 %collective-permute-start.29 = (bf16[160,2048]{1,0:T(8,128)(2,1)S(1)}, bf16[160,2048]{1,0:T(8,128)(2,1)S(1)}, u32[]{:S(2)}, u32[]{:S(2)}) collective-permute-start(bf16[160,2048]{1,0:T(8,128)(2,1)S(1)} %collective-permute-done.27), channel_id=1, source_target_pairs={{0,1},{2,0},{4,2},{6,4},{7,6},{5,7},{3,5},{1,3},{8,9},{10,8},{12,1... | collective-permute-start | bytes 1966088 | tf_op jit(solution)/shard_map/ppermute | solution.py:88
  246.4 25.2 %collective-permute-start.28 = (bf16[160,2048]{1,0:T(8,128)(2,1)S(1)}, bf16[160,2048]{1,0:T(8,128)(2,1)S(1)}, u32[]{:S(2)}, u32[]{:S(2)}) collective-permute-start(bf16[160,2048]{1,0:T(8,128)(2,1)S(1)} %collective-permute-done.26), channel_id=1, source_target_pairs={{0,2},{2,4},{4,6},{6,7},{7,5},{5,3},{3,1},{1,0},{8,10},{10,12},{12... | collective-permute-start | bytes 1966088 | tf_op jit(solution)/shard_map/ppermute | solution.py:88
  325.1 23.0 %collective-permute-start.32 = (bf16[80,2048]{1,0:T(8,128)(2,1)S(1)}, bf16[80,2048]{1,0:T(8,128)(2,1)S(1)}, u32[]{:S(2)}, u32[]{:S(2)}) collective-permute-start(bf16[80,2048]{1,0:T(8,128)(2,1)S(1)} %get-tuple-element.518), channel_id=1, source_target_pairs={{0,2},{2,4},{4,6},{6,7},{7,5},{5,3},{3,1},{1,0},{8,10},{10,12},{12... | collective-permute-start | bytes 983048 | tf_op jit(solution)/shard_map/ppermute | solution.py:88
  326.9 21.2 %collective-permute-start.33 = (bf16[80,2048]{1,0:T(8,128)(2,1)S(1)}, bf16[80,2048]{1,0:T(8,128)(2,1)}, u32[]{:S(2)}, u32[]{:S(2)}) collective-permute-start(bf16[80,2048]{1,0:T(8,128)(2,1)S(1)} %get-tuple-element.517), channel_id=1, source_target_pairs={{0,1},{2,0},{4,2},{6,4},{7,6},{5,7},{3,5},{1,3},{8,9},{10,8},{12,1... | collective-permute-start | bytes 983048 | tf_op jit(solution)/shard_map/ppermute | solution.py:88
  328.2 19.9 %all-to-all-start.3 = ((f32[8,160,2]{1,2,0:T(2,128)}), f32[8,160,2]{1,2,0:T(2,128)S(1)}, u32[]{:S(2)}, u32[]{:S(2)}) async-start(f32[8,160,2]{1,2,0:T(2,128)} %copy.172), calls=%async_computation.3 | async-start | bytes 32768 | tf_op jit(solution)/shard_map/all_to_all | solution.py:250
  331.6 194.5 %reduce-scatter.4.cloned.1.call-start = ((), (), s32[]{:S(2)}) async-start(), calls=%async_computation.11 | async-start | bytes 10485760 | tf_op jit(solution)/shard_map/reduce_scatter | solution.py:824
  351.8 22.0 %collective-permute-start.35 = (bf16[160,2048]{1,0:T(8,128)(2,1)S(1)}, bf16[160,2048]{1,0:T(8,128)(2,1)}, u32[]{:S(2)}, u32[]{:S(2)}) collective-permute-start(bf16[160,2048]{1,0:T(8,128)(2,1)S(1)} %pad_maximum_fusion.7), channel_id=1, source_target_pairs={{0,1},{2,0},{4,2},{6,4},{7,6},{5,7},{3,5},{1,3},{8,9},{10,8},{12,1... | collective-permute-start | bytes 1966088 | tf_op jit(solution)/shard_map/ppermute | solution.py:88
  354.6 19.2 %collective-permute-start.34 = (bf16[160,2048]{1,0:T(8,128)(2,1)}, bf16[160,2048]{1,0:T(8,128)(2,1)}, u32[]{:S(2)}, u32[]{:S(2)}) collective-permute-start(bf16[160,2048]{1,0:T(8,128)(2,1)} %pad_maximum_fusion.6), channel_id=1, source_target_pairs={{0,2},{2,4},{4,6},{6,7},{7,5},{5,3},{3,1},{1,0},{8,10},{10,12},{12... | collective-permute-start | bytes 1966088 | tf_op jit(solution)/shard_map/ppermute | solution.py:88
  354.8 19.0 %collective-permute-start.36 = (bf16[80,2048]{1,0:T(8,128)(2,1)}, bf16[80,2048]{1,0:T(8,128)(2,1)S(1)}, u32[]{:S(2)}, u32[]{:S(2)}) collective-permute-start(bf16[80,2048]{1,0:T(8,128)(2,1)} %get-tuple-element.503), channel_id=1, source_target_pairs={{0,2},{2,4},{4,6},{6,7},{7,5},{5,3},{3,1},{1,0},{8,10},{10,12},{12... | collective-permute-start | bytes 983048 | tf_op jit(solution)/shard_map/ppermute | solution.py:88
  356.7 17.2 %collective-permute-start.37 = (bf16[80,2048]{1,0:T(8,128)(2,1)}, bf16[80,2048]{1,0:T(8,128)(2,1)}, u32[]{:S(2)}, u32[]{:S(2)}) collective-permute-start(bf16[80,2048]{1,0:T(8,128)(2,1)} %get-tuple-element.502), channel_id=1, source_target_pairs={{0,1},{2,0},{4,2},{6,4},{7,6},{5,7},{3,5},{1,3},{8,9},{10,8},{12,1... | collective-permute-start | bytes 983048 | tf_op jit(solution)/shard_map/ppermute | solution.py:88
  380.1 23.3 %collective-permute-start.41 = (bf16[160,2048]{1,0:T(8,128)(2,1)S(1)}, bf16[160,2048]{1,0:T(8,128)(2,1)}, u32[]{:S(2)}, u32[]{:S(2)}) collective-permute-start(bf16[160,2048]{1,0:T(8,128)(2,1)S(1)} %pad_maximum_fusion.9), channel_id=1, source_target_pairs={{0,1},{2,0},{4,2},{6,4},{7,6},{5,7},{3,5},{1,3},{8,9},{10,8},{12,1... | collective-permute-start | bytes 1966088 | tf_op jit(solution)/shard_map/ppermute | solution.py:88
  382.9 20.5 %collective-permute-start.40 = (bf16[160,2048]{1,0:T(8,128)(2,1)}, bf16[160,2048]{1,0:T(8,128)(2,1)}, u32[]{:S(2)}, u32[]{:S(2)}) collective-permute-start(bf16[160,2048]{1,0:T(8,128)(2,1)} %pad_maximum_fusion.8), channel_id=1, source_target_pairs={{0,2},{2,4},{4,6},{6,7},{7,5},{5,3},{3,1},{1,0},{8,10},{10,12},{12... | collective-permute-start | bytes 1966088 | tf_op jit(solution)/shard_map/ppermute | solution.py:88
  383.1 21.1 %collective-permute-start.39 = (bf16[160,2048]{1,0:T(8,128)(2,1)}, bf16[160,2048]{1,0:T(8,128)(2,1)S(1)}, u32[]{:S(2)}, u32[]{:S(2)}) collective-permute-start(bf16[160,2048]{1,0:T(8,128)(2,1)} %add_convert_fusion.11), channel_id=1, source_target_pairs={{0,1},{2,0},{4,2},{6,4},{7,6},{5,7},{3,5},{1,3},{8,9},{10,8},{12,1... | collective-permute-start | bytes 1966088 | tf_op jit(solution)/shard_map/ppermute | solution.py:88
  385.0 23.4 %collective-permute-start.38 = (bf16[160,2048]{1,0:T(8,128)(2,1)}, bf16[160,2048]{1,0:T(8,128)(2,1)}, u32[]{:S(2)}, u32[]{:S(2)}) collective-permute-start(bf16[160,2048]{1,0:T(8,128)(2,1)} %add_convert_fusion.12), channel_id=1, source_target_pairs={{0,2},{2,4},{4,6},{6,7},{7,5},{5,3},{3,1},{1,0},{8,10},{10,12},{12... | collective-permute-start | bytes 1966088 | tf_op jit(solution)/shard_map/ppermute | solution.py:88
  408.4 192.2 %reduce-scatter.6.cloned.1.call-start = ((), (), s32[]{:S(2)}) async-start(), calls=%async_computation.12 | async-start | bytes 10485760 | tf_op jit(solution)/shard_map/reduce_scatter | solution.py:871
  411.9 25.6 %collective-permute-start.44 = (bf16[160,2048]{1,0:T(8,128)(2,1)}, bf16[160,2048]{1,0:T(8,128)(2,1)S(1)}, u32[]{:S(2)}, u32[]{:S(2)}) collective-permute-start(bf16[160,2048]{1,0:T(8,128)(2,1)} %get-tuple-element.499), channel_id=1, source_target_pairs={{0,2},{2,4},{4,6},{6,7},{7,5},{5,3},{3,1},{1,0},{8,10},{10,12},{12... | collective-permute-start | bytes 1966088 | tf_op jit(solution)/shard_map/ppermute | solution.py:88
  412.0 25.4 %collective-permute-start.45 = (bf16[160,2048]{1,0:T(8,128)(2,1)}, bf16[160,2048]{1,0:T(8,128)(2,1)}, u32[]{:S(2)}, u32[]{:S(2)}) collective-permute-start(bf16[160,2048]{1,0:T(8,128)(2,1)} %get-tuple-element.498), channel_id=1, source_target_pairs={{0,1},{2,0},{4,2},{6,4},{7,6},{5,7},{3,5},{1,3},{8,9},{10,8},{12,1... | collective-permute-start | bytes 1966088 | tf_op jit(solution)/shard_map/ppermute | solution.py:88
  416.6 21.5 %collective-permute-start.42 = (bf16[160,2048]{1,0:T(8,128)(2,1)}, bf16[160,2048]{1,0:T(8,128)(2,1)S(1)}, u32[]{:S(2)}, u32[]{:S(2)}) collective-permute-start(bf16[160,2048]{1,0:T(8,128)(2,1)} %get-tuple-element.514), channel_id=1, source_target_pairs={{0,2},{2,4},{4,6},{6,7},{7,5},{5,3},{3,1},{1,0},{8,10},{10,12},{12... | collective-permute-start | bytes 1966088 | tf_op jit(solution)/shard_map/ppermute | solution.py:88
  416.7 21.3 %collective-permute-start.43 = (bf16[160,2048]{1,0:T(8,128)(2,1)}, bf16[160,2048]{1,0:T(8,128)(2,1)S(1)}, u32[]{:S(2)}, u32[]{:S(2)}) collective-permute-start(bf16[160,2048]{1,0:T(8,128)(2,1)} %get-tuple-element.513), channel_id=1, source_target_pairs={{0,1},{2,0},{4,2},{6,4},{7,6},{5,7},{3,5},{1,3},{8,9},{10,8},{12,1... | collective-permute-start | bytes 1966088 | tf_op jit(solution)/shard_map/ppermute | solution.py:88
  440.9 15.5 %collective-permute-start.46 = (bf16[160,2048]{1,0:T(8,128)(2,1)S(1)}, bf16[160,2048]{1,0:T(8,128)(2,1)S(1)}, u32[]{:S(2)}, u32[]{:S(2)}) collective-permute-start(bf16[160,2048]{1,0:T(8,128)(2,1)S(1)} %get-tuple-element.497), channel_id=1, source_target_pairs={{0,2},{2,4},{4,6},{6,7},{7,5},{5,3},{3,1},{1,0},{8,10},{10,12},{12... | collective-permute-start | bytes 1966088 | tf_op jit(solution)/shard_map/ppermute | solution.py:88
  441.0 15.4 %collective-permute-start.47 = (bf16[160,2048]{1,0:T(8,128)(2,1)S(1)}, bf16[160,2048]{1,0:T(8,128)(2,1)S(1)}, u32[]{:S(2)}, u32[]{:S(2)}) collective-permute-start(bf16[160,2048]{1,0:T(8,128)(2,1)S(1)} %get-tuple-element.496), channel_id=1, source_target_pairs={{0,1},{2,0},{4,2},{6,4},{7,6},{5,7},{3,5},{1,3},{8,9},{10,8},{12,1... | collective-permute-start | bytes 1966088 | tf_op jit(solution)/shard_map/ppermute | solution.py:88
  457.2 24.7 %collective-permute-start.48 = (bf16[160,2048]{1,0:T(8,128)(2,1)S(1)}, bf16[160,2048]{1,0:T(8,128)(2,1)}, u32[]{:S(2)}, u32[]{:S(2)}) collective-permute-start(bf16[160,2048]{1,0:T(8,128)(2,1)S(1)} %get-tuple-element.336.refs_0_), channel_id=1, source_target_pairs={{0,2},{2,4},{4,6},{6,7},{7,5},{5,3},{3,1},{1,0},{8,10},{10,12},{12... | collective-permute-start | bytes 1966088 | tf_op jit(solution)/shard_map/ppermute | solution.py:88
  458.5 23.4 %collective-permute-start.49 = (bf16[160,2048]{1,0:T(8,128)(2,1)S(1)}, bf16[160,2048]{1,0:T(8,128)(2,1)}, u32[]{:S(2)}, u32[]{:S(2)}) collective-permute-start(bf16[160,2048]{1,0:T(8,128)(2,1)S(1)} %get-tuple-element.336.refs_0_), channel_id=1, source_target_pairs={{0,1},{2,0},{4,2},{6,4},{7,6},{5,7},{3,5},{1,3},{8,9},{10,8},{12,1... | collective-permute-start | bytes 1966088 | tf_op jit(solution)/shard_map/ppermute | solution.py:88
  459.5 25.5 %all-to-all-start.4 = ((bf16[8,160,256]{2,1,0:T(8,128)(2,1)}), bf16[8,160,256]{2,1,0:T(8,128)(2,1)S(1)}, u32[]{:S(2)}, u32[]{:S(2)}) async-start(bf16[8,160,256]{2,1,0:T(8,128)(2,1)} %bitcast.193), calls=%async_computation.4 | async-start | bytes 1310720 | tf_op jit(solution)/shard_map/all_to_all | solution.py:250
  465.0 175.4 %reduce-scatter.8.cloned.1.call-start = ((), (), s32[]{:S(2)}) async-start(), calls=%async_computation.13 | async-start | bytes 10485760 | tf_op jit(solution)/shard_map/reduce_scatter | solution.py:872
  485.9 18.9 %collective-permute-start.50 = (bf16[160,2048]{1,0:T(8,128)(2,1)}, bf16[160,2048]{1,0:T(8,128)(2,1)S(1)}, u32[]{:S(2)}, u32[]{:S(2)}) collective-permute-start(bf16[160,2048]{1,0:T(8,128)(2,1)} %collective-permute-done.48.refs_2_), channel_id=1, source_target_pairs={{0,2},{2,4},{4,6},{6,7},{7,5},{5,3},{3,1},{1,0},{8,10},{10,12},{12... | collective-permute-start | bytes 1966088 | tf_op jit(solution)/shard_map/ppermute | solution.py:88
  485.9 18.9 %collective-permute-start.51 = (bf16[160,2048]{1,0:T(8,128)(2,1)}, bf16[160,2048]{1,0:T(8,128)(2,1)S(1)}, u32[]{:S(2)}, u32[]{:S(2)}) collective-permute-start(bf16[160,2048]{1,0:T(8,128)(2,1)} %collective-permute-done.49.refs_1_), channel_id=1, source_target_pairs={{0,1},{2,0},{4,2},{6,4},{7,6},{5,7},{3,5},{1,3},{8,9},{10,8},{12,1... | collective-permute-start | bytes 1966088 | tf_op jit(solution)/shard_map/ppermute | solution.py:88
  505.8 16.5 %collective-permute-start.52 = (bf16[160,2048]{1,0:T(8,128)(2,1)}, bf16[160,2048]{1,0:T(8,128)(2,1)S(1)}, u32[]{:S(2)}, u32[]{:S(2)}) collective-permute-start(bf16[160,2048]{1,0:T(8,128)(2,1)} %copy-done.57), channel_id=1, source_target_pairs={{0,2},{2,4},{4,6},{6,7},{7,5},{5,3},{3,1},{1,0},{8,10},{10,12},{12... | collective-permute-start | bytes 1966088 | tf_op jit(solution)/shard_map/ppermute | solution.py:88
  506.6 15.8 %collective-permute-start.53 = (bf16[160,2048]{1,0:T(8,128)(2,1)}, bf16[160,2048]{1,0:T(8,128)(2,1)S(1)}, u32[]{:S(2)}, u32[]{:S(2)}) collective-permute-start(bf16[160,2048]{1,0:T(8,128)(2,1)} %copy-done.58), channel_id=1, source_target_pairs={{0,1},{2,0},{4,2},{6,4},{7,6},{5,7},{3,5},{1,3},{8,9},{10,8},{12,1... | collective-permute-start | bytes 1966088 | tf_op jit(solution)/shard_map/ppermute | solution.py:88
  552.1 31.5 %collective-permute-start.61 = (bf16[8,1,64,768]{3,2,1,0:T(8,128)(2,1)}, bf16[8,1,64,768]{3,2,1,0:T(8,128)(2,1)}, u32[]{:S(2)}, u32[]{:S(2)}) collective-permute-start(bf16[8,1,64,768]{3,2,1,0:T(8,128)(2,1)} %constant_dynamic-slice_fusion.1), channel_id=1, source_target_pairs={{0,16},{8,24},{16,0},{24,8},{1,17},{9,25},{17,1},{25,9},{2,18},{10... | collective-permute-start | bytes 2359304 | tf_op jit(solution)/shard_map/ppermute | solution.py:204
  564.9 21.1 %collective-permute-start.62 = (bf16[2,64,2048]{2,1,0:T(8,128)(2,1)}, bf16[2,64,2048]{2,1,0:T(8,128)(2,1)}, u32[]{:S(2)}, u32[]{:S(2)}) collective-permute-start(bf16[2,64,2048]{2,1,0:T(8,128)(2,1)} %dynamic-slice_bitcast_fusion.1), channel_id=1, source_target_pairs={{0,8},{8,0},{16,24},{24,16},{1,9},{9,1},{17,25},{25,17},{2,10},{10... | collective-permute-start | bytes 1572872 | tf_op jit(solution)/shard_map/ppermute | solution.py:204
  574.4 19.5 %collective-permute-start.60 = (bf16[160,2048]{1,0:T(8,128)(2,1)}, bf16[160,2048]{1,0:T(8,128)(2,1)S(1)}, u32[]{:S(2)}, u32[]{:S(2)}) collective-permute-start(bf16[160,2048]{1,0:T(8,128)(2,1)} %pad_maximum_fusion.12), channel_id=1, source_target_pairs={{0,1},{2,0},{4,2},{6,4},{7,6},{5,7},{3,5},{1,3},{8,9},{10,8},{12,1... | collective-permute-start | bytes 1966088 | tf_op jit(solution)/shard_map/ppermute | solution.py:88
  576.5 17.8 %collective-permute-start.59 = (bf16[160,2048]{1,0:T(8,128)(2,1)}, bf16[160,2048]{1,0:T(8,128)(2,1)}, u32[]{:S(2)}, u32[]{:S(2)}) collective-permute-start(bf16[160,2048]{1,0:T(8,128)(2,1)} %pad_maximum_fusion.11), channel_id=1, source_target_pairs={{0,2},{2,4},{4,6},{6,7},{7,5},{5,3},{3,1},{1,0},{8,10},{10,12},{12... | collective-permute-start | bytes 1966088 | tf_op jit(solution)/shard_map/ppermute | solution.py:88
  598.1 28.1 %collective-permute-start.63 = (bf16[160,2048]{1,0:T(8,128)(2,1)}, bf16[160,2048]{1,0:T(8,128)(2,1)}, u32[]{:S(2)}, u32[]{:S(2)}) collective-permute-start(bf16[160,2048]{1,0:T(8,128)(2,1)} %get-tuple-element.489), channel_id=1, source_target_pairs={{0,2},{2,4},{4,6},{6,7},{7,5},{5,3},{3,1},{1,0},{8,10},{10,12},{12... | collective-permute-start | bytes 1966088 | tf_op jit(solution)/shard_map/ppermute | solution.py:88
  600.6 25.6 %collective-permute-start.64 = (bf16[160,2048]{1,0:T(8,128)(2,1)}, bf16[160,2048]{1,0:T(8,128)(2,1)}, u32[]{:S(2)}, u32[]{:S(2)}) collective-permute-start(bf16[160,2048]{1,0:T(8,128)(2,1)} %get-tuple-element.488), channel_id=1, source_target_pairs={{0,1},{2,0},{4,2},{6,4},{7,6},{5,7},{3,5},{1,3},{8,9},{10,8},{12,1... | collective-permute-start | bytes 1966088 | tf_op jit(solution)/shard_map/ppermute | solution.py:88
  600.6 32.8 %all-to-all-start.6 = ((bf16[8,64,768]{2,1,0:T(8,128)(2,1)}), bf16[8,64,768]{2,1,0:T(8,128)(2,1)S(1)}, u32[]{:S(2)}, u32[]{:S(2)}) async-start(bf16[8,64,768]{2,1,0:T(8,128)(2,1)} %bitcast.63), calls=%async_computation.7 | async-start | bytes 1572864 | tf_op jit(solution)/shard_map/all_to_all | solution.py:250
  609.4 16.7 %collective-permute-start.65 = (bf16[1,64,2048]{2,1,0:T(8,128)(2,1)S(1)}, bf16[1,64,2048]{2,1,0:T(8,128)(2,1)S(1)}, u32[]{:S(2)}, u32[]{:S(2)}) collective-permute-start(bf16[1,64,2048]{2,1,0:T(8,128)(2,1)S(1)} %constant_dynamic-slice_fusion), channel_id=1, source_target_pairs={{0,16},{8,24},{16,0},{24,8},{1,17},{9,25},{17,1},{25,9},{2,18},{10... | collective-permute-start | bytes 786440 | tf_op jit(solution)/shard_map/ppermute | solution.py:204
  609.6 15.3 %collective-permute-start.67 = (f32[4640]{0:T(1024)S(1)}, f32[4640]{0:T(1024)S(1)}, u32[]{:S(2)}, u32[]{:S(2)}) collective-permute-start(f32[4640]{0:T(1024)S(1)} %add.650), channel_id=1, source_target_pairs={{0,16},{8,24},{16,0},{24,8},{1,17},{9,25},{17,1},{25,9},{2,18},{10... | collective-permute-start | bytes 55688 | tf_op jit(solution)/shard_map/ppermute | solution.py:204
  635.0 24.4 %collective-permute-start.70 = (bf16[1,3,64,2048]{3,2,1,0:T(8,128)(2,1)S(1)}, bf16[1,3,64,2048]{3,2,1,0:T(8,128)(2,1)}, u32[]{:S(2)}, u32[]{:S(2)}) collective-permute-start(bf16[1,3,64,2048]{3,2,1,0:T(8,128)(2,1)S(1)} %stack.161), channel_id=1, source_target_pairs={{0,16},{8,24},{16,0},{24,8},{1,17},{9,25},{17,1},{25,9},{2,18},{10... | collective-permute-start | bytes 2359304 | tf_op jit(solution)/shard_map/ppermute | solution.py:204
  638.6 19.6 %collective-permute-start.71 = (bf16[1,64,2048]{2,1,0:T(8,128)(2,1)S(1)}, bf16[1,64,2048]{2,1,0:T(8,128)(2,1)}, u32[]{:S(2)}, u32[]{:S(2)}) collective-permute-start(bf16[1,64,2048]{2,1,0:T(8,128)(2,1)S(1)} %add_convert_fusion.19), channel_id=1, source_target_pairs={{0,16},{8,24},{16,0},{24,8},{1,17},{9,25},{17,1},{25,9},{2,18},{10... | collective-permute-start | bytes 786440 | tf_op jit(solution)/shard_map/ppermute | solution.py:204
  642.1 19.0 %collective-permute-start.68 = (bf16[160,2048]{1,0:T(8,128)(2,1)}, bf16[160,2048]{1,0:T(8,128)(2,1)S(1)}, u32[]{:S(2)}, u32[]{:S(2)}) collective-permute-start(bf16[160,2048]{1,0:T(8,128)(2,1)} %get-tuple-element.487), channel_id=1, source_target_pairs={{0,2},{2,4},{4,6},{6,7},{7,5},{5,3},{3,1},{1,0},{8,10},{10,12},{12... | collective-permute-start | bytes 1966088 | tf_op jit(solution)/shard_map/ppermute | solution.py:88
  642.2 19.0 %collective-permute-start.69 = (bf16[160,2048]{1,0:T(8,128)(2,1)}, bf16[160,2048]{1,0:T(8,128)(2,1)S(1)}, u32[]{:S(2)}, u32[]{:S(2)}) collective-permute-start(bf16[160,2048]{1,0:T(8,128)(2,1)} %get-tuple-element.486), channel_id=1, source_target_pairs={{0,1},{2,0},{4,2},{6,4},{7,6},{5,7},{3,5},{1,3},{8,9},{10,8},{12,1... | collective-permute-start | bytes 1966088 | tf_op jit(solution)/shard_map/ppermute | solution.py:88
  (165 other events, 1760.7 us)
Sparse Core Ops, SparseCore 0:
  42.8 57.6 all-gather.1
  408.5 72.9 reduce-scatter.3
  484.3 71.6 reduce-scatter.5
  558.5 77.7 reduce-scatter.7
